TPU v7x, 32 devices: a whole 2x2x4 slice. The times are simulated.
32 devices in a mesh: dp: 8 (over z, x), mp: 4 (over y, core).
Axes of the slice: x: 2, y: 2, z: 4, core: 2. Of those that a mesh axis runs over, the one named last changes fastest.
Arguments:
- residual: bfloat16 [8, 512, 2048], P(None, 'dp', 'mp'), may hold values from -61 to 61
- attention_gain: bfloat16 [2048], P('mp'), may hold values from 0.25 to 1.75
- query_matrix: bfloat16 [2048, 2048], P(None, 'mp'), may hold values from -0.125 to 0.125
- key_value_matrix: bfloat16 [2, 2048, 512], P(None, None, 'mp'), may hold values from -0.125 to 0.125
- output_matrix: bfloat16 [2048, 2048], P('mp'), may hold values from -0.5 to 0.5
- feedfwd_gain: bfloat16 [2048], P('mp'), may hold values from 0.25 to 1.75
- gate_up_matrix: bfloat16 [2, 2048, 8192], P(None, None, 'mp'), may hold values from -0.125 to 0.125
- down_matrix: bfloat16 [8192, 2048], P('mp'), may hold values from -0.0625 to 0.0625
- attention_adapter_input: bfloat16 [8, 48, 2048], replicated, may hold values from -0.125 to 0.125
- query_adapter_output: bfloat16 [8, 16, 2048], P(None, None, 'mp'), may hold values from -0.75 to 0.75
- key_value_adapter_output: bfloat16 [8, 2, 16, 512], P(None, None, None, 'mp'), may hold values from -0.75 to 0.75
- output_adapter_input: bfloat16 [8, 16, 2048], P(None, None, 'mp'), may hold values from -0.5 to 0.5
- output_adapter_output: bfloat16 [8, 16, 2048], replicated, may hold values from -0.75 to 0.75
- feedfwd_adapter_input: bfloat16 [8, 32, 2048], replicated, may hold values from -0.125 to 0.125
- feedfwd_adapter_output: bfloat16 [8, 2, 16, 8192], P(None, None, None, 'mp'), may hold values from -0.75 to 0.75
- down_adapter_input: bfloat16 [8, 16, 8192], P(None, None, 'mp'), may hold values from -0.0625 to 0.0625
- down_adapter_output: bfloat16 [8, 16, 2048], replicated, may hold values from -0.75 to 0.75
- lengths: int32 [8], replicated, may hold values from 1 to 512, 2560 in all
- adapter_index: int32 [8], replicated, may hold values from 0 to 7
- dealing_slots: int32 [8], replicated, may hold values from 0 to 7, each once
- cotangent: bfloat16 [8, 512, 2048], P('dp', None, 'mp'), may hold values from -6 to 6
Outputs:
- output: bfloat16 [8, 512, 2048], P(None, 'dp', 'mp')
- input_grad: bfloat16 [8, 512, 2048], P(None, 'dp', 'mp')
- qkv_lora_a_grad: float32 [8, 48, 2048], replicated
- query_lora_b_grad: float32 [8, 16, 2048], P(None, None, 'mp')
- kv_lora_b_grad: float32 [8, 2, 16, 512], P(None, None, None, 'mp')
- out_lora_a_grad: float32 [8, 16, 2048], P(None, None, 'mp')
- out_lora_b_grad: float32 [8, 16, 2048], replicated
- ffn_lora_a_grad: float32 [8, 32, 2048], replicated
- ffn_lora_b_grad: float32 [8, 2, 16, 8192], P(None, None, None, 'mp')
- down_lora_a_grad: float32 [8, 16, 8192], P(None, None, 'mp')
- down_lora_b_grad: float32 [8, 16, 2048], replicated
Inputs may be any that keep to these rules, and one draw needn't show every extreme that they name: `lengths`: the longest sequence has exactly 512 valid positions. `dealing_slots`: each slot receives exactly one sequence.
All inputs are finite; a program needn't handle non-finite values.
Results may differ from a plain program's by a relative error of at most 0.023.
Values may be sent and summed in bfloat16 or wider, within the bound.
No kernel may reach another device: no remote copies, remote signals or barrier semaphores. Data moves between devices by JAX's collectives and lax.ppermute only.
A program may use at most 192 MiB of HBM per device.

v0:
```python
import functools

import jax
import jax.numpy as jnp
import numpy as np
from jax import lax
from jax.experimental import pallas as pl
from jax.experimental.pallas import tpu as pltpu
from jax.sharding import PartitionSpec as P

WIDTH = 2048
HEAD = 64
HALF = HEAD // 2
RANK = 16
EPS = 1e-05
ROPE_BASE = 500000.0
NEG_FILL = -1e30
PARTS = 4
LANES = 128
ROW_BLOCK = 64
QUARTER = WIDTH // PARTS
CHUNKS = 2
MIB = 1024 * 1024
F32 = jnp.float32
BF16 = jnp.bfloat16


def nn(a, b):
    return lax.dot_general(a, b, (((1,), (0,)), ((), ())), preferred_element_type=F32)


def nt(a, b):
    return lax.dot_general(a, b, (((1,), (1,)), ((), ())), preferred_element_type=F32)


def rope_tables(length):
    freq = ROPE_BASE ** (-np.arange(HALF, dtype=np.float32) * np.float32(2.0 / HEAD))
    angles = (np.arange(length, dtype=np.float32)[None, :] * freq.astype(np.float32)[:, None]).astype(np.float32)
    return np.cos(angles).astype(np.float32), np.sin(angles).astype(np.float32)


def quarter(me, rel):
    return pl.ds(pl.multiple_of((me ^ rel) * QUARTER, QUARTER), QUARTER)


LO, HI = slice(0, QUARTER), slice(QUARTER, 2 * QUARTER)


def total_block(rel, rows_at, own, oth):
    return (own if rel in (0, 2) else oth)[rows_at, LO if rel in (0, 1) else HI].astype(F32)


def store_block(rel, value, rows_at, keep_ref, send_ref):
    to = pl.ds(pl.multiple_of((rel // 2) * QUARTER, QUARTER), QUARTER)

    @pl.when(rel % 2 == 0)
    def _():
        keep_ref[rows_at, to] = value[...]

    @pl.when(rel % 2 == 1)
    def _():
        send_ref[rows_at, to] = value[...].astype(BF16)


def chunk_of(ref, chunk, rows):
    return ref if ref.shape[0] == rows else ref.at[chunk * rows:(chunk + 1) * rows]


def row_block(i):
    return pl.ds(pl.multiple_of(i * ROW_BLOCK, ROW_BLOCK), ROW_BLOCK)


def is_valid(chunk, i, rows, length):
    return chunk * rows + i * ROW_BLOCK + lax.broadcasted_iota(jnp.int32, (ROW_BLOCK, 1), 0) < length


def copies_of(pairs, sems):
    made = [pltpu.make_async_copy(source, target, sems.at[i]) for i, (source, target) in enumerate(pairs)]
    for copy in made:
        copy.start()
    return made


def put_block(rel, value, keep_ref, send_ref):
    ref = keep_ref if rel in (0, 2) else send_ref
    ref[:, LO if rel in (0, 1) else HI] = value.astype(ref.dtype)


def rotate(value, cos, sin, out_ref):
    for i in range(value.shape[0] // HEAD):
        u1, u2 = value[i * HEAD:i * HEAD + HALF], value[i * HEAD + HALF:(i + 1) * HEAD]
        out_ref[i * HEAD:i * HEAD + HALF, :] = (u1 * cos - u2 * sin).astype(BF16)
        out_ref[i * HEAD + HALF:(i + 1) * HEAD, :] = (u2 * cos + u1 * sin).astype(BF16)


def turn_back(value, cos, sin, out_ref):
    for i in range(value.shape[0] // HEAD):
        w1, w2 = value[i * HEAD:i * HEAD + HALF], value[i * HEAD + HALF:(i + 1) * HEAD]
        out_ref[i * HEAD:i * HEAD + HALF, :] = (w1 * cos + w2 * sin).astype(BF16)
        out_ref[i * HEAD + HALF:(i + 1) * HEAD, :] = (w2 * cos - w1 * sin).astype(BF16)


def head_rows(i):
    return pl.ds(pl.multiple_of(i * HEAD, HEAD), HEAD)


def visible(key_start, query_start, rows, length):
    kpos = key_start + lax.broadcasted_iota(jnp.int32, (rows, rows), 0)
    qpos = query_start + lax.broadcasted_iota(jnp.int32, (rows, rows), 1)
    return (kpos <= qpos) & (kpos < length)


def project_kernel(chunk, info, wq_h, wkv_h, x0, x1, x2, x3, gains, a1, qb, kvb, cos_t, sin_t,
                   h_out, t1t_out, qt_out, kn_out, vn_out, kt_out, vt_out, wq, wkv, sems):
    copies = copies_of(((wkv_h, wkv), (wq_h, wq)), sems)
    me = info[0]
    rows = h_out.shape[0]
    kv_heads = kn_out.shape[0]
    xs = [chunk_of(x, chunk, rows) for x in (x0, x1, x2, x3)]

    def norm(i, carry):
        at = row_block(i)
        square = jnp.zeros((ROW_BLOCK, 1), F32)
        for r in range(PARTS):
            v = xs[r][at, :].astype(F32)
            square = square + jnp.sum(v * v, axis=1, keepdims=True)
        inv = lax.rsqrt(square / WIDTH + EPS)
        for r in range(PARTS):
            v = xs[r][at, :].astype(F32)
            h_out[at, quarter(me, r)] = (v * inv * gains[r, 0:1, :].astype(F32)).astype(BF16)
        return carry

    lax.fori_loop(0, rows // ROW_BLOCK, norm, 0)
    h = h_out[...]
    t1 = nt(h, a1[...])
    t1t_out[...] = t1.T.astype(BF16)
    t1b = t1.astype(BF16)
    cos, sin = cos_t[...], sin_t[...]
    copies[0].wait()
    k = nn(h, wkv[0]) + nn(t1b[:, RANK:2 * RANK], kvb[0])
    rotate(k.T, cos, sin, kt_out)
    k_n = kt_out[...].T
    v_n = (nn(h, wkv[1]) + nn(t1b[:, 2 * RANK:], kvb[1])).astype(BF16)
    vt_out[...] = v_n.T
    for i in range(kv_heads):
        kn_out[i] = k_n[:, i * HEAD:(i + 1) * HEAD]
        vn_out[i] = v_n[:, i * HEAD:(i + 1) * HEAD]
    copies[1].wait()
    q = nn(h, wq[...]) + nn(t1b[:, :RANK], qb[...])
    rotate(q.T * (HEAD ** -0.5), cos, sin, qt_out)


def attend_kernel(chunk, info, wo_h, qt, oa, ob, *rest):
    pairs, rest = rest[:2 * (chunk + 1)], rest[2 * (chunk + 1):]
    z_keep, z_send, ot_out, lse_out, tot_out, wo, sems = rest
    copies = copies_of(((wo_h, wo),), sems)
    keys, values = pairs[0::2], pairs[1::2]
    me, length = info[0], info[1]
    rows = qt.shape[1]
    kv_heads = keys[0].shape[0]
    heads = qt.shape[0] // HEAD
    group = heads // kv_heads

    def one_head(i, carry):
        j = i // group
        q_h = qt[head_rows(i), :]
        parts = []
        for c, key in enumerate(keys):
            s = nn(key[j], q_h)
            parts.append(jnp.where(visible(c * rows, chunk * rows, rows, length), s, NEG_FILL))
        top = functools.reduce(jnp.maximum, [jnp.max(s, axis=0, keepdims=True) for s in parts])
        es = [jnp.exp(s - top) for s in parts]
        total = sum(jnp.sum(e, axis=0, keepdims=True) for e in es)
        lse_out[pl.ds(i, 1), :] = top + jnp.log(total)
        o_t = sum(nn(value[head_rows(j), :], e.astype(BF16)) for value, e in zip(values, es))
        ot_out[head_rows(i), :] = (o_t / total).astype(BF16)
        return carry

    lax.fori_loop(0, heads, one_head, 0, unroll=2)
    o = ot_out[...].T
    to = nt(o, oa[...])
    tot_out[...] = to.T.astype(BF16)
    to = to.astype(BF16)
    copies[0].wait()
    for r in range(PARTS):
        at = quarter(me, r)
        put_block(r, nn(o, wo[:, at]) + nn(to, ob[:, at]), z_keep, z_send)


def front_kernel(chunk, last, info, wgu_h, wd_h, x0, x1, x2, x3, zo, zp, g0, g1, g2, g3, gains, a2, bd, fb, da,
                 *rest):
    f_s, wgu, wd, sems = rest[-4:]
    xm_out, xq_out, h_out, g_out, act_out, dg_out, du_out, t2_s, dtd_s, b_out = rest[-14:-4]
    units = wd.shape[0]

    def copies(i):
        c = pl.ds(pl.multiple_of(i * QUARTER, QUARTER), QUARTER)
        return (pltpu.make_async_copy(wgu_h.at[:, :, c], wgu.at[:, :, c], sems.at[0, i]),
                pltpu.make_async_copy(wd_h.at[c, :], wd.at[c, :], sems.at[1, i]))

    for i in range(units // QUARTER):
        for copy in copies(i):
            copy.start()
    me, length = info[0], info[1]
    rows = h_out.shape[0]
    xs, gs = ([chunk_of(v, chunk, rows) for v in vs] for vs in ((x0, x1, x2, x3), (g0, g1, g2, g3)))

    def norm(i, carry):
        at = row_block(i)
        valid = is_valid(chunk, i, rows, length)
        square = jnp.zeros((ROW_BLOCK, 1), F32)
        for r in range(PARTS):
            v = xs[r][at, :].astype(F32) + total_block(r, at, zo, zp)
            if r == 0:
                xq_out[at, :] = v
            f_s[:, quarter(me, r)] = v
            square = square + jnp.sum(v * v, axis=1, keepdims=True)
            g_out[at, quarter(me, r)] = jnp.where(valid, gs[r][at, :], jnp.zeros((), BF16))
        inv = lax.rsqrt(square / WIDTH + EPS)
        for r in range(PARTS):
            v = f_s[:, quarter(me, r)]
            xm_out[at, quarter(me, r)] = v.astype(BF16)
            h_out[at, quarter(me, r)] = (v * inv * gains[r, 1:2, :].astype(F32)).astype(BF16)
        return carry

    lax.fori_loop(0, rows // ROW_BLOCK, norm, 0)
    t2 = nt(h_out[...], a2[...])
    t2_s[...] = t2.astype(BF16)
    dtd = nt(g_out[...], bd[...])
    dtd_s[...] = dtd.astype(BF16)
    t2t, dtdt = t2.T.astype(BF16), dtd.T.astype(BF16)

    def block(i, carry):
        c = pl.ds(pl.multiple_of(i * QUARTER, QUARTER), QUARTER)
        for copy in copies(i):
            copy.wait()
        h, g = h_out[...], g_out[...]
        gate = nn(h, wgu[0, :, c]) + nn(t2_s[:, :RANK], fb[0, :, c])
        up = nn(h, wgu[1, :, c]) + nn(t2_s[:, RANK:], fb[1, :, c])
        dact = nt(g, wd[c, :]) + nn(dtd_s[...], da[:, c])
        sig = 1.0 / (1.0 + jnp.exp(-gate))
        silu = gate * sig
        act = (silu * up).astype(BF16)
        dgate = (dact * up * sig * (1.0 + gate * (1.0 - sig))).astype(BF16)
        dup = (dact * silu).astype(BF16)
        act_out[:, c], dg_out[:, c], du_out[:, c] = act, dgate, dup
        for k, value in enumerate((nn(t2t[:RANK], dgate), nn(t2t[RANK:], dup), nn(dtdt, act))):
            at = pl.ds(pl.multiple_of((3 * i + k) * RANK, RANK), RANK)
            if last:
                value = value + rest[0][at, :]
            b_out[at, :] = value.astype(b_out.dtype)
        return carry

    lax.fori_loop(0, units // QUARTER, block, 0)


def back_kernel(last, info, wgu_h, wd_h, h, g, act, dg, du, a2, bd, fb, da, *rest):
    (value_s, low_s, wgu, wd, sems), rest = rest[-5:], rest[:-5]
    outs, rest = (rest[-4:], rest[:-4]) if last else (rest[-5:], rest[:-5])
    d_keep, d_send, y_keep, y_send = outs[:4]
    me = info[0]
    rows = h.shape[0]
    own = slice(0, rows)

    def copies(r):
        at = quarter(me, r)
        return (pltpu.make_async_copy(wgu_h.at[:, at, :], wgu.at[:, at, :], sems.at[0, r]),
                pltpu.make_async_copy(wd_h.at[:, at], wd.at[:, at], sems.at[1, r]))

    for r in range(PARTS):
        for copy in copies(r):
            copy.start()
    if last:
        y_keep[rows:, :], y_send[rows:, :] = rest[1][...], rest[2][...]
    dt2 = jnp.concatenate([nt(dg[...], fb[0]), nt(du[...], fb[1])], axis=1)
    dt2b = dt2.astype(BF16)
    td = nt(act[...], da[...])
    tdb = td.astype(BF16)
    dt2t, tdt = dt2.T.astype(BF16), td.T.astype(BF16)

    def block(r, carry):
        at = quarter(me, r)
        for copy in copies(r):
            copy.wait()
        value_s[...] = nt(dg[...], wgu[0, at, :]) + nt(du[...], wgu[1, at, :]) + nn(dt2b, a2[:, at])
        store_block(r, value_s, own, d_keep, d_send)
        value_s[...] = nn(act[...], wd[:, at]) + nn(tdb, bd[:, at])
        store_block(r, value_s, own, y_keep, y_send)
        low_s[:2 * RANK, :] = nn(dt2t, h[:, at])
        low_s[2 * RANK:, :] = nn(tdt, g[:, at])
        if last:
            low_s[...] += rest[0][:, at]
            store_block(r, low_s, slice(rows, rows + 3 * RANK), d_keep, d_send)
        else:
            outs[4][:, at] = low_s[...]
        return carry

    lax.fori_loop(0, PARTS, block, 0)


def attend_back_kernel(chunk, last, info, wq_h, wkv_h, wo_h, x0, x1, x2, x3, g0, g1, g2, g3, xm, do_, dp, gains, a1,
                       qb, kvb, oa, ob, cos_t, sin_t, h_in, t1t, qt, ot, lse, tot, *rest):
    scratch, rest = rest[-13:], rest[:-13]
    z_s, f_s, dot_s, dqt_s, dkt_s, dvt_s, dq_s, value_s, low_s, wq, wkv, wo, sems = scratch
    copies = copies_of(((wo_h, wo), (wq_h, wq), (wkv_h, wkv)), sems)
    n_out = 5 if last else 8
    outs, rest = rest[-n_out:], rest[:-n_out]
    dxq_out, h_keep, h_send, inv_out, b_out = outs[:5]
    triples, rest = rest[:3 * (chunk + 1)], rest[3 * (chunk + 1):]
    keys, values, keys_t = triples[0::3], triples[1::3], triples[2::3]
    me, length = info[0], info[1]
    rows = xm.shape[0]
    kv_heads = keys[0].shape[0]
    heads = qt.shape[0] // HEAD
    group = heads // kv_heads
    q_cols, kv_cols = heads * HEAD, kv_heads * HEAD
    xs, gs = ([chunk_of(v, chunk, rows) for v in vs] for vs in ((x0, x1, x2, x3), (g0, g1, g2, g3)))

    def norm_back(i, carry):
        at = row_block(i)
        valid = is_valid(chunk, i, rows, length)
        square, first, inner = (jnp.zeros((ROW_BLOCK, 1), F32) for _ in range(3))
        for r in range(PARTS):
            v = xm[at, quarter(me, r)].astype(F32)
            square = square + jnp.sum(v * v, axis=1, keepdims=True)
            w = total_block(r, at, do_, dp) * gains[r, 1:2, :].astype(F32)
            f_s[:, quarter(me, r)] = w
            inner = inner + jnp.sum(v * w, axis=1, keepdims=True)
            u = xs[r][at, :].astype(F32)
            first = first + jnp.sum(u * u, axis=1, keepdims=True)
        inv_out[at, :] = lax.rsqrt(first / WIDTH + EPS)
        inv = lax.rsqrt(square / WIDTH + EPS)
        back = inv * inv * inv * inner / WIDTH
        for r in range(PARTS):
            v = xm[at, quarter(me, r)].astype(F32)
            g = jnp.where(valid, gs[r][at, :].astype(F32), 0.0)
            d = g + inv * f_s[:, quarter(me, r)] - v * back
            if r == 0:
                dxq_out[at, :] = d
            z_s[at, quarter(me, r)] = d.astype(BF16)
        return carry

    lax.fori_loop(0, rows // ROW_BLOCK, norm_back, 0)
    dz = z_s[...]
    dto = nt(dz, ob[...])
    copies[0].wait()
    d_o = nt(dz, wo[...]) + nn(dto.astype(BF16), oa[...])
    dot_s[...] = d_o.T.astype(BF16)
    if last:
        for c in range(chunk + 1):
            dkt_s[c], dvt_s[c] = rest[2][...], rest[3][...]
    else:
        dkt_s[...] = jnp.zeros_like(dkt_s)
        dvt_s[...] = jnp.zeros_like(dvt_s)

    def one_head(i, carry):
        j = i // group
        q_h, do_h = qt[head_rows(i), :], dot_s[head_rows(i), :]
        dots = jnp.sum(do_h.astype(F32) * ot[head_rows(i), :].astype(F32), axis=0, keepdims=True)
        low = lse[pl.ds(i, 1), :]
        dq_h = jnp.zeros((HEAD, rows), F32)
        for c in range(chunk + 1):
            prob = jnp.exp(nn(keys[c][j], q_h) - low)
            prob = jnp.where(visible(c * rows, chunk * rows, rows, length), prob, 0.0)
            ds = (prob * (nn(values[c][j], do_h) - dots)).astype(BF16)
            dq_h = dq_h + nn(keys_t[c][head_rows(j), :], ds)
            dkt_s[c, head_rows(j), :] += nt(q_h, ds)
            dvt_s[c, head_rows(j), :] += nt(do_h, prob.astype(BF16))
        dqt_s[head_rows(i), :] = dq_h
        return carry

    lax.fori_loop(0, heads, one_head, 0, unroll=2)
    if not last:
        outs[6][...], outs[7][...] = dkt_s[0], dvt_s[0]
    cos, sin = cos_t[...], sin_t[...]
    dto_t, o_t = dto.T.astype(BF16), ot[...]
    d_out_a = nt(dto_t, o_t)
    turn_back(dqt_s[...], cos * (HEAD ** -0.5), sin * (HEAD ** -0.5), dot_s)
    dq_s[:, :q_cols] = dot_s[...].T
    turn_back(dkt_s[chunk], cos, sin, dot_s)
    dq_s[:, q_cols:q_cols + kv_cols] = dot_s[:kv_cols, :].T
    dq_s[:, q_cols + kv_cols:] = dvt_s[chunk].T.astype(BF16)
    dq, dk, dv = dq_s[:, :q_cols], dq_s[:, q_cols:q_cols + kv_cols], dq_s[:, q_cols + kv_cols:]
    dt1 = jnp.concatenate([nt(dq, qb[...]), nt(dk, kvb[0]), nt(dv, kvb[1])], axis=1)
    dt1b = dt1.astype(BF16)
    kv_pad = jnp.zeros((RANK, QUARTER - 2 * kv_cols), F32)
    d_kv = jnp.concatenate([nn(t1t[RANK:2 * RANK, :], dk), nn(t1t[2 * RANK:, :], dv), kv_pad], axis=1)
    for k, value in enumerate((nn(t1t[:RANK, :], dq), d_out_a, d_kv)):
        at = slice(k * RANK, (k + 1) * RANK)
        if last:
            value = value + rest[0][at, :]
        b_out[at, :] = value.astype(b_out.dtype)
    dt1t = dt1.T.astype(BF16)
    copies[1].wait()
    copies[2].wait()

    def block(r, inner):
        at = quarter(me, r)
        d = nt(dq_s[:, :q_cols], wq[at, :]) + nn(dt1b, a1[:, at])
        d = d + nt(dq_s[:, q_cols:q_cols + kv_cols], wkv[0, at, :]) + nt(dq_s[:, q_cols + kv_cols:], wkv[1, at, :])
        value_s[...] = d
        store_block(r, value_s, slice(0, rows), h_keep, h_send)
        low_s[:3 * RANK, :] = nn(dt1t, h_in[:, at])
        low_s[3 * RANK:, :] = nn(tot[...], z_s[:, at])
        if last:
            low_s[...] += rest[1][:, at]
            store_block(r, low_s, slice(rows, rows + 4 * RANK), h_keep, h_send)
        else:
            outs[5][:, at] = low_s[...]
        return inner + jnp.sum(d * h_in[:, at].astype(F32), axis=1, keepdims=True)

    inner = lax.fori_loop(0, PARTS, block, jnp.zeros((rows, 1), F32))
    for ref in (h_keep, h_send):
        ref[:rows, 2 * QUARTER:] = jnp.broadcast_to(inner, (rows, LANES)).astype(ref.dtype)
        if last:
            ref[rows:, 2 * QUARTER:] = jnp.zeros((4 * RANK, LANES), ref.dtype)


def finish_kernel(gains, x_all, *refs):
    out = refs[-1]
    gain = gains[0, 0:1, :].astype(F32)
    rows = out.shape[0] // CHUNKS
    for c in range(CHUNKS):
        dx, low, high, got, inv = refs[5 * c:5 * (c + 1)]
        x = chunk_of(x_all, c, rows)
        inv = inv[...]
        inner = high[:rows, QUARTER:QUARTER + 1].astype(F32) + got[:rows, QUARTER:QUARTER + 1].astype(F32)
        scale = inv * inv * inner / WIDTH
        grad = inv * (gain * (low[:rows, :] + got[:rows, :QUARTER].astype(F32))) - x[...].astype(F32) * scale
        out[c * rows:(c + 1) * rows, :] = (dx[...] + grad).astype(BF16)


def split_refs(refs, counts):
    groups = []
    for count in counts:
        groups.append(refs[:count])
        refs = refs[count:]
    return groups, refs


def with_entry(parts, at, use):
    start = 0
    for ref in parts:
        @pl.when((at >= start) & (at < start + ref.shape[0]))
        def _(ref=ref, start=start):
            use(ref, at - start)
        start += ref.shape[0]


def sum_slots(info, owners, out_refs, one_slot):
    count = out_refs[0].shape[0]
    base = pl.program_id(0) * count
    slots = owners.shape[0]
    for ref in out_refs:
        ref[...] = jnp.zeros_like(ref)

    def add(slot, carry):
        owner = owners[slot] - base

        @pl.when((owner >= 0) & (owner < count))
        def _():
            one_slot(owner, entry_of(slot, info[3], slots))
        return carry

    lax.fori_loop(0, slots, add, 0)


def feedforward_sum_kernel(counts, info, owners, *refs):
    (b_parts, *a_parts), outs = split_refs(refs, counts)
    ga, gdb, gb, gda = outs
    me = info[0]

    def one_slot(owner, at):
        def add_b(ref, e):
            for i in range(gda.shape[2] // QUARTER):
                cols = slice(i * QUARTER, (i + 1) * QUARTER)
                base = i * 3 * RANK
                gb[owner, 0, :, cols] += ref[e, base:base + RANK, :].astype(F32)
                gb[owner, 1, :, cols] += ref[e, base + RANK:base + 2 * RANK, :].astype(F32)
                gda[owner, :, cols] += ref[e, base + 2 * RANK:base + 3 * RANK, :].astype(F32)

        with_entry(b_parts, at, add_b)
        for r, parts in enumerate(a_parts):
            def add_a(ref, e, r=r):
                ga[owner, :, quarter(me, r)] += ref[e, :2 * RANK, :].astype(F32)
                gdb[owner, :, quarter(me, r)] += ref[e, 2 * RANK:, :].astype(F32)

            with_entry(parts, at, add_a)

    sum_slots(info, owners, outs, one_slot)


def attention_sum_kernel(counts, info, owners, *refs):
    (b_parts, *a_parts), outs = split_refs(refs, counts)
    ga, gob, gq, gkv, goa = outs
    me = info[0]
    kv_cols = gkv.shape[3]

    def one_slot(owner, at):
        def add_b(ref, e):
            gq[owner] += ref[e, :RANK, :].astype(F32)
            goa[owner] += ref[e, RANK:2 * RANK, :].astype(F32)
            gkv[owner, 0] += ref[e, 2 * RANK:3 * RANK, :kv_cols].astype(F32)
            gkv[owner, 1] += ref[e, 2 * RANK:3 * RANK, kv_cols:2 * kv_cols].astype(F32)

        with_entry(b_parts, at, add_b)
        for r, parts in enumerate(a_parts):
            def add_a(ref, e, r=r):
                ga[owner, :, quarter(me, r)] += ref[e, :3 * RANK, :].astype(F32)
                gob[owner, :, quarter(me, r)] += ref[e, 3 * RANK:, :].astype(F32)

            with_entry(parts, at, add_a)

    sum_slots(info, owners, outs, one_slot)


def deal_kernel(slots, source, out, sems):
    made = [pltpu.make_async_copy(source.at[i], out.at[slots[i]], sems.at[i]) for i in range(source.shape[0])]
    for copy in made:
        copy.start()
    for copy in made:
        copy.wait()


def collect_kernel(slots, source, out, sems):
    made = [pltpu.make_async_copy(source.at[slots[i]], out.at[i], sems.at[i]) for i in range(source.shape[0])]
    for copy in made:
        copy.start()
    for copy in made:
        copy.wait()


def move_rows(kernel, value, slots, name):
    return pl.pallas_call(
        kernel,
        in_specs=[pl.BlockSpec(memory_space=pltpu.SMEM), pl.BlockSpec(memory_space=pl.ANY)],
        out_specs=pl.BlockSpec(memory_space=pl.ANY),
        out_shape=jax.ShapeDtypeStruct(value.shape, value.dtype),
        scratch_shapes=[pltpu.SemaphoreType.DMA((value.shape[0],))],
        compiler_params=pltpu.CompilerParams(vmem_limit_bytes=MIB),
        cost_estimate=pl.CostEstimate(flops=1000, transcendentals=0, bytes_accessed=1000),
        name=name,
    )(slots, value)


def sds(shape, dtype):
    return jax.ShapeDtypeStruct(tuple(shape), dtype)


def in_vmem(value):
    return pltpu.with_memory_space_constraint(value, pltpu.VMEM)


def in_hbm(value):
    return pltpu.with_memory_space_constraint(value, pltpu.HBM)


def call(kernel, info, weights, args, outs, scratch, name, mib, after=(), sems=()):
    vmem = pl.BlockSpec(memory_space=pltpu.VMEM)
    scalars = () if info is None else (info,)
    n, w = len(scalars), len(weights)

    def body(*refs):
        at = n + w + len(args)
        kernel(*refs[:at], *refs[at + len(after):])

    return pl.pallas_call(
        body,
        in_specs=[pl.BlockSpec(memory_space=pltpu.SMEM)] * n + [pl.BlockSpec(memory_space=pltpu.HBM)] * w + [vmem] * len(args)
        + [pl.BlockSpec(memory_space=pl.ANY)] * len(after),
        out_specs=[vmem] * len(outs),
        out_shape=[pltpu.VMEM(tuple(s), d) for s, d in outs],
        scratch_shapes=[pltpu.VMEM(s, d) for s, d in scratch] + ([pltpu.SemaphoreType.DMA(sems)] if sems else []),
        compiler_params=pltpu.CompilerParams(vmem_limit_bytes=mib * MIB),
        cost_estimate=pl.CostEstimate(flops=1000, transcendentals=0, bytes_accessed=1000),
        name=name,
    )(*scalars, *(in_hbm(a) for a in weights), *(in_vmem(a) for a in args), *after)


def sum_call(kernel, scalars, groups, outs, name):
    args = [v for group in groups for v in group]
    steps = 2
    specs = [pl.BlockSpec((o.shape[0] // steps,) + o.shape[1:], (lambda n: lambda i, *_: (i,) + (0,) * n)(o.ndim - 1))
             for o in outs]
    return pl.pallas_call(
        functools.partial(kernel, [len(group) for group in groups]),
        grid_spec=pltpu.PrefetchScalarGridSpec(
            num_scalar_prefetch=len(scalars), grid=(steps,),
            in_specs=[pl.BlockSpec(memory_space=pltpu.VMEM)] * len(args), out_specs=specs),
        out_shape=outs,
        compiler_params=pltpu.CompilerParams(
            dimension_semantics=("arbitrary",),
            vmem_limit_bytes=4 * MIB + sum(a.size * a.dtype.itemsize for a in args)
            + sum(o.size * o.dtype.itemsize for o in outs)),
        cost_estimate=pl.CostEstimate(flops=0, transcendentals=0, bytes_accessed=12000000),
        name=name,
    )(*scalars, *(in_vmem(a) for a in args))


def swap(value, bit, axis, size):
    return lax.ppermute(value, axis, [(i, i ^ bit) for i in range(size)])


def near(value):
    return swap(value, 1, "mp", PARTS)


def far(value):
    return swap(value, 2, "mp", PARTS)


def spread(value):
    there = far(value)
    return (value, near(value), there, near(there))


def chip_sum(keep, send):
    got = near(send)
    lo = keep[:, :QUARTER].astype(F32) + got[:, :QUARTER].astype(F32)
    hi = keep[:, QUARTER:].astype(F32) + got[:, QUARTER:].astype(F32)
    return lo, hi.astype(BF16)


def far_sum_kernel(own, got, out):
    for to, other in ((LO, HI), (HI, LO)):
        out[:, to] = (own[:, to].astype(F32) + got[:, other].astype(F32)).astype(BF16)


def far_sum(own, got):
    return call(far_sum_kernel, None, (), (own, got), [(own.shape, BF16)], [], "far_sum", 6)[0]


def pair_sum_kernel(keep, got, out):
    out[...] = (keep[...] + got[...].astype(F32)).astype(BF16)


def pair_sum(keep, send):
    return call(pair_sum_kernel, None, (), (keep, near(send)), [(send.shape, BF16)], [], "pair_sum", 6)[0]


def late(value, *others):
    return lax.optimization_barrier((value, *others))[0]


def doubled(stack, bit, size):
    return jnp.concatenate([stack, swap(stack, bit, "dp", size)], axis=0)


def entry_of(slot, place, size):
    bits = size.bit_length() - 1
    apart = slot ^ place
    return sum(((apart >> b) & 1) << (bits - 1 - b) for b in range(bits))


def shards(dp, residual, attention_gain, query_matrix, key_value_matrix, output_matrix, feedfwd_gain,
           gate_up_matrix, down_matrix, attention_adapter_input, query_adapter_output,
           key_value_adapter_output, output_adapter_input, output_adapter_output, feedfwd_adapter_input,
           feedfwd_adapter_output, down_adapter_input, down_adapter_output, lengths, adapter_index,
           dealing_slots, cotangent):
    seqs = residual.shape[0]
    length = cotangent.shape[1]
    units = down_matrix.shape[0]
    adapters = attention_adapter_input.shape[0]
    q_cols = query_matrix.shape[1]
    kv_cols = key_value_matrix.shape[2]
    kv_heads = kv_cols // HEAD
    heads = q_cols // HEAD
    rows = length // CHUNKS
    half = 2 * QUARTER
    me = lax.axis_index("mp")
    place = lax.axis_index("dp")

    is_there = dealing_slots[None, :] == jnp.arange(seqs, dtype=jnp.int32)[:, None]
    owners = jnp.sum(jnp.where(is_there, adapter_index[None, :], 0), axis=1)
    spans = jnp.sum(jnp.where(is_there, lengths[None, :], 0), axis=1)
    mine = jnp.arange(seqs, dtype=jnp.int32) == place
    my_length = jnp.sum(jnp.where(mine, spans, 0))
    my_adapter = jnp.sum(jnp.where(mine, owners, 0))
    info = jnp.stack([me.astype(jnp.int32), my_length, my_adapter, place.astype(jnp.int32)])

    gs = spread(cotangent[0])
    gains = jnp.stack(spread(jnp.stack([attention_gain, feedfwd_gain])))
    dealt = lax.all_to_all(
        move_rows(deal_kernel, residual, dealing_slots, "deal"), "dp", split_axis=0, concat_axis=1, tiled=True
    )[0]
    dealt = late(dealt, gs[2])
    beside = near(dealt)
    there = [far(dealt[c * rows:(c + 1) * rows]) for c in range(CHUNKS)]
    xs = [None] * CHUNKS
    cos_np, sin_np = rope_tables(length)
    cos = [jnp.asarray(cos_np[:, c * rows:(c + 1) * rows]) for c in range(CHUNKS)]
    sin = [jnp.asarray(sin_np[:, c * rows:(c + 1) * rows]) for c in range(CHUNKS)]
    a1, qb, kvb, oa, ob, a2, fba, da, bd = (
        lax.dynamic_index_in_dim(v, my_adapter, 0, keepdims=False) for v in (
            attention_adapter_input, query_adapter_output, key_value_adapter_output, output_adapter_input,
            output_adapter_output, feedfwd_adapter_input, feedfwd_adapter_output, down_adapter_input,
            down_adapter_output))
    wq, wkv, wo, wgu, wd = query_matrix, key_value_matrix, output_matrix, gate_up_matrix, down_matrix

    def like(*arrays):
        return [(a.shape, a.dtype) for a in arrays]

    wide, col, block, thin = (rows, WIDTH), (rows, half), (rows, QUARTER), (rows, 1)
    saved = [None] * CHUNKS
    order = ()
    for c in range(CHUNKS):
        xs[c] = (dealt, beside, there[c], near(late(there[c], *order)))
        outs = [(wide, BF16), ((3 * RANK, rows), BF16), ((q_cols, rows), BF16), ((kv_heads, rows, HEAD), BF16),
                ((kv_heads, rows, HEAD), BF16), ((kv_cols, rows), BF16), ((kv_cols, rows), BF16)]
        saved[c] = call(
            functools.partial(project_kernel, c), info, (wq, wkv), (*xs[c], gains, a1, qb, kvb, cos[c], sin[c]), outs,
            like(wq, wkv), "project_%d" % c, 12, order, (2,))
        order = (saved[c][1],)

    kept, z_own = [None] * CHUNKS, [None] * CHUNKS
    for c in reversed(range(CHUNKS)):
        outs = [(col, F32), (col, BF16), ((q_cols, rows), BF16), ((heads, rows), F32), ((RANK, rows), BF16)]
        pairs = [v for p in saved[:c + 1] for v in (p[3], p[6])]
        z_keep, z_send, *kept[c] = call(
            functools.partial(attend_kernel, c), info, (wo,), (saved[c][2], oa, ob, *pairs), outs, like(wo),
            "attend_%d" % c, 10, order, (1,))
        z_own[c] = pair_sum(z_keep, z_send)
        order = (kept[c][1], z_own[1])
    z_far = [far(v) for v in z_own]

    def front(c, total, partial, order):
        hidden = (rows, units)
        outs = [(wide, BF16), (block, F32), (wide, BF16), (wide, BF16), (hidden, BF16), (hidden, BF16), (hidden, BF16),
                ((rows, 2 * RANK), BF16), ((rows, RANK), BF16),
                ((3 * RANK * units // QUARTER, QUARTER), F32 if c else BF16)]
        return call(
            functools.partial(front_kernel, c, c == 0), info, (wgu, wd),
            (*xs[c], total, near(total), *gs, gains, a2, bd, fba, da, *partial), outs,
            [((ROW_BLOCK, WIDTH), F32)] + like(wgu, wd),
            "front_%d" % c, 34, order, (2, units // QUARTER))

    def back(c, hidden, partial, order):
        first, second = (col, col) if c else ((rows + 3 * RANK, half), (length, half))
        outs = [(first, F32), (first, BF16), (second, F32), (second, BF16)]
        outs += [((3 * RANK, WIDTH), F32)] if c else []
        return call(
            functools.partial(back_kernel, c == 0), info, (wgu, wd), (*hidden[2:7], a2, bd, fba, da, *partial), outs,
            [(block, F32), ((3 * RANK, QUARTER), F32)] + like(wgu, wd), "back_%d" % c, 32, order, (2, PARTS))

    def attend_back(c, total, partial, order):
        padded = (rows if c else rows + 4 * RANK, half + LANES)
        outs = [(block, F32), (padded, F32), (padded, BF16), (thin, F32), ((3 * RANK, QUARTER), F32 if c else BF16)]
        outs += [((4 * RANK, WIDTH), F32), ((kv_cols, rows), F32), ((kv_cols, rows), F32)] if c else []
        scratch = [(wide, BF16), ((ROW_BLOCK, WIDTH), F32), ((q_cols, rows), BF16), ((q_cols, rows), F32),
                   ((c + 1, kv_cols, rows), F32), ((c + 1, kv_cols, rows), F32), ((rows, q_cols + 2 * kv_cols), BF16),
                   (block, F32), ((4 * RANK, QUARTER), F32)]
        triples = [v for p in saved[:c + 1] for v in (p[3], p[4], p[5])]
        return call(
            functools.partial(attend_back_kernel, c, c == 0), info, (wq, wkv, wo),
            (*xs[c], *gs, hidden[c][0], total, near(total), gains, a1, qb, kvb, oa, ob, cos[c], sin[c], *saved[c][:3],
             *kept[c], *triples, *partial), outs, scratch + like(wq, wkv, wo), "attend_back_%d" % c, 18, order, (3,))

    bits = [1 << b for b in reversed(range(dp.bit_length() - 1))]
    hidden, d_own, d_far = ([None] * CHUNKS for _ in range(3))
    hidden[1] = front(1, far_sum(z_own[1], z_far[1]), (), order)
    step = hidden[1][8]
    total = far_sum(z_own[0], late(z_far[0], step))
    d_keep, d_send, y_keep, y_send, fa = back(1, hidden[1], (), (step, total))
    d_own[1] = pair_sum(d_keep, d_send)
    d_far[1] = far(d_own[1])
    hidden[0] = front(0, total, hidden[1][9:], (d_own[1],))
    step = hidden[0][8]
    total = far_sum(d_own[1], late(d_far[1], step))
    fb = hidden[0][9][None]
    fb_first = swap(fb, bits[0], "dp", dp)
    d_keep, d_send, y_keep, y_send = back(0, hidden[0], (fa, y_keep, y_send), (step, total))
    d_own[0] = pair_sum(d_keep, late(d_send, fb_first))
    d_far[0] = far(d_own[0])
    fb = fb_more = jnp.concatenate([fb, fb_first], axis=0)
    for bit in bits[1:-1]:
        fb_more = doubled(fb_more, bit, dp)
    fb_more = fb_more[2:]
    fb_side = swap(fb, bits[-1], "dp", dp)
    dxq, h_keep, h_send, inv, *sums = attend_back(1, total, (), (d_own[0],))
    total = far_sum(d_own[0], late(d_far[0], inv))
    h_low, h_high = chip_sum(h_keep, late(h_send, fb_more, fb_side))
    h_far = far(h_high)
    final = [None, (dxq, h_low, h_high, h_far, inv)]
    y_send = late(y_send, inv)
    fa = total[rows:, :QUARTER][None]
    fa_first = swap(fa, bits[0], "dp", dp)
    fb_more_side = swap(fb_more, bits[-1], "dp", dp)
    dxq, h_keep, h_send, inv, att_b = attend_back(0, total, sums, (h_high,))
    h_low, h_high = chip_sum(h_keep, late(h_send, fa_first, fb_more_side, h_far))
    h_far = far(h_high)
    final[0] = (dxq, h_low, h_high, h_far, inv)
    att_a = (h_low[rows:] + h_far[rows:, :QUARTER].astype(F32)).astype(BF16)
    att = jnp.concatenate([att_b, att_a], axis=0)[None]

    dinput, = call(finish_kernel, None, (), (gains, dealt, *(v for f in final for v in f)), [((length, QUARTER), BF16)],
                   [], "finish", 8)
    back_grad = lax.all_to_all(
        dinput.reshape(dp, length // dp, QUARTER), "dp", split_axis=0, concat_axis=0, tiled=True)
    input_grad = move_rows(collect_kernel, back_grad, dealing_slots, "collect_grad")

    valid = (jnp.arange(length, dtype=jnp.int32) < my_length)[:, None]
    y_low, y_high = chip_sum(y_keep, y_send)
    result = jnp.concatenate([h[1] for h in hidden], axis=0) + y_low + far(late(y_high, h_high)).astype(F32)
    result = late(jnp.where(valid, result, 0.0).astype(BF16), dinput)
    back_out = lax.all_to_all(
        result.reshape(dp, length // dp, QUARTER), "dp", split_axis=0, concat_axis=0, tiled=True)
    output = move_rows(collect_kernel, back_out, dealing_slots, "collect_out")

    n_b = att_b.shape[0]
    for bit in bits[:-1]:
        att = doubled(att, bit, dp)
    att_side = swap(att, bits[-1], "dp", dp)
    a_parts = [att[:, n_b:], att_side[:, n_b:]]
    a_far = [far(v) for v in a_parts]
    outs = [sds((adapters, 3 * RANK, WIDTH), F32), sds((adapters, RANK, WIDTH), F32),
            sds((adapters, RANK, q_cols), F32), sds((adapters, 2, RANK, kv_cols), F32),
            sds((adapters, RANK, q_cols), F32)]
    ga_att, g_out_b, g_query_b, g_kv_b, g_out_a = sum_call(
        attention_sum_kernel, (info, owners),
        ((att, att_side), a_parts, [near(v) for v in a_parts], a_far, [near(v) for v in a_far]), outs, "attention_sum")

    fa = late(jnp.concatenate([fa, fa_first], axis=0), h_high)
    for bit in bits[1:]:
        fa = doubled(fa, bit, dp)
    outs = [sds((adapters, 2 * RANK, WIDTH), F32), sds((adapters, RANK, WIDTH), F32),
            sds((adapters, 2, RANK, units), F32), sds((adapters, RANK, units), F32)]
    ga_ffn, g_down_b, g_ffn_b, g_down_a = sum_call(
        feedforward_sum_kernel, (info, owners), ((fb, fb_more, fb_side, fb_more_side), *([v] for v in spread(fa))), outs,
        "feedforward_sum")
    return (output, input_grad, ga_att, g_query_b, g_kv_b, g_out_a, g_out_b, ga_ffn, g_ffn_b, g_down_a, g_down_b)


def solution(mesh):
    in_specs = (
        P(None, "dp", "mp"), P("mp"), P(None, "mp"), P(None, None, "mp"), P("mp", None), P("mp"),
        P(None, None, "mp"), P("mp", None), P(), P(None, None, "mp"), P(None, None, None, "mp"),
        P(None, None, "mp"), P(), P(), P(None, None, None, "mp"), P(None, None, "mp"), P(), P(), P(), P(),
        P("dp", None, "mp"),
    )
    out_specs = (
        P(None, "dp", "mp"), P(None, "dp", "mp"), P(), P(None, None, "mp"), P(None, None, None, "mp"),
        P(None, None, "mp"), P(), P(), P(None, None, None, "mp"), P(None, None, "mp"), P(),
    )
    return jax.shard_map(
        functools.partial(shards, mesh.shape["dp"]), mesh=mesh, in_specs=in_specs, out_specs=out_specs,
        check_vma=False)
```

profile of v0, /device:TPU:0, one launch (start us, length us, event | category | flops | bytes accessed | tf_op | source)
XLA Modules:
  0.0 252.6 jit_solution(4336804771385959531)
XLA Ops:
  0.7 1.2 copy-done.9
  2.6 1.4 deal.1
  4.0 7.3 %all-to-all-start = ((bf16[8,64,512]{2,1,0:T(8,128)(2,1)}), bf16[8,64,512]{2,1,0:T(8,128)(2,1)S(1)}, u32[]{:S(2)}, u32[]{:S(2)}) async-start(bf16[8,64,512]{2,1,0:T(8,128)(2,1)} %deal.1), calls=%async_computation | async-start | bytes 1048576 | tf_op jit(solution)/shard_map/all_to_all | solution.py:683
  11.2 1.6 collective-permute-start
  17.0 0.7 dynamic-slice_bitcast_fusion.7.refs_9_.refs_17_
  17.7 7.0 %collective-permute-done.refs_11_.refs_10_ = bf16[512,512]{1,0:T(8,128)(2,1)S(1)} collective-permute-done((bf16[512,512]{1,0:T(8,128)(2,1)S(1)}, bf16[512,512]{1,0:T(8,128)(2,1)S(1)}, u32[]{:S(2)}, u32[]{:S(2)}) %collective-permute-start) | collective-permute-done | bytes 524320 | tf_op jit(solution)/shard_map/ppermute | solution.py:601
  24.7 1.0 all-to-all-done
  25.7 0.7 fusion.6
  26.5 1.5 collective-permute-start.2
  29.2 5.2 %collective-permute-done.2.refs_5_.refs_6_ = bf16[256,512]{1,0:T(8,128)(2,1)} collective-permute-done((bf16[256,512]{1,0:T(8,128)(2,1)S(1)}, bf16[256,512]{1,0:T(8,128)(2,1)}, u32[]{:S(2)}, u32[]{:S(2)}) %collective-permute-start.2) | collective-permute-done | bytes 262176 | tf_op jit(solution)/shard_map/ppermute | solution.py:601
  35.0 1.4 pad_add_fusion.refs_0_.info
  36.4 4.5 %project_0.1 = (bf16[256,2048]{1,0:T(8,128)(2,1)S(1)}, bf16[48,256]{1,0:T(8,128)(2,1)S(1)}, bf16[512,256]{1,0:T(8,128)(2,1)S(1)}, bf16[2,256,64]{2,1,0:T(8,128)(...) custom-call(s32[4]{0:T(128)S(1)} %pad_add_fusion.refs_0_.info, ...), custom_call_target="tpu_custom_call" | custom-call | flops 1000 | bytes 1000 | tf_op jit(solution)/shard_map/project_0/pallas_call | solution.py:567
  41.0 0.7 dynamic-slice_bitcast_fusion.6.refs_3_.refs_19_
  41.8 0.8 dynamic-slice_bitcast_fusion.5.refs_4_.refs_20_
  42.6 4.1 %project_1.1 = (bf16[256,2048]{1,0:T(8,128)(2,1)S(1)}, bf16[48,256]{1,0:T(8,128)(2,1)S(1)}, bf16[512,256]{1,0:T(8,128)(2,1)S(1)}, bf16[2,256,64]{2,1,0:T(8,128)(...) custom-call(s32[4]{0:T(128)S(1)} %pad_add_fusion.refs_0_.info, ...), custom_call_target="tpu_custom_call" | custom-call | flops 1000 | bytes 1000 | tf_op jit(solution)/shard_map/project_1/pallas_call | solution.py:567
  46.7 5.0 %attend_1.1 = (f32[256,1024]{1,0:T(8,128)S(1)}, bf16[256,1024]{1,0:T(8,128)(2,1)S(1)}, bf16[512,256]{1,0:T(8,128)(2,1)S(1)}, f32[8,256]{1,0:T(8,128)S(1)}, bf16[16,256]{1,0:T(8,128)(2,1)S(1)}) custom-call(s32[4]{0:T(128)S(1)} %pad_add_fusion.refs_0_.info, bf16[512,2048]{1,0:T(8,128)(2,1)} %refs_3_.3, ...), custom_call_target="tpu_custom_call" | custom-call | flops 1000 | bytes 1000 | tf_op jit(solution)/shard_map/attend_1/pallas_call | solution.py:567
  52.3 1.5 collective-permute-done.9.refs_1_
  54.0 2.7 %collective-permute-start.12 = (bf16[256,1024]{1,0:T(8,128)(2,1)S(1)}, bf16[256,1024]{1,0:T(8,128)(2,1)S(1)}, u32[]{:S(2)}, u32[]{:S(2)}) collective-permute-start(bf16[256,1024]{1,0:T(8,128)(2,1)S(1)} %pair_sum.4.refs_8_.refs_0_.refs_19_), channel_id=1, source_target_pairs={{0,2},{1,3},{2,0},{3,1},{4,6},{5,7},{6,4},{7,5},{8,10},{9,11},{10,... | collective-permute-start | bytes 1572872 | tf_op jit(solution)/shard_map/ppermute | solution.py:601
  56.6 4.3 %attend_0.1 = (f32[256,1024]{1,0:T(8,128)S(1)}, bf16[256,1024]{1,0:T(8,128)(2,1)S(1)}, bf16[512,256]{1,0:T(8,128)(2,1)S(1)}, f32[8,256]{1,0:T(8,128)S(1)}, bf16[16,256]{1,0:T(8,128)(2,1)S(1)}) custom-call(s32[4]{0:T(128)S(1)} %pad_add_fusion.refs_0_.info, bf16[512,2048]{1,0:T(8,128)(2,1)} %refs_3_.3, ...), custom_call_target="tpu_custom_call" | custom-call | flops 1000 | bytes 1000 | tf_op jit(solution)/shard_map/attend_0/pallas_call | solution.py:567
  61.6 7.5 %collective-permute-done.12.refs_1_ = bf16[256,1024]{1,0:T(8,128)(2,1)S(1)} collective-permute-done((bf16[256,1024]{1,0:T(8,128)(2,1)S(1)}, bf16[256,1024]{1,0:T(8,128)(2,1)S(1)}, u32[]{:S(2)}, u32[]{:S(2)}) %collective-permute-start.12) | collective-permute-done | bytes 524320 | tf_op jit(solution)/shard_map/ppermute | solution.py:601
  69.5 1.8 collective-permute-start.11
  71.3 0.9 dynamic-slice_bitcast_fusion.1.refs_16_.refs_10_
  72.2 0.9 dynamic-slice_bitcast_fusion.2.refs_14_.refs_8_
  73.1 0.9 dynamic-slice_bitcast_fusion.3
  74.1 13.0 %front_1.1 = (bf16[256,2048]{1,0:T(8,128)(2,1)S(1)}, f32[256,512]{1,0:T(8,128)S(1)}, bf16[256,2048]{1,0:T(8,128)(2,1)S(1)}, bf16[256,2048]{1,0:T(8,128)(2,1)S(1)...) custom-call(s32[4]{0:T(128)S(1)} %pad_add_fusion.refs_0_.info, ...), custom_call_target="tpu_custom_call" | custom-call | flops 1000 | bytes 1000 | tf_op jit(solution)/shard_map/front_1/pallas_call | solution.py:567
  87.3 13.1 %back_1.1 = (f32[256,1024]{1,0:T(8,128)S(1)}, bf16[256,1024]{1,0:T(8,128)(2,1)S(1)}, f32[256,1024]{1,0:T(8,128)S(1)}, bf16[256,1024]{1,0:T(8,128)(2,1)S(1)}, f32[48,2048]{1,0:T(8,128)S(1)}) custom-call(s32[4]{0:T(128)S(1)} %pad_add_fusion.refs_0_.info, bf16[2,2048,2048]{2,1,0:T(8,128)(2,1)} %refs_1_.17, bf16[2048,2048]{1,0:T(8,128)(2,1)} %refs_2_.13, ...), custom_call_target="tpu_custom_call" | custom-call | flops 1000 | bytes 1000 | tf_op jit(solution)/shard_map/back_1/pallas_call | solution.py:567
  101.0 1.4 collective-permute-done.17.refs_1_
  103.2 13.7 %front_0.1 = (bf16[256,2048]{1,0:T(8,128)(2,1)S(1)}, f32[256,512]{1,0:T(8,128)S(1)}, bf16[256,2048]{1,0:T(8,128)(2,1)S(1)}, bf16[256,2048]{1,0:T(8,128)(2,1)S(1)...) custom-call(s32[4]{0:T(128)S(1)} %pad_add_fusion.refs_0_.info, ...), custom_call_target="tpu_custom_call" | custom-call | flops 1000 | bytes 1000 | tf_op jit(solution)/shard_map/front_0/pallas_call | solution.py:567
  116.9 0.8 copy-done.12
  117.7 1.5 collective-permute-start.20
  119.4 13.7 %back_0.1 = (f32[304,1024]{1,0:T(8,128)S(1)}, bf16[304,1024]{1,0:T(8,128)(2,1)S(1)}, f32[512,1024]{1,0:T(8,128)S(1)}, bf16[512,1024]{1,0:T(8,128)(2,1)S(1)}) custom-call(s32[4]{0:T(128)S(1)} %pad_add_fusion.refs_0_.info, bf16[2,2048,2048]{2,1,0:T(8,128)(2,1)} %refs_1_.17, bf16[2048,2048]{1,0:T(8,128)(2,1)} %refs_2_.13, ...), custom_call_target="tpu_custom_call" | custom-call | flops 1000 | bytes 1000 | tf_op jit(solution)/shard_map/back_0/pallas_call | solution.py:567
  133.8 1.3 collective-permute-start.26
  135.0 2.2 collective-permute-start.25
  137.3 1.5 collective-permute-start.23
  138.8 12.4 %attend_back_1.1 = (f32[256,512]{1,0:T(8,128)S(1)}, f32[256,1152]{1,0:T(8,128)S(1)}, bf16[256,1152]{1,0:T(8,128)(2,1)S(1)}, f32[256,1]{1,0:T(8,128)S(1)}, f32[48...) custom-call(s32[4]{0:T(128)S(1)} %pad_add_fusion.refs_0_.info, ...), custom_call_target="tpu_custom_call" | custom-call | flops 1000 | bytes 1000 | tf_op jit(solution)/shard_map/attend_back_1/pallas_call | solution.py:567
  151.4 1.5 collective-permute-done.23.refs_1_
  153.6 1.5 collective-permute-start.30
  155.1 1.5 collective-permute-start.28
  156.6 11.1 %attend_back_0.1 = (f32[256,512]{1,0:T(8,128)S(1)}, f32[320,1152]{1,0:T(8,128)S(1)}, bf16[320,1152]{1,0:T(8,128)(2,1)S(1)}, f32[256,1]{1,0:T(8,128)S(1)}, bf16[48,512]{1,0:T(8,128)(2,1)S(1)}) custom-call(s32[4]{0:T(128)S(1)} %pad_add_fusion.refs_0_.info, bf16[2048,512]{1,0:T(8,128)(2,1)} %refs_1_.19, bf16[2,2048,128]{2,1,0:T(8,128)(2,1)} %refs_2_.15, ...), custom_call_target="tpu_custom_call" | custom-call | flops 1000 | bytes 1000 | tf_op jit(solution)/shard_map/attend_back_0/pallas_call | solution.py:567
  169.0 1.1 collective-permute-done.31
  170.9 1.1 add_convert_fusion
  172.4 1.4 collective-permute-start.32
  174.5 8.0 %collective-permute-done.33.refs_5_ = bf16[320,640]{1,0:T(8,128)(2,1)S(1)} collective-permute-done((bf16[320,640]{1,0:T(8,128)(2,1)S(1)}, bf16[320,640]{1,0:T(8,128)(2,1)S(1)}, u32[]{:S(2)}, u32[]{:S(2)}) %collective-permute-start.33) | collective-permute-done | bytes 409632 | tf_op jit(solution)/shard_map/ppermute | solution.py:601
  182.6 1.2 finish.1
  183.8 3.9 %all-to-all-start.2 = ((bf16[8,64,512]{2,1,0:T(8,128)(2,1)}), bf16[8,64,512]{2,1,0:T(8,128)(2,1)S(1)}, u32[]{:S(2)}, u32[]{:S(2)}) async-start(bf16[8,64,512]{2,1,0:T(8,128)(2,1)} %bitcast.22), calls=%async_computation.2 | async-start | bytes 1048576 | tf_op jit(solution)/shard_map/all_to_all | solution.py:797
  187.7 3.0 %collective-permute-start.34 = (bf16[1,112,512]{2,1,0:T(8,128)(2,1)S(1)}, bf16[1,112,512]{2,1,0:T(8,128)(2,1)S(1)}, u32[]{:S(2)}, u32[]{:S(2)}) collective-permute-start(bf16[1,112,512]{2,1,0:T(8,128)(2,1)S(1)} %maximum_bitcast_fusion), channel_id=1, source_target_pairs={{0,16},{4,20},{8,24},{12,28},{16,0},{20,4},{24,8},{28,12},{1,17},{... | collective-permute-start | bytes 344072 | tf_op jit(solution)/shard_map/ppermute | solution.py:601
  191.4 1.5 collective-permute-start.44
  192.9 13.4 %collective-permute-done.34 = bf16[1,112,512]{2,1,0:T(8,128)(2,1)S(1)} collective-permute-done((bf16[1,112,512]{2,1,0:T(8,128)(2,1)S(1)}, bf16[1,112,512]{2,1,0:T(8,128)(2,1)S(1)}, u32[]{:S(2)}, u32[]{:S(2)}) %collective-permute-start.34) | collective-permute-done | bytes 114720 | tf_op jit(solution)/shard_map/ppermute | solution.py:601
  206.5 2.6 %fusion.2 = bf16[512,512]{1,0:T(8,128)(2,1)} fusion(f32[256,512]{1,0:T(8,128)S(1)} %copy-done.11, f32[256,512]{1,0:T(8,128)S(1)} %copy-done.13, bf16[512,512]{1,0:T(8,128)(2,1)} %collective-permute-done.32, f32[512,1024]{1,0:T(8,128)} %copy-done.5, bf16[512,1024]{1,0:T(8,128)(2,1)} %copy-done.26, pred[512]{0:T(512)(128)(4,1)S(1)} %iota_compare_fusion.1), kind=kLoop, calls=%fused_computation.3 | loop fusion | flops 2097152 | bytes 3670528 | tf_op jit(solution)/shard_map/convert_element_type | solution.py:804
  209.1 3.4 %collective-permute-done.35 = bf16[2,112,512]{2,1,0:T(8,128)(2,1)S(1)} collective-permute-done((bf16[2,112,512]{2,1,0:T(8,128)(2,1)S(1)}, bf16[2,112,512]{2,1,0:T(8,128)(2,1)S(1)}, u32[]{:S(2)}, u32[]{:S(2)}) %collective-permute-start.35) | collective-permute-done | bytes 229408 | tf_op jit(solution)/shard_map/ppermute | solution.py:601
  212.5 1.5 collective-permute-start.36
  214.0 3.6 %all-to-all-start.1 = ((bf16[8,64,512]{2,1,0:T(8,128)(2,1)}), bf16[8,64,512]{2,1,0:T(8,128)(2,1)S(1)}, u32[]{:S(2)}, u32[]{:S(2)}) async-start(bf16[8,64,512]{2,1,0:T(8,128)(2,1)} %bitcast.53), calls=%async_computation.1 | async-start | bytes 1048576 | tf_op jit(solution)/shard_map/all_to_all | solution.py:805
  217.5 0.9 constant_dynamic-update-slice_fusion.1
  218.4 0.9 constant_dynamic-update-slice_fusion.refs_4_
  220.7 1.4 collective-permute-start.39
  222.2 3.9 %collective-permute-done.36.refs_1_ = bf16[4,112,512]{2,1,0:T(8,128)(2,1)S(1)} collective-permute-done((bf16[4,112,512]{2,1,0:T(8,128)(2,1)S(1)}, bf16[4,112,512]{2,1,0:T(8,128)(2,1)S(1)}, u32[]{:S(2)}, u32[]{:S(2)}) %collective-permute-start.36) | collective-permute-done | bytes 458784 | tf_op jit(solution)/shard_map/ppermute | solution.py:601
  227.4 4.1 %collective-permute-done.46.refs_6_ = bf16[8,48,512]{2,1,0:T(8,128)(2,1)S(1)} collective-permute-done((bf16[8,48,512]{2,1,0:T(8,128)(2,1)S(1)}, bf16[8,48,512]{2,1,0:T(8,128)(2,1)S(1)}, u32[]{:S(2)}, u32[]{:S(2)}) %collective-permute-start.46) | collective-permute-done | bytes 393248 | tf_op jit(solution)/shard_map/ppermute | solution.py:601
  232.0 4.8 %collective-permute-done.39.refs_6_ = bf16[4,64,512]{2,1,0:T(8,128)(2,1)} collective-permute-done((bf16[4,64,512]{2,1,0:T(8,128)(2,1)}, bf16[4,64,512]{2,1,0:T(8,128)(2,1)}, u32[]{:S(2)}, u32[]{:S(2)}) %collective-permute-start.39) | collective-permute-done | bytes 262176 | tf_op jit(solution)/shard_map/ppermute | solution.py:601
  237.3 2.3 collective-permute-done.40.refs_7_
  239.7 1.0 copy-done.19
  240.6 4.0 %feedforward_sum.1 = (f32[8,32,2048]{2,1,0:T(8,128)}, f32[8,16,2048]{2,1,0:T(8,128)}, f32[8,2,16,2048]{3,2,1,0:T(8,128)}, f32[8,16,2048]{2,1,0:T(8,128)}) custom-call(s32[4]{0:T(128)S(1)} %pad_add_fusion.refs_0_.info, s32[8]{0:T(128)S(1)} %get-tuple-element.182.owners, bf16[2,192,512]{2,1,0:T(8,128)(2,1)S(1)} %copy-done.7, ...), custom_call_target="tpu_custom_call" | custom-call | bytes 12000000 | tf_op jit(solution)/shard_map/feedforward_sum/pallas_call | solution.py:585
  244.6 1.4 collect_grad.1
  246.0 1.4 collect_out.1
  247.5 5.0 %attention_sum.1 = (f32[8,48,2048]{2,1,0:T(8,128)}, f32[8,16,2048]{2,1,0:T(8,128)}, f32[8,16,512]{2,1,0:T(8,128)}, f32[8,2,16,128]{3,2,1,0:T(8,128)}, f32[8,16,512]{2,1,0:T(8,128)}) custom-call(s32[4]{0:T(128)S(1)} %pad_add_fusion.refs_0_.info, s32[8]{0:T(128)S(1)} %get-tuple-element.182.owners, bf16[4,112,512]{2,1,0:T(8,128)(2,1)S(1)} %pad_maximum_fusion.refs_0_, ...), custom_call_target="tpu_custom_call" | custom-call | bytes 12000000 | tf_op jit(solution)/shard_map/attention_sum/pallas_call | solution.py:585
  (164 shorter events, 17.5 us)
Async XLA Ops:
  0.6 28.0 %copy-start = (bf16[8,48,2048]{2,1,0:T(8,128)(2,1)S(1)}, bf16[8,48,2048]{2,1,0:T(8,128)(2,1)}, u32[]{:S(2)}) copy-start(bf16[8,48,2048]{2,1,0:T(8,128)(2,1)} %param.33) | copy-start | bytes 4718596
  2.5 33.9 %copy-start.20 = (f32[32,256]{1,0:T(8,128)S(1)}, f32[32,256]{1,0:T(8,128)}, u32[]{:S(2)}) copy-start(f32[32,256]{1,0:T(8,128)} %constant.54.clone.refs_12_.refs_22_) | copy-start | bytes 98308
  2.6 33.9 %copy-start.21 = (f32[32,256]{1,0:T(8,128)S(1)}, f32[32,256]{1,0:T(8,128)}, u32[]{:S(2)}) copy-start(f32[32,256]{1,0:T(8,128)} %constant.52.clone.refs_11_.refs_21_) | copy-start | bytes 98308
  4.0 21.8 %all-to-all-start = ((bf16[8,64,512]{2,1,0:T(8,128)(2,1)}), bf16[8,64,512]{2,1,0:T(8,128)(2,1)S(1)}, u32[]{:S(2)}, u32[]{:S(2)}) async-start(bf16[8,64,512]{2,1,0:T(8,128)(2,1)} %deal.1), calls=%async_computation | async-start | bytes 1048576 | tf_op jit(solution)/shard_map/all_to_all | solution.py:683
  11.2 13.5 %collective-permute-start = (bf16[512,512]{1,0:T(8,128)(2,1)S(1)}, bf16[512,512]{1,0:T(8,128)(2,1)S(1)}, u32[]{:S(2)}, u32[]{:S(2)}) collective-permute-start(bf16[512,512]{1,0:T(8,128)(2,1)S(1)} %bitcast.45), channel_id=1, source_target_pairs={{0,2},{1,3},{2,0},{3,1},{4,6},{5,7},{6,4},{7,5},{8,10},{9,11},{10,... | collective-permute-start | bytes 1572872 | tf_op jit(solution)/shard_map/ppermute | solution.py:601
  12.9 23.5 %collective-permute-start.4 = (bf16[2,512]{1,0:T(2,128)(2,1)S(1)}, bf16[2,512]{1,0:T(2,128)(2,1)S(1)}, u32[]{:S(2)}, u32[]{:S(2)}) collective-permute-start(bf16[2,512]{1,0:T(2,128)(2,1)S(1)} %pad_maximum_fusion.6), channel_id=1, source_target_pairs={{0,1},{1,0},{2,3},{3,2},{4,5},{5,4},{6,7},{7,6},{8,9},{9,8},{10,11... | collective-permute-start | bytes 6152 | tf_op jit(solution)/shard_map/ppermute | solution.py:601
  12.9 21.4 %collective-permute-start.5 = (bf16[2,512]{1,0:T(2,128)(2,1)S(1)}, bf16[2,512]{1,0:T(2,128)(2,1)S(1)}, u32[]{:S(2)}, u32[]{:S(2)}) collective-permute-start(bf16[2,512]{1,0:T(2,128)(2,1)S(1)} %pad_maximum_fusion.6), channel_id=1, source_target_pairs={{0,2},{1,3},{2,0},{3,1},{4,6},{5,7},{6,4},{7,5},{8,10},{9,11},{10,... | collective-permute-start | bytes 6152 | tf_op jit(solution)/shard_map/ppermute | solution.py:601
  26.5 7.9 %collective-permute-start.2 = (bf16[256,512]{1,0:T(8,128)(2,1)S(1)}, bf16[256,512]{1,0:T(8,128)(2,1)}, u32[]{:S(2)}, u32[]{:S(2)}) collective-permute-start(bf16[256,512]{1,0:T(8,128)(2,1)S(1)} %get-tuple-element.183), channel_id=1, source_target_pairs={{0,2},{1,3},{2,0},{3,1},{4,6},{5,7},{6,4},{7,5},{8,10},{9,11},{10,... | collective-permute-start | bytes 786440 | tf_op jit(solution)/shard_map/ppermute | solution.py:601
  28.6 7.8 %collective-permute-start.1 = (bf16[512,512]{1,0:T(8,128)(2,1)S(1)}, bf16[512,512]{1,0:T(8,128)(2,1)S(1)}, u32[]{:S(2)}, u32[]{:S(2)}) collective-permute-start(bf16[512,512]{1,0:T(8,128)(2,1)S(1)} %bitcast.37), channel_id=1, source_target_pairs={{0,1},{1,0},{2,3},{3,2},{4,5},{5,4},{6,7},{7,6},{8,9},{9,8},{10,11... | collective-permute-start | bytes 1572872 | tf_op jit(solution)/shard_map/ppermute | solution.py:601
  28.6 12.3 %collective-permute-start.7 = (bf16[256,512]{1,0:T(8,128)(2,1)}, bf16[256,512]{1,0:T(8,128)(2,1)S(1)}, u32[]{:S(2)}, u32[]{:S(2)}) collective-permute-start(bf16[256,512]{1,0:T(8,128)(2,1)} %get-tuple-element.184), channel_id=1, source_target_pairs={{0,2},{1,3},{2,0},{3,1},{4,6},{5,7},{6,4},{7,5},{8,10},{9,11},{10,... | collective-permute-start | bytes 786440 | tf_op jit(solution)/shard_map/ppermute | solution.py:601
  34.4 2.0 collective-permute-start.3
  34.4 1.9 collective-permute-start.6
  41.0 1.7 collective-permute-start.8
  51.7 2.1 collective-permute-start.9
  54.0 15.1 %collective-permute-start.12 = (bf16[256,1024]{1,0:T(8,128)(2,1)S(1)}, bf16[256,1024]{1,0:T(8,128)(2,1)S(1)}, u32[]{:S(2)}, u32[]{:S(2)}) collective-permute-start(bf16[256,1024]{1,0:T(8,128)(2,1)S(1)} %pair_sum.4.refs_8_.refs_0_.refs_19_), channel_id=1, source_target_pairs={{0,2},{1,3},{2,0},{3,1},{4,6},{5,7},{6,4},{7,5},{8,10},{9,11},{10,... | collective-permute-start | bytes 1572872 | tf_op jit(solution)/shard_map/ppermute | solution.py:601
  61.0 8.4 %collective-permute-start.10 = (bf16[256,1024]{1,0:T(8,128)(2,1)S(1)}, bf16[256,1024]{1,0:T(8,128)(2,1)S(1)}, u32[]{:S(2)}, u32[]{:S(2)}) collective-permute-start(bf16[256,1024]{1,0:T(8,128)(2,1)S(1)} %get-tuple-element.110), channel_id=1, source_target_pairs={{0,1},{1,0},{2,3},{3,2},{4,5},{5,4},{6,7},{7,6},{8,9},{9,8},{10,11... | collective-permute-start | bytes 1572872 | tf_op jit(solution)/shard_map/ppermute | solution.py:601
  61.1 12.9 %collective-permute-start.14 = (bf16[512,512]{1,0:T(8,128)(2,1)S(1)}, bf16[512,512]{1,0:T(8,128)(2,1)S(1)}, u32[]{:S(2)}, u32[]{:S(2)}) collective-permute-start(bf16[512,512]{1,0:T(8,128)(2,1)S(1)} %bitcast.46), channel_id=1, source_target_pairs={{0,1},{1,0},{2,3},{3,2},{4,5},{5,4},{6,7},{7,6},{8,9},{9,8},{10,11... | collective-permute-start | bytes 1572872 | tf_op jit(solution)/shard_map/ppermute | solution.py:601
  61.6 12.5 %collective-permute-start.15 = (bf16[512,512]{1,0:T(8,128)(2,1)S(1)}, bf16[512,512]{1,0:T(8,128)(2,1)S(1)}, u32[]{:S(2)}, u32[]{:S(2)}) collective-permute-start(bf16[512,512]{1,0:T(8,128)(2,1)S(1)} %copy-done.4), channel_id=1, source_target_pairs={{0,1},{1,0},{2,3},{3,2},{4,5},{5,4},{6,7},{7,6},{8,9},{9,8},{10,11... | collective-permute-start | bytes 1572872 | tf_op jit(solution)/shard_map/ppermute | solution.py:601
  69.3 4.8 %collective-permute-start.13 = (bf16[256,1024]{1,0:T(8,128)(2,1)S(1)}, bf16[256,1024]{1,0:T(8,128)(2,1)S(1)}, u32[]{:S(2)}, u32[]{:S(2)}) collective-permute-start(bf16[256,1024]{1,0:T(8,128)(2,1)S(1)} %far_sum.4.refs_7_), channel_id=1, source_target_pairs={{0,1},{1,0},{2,3},{3,2},{4,5},{5,4},{6,7},{7,6},{8,9},{9,8},{10,11... | collective-permute-start | bytes 1572872 | tf_op jit(solution)/shard_map/ppermute | solution.py:601
  69.5 17.6 %collective-permute-start.11 = (bf16[256,1024]{1,0:T(8,128)(2,1)S(1)}, bf16[256,1024]{1,0:T(8,128)(2,1)S(1)}, u32[]{:S(2)}, u32[]{:S(2)}) collective-permute-start(bf16[256,1024]{1,0:T(8,128)(2,1)S(1)} %pair_sum.5.refs_0_), channel_id=1, source_target_pairs={{0,2},{1,3},{2,0},{3,1},{4,6},{5,7},{6,4},{7,5},{8,10},{9,11},{10,... | collective-permute-start | bytes 1572872 | tf_op jit(solution)/shard_map/ppermute | solution.py:601
  87.1 13.4 %copy-start.10 = (f32[256,512]{1,0:T(8,128)}, f32[256,512]{1,0:T(8,128)S(1)}, u32[]{:S(2)}) copy-start(f32[256,512]{1,0:T(8,128)S(1)} %get-tuple-element.123) | copy-start | bytes 1572868
  100.4 2.0 collective-permute-start.17
  100.7 2.4 collective-permute-start.16
  102.5 16.7 %collective-permute-start.18 = (bf16[256,1024]{1,0:T(8,128)(2,1)S(1)}, bf16[256,1024]{1,0:T(8,128)(2,1)S(1)}, u32[]{:S(2)}, u32[]{:S(2)}) collective-permute-start(bf16[256,1024]{1,0:T(8,128)(2,1)S(1)} %pair_sum.6.refs_19_.refs_0_), channel_id=1, source_target_pairs={{0,2},{1,3},{2,0},{3,1},{4,6},{5,7},{6,4},{7,5},{8,10},{9,11},{10,... | collective-permute-start | bytes 1572872 | tf_op jit(solution)/shard_map/ppermute | solution.py:601
  117.7 15.4 %collective-permute-start.20 = (bf16[1,192,512]{2,1,0:T(8,128)(2,1)S(1)}, bf16[1,192,512]{2,1,0:T(8,128)(2,1)S(1)}, u32[]{:S(2)}, u32[]{:S(2)}) collective-permute-start(bf16[1,192,512]{2,1,0:T(8,128)(2,1)S(1)} %bitcast.51), channel_id=1, source_target_pairs={{0,16},{4,20},{8,24},{12,28},{16,0},{20,4},{24,8},{28,12},{1,17},{... | collective-permute-start | bytes 589832 | tf_op jit(solution)/shard_map/ppermute | solution.py:601
  133.1 37.7 %copy-start.5 = (f32[512,1024]{1,0:T(8,128)}, f32[512,1024]{1,0:T(8,128)S(1)}, u32[]{:S(2)}) copy-start(f32[512,1024]{1,0:T(8,128)S(1)} %get-tuple-element.134) | copy-start | bytes 6291460
  133.1 4.1 %collective-permute-start.21 = (bf16[304,1024]{1,0:T(8,128)(2,1)S(1)}, bf16[304,1024]{1,0:T(8,128)(2,1)S(1)}, u32[]{:S(2)}, u32[]{:S(2)}) collective-permute-start(bf16[304,1024]{1,0:T(8,128)(2,1)S(1)} %get-tuple-element.147), channel_id=1, source_target_pairs={{0,1},{1,0},{2,3},{3,2},{4,5},{5,4},{6,7},{7,6},{8,9},{9,8},{10,11... | collective-permute-start | bytes 1867784 | tf_op jit(solution)/shard_map/ppermute | solution.py:601
  133.2 5.6 %collective-permute-start.19 = (bf16[256,1024]{1,0:T(8,128)(2,1)S(1)}, bf16[256,1024]{1,0:T(8,128)(2,1)S(1)}, u32[]{:S(2)}, u32[]{:S(2)}) collective-permute-start(bf16[256,1024]{1,0:T(8,128)(2,1)S(1)} %far_sum.6.refs_16_.refs_13_), channel_id=1, source_target_pairs={{0,1},{1,0},{2,3},{3,2},{4,5},{5,4},{6,7},{7,6},{8,9},{9,8},{10,11... | collective-permute-start | bytes 1572872 | tf_op jit(solution)/shard_map/ppermute | solution.py:601
  133.8 17.5 %copy-start.6 = (bf16[2,192,512]{2,1,0:T(8,128)(2,1)}, bf16[2,192,512]{2,1,0:T(8,128)(2,1)S(1)}, u32[]{:S(2)}) copy-start(bf16[2,192,512]{2,1,0:T(8,128)(2,1)S(1)} %pad_maximum_fusion.1.refs_0_) | copy-start | bytes 1179652
  133.8 17.5 %collective-permute-start.26 = (bf16[2,192,512]{2,1,0:T(8,128)(2,1)S(1)}, bf16[2,192,512]{2,1,0:T(8,128)(2,1)S(1)}, u32[]{:S(2)}, u32[]{:S(2)}) collective-permute-start(bf16[2,192,512]{2,1,0:T(8,128)(2,1)S(1)} %pad_maximum_fusion.1.refs_0_), channel_id=1, source_target_pairs={{0,4},{4,0},{8,12},{12,8},{16,20},{20,16},{24,28},{28,24},{1,5},{5... | collective-permute-start | bytes 1179656 | tf_op jit(solution)/shard_map/ppermute | solution.py:601
  135.0 16.3 %collective-permute-start.25 = (bf16[2,192,512]{2,1,0:T(8,128)(2,1)S(1)}, bf16[2,192,512]{2,1,0:T(8,128)(2,1)S(1)}, u32[]{:S(2)}, u32[]{:S(2)}) collective-permute-start(bf16[2,192,512]{2,1,0:T(8,128)(2,1)S(1)} %pad_maximum_fusion.1.refs_0_), channel_id=1, source_target_pairs={{0,8},{4,12},{8,0},{12,4},{16,24},{20,28},{24,16},{28,20},{1,9},{5... | collective-permute-start | bytes 1179656 | tf_op jit(solution)/shard_map/ppermute | solution.py:601
  137.3 15.5 %collective-permute-start.23 = (bf16[304,1024]{1,0:T(8,128)(2,1)S(1)}, bf16[304,1024]{1,0:T(8,128)(2,1)S(1)}, u32[]{:S(2)}, u32[]{:S(2)}) collective-permute-start(bf16[304,1024]{1,0:T(8,128)(2,1)S(1)} %pair_sum.7.refs_35_.refs_0_), channel_id=1, source_target_pairs={{0,2},{1,3},{2,0},{3,1},{4,6},{5,7},{6,4},{7,5},{8,10},{9,11},{10,... | collective-permute-start | bytes 1867784 | tf_op jit(solution)/shard_map/ppermute | solution.py:601
  151.3 16.4 %copy-start.16 = (bf16[2,192,512]{2,1,0:T(8,128)(2,1)}, bf16[2,192,512]{2,1,0:T(8,128)(2,1)S(1)}, u32[]{:S(2)}) copy-start(bf16[2,192,512]{2,1,0:T(8,128)(2,1)S(1)} %collective-permute-done.25.refs_1_) | copy-start | bytes 1179652
  151.3 2.2 collective-permute-start.27
  153.0 3.6 %collective-permute-start.24 = (bf16[304,1024]{1,0:T(8,128)(2,1)S(1)}, bf16[304,1024]{1,0:T(8,128)(2,1)S(1)}, u32[]{:S(2)}, u32[]{:S(2)}) collective-permute-start(bf16[304,1024]{1,0:T(8,128)(2,1)S(1)} %far_sum.7.refs_13_), channel_id=1, source_target_pairs={{0,1},{1,0},{2,3},{3,2},{4,5},{5,4},{6,7},{7,6},{8,9},{9,8},{10,11... | collective-permute-start | bytes 1867784 | tf_op jit(solution)/shard_map/ppermute | solution.py:601
  153.1 14.7 %collective-permute-start.29 = (bf16[2,192,512]{2,1,0:T(8,128)(2,1)S(1)}, bf16[2,192,512]{2,1,0:T(8,128)(2,1)S(1)}, u32[]{:S(2)}, u32[]{:S(2)}) collective-permute-start(bf16[2,192,512]{2,1,0:T(8,128)(2,1)S(1)} %collective-permute-done.25.refs_1_), channel_id=1, source_target_pairs={{0,4},{4,0},{8,12},{12,8},{16,20},{20,16},{24,28},{28,24},{1,5},{5... | collective-permute-start | bytes 1179656 | tf_op jit(solution)/shard_map/ppermute | solution.py:601
  153.6 14.2 %collective-permute-start.30 = (bf16[256,640]{1,0:T(8,128)(2,1)S(1)}, bf16[256,640]{1,0:T(8,128)(2,1)S(1)}, u32[]{:S(2)}, u32[]{:S(2)}) collective-permute-start(bf16[256,640]{1,0:T(8,128)(2,1)S(1)} %add_convert_fusion.2.refs_36_.refs_9_), channel_id=1, source_target_pairs={{0,2},{1,3},{2,0},{3,1},{4,6},{5,7},{6,4},{7,5},{8,10},{9,11},{10,... | collective-permute-start | bytes 983048 | tf_op jit(solution)/shard_map/ppermute | solution.py:601
  155.1 12.7 %collective-permute-start.28 = (bf16[1,48,512]{2,1,0:T(8,128)(2,1)S(1)}, bf16[1,48,512]{2,1,0:T(8,128)(2,1)S(1)}, u32[]{:S(2)}, u32[]{:S(2)}) collective-permute-start(bf16[1,48,512]{2,1,0:T(8,128)(2,1)S(1)} %slice_bitcast_fusion), channel_id=1, source_target_pairs={{0,16},{4,20},{8,24},{12,28},{16,0},{20,4},{24,8},{28,12},{1,17},{... | collective-permute-start | bytes 147464 | tf_op jit(solution)/shard_map/ppermute | solution.py:601
  156.6 14.3 %collective-permute-start.22 = (bf16[512,1024]{1,0:T(8,128)(2,1)S(1)}, bf16[512,1024]{1,0:T(8,128)(2,1)S(1)}, u32[]{:S(2)}, u32[]{:S(2)}) collective-permute-start(bf16[512,1024]{1,0:T(8,128)(2,1)S(1)} %get-tuple-element.149), channel_id=1, source_target_pairs={{0,1},{1,0},{2,3},{3,2},{4,5},{5,4},{6,7},{7,6},{8,9},{9,8},{10,11... | collective-permute-start | bytes 3145736 | tf_op jit(solution)/shard_map/ppermute | solution.py:601
  167.8 2.3 collective-permute-start.31
  170.2 12.4 %collective-permute-start.33 = (bf16[320,640]{1,0:T(8,128)(2,1)S(1)}, bf16[320,640]{1,0:T(8,128)(2,1)S(1)}, u32[]{:S(2)}, u32[]{:S(2)}) collective-permute-start(bf16[320,640]{1,0:T(8,128)(2,1)S(1)} %add_convert_fusion.1.refs_4_), channel_id=1, source_target_pairs={{0,2},{1,3},{2,0},{3,1},{4,6},{5,7},{6,4},{7,5},{8,10},{9,11},{10,... | collective-permute-start | bytes 1228808 | tf_op jit(solution)/shard_map/ppermute | solution.py:601
  172.0 18.7 %collective-permute-start.43 = (bf16[2,48,512]{2,1,0:T(8,128)(2,1)S(1)}, bf16[2,48,512]{2,1,0:T(8,128)(2,1)S(1)}, u32[]{:S(2)}, u32[]{:S(2)}) collective-permute-start(bf16[2,48,512]{2,1,0:T(8,128)(2,1)S(1)} %pad_maximum_fusion.4), channel_id=1, source_target_pairs={{0,8},{4,12},{8,0},{12,4},{16,24},{20,28},{24,16},{28,20},{1,9},{5... | collective-permute-start | bytes 294920 | tf_op jit(solution)/shard_map/ppermute | solution.py:601
  172.4 34.1 %collective-permute-start.32 = (bf16[512,512]{1,0:T(8,128)(2,1)}, bf16[512,512]{1,0:T(8,128)(2,1)}, u32[]{:S(2)}, u32[]{:S(2)}) collective-permute-start(bf16[512,512]{1,0:T(8,128)(2,1)} %add_convert_fusion), channel_id=1, source_target_pairs={{0,2},{1,3},{2,0},{3,1},{4,6},{5,7},{6,4},{7,5},{8,10},{9,11},{10,... | collective-permute-start | bytes 1572872 | tf_op jit(solution)/shard_map/ppermute | solution.py:601
  183.8 22.7 %copy-start.11 = (f32[256,512]{1,0:T(8,128)S(1)}, f32[256,512]{1,0:T(8,128)}, u32[]{:S(2)}) copy-start(f32[256,512]{1,0:T(8,128)} %copy-done.10) | copy-start | bytes 1572868
  183.8 22.7 %copy-start.13 = (f32[256,512]{1,0:T(8,128)S(1)}, f32[256,512]{1,0:T(8,128)}, u32[]{:S(2)}) copy-start(f32[256,512]{1,0:T(8,128)} %copy-done.12) | copy-start | bytes 1572868
  183.8 30.2 %all-to-all-start.2 = ((bf16[8,64,512]{2,1,0:T(8,128)(2,1)}), bf16[8,64,512]{2,1,0:T(8,128)(2,1)S(1)}, u32[]{:S(2)}, u32[]{:S(2)}) async-start(bf16[8,64,512]{2,1,0:T(8,128)(2,1)} %bitcast.22), calls=%async_computation.2 | async-start | bytes 1048576 | tf_op jit(solution)/shard_map/all_to_all | solution.py:797
  187.7 18.6 %collective-permute-start.34 = (bf16[1,112,512]{2,1,0:T(8,128)(2,1)S(1)}, bf16[1,112,512]{2,1,0:T(8,128)(2,1)S(1)}, u32[]{:S(2)}, u32[]{:S(2)}) collective-permute-start(bf16[1,112,512]{2,1,0:T(8,128)(2,1)S(1)} %maximum_bitcast_fusion), channel_id=1, source_target_pairs={{0,16},{4,20},{8,24},{12,28},{16,0},{20,4},{24,8},{28,12},{1,17},{... | collective-permute-start | bytes 344072 | tf_op jit(solution)/shard_map/ppermute | solution.py:601
  190.7 21.7 %copy-start.27 = (bf16[2,48,512]{2,1,0:T(8,128)(2,1)}, bf16[2,48,512]{2,1,0:T(8,128)(2,1)S(1)}, u32[]{:S(2)}) copy-start(bf16[2,48,512]{2,1,0:T(8,128)(2,1)S(1)} %collective-permute-done.43) | copy-start | bytes 294916
  191.4 27.0 %collective-permute-start.44 = (bf16[4,48,512]{2,1,0:T(8,128)(2,1)}, bf16[4,48,512]{2,1,0:T(8,128)(2,1)}, u32[]{:S(2)}, u32[]{:S(2)}) collective-permute-start(bf16[4,48,512]{2,1,0:T(8,128)(2,1)} %pad_maximum_fusion.3), channel_id=1, source_target_pairs={{0,4},{4,0},{8,12},{12,8},{16,20},{20,16},{24,28},{28,24},{1,5},{5... | collective-permute-start | bytes 589832 | tf_op jit(solution)/shard_map/ppermute | solution.py:601
  206.3 6.1 %collective-permute-start.35 = (bf16[2,112,512]{2,1,0:T(8,128)(2,1)S(1)}, bf16[2,112,512]{2,1,0:T(8,128)(2,1)S(1)}, u32[]{:S(2)}, u32[]{:S(2)}) collective-permute-start(bf16[2,112,512]{2,1,0:T(8,128)(2,1)S(1)} %pad_maximum_fusion.2), channel_id=1, source_target_pairs={{0,8},{4,12},{8,0},{12,4},{16,24},{20,28},{24,16},{28,20},{1,9},{5... | collective-permute-start | bytes 688136 | tf_op jit(solution)/shard_map/ppermute | solution.py:601
  209.0 30.6 %copy-start.7 = (bf16[2,192,512]{2,1,0:T(8,128)(2,1)S(1)}, bf16[2,192,512]{2,1,0:T(8,128)(2,1)}, u32[]{:S(2)}) copy-start(bf16[2,192,512]{2,1,0:T(8,128)(2,1)} %copy-done.6) | copy-start | bytes 1179652
  209.0 30.6 %copy-start.15 = (bf16[2,192,512]{2,1,0:T(8,128)(2,1)S(1)}, bf16[2,192,512]{2,1,0:T(8,128)(2,1)}, u32[]{:S(2)}) copy-start(bf16[2,192,512]{2,1,0:T(8,128)(2,1)} %copy-done.14) | copy-start | bytes 1179652
  209.0 30.6 %copy-start.17 = (bf16[2,192,512]{2,1,0:T(8,128)(2,1)S(1)}, bf16[2,192,512]{2,1,0:T(8,128)(2,1)}, u32[]{:S(2)}) copy-start(bf16[2,192,512]{2,1,0:T(8,128)(2,1)} %copy-done.16) | copy-start | bytes 1179652
  212.5 13.6 %collective-permute-start.36 = (bf16[4,112,512]{2,1,0:T(8,128)(2,1)S(1)}, bf16[4,112,512]{2,1,0:T(8,128)(2,1)S(1)}, u32[]{:S(2)}, u32[]{:S(2)}) collective-permute-start(bf16[4,112,512]{2,1,0:T(8,128)(2,1)S(1)} %pad_maximum_fusion.refs_0_), channel_id=1, source_target_pairs={{0,4},{4,0},{8,12},{12,8},{16,20},{20,16},{24,28},{28,24},{1,5},{5... | collective-permute-start | bytes 1376264 | tf_op jit(solution)/shard_map/ppermute | solution.py:601
  214.0 32.1 %all-to-all-start.1 = ((bf16[8,64,512]{2,1,0:T(8,128)(2,1)}), bf16[8,64,512]{2,1,0:T(8,128)(2,1)S(1)}, u32[]{:S(2)}, u32[]{:S(2)}) async-start(bf16[8,64,512]{2,1,0:T(8,128)(2,1)} %bitcast.53), calls=%async_computation.1 | async-start | bytes 1048576 | tf_op jit(solution)/shard_map/all_to_all | solution.py:805
  219.4 12.1 %collective-permute-start.46 = (bf16[8,48,512]{2,1,0:T(8,128)(2,1)S(1)}, bf16[8,48,512]{2,1,0:T(8,128)(2,1)S(1)}, u32[]{:S(2)}, u32[]{:S(2)}) collective-permute-start(bf16[8,48,512]{2,1,0:T(8,128)(2,1)S(1)} %constant_dynamic-update-slice_fusion.refs_4_), channel_id=1, source_target_pairs={{0,2},{1,3},{2,0},{3,1},{4,6},{5,7},{6,4},{7,5},{8,10},{9,11},{10,... | collective-permute-start | bytes 1179656 | tf_op jit(solution)/shard_map/ppermute | solution.py:601
  220.0 16.8 %collective-permute-start.45 = (bf16[8,48,512]{2,1,0:T(8,128)(2,1)S(1)}, bf16[8,48,512]{2,1,0:T(8,128)(2,1)S(1)}, u32[]{:S(2)}, u32[]{:S(2)}) collective-permute-start(bf16[8,48,512]{2,1,0:T(8,128)(2,1)S(1)} %constant_dynamic-update-slice_fusion.refs_4_), channel_id=1, source_target_pairs={{0,1},{1,0},{2,3},{3,2},{4,5},{5,4},{6,7},{7,6},{8,9},{9,8},{10,11... | collective-permute-start | bytes 1179656 | tf_op jit(solution)/shard_map/ppermute | solution.py:601
  220.7 16.1 %collective-permute-start.39 = (bf16[4,64,512]{2,1,0:T(8,128)(2,1)}, bf16[4,64,512]{2,1,0:T(8,128)(2,1)}, u32[]{:S(2)}, u32[]{:S(2)}) collective-permute-start(bf16[4,64,512]{2,1,0:T(8,128)(2,1)} %slice.85.refs_2_), channel_id=1, source_target_pairs={{0,2},{1,3},{2,0},{3,1},{4,6},{5,7},{6,4},{7,5},{8,10},{9,11},{10,... | collective-permute-start | bytes 786440 | tf_op jit(solution)/shard_map/ppermute | solution.py:601
  226.8 12.8 %collective-permute-start.40 = (bf16[4,64,512]{2,1,0:T(8,128)(2,1)}, bf16[4,64,512]{2,1,0:T(8,128)(2,1)}, u32[]{:S(2)}, u32[]{:S(2)}) collective-permute-start(bf16[4,64,512]{2,1,0:T(8,128)(2,1)} %slice.86.refs_3_), channel_id=1, source_target_pairs={{0,2},{1,3},{2,0},{3,1},{4,6},{5,7},{6,4},{7,5},{8,10},{9,11},{10,... | collective-permute-start | bytes 786440 | tf_op jit(solution)/shard_map/ppermute | solution.py:601
  231.5 8.1 %collective-permute-start.47 = (bf16[8,48,512]{2,1,0:T(8,128)(2,1)S(1)}, bf16[8,48,512]{2,1,0:T(8,128)(2,1)S(1)}, u32[]{:S(2)}, u32[]{:S(2)}) collective-permute-start(bf16[8,48,512]{2,1,0:T(8,128)(2,1)S(1)} %collective-permute-done.46.refs_6_), channel_id=1, source_target_pairs={{0,1},{1,0},{2,3},{3,2},{4,5},{5,4},{6,7},{7,6},{8,9},{9,8},{10,11... | collective-permute-start | bytes 1179656 | tf_op jit(solution)/shard_map/ppermute | solution.py:601
  231.5 15.9 %collective-permute-start.37 = (bf16[4,64,512]{2,1,0:T(8,128)(2,1)}, bf16[4,64,512]{2,1,0:T(8,128)(2,1)}, u32[]{:S(2)}, u32[]{:S(2)}) collective-permute-start(bf16[4,64,512]{2,1,0:T(8,128)(2,1)} %slice.85.refs_2_), channel_id=1, source_target_pairs={{0,1},{1,0},{2,3},{3,2},{4,5},{5,4},{6,7},{7,6},{8,9},{9,8},{10,11... | collective-permute-start | bytes 786440 | tf_op jit(solution)/shard_map/ppermute | solution.py:601
  236.8 10.6 %collective-permute-start.41 = (bf16[4,64,512]{2,1,0:T(8,128)(2,1)}, bf16[4,64,512]{2,1,0:T(8,128)(2,1)}, u32[]{:S(2)}, u32[]{:S(2)}) collective-permute-start(bf16[4,64,512]{2,1,0:T(8,128)(2,1)} %collective-permute-done.39.refs_6_), channel_id=1, source_target_pairs={{0,1},{1,0},{2,3},{3,2},{4,5},{5,4},{6,7},{7,6},{8,9},{9,8},{10,11... | collective-permute-start | bytes 786440 | tf_op jit(solution)/shard_map/ppermute | solution.py:601
  236.8 10.6 %collective-permute-start.38 = (bf16[4,64,512]{2,1,0:T(8,128)(2,1)}, bf16[4,64,512]{2,1,0:T(8,128)(2,1)}, u32[]{:S(2)}, u32[]{:S(2)}) collective-permute-start(bf16[4,64,512]{2,1,0:T(8,128)(2,1)} %slice.86.refs_3_), channel_id=1, source_target_pairs={{0,1},{1,0},{2,3},{3,2},{4,5},{5,4},{6,7},{7,6},{8,9},{9,8},{10,11... | collective-permute-start | bytes 786440 | tf_op jit(solution)/shard_map/ppermute | solution.py:601
  239.6 7.8 %collective-permute-start.42 = (bf16[4,64,512]{2,1,0:T(8,128)(2,1)}, bf16[4,64,512]{2,1,0:T(8,128)(2,1)}, u32[]{:S(2)}, u32[]{:S(2)}) collective-permute-start(bf16[4,64,512]{2,1,0:T(8,128)(2,1)} %collective-permute-done.40.refs_7_), channel_id=1, source_target_pairs={{0,1},{1,0},{2,3},{3,2},{4,5},{5,4},{6,7},{7,6},{8,9},{9,8},{10,11... | collective-permute-start | bytes 786440 | tf_op jit(solution)/shard_map/ppermute | solution.py:601
  (19 other events, 132.6 us)
where the time goes:
time: 254 us; the launch traced here: 253 us
  Pallas kernels  110 us (43%)
  waiting for transfers between devices  66.4 us (26%)
  starting transfers between devices  49.7 us (20%)
  local copies, waits for them, and re-layouts  14.1 us (6%)
  other arithmetic  8.36 us (3%)
  between operations  3.51 us (1%)
    pallas_call x19, Pallas kernels, call(): pl.pallas_call(body, in_specs=[pl.BlockSpec(memory_space=pltpu.SMEM)] * n...  97.3 us
    ppermute x48, waiting for transfers between devices, swap(): return lax.ppermute(value, axis, [(i, i ^ bit) for i in range(size)])  65.4 us
    ppermute x48, starting transfers between devices, swap(): return lax.ppermute(value, axis, [(i, i ^ bit) for i in range(size)])  35 us
    pallas_call x2, Pallas kernels, sum_call(): pl.pallas_call(functools.partial(kernel, [len(group) for group in groups]...  8.97 us
    all_to_all x1, starting transfers between devices, shards(): lax.all_to_all(move_rows(deal_kernel, residual, dealing_slots, 'deal'), '...  7.26 us
    squeeze x8, local copies, waits for them, and re-layouts, shards(): lax.dynamic_index_in_dim(v, my_adapter, 0, keepdims=False)  5.72 us
    unnamed x66, local copies, waits for them, and re-layouts  5.3 us
  transfers between devices with their start and end apart: 51, of which 16 were waited for; matrix products, arithmetic and copies ran while one was open for 7% of the time, Pallas kernels for 32%

commit v1 on v0

--- a/solution.py
+++ b/solution.py
@@ -187,20 +187,11 @@
         put_block(r, nn(o, wo[:, at]) + nn(to, ob[:, at]), z_keep, z_send)
 
 
-def front_kernel(chunk, last, info, wgu_h, wd_h, x0, x1, x2, x3, zo, zp, g0, g1, g2, g3, gains, a2, bd, fb, da,
+def front_kernel(chunk, last, info, wgu, wd, x0, x1, x2, x3, zo, zp, g0, g1, g2, g3, gains, a2, bd, fb, da,
                  *rest):
-    f_s, wgu, wd, sems = rest[-4:]
-    xm_out, xq_out, h_out, g_out, act_out, dg_out, du_out, t2_s, dtd_s, b_out = rest[-14:-4]
+    f_s = rest[-1]
+    xm_out, xq_out, h_out, g_out, act_out, dg_out, du_out, t2_s, dtd_s, b_out = rest[-11:-1]
     units = wd.shape[0]
-
-    def copies(i):
-        c = pl.ds(pl.multiple_of(i * QUARTER, QUARTER), QUARTER)
-        return (pltpu.make_async_copy(wgu_h.at[:, :, c], wgu.at[:, :, c], sems.at[0, i]),
-                pltpu.make_async_copy(wd_h.at[c, :], wd.at[c, :], sems.at[1, i]))
-
-    for i in range(units // QUARTER):
-        for copy in copies(i):
-            copy.start()
     me, length = info[0], info[1]
     rows = h_out.shape[0]
     xs, gs = ([chunk_of(v, chunk, rows) for v in vs] for vs in ((x0, x1, x2, x3), (g0, g1, g2, g3)))
@@ -232,8 +223,6 @@
 
     def block(i, carry):
         c = pl.ds(pl.multiple_of(i * QUARTER, QUARTER), QUARTER)
-        for copy in copies(i):
-            copy.wait()
         h, g = h_out[...], g_out[...]
         gate = nn(h, wgu[0, :, c]) + nn(t2_s[:, :RANK], fb[0, :, c])
         up = nn(h, wgu[1, :, c]) + nn(t2_s[:, RANK:], fb[1, :, c])
@@ -254,24 +243,14 @@
     lax.fori_loop(0, units // QUARTER, block, 0)
 
 
-def back_kernel(last, info, wgu_h, wd_h, h, g, act, dg, du, a2, bd, fb, da, *rest):
-    (value_s, low_s, wgu, wd, sems), rest = rest[-5:], rest[:-5]
+def back_kernel(last, info, wgu, wd, h, g, act, dg, du, a2, bd, fb, da, *rest):
+    (value_s, low_s), rest = rest[-2:], rest[:-2]
     outs, rest = (rest[-4:], rest[:-4]) if last else (rest[-5:], rest[:-5])
     d_keep, d_send, y_keep, y_send = outs[:4]
     me = info[0]
     rows = h.shape[0]
     own = slice(0, rows)
 
-    def copies(r):
-        at = quarter(me, r)
-        return (pltpu.make_async_copy(wgu_h.at[:, at, :], wgu.at[:, at, :], sems.at[0, r]),
-                pltpu.make_async_copy(wd_h.at[:, at], wd.at[:, at], sems.at[1, r]))
-
-    for r in range(PARTS):
-        for copy in copies(r):
-            copy.start()
-    if last:
-        y_keep[rows:, :], y_send[rows:, :] = rest[1][...], rest[2][...]
     dt2 = jnp.concatenate([nt(dg[...], fb[0]), nt(du[...], fb[1])], axis=1)
     dt2b = dt2.astype(BF16)
     td = nt(act[...], da[...])
@@ -280,8 +259,6 @@
 
     def block(r, carry):
         at = quarter(me, r)
-        for copy in copies(r):
-            copy.wait()
         value_s[...] = nt(dg[...], wgu[0, at, :]) + nt(du[...], wgu[1, at, :]) + nn(dt2b, a2[:, at])
         store_block(r, value_s, own, d_keep, d_send)
         value_s[...] = nn(act[...], wd[:, at]) + nn(tdb, bd[:, at])
@@ -303,7 +280,7 @@
     scratch, rest = rest[-13:], rest[:-13]
     z_s, f_s, dot_s, dqt_s, dkt_s, dvt_s, dq_s, value_s, low_s, wq, wkv, wo, sems = scratch
     copies = copies_of(((wo_h, wo), (wq_h, wq), (wkv_h, wkv)), sems)
-    n_out = 5 if last else 8
+    n_out = 7 if last else 8
     outs, rest = rest[-n_out:], rest[:-n_out]
     dxq_out, h_keep, h_send, inv_out, b_out = outs[:5]
     triples, rest = rest[:3 * (chunk + 1)], rest[3 * (chunk + 1):]
@@ -404,16 +381,14 @@
         low_s[3 * RANK:, :] = nn(tot[...], z_s[:, at])
         if last:
             low_s[...] += rest[1][:, at]
-            store_block(r, low_s, slice(rows, rows + 4 * RANK), h_keep, h_send)
+            store_block(r, low_s, slice(0, 4 * RANK), outs[5], outs[6])
         else:
             outs[5][:, at] = low_s[...]
         return inner + jnp.sum(d * h_in[:, at].astype(F32), axis=1, keepdims=True)
 
     inner = lax.fori_loop(0, PARTS, block, jnp.zeros((rows, 1), F32))
     for ref in (h_keep, h_send):
-        ref[:rows, 2 * QUARTER:] = jnp.broadcast_to(inner, (rows, LANES)).astype(ref.dtype)
-        if last:
-            ref[rows:, 2 * QUARTER:] = jnp.zeros((4 * RANK, LANES), ref.dtype)
+        ref[:, 2 * QUARTER:] = jnp.broadcast_to(inner, (rows, LANES)).astype(ref.dtype)
 
 
 def finish_kernel(gains, x_all, *refs):
@@ -480,10 +455,11 @@
                 gda[owner, :, cols] += ref[e, base + 2 * RANK:base + 3 * RANK, :].astype(F32)
 
         with_entry(b_parts, at, add_b)
-        for r, parts in enumerate(a_parts):
-            def add_a(ref, e, r=r):
-                ga[owner, :, quarter(me, r)] += ref[e, :2 * RANK, :].astype(F32)
-                gdb[owner, :, quarter(me, r)] += ref[e, 2 * RANK:, :].astype(F32)
+        for near_bit, parts in enumerate(a_parts):
+            def add_a(ref, e, near_bit=near_bit):
+                for r, cols in ((near_bit, LO), (near_bit ^ 2, HI)):
+                    ga[owner, :, quarter(me, r)] += ref[e, :2 * RANK, cols].astype(F32)
+                    gdb[owner, :, quarter(me, r)] += ref[e, 2 * RANK:, cols].astype(F32)
 
             with_entry(parts, at, add_a)
 
@@ -528,6 +504,45 @@
         copy.start()
     for copy in made:
         copy.wait()
+
+
+def load_kernel(count, *refs):
+    made = [pltpu.make_async_copy(refs[i], refs[count + i], refs[-1].at[i]) for i in range(count)]
+    for copy in made:
+        copy.start()
+    for copy in made:
+        copy.wait()
+
+
+def adapter_kernel(count, info, *refs):
+    made = [pltpu.make_async_copy(refs[i].at[info[2]], refs[count + i], refs[-1].at[i]) for i in range(count)]
+    for copy in made:
+        copy.start()
+    for copy in made:
+        copy.wait()
+
+
+def load(arrays, name, info=None, after=()):
+    count = len(arrays)
+    scalars = () if info is None else (info,)
+    kernel = load_kernel if info is None else adapter_kernel
+    shapes = [a.shape if info is None else a.shape[1:] for a in arrays]
+
+    def body(*refs):
+        at = len(scalars) + count
+        kernel(count, *refs[:at], *refs[at + len(after):])
+
+    return pl.pallas_call(
+        body,
+        in_specs=[pl.BlockSpec(memory_space=pltpu.SMEM)] * len(scalars) + [pl.BlockSpec(memory_space=pltpu.HBM)] * count
+        + [pl.BlockSpec(memory_space=pl.ANY)] * len(after),
+        out_specs=[pl.BlockSpec(memory_space=pltpu.VMEM)] * count,
+        out_shape=[pltpu.VMEM(tuple(s), a.dtype) for s, a in zip(shapes, arrays)],
+        scratch_shapes=[pltpu.SemaphoreType.DMA((count,))],
+        compiler_params=pltpu.CompilerParams(vmem_limit_bytes=MIB),
+        cost_estimate=pl.CostEstimate(flops=1000, transcendentals=0, bytes_accessed=1000),
+        name=name,
+    )(*scalars, *(in_hbm(a) for a in arrays), *after)
 
 
 def move_rows(kernel, value, slots, name):
@@ -681,7 +696,7 @@
     gs = spread(cotangent[0])
     gains = jnp.stack(spread(jnp.stack([attention_gain, feedfwd_gain])))
     dealt = lax.all_to_all(
-        move_rows(deal_kernel, residual, dealing_slots, "deal"), "dp", split_axis=0, concat_axis=1, tiled=True
+        move_rows(deal_kernel, in_hbm(residual), dealing_slots, "deal"), "dp", split_axis=0, concat_axis=1, tiled=True
     )[0]
     dealt = late(dealt, gs[2])
     beside = near(dealt)
@@ -690,11 +705,11 @@
     cos_np, sin_np = rope_tables(length)
     cos = [jnp.asarray(cos_np[:, c * rows:(c + 1) * rows]) for c in range(CHUNKS)]
     sin = [jnp.asarray(sin_np[:, c * rows:(c + 1) * rows]) for c in range(CHUNKS)]
-    a1, qb, kvb, oa, ob, a2, fba, da, bd = (
-        lax.dynamic_index_in_dim(v, my_adapter, 0, keepdims=False) for v in (
-            attention_adapter_input, query_adapter_output, key_value_adapter_output, output_adapter_input,
-            output_adapter_output, feedfwd_adapter_input, feedfwd_adapter_output, down_adapter_input,
-            down_adapter_output))
+    adapters_here = load(
+        (attention_adapter_input, query_adapter_output, key_value_adapter_output, output_adapter_input,
+         output_adapter_output, feedfwd_adapter_input, feedfwd_adapter_output, down_adapter_input,
+         down_adapter_output), "adapters", info)
+    a1, qb, kvb, oa, ob, a2, fba, da, bd = adapters_here
     wq, wkv, wo, wgu, wd = query_matrix, key_value_matrix, output_matrix, gate_up_matrix, down_matrix
 
     def like(*arrays):
@@ -722,6 +737,7 @@
         z_own[c] = pair_sum(z_keep, z_send)
         order = (kept[c][1], z_own[1])
     z_far = [far(v) for v in z_own]
+    wgu, wd = load((wgu, wd), "load", None, order)
 
     def front(c, total, partial, order):
         hidden = (rows, units)
@@ -729,23 +745,23 @@
                 ((rows, 2 * RANK), BF16), ((rows, RANK), BF16),
                 ((3 * RANK * units // QUARTER, QUARTER), F32 if c else BF16)]
         return call(
-            functools.partial(front_kernel, c, c == 0), info, (wgu, wd),
-            (*xs[c], total, near(total), *gs, gains, a2, bd, fba, da, *partial), outs,
-            [((ROW_BLOCK, WIDTH), F32)] + like(wgu, wd),
-            "front_%d" % c, 34, order, (2, units // QUARTER))
+            functools.partial(front_kernel, c, c == 0), info, (),
+            (wgu, wd, *xs[c], total, near(total), *gs, gains, a2, bd, fba, da, *partial), outs,
+            [((ROW_BLOCK, WIDTH), F32)], "front_%d" % c, 8, order)
 
     def back(c, hidden, partial, order):
-        first, second = (col, col) if c else ((rows + 3 * RANK, half), (length, half))
-        outs = [(first, F32), (first, BF16), (second, F32), (second, BF16)]
+        first = col if c else (rows + 3 * RANK, half)
+        outs = [(first, F32), (first, BF16), (col, F32), (col, BF16)]
         outs += [((3 * RANK, WIDTH), F32)] if c else []
         return call(
-            functools.partial(back_kernel, c == 0), info, (wgu, wd), (*hidden[2:7], a2, bd, fba, da, *partial), outs,
-            [(block, F32), ((3 * RANK, QUARTER), F32)] + like(wgu, wd), "back_%d" % c, 32, order, (2, PARTS))
+            functools.partial(back_kernel, c == 0), info, (), (wgu, wd, *hidden[2:7], a2, bd, fba, da, *partial), outs,
+            [(block, F32), ((3 * RANK, QUARTER), F32)], "back_%d" % c, 8, order)
 
     def attend_back(c, total, partial, order):
-        padded = (rows if c else rows + 4 * RANK, half + LANES)
+        padded = (rows, half + LANES)
         outs = [(block, F32), (padded, F32), (padded, BF16), (thin, F32), ((3 * RANK, QUARTER), F32 if c else BF16)]
-        outs += [((4 * RANK, WIDTH), F32), ((kv_cols, rows), F32), ((kv_cols, rows), F32)] if c else []
+        outs += ([((4 * RANK, WIDTH), F32), ((kv_cols, rows), F32), ((kv_cols, rows), F32)] if c
+                 else [((4 * RANK, half), F32), ((4 * RANK, half), BF16)])
         scratch = [(wide, BF16), ((ROW_BLOCK, WIDTH), F32), ((q_cols, rows), BF16), ((q_cols, rows), F32),
                    ((c + 1, kv_cols, rows), F32), ((c + 1, kv_cols, rows), F32), ((rows, q_cols + 2 * kv_cols), BF16),
                    (block, F32), ((4 * RANK, QUARTER), F32)]
@@ -760,7 +776,7 @@
     hidden[1] = front(1, far_sum(z_own[1], z_far[1]), (), order)
     step = hidden[1][8]
     total = far_sum(z_own[0], late(z_far[0], step))
-    d_keep, d_send, y_keep, y_send, fa = back(1, hidden[1], (), (step, total))
+    d_keep, d_send, y_keep_1, y_send_1, fa = back(1, hidden[1], (), (step, total))
     d_own[1] = pair_sum(d_keep, d_send)
     d_far[1] = far(d_own[1])
     hidden[0] = front(0, total, hidden[1][9:], (d_own[1],))
@@ -768,7 +784,7 @@
     total = far_sum(d_own[1], late(d_far[1], step))
     fb = hidden[0][9][None]
     fb_first = swap(fb, bits[0], "dp", dp)
-    d_keep, d_send, y_keep, y_send = back(0, hidden[0], (fa, y_keep, y_send), (step, total))
+    d_keep, d_send, y_keep_0, y_send_0 = back(0, hidden[0], (fa,), (step, total))
     d_own[0] = pair_sum(d_keep, late(d_send, fb_first))
     d_far[0] = far(d_own[0])
     fb = fb_more = jnp.concatenate([fb, fb_first], axis=0)
@@ -776,57 +792,63 @@
         fb_more = doubled(fb_more, bit, dp)
     fb_more = fb_more[2:]
     fb_side = swap(fb, bits[-1], "dp", dp)
+    y_keep, y_got = (y_keep_0, y_keep_1), (near(y_send_0), near(late(y_send_1, step)))
     dxq, h_keep, h_send, inv, *sums = attend_back(1, total, (), (d_own[0],))
     total = far_sum(d_own[0], late(d_far[0], inv))
-    h_low, h_high = chip_sum(h_keep, late(h_send, fb_more, fb_side))
+    h_low, h_high = chip_sum(h_keep, late(h_send, fb_more, fb_side, d_far[0]))
     h_far = far(h_high)
     final = [None, (dxq, h_low, h_high, h_far, inv)]
-    y_send = late(y_send, inv)
-    fa = total[rows:, :QUARTER][None]
+    y_high = [(k[:, QUARTER:] + late(g, h_high)[:, QUARTER:].astype(F32)).astype(BF16) for k, g in zip(y_keep, y_got)]
+    y_high = jnp.concatenate(y_high, axis=0)
+    fa = total[rows:][None]
     fa_first = swap(fa, bits[0], "dp", dp)
     fb_more_side = swap(fb_more, bits[-1], "dp", dp)
-    dxq, h_keep, h_send, inv, att_b = attend_back(0, total, sums, (h_high,))
-    h_low, h_high = chip_sum(h_keep, late(h_send, fa_first, fb_more_side, h_far))
+    dxq, h_keep, h_send, inv, att_b, aa_keep, aa_send = attend_back(0, total, sums, (h_high, y_high))
+    ready = (fa_first, fb_more_side, h_far)
+    aa_low, aa_high = chip_sum(aa_keep, late(aa_send, *ready))
+    aa_far = far(aa_high)
+    h_low, h_high = chip_sum(h_keep, late(h_send, *ready))
     h_far = far(h_high)
     final[0] = (dxq, h_low, h_high, h_far, inv)
-    att_a = (h_low[rows:] + h_far[rows:, :QUARTER].astype(F32)).astype(BF16)
-    att = jnp.concatenate([att_b, att_a], axis=0)[None]
+    att = jnp.concatenate([att_b, (aa_low + late(aa_far, h_high).astype(F32)).astype(BF16)], axis=0)[None]
+    att = doubled(att, bits[0], dp)
 
     dinput, = call(finish_kernel, None, (), (gains, dealt, *(v for f in final for v in f)), [((length, QUARTER), BF16)],
-                   [], "finish", 8)
+                   [], "finish", 8, (att,))
     back_grad = lax.all_to_all(
         dinput.reshape(dp, length // dp, QUARTER), "dp", split_axis=0, concat_axis=0, tiled=True)
     input_grad = move_rows(collect_kernel, back_grad, dealing_slots, "collect_grad")
 
     valid = (jnp.arange(length, dtype=jnp.int32) < my_length)[:, None]
-    y_low, y_high = chip_sum(y_keep, y_send)
-    result = jnp.concatenate([h[1] for h in hidden], axis=0) + y_low + far(late(y_high, h_high)).astype(F32)
-    result = late(jnp.where(valid, result, 0.0).astype(BF16), dinput)
+    result = [h[1] + k[:, :QUARTER] + g[:, :QUARTER].astype(F32) for h, k, g in zip(hidden, y_keep, y_got)]
+    result = jnp.concatenate(result, axis=0) + late(far(late(y_high, h_high)), dinput).astype(F32)
+    result = jnp.where(valid, result, 0.0).astype(BF16)
     back_out = lax.all_to_all(
         result.reshape(dp, length // dp, QUARTER), "dp", split_axis=0, concat_axis=0, tiled=True)
-    output = move_rows(collect_kernel, back_out, dealing_slots, "collect_out")
+    output = move_rows(collect_kernel, back_out, late(dealing_slots, input_grad), "collect_out")
 
     n_b = att_b.shape[0]
-    for bit in bits[:-1]:
+    for bit in bits[1:-1]:
         att = doubled(att, bit, dp)
     att_side = swap(att, bits[-1], "dp", dp)
     a_parts = [att[:, n_b:], att_side[:, n_b:]]
     a_far = [far(v) for v in a_parts]
+    fa = late(jnp.concatenate([fa, fa_first], axis=0), h_high)
+    for bit in bits[1:-1]:
+        fa = doubled(fa, bit, dp)
+    fa_side = swap(fa, bits[-1], "dp", dp)
+    outs = [sds((adapters, 2 * RANK, WIDTH), F32), sds((adapters, RANK, WIDTH), F32),
+            sds((adapters, 2, RANK, units), F32), sds((adapters, RANK, units), F32)]
+    ga_ffn, g_down_b, g_ffn_b, g_down_a = sum_call(
+        feedforward_sum_kernel, (info, owners),
+        ((fb, fb_more, fb_side, fb_more_side), (fa, fa_side), (near(fa), near(fa_side))), outs, "feedforward_sum")
+
     outs = [sds((adapters, 3 * RANK, WIDTH), F32), sds((adapters, RANK, WIDTH), F32),
             sds((adapters, RANK, q_cols), F32), sds((adapters, 2, RANK, kv_cols), F32),
             sds((adapters, RANK, q_cols), F32)]
     ga_att, g_out_b, g_query_b, g_kv_b, g_out_a = sum_call(
         attention_sum_kernel, (info, owners),
-        ((att, att_side), a_parts, [near(v) for v in a_parts], a_far, [near(v) for v in a_far]), outs, "attention_sum")
-
-    fa = late(jnp.concatenate([fa, fa_first], axis=0), h_high)
-    for bit in bits[1:]:
-        fa = doubled(fa, bit, dp)
-    outs = [sds((adapters, 2 * RANK, WIDTH), F32), sds((adapters, RANK, WIDTH), F32),
-            sds((adapters, 2, RANK, units), F32), sds((adapters, RANK, units), F32)]
-    ga_ffn, g_down_b, g_ffn_b, g_down_a = sum_call(
-        feedforward_sum_kernel, (info, owners), ((fb, fb_more, fb_side, fb_more_side), *([v] for v in spread(fa))), outs,
-        "feedforward_sum")
+        ((att, att_side), a_parts, [near(v) for v in a_parts], a_far, (near(a_far[0]), near(late(a_far[1], g_down_a)))), outs, "attention_sum")
     return (output, input_grad, ga_att, g_query_b, g_kv_b, g_out_a, g_out_b, ga_ffn, g_ffn_b, g_down_a, g_down_b)
 
 

time: 254 us -> 256 us (level)
  Pallas kernels: 110 us -> 127 us
  local copies, waits for them, and re-layouts: 14.1 us -> 4.89 us
    pallas_call x3, Pallas kernels: 4.18 us -> 20.4 us  [move_rows(): pl.pallas_call(kernel, in_specs=[pl.BlockSpec(memory_space=pltpu.SMEM), p...]
    pallas_call x0 -> x2, Pallas kernels: none -> 9.95 us  [load(): pl.pallas_call(body, in_specs=[pl.BlockSpec(memory_space=pltpu.SMEM)] * l...]
    pallas_call x19, Pallas kernels: 97.3 us -> 88.2 us  [call(): pl.pallas_call(body, in_specs=[pl.BlockSpec(memory_space=pltpu.SMEM)] * n...]
    squeeze x8 -> x0, local copies, waits for them, and re-layouts: 5.72 us -> none  [shards(): lax.dynamic_index_in_dim(v, my_adapter, 0, keepdims=False)]
    ppermute x48 -> x50, starting transfers between devices: 35 us -> 32.8 us  [swap(): return lax.ppermute(value, axis, [(i, i ^ bit) for i in range(size)])]
    unnamed x66 -> x57, local copies, waits for them, and re-layouts: 5.3 us -> 4.12 us
    ppermute x48 -> x50, waiting for transfers between devices: 65.4 us -> 64.8 us  [swap(): return lax.ppermute(value, axis, [(i, i ^ bit) for i in range(size)])]
  transfers between devices with their start and end apart: 51 -> 53, of which waited for: 16 -> 18; matrix products, arithmetic and copies ran while one was open for 7% -> 3% of each run, Pallas kernels for 32% -> 34%
where the time goes in v1:
time: 256 us; the launch traced here: 255 us
  Pallas kernels  127 us (50%)
  waiting for transfers between devices  65.9 us (26%)
  starting transfers between devices  47.8 us (19%)
  other arithmetic  7.46 us (3%)
  local copies, waits for them, and re-layouts  4.89 us (2%)
    pallas_call x19, Pallas kernels, call(): pl.pallas_call(body, in_specs=[pl.BlockSpec(memory_space=pltpu.SMEM)] * n...  88.2 us
    ppermute x50, waiting for transfers between devices, swap(): return lax.ppermute(value, axis, [(i, i ^ bit) for i in range(size)])  64.8 us
    ppermute x50, starting transfers between devices, swap(): return lax.ppermute(value, axis, [(i, i ^ bit) for i in range(size)])  32.8 us
    pallas_call x3, Pallas kernels, move_rows(): pl.pallas_call(kernel, in_specs=[pl.BlockSpec(memory_space=pltpu.SMEM), p...  20.4 us
    pallas_call x2, Pallas kernels, load(): pl.pallas_call(body, in_specs=[pl.BlockSpec(memory_space=pltpu.SMEM)] * l...  9.95 us
    pallas_call x2, Pallas kernels, sum_call(): pl.pallas_call(functools.partial(kernel, [len(group) for group in groups]...  8.45 us
    all_to_all x1, starting transfers between devices, shards(): lax.all_to_all(move_rows(deal_kernel, in_hbm(residual), dealing_slots, 'd...  7.26 us
  transfers between devices with their start and end apart: 53, of which 18 were waited for; matrix products, arithmetic and copies ran while one was open for 3% of the time, Pallas kernels for 34%

profile of v1, /device:TPU:0, one launch (start us, length us, event | category | flops | bytes accessed | tf_op | source)
XLA Modules:
  0.0 254.6 jit_solution(16786600868799224683)
XLA Ops:
  0.7 0.7 copy-done.19
  1.4 17.6 %deal.1 = bf16[8,64,512]{2,1,0:T(8,128)(2,1)} custom-call(s32[8]{0:T(128)S(1)} %copy-done.19, bf16[8,64,512]{2,1,0:T(8,128)(2,1)} %source.1), custom_call_target="tpu_custom_call" | custom-call | flops 1000 | bytes 1000 | tf_op jit(solution)/shard_map/deal/pallas_call | solution.py:549
  19.0 7.3 %all-to-all-start = ((bf16[8,64,512]{2,1,0:T(8,128)(2,1)}), bf16[8,64,512]{2,1,0:T(8,128)(2,1)S(1)}, u32[]{:S(2)}, u32[]{:S(2)}) async-start(bf16[8,64,512]{2,1,0:T(8,128)(2,1)} %deal.1), calls=%async_computation | async-start | bytes 1048576 | tf_op jit(solution)/shard_map/all_to_all | solution.py:698
  26.3 1.6 collective-permute-start.3
  27.9 11.8 %collective-permute-done.3.refs_11_.refs_10_ = bf16[512,512]{1,0:T(8,128)(2,1)S(1)} collective-permute-done((bf16[512,512]{1,0:T(8,128)(2,1)S(1)}, bf16[512,512]{1,0:T(8,128)(2,1)S(1)}, u32[]{:S(2)}, u32[]{:S(2)}) %collective-permute-start.3) | collective-permute-done | bytes 524320 | tf_op jit(solution)/shard_map/ppermute | solution.py:616
  39.7 1.0 all-to-all-done
  40.8 1.6 collective-permute-start.5
  44.0 1.5 collective-permute-start.9
  45.5 2.6 %collective-permute-done.5.refs_5_.refs_6_ = bf16[256,512]{1,0:T(8,128)(2,1)S(1)} collective-permute-done((bf16[256,512]{1,0:T(8,128)(2,1)S(1)}, bf16[256,512]{1,0:T(8,128)(2,1)S(1)}, u32[]{:S(2)}, u32[]{:S(2)}) %collective-permute-start.5) | collective-permute-done | bytes 262176 | tf_op jit(solution)/shard_map/ppermute | solution.py:616
  48.8 1.4 pad_add_fusion.refs_0_.info
  50.1 1.8 adapters.1
  52.0 4.1 %project_0.1 = (bf16[256,2048]{1,0:T(8,128)(2,1)S(1)}, bf16[48,256]{1,0:T(8,128)(2,1)S(1)}, bf16[512,256]{1,0:T(8,128)(2,1)S(1)}, bf16[2,256,64]{2,1,0:T(8,128)(...) custom-call(s32[4]{0:T(128)S(1)} %pad_add_fusion.refs_0_.info, ...), custom_call_target="tpu_custom_call" | custom-call | flops 1000 | bytes 1000 | tf_op jit(solution)/shard_map/project_0/pallas_call | solution.py:582
  56.1 1.0 copy-done.3
  57.1 1.5 collective-permute-done.10.refs_6_.refs_7_
  58.6 4.1 %project_1.1 = (bf16[256,2048]{1,0:T(8,128)(2,1)S(1)}, bf16[48,256]{1,0:T(8,128)(2,1)S(1)}, bf16[512,256]{1,0:T(8,128)(2,1)S(1)}, bf16[2,256,64]{2,1,0:T(8,128)(...) custom-call(s32[4]{0:T(128)S(1)} %pad_add_fusion.refs_0_.info, ...), custom_call_target="tpu_custom_call" | custom-call | flops 1000 | bytes 1000 | tf_op jit(solution)/shard_map/project_1/pallas_call | solution.py:582
  62.7 5.0 %attend_1.1 = (f32[256,1024]{1,0:T(8,128)S(1)}, bf16[256,1024]{1,0:T(8,128)(2,1)S(1)}, bf16[512,256]{1,0:T(8,128)(2,1)S(1)}, f32[8,256]{1,0:T(8,128)S(1)}, bf16[16,256]{1,0:T(8,128)(2,1)S(1)}) custom-call(s32[4]{0:T(128)S(1)} %pad_add_fusion.refs_0_.info, bf16[512,2048]{1,0:T(8,128)(2,1)} %refs_3_.5, ...), custom_call_target="tpu_custom_call" | custom-call | flops 1000 | bytes 1000 | tf_op jit(solution)/shard_map/attend_1/pallas_call | solution.py:582
  67.9 1.8 collective-permute-done.11.refs_1_
  69.8 1.6 collective-permute-start.14
  71.4 4.3 %attend_0.1 = (f32[256,1024]{1,0:T(8,128)S(1)}, bf16[256,1024]{1,0:T(8,128)(2,1)S(1)}, bf16[512,256]{1,0:T(8,128)(2,1)S(1)}, f32[8,256]{1,0:T(8,128)S(1)}, bf16[16,256]{1,0:T(8,128)(2,1)S(1)}) custom-call(s32[4]{0:T(128)S(1)} %pad_add_fusion.refs_0_.info, bf16[512,2048]{1,0:T(8,128)(2,1)} %refs_3_.5, ...), custom_call_target="tpu_custom_call" | custom-call | flops 1000 | bytes 1000 | tf_op jit(solution)/shard_map/attend_0/pallas_call | solution.py:582
  76.4 7.5 %collective-permute-done.14.refs_1_ = bf16[256,1024]{1,0:T(8,128)(2,1)S(1)} collective-permute-done((bf16[256,1024]{1,0:T(8,128)(2,1)S(1)}, bf16[256,1024]{1,0:T(8,128)(2,1)S(1)}, u32[]{:S(2)}, u32[]{:S(2)}) %collective-permute-start.14) | collective-permute-done | bytes 524320 | tf_op jit(solution)/shard_map/ppermute | solution.py:616
  84.2 1.6 collective-permute-start.13
  85.8 8.2 %load.1 = (bf16[2,2048,2048]{2,1,0:T(8,128)(2,1)S(1)}, bf16[2048,2048]{1,0:T(8,128)(2,1)S(1)}) custom-call(bf16[2,2048,2048]{2,1,0:T(8,128)(2,1)} %refs_0_.1, bf16[2048,2048]{1,0:T(8,128)(2,1)} %refs_1_.13, f32[8,256]{1,0:T(8,128)S(1)} %get-tuple-element.133.refs_2_.refs_18_.refs_27_, bf16[256,1024]{1,0:T(8,128)(2,1)S(1)} %pair_sum.4.refs_8_.refs_3_.refs_0_.refs_19_), custom_call_target="tpu_custom_call" | custom-call | flops 1000 | bytes 1000 | tf_op jit(solution)/shard_map/load/pallas_call | solution.py:535
  94.0 11.5 %front_1.1 = (bf16[256,2048]{1,0:T(8,128)(2,1)S(1)}, f32[256,512]{1,0:T(8,128)S(1)}, bf16[256,2048]{1,0:T(8,128)(2,1)S(1)}, bf16[256,2048]{1,0:T(8,128)(2,1)S(1)...) custom-call(s32[4]{0:T(128)S(1)} %pad_add_fusion.refs_0_.info, ...), custom_call_target="tpu_custom_call" | custom-call | flops 1000 | bytes 1000 | tf_op jit(solution)/shard_map/front_1/pallas_call | solution.py:582
  105.6 11.1 %back_1.1 = (f32[256,1024]{1,0:T(8,128)S(1)}, bf16[256,1024]{1,0:T(8,128)(2,1)S(1)}, f32[256,1024]{1,0:T(8,128)S(1)}, bf16[256,1024]{1,0:T(8,128)(2,1)S(1)}, f32[48,2048]{1,0:T(8,128)S(1)}) custom-call(s32[4]{0:T(128)S(1)} %pad_add_fusion.refs_0_.info, bf16[2,2048,2048]{2,1,0:T(8,128)(2,1)S(1)} %get-tuple-element.134.refs_1_, ...), custom_call_target="tpu_custom_call" | custom-call | flops 1000 | bytes 1000 | tf_op jit(solution)/shard_map/back_1/pallas_call | solution.py:582
  117.3 1.4 collective-permute-done.17.refs_1_
  119.5 11.9 %front_0.1 = (bf16[256,2048]{1,0:T(8,128)(2,1)S(1)}, f32[256,512]{1,0:T(8,128)S(1)}, bf16[256,2048]{1,0:T(8,128)(2,1)S(1)}, bf16[256,2048]{1,0:T(8,128)(2,1)S(1)...) custom-call(s32[4]{0:T(128)S(1)} %pad_add_fusion.refs_0_.info, ...), custom_call_target="tpu_custom_call" | custom-call | flops 1000 | bytes 1000 | tf_op jit(solution)/shard_map/front_0/pallas_call | solution.py:582
  131.4 1.0 copy-done.5
  132.4 1.6 collective-permute-start.19
  134.1 11.0 %back_0.1 = (f32[304,1024]{1,0:T(8,128)S(1)}, bf16[304,1024]{1,0:T(8,128)(2,1)S(1)}, f32[256,1024]{1,0:T(8,128)S(1)}, bf16[256,1024]{1,0:T(8,128)(2,1)S(1)}) custom-call(s32[4]{0:T(128)S(1)} %pad_add_fusion.refs_0_.info, bf16[2,2048,2048]{2,1,0:T(8,128)(2,1)S(1)} %get-tuple-element.134.refs_1_, bf16[2048,2048]{1,0:T(8,128)(2,1)S(1)} %get-tuple-element.135.refs_2_, ...), custom_call_target="tpu_custom_call" | custom-call | flops 1000 | bytes 1000 | tf_op jit(solution)/shard_map/back_0/pallas_call | solution.py:582
  145.2 2.0 collective-permute-done.20.refs_1_
  147.4 1.5 collective-permute-start.21
  149.0 1.4 collective-permute-start.25
  150.3 2.6 %collective-permute-start.24 = (bf16[2,192,512]{2,1,0:T(8,128)(2,1)S(1)}, bf16[2,192,512]{2,1,0:T(8,128)(2,1)S(1)}, u32[]{:S(2)}, u32[]{:S(2)}) collective-permute-start(bf16[2,192,512]{2,1,0:T(8,128)(2,1)S(1)} %pad_maximum_fusion.2.refs_0_), channel_id=1, source_target_pairs={{0,8},{4,12},{8,0},{12,4},{16,24},{20,28},{24,16},{28,20},{1,9},{5... | collective-permute-start | bytes 1179656 | tf_op jit(solution)/shard_map/ppermute | solution.py:616
  153.0 12.4 %attend_back_1.1 = (f32[256,512]{1,0:T(8,128)S(1)}, f32[256,1152]{1,0:T(8,128)S(1)}, bf16[256,1152]{1,0:T(8,128)(2,1)S(1)}, f32[256,1]{1,0:T(8,128)S(1)}, f32[48...) custom-call(s32[4]{0:T(128)S(1)} %pad_add_fusion.refs_0_.info, ...), custom_call_target="tpu_custom_call" | custom-call | flops 1000 | bytes 1000 | tf_op jit(solution)/shard_map/attend_back_1/pallas_call | solution.py:582
  166.8 0.8 collective-permute-done.26
  167.5 1.0 collective-permute-start.29
  168.5 1.5 collective-permute-start.31
  170.1 1.0 convert_add_fusion
  171.1 1.0 convert_add_fusion.1
  172.8 10.6 %attend_back_0.1 = (f32[256,512]{1,0:T(8,128)S(1)}, f32[256,1152]{1,0:T(8,128)S(1)}, bf16[256,1152]{1,0:T(8,128)(2,1)S(1)}, f32[256,1]{1,0:T(8,128)S(1)}, bf16[4...) custom-call(s32[4]{0:T(128)S(1)} %pad_add_fusion.refs_0_.info, ...), custom_call_target="tpu_custom_call" | custom-call | flops 1000 | bytes 1000 | tf_op jit(solution)/shard_map/attend_back_0/pallas_call | solution.py:582
  184.1 1.6 collective-permute-done.34
  186.4 1.5 collective-permute-start.33
  188.0 2.8 %collective-permute-done.35 = bf16[64,512]{1,0:T(8,128)(2,1)S(1)} collective-permute-done((bf16[64,512]{1,0:T(8,128)(2,1)S(1)}, bf16[64,512]{1,0:T(8,128)(2,1)S(1)}, u32[]{:S(2)}, u32[]{:S(2)}) %collective-permute-start.35) | collective-permute-done | bytes 65568 | tf_op jit(solution)/shard_map/ppermute | solution.py:616
  190.8 0.8 collective-permute-start.36
  191.6 5.7 %collective-permute-done.36 = bf16[1,112,512]{2,1,0:T(8,128)(2,1)S(1)} collective-permute-done((bf16[1,112,512]{2,1,0:T(8,128)(2,1)S(1)}, bf16[1,112,512]{2,1,0:T(8,128)(2,1)S(1)}, u32[]{:S(2)}, u32[]{:S(2)}) %collective-permute-start.36) | collective-permute-done | bytes 114720 | tf_op jit(solution)/shard_map/ppermute | solution.py:616
  197.4 1.2 finish.1
  198.6 4.2 %all-to-all-start.1 = ((bf16[8,64,512]{2,1,0:T(8,128)(2,1)}), bf16[8,64,512]{2,1,0:T(8,128)(2,1)S(1)}, u32[]{:S(2)}, u32[]{:S(2)}) async-start(bf16[8,64,512]{2,1,0:T(8,128)(2,1)} %bitcast.13), calls=%async_computation.1 | async-start | bytes 1048576 | tf_op jit(solution)/shard_map/all_to_all | solution.py:818
  202.7 0.9 collective-permute-start.37
  203.6 2.1 collective-permute-start.45
  206.4 0.7 constant_dynamic-update-slice_fusion.1
  207.1 12.0 %collective-permute-done.45 = bf16[2,48,1024]{2,1,0:T(8,128)(2,1)S(1)} collective-permute-done((bf16[2,48,1024]{2,1,0:T(8,128)(2,1)S(1)}, bf16[2,48,1024]{2,1,0:T(8,128)(2,1)S(1)}, u32[]{:S(2)}, u32[]{:S(2)}) %collective-permute-start.45) | collective-permute-done | bytes 196640 | tf_op jit(solution)/shard_map/ppermute | solution.py:616
  219.2 0.7 constant_dynamic-update-slice_fusion.refs_4_
  219.9 0.8 collective-permute-start.46
  220.6 1.1 collective-permute-done.38
  221.8 1.5 collective-permute-start.39
  223.3 2.1 fusion.1
  225.5 3.6 %all-to-all-start.2 = ((bf16[8,64,512]{2,1,0:T(8,128)(2,1)}), bf16[8,64,512]{2,1,0:T(8,128)(2,1)S(1)}, u32[]{:S(2)}, u32[]{:S(2)}) async-start(bf16[8,64,512]{2,1,0:T(8,128)(2,1)} %bitcast.35), calls=%async_computation.2 | async-start | bytes 1048576 | tf_op jit(solution)/shard_map/all_to_all | solution.py:826
  229.1 3.1 %collective-permute-done.46.refs_5_ = bf16[4,48,1024]{2,1,0:T(8,128)(2,1)} collective-permute-done((bf16[4,48,1024]{2,1,0:T(8,128)(2,1)}, bf16[4,48,1024]{2,1,0:T(8,128)(2,1)}, u32[]{:S(2)}, u32[]{:S(2)}) %collective-permute-start.46) | collective-permute-done | bytes 393248 | tf_op jit(solution)/shard_map/ppermute | solution.py:616
  232.2 0.8 collective-permute-start.42
  233.0 8.6 %collective-permute-done.39.refs_1_ = bf16[4,112,512]{2,1,0:T(8,128)(2,1)S(1)} collective-permute-done((bf16[4,112,512]{2,1,0:T(8,128)(2,1)S(1)}, bf16[4,112,512]{2,1,0:T(8,128)(2,1)S(1)}, u32[]{:S(2)}, u32[]{:S(2)}) %collective-permute-start.39) | collective-permute-done | bytes 458784 | tf_op jit(solution)/shard_map/ppermute | solution.py:616
  242.6 5.0 %feedforward_sum.1 = (f32[8,32,2048]{2,1,0:T(8,128)}, f32[8,16,2048]{2,1,0:T(8,128)}, f32[8,2,16,2048]{3,2,1,0:T(8,128)}, f32[8,16,2048]{2,1,0:T(8,128)}) custom-call(s32[4]{0:T(128)S(1)} %pad_add_fusion.refs_0_.info, s32[8]{0:T(128)S(1)} %get-tuple-element.220.owners, bf16[2,192,512]{2,1,0:T(8,128)(2,1)S(1)} %copy-done.2, ...), custom_call_target="tpu_custom_call" | custom-call | bytes 12000000 | tf_op jit(solution)/shard_map/feedforward_sum/pallas_call | solution.py:600
  248.1 1.4 collect_grad.1
  249.6 3.4 %attention_sum.1 = (f32[8,48,2048]{2,1,0:T(8,128)}, f32[8,16,2048]{2,1,0:T(8,128)}, f32[8,16,512]{2,1,0:T(8,128)}, f32[8,2,16,128]{3,2,1,0:T(8,128)}, f32[8,16,512]{2,1,0:T(8,128)}) custom-call(s32[4]{0:T(128)S(1)} %pad_add_fusion.refs_0_.info, s32[8]{0:T(128)S(1)} %get-tuple-element.220.owners, bf16[4,112,512]{2,1,0:T(8,128)(2,1)S(1)} %pad_maximum_fusion.1.refs_0_, ...), custom_call_target="tpu_custom_call" | custom-call | bytes 12000000 | tf_op jit(solution)/shard_map/attention_sum/pallas_call | solution.py:600
  253.0 1.4 collect_out.1
  (154 shorter events, 11.4 us)
Async XLA Ops:
  0.6 25.6 %copy-start = (bf16[1,512,512]{2,1,0:T(8,128)(2,1)S(1)}, bf16[1,512,512]{2,1,0:T(8,128)(2,1)}, u32[]{:S(2)}) copy-start(bf16[1,512,512]{2,1,0:T(8,128)(2,1)} %param.45) | copy-start | bytes 1572868
  1.4 26.5 %copy-start.24 = (bf16[512]{0:T(512)(128)(2,1)S(1)}, bf16[512]{0:T(512)(128)(2,1)}, u32[]{:S(2)}) copy-start(bf16[512]{0:T(512)(128)(2,1)} %param.26) | copy-start | bytes 3076
  1.4 26.5 %copy-start.25 = (bf16[512]{0:T(512)(128)(2,1)S(1)}, bf16[512]{0:T(512)(128)(2,1)}, u32[]{:S(2)}) copy-start(bf16[512]{0:T(512)(128)(2,1)} %param.30) | copy-start | bytes 3076
  1.4 41.8 %copy-start.20 = (s32[8]{0:T(128)S(1)}, s32[8]{0:T(128)}, u32[]{:S(2)}) copy-start(s32[8]{0:T(128)} %slots.4) | copy-start | bytes 100
  1.4 41.8 %copy-start.26 = (s32[8]{0:T(128)S(1)}, s32[8]{0:T(128)}, u32[]{:S(2)}) copy-start(s32[8]{0:T(128)} %param.42) | copy-start | bytes 100
  1.4 41.8 %copy-start.27 = (s32[8]{0:T(128)S(1)}, s32[8]{0:T(128)}, u32[]{:S(2)}) copy-start(s32[8]{0:T(128)} %param.43) | copy-start | bytes 100
  19.0 21.8 %all-to-all-start = ((bf16[8,64,512]{2,1,0:T(8,128)(2,1)}), bf16[8,64,512]{2,1,0:T(8,128)(2,1)S(1)}, u32[]{:S(2)}, u32[]{:S(2)}) async-start(bf16[8,64,512]{2,1,0:T(8,128)(2,1)} %deal.1), calls=%async_computation | async-start | bytes 1048576 | tf_op jit(solution)/shard_map/all_to_all | solution.py:698
  26.3 13.4 %collective-permute-start.3 = (bf16[512,512]{1,0:T(8,128)(2,1)S(1)}, bf16[512,512]{1,0:T(8,128)(2,1)S(1)}, u32[]{:S(2)}, u32[]{:S(2)}) collective-permute-start(bf16[512,512]{1,0:T(8,128)(2,1)S(1)} %bitcast.27), channel_id=1, source_target_pairs={{0,2},{1,3},{2,0},{3,1},{4,6},{5,7},{6,4},{7,5},{8,10},{9,11},{10,... | collective-permute-start | bytes 1572872 | tf_op jit(solution)/shard_map/ppermute | solution.py:616
  40.8 7.4 %collective-permute-start.5 = (bf16[256,512]{1,0:T(8,128)(2,1)S(1)}, bf16[256,512]{1,0:T(8,128)(2,1)S(1)}, u32[]{:S(2)}, u32[]{:S(2)}) collective-permute-start(bf16[256,512]{1,0:T(8,128)(2,1)S(1)} %get-tuple-element.226), channel_id=1, source_target_pairs={{0,2},{1,3},{2,0},{3,1},{4,6},{5,7},{6,4},{7,5},{8,10},{9,11},{10,... | collective-permute-start | bytes 786440 | tf_op jit(solution)/shard_map/ppermute | solution.py:616
  42.4 9.5 %collective-permute-start = (bf16[2,512]{1,0:T(2,128)(2,1)S(1)}, bf16[2,512]{1,0:T(2,128)(2,1)S(1)}, u32[]{:S(2)}, u32[]{:S(2)}) collective-permute-start(bf16[2,512]{1,0:T(2,128)(2,1)S(1)} %pad_maximum_fusion.6), channel_id=1, source_target_pairs={{0,1},{1,0},{2,3},{3,2},{4,5},{5,4},{6,7},{7,6},{8,9},{9,8},{10,11... | collective-permute-start | bytes 6152 | tf_op jit(solution)/shard_map/ppermute | solution.py:616
  42.5 5.7 %collective-permute-start.1 = (bf16[2,512]{1,0:T(2,128)(2,1)S(1)}, bf16[2,512]{1,0:T(2,128)(2,1)S(1)}, u32[]{:S(2)}, u32[]{:S(2)}) collective-permute-start(bf16[2,512]{1,0:T(2,128)(2,1)S(1)} %pad_maximum_fusion.6), channel_id=1, source_target_pairs={{0,2},{1,3},{2,0},{3,1},{4,6},{5,7},{6,4},{7,5},{8,10},{9,11},{10,... | collective-permute-start | bytes 6152 | tf_op jit(solution)/shard_map/ppermute | solution.py:616
  43.0 8.9 %collective-permute-start.4 = (bf16[512,512]{1,0:T(8,128)(2,1)S(1)}, bf16[512,512]{1,0:T(8,128)(2,1)S(1)}, u32[]{:S(2)}, u32[]{:S(2)}) collective-permute-start(bf16[512,512]{1,0:T(8,128)(2,1)S(1)} %bitcast.19), channel_id=1, source_target_pairs={{0,1},{1,0},{2,3},{3,2},{4,5},{5,4},{6,7},{7,6},{8,9},{9,8},{10,11... | collective-permute-start | bytes 1572872 | tf_op jit(solution)/shard_map/ppermute | solution.py:616
  44.0 13.1 %collective-permute-start.9 = (bf16[256,512]{1,0:T(8,128)(2,1)S(1)}, bf16[256,512]{1,0:T(8,128)(2,1)S(1)}, u32[]{:S(2)}, u32[]{:S(2)}) collective-permute-start(bf16[256,512]{1,0:T(8,128)(2,1)S(1)} %get-tuple-element.225), channel_id=1, source_target_pairs={{0,2},{1,3},{2,0},{3,1},{4,6},{5,7},{6,4},{7,5},{8,10},{9,11},{10,... | collective-permute-start | bytes 786440 | tf_op jit(solution)/shard_map/ppermute | solution.py:616
  48.2 3.8 %collective-permute-start.6 = (bf16[256,512]{1,0:T(8,128)(2,1)S(1)}, bf16[256,512]{1,0:T(8,128)(2,1)S(1)}, u32[]{:S(2)}, u32[]{:S(2)}) collective-permute-start(bf16[256,512]{1,0:T(8,128)(2,1)S(1)} %collective-permute-done.5.refs_5_.refs_6_), channel_id=1, source_target_pairs={{0,1},{1,0},{2,3},{3,2},{4,5},{5,4},{6,7},{7,6},{8,9},{9,8},{10,11... | collective-permute-start | bytes 786440 | tf_op jit(solution)/shard_map/ppermute | solution.py:616
  48.2 3.7 %collective-permute-start.2 = (bf16[2,512]{1,0:T(2,128)(2,1)S(1)}, bf16[2,512]{1,0:T(2,128)(2,1)S(1)}, u32[]{:S(2)}, u32[]{:S(2)}) collective-permute-start(bf16[2,512]{1,0:T(2,128)(2,1)S(1)} %collective-permute-done.1), channel_id=1, source_target_pairs={{0,1},{1,0},{2,3},{3,2},{4,5},{5,4},{6,7},{7,6},{8,9},{9,8},{10,11... | collective-permute-start | bytes 6152 | tf_op jit(solution)/shard_map/ppermute | solution.py:616
  57.1 1.5 collective-permute-start.10
  67.7 2.0 collective-permute-start.11
  69.8 14.0 %collective-permute-start.14 = (bf16[256,1024]{1,0:T(8,128)(2,1)S(1)}, bf16[256,1024]{1,0:T(8,128)(2,1)S(1)}, u32[]{:S(2)}, u32[]{:S(2)}) collective-permute-start(bf16[256,1024]{1,0:T(8,128)(2,1)S(1)} %pair_sum.4.refs_8_.refs_3_.refs_0_.refs_19_), channel_id=1, source_target_pairs={{0,2},{1,3},{2,0},{3,1},{4,6},{5,7},{6,4},{7,5},{8,10},{9,11},{10,... | collective-permute-start | bytes 1572872 | tf_op jit(solution)/shard_map/ppermute | solution.py:616
  75.8 8.3 %collective-permute-start.12 = (bf16[256,1024]{1,0:T(8,128)(2,1)S(1)}, bf16[256,1024]{1,0:T(8,128)(2,1)S(1)}, u32[]{:S(2)}, u32[]{:S(2)}) collective-permute-start(bf16[256,1024]{1,0:T(8,128)(2,1)S(1)} %get-tuple-element.137), channel_id=1, source_target_pairs={{0,1},{1,0},{2,3},{3,2},{4,5},{5,4},{6,7},{7,6},{8,9},{9,8},{10,11... | collective-permute-start | bytes 1572872 | tf_op jit(solution)/shard_map/ppermute | solution.py:616
  75.8 18.1 %collective-permute-start.7 = (bf16[512,512]{1,0:T(8,128)(2,1)S(1)}, bf16[512,512]{1,0:T(8,128)(2,1)S(1)}, u32[]{:S(2)}, u32[]{:S(2)}) collective-permute-start(bf16[512,512]{1,0:T(8,128)(2,1)S(1)} %bitcast.28), channel_id=1, source_target_pairs={{0,1},{1,0},{2,3},{3,2},{4,5},{5,4},{6,7},{7,6},{8,9},{9,8},{10,11... | collective-permute-start | bytes 1572872 | tf_op jit(solution)/shard_map/ppermute | solution.py:616
  76.3 17.6 %collective-permute-start.8 = (bf16[512,512]{1,0:T(8,128)(2,1)S(1)}, bf16[512,512]{1,0:T(8,128)(2,1)S(1)}, u32[]{:S(2)}, u32[]{:S(2)}) collective-permute-start(bf16[512,512]{1,0:T(8,128)(2,1)S(1)} %collective-permute-done.3.refs_11_.refs_10_), channel_id=1, source_target_pairs={{0,1},{1,0},{2,3},{3,2},{4,5},{5,4},{6,7},{7,6},{8,9},{9,8},{10,11... | collective-permute-start | bytes 1572872 | tf_op jit(solution)/shard_map/ppermute | solution.py:616
  84.0 10.0 %collective-permute-start.15 = (bf16[256,1024]{1,0:T(8,128)(2,1)S(1)}, bf16[256,1024]{1,0:T(8,128)(2,1)S(1)}, u32[]{:S(2)}, u32[]{:S(2)}) collective-permute-start(bf16[256,1024]{1,0:T(8,128)(2,1)S(1)} %far_sum.4.refs_7_), channel_id=1, source_target_pairs={{0,1},{1,0},{2,3},{3,2},{4,5},{5,4},{6,7},{7,6},{8,9},{9,8},{10,11... | collective-permute-start | bytes 1572872 | tf_op jit(solution)/shard_map/ppermute | solution.py:616
  84.2 21.3 %collective-permute-start.13 = (bf16[256,1024]{1,0:T(8,128)(2,1)S(1)}, bf16[256,1024]{1,0:T(8,128)(2,1)S(1)}, u32[]{:S(2)}, u32[]{:S(2)}) collective-permute-start(bf16[256,1024]{1,0:T(8,128)(2,1)S(1)} %pair_sum.5.refs_0_), channel_id=1, source_target_pairs={{0,2},{1,3},{2,0},{3,1},{4,6},{5,7},{6,4},{7,5},{8,10},{9,11},{10,... | collective-permute-start | bytes 1572872 | tf_op jit(solution)/shard_map/ppermute | solution.py:616
  116.8 2.0 collective-permute-start.17
  117.0 2.5 collective-permute-start.16
  118.8 15.2 %collective-permute-start.18 = (bf16[256,1024]{1,0:T(8,128)(2,1)S(1)}, bf16[256,1024]{1,0:T(8,128)(2,1)S(1)}, u32[]{:S(2)}, u32[]{:S(2)}) collective-permute-start(bf16[256,1024]{1,0:T(8,128)(2,1)S(1)} %pair_sum.6.refs_19_.refs_0_), channel_id=1, source_target_pairs={{0,2},{1,3},{2,0},{3,1},{4,6},{5,7},{6,4},{7,5},{8,10},{9,11},{10,... | collective-permute-start | bytes 1572872 | tf_op jit(solution)/shard_map/ppermute | solution.py:616
  132.4 12.8 %collective-permute-start.19 = (bf16[1,192,512]{2,1,0:T(8,128)(2,1)S(1)}, bf16[1,192,512]{2,1,0:T(8,128)(2,1)S(1)}, u32[]{:S(2)}, u32[]{:S(2)}) collective-permute-start(bf16[1,192,512]{2,1,0:T(8,128)(2,1)S(1)} %bitcast.33), channel_id=1, source_target_pairs={{0,16},{4,20},{8,24},{12,28},{16,0},{20,4},{24,8},{28,12},{1,17},{... | collective-permute-start | bytes 589832 | tf_op jit(solution)/shard_map/ppermute | solution.py:616
  145.2 2.1 collective-permute-start.20
  147.4 18.0 %collective-permute-start.21 = (bf16[304,1024]{1,0:T(8,128)(2,1)S(1)}, bf16[304,1024]{1,0:T(8,128)(2,1)S(1)}, u32[]{:S(2)}, u32[]{:S(2)}) collective-permute-start(bf16[304,1024]{1,0:T(8,128)(2,1)S(1)} %pair_sum.7.refs_35_.refs_0_), channel_id=1, source_target_pairs={{0,2},{1,3},{2,0},{3,1},{4,6},{5,7},{6,4},{7,5},{8,10},{9,11},{10,... | collective-permute-start | bytes 1867784 | tf_op jit(solution)/shard_map/ppermute | solution.py:616
  148.9 4.1 %collective-permute-start.22 = (bf16[256,1024]{1,0:T(8,128)(2,1)S(1)}, bf16[256,1024]{1,0:T(8,128)(2,1)S(1)}, u32[]{:S(2)}, u32[]{:S(2)}) collective-permute-start(bf16[256,1024]{1,0:T(8,128)(2,1)S(1)} %far_sum.6.refs_14_.refs_13_), channel_id=1, source_target_pairs={{0,1},{1,0},{2,3},{3,2},{4,5},{5,4},{6,7},{7,6},{8,9},{9,8},{10,11... | collective-permute-start | bytes 1572872 | tf_op jit(solution)/shard_map/ppermute | solution.py:616
  149.0 16.4 %collective-permute-start.25 = (bf16[2,192,512]{2,1,0:T(8,128)(2,1)S(1)}, bf16[2,192,512]{2,1,0:T(8,128)(2,1)S(1)}, u32[]{:S(2)}, u32[]{:S(2)}) collective-permute-start(bf16[2,192,512]{2,1,0:T(8,128)(2,1)S(1)} %pad_maximum_fusion.2.refs_0_), channel_id=1, source_target_pairs={{0,4},{4,0},{8,12},{12,8},{16,20},{20,16},{24,28},{28,24},{1,5},{5... | collective-permute-start | bytes 1179656 | tf_op jit(solution)/shard_map/ppermute | solution.py:616
  150.3 15.1 %collective-permute-start.24 = (bf16[2,192,512]{2,1,0:T(8,128)(2,1)S(1)}, bf16[2,192,512]{2,1,0:T(8,128)(2,1)S(1)}, u32[]{:S(2)}, u32[]{:S(2)}) collective-permute-start(bf16[2,192,512]{2,1,0:T(8,128)(2,1)S(1)} %pad_maximum_fusion.2.refs_0_), channel_id=1, source_target_pairs={{0,8},{4,12},{8,0},{12,4},{16,24},{20,28},{24,16},{28,20},{1,9},{5... | collective-permute-start | bytes 1179656 | tf_op jit(solution)/shard_map/ppermute | solution.py:616
  165.4 2.1 collective-permute-start.26
  165.5 3.0 %collective-permute-start.28 = (bf16[256,1024]{1,0:T(8,128)(2,1)S(1)}, bf16[256,1024]{1,0:T(8,128)(2,1)S(1)}, u32[]{:S(2)}, u32[]{:S(2)}) collective-permute-start(bf16[256,1024]{1,0:T(8,128)(2,1)S(1)} %get-tuple-element.190), channel_id=1, source_target_pairs={{0,1},{1,0},{2,3},{3,2},{4,5},{5,4},{6,7},{7,6},{8,9},{9,8},{10,11... | collective-permute-start | bytes 1572872 | tf_op jit(solution)/shard_map/ppermute | solution.py:616
  166.0 4.0 %collective-permute-start.27 = (bf16[256,1024]{1,0:T(8,128)(2,1)S(1)}, bf16[256,1024]{1,0:T(8,128)(2,1)S(1)}, u32[]{:S(2)}, u32[]{:S(2)}) collective-permute-start(bf16[256,1024]{1,0:T(8,128)(2,1)S(1)} %get-tuple-element.186), channel_id=1, source_target_pairs={{0,1},{1,0},{2,3},{3,2},{4,5},{5,4},{6,7},{7,6},{8,9},{9,8},{10,11... | collective-permute-start | bytes 1572872 | tf_op jit(solution)/shard_map/ppermute | solution.py:616
  166.1 17.3 %collective-permute-start.30 = (bf16[2,192,512]{2,1,0:T(8,128)(2,1)S(1)}, bf16[2,192,512]{2,1,0:T(8,128)(2,1)S(1)}, u32[]{:S(2)}, u32[]{:S(2)}) collective-permute-start(bf16[2,192,512]{2,1,0:T(8,128)(2,1)S(1)} %collective-permute-done.24.refs_1_), channel_id=1, source_target_pairs={{0,4},{4,0},{8,12},{12,8},{16,20},{20,16},{24,28},{28,24},{1,5},{5... | collective-permute-start | bytes 1179656 | tf_op jit(solution)/shard_map/ppermute | solution.py:616
  166.4 5.7 %collective-permute-start.23 = (bf16[304,1024]{1,0:T(8,128)(2,1)S(1)}, bf16[304,1024]{1,0:T(8,128)(2,1)S(1)}, u32[]{:S(2)}, u32[]{:S(2)}) collective-permute-start(bf16[304,1024]{1,0:T(8,128)(2,1)S(1)} %far_sum.7.refs_13_), channel_id=1, source_target_pairs={{0,1},{1,0},{2,3},{3,2},{4,5},{5,4},{6,7},{7,6},{8,9},{9,8},{10,11... | collective-permute-start | bytes 1867784 | tf_op jit(solution)/shard_map/ppermute | solution.py:616
  167.5 15.9 %collective-permute-start.29 = (bf16[1,48,1024]{2,1,0:T(8,128)(2,1)S(1)}, bf16[1,48,1024]{2,1,0:T(8,128)(2,1)S(1)}, u32[]{:S(2)}, u32[]{:S(2)}) collective-permute-start(bf16[1,48,1024]{2,1,0:T(8,128)(2,1)S(1)} %slice_bitcast_fusion), channel_id=1, source_target_pairs={{0,16},{4,20},{8,24},{12,28},{16,0},{20,4},{24,8},{28,12},{1,17},{... | collective-permute-start | bytes 294920 | tf_op jit(solution)/shard_map/ppermute | solution.py:616
  168.5 14.9 %collective-permute-start.31 = (bf16[256,640]{1,0:T(8,128)(2,1)S(1)}, bf16[256,640]{1,0:T(8,128)(2,1)S(1)}, u32[]{:S(2)}, u32[]{:S(2)}) collective-permute-start(bf16[256,640]{1,0:T(8,128)(2,1)S(1)} %add_convert_fusion.1.refs_36_.refs_9_), channel_id=1, source_target_pairs={{0,2},{1,3},{2,0},{3,1},{4,6},{5,7},{6,4},{7,5},{8,10},{9,11},{10,... | collective-permute-start | bytes 983048 | tf_op jit(solution)/shard_map/ppermute | solution.py:616
  183.4 2.9 %collective-permute-start.32 = (bf16[256,1152]{1,0:T(8,128)(2,1)S(1)}, bf16[256,1152]{1,0:T(8,128)(2,1)S(1)}, u32[]{:S(2)}, u32[]{:S(2)}) collective-permute-start(bf16[256,1152]{1,0:T(8,128)(2,1)S(1)} %get-tuple-element.195), channel_id=1, source_target_pairs={{0,1},{1,0},{2,3},{3,2},{4,5},{5,4},{6,7},{7,6},{8,9},{9,8},{10,11... | collective-permute-start | bytes 1769480 | tf_op jit(solution)/shard_map/ppermute | solution.py:616
  183.5 2.2 collective-permute-start.34
  185.7 5.0 %collective-permute-start.35 = (bf16[64,512]{1,0:T(8,128)(2,1)S(1)}, bf16[64,512]{1,0:T(8,128)(2,1)S(1)}, u32[]{:S(2)}, u32[]{:S(2)}) collective-permute-start(bf16[64,512]{1,0:T(8,128)(2,1)S(1)} %add_convert_fusion.5), channel_id=1, source_target_pairs={{0,2},{1,3},{2,0},{3,1},{4,6},{5,7},{6,4},{7,5},{8,10},{9,11},{10,... | collective-permute-start | bytes 196616 | tf_op jit(solution)/shard_map/ppermute | solution.py:616
  186.4 10.9 %collective-permute-start.33 = (bf16[256,640]{1,0:T(8,128)(2,1)S(1)}, bf16[256,640]{1,0:T(8,128)(2,1)S(1)}, u32[]{:S(2)}, u32[]{:S(2)}) collective-permute-start(bf16[256,640]{1,0:T(8,128)(2,1)S(1)} %add_convert_fusion.refs_4_), channel_id=1, source_target_pairs={{0,2},{1,3},{2,0},{3,1},{4,6},{5,7},{6,4},{7,5},{8,10},{9,11},{10,... | collective-permute-start | bytes 983048 | tf_op jit(solution)/shard_map/ppermute | solution.py:616
  190.8 6.5 %collective-permute-start.36 = (bf16[1,112,512]{2,1,0:T(8,128)(2,1)S(1)}, bf16[1,112,512]{2,1,0:T(8,128)(2,1)S(1)}, u32[]{:S(2)}, u32[]{:S(2)}) collective-permute-start(bf16[1,112,512]{2,1,0:T(8,128)(2,1)S(1)} %maximum_bitcast_fusion), channel_id=1, source_target_pairs={{0,16},{4,20},{8,24},{12,28},{16,0},{20,4},{24,8},{28,12},{1,17},{... | collective-permute-start | bytes 344072 | tf_op jit(solution)/shard_map/ppermute | solution.py:616
  198.6 24.8 %copy-start.21 = (f32[256,512]{1,0:T(8,128)S(1)}, f32[256,512]{1,0:T(8,128)}, u32[]{:S(2)}) copy-start(f32[256,512]{1,0:T(8,128)} %get-tuple-element.223) | copy-start | bytes 1572868
  198.6 26.9 %all-to-all-start.1 = ((bf16[8,64,512]{2,1,0:T(8,128)(2,1)}), bf16[8,64,512]{2,1,0:T(8,128)(2,1)S(1)}, u32[]{:S(2)}, u32[]{:S(2)}) async-start(bf16[8,64,512]{2,1,0:T(8,128)(2,1)} %bitcast.13), calls=%async_computation.1 | async-start | bytes 1048576 | tf_op jit(solution)/shard_map/all_to_all | solution.py:818
  202.7 20.6 %collective-permute-start.37 = (bf16[512,512]{1,0:T(8,128)(2,1)S(1)}, bf16[512,512]{1,0:T(8,128)(2,1)S(1)}, u32[]{:S(2)}, u32[]{:S(2)}) collective-permute-start(bf16[512,512]{1,0:T(8,128)(2,1)S(1)} %pad_maximum_fusion.refs_37_), channel_id=1, source_target_pairs={{0,2},{1,3},{2,0},{3,1},{4,6},{5,7},{6,4},{7,5},{8,10},{9,11},{10,... | collective-permute-start | bytes 1572872 | tf_op jit(solution)/shard_map/ppermute | solution.py:616
  203.6 15.6 %collective-permute-start.45 = (bf16[2,48,1024]{2,1,0:T(8,128)(2,1)S(1)}, bf16[2,48,1024]{2,1,0:T(8,128)(2,1)S(1)}, u32[]{:S(2)}, u32[]{:S(2)}) collective-permute-start(bf16[2,48,1024]{2,1,0:T(8,128)(2,1)S(1)} %pad_maximum_fusion.4), channel_id=1, source_target_pairs={{0,8},{4,12},{8,0},{12,4},{16,24},{20,28},{24,16},{28,20},{1,9},{5... | collective-permute-start | bytes 589832 | tf_op jit(solution)/shard_map/ppermute | solution.py:616
  206.4 15.4 %collective-permute-start.38 = (bf16[2,112,512]{2,1,0:T(8,128)(2,1)S(1)}, bf16[2,112,512]{2,1,0:T(8,128)(2,1)S(1)}, u32[]{:S(2)}, u32[]{:S(2)}) collective-permute-start(bf16[2,112,512]{2,1,0:T(8,128)(2,1)S(1)} %pad_maximum_fusion.3.refs_12_), channel_id=1, source_target_pairs={{0,8},{4,12},{8,0},{12,4},{16,24},{20,28},{24,16},{28,20},{1,9},{5... | collective-permute-start | bytes 688136 | tf_op jit(solution)/shard_map/ppermute | solution.py:616
  219.9 12.3 %collective-permute-start.46 = (bf16[4,48,1024]{2,1,0:T(8,128)(2,1)}, bf16[4,48,1024]{2,1,0:T(8,128)(2,1)}, u32[]{:S(2)}, u32[]{:S(2)}) collective-permute-start(bf16[4,48,1024]{2,1,0:T(8,128)(2,1)} %constant_dynamic-update-slice_fusion.refs_4_), channel_id=1, source_target_pairs={{0,4},{4,0},{8,12},{12,8},{16,20},{20,16},{24,28},{28,24},{1,5},{5... | collective-permute-start | bytes 1179656 | tf_op jit(solution)/shard_map/ppermute | solution.py:616
  221.8 19.8 %collective-permute-start.39 = (bf16[4,112,512]{2,1,0:T(8,128)(2,1)S(1)}, bf16[4,112,512]{2,1,0:T(8,128)(2,1)S(1)}, u32[]{:S(2)}, u32[]{:S(2)}) collective-permute-start(bf16[4,112,512]{2,1,0:T(8,128)(2,1)S(1)} %pad_maximum_fusion.1.refs_0_), channel_id=1, source_target_pairs={{0,4},{4,0},{8,12},{12,8},{16,20},{20,16},{24,28},{28,24},{1,5},{5... | collective-permute-start | bytes 1376264 | tf_op jit(solution)/shard_map/ppermute | solution.py:616
  223.3 19.3 %copy-start.2 = (bf16[2,192,512]{2,1,0:T(8,128)(2,1)S(1)}, bf16[2,192,512]{2,1,0:T(8,128)(2,1)}, u32[]{:S(2)}) copy-start(bf16[2,192,512]{2,1,0:T(8,128)(2,1)} %copy-done.1) | copy-start | bytes 1179652
  223.3 19.3 %copy-start.10 = (bf16[2,192,512]{2,1,0:T(8,128)(2,1)S(1)}, bf16[2,192,512]{2,1,0:T(8,128)(2,1)}, u32[]{:S(2)}) copy-start(bf16[2,192,512]{2,1,0:T(8,128)(2,1)} %copy-done.9) | copy-start | bytes 1179652
  223.3 19.3 %copy-start.12 = (bf16[2,192,512]{2,1,0:T(8,128)(2,1)S(1)}, bf16[2,192,512]{2,1,0:T(8,128)(2,1)}, u32[]{:S(2)}) copy-start(bf16[2,192,512]{2,1,0:T(8,128)(2,1)} %copy-done.11) | copy-start | bytes 1179652
  223.3 19.3 %copy-start.14 = (bf16[2,192,512]{2,1,0:T(8,128)(2,1)S(1)}, bf16[2,192,512]{2,1,0:T(8,128)(2,1)}, u32[]{:S(2)}) copy-start(bf16[2,192,512]{2,1,0:T(8,128)(2,1)} %copy-done.13) | copy-start | bytes 1179652
  225.5 27.5 %all-to-all-start.2 = ((bf16[8,64,512]{2,1,0:T(8,128)(2,1)}), bf16[8,64,512]{2,1,0:T(8,128)(2,1)S(1)}, u32[]{:S(2)}, u32[]{:S(2)}) async-start(bf16[8,64,512]{2,1,0:T(8,128)(2,1)} %bitcast.35), calls=%async_computation.2 | async-start | bytes 1048576 | tf_op jit(solution)/shard_map/all_to_all | solution.py:826
  229.1 13.4 %collective-permute-start.47 = (bf16[4,48,1024]{2,1,0:T(8,128)(2,1)}, bf16[4,48,1024]{2,1,0:T(8,128)(2,1)S(1)}, u32[]{:S(2)}, u32[]{:S(2)}) collective-permute-start(bf16[4,48,1024]{2,1,0:T(8,128)(2,1)} %constant_dynamic-update-slice_fusion.refs_4_), channel_id=1, source_target_pairs={{0,1},{1,0},{2,3},{3,2},{4,5},{5,4},{6,7},{7,6},{8,9},{9,8},{10,11... | collective-permute-start | bytes 1179656 | tf_op jit(solution)/shard_map/ppermute | solution.py:616
  232.2 10.4 %collective-permute-start.48 = (bf16[4,48,1024]{2,1,0:T(8,128)(2,1)}, bf16[4,48,1024]{2,1,0:T(8,128)(2,1)S(1)}, u32[]{:S(2)}, u32[]{:S(2)}) collective-permute-start(bf16[4,48,1024]{2,1,0:T(8,128)(2,1)} %collective-permute-done.46.refs_5_), channel_id=1, source_target_pairs={{0,1},{1,0},{2,3},{3,2},{4,5},{5,4},{6,7},{7,6},{8,9},{9,8},{10,11... | collective-permute-start | bytes 1179656 | tf_op jit(solution)/shard_map/ppermute | solution.py:616
  232.2 9.8 %collective-permute-start.42 = (bf16[4,64,512]{2,1,0:T(8,128)(2,1)S(1)}, bf16[4,64,512]{2,1,0:T(8,128)(2,1)S(1)}, u32[]{:S(2)}, u32[]{:S(2)}) collective-permute-start(bf16[4,64,512]{2,1,0:T(8,128)(2,1)S(1)} %slice.109.refs_2_), channel_id=1, source_target_pairs={{0,2},{1,3},{2,0},{3,1},{4,6},{5,7},{6,4},{7,5},{8,10},{9,11},{10,... | collective-permute-start | bytes 786440 | tf_op jit(solution)/shard_map/ppermute | solution.py:616
  241.6 6.4 %collective-permute-start.43 = (bf16[4,64,512]{2,1,0:T(8,128)(2,1)S(1)}, bf16[4,64,512]{2,1,0:T(8,128)(2,1)S(1)}, u32[]{:S(2)}, u32[]{:S(2)}) collective-permute-start(bf16[4,64,512]{2,1,0:T(8,128)(2,1)S(1)} %slice.110.refs_3_), channel_id=1, source_target_pairs={{0,2},{1,3},{2,0},{3,1},{4,6},{5,7},{6,4},{7,5},{8,10},{9,11},{10,... | collective-permute-start | bytes 786440 | tf_op jit(solution)/shard_map/ppermute | solution.py:616
  242.0 7.5 %collective-permute-start.40 = (bf16[4,64,512]{2,1,0:T(8,128)(2,1)S(1)}, bf16[4,64,512]{2,1,0:T(8,128)(2,1)S(1)}, u32[]{:S(2)}, u32[]{:S(2)}) collective-permute-start(bf16[4,64,512]{2,1,0:T(8,128)(2,1)S(1)} %slice.109.refs_2_), channel_id=1, source_target_pairs={{0,1},{1,0},{2,3},{3,2},{4,5},{5,4},{6,7},{7,6},{8,9},{9,8},{10,11... | collective-permute-start | bytes 786440 | tf_op jit(solution)/shard_map/ppermute | solution.py:616
  242.0 7.5 %collective-permute-start.44 = (bf16[4,64,512]{2,1,0:T(8,128)(2,1)S(1)}, bf16[4,64,512]{2,1,0:T(8,128)(2,1)S(1)}, u32[]{:S(2)}, u32[]{:S(2)}) collective-permute-start(bf16[4,64,512]{2,1,0:T(8,128)(2,1)S(1)} %collective-permute-done.42.refs_6_), channel_id=1, source_target_pairs={{0,1},{1,0},{2,3},{3,2},{4,5},{5,4},{6,7},{7,6},{8,9},{9,8},{10,11... | collective-permute-start | bytes 786440 | tf_op jit(solution)/shard_map/ppermute | solution.py:616
  242.5 7.0 %collective-permute-start.41 = (bf16[4,64,512]{2,1,0:T(8,128)(2,1)S(1)}, bf16[4,64,512]{2,1,0:T(8,128)(2,1)S(1)}, u32[]{:S(2)}, u32[]{:S(2)}) collective-permute-start(bf16[4,64,512]{2,1,0:T(8,128)(2,1)S(1)} %slice.110.refs_3_), channel_id=1, source_target_pairs={{0,1},{1,0},{2,3},{3,2},{4,5},{5,4},{6,7},{7,6},{8,9},{9,8},{10,11... | collective-permute-start | bytes 786440 | tf_op jit(solution)/shard_map/ppermute | solution.py:616
  248.0 1.5 collective-permute-start.49
  (17 other events, 92.6 us)

commit v2 on v1

--- a/solution.py
+++ b/solution.py
@@ -545,17 +545,18 @@
     )(*scalars, *(in_hbm(a) for a in arrays), *after)
 
 
-def move_rows(kernel, value, slots, name):
+def move_rows(kernel, value, slots, name, here):
+    space = pltpu.VMEM if here else pl.ANY
     return pl.pallas_call(
         kernel,
-        in_specs=[pl.BlockSpec(memory_space=pltpu.SMEM), pl.BlockSpec(memory_space=pl.ANY)],
-        out_specs=pl.BlockSpec(memory_space=pl.ANY),
-        out_shape=jax.ShapeDtypeStruct(value.shape, value.dtype),
+        in_specs=[pl.BlockSpec(memory_space=pltpu.SMEM), pl.BlockSpec(memory_space=pl.ANY if here else pltpu.VMEM)],
+        out_specs=pl.BlockSpec(memory_space=space),
+        out_shape=(pltpu.VMEM if here else jax.ShapeDtypeStruct)(value.shape, value.dtype),
         scratch_shapes=[pltpu.SemaphoreType.DMA((value.shape[0],))],
         compiler_params=pltpu.CompilerParams(vmem_limit_bytes=MIB),
         cost_estimate=pl.CostEstimate(flops=1000, transcendentals=0, bytes_accessed=1000),
         name=name,
-    )(slots, value)
+    )(slots, in_hbm(value) if here else in_vmem(value))
 
 
 def sds(shape, dtype):
@@ -696,20 +697,20 @@
     gs = spread(cotangent[0])
     gains = jnp.stack(spread(jnp.stack([attention_gain, feedfwd_gain])))
     dealt = lax.all_to_all(
-        move_rows(deal_kernel, in_hbm(residual), dealing_slots, "deal"), "dp", split_axis=0, concat_axis=1, tiled=True
+        move_rows(deal_kernel, residual, dealing_slots, "deal", True), "dp", split_axis=0, concat_axis=1, tiled=True
     )[0]
-    dealt = late(dealt, gs[2])
+    adapters_here = load(
+        (attention_adapter_input, query_adapter_output, key_value_adapter_output, output_adapter_input,
+         output_adapter_output, feedfwd_adapter_input, feedfwd_adapter_output, down_adapter_input,
+         down_adapter_output), "adapters", info)
+    a1, qb, kvb, oa, ob, a2, fba, da, bd = adapters_here
+    dealt = late(dealt, gs[2], a1)
     beside = near(dealt)
     there = [far(dealt[c * rows:(c + 1) * rows]) for c in range(CHUNKS)]
     xs = [None] * CHUNKS
     cos_np, sin_np = rope_tables(length)
     cos = [jnp.asarray(cos_np[:, c * rows:(c + 1) * rows]) for c in range(CHUNKS)]
     sin = [jnp.asarray(sin_np[:, c * rows:(c + 1) * rows]) for c in range(CHUNKS)]
-    adapters_here = load(
-        (attention_adapter_input, query_adapter_output, key_value_adapter_output, output_adapter_input,
-         output_adapter_output, feedfwd_adapter_input, feedfwd_adapter_output, down_adapter_input,
-         down_adapter_output), "adapters", info)
-    a1, qb, kvb, oa, ob, a2, fba, da, bd = adapters_here
     wq, wkv, wo, wgu, wd = query_matrix, key_value_matrix, output_matrix, gate_up_matrix, down_matrix
 
     def like(*arrays):
@@ -773,7 +774,7 @@
 
     bits = [1 << b for b in reversed(range(dp.bit_length() - 1))]
     hidden, d_own, d_far = ([None] * CHUNKS for _ in range(3))
-    hidden[1] = front(1, far_sum(z_own[1], z_far[1]), (), order)
+    hidden[1] = front(1, far_sum(z_own[1], late(z_far[1], wd)), (), order)
     step = hidden[1][8]
     total = far_sum(z_own[0], late(z_far[0], step))
     d_keep, d_send, y_keep_1, y_send_1, fa = back(1, hidden[1], (), (step, total))
@@ -784,27 +785,34 @@
     total = far_sum(d_own[1], late(d_far[1], step))
     fb = hidden[0][9][None]
     fb_first = swap(fb, bits[0], "dp", dp)
-    d_keep, d_send, y_keep_0, y_send_0 = back(0, hidden[0], (fa,), (step, total))
-    d_own[0] = pair_sum(d_keep, late(d_send, fb_first))
+    y_keep, y_got = [None, y_keep_1], [None, near(y_send_1)]
+
+    def y_high(c, *others):
+        return (y_keep[c][:, QUARTER:] + late(y_got[c], *others)[:, QUARTER:].astype(F32)).astype(BF16)
+
+    high = y_high(1, step)
+    y_far = [None, far(high)]
+    d_keep, d_send, y_keep[0], y_send_0 = back(0, hidden[0], (fa,), (step, total, high))
+    d_own[0] = pair_sum(d_keep, late(d_send, fb_first, y_far[1]))
     d_far[0] = far(d_own[0])
     fb = fb_more = jnp.concatenate([fb, fb_first], axis=0)
     for bit in bits[1:-1]:
         fb_more = doubled(fb_more, bit, dp)
     fb_more = fb_more[2:]
     fb_side = swap(fb, bits[-1], "dp", dp)
-    y_keep, y_got = (y_keep_0, y_keep_1), (near(y_send_0), near(late(y_send_1, step)))
+    y_got[0] = near(y_send_0)
     dxq, h_keep, h_send, inv, *sums = attend_back(1, total, (), (d_own[0],))
     total = far_sum(d_own[0], late(d_far[0], inv))
     h_low, h_high = chip_sum(h_keep, late(h_send, fb_more, fb_side, d_far[0]))
     h_far = far(h_high)
     final = [None, (dxq, h_low, h_high, h_far, inv)]
-    y_high = [(k[:, QUARTER:] + late(g, h_high)[:, QUARTER:].astype(F32)).astype(BF16) for k, g in zip(y_keep, y_got)]
-    y_high = jnp.concatenate(y_high, axis=0)
+    high = y_high(0, h_high)
+    y_far[0] = far(high)
     fa = total[rows:][None]
     fa_first = swap(fa, bits[0], "dp", dp)
     fb_more_side = swap(fb_more, bits[-1], "dp", dp)
-    dxq, h_keep, h_send, inv, att_b, aa_keep, aa_send = attend_back(0, total, sums, (h_high, y_high))
-    ready = (fa_first, fb_more_side, h_far)
+    dxq, h_keep, h_send, inv, att_b, aa_keep, aa_send = attend_back(0, total, sums, (h_high, high))
+    ready = (fa_first, fb_more_side, h_far, y_far[0])
     aa_low, aa_high = chip_sum(aa_keep, late(aa_send, *ready))
     aa_far = far(aa_high)
     h_low, h_high = chip_sum(h_keep, late(h_send, *ready))
@@ -813,21 +821,23 @@
     att = jnp.concatenate([att_b, (aa_low + late(aa_far, h_high).astype(F32)).astype(BF16)], axis=0)[None]
     att = doubled(att, bits[0], dp)
 
+    valid = (jnp.arange(length, dtype=jnp.int32) < my_length)[:, None]
+    result = jnp.concatenate(
+        [hidden[c][1] + y_keep[c][:, :QUARTER] + late(y_got[c], h_high)[:, :QUARTER].astype(F32) + y_far[c].astype(F32)
+         for c in range(CHUNKS)], axis=0)
+    result = jnp.where(valid, result, 0.0).astype(BF16)
+    back_out = lax.all_to_all(
+        result.reshape(dp, length // dp, QUARTER), "dp", split_axis=0, concat_axis=0, tiled=True)
+    output = move_rows(collect_kernel, back_out, dealing_slots, "collect_out", False)
+
     dinput, = call(finish_kernel, None, (), (gains, dealt, *(v for f in final for v in f)), [((length, QUARTER), BF16)],
                    [], "finish", 8, (att,))
     back_grad = lax.all_to_all(
         dinput.reshape(dp, length // dp, QUARTER), "dp", split_axis=0, concat_axis=0, tiled=True)
-    input_grad = move_rows(collect_kernel, back_grad, dealing_slots, "collect_grad")
-
-    valid = (jnp.arange(length, dtype=jnp.int32) < my_length)[:, None]
-    result = [h[1] + k[:, :QUARTER] + g[:, :QUARTER].astype(F32) for h, k, g in zip(hidden, y_keep, y_got)]
-    result = jnp.concatenate(result, axis=0) + late(far(late(y_high, h_high)), dinput).astype(F32)
-    result = jnp.where(valid, result, 0.0).astype(BF16)
-    back_out = lax.all_to_all(
-        result.reshape(dp, length // dp, QUARTER), "dp", split_axis=0, concat_axis=0, tiled=True)
-    output = move_rows(collect_kernel, back_out, late(dealing_slots, input_grad), "collect_out")
+    input_grad = move_rows(collect_kernel, back_grad, late(dealing_slots, output), "collect_grad", False)
 
     n_b = att_b.shape[0]
+    att = late(att, h_far)
     for bit in bits[1:-1]:
         att = doubled(att, bit, dp)
     att_side = swap(att, bits[-1], "dp", dp)

time: 256 us -> 240 us (0.938)
  Pallas kernels: 127 us -> 115 us
  waiting for transfers between devices: 65.9 us -> 56.6 us
  local copies, waits for them, and re-layouts: 4.89 us -> 9.55 us
  starting transfers between devices: 47.8 us -> 50.6 us
    pallas_call x3, Pallas kernels: 20.4 us -> 5.25 us  [move_rows(): pl.pallas_call(kernel, in_specs=[pl.BlockSpec(memory_space=pltpu.SMEM), p...]
    ppermute x50 -> x51, waiting for transfers between devices: 64.8 us -> 55.5 us  [swap(): return lax.ppermute(value, axis, [(i, i ^ bit) for i in range(size)])]
    ppermute x50 -> x51, starting transfers between devices: 32.8 us -> 36.2 us  [swap(): return lax.ppermute(value, axis, [(i, i ^ bit) for i in range(size)])]
    unnamed x57 -> x92, local copies, waits for them, and re-layouts: 4.12 us -> 6.88 us
  transfers between devices with their start and end apart: 53 -> 54, of which waited for: 18 -> 18; matrix products, arithmetic and copies ran while one was open for 3% -> 5% of each run, Pallas kernels for 34% -> 36%
where the time goes in v2:
time: 240 us
  Pallas kernels  115 us (48%)
  waiting for transfers between devices  56.6 us (24%)
  starting transfers between devices  50.6 us (21%)
  local copies, waits for them, and re-layouts  9.55 us (4%)
  other arithmetic  6.57 us (3%)
    pallas_call x19, Pallas kernels, call(): pl.pallas_call(body, in_specs=[pl.BlockSpec(memory_space=pltpu.SMEM)] * n...  89.5 us
    ppermute x51, waiting for transfers between devices, swap(): return lax.ppermute(value, axis, [(i, i ^ bit) for i in range(size)])  55.5 us
    ppermute x51, starting transfers between devices, swap(): return lax.ppermute(value, axis, [(i, i ^ bit) for i in range(size)])  36.2 us
    pallas_call x2, Pallas kernels, sum_call(): pl.pallas_call(functools.partial(kernel, [len(group) for group in groups]...  10.3 us
    pallas_call x2, Pallas kernels, load(): pl.pallas_call(body, in_specs=[pl.BlockSpec(memory_space=pltpu.SMEM)] * l...  9.97 us
    all_to_all x1, starting transfers between devices, shards(): lax.all_to_all(move_rows(deal_kernel, residual, dealing_slots, 'deal', Tr...  7.26 us
    unnamed x92, local copies, waits for them, and re-layouts  6.88 us
    pallas_call x3, Pallas kernels, move_rows(): pl.pallas_call(kernel, in_specs=[pl.BlockSpec(memory_space=pltpu.SMEM), p...  5.25 us
  transfers between devices with their start and end apart: 54, of which 18 were waited for; matrix products, arithmetic and copies ran while one was open for 5% of the time, Pallas kernels for 36%

profile of v2, /device:TPU:0, one launch (start us, length us, event | category | flops | bytes accessed | tf_op | source)
XLA Modules:
  0.0 239.9 jit_solution(3789517047234097650)
XLA Ops:
  1.4 2.5 %deal.1 = bf16[8,64,512]{2,1,0:T(8,128)(2,1)} custom-call(s32[8]{0:T(128)S(1)} %copy-done.36, bf16[8,64,512]{2,1,0:T(8,128)(2,1)} %source.1), custom_call_target="tpu_custom_call" | custom-call | flops 1000 | bytes 1000 | tf_op jit(solution)/shard_map/deal/pallas_call | solution.py:550
  3.8 7.3 %all-to-all-start = ((bf16[8,64,512]{2,1,0:T(8,128)(2,1)}), bf16[8,64,512]{2,1,0:T(8,128)(2,1)S(1)}, u32[]{:S(2)}, u32[]{:S(2)}) async-start(bf16[8,64,512]{2,1,0:T(8,128)(2,1)} %deal.1), calls=%async_computation | async-start | bytes 1048576 | tf_op jit(solution)/shard_map/all_to_all | solution.py:699
  11.1 1.6 collective-permute-start
  13.5 1.4 pad_add_fusion.refs_0_.info
  14.9 1.8 adapters.1
  16.7 7.9 %collective-permute-done.refs_11_.refs_10_ = bf16[512,512]{1,0:T(8,128)(2,1)S(1)} collective-permute-done((bf16[512,512]{1,0:T(8,128)(2,1)S(1)}, bf16[512,512]{1,0:T(8,128)(2,1)S(1)}, u32[]{:S(2)}, u32[]{:S(2)}) %collective-permute-start) | collective-permute-done | bytes 524320 | tf_op jit(solution)/shard_map/ppermute | solution.py:617
  24.6 1.0 all-to-all-done
  25.6 1.6 collective-permute-start.2
  27.8 6.6 %collective-permute-done.2.refs_5_.refs_6_ = bf16[256,512]{1,0:T(8,128)(2,1)S(1)} collective-permute-done((bf16[256,512]{1,0:T(8,128)(2,1)S(1)}, bf16[256,512]{1,0:T(8,128)(2,1)S(1)}, u32[]{:S(2)}, u32[]{:S(2)}) %collective-permute-start.2) | collective-permute-done | bytes 262176 | tf_op jit(solution)/shard_map/ppermute | solution.py:617
  34.4 2.1 collective-permute-start.5
  36.8 1.3 collective-permute-done.5
  38.2 1.1 collective-permute-done.6
  39.4 4.1 %project_0.1 = (bf16[256,2048]{1,0:T(8,128)(2,1)S(1)}, bf16[48,256]{1,0:T(8,128)(2,1)S(1)}, bf16[512,256]{1,0:T(8,128)(2,1)S(1)}, bf16[2,256,64]{2,1,0:T(8,128)(...) custom-call(s32[4]{0:T(128)S(1)} %pad_add_fusion.refs_0_.info, ...), custom_call_target="tpu_custom_call" | custom-call | flops 1000 | bytes 1000 | tf_op jit(solution)/shard_map/project_0/pallas_call | solution.py:583
  43.5 1.0 copy-done.4
  44.6 1.4 collective-permute-done.8.refs_6_.refs_7_
  46.0 4.1 %project_1.1 = (bf16[256,2048]{1,0:T(8,128)(2,1)S(1)}, bf16[48,256]{1,0:T(8,128)(2,1)S(1)}, bf16[512,256]{1,0:T(8,128)(2,1)S(1)}, bf16[2,256,64]{2,1,0:T(8,128)(...) custom-call(s32[4]{0:T(128)S(1)} %pad_add_fusion.refs_0_.info, ...), custom_call_target="tpu_custom_call" | custom-call | flops 1000 | bytes 1000 | tf_op jit(solution)/shard_map/project_1/pallas_call | solution.py:583
  50.1 5.0 %attend_1.1 = (f32[256,1024]{1,0:T(8,128)S(1)}, bf16[256,1024]{1,0:T(8,128)(2,1)S(1)}, bf16[512,256]{1,0:T(8,128)(2,1)S(1)}, f32[8,256]{1,0:T(8,128)S(1)}, bf16[16,256]{1,0:T(8,128)(2,1)S(1)}) custom-call(s32[4]{0:T(128)S(1)} %pad_add_fusion.refs_0_.info, bf16[512,2048]{1,0:T(8,128)(2,1)} %refs_3_.5, ...), custom_call_target="tpu_custom_call" | custom-call | flops 1000 | bytes 1000 | tf_op jit(solution)/shard_map/attend_1/pallas_call | solution.py:583
  55.3 1.7 collective-permute-done.9.refs_1_
  57.1 2.1 collective-permute-start.12
  59.2 4.3 %attend_0.1 = (f32[256,1024]{1,0:T(8,128)S(1)}, bf16[256,1024]{1,0:T(8,128)(2,1)S(1)}, bf16[512,256]{1,0:T(8,128)(2,1)S(1)}, f32[8,256]{1,0:T(8,128)S(1)}, bf16[16,256]{1,0:T(8,128)(2,1)S(1)}) custom-call(s32[4]{0:T(128)S(1)} %pad_add_fusion.refs_0_.info, bf16[512,2048]{1,0:T(8,128)(2,1)} %refs_3_.5, ...), custom_call_target="tpu_custom_call" | custom-call | flops 1000 | bytes 1000 | tf_op jit(solution)/shard_map/attend_0/pallas_call | solution.py:583
  64.2 8.2 %load.1 = (bf16[2,2048,2048]{2,1,0:T(8,128)(2,1)S(1)}, bf16[2048,2048]{1,0:T(8,128)(2,1)S(1)}) custom-call(bf16[2,2048,2048]{2,1,0:T(8,128)(2,1)} %refs_0_.1, bf16[2048,2048]{1,0:T(8,128)(2,1)} %refs_1_.13, f32[8,256]{1,0:T(8,128)S(1)} %get-tuple-element.134.refs_2_.refs_18_.refs_27_, bf16[256,1024]{1,0:T(8,128)(2,1)S(1)} %pair_sum.4.refs_8_.refs_3_.refs_0_.refs_19_), custom_call_target="tpu_custom_call" | custom-call | flops 1000 | bytes 1000 | tf_op jit(solution)/shard_map/load/pallas_call | solution.py:535
  73.6 1.0 collective-permute-done.13.refs_8_
  74.6 11.5 %front_1.1 = (bf16[256,2048]{1,0:T(8,128)(2,1)S(1)}, f32[256,512]{1,0:T(8,128)S(1)}, bf16[256,2048]{1,0:T(8,128)(2,1)S(1)}, bf16[256,2048]{1,0:T(8,128)(2,1)S(1)...) custom-call(s32[4]{0:T(128)S(1)} %pad_add_fusion.refs_0_.info, ...), custom_call_target="tpu_custom_call" | custom-call | flops 1000 | bytes 1000 | tf_op jit(solution)/shard_map/front_1/pallas_call | solution.py:583
  86.1 1.0 collective-permute-done.11.refs_1_
  87.3 11.1 %back_1.1 = (f32[256,1024]{1,0:T(8,128)S(1)}, bf16[256,1024]{1,0:T(8,128)(2,1)S(1)}, f32[256,1024]{1,0:T(8,128)S(1)}, bf16[256,1024]{1,0:T(8,128)(2,1)S(1)}, f32[48,2048]{1,0:T(8,128)S(1)}) custom-call(s32[4]{0:T(128)S(1)} %pad_add_fusion.refs_0_.info, bf16[2,2048,2048]{2,1,0:T(8,128)(2,1)S(1)} %get-tuple-element.135.refs_1_, ...), custom_call_target="tpu_custom_call" | custom-call | flops 1000 | bytes 1000 | tf_op jit(solution)/shard_map/back_1/pallas_call | solution.py:583
  99.1 1.3 collective-permute-done.17.refs_1_
  100.5 0.9 collective-permute-start.18
  101.4 12.0 %front_0.1 = (bf16[256,2048]{1,0:T(8,128)(2,1)S(1)}, f32[256,512]{1,0:T(8,128)S(1)}, bf16[256,2048]{1,0:T(8,128)(2,1)S(1)}, bf16[256,2048]{1,0:T(8,128)(2,1)S(1)...) custom-call(s32[4]{0:T(128)S(1)} %pad_add_fusion.refs_0_.info, ...), custom_call_target="tpu_custom_call" | custom-call | flops 1000 | bytes 1000 | tf_op jit(solution)/shard_map/front_0/pallas_call | solution.py:583
  113.3 1.0 copy-done.6
  114.4 1.3 collective-permute-start.22
  115.7 1.5 collective-permute-start.21
  117.3 11.1 %back_0.1 = (f32[304,1024]{1,0:T(8,128)S(1)}, bf16[304,1024]{1,0:T(8,128)(2,1)S(1)}, f32[256,1024]{1,0:T(8,128)S(1)}, bf16[256,1024]{1,0:T(8,128)(2,1)S(1)}) custom-call(s32[4]{0:T(128)S(1)} %pad_add_fusion.refs_0_.info, bf16[2,2048,2048]{2,1,0:T(8,128)(2,1)S(1)} %get-tuple-element.135.refs_1_, bf16[2048,2048]{1,0:T(8,128)(2,1)S(1)} %get-tuple-element.136.refs_2_, ...), custom_call_target="tpu_custom_call" | custom-call | flops 1000 | bytes 1000 | tf_op jit(solution)/shard_map/back_0/pallas_call | solution.py:583
  128.5 2.0 collective-permute-done.23.refs_1_
  130.7 0.9 collective-permute-start.24
  131.6 1.5 collective-permute-start.27
  133.1 1.4 collective-permute-start.28
  134.6 12.2 %attend_back_1.1 = (f32[256,512]{1,0:T(8,128)S(1)}, f32[256,1152]{1,0:T(8,128)S(1)}, bf16[256,1152]{1,0:T(8,128)(2,1)S(1)}, f32[256,1]{1,0:T(8,128)S(1)}, f32[48...) custom-call(s32[4]{0:T(128)S(1)} %pad_add_fusion.refs_0_.info, ...), custom_call_target="tpu_custom_call" | custom-call | flops 1000 | bytes 1000 | tf_op jit(solution)/shard_map/attend_back_1/pallas_call | solution.py:583
  150.4 1.3 collective-permute-start.32
  154.0 10.9 %attend_back_0.1 = (f32[256,512]{1,0:T(8,128)S(1)}, f32[256,1152]{1,0:T(8,128)S(1)}, bf16[256,1152]{1,0:T(8,128)(2,1)S(1)}, f32[256,1]{1,0:T(8,128)S(1)}, bf16[4...) custom-call(s32[4]{0:T(128)S(1)} %pad_add_fusion.refs_0_.info, ...), custom_call_target="tpu_custom_call" | custom-call | flops 1000 | bytes 1000 | tf_op jit(solution)/shard_map/attend_back_0/pallas_call | solution.py:583
  167.2 0.9 collective-permute-done.36
  168.1 1.3 collective-permute-start.37
  170.4 0.9 collective-permute-start.46
  171.3 1.7 collective-permute-done.37
  173.5 1.0 select_convert_fusion
  174.4 3.5 %all-to-all-start.1 = ((bf16[8,64,512]{2,1,0:T(8,128)(2,1)}), bf16[8,64,512]{2,1,0:T(8,128)(2,1)S(1)}, u32[]{:S(2)}, u32[]{:S(2)}) async-start(bf16[8,64,512]{2,1,0:T(8,128)(2,1)} %select_convert_fusion), calls=%async_computation.1 | async-start | bytes 1048576 | tf_op jit(solution)/shard_map/all_to_all | solution.py:829
  178.1 3.0 %collective-permute-start.38 = (bf16[1,112,512]{2,1,0:T(8,128)(2,1)S(1)}, bf16[1,112,512]{2,1,0:T(8,128)(2,1)S(1)}, u32[]{:S(2)}, u32[]{:S(2)}) collective-permute-start(bf16[1,112,512]{2,1,0:T(8,128)(2,1)S(1)} %maximum_bitcast_fusion), channel_id=1, source_target_pairs={{0,16},{4,20},{8,24},{12,28},{16,0},{20,4},{24,8},{28,12},{1,17},{... | collective-permute-start | bytes 344072 | tf_op jit(solution)/shard_map/ppermute | solution.py:617
  181.1 1.6 constant_dynamic-update-slice_fusion.3
  182.7 14.2 %collective-permute-done.38 = bf16[1,112,512]{2,1,0:T(8,128)(2,1)S(1)} collective-permute-done((bf16[1,112,512]{2,1,0:T(8,128)(2,1)S(1)}, bf16[1,112,512]{2,1,0:T(8,128)(2,1)S(1)}, u32[]{:S(2)}, u32[]{:S(2)}) %collective-permute-start.38) | collective-permute-done | bytes 114720 | tf_op jit(solution)/shard_map/ppermute | solution.py:617
  197.0 1.6 constant_dynamic-update-slice_fusion.2.refs_4_
  198.6 1.4 collective-permute-start.47
  200.1 2.9 %collective-permute-done.39 = bf16[2,112,512]{2,1,0:T(8,128)(2,1)S(1)} collective-permute-done((bf16[2,112,512]{2,1,0:T(8,128)(2,1)S(1)}, bf16[2,112,512]{2,1,0:T(8,128)(2,1)S(1)}, u32[]{:S(2)}, u32[]{:S(2)}) %collective-permute-start.39) | collective-permute-done | bytes 229408 | tf_op jit(solution)/shard_map/ppermute | solution.py:617
  203.0 1.8 collective-permute-start.40
  204.8 1.2 convert_add_fusion.1.refs_3_
  206.1 2.2 finish.1
  208.3 3.6 %all-to-all-start.2 = ((bf16[8,64,512]{2,1,0:T(8,128)(2,1)}), bf16[8,64,512]{2,1,0:T(8,128)(2,1)S(1)}, u32[]{:S(2)}, u32[]{:S(2)}) async-start(bf16[8,64,512]{2,1,0:T(8,128)(2,1)} %bitcast.14), calls=%async_computation.2 | async-start | bytes 1048576 | tf_op jit(solution)/shard_map/all_to_all | solution.py:835
  212.5 1.1 collective-permute-start.43
  213.6 8.9 %collective-permute-done.40.refs_1_ = bf16[4,112,512]{2,1,0:T(8,128)(2,1)} collective-permute-done((bf16[4,112,512]{2,1,0:T(8,128)(2,1)S(1)}, bf16[4,112,512]{2,1,0:T(8,128)(2,1)}, u32[]{:S(2)}, u32[]{:S(2)}) %collective-permute-start.40) | collective-permute-done | bytes 458784 | tf_op jit(solution)/shard_map/ppermute | solution.py:617
  222.5 1.0 slice.108.refs_3_
  223.5 1.1 collective-permute-start.44
  225.2 1.0 copy-done.23
  226.2 5.3 %feedforward_sum.1 = (f32[8,32,2048]{2,1,0:T(8,128)}, f32[8,16,2048]{2,1,0:T(8,128)}, f32[8,2,16,2048]{3,2,1,0:T(8,128)}, f32[8,16,2048]{2,1,0:T(8,128)}) custom-call(s32[4]{0:T(128)S(1)} %pad_add_fusion.refs_0_.info, s32[8]{0:T(128)S(1)} %get-tuple-element.222.owners, bf16[2,192,512]{2,1,0:T(8,128)(2,1)S(1)} %pad_maximum_fusion.1.refs_0_, ...), custom_call_target="tpu_custom_call" | custom-call | bytes 12000000 | tf_op jit(solution)/shard_map/feedforward_sum/pallas_call | solution.py:601
  232.0 1.4 collect_out.1
  233.4 1.4 collect_grad.1
  234.9 5.0 %attention_sum.1 = (f32[8,48,2048]{2,1,0:T(8,128)}, f32[8,16,2048]{2,1,0:T(8,128)}, f32[8,16,512]{2,1,0:T(8,128)}, f32[8,2,16,128]{3,2,1,0:T(8,128)}, f32[8,16,512]{2,1,0:T(8,128)}) custom-call(s32[4]{0:T(128)S(1)} %pad_add_fusion.refs_0_.info, s32[8]{0:T(128)S(1)} %get-tuple-element.222.owners, ...), custom_call_target="tpu_custom_call" | custom-call | bytes 12000000 | tf_op jit(solution)/shard_map/attention_sum/pallas_call | solution.py:601
  (193 shorter events, 17.3 us)
Async XLA Ops:
  3.8 21.8 %all-to-all-start = ((bf16[8,64,512]{2,1,0:T(8,128)(2,1)}), bf16[8,64,512]{2,1,0:T(8,128)(2,1)S(1)}, u32[]{:S(2)}, u32[]{:S(2)}) async-start(bf16[8,64,512]{2,1,0:T(8,128)(2,1)} %deal.1), calls=%async_computation | async-start | bytes 1048576 | tf_op jit(solution)/shard_map/all_to_all | solution.py:699
  11.1 13.4 %collective-permute-start = (bf16[512,512]{1,0:T(8,128)(2,1)S(1)}, bf16[512,512]{1,0:T(8,128)(2,1)S(1)}, u32[]{:S(2)}, u32[]{:S(2)}) collective-permute-start(bf16[512,512]{1,0:T(8,128)(2,1)S(1)} %bitcast.27), channel_id=1, source_target_pairs={{0,2},{1,3},{2,0},{3,1},{4,6},{5,7},{6,4},{7,5},{8,10},{9,11},{10,... | collective-permute-start | bytes 1572872 | tf_op jit(solution)/shard_map/ppermute | solution.py:617
  14.9 24.4 %copy-start.32 = (f32[32,256]{1,0:T(8,128)S(1)}, f32[32,256]{1,0:T(8,128)}, u32[]{:S(2)}) copy-start(f32[32,256]{1,0:T(8,128)} %constant.23.clone.refs_11_.refs_21_) | copy-start | bytes 98308
  14.9 24.4 %copy-start.33 = (f32[32,256]{1,0:T(8,128)S(1)}, f32[32,256]{1,0:T(8,128)}, u32[]{:S(2)}) copy-start(f32[32,256]{1,0:T(8,128)} %constant.25.clone.refs_12_.refs_22_) | copy-start | bytes 98308
  25.6 8.7 %collective-permute-start.2 = (bf16[256,512]{1,0:T(8,128)(2,1)S(1)}, bf16[256,512]{1,0:T(8,128)(2,1)S(1)}, u32[]{:S(2)}, u32[]{:S(2)}) collective-permute-start(bf16[256,512]{1,0:T(8,128)(2,1)S(1)} %get-tuple-element.224), channel_id=1, source_target_pairs={{0,2},{1,3},{2,0},{3,1},{4,6},{5,7},{6,4},{7,5},{8,10},{9,11},{10,... | collective-permute-start | bytes 786440 | tf_op jit(solution)/shard_map/ppermute | solution.py:617
  27.2 12.1 %collective-permute-start.1 = (bf16[512,512]{1,0:T(8,128)(2,1)S(1)}, bf16[512,512]{1,0:T(8,128)(2,1)S(1)}, u32[]{:S(2)}, u32[]{:S(2)}) collective-permute-start(bf16[512,512]{1,0:T(8,128)(2,1)S(1)} %bitcast.19), channel_id=1, source_target_pairs={{0,1},{1,0},{2,3},{3,2},{4,5},{5,4},{6,7},{7,6},{8,9},{9,8},{10,11... | collective-permute-start | bytes 1572872 | tf_op jit(solution)/shard_map/ppermute | solution.py:617
  27.3 17.2 %collective-permute-start.7 = (bf16[256,512]{1,0:T(8,128)(2,1)S(1)}, bf16[256,512]{1,0:T(8,128)(2,1)S(1)}, u32[]{:S(2)}, u32[]{:S(2)}) collective-permute-start(bf16[256,512]{1,0:T(8,128)(2,1)S(1)} %get-tuple-element.223), channel_id=1, source_target_pairs={{0,2},{1,3},{2,0},{3,1},{4,6},{5,7},{6,4},{7,5},{8,10},{9,11},{10,... | collective-permute-start | bytes 786440 | tf_op jit(solution)/shard_map/ppermute | solution.py:617
  34.4 4.9 %collective-permute-start.3 = (bf16[256,512]{1,0:T(8,128)(2,1)S(1)}, bf16[256,512]{1,0:T(8,128)(2,1)S(1)}, u32[]{:S(2)}, u32[]{:S(2)}) collective-permute-start(bf16[256,512]{1,0:T(8,128)(2,1)S(1)} %collective-permute-done.2.refs_5_.refs_6_), channel_id=1, source_target_pairs={{0,1},{1,0},{2,3},{3,2},{4,5},{5,4},{6,7},{7,6},{8,9},{9,8},{10,11... | collective-permute-start | bytes 786440 | tf_op jit(solution)/shard_map/ppermute | solution.py:617
  34.4 3.7 %collective-permute-start.5 = (bf16[2,512]{1,0:T(2,128)(2,1)S(1)}, bf16[2,512]{1,0:T(2,128)(2,1)S(1)}, u32[]{:S(2)}, u32[]{:S(2)}) collective-permute-start(bf16[2,512]{1,0:T(2,128)(2,1)S(1)} %pad_maximum_fusion.5), channel_id=1, source_target_pairs={{0,2},{1,3},{2,0},{3,1},{4,6},{5,7},{6,4},{7,5},{8,10},{9,11},{10,... | collective-permute-start | bytes 6152 | tf_op jit(solution)/shard_map/ppermute | solution.py:617
  36.5 1.6 collective-permute-start.4
  38.1 1.2 collective-permute-start.6
  44.4 1.5 collective-permute-start.8
  55.1 2.0 collective-permute-start.9
  57.1 15.3 %collective-permute-start.12 = (bf16[256,1024]{1,0:T(8,128)(2,1)S(1)}, bf16[256,1024]{1,0:T(8,128)(2,1)S(1)}, u32[]{:S(2)}, u32[]{:S(2)}) collective-permute-start(bf16[256,1024]{1,0:T(8,128)(2,1)S(1)} %pair_sum.4.refs_8_.refs_3_.refs_0_.refs_19_), channel_id=1, source_target_pairs={{0,2},{1,3},{2,0},{3,1},{4,6},{5,7},{6,4},{7,5},{8,10},{9,11},{10,... | collective-permute-start | bytes 1572872 | tf_op jit(solution)/shard_map/ppermute | solution.py:617
  63.5 9.5 %collective-permute-start.10 = (bf16[256,1024]{1,0:T(8,128)(2,1)S(1)}, bf16[256,1024]{1,0:T(8,128)(2,1)S(1)}, u32[]{:S(2)}, u32[]{:S(2)}) collective-permute-start(bf16[256,1024]{1,0:T(8,128)(2,1)S(1)} %get-tuple-element.138), channel_id=1, source_target_pairs={{0,1},{1,0},{2,3},{3,2},{4,5},{5,4},{6,7},{7,6},{8,9},{9,8},{10,11... | collective-permute-start | bytes 1572872 | tf_op jit(solution)/shard_map/ppermute | solution.py:617
  63.6 10.0 %collective-permute-start.14 = (bf16[512,512]{1,0:T(8,128)(2,1)S(1)}, bf16[512,512]{1,0:T(8,128)(2,1)S(1)}, u32[]{:S(2)}, u32[]{:S(2)}) collective-permute-start(bf16[512,512]{1,0:T(8,128)(2,1)S(1)} %bitcast.28), channel_id=1, source_target_pairs={{0,1},{1,0},{2,3},{3,2},{4,5},{5,4},{6,7},{7,6},{8,9},{9,8},{10,11... | collective-permute-start | bytes 1572872 | tf_op jit(solution)/shard_map/ppermute | solution.py:617
  64.1 9.5 %collective-permute-start.15 = (bf16[512,512]{1,0:T(8,128)(2,1)S(1)}, bf16[512,512]{1,0:T(8,128)(2,1)S(1)}, u32[]{:S(2)}, u32[]{:S(2)}) collective-permute-start(bf16[512,512]{1,0:T(8,128)(2,1)S(1)} %collective-permute-done.refs_11_.refs_10_), channel_id=1, source_target_pairs={{0,1},{1,0},{2,3},{3,2},{4,5},{5,4},{6,7},{7,6},{8,9},{9,8},{10,11... | collective-permute-start | bytes 1572872 | tf_op jit(solution)/shard_map/ppermute | solution.py:617
  72.5 2.0 collective-permute-start.13
  73.1 14.0 %collective-permute-start.11 = (bf16[256,1024]{1,0:T(8,128)(2,1)S(1)}, bf16[256,1024]{1,0:T(8,128)(2,1)S(1)}, u32[]{:S(2)}, u32[]{:S(2)}) collective-permute-start(bf16[256,1024]{1,0:T(8,128)(2,1)S(1)} %pair_sum.5.refs_0_), channel_id=1, source_target_pairs={{0,2},{1,3},{2,0},{3,1},{4,6},{5,7},{6,4},{7,5},{8,10},{9,11},{10,... | collective-permute-start | bytes 1572872 | tf_op jit(solution)/shard_map/ppermute | solution.py:617
  98.4 2.0 collective-permute-start.17
  98.5 2.9 %collective-permute-start.16 = (bf16[256,1024]{1,0:T(8,128)(2,1)S(1)}, bf16[256,1024]{1,0:T(8,128)(2,1)S(1)}, u32[]{:S(2)}, u32[]{:S(2)}) collective-permute-start(bf16[256,1024]{1,0:T(8,128)(2,1)S(1)} %far_sum.5.refs_13_.refs_7_), channel_id=1, source_target_pairs={{0,1},{1,0},{2,3},{3,2},{4,5},{5,4},{6,7},{7,6},{8,9},{9,8},{10,11... | collective-permute-start | bytes 1572872 | tf_op jit(solution)/shard_map/ppermute | solution.py:617
  99.0 15.3 %collective-permute-start.19 = (bf16[256,1024]{1,0:T(8,128)(2,1)S(1)}, bf16[256,1024]{1,0:T(8,128)(2,1)S(1)}, u32[]{:S(2)}, u32[]{:S(2)}) collective-permute-start(bf16[256,1024]{1,0:T(8,128)(2,1)S(1)} %get-tuple-element.164), channel_id=1, source_target_pairs={{0,1},{1,0},{2,3},{3,2},{4,5},{5,4},{6,7},{7,6},{8,9},{9,8},{10,11... | collective-permute-start | bytes 1572872 | tf_op jit(solution)/shard_map/ppermute | solution.py:617
  100.5 16.7 %collective-permute-start.18 = (bf16[256,1024]{1,0:T(8,128)(2,1)S(1)}, bf16[256,1024]{1,0:T(8,128)(2,1)S(1)}, u32[]{:S(2)}, u32[]{:S(2)}) collective-permute-start(bf16[256,1024]{1,0:T(8,128)(2,1)S(1)} %pair_sum.6.refs_19_.refs_0_), channel_id=1, source_target_pairs={{0,2},{1,3},{2,0},{3,1},{4,6},{5,7},{6,4},{7,5},{8,10},{9,11},{10,... | collective-permute-start | bytes 1572872 | tf_op jit(solution)/shard_map/ppermute | solution.py:617
  114.4 14.0 %collective-permute-start.22 = (bf16[256,512]{1,0:T(8,128)(2,1)S(1)}, bf16[256,512]{1,0:T(8,128)(2,1)S(1)}, u32[]{:S(2)}, u32[]{:S(2)}) collective-permute-start(bf16[256,512]{1,0:T(8,128)(2,1)S(1)} %add_convert_fusion.3.refs_15_), channel_id=1, source_target_pairs={{0,2},{1,3},{2,0},{3,1},{4,6},{5,7},{6,4},{7,5},{8,10},{9,11},{10,... | collective-permute-start | bytes 786440 | tf_op jit(solution)/shard_map/ppermute | solution.py:617
  115.7 12.7 %collective-permute-start.21 = (bf16[1,192,512]{2,1,0:T(8,128)(2,1)S(1)}, bf16[1,192,512]{2,1,0:T(8,128)(2,1)S(1)}, u32[]{:S(2)}, u32[]{:S(2)}) collective-permute-start(bf16[1,192,512]{2,1,0:T(8,128)(2,1)S(1)} %bitcast.33), channel_id=1, source_target_pairs={{0,16},{4,20},{8,24},{12,28},{16,0},{20,4},{24,8},{28,12},{1,17},{... | collective-permute-start | bytes 589832 | tf_op jit(solution)/shard_map/ppermute | solution.py:617
  128.4 2.1 collective-permute-start.23
  130.7 17.6 %collective-permute-start.24 = (bf16[304,1024]{1,0:T(8,128)(2,1)S(1)}, bf16[304,1024]{1,0:T(8,128)(2,1)S(1)}, u32[]{:S(2)}, u32[]{:S(2)}) collective-permute-start(bf16[304,1024]{1,0:T(8,128)(2,1)S(1)} %pair_sum.7.refs_35_.refs_0_), channel_id=1, source_target_pairs={{0,2},{1,3},{2,0},{3,1},{4,6},{5,7},{6,4},{7,5},{8,10},{9,11},{10,... | collective-permute-start | bytes 1867784 | tf_op jit(solution)/shard_map/ppermute | solution.py:617
  131.6 3.0 %collective-permute-start.25 = (bf16[256,1024]{1,0:T(8,128)(2,1)S(1)}, bf16[256,1024]{1,0:T(8,128)(2,1)S(1)}, u32[]{:S(2)}, u32[]{:S(2)}) collective-permute-start(bf16[256,1024]{1,0:T(8,128)(2,1)S(1)} %far_sum.6.refs_14_.refs_13_), channel_id=1, source_target_pairs={{0,1},{1,0},{2,3},{3,2},{4,5},{5,4},{6,7},{7,6},{8,9},{9,8},{10,11... | collective-permute-start | bytes 1572872 | tf_op jit(solution)/shard_map/ppermute | solution.py:617
  131.6 16.7 %collective-permute-start.27 = (bf16[2,192,512]{2,1,0:T(8,128)(2,1)S(1)}, bf16[2,192,512]{2,1,0:T(8,128)(2,1)S(1)}, u32[]{:S(2)}, u32[]{:S(2)}) collective-permute-start(bf16[2,192,512]{2,1,0:T(8,128)(2,1)S(1)} %pad_maximum_fusion.1.refs_0_), channel_id=1, source_target_pairs={{0,8},{4,12},{8,0},{12,4},{16,24},{20,28},{24,16},{28,20},{1,9},{5... | collective-permute-start | bytes 1179656 | tf_op jit(solution)/shard_map/ppermute | solution.py:617
  133.1 15.1 %collective-permute-start.28 = (bf16[2,192,512]{2,1,0:T(8,128)(2,1)S(1)}, bf16[2,192,512]{2,1,0:T(8,128)(2,1)S(1)}, u32[]{:S(2)}, u32[]{:S(2)}) collective-permute-start(bf16[2,192,512]{2,1,0:T(8,128)(2,1)S(1)} %pad_maximum_fusion.1.refs_0_), channel_id=1, source_target_pairs={{0,4},{4,0},{8,12},{12,8},{16,20},{20,16},{24,28},{28,24},{1,5},{5... | collective-permute-start | bytes 1179656 | tf_op jit(solution)/shard_map/ppermute | solution.py:617
  148.3 2.1 collective-permute-start.29
  148.4 3.3 %collective-permute-start.20 = (bf16[256,1024]{1,0:T(8,128)(2,1)S(1)}, bf16[256,1024]{1,0:T(8,128)(2,1)S(1)}, u32[]{:S(2)}, u32[]{:S(2)}) collective-permute-start(bf16[256,1024]{1,0:T(8,128)(2,1)S(1)} %get-tuple-element.167), channel_id=1, source_target_pairs={{0,1},{1,0},{2,3},{3,2},{4,5},{5,4},{6,7},{7,6},{8,9},{9,8},{10,11... | collective-permute-start | bytes 1572872 | tf_op jit(solution)/shard_map/ppermute | solution.py:617
  148.9 16.1 %collective-permute-start.31 = (bf16[2,192,512]{2,1,0:T(8,128)(2,1)S(1)}, bf16[2,192,512]{2,1,0:T(8,128)(2,1)S(1)}, u32[]{:S(2)}, u32[]{:S(2)}) collective-permute-start(bf16[2,192,512]{2,1,0:T(8,128)(2,1)S(1)} %collective-permute-done.27.refs_1_), channel_id=1, source_target_pairs={{0,4},{4,0},{8,12},{12,8},{16,20},{20,16},{24,28},{28,24},{1,5},{5... | collective-permute-start | bytes 1179656 | tf_op jit(solution)/shard_map/ppermute | solution.py:617
  149.6 4.4 %collective-permute-start.26 = (bf16[304,1024]{1,0:T(8,128)(2,1)S(1)}, bf16[304,1024]{1,0:T(8,128)(2,1)S(1)}, u32[]{:S(2)}, u32[]{:S(2)}) collective-permute-start(bf16[304,1024]{1,0:T(8,128)(2,1)S(1)} %far_sum.7.refs_13_), channel_id=1, source_target_pairs={{0,1},{1,0},{2,3},{3,2},{4,5},{5,4},{6,7},{7,6},{8,9},{9,8},{10,11... | collective-permute-start | bytes 1867784 | tf_op jit(solution)/shard_map/ppermute | solution.py:617
  150.4 15.4 %collective-permute-start.32 = (bf16[256,640]{1,0:T(8,128)(2,1)S(1)}, bf16[256,640]{1,0:T(8,128)(2,1)S(1)}, u32[]{:S(2)}, u32[]{:S(2)}) collective-permute-start(bf16[256,640]{1,0:T(8,128)(2,1)S(1)} %add_convert_fusion.1.refs_36_.refs_9_), channel_id=1, source_target_pairs={{0,2},{1,3},{2,0},{3,1},{4,6},{5,7},{6,4},{7,5},{8,10},{9,11},{10,... | collective-permute-start | bytes 983048 | tf_op jit(solution)/shard_map/ppermute | solution.py:617
  151.8 14.1 %collective-permute-start.33 = (bf16[256,512]{1,0:T(8,128)(2,1)S(1)}, bf16[256,512]{1,0:T(8,128)(2,1)S(1)}, u32[]{:S(2)}, u32[]{:S(2)}) collective-permute-start(bf16[256,512]{1,0:T(8,128)(2,1)S(1)} %add_convert_fusion.2.refs_37_), channel_id=1, source_target_pairs={{0,2},{1,3},{2,0},{3,1},{4,6},{5,7},{6,4},{7,5},{8,10},{9,11},{10,... | collective-permute-start | bytes 786440 | tf_op jit(solution)/shard_map/ppermute | solution.py:617
  152.7 12.3 %collective-permute-start.30 = (bf16[1,48,1024]{2,1,0:T(8,128)(2,1)S(1)}, bf16[1,48,1024]{2,1,0:T(8,128)(2,1)S(1)}, u32[]{:S(2)}, u32[]{:S(2)}) collective-permute-start(bf16[1,48,1024]{2,1,0:T(8,128)(2,1)S(1)} %slice_bitcast_fusion), channel_id=1, source_target_pairs={{0,16},{4,20},{8,24},{12,28},{16,0},{20,4},{24,8},{28,12},{1,17},{... | collective-permute-start | bytes 294920 | tf_op jit(solution)/shard_map/ppermute | solution.py:617
  165.9 3.5 %collective-permute-start.34 = (bf16[256,1152]{1,0:T(8,128)(2,1)S(1)}, bf16[256,1152]{1,0:T(8,128)(2,1)S(1)}, u32[]{:S(2)}, u32[]{:S(2)}) collective-permute-start(bf16[256,1152]{1,0:T(8,128)(2,1)S(1)} %get-tuple-element.196), channel_id=1, source_target_pairs={{0,1},{1,0},{2,3},{3,2},{4,5},{5,4},{6,7},{7,6},{8,9},{9,8},{10,11... | collective-permute-start | bytes 1769480 | tf_op jit(solution)/shard_map/ppermute | solution.py:617
  166.6 1.4 collective-permute-start.36
  168.1 4.8 %collective-permute-start.37 = (bf16[64,512]{1,0:T(8,128)(2,1)S(1)}, bf16[64,512]{1,0:T(8,128)(2,1)S(1)}, u32[]{:S(2)}, u32[]{:S(2)}) collective-permute-start(bf16[64,512]{1,0:T(8,128)(2,1)S(1)} %add_convert_fusion.5), channel_id=1, source_target_pairs={{0,2},{1,3},{2,0},{3,1},{4,6},{5,7},{6,4},{7,5},{8,10},{9,11},{10,... | collective-permute-start | bytes 196616 | tf_op jit(solution)/shard_map/ppermute | solution.py:617
  169.5 27.5 %collective-permute-start.35 = (bf16[256,640]{1,0:T(8,128)(2,1)S(1)}, bf16[256,640]{1,0:T(8,128)(2,1)}, u32[]{:S(2)}, u32[]{:S(2)}) collective-permute-start(bf16[256,640]{1,0:T(8,128)(2,1)S(1)} %add_convert_fusion.refs_4_), channel_id=1, source_target_pairs={{0,2},{1,3},{2,0},{3,1},{4,6},{5,7},{6,4},{7,5},{8,10},{9,11},{10,... | collective-permute-start | bytes 983048 | tf_op jit(solution)/shard_map/ppermute | solution.py:617
  170.4 26.7 %collective-permute-start.46 = (bf16[2,48,1024]{2,1,0:T(8,128)(2,1)}, bf16[2,48,1024]{2,1,0:T(8,128)(2,1)}, u32[]{:S(2)}, u32[]{:S(2)}) collective-permute-start(bf16[2,48,1024]{2,1,0:T(8,128)(2,1)} %pad_maximum_fusion.3), channel_id=1, source_target_pairs={{0,8},{4,12},{8,0},{12,4},{16,24},{20,28},{24,16},{28,20},{1,9},{5... | collective-permute-start | bytes 589832 | tf_op jit(solution)/shard_map/ppermute | solution.py:617
  174.4 33.8 %all-to-all-start.1 = ((bf16[8,64,512]{2,1,0:T(8,128)(2,1)}), bf16[8,64,512]{2,1,0:T(8,128)(2,1)S(1)}, u32[]{:S(2)}, u32[]{:S(2)}) async-start(bf16[8,64,512]{2,1,0:T(8,128)(2,1)} %select_convert_fusion), calls=%async_computation.1 | async-start | bytes 1048576 | tf_op jit(solution)/shard_map/all_to_all | solution.py:829
  178.0 28.0 %copy-start.2 = (bf16[256,640]{1,0:T(8,128)(2,1)S(1)}, bf16[256,640]{1,0:T(8,128)(2,1)}, u32[]{:S(2)}) copy-start(bf16[256,640]{1,0:T(8,128)(2,1)} %copy-done.1) | copy-start | bytes 983044
  178.0 28.0 %copy-start.15 = (f32[256,512]{1,0:T(8,128)S(1)}, f32[256,512]{1,0:T(8,128)}, u32[]{:S(2)}) copy-start(f32[256,512]{1,0:T(8,128)} %copy-done.14) | copy-start | bytes 1572868
  178.0 28.0 %copy-start.17 = (f32[256,512]{1,0:T(8,128)S(1)}, f32[256,512]{1,0:T(8,128)}, u32[]{:S(2)}) copy-start(f32[256,512]{1,0:T(8,128)} %copy-done.16) | copy-start | bytes 1572868
  178.0 28.0 %copy-start.25 = (bf16[256,640]{1,0:T(8,128)(2,1)S(1)}, bf16[256,640]{1,0:T(8,128)(2,1)}, u32[]{:S(2)}) copy-start(bf16[256,640]{1,0:T(8,128)(2,1)} %copy-done.24) | copy-start | bytes 983044
  178.0 28.0 %copy-start.29 = (f32[256,1]{1,0:T(8,128)S(1)}, f32[256,1]{1,0:T(8,128)}, u32[]{:S(2)}) copy-start(f32[256,1]{1,0:T(8,128)} %copy-done.28) | copy-start | bytes 3076
  178.0 28.0 %copy-start.31 = (f32[256,1]{1,0:T(8,128)S(1)}, f32[256,1]{1,0:T(8,128)}, u32[]{:S(2)}) copy-start(f32[256,1]{1,0:T(8,128)} %copy-done.30) | copy-start | bytes 3076
  178.1 18.8 %collective-permute-start.38 = (bf16[1,112,512]{2,1,0:T(8,128)(2,1)S(1)}, bf16[1,112,512]{2,1,0:T(8,128)(2,1)S(1)}, u32[]{:S(2)}, u32[]{:S(2)}) collective-permute-start(bf16[1,112,512]{2,1,0:T(8,128)(2,1)S(1)} %maximum_bitcast_fusion), channel_id=1, source_target_pairs={{0,16},{4,20},{8,24},{12,28},{16,0},{20,4},{24,8},{28,12},{1,17},{... | collective-permute-start | bytes 344072 | tf_op jit(solution)/shard_map/ppermute | solution.py:617
  196.9 6.1 %collective-permute-start.39 = (bf16[2,112,512]{2,1,0:T(8,128)(2,1)S(1)}, bf16[2,112,512]{2,1,0:T(8,128)(2,1)S(1)}, u32[]{:S(2)}, u32[]{:S(2)}) collective-permute-start(bf16[2,112,512]{2,1,0:T(8,128)(2,1)S(1)} %pad_maximum_fusion.2.refs_12_), channel_id=1, source_target_pairs={{0,8},{4,12},{8,0},{12,4},{16,24},{20,28},{24,16},{28,20},{1,9},{5... | collective-permute-start | bytes 688136 | tf_op jit(solution)/shard_map/ppermute | solution.py:617
  198.6 13.4 %collective-permute-start.47 = (bf16[4,48,1024]{2,1,0:T(8,128)(2,1)}, bf16[4,48,1024]{2,1,0:T(8,128)(2,1)}, u32[]{:S(2)}, u32[]{:S(2)}) collective-permute-start(bf16[4,48,1024]{2,1,0:T(8,128)(2,1)} %constant_dynamic-update-slice_fusion.2.refs_4_), channel_id=1, source_target_pairs={{0,4},{4,0},{8,12},{12,8},{16,20},{20,16},{24,28},{28,24},{1,5},{5... | collective-permute-start | bytes 1179656 | tf_op jit(solution)/shard_map/ppermute | solution.py:617
  203.0 19.5 %collective-permute-start.40 = (bf16[4,112,512]{2,1,0:T(8,128)(2,1)S(1)}, bf16[4,112,512]{2,1,0:T(8,128)(2,1)}, u32[]{:S(2)}, u32[]{:S(2)}) collective-permute-start(bf16[4,112,512]{2,1,0:T(8,128)(2,1)S(1)} %constant_dynamic-update-slice_fusion.refs_0_), channel_id=1, source_target_pairs={{0,4},{4,0},{8,12},{12,8},{16,20},{20,16},{24,28},{28,24},{1,5},{5... | collective-permute-start | bytes 1376264 | tf_op jit(solution)/shard_map/ppermute | solution.py:617
  208.3 16.9 %copy-start.19 = (bf16[2,192,512]{2,1,0:T(8,128)(2,1)S(1)}, bf16[2,192,512]{2,1,0:T(8,128)(2,1)}, u32[]{:S(2)}) copy-start(bf16[2,192,512]{2,1,0:T(8,128)(2,1)} %copy-done.18) | copy-start | bytes 1179652
  208.3 16.9 %copy-start.21 = (bf16[2,192,512]{2,1,0:T(8,128)(2,1)S(1)}, bf16[2,192,512]{2,1,0:T(8,128)(2,1)}, u32[]{:S(2)}) copy-start(bf16[2,192,512]{2,1,0:T(8,128)(2,1)} %copy-done.20) | copy-start | bytes 1179652
  208.3 25.1 %all-to-all-start.2 = ((bf16[8,64,512]{2,1,0:T(8,128)(2,1)}), bf16[8,64,512]{2,1,0:T(8,128)(2,1)S(1)}, u32[]{:S(2)}, u32[]{:S(2)}) async-start(bf16[8,64,512]{2,1,0:T(8,128)(2,1)} %bitcast.14), calls=%async_computation.2 | async-start | bytes 1048576 | tf_op jit(solution)/shard_map/all_to_all | solution.py:835
  211.9 13.2 %collective-permute-start.48 = (bf16[4,48,1024]{2,1,0:T(8,128)(2,1)}, bf16[4,48,1024]{2,1,0:T(8,128)(2,1)S(1)}, u32[]{:S(2)}, u32[]{:S(2)}) collective-permute-start(bf16[4,48,1024]{2,1,0:T(8,128)(2,1)} %constant_dynamic-update-slice_fusion.2.refs_4_), channel_id=1, source_target_pairs={{0,1},{1,0},{2,3},{3,2},{4,5},{5,4},{6,7},{7,6},{8,9},{9,8},{10,11... | collective-permute-start | bytes 1179656 | tf_op jit(solution)/shard_map/ppermute | solution.py:617
  212.0 13.1 %collective-permute-start.49 = (bf16[4,48,1024]{2,1,0:T(8,128)(2,1)}, bf16[4,48,1024]{2,1,0:T(8,128)(2,1)S(1)}, u32[]{:S(2)}, u32[]{:S(2)}) collective-permute-start(bf16[4,48,1024]{2,1,0:T(8,128)(2,1)} %collective-permute-done.47.refs_5_), channel_id=1, source_target_pairs={{0,1},{1,0},{2,3},{3,2},{4,5},{5,4},{6,7},{7,6},{8,9},{9,8},{10,11... | collective-permute-start | bytes 1179656 | tf_op jit(solution)/shard_map/ppermute | solution.py:617
  212.5 12.1 %collective-permute-start.43 = (bf16[4,64,512]{2,1,0:T(8,128)(2,1)S(1)}, bf16[4,64,512]{2,1,0:T(8,128)(2,1)S(1)}, u32[]{:S(2)}, u32[]{:S(2)}) collective-permute-start(bf16[4,64,512]{2,1,0:T(8,128)(2,1)S(1)} %slice.107.refs_2_), channel_id=1, source_target_pairs={{0,2},{1,3},{2,0},{3,1},{4,6},{5,7},{6,4},{7,5},{8,10},{9,11},{10,... | collective-permute-start | bytes 786440 | tf_op jit(solution)/shard_map/ppermute | solution.py:617
  223.5 8.0 %collective-permute-start.44 = (bf16[4,64,512]{2,1,0:T(8,128)(2,1)S(1)}, bf16[4,64,512]{2,1,0:T(8,128)(2,1)}, u32[]{:S(2)}, u32[]{:S(2)}) collective-permute-start(bf16[4,64,512]{2,1,0:T(8,128)(2,1)S(1)} %slice.108.refs_3_), channel_id=1, source_target_pairs={{0,2},{1,3},{2,0},{3,1},{4,6},{5,7},{6,4},{7,5},{8,10},{9,11},{10,... | collective-permute-start | bytes 786440 | tf_op jit(solution)/shard_map/ppermute | solution.py:617
  224.6 10.2 %collective-permute-start.41 = (bf16[4,64,512]{2,1,0:T(8,128)(2,1)S(1)}, bf16[4,64,512]{2,1,0:T(8,128)(2,1)}, u32[]{:S(2)}, u32[]{:S(2)}) collective-permute-start(bf16[4,64,512]{2,1,0:T(8,128)(2,1)S(1)} %slice.107.refs_2_), channel_id=1, source_target_pairs={{0,1},{1,0},{2,3},{3,2},{4,5},{5,4},{6,7},{7,6},{8,9},{9,8},{10,11... | collective-permute-start | bytes 786440 | tf_op jit(solution)/shard_map/ppermute | solution.py:617
  224.6 10.2 %collective-permute-start.45 = (bf16[4,64,512]{2,1,0:T(8,128)(2,1)S(1)}, bf16[4,64,512]{2,1,0:T(8,128)(2,1)}, u32[]{:S(2)}, u32[]{:S(2)}) collective-permute-start(bf16[4,64,512]{2,1,0:T(8,128)(2,1)S(1)} %collective-permute-done.43.refs_6_), channel_id=1, source_target_pairs={{0,1},{1,0},{2,3},{3,2},{4,5},{5,4},{6,7},{7,6},{8,9},{9,8},{10,11... | collective-permute-start | bytes 786440 | tf_op jit(solution)/shard_map/ppermute | solution.py:617
  231.5 3.3 %collective-permute-start.42 = (bf16[4,64,512]{2,1,0:T(8,128)(2,1)S(1)}, bf16[4,64,512]{2,1,0:T(8,128)(2,1)S(1)}, u32[]{:S(2)}, u32[]{:S(2)}) collective-permute-start(bf16[4,64,512]{2,1,0:T(8,128)(2,1)S(1)} %slice.108.refs_3_), channel_id=1, source_target_pairs={{0,1},{1,0},{2,3},{3,2},{4,5},{5,4},{6,7},{7,6},{8,9},{9,8},{10,11... | collective-permute-start | bytes 786440 | tf_op jit(solution)/shard_map/ppermute | solution.py:617
  231.5 3.3 %collective-permute-start.50 = (bf16[4,64,512]{2,1,0:T(8,128)(2,1)}, bf16[4,64,512]{2,1,0:T(8,128)(2,1)S(1)}, u32[]{:S(2)}, u32[]{:S(2)}) collective-permute-start(bf16[4,64,512]{2,1,0:T(8,128)(2,1)} %collective-permute-done.44.refs_7_), channel_id=1, source_target_pairs={{0,1},{1,0},{2,3},{3,2},{4,5},{5,4},{6,7},{7,6},{8,9},{9,8},{10,11... | collective-permute-start | bytes 786440 | tf_op jit(solution)/shard_map/ppermute | solution.py:617
  (35 other events, 225.1 us)

commit v3 on v2

--- a/solution.py
+++ b/solution.py
@@ -161,22 +161,24 @@
     heads = qt.shape[0] // HEAD
     group = heads // kv_heads
 
-    def one_head(i, carry):
-        j = i // group
-        q_h = qt[head_rows(i), :]
-        parts = []
-        for c, key in enumerate(keys):
-            s = nn(key[j], q_h)
-            parts.append(jnp.where(visible(c * rows, chunk * rows, rows, length), s, NEG_FILL))
+    kept = [jnp.concatenate([visible(c * rows, chunk * rows, rows, length)] * group, axis=1) for c in range(chunk + 1)]
+
+    def one_group(j, carry):
+        q_g = jnp.concatenate([qt[head_rows(j * group + g), :] for g in range(group)], axis=1)
+        parts = [jnp.where(kept[c], nn(keys[c][j], q_g), NEG_FILL) for c in range(chunk + 1)]
         top = functools.reduce(jnp.maximum, [jnp.max(s, axis=0, keepdims=True) for s in parts])
         es = [jnp.exp(s - top) for s in parts]
         total = sum(jnp.sum(e, axis=0, keepdims=True) for e in es)
-        lse_out[pl.ds(i, 1), :] = top + jnp.log(total)
+        low = top + jnp.log(total)
         o_t = sum(nn(value[head_rows(j), :], e.astype(BF16)) for value, e in zip(values, es))
-        ot_out[head_rows(i), :] = (o_t / total).astype(BF16)
+        o_t = (o_t / total).astype(BF16)
+        for g in range(group):
+            cols = slice(g * rows, (g + 1) * rows)
+            lse_out[pl.ds(j * group + g, 1), :] = low[:, cols]
+            ot_out[head_rows(j * group + g), :] = o_t[:, cols]
         return carry
 
-    lax.fori_loop(0, heads, one_head, 0, unroll=2)
+    lax.fori_loop(0, kv_heads, one_group, 0)
     o = ot_out[...].T
     to = nt(o, oa[...])
     tot_out[...] = to.T.astype(BF16)
@@ -323,30 +325,29 @@
     copies[0].wait()
     d_o = nt(dz, wo[...]) + nn(dto.astype(BF16), oa[...])
     dot_s[...] = d_o.T.astype(BF16)
-    if last:
+    kept = [jnp.concatenate([visible(c * rows, chunk * rows, rows, length)] * group, axis=1) for c in range(chunk + 1)]
+
+    def one_group(j, carry):
+        places = [head_rows(j * group + g) for g in range(group)]
+        q_g = jnp.concatenate([qt[at, :] for at in places], axis=1)
+        do_g = jnp.concatenate([dot_s[at, :] for at in places], axis=1)
+        o_g = jnp.concatenate([ot[at, :] for at in places], axis=1)
+        low = jnp.concatenate([lse[pl.ds(j * group + g, 1), :] for g in range(group)], axis=1)
+        dots = jnp.sum(do_g.astype(F32) * o_g.astype(F32), axis=0, keepdims=True)
+        dq_g = 0.0
         for c in range(chunk + 1):
-            dkt_s[c], dvt_s[c] = rest[2][...], rest[3][...]
-    else:
-        dkt_s[...] = jnp.zeros_like(dkt_s)
-        dvt_s[...] = jnp.zeros_like(dvt_s)
-
-    def one_head(i, carry):
-        j = i // group
-        q_h, do_h = qt[head_rows(i), :], dot_s[head_rows(i), :]
-        dots = jnp.sum(do_h.astype(F32) * ot[head_rows(i), :].astype(F32), axis=0, keepdims=True)
-        low = lse[pl.ds(i, 1), :]
-        dq_h = jnp.zeros((HEAD, rows), F32)
-        for c in range(chunk + 1):
-            prob = jnp.exp(nn(keys[c][j], q_h) - low)
-            prob = jnp.where(visible(c * rows, chunk * rows, rows, length), prob, 0.0)
-            ds = (prob * (nn(values[c][j], do_h) - dots)).astype(BF16)
-            dq_h = dq_h + nn(keys_t[c][head_rows(j), :], ds)
-            dkt_s[c, head_rows(j), :] += nt(q_h, ds)
-            dvt_s[c, head_rows(j), :] += nt(do_h, prob.astype(BF16))
-        dqt_s[head_rows(i), :] = dq_h
+            prob = jnp.where(kept[c], jnp.exp(nn(keys[c][j], q_g) - low), 0.0)
+            ds = (prob * (nn(values[c][j], do_g) - dots)).astype(BF16)
+            dq_g = dq_g + nn(keys_t[c][head_rows(j), :], ds)
+            dk, dv = nt(q_g, ds), nt(do_g, prob.astype(BF16))
+            if last:
+                dk, dv = dk + rest[2][head_rows(j), :], dv + rest[3][head_rows(j), :]
+            dkt_s[c, head_rows(j), :], dvt_s[c, head_rows(j), :] = dk, dv
+        for g in range(group):
+            dqt_s[places[g], :] = dq_g[:, g * rows:(g + 1) * rows]
         return carry
 
-    lax.fori_loop(0, heads, one_head, 0, unroll=2)
+    lax.fori_loop(0, kv_heads, one_group, 0)
     if not last:
         outs[6][...], outs[7][...] = dkt_s[0], dvt_s[0]
     cos, sin = cos_t[...], sin_t[...]
@@ -704,7 +705,7 @@
          output_adapter_output, feedfwd_adapter_input, feedfwd_adapter_output, down_adapter_input,
          down_adapter_output), "adapters", info)
     a1, qb, kvb, oa, ob, a2, fba, da, bd = adapters_here
-    dealt = late(dealt, gs[2], a1)
+    dealt = late(dealt, gs[2], a1, gains)
     beside = near(dealt)
     there = [far(dealt[c * rows:(c + 1) * rows]) for c in range(CHUNKS)]
     xs = [None] * CHUNKS
@@ -821,23 +822,22 @@
     att = jnp.concatenate([att_b, (aa_low + late(aa_far, h_high).astype(F32)).astype(BF16)], axis=0)[None]
     att = doubled(att, bits[0], dp)
 
+    dinput, = call(finish_kernel, None, (), (gains, dealt, *(v for f in final for v in f)), [((length, QUARTER), BF16)],
+                   [], "finish", 8, (att,))
+    back_grad = lax.all_to_all(
+        dinput.reshape(dp, length // dp, QUARTER), "dp", split_axis=0, concat_axis=0, tiled=True)
+    input_grad = move_rows(collect_kernel, back_grad, dealing_slots, "collect_grad", False)
+
     valid = (jnp.arange(length, dtype=jnp.int32) < my_length)[:, None]
     result = jnp.concatenate(
         [hidden[c][1] + y_keep[c][:, :QUARTER] + late(y_got[c], h_high)[:, :QUARTER].astype(F32) + y_far[c].astype(F32)
          for c in range(CHUNKS)], axis=0)
-    result = jnp.where(valid, result, 0.0).astype(BF16)
+    result = late(jnp.where(valid, result, 0.0).astype(BF16), dinput)
     back_out = lax.all_to_all(
         result.reshape(dp, length // dp, QUARTER), "dp", split_axis=0, concat_axis=0, tiled=True)
-    output = move_rows(collect_kernel, back_out, dealing_slots, "collect_out", False)
-
-    dinput, = call(finish_kernel, None, (), (gains, dealt, *(v for f in final for v in f)), [((length, QUARTER), BF16)],
-                   [], "finish", 8, (att,))
-    back_grad = lax.all_to_all(
-        dinput.reshape(dp, length // dp, QUARTER), "dp", split_axis=0, concat_axis=0, tiled=True)
-    input_grad = move_rows(collect_kernel, back_grad, late(dealing_slots, output), "collect_grad", False)
+    output = move_rows(collect_kernel, back_out, late(dealing_slots, input_grad), "collect_out", False)
 
     n_b = att_b.shape[0]
-    att = late(att, h_far)
     for bit in bits[1:-1]:
         att = doubled(att, bit, dp)
     att_side = swap(att, bits[-1], "dp", dp)

time: 240 us -> 235 us (0.979)
  Pallas kernels: 115 us -> 108 us
  starting transfers between devices: 50.6 us -> 46 us
    pallas_call x19, Pallas kernels: 89.5 us -> 82.5 us  [call(): pl.pallas_call(body, in_specs=[pl.BlockSpec(memory_space=pltpu.SMEM)] * n...]
    ppermute x51, starting transfers between devices: 36.2 us -> 31.6 us  [swap(): return lax.ppermute(value, axis, [(i, i ^ bit) for i in range(size)])]
    ppermute x51, waiting for transfers between devices: 55.5 us -> 58.8 us  [swap(): return lax.ppermute(value, axis, [(i, i ^ bit) for i in range(size)])]
    unnamed x92 -> x91, local copies, waits for them, and re-layouts: 6.88 us -> 9.8 us
  transfers between devices with their start and end apart: 54 -> 54, of which waited for: 18 -> 19; matrix products, arithmetic and copies ran while one was open for 5% -> 5% of each run, Pallas kernels for 36% -> 35%
where the time goes in v3:
time: 235 us; the launch traced here: 234 us
  Pallas kernels  108 us (46%)
  waiting for transfers between devices  58.8 us (25%)
  starting transfers between devices  46 us (20%)
  local copies, waits for them, and re-layouts  10.8 us (5%)
  other arithmetic  8.81 us (4%)
    pallas_call x19, Pallas kernels, call(): pl.pallas_call(body, in_specs=[pl.BlockSpec(memory_space=pltpu.SMEM)] * n...  82.5 us
    ppermute x51, waiting for transfers between devices, swap(): return lax.ppermute(value, axis, [(i, i ^ bit) for i in range(size)])  58.8 us
    ppermute x51, starting transfers between devices, swap(): return lax.ppermute(value, axis, [(i, i ^ bit) for i in range(size)])  31.6 us
    pallas_call x2, Pallas kernels, sum_call(): pl.pallas_call(functools.partial(kernel, [len(group) for group in groups]...  10.1 us
    pallas_call x2, Pallas kernels, load(): pl.pallas_call(body, in_specs=[pl.BlockSpec(memory_space=pltpu.SMEM)] * l...  9.97 us
    unnamed x91, local copies, waits for them, and re-layouts  9.8 us
    all_to_all x1, starting transfers between devices, shards(): lax.all_to_all(move_rows(deal_kernel, residual, dealing_slots, 'deal', Tr...  7.26 us
    pallas_call x3, Pallas kernels, move_rows(): pl.pallas_call(kernel, in_specs=[pl.BlockSpec(memory_space=pltpu.SMEM), p...  5.25 us
  transfers between devices with their start and end apart: 54, of which 19 were waited for; matrix products, arithmetic and copies ran while one was open for 5% of the time, Pallas kernels for 35%

profile of v3, /device:TPU:0, one launch (start us, length us, event | category | flops | bytes accessed | tf_op | source)
XLA Modules:
  0.0 233.9 jit_solution(17233777038360395853)
XLA Ops:
  1.4 2.5 %deal.1 = bf16[8,64,512]{2,1,0:T(8,128)(2,1)} custom-call(s32[8]{0:T(128)S(1)} %copy-done.26, bf16[8,64,512]{2,1,0:T(8,128)(2,1)} %source.1), custom_call_target="tpu_custom_call" | custom-call | flops 1000 | bytes 1000 | tf_op jit(solution)/shard_map/deal/pallas_call | solution.py:551
  3.9 7.3 %all-to-all-start = ((bf16[8,64,512]{2,1,0:T(8,128)(2,1)}), bf16[8,64,512]{2,1,0:T(8,128)(2,1)S(1)}, u32[]{:S(2)}, u32[]{:S(2)}) async-start(bf16[8,64,512]{2,1,0:T(8,128)(2,1)} %deal.1), calls=%async_computation | async-start | bytes 1048576 | tf_op jit(solution)/shard_map/all_to_all | solution.py:700
  11.2 1.6 collective-permute-start.1
  15.6 1.4 pad_add_fusion.refs_0_.info
  16.9 1.8 adapters.1
  18.8 8.3 %collective-permute-done.3.refs_11_.refs_10_ = bf16[512,512]{1,0:T(8,128)(2,1)S(1)} collective-permute-done((bf16[512,512]{1,0:T(8,128)(2,1)S(1)}, bf16[512,512]{1,0:T(8,128)(2,1)S(1)}, u32[]{:S(2)}, u32[]{:S(2)}) %collective-permute-start.3) | collective-permute-done | bytes 524320 | tf_op jit(solution)/shard_map/ppermute | solution.py:618
  27.7 7.4 %collective-permute-done.5.refs_5_.refs_6_ = bf16[256,512]{1,0:T(8,128)(2,1)S(1)} collective-permute-done((bf16[256,512]{1,0:T(8,128)(2,1)S(1)}, bf16[256,512]{1,0:T(8,128)(2,1)S(1)}, u32[]{:S(2)}, u32[]{:S(2)}) %collective-permute-start.5) | collective-permute-done | bytes 262176 | tf_op jit(solution)/shard_map/ppermute | solution.py:618
  35.7 1.0 collective-permute-done.6.refs_6_.refs_7_
  36.7 4.1 %project_0.1 = (bf16[256,2048]{1,0:T(8,128)(2,1)S(1)}, bf16[48,256]{1,0:T(8,128)(2,1)S(1)}, bf16[512,256]{1,0:T(8,128)(2,1)S(1)}, bf16[2,256,64]{2,1,0:T(8,128)(...) custom-call(s32[4]{0:T(128)S(1)} %pad_add_fusion.refs_0_.info, ...), custom_call_target="tpu_custom_call" | custom-call | flops 1000 | bytes 1000 | tf_op jit(solution)/shard_map/project_0/pallas_call | solution.py:584
  40.8 1.0 copy-done.1
  41.8 2.1 collective-permute-done.9.refs_5_.refs_6_
  43.9 1.5 collective-permute-done.10.refs_6_.refs_7_
  45.4 4.1 %project_1.1 = (bf16[256,2048]{1,0:T(8,128)(2,1)S(1)}, bf16[48,256]{1,0:T(8,128)(2,1)S(1)}, bf16[512,256]{1,0:T(8,128)(2,1)S(1)}, bf16[2,256,64]{2,1,0:T(8,128)(...) custom-call(s32[4]{0:T(128)S(1)} %pad_add_fusion.refs_0_.info, ...), custom_call_target="tpu_custom_call" | custom-call | flops 1000 | bytes 1000 | tf_op jit(solution)/shard_map/project_1/pallas_call | solution.py:584
  49.5 3.7 %attend_1.1 = (f32[256,1024]{1,0:T(8,128)S(1)}, bf16[256,1024]{1,0:T(8,128)(2,1)S(1)}, bf16[512,256]{1,0:T(8,128)(2,1)S(1)}, f32[8,256]{1,0:T(8,128)S(1)}, bf16[16,256]{1,0:T(8,128)(2,1)S(1)}) custom-call(s32[4]{0:T(128)S(1)} %pad_add_fusion.refs_0_.info, bf16[512,2048]{1,0:T(8,128)(2,1)} %refs_3_.5, ...), custom_call_target="tpu_custom_call" | custom-call | flops 1000 | bytes 1000 | tf_op jit(solution)/shard_map/attend_1/pallas_call | solution.py:584
  53.5 1.8 collective-permute-done.11.refs_1_
  55.9 3.1 %attend_0.1 = (f32[256,1024]{1,0:T(8,128)S(1)}, bf16[256,1024]{1,0:T(8,128)(2,1)S(1)}, bf16[512,256]{1,0:T(8,128)(2,1)S(1)}, f32[8,256]{1,0:T(8,128)S(1)}, bf16[16,256]{1,0:T(8,128)(2,1)S(1)}) custom-call(s32[4]{0:T(128)S(1)} %pad_add_fusion.refs_0_.info, bf16[512,2048]{1,0:T(8,128)(2,1)} %refs_3_.5, ...), custom_call_target="tpu_custom_call" | custom-call | flops 1000 | bytes 1000 | tf_op jit(solution)/shard_map/attend_0/pallas_call | solution.py:584
  59.6 8.2 %load.1 = (bf16[2,2048,2048]{2,1,0:T(8,128)(2,1)S(1)}, bf16[2048,2048]{1,0:T(8,128)(2,1)S(1)}) custom-call(bf16[2,2048,2048]{2,1,0:T(8,128)(2,1)} %refs_0_.1, bf16[2048,2048]{1,0:T(8,128)(2,1)} %refs_1_.13, f32[8,256]{1,0:T(8,128)S(1)} %get-tuple-element.134.refs_2_.refs_18_.refs_27_, bf16[256,1024]{1,0:T(8,128)(2,1)S(1)} %pair_sum.4.refs_8_.refs_3_.refs_0_.refs_19_), custom_call_target="tpu_custom_call" | custom-call | flops 1000 | bytes 1000 | tf_op jit(solution)/shard_map/load/pallas_call | solution.py:536
  67.8 1.5 collective-permute-done.14.refs_1_
  70.3 1.2 collective-permute-done.15.refs_8_
  71.5 11.5 %front_1.1 = (bf16[256,2048]{1,0:T(8,128)(2,1)S(1)}, f32[256,512]{1,0:T(8,128)S(1)}, bf16[256,2048]{1,0:T(8,128)(2,1)S(1)}, bf16[256,2048]{1,0:T(8,128)(2,1)S(1)...) custom-call(s32[4]{0:T(128)S(1)} %pad_add_fusion.refs_0_.info, ...), custom_call_target="tpu_custom_call" | custom-call | flops 1000 | bytes 1000 | tf_op jit(solution)/shard_map/front_1/pallas_call | solution.py:584
  83.0 1.1 collective-permute-done.13.refs_1_
  84.2 11.0 %back_1.1 = (f32[256,1024]{1,0:T(8,128)S(1)}, bf16[256,1024]{1,0:T(8,128)(2,1)S(1)}, f32[256,1024]{1,0:T(8,128)S(1)}, bf16[256,1024]{1,0:T(8,128)(2,1)S(1)}, f32[48,2048]{1,0:T(8,128)S(1)}) custom-call(s32[4]{0:T(128)S(1)} %pad_add_fusion.refs_0_.info, bf16[2,2048,2048]{2,1,0:T(8,128)(2,1)S(1)} %get-tuple-element.135.refs_1_, ...), custom_call_target="tpu_custom_call" | custom-call | flops 1000 | bytes 1000 | tf_op jit(solution)/shard_map/back_1/pallas_call | solution.py:584
  95.9 1.3 collective-permute-done.17.refs_1_
  97.9 11.9 %front_0.1 = (bf16[256,2048]{1,0:T(8,128)(2,1)S(1)}, f32[256,512]{1,0:T(8,128)S(1)}, bf16[256,2048]{1,0:T(8,128)(2,1)S(1)}, bf16[256,2048]{1,0:T(8,128)(2,1)S(1)...) custom-call(s32[4]{0:T(128)S(1)} %pad_add_fusion.refs_0_.info, ...), custom_call_target="tpu_custom_call" | custom-call | flops 1000 | bytes 1000 | tf_op jit(solution)/shard_map/front_0/pallas_call | solution.py:584
  109.9 1.0 copy-done.3
  111.7 1.5 collective-permute-start.21
  113.2 2.9 %collective-permute-start.20 = (bf16[1,192,512]{2,1,0:T(8,128)(2,1)S(1)}, bf16[1,192,512]{2,1,0:T(8,128)(2,1)S(1)}, u32[]{:S(2)}, u32[]{:S(2)}) collective-permute-start(bf16[1,192,512]{2,1,0:T(8,128)(2,1)S(1)} %bitcast.33), channel_id=1, source_target_pairs={{0,16},{4,20},{8,24},{12,28},{16,0},{20,4},{24,8},{28,12},{1,17},{... | collective-permute-start | bytes 589832 | tf_op jit(solution)/shard_map/ppermute | solution.py:618
  116.2 11.1 %back_0.1 = (f32[304,1024]{1,0:T(8,128)S(1)}, bf16[304,1024]{1,0:T(8,128)(2,1)S(1)}, f32[256,1024]{1,0:T(8,128)S(1)}, bf16[256,1024]{1,0:T(8,128)(2,1)S(1)}) custom-call(s32[4]{0:T(128)S(1)} %copy-done.24, bf16[2,2048,2048]{2,1,0:T(8,128)(2,1)S(1)} %get-tuple-element.135.refs_1_, bf16[2048,2048]{1,0:T(8,128)(2,1)S(1)} %get-tuple-element.136.refs_2_, ...), custom_call_target="tpu_custom_call" | custom-call | flops 1000 | bytes 1000 | tf_op jit(solution)/shard_map/back_0/pallas_call | solution.py:584
  127.5 2.0 collective-permute-done.22.refs_1_
  130.3 1.6 collective-permute-start.26
  131.9 1.5 collective-permute-start.27
  133.3 10.4 %attend_back_1.1 = (f32[256,512]{1,0:T(8,128)S(1)}, f32[256,1152]{1,0:T(8,128)S(1)}, bf16[256,1152]{1,0:T(8,128)(2,1)S(1)}, f32[256,1]{1,0:T(8,128)S(1)}, f32[48...) custom-call(s32[4]{0:T(128)S(1)} %copy-done.24, ...), custom_call_target="tpu_custom_call" | custom-call | flops 1000 | bytes 1000 | tf_op jit(solution)/shard_map/attend_back_1/pallas_call | solution.py:584
  144.6 1.2 collective-permute-done.23.refs_1_
  146.2 1.5 collective-permute-start.31
  148.8 1.5 collective-permute-start.33
  150.9 1.2 iota_compare_fusion.1
  152.1 9.5 %attend_back_0.1 = (f32[256,512]{1,0:T(8,128)S(1)}, f32[256,1152]{1,0:T(8,128)S(1)}, bf16[256,1152]{1,0:T(8,128)(2,1)S(1)}, f32[256,1]{1,0:T(8,128)S(1)}, bf16[4...) custom-call(s32[4]{0:T(128)S(1)} %copy-done.24, bf16[2048,512]{1,0:T(8,128)(2,1)} %refs_1_.15, ...), custom_call_target="tpu_custom_call" | custom-call | flops 1000 | bytes 1000 | tf_op jit(solution)/shard_map/attend_back_0/pallas_call | solution.py:584
  161.6 2.2 collective-permute-done.33
  165.1 0.9 collective-permute-done.36
  166.8 1.5 collective-permute-start.35
  168.3 1.5 collective-permute-start.46
  169.8 1.3 collective-permute-done.37
  171.8 7.0 %collective-permute-done.38 = bf16[1,112,512]{2,1,0:T(8,128)(2,1)S(1)} collective-permute-done((bf16[1,112,512]{2,1,0:T(8,128)(2,1)S(1)}, bf16[1,112,512]{2,1,0:T(8,128)(2,1)S(1)}, u32[]{:S(2)}, u32[]{:S(2)}) %collective-permute-start.38) | collective-permute-done | bytes 114720 | tf_op jit(solution)/shard_map/ppermute | solution.py:618
  178.8 1.2 finish.1
  180.0 3.6 %all-to-all-start.1 = ((bf16[8,64,512]{2,1,0:T(8,128)(2,1)}), bf16[8,64,512]{2,1,0:T(8,128)(2,1)S(1)}, u32[]{:S(2)}, u32[]{:S(2)}) async-start(bf16[8,64,512]{2,1,0:T(8,128)(2,1)} %bitcast.13), calls=%async_computation.1 | async-start | bytes 1048576 | tf_op jit(solution)/shard_map/all_to_all | solution.py:827
  183.7 1.4 convert_add_fusion.1
  185.2 1.1 convert_add_fusion
  186.3 2.0 collective-permute-start.39
  188.2 0.9 constant_dynamic-update-slice_fusion.1
  189.2 0.9 constant_dynamic-update-slice_fusion.refs_4_
  190.2 1.5 collective-permute-start.47
  191.7 7.1 %collective-permute-done.39 = bf16[2,112,512]{2,1,0:T(8,128)(2,1)S(1)} collective-permute-done((bf16[2,112,512]{2,1,0:T(8,128)(2,1)S(1)}, bf16[2,112,512]{2,1,0:T(8,128)(2,1)S(1)}, u32[]{:S(2)}, u32[]{:S(2)}) %collective-permute-start.39) | collective-permute-done | bytes 229408 | tf_op jit(solution)/shard_map/ppermute | solution.py:618
  198.9 1.2 collective-permute-start.40
  200.1 1.0 fusion
  201.1 3.5 %all-to-all-start.2 = ((bf16[8,64,512]{2,1,0:T(8,128)(2,1)}), bf16[8,64,512]{2,1,0:T(8,128)(2,1)S(1)}, u32[]{:S(2)}, u32[]{:S(2)}) async-start(bf16[8,64,512]{2,1,0:T(8,128)(2,1)} %bitcast.14), calls=%async_computation.2 | async-start | bytes 1048576 | tf_op jit(solution)/shard_map/all_to_all | solution.py:836
  205.7 9.6 %collective-permute-done.40.refs_1_ = bf16[4,112,512]{2,1,0:T(8,128)(2,1)S(1)} collective-permute-done((bf16[4,112,512]{2,1,0:T(8,128)(2,1)S(1)}, bf16[4,112,512]{2,1,0:T(8,128)(2,1)S(1)}, u32[]{:S(2)}, u32[]{:S(2)}) %collective-permute-start.40) | collective-permute-done | bytes 458784 | tf_op jit(solution)/shard_map/ppermute | solution.py:618
  216.4 1.0 copy-done.8
  217.4 1.0 copy-done.13
  218.4 1.0 copy-done.15
  219.4 1.0 copy-done.17
  220.4 5.2 %feedforward_sum.1 = (f32[8,32,2048]{2,1,0:T(8,128)}, f32[8,16,2048]{2,1,0:T(8,128)}, f32[8,2,16,2048]{3,2,1,0:T(8,128)}, f32[8,16,2048]{2,1,0:T(8,128)}) custom-call(s32[4]{0:T(128)S(1)} %copy-done.25, s32[8]{0:T(128)S(1)} %copy-done.30, bf16[2,192,512]{2,1,0:T(8,128)(2,1)S(1)} %pad_maximum_fusion.1.refs_0_, bf16[2,192,512]{2,1,0:T(8,128)(2,1)S(1)} %copy-done.13, ...), custom_call_target="tpu_custom_call" | custom-call | bytes 12000000 | tf_op jit(solution)/shard_map/feedforward_sum/pallas_call | solution.py:602
  226.0 1.4 collect_grad.1
  227.4 1.4 collect_out.1
  228.9 4.9 %attention_sum.1 = (f32[8,48,2048]{2,1,0:T(8,128)}, f32[8,16,2048]{2,1,0:T(8,128)}, f32[8,16,512]{2,1,0:T(8,128)}, f32[8,2,16,128]{3,2,1,0:T(8,128)}, f32[8,16,512]{2,1,0:T(8,128)}) custom-call(s32[4]{0:T(128)S(1)} %copy-done.25, s32[8]{0:T(128)S(1)} %copy-done.30, bf16[4,112,512]{2,1,0:T(8,128)(2,1)S(1)} %pad_maximum_fusion.refs_0_, ...), custom_call_target="tpu_custom_call" | custom-call | bytes 12000000 | tf_op jit(solution)/shard_map/attention_sum/pallas_call | solution.py:602
  (192 shorter events, 18.9 us)
Async XLA Ops:
  3.9 23.3 %all-to-all-start = ((bf16[8,64,512]{2,1,0:T(8,128)(2,1)}), bf16[8,64,512]{2,1,0:T(8,128)(2,1)S(1)}, u32[]{:S(2)}, u32[]{:S(2)}) async-start(bf16[8,64,512]{2,1,0:T(8,128)(2,1)} %deal.1), calls=%async_computation | async-start | bytes 1048576 | tf_op jit(solution)/shard_map/all_to_all | solution.py:700
  11.2 4.1 %collective-permute-start.1 = (bf16[2,512]{1,0:T(2,128)(2,1)S(1)}, bf16[2,512]{1,0:T(2,128)(2,1)S(1)}, u32[]{:S(2)}, u32[]{:S(2)}) collective-permute-start(bf16[2,512]{1,0:T(2,128)(2,1)S(1)} %pad_maximum_fusion.5), channel_id=1, source_target_pairs={{0,2},{1,3},{2,0},{3,1},{4,6},{5,7},{6,4},{7,5},{8,10},{9,11},{10,... | collective-permute-start | bytes 6152 | tf_op jit(solution)/shard_map/ppermute | solution.py:618
  12.8 6.0 %collective-permute-start = (bf16[2,512]{1,0:T(2,128)(2,1)S(1)}, bf16[2,512]{1,0:T(2,128)(2,1)S(1)}, u32[]{:S(2)}, u32[]{:S(2)}) collective-permute-start(bf16[2,512]{1,0:T(2,128)(2,1)S(1)} %pad_maximum_fusion.5), channel_id=1, source_target_pairs={{0,1},{1,0},{2,3},{3,2},{4,5},{5,4},{6,7},{7,6},{8,9},{9,8},{10,11... | collective-permute-start | bytes 6152 | tf_op jit(solution)/shard_map/ppermute | solution.py:618
  12.8 14.3 %collective-permute-start.3 = (bf16[512,512]{1,0:T(8,128)(2,1)S(1)}, bf16[512,512]{1,0:T(8,128)(2,1)S(1)}, u32[]{:S(2)}, u32[]{:S(2)}) collective-permute-start(bf16[512,512]{1,0:T(8,128)(2,1)S(1)} %bitcast.27), channel_id=1, source_target_pairs={{0,2},{1,3},{2,0},{3,1},{4,6},{5,7},{6,4},{7,5},{8,10},{9,11},{10,... | collective-permute-start | bytes 1572872 | tf_op jit(solution)/shard_map/ppermute | solution.py:618
  15.3 3.5 %collective-permute-start.2 = (bf16[2,512]{1,0:T(2,128)(2,1)S(1)}, bf16[2,512]{1,0:T(2,128)(2,1)S(1)}, u32[]{:S(2)}, u32[]{:S(2)}) collective-permute-start(bf16[2,512]{1,0:T(2,128)(2,1)S(1)} %collective-permute-done.1), channel_id=1, source_target_pairs={{0,1},{1,0},{2,3},{3,2},{4,5},{5,4},{6,7},{7,6},{8,9},{9,8},{10,11... | collective-permute-start | bytes 6152 | tf_op jit(solution)/shard_map/ppermute | solution.py:618
  16.9 81.0 %copy-start.23 = (s32[4]{0:T(128)}, s32[4]{0:T(128)S(1)}, u32[]{:S(2)}) copy-start(s32[4]{0:T(128)S(1)} %pad_add_fusion.refs_0_.info) | copy-start | bytes 52
  16.9 19.8 %copy-start.18 = (f32[32,256]{1,0:T(8,128)S(1)}, f32[32,256]{1,0:T(8,128)}, u32[]{:S(2)}) copy-start(f32[32,256]{1,0:T(8,128)} %constant.21.clone.refs_11_.refs_21_) | copy-start | bytes 98308
  16.9 19.8 %copy-start.19 = (f32[32,256]{1,0:T(8,128)S(1)}, f32[32,256]{1,0:T(8,128)}, u32[]{:S(2)}) copy-start(f32[32,256]{1,0:T(8,128)} %constant.23.clone.refs_12_.refs_22_) | copy-start | bytes 98308
  27.2 8.0 %collective-permute-start.5 = (bf16[256,512]{1,0:T(8,128)(2,1)S(1)}, bf16[256,512]{1,0:T(8,128)(2,1)S(1)}, u32[]{:S(2)}, u32[]{:S(2)}) collective-permute-start(bf16[256,512]{1,0:T(8,128)(2,1)S(1)} %get-tuple-element.224), channel_id=1, source_target_pairs={{0,2},{1,3},{2,0},{3,1},{4,6},{5,7},{6,4},{7,5},{8,10},{9,11},{10,... | collective-permute-start | bytes 786440 | tf_op jit(solution)/shard_map/ppermute | solution.py:618
  27.7 9.0 %collective-permute-start.4 = (bf16[512,512]{1,0:T(8,128)(2,1)S(1)}, bf16[512,512]{1,0:T(8,128)(2,1)S(1)}, u32[]{:S(2)}, u32[]{:S(2)}) collective-permute-start(bf16[512,512]{1,0:T(8,128)(2,1)S(1)} %bitcast.19), channel_id=1, source_target_pairs={{0,1},{1,0},{2,3},{3,2},{4,5},{5,4},{6,7},{7,6},{8,9},{9,8},{10,11... | collective-permute-start | bytes 1572872 | tf_op jit(solution)/shard_map/ppermute | solution.py:618
  35.2 1.5 collective-permute-start.6
  35.2 8.7 %collective-permute-start.9 = (bf16[256,512]{1,0:T(8,128)(2,1)S(1)}, bf16[256,512]{1,0:T(8,128)(2,1)S(1)}, u32[]{:S(2)}, u32[]{:S(2)}) collective-permute-start(bf16[256,512]{1,0:T(8,128)(2,1)S(1)} %get-tuple-element.223), channel_id=1, source_target_pairs={{0,2},{1,3},{2,0},{3,1},{4,6},{5,7},{6,4},{7,5},{8,10},{9,11},{10,... | collective-permute-start | bytes 786440 | tf_op jit(solution)/shard_map/ppermute | solution.py:618
  43.9 1.5 collective-permute-start.10
  53.3 2.0 collective-permute-start.11
  55.3 14.0 %collective-permute-start.14 = (bf16[256,1024]{1,0:T(8,128)(2,1)S(1)}, bf16[256,1024]{1,0:T(8,128)(2,1)S(1)}, u32[]{:S(2)}, u32[]{:S(2)}) collective-permute-start(bf16[256,1024]{1,0:T(8,128)(2,1)S(1)} %pair_sum.4.refs_8_.refs_3_.refs_0_.refs_19_), channel_id=1, source_target_pairs={{0,2},{1,3},{2,0},{3,1},{4,6},{5,7},{6,4},{7,5},{8,10},{9,11},{10,... | collective-permute-start | bytes 1572872 | tf_op jit(solution)/shard_map/ppermute | solution.py:618
  59.0 10.6 %collective-permute-start.12 = (bf16[256,1024]{1,0:T(8,128)(2,1)S(1)}, bf16[256,1024]{1,0:T(8,128)(2,1)S(1)}, u32[]{:S(2)}, u32[]{:S(2)}) collective-permute-start(bf16[256,1024]{1,0:T(8,128)(2,1)S(1)} %get-tuple-element.138), channel_id=1, source_target_pairs={{0,1},{1,0},{2,3},{3,2},{4,5},{5,4},{6,7},{7,6},{8,9},{9,8},{10,11... | collective-permute-start | bytes 1572872 | tf_op jit(solution)/shard_map/ppermute | solution.py:618
  59.1 11.2 %collective-permute-start.7 = (bf16[512,512]{1,0:T(8,128)(2,1)S(1)}, bf16[512,512]{1,0:T(8,128)(2,1)S(1)}, u32[]{:S(2)}, u32[]{:S(2)}) collective-permute-start(bf16[512,512]{1,0:T(8,128)(2,1)S(1)} %bitcast.28), channel_id=1, source_target_pairs={{0,1},{1,0},{2,3},{3,2},{4,5},{5,4},{6,7},{7,6},{8,9},{9,8},{10,11... | collective-permute-start | bytes 1572872 | tf_op jit(solution)/shard_map/ppermute | solution.py:618
  59.6 10.7 %collective-permute-start.8 = (bf16[512,512]{1,0:T(8,128)(2,1)S(1)}, bf16[512,512]{1,0:T(8,128)(2,1)S(1)}, u32[]{:S(2)}, u32[]{:S(2)}) collective-permute-start(bf16[512,512]{1,0:T(8,128)(2,1)S(1)} %collective-permute-done.3.refs_11_.refs_10_), channel_id=1, source_target_pairs={{0,1},{1,0},{2,3},{3,2},{4,5},{5,4},{6,7},{7,6},{8,9},{9,8},{10,11... | collective-permute-start | bytes 1572872 | tf_op jit(solution)/shard_map/ppermute | solution.py:618
  69.5 2.0 collective-permute-start.15
  69.7 14.4 %collective-permute-start.13 = (bf16[256,1024]{1,0:T(8,128)(2,1)S(1)}, bf16[256,1024]{1,0:T(8,128)(2,1)S(1)}, u32[]{:S(2)}, u32[]{:S(2)}) collective-permute-start(bf16[256,1024]{1,0:T(8,128)(2,1)S(1)} %pair_sum.5.refs_0_), channel_id=1, source_target_pairs={{0,2},{1,3},{2,0},{3,1},{4,6},{5,7},{6,4},{7,5},{8,10},{9,11},{10,... | collective-permute-start | bytes 1572872 | tf_op jit(solution)/shard_map/ppermute | solution.py:618
  95.2 16.4 %copy-start.5 = (f32[256,1024]{1,0:T(8,128)}, f32[256,1024]{1,0:T(8,128)S(1)}, u32[]{:S(2)}) copy-start(f32[256,1024]{1,0:T(8,128)S(1)} %get-tuple-element.163) | copy-start | bytes 3145732
  95.2 2.0 collective-permute-start.17
  95.3 2.6 %collective-permute-start.16 = (bf16[256,1024]{1,0:T(8,128)(2,1)S(1)}, bf16[256,1024]{1,0:T(8,128)(2,1)S(1)}, u32[]{:S(2)}, u32[]{:S(2)}) collective-permute-start(bf16[256,1024]{1,0:T(8,128)(2,1)S(1)} %far_sum.5.refs_13_.refs_7_), channel_id=1, source_target_pairs={{0,1},{1,0},{2,3},{3,2},{4,5},{5,4},{6,7},{7,6},{8,9},{9,8},{10,11... | collective-permute-start | bytes 1572872 | tf_op jit(solution)/shard_map/ppermute | solution.py:618
  95.8 15.1 %collective-permute-start.19 = (bf16[256,1024]{1,0:T(8,128)(2,1)S(1)}, bf16[256,1024]{1,0:T(8,128)(2,1)S(1)}, u32[]{:S(2)}, u32[]{:S(2)}) collective-permute-start(bf16[256,1024]{1,0:T(8,128)(2,1)S(1)} %get-tuple-element.164), channel_id=1, source_target_pairs={{0,1},{1,0},{2,3},{3,2},{4,5},{5,4},{6,7},{7,6},{8,9},{9,8},{10,11... | collective-permute-start | bytes 1572872 | tf_op jit(solution)/shard_map/ppermute | solution.py:618
  97.3 18.8 %collective-permute-start.18 = (bf16[256,1024]{1,0:T(8,128)(2,1)S(1)}, bf16[256,1024]{1,0:T(8,128)(2,1)S(1)}, u32[]{:S(2)}, u32[]{:S(2)}) collective-permute-start(bf16[256,1024]{1,0:T(8,128)(2,1)S(1)} %pair_sum.6.refs_19_.refs_0_), channel_id=1, source_target_pairs={{0,2},{1,3},{2,0},{3,1},{4,6},{5,7},{6,4},{7,5},{8,10},{9,11},{10,... | collective-permute-start | bytes 1572872 | tf_op jit(solution)/shard_map/ppermute | solution.py:618
  110.8 16.5 %copy-start.33 = (bf16[256,1024]{1,0:T(8,128)(2,1)}, bf16[256,1024]{1,0:T(8,128)(2,1)S(1)}, u32[]{:S(2)}) copy-start(bf16[256,1024]{1,0:T(8,128)(2,1)S(1)} %collective-permute-done.19) | copy-start | bytes 1572868
  111.7 15.7 %collective-permute-start.21 = (bf16[256,512]{1,0:T(8,128)(2,1)S(1)}, bf16[256,512]{1,0:T(8,128)(2,1)S(1)}, u32[]{:S(2)}, u32[]{:S(2)}) collective-permute-start(bf16[256,512]{1,0:T(8,128)(2,1)S(1)} %add_convert_fusion.3.refs_15_), channel_id=1, source_target_pairs={{0,2},{1,3},{2,0},{3,1},{4,6},{5,7},{6,4},{7,5},{8,10},{9,11},{10,... | collective-permute-start | bytes 786440 | tf_op jit(solution)/shard_map/ppermute | solution.py:618
  113.2 14.2 %collective-permute-start.20 = (bf16[1,192,512]{2,1,0:T(8,128)(2,1)S(1)}, bf16[1,192,512]{2,1,0:T(8,128)(2,1)S(1)}, u32[]{:S(2)}, u32[]{:S(2)}) collective-permute-start(bf16[1,192,512]{2,1,0:T(8,128)(2,1)S(1)} %bitcast.33), channel_id=1, source_target_pairs={{0,16},{4,20},{8,24},{12,28},{16,0},{20,4},{24,8},{28,12},{1,17},{... | collective-permute-start | bytes 589832 | tf_op jit(solution)/shard_map/ppermute | solution.py:618
  127.4 16.4 %copy-start.37 = (bf16[256,512]{1,0:T(8,128)(2,1)}, bf16[256,512]{1,0:T(8,128)(2,1)S(1)}, u32[]{:S(2)}) copy-start(bf16[256,512]{1,0:T(8,128)(2,1)S(1)} %collective-permute-done.21) | copy-start | bytes 786436
  127.4 2.1 collective-permute-start.22
  129.6 16.1 %collective-permute-start.23 = (bf16[304,1024]{1,0:T(8,128)(2,1)S(1)}, bf16[304,1024]{1,0:T(8,128)(2,1)S(1)}, u32[]{:S(2)}, u32[]{:S(2)}) collective-permute-start(bf16[304,1024]{1,0:T(8,128)(2,1)S(1)} %pair_sum.7.refs_35_.refs_0_), channel_id=1, source_target_pairs={{0,2},{1,3},{2,0},{3,1},{4,6},{5,7},{6,4},{7,5},{8,10},{9,11},{10,... | collective-permute-start | bytes 1867784 | tf_op jit(solution)/shard_map/ppermute | solution.py:618
  130.2 3.1 %collective-permute-start.24 = (bf16[256,1024]{1,0:T(8,128)(2,1)S(1)}, bf16[256,1024]{1,0:T(8,128)(2,1)S(1)}, u32[]{:S(2)}, u32[]{:S(2)}) collective-permute-start(bf16[256,1024]{1,0:T(8,128)(2,1)S(1)} %far_sum.6.refs_14_.refs_13_), channel_id=1, source_target_pairs={{0,1},{1,0},{2,3},{3,2},{4,5},{5,4},{6,7},{7,6},{8,9},{9,8},{10,11... | collective-permute-start | bytes 1572872 | tf_op jit(solution)/shard_map/ppermute | solution.py:618
  130.3 13.5 %collective-permute-start.26 = (bf16[2,192,512]{2,1,0:T(8,128)(2,1)S(1)}, bf16[2,192,512]{2,1,0:T(8,128)(2,1)S(1)}, u32[]{:S(2)}, u32[]{:S(2)}) collective-permute-start(bf16[2,192,512]{2,1,0:T(8,128)(2,1)S(1)} %pad_maximum_fusion.1.refs_0_), channel_id=1, source_target_pairs={{0,8},{4,12},{8,0},{12,4},{16,24},{20,28},{24,16},{28,20},{1,9},{5... | collective-permute-start | bytes 1179656 | tf_op jit(solution)/shard_map/ppermute | solution.py:618
  131.9 11.9 %collective-permute-start.27 = (bf16[2,192,512]{2,1,0:T(8,128)(2,1)S(1)}, bf16[2,192,512]{2,1,0:T(8,128)(2,1)S(1)}, u32[]{:S(2)}, u32[]{:S(2)}) collective-permute-start(bf16[2,192,512]{2,1,0:T(8,128)(2,1)S(1)} %pad_maximum_fusion.1.refs_0_), channel_id=1, source_target_pairs={{0,4},{4,0},{8,12},{12,8},{16,20},{20,16},{24,28},{28,24},{1,5},{5... | collective-permute-start | bytes 1179656 | tf_op jit(solution)/shard_map/ppermute | solution.py:618
  145.7 2.2 collective-permute-start.28
  145.7 2.9 %collective-permute-start.29 = (bf16[256,1024]{1,0:T(8,128)(2,1)S(1)}, bf16[256,1024]{1,0:T(8,128)(2,1)S(1)}, u32[]{:S(2)}, u32[]{:S(2)}) collective-permute-start(bf16[256,1024]{1,0:T(8,128)(2,1)S(1)} %get-tuple-element.191), channel_id=1, source_target_pairs={{0,1},{1,0},{2,3},{3,2},{4,5},{5,4},{6,7},{7,6},{8,9},{9,8},{10,11... | collective-permute-start | bytes 1572872 | tf_op jit(solution)/shard_map/ppermute | solution.py:618
  146.2 15.4 %collective-permute-start.31 = (bf16[2,192,512]{2,1,0:T(8,128)(2,1)S(1)}, bf16[2,192,512]{2,1,0:T(8,128)(2,1)S(1)}, u32[]{:S(2)}, u32[]{:S(2)}) collective-permute-start(bf16[2,192,512]{2,1,0:T(8,128)(2,1)S(1)} %collective-permute-done.26.refs_1_), channel_id=1, source_target_pairs={{0,4},{4,0},{8,12},{12,8},{16,20},{20,16},{24,28},{28,24},{1,5},{5... | collective-permute-start | bytes 1179656 | tf_op jit(solution)/shard_map/ppermute | solution.py:618
  147.9 4.2 %collective-permute-start.25 = (bf16[304,1024]{1,0:T(8,128)(2,1)S(1)}, bf16[304,1024]{1,0:T(8,128)(2,1)S(1)}, u32[]{:S(2)}, u32[]{:S(2)}) collective-permute-start(bf16[304,1024]{1,0:T(8,128)(2,1)S(1)} %far_sum.7.refs_13_), channel_id=1, source_target_pairs={{0,1},{1,0},{2,3},{3,2},{4,5},{5,4},{6,7},{7,6},{8,9},{9,8},{10,11... | collective-permute-start | bytes 1867784 | tf_op jit(solution)/shard_map/ppermute | solution.py:618
  148.0 15.8 %collective-permute-start.32 = (bf16[256,640]{1,0:T(8,128)(2,1)S(1)}, bf16[256,640]{1,0:T(8,128)(2,1)S(1)}, u32[]{:S(2)}, u32[]{:S(2)}) collective-permute-start(bf16[256,640]{1,0:T(8,128)(2,1)S(1)} %add_convert_fusion.1.refs_36_.refs_9_), channel_id=1, source_target_pairs={{0,2},{1,3},{2,0},{3,1},{4,6},{5,7},{6,4},{7,5},{8,10},{9,11},{10,... | collective-permute-start | bytes 983048 | tf_op jit(solution)/shard_map/ppermute | solution.py:618
  148.8 15.1 %collective-permute-start.33 = (bf16[256,512]{1,0:T(8,128)(2,1)S(1)}, bf16[256,512]{1,0:T(8,128)(2,1)S(1)}, u32[]{:S(2)}, u32[]{:S(2)}) collective-permute-start(bf16[256,512]{1,0:T(8,128)(2,1)S(1)} %add_convert_fusion.2.refs_37_), channel_id=1, source_target_pairs={{0,2},{1,3},{2,0},{3,1},{4,6},{5,7},{6,4},{7,5},{8,10},{9,11},{10,... | collective-permute-start | bytes 786440 | tf_op jit(solution)/shard_map/ppermute | solution.py:618
  150.3 11.3 %collective-permute-start.30 = (bf16[1,48,1024]{2,1,0:T(8,128)(2,1)S(1)}, bf16[1,48,1024]{2,1,0:T(8,128)(2,1)S(1)}, u32[]{:S(2)}, u32[]{:S(2)}) collective-permute-start(bf16[1,48,1024]{2,1,0:T(8,128)(2,1)S(1)} %slice_bitcast_fusion), channel_id=1, source_target_pairs={{0,16},{4,20},{8,24},{12,28},{16,0},{20,4},{24,8},{28,12},{1,17},{... | collective-permute-start | bytes 294920 | tf_op jit(solution)/shard_map/ppermute | solution.py:618
  163.8 2.9 %collective-permute-start.34 = (bf16[256,1152]{1,0:T(8,128)(2,1)S(1)}, bf16[256,1152]{1,0:T(8,128)(2,1)S(1)}, u32[]{:S(2)}, u32[]{:S(2)}) collective-permute-start(bf16[256,1152]{1,0:T(8,128)(2,1)S(1)} %get-tuple-element.196), channel_id=1, source_target_pairs={{0,1},{1,0},{2,3},{3,2},{4,5},{5,4},{6,7},{7,6},{8,9},{9,8},{10,11... | collective-permute-start | bytes 1769480 | tf_op jit(solution)/shard_map/ppermute | solution.py:618
  164.6 1.4 collective-permute-start.36
  166.1 5.0 %collective-permute-start.37 = (bf16[64,512]{1,0:T(8,128)(2,1)S(1)}, bf16[64,512]{1,0:T(8,128)(2,1)S(1)}, u32[]{:S(2)}, u32[]{:S(2)}) collective-permute-start(bf16[64,512]{1,0:T(8,128)(2,1)S(1)} %add_convert_fusion.5), channel_id=1, source_target_pairs={{0,2},{1,3},{2,0},{3,1},{4,6},{5,7},{6,4},{7,5},{8,10},{9,11},{10,... | collective-permute-start | bytes 196616 | tf_op jit(solution)/shard_map/ppermute | solution.py:618
  166.8 12.0 %collective-permute-start.35 = (bf16[256,640]{1,0:T(8,128)(2,1)S(1)}, bf16[256,640]{1,0:T(8,128)(2,1)S(1)}, u32[]{:S(2)}, u32[]{:S(2)}) collective-permute-start(bf16[256,640]{1,0:T(8,128)(2,1)S(1)} %add_convert_fusion.refs_4_), channel_id=1, source_target_pairs={{0,2},{1,3},{2,0},{3,1},{4,6},{5,7},{6,4},{7,5},{8,10},{9,11},{10,... | collective-permute-start | bytes 983048 | tf_op jit(solution)/shard_map/ppermute | solution.py:618
  168.3 20.9 %collective-permute-start.46 = (bf16[2,48,1024]{2,1,0:T(8,128)(2,1)}, bf16[2,48,1024]{2,1,0:T(8,128)(2,1)}, u32[]{:S(2)}, u32[]{:S(2)}) collective-permute-start(bf16[2,48,1024]{2,1,0:T(8,128)(2,1)} %pad_maximum_fusion.3), channel_id=1, source_target_pairs={{0,8},{4,12},{8,0},{12,4},{16,24},{20,28},{24,16},{28,20},{1,9},{5... | collective-permute-start | bytes 589832 | tf_op jit(solution)/shard_map/ppermute | solution.py:618
  171.1 7.7 %collective-permute-start.38 = (bf16[1,112,512]{2,1,0:T(8,128)(2,1)S(1)}, bf16[1,112,512]{2,1,0:T(8,128)(2,1)S(1)}, u32[]{:S(2)}, u32[]{:S(2)}) collective-permute-start(bf16[1,112,512]{2,1,0:T(8,128)(2,1)S(1)} %maximum_bitcast_fusion), channel_id=1, source_target_pairs={{0,16},{4,20},{8,24},{12,28},{16,0},{20,4},{24,8},{28,12},{1,17},{... | collective-permute-start | bytes 344072 | tf_op jit(solution)/shard_map/ppermute | solution.py:618
  180.0 21.1 %all-to-all-start.1 = ((bf16[8,64,512]{2,1,0:T(8,128)(2,1)}), bf16[8,64,512]{2,1,0:T(8,128)(2,1)S(1)}, u32[]{:S(2)}, u32[]{:S(2)}) async-start(bf16[8,64,512]{2,1,0:T(8,128)(2,1)} %bitcast.13), calls=%async_computation.1 | async-start | bytes 1048576 | tf_op jit(solution)/shard_map/all_to_all | solution.py:827
  186.3 12.6 %collective-permute-start.39 = (bf16[2,112,512]{2,1,0:T(8,128)(2,1)S(1)}, bf16[2,112,512]{2,1,0:T(8,128)(2,1)S(1)}, u32[]{:S(2)}, u32[]{:S(2)}) collective-permute-start(bf16[2,112,512]{2,1,0:T(8,128)(2,1)S(1)} %pad_maximum_fusion.2.refs_12_), channel_id=1, source_target_pairs={{0,8},{4,12},{8,0},{12,4},{16,24},{20,28},{24,16},{28,20},{1,9},{5... | collective-permute-start | bytes 688136 | tf_op jit(solution)/shard_map/ppermute | solution.py:618
  190.1 26.1 %copy-start.7 = (bf16[4,48,1024]{2,1,0:T(8,128)(2,1)}, bf16[4,48,1024]{2,1,0:T(8,128)(2,1)S(1)}, u32[]{:S(2)}) copy-start(bf16[4,48,1024]{2,1,0:T(8,128)(2,1)S(1)} %constant_dynamic-update-slice_fusion.refs_4_) | copy-start | bytes 1179652
  190.1 26.2 %copy-start.25 = (s32[4]{0:T(128)S(1)}, s32[4]{0:T(128)}, u32[]{:S(2)}) copy-start(s32[4]{0:T(128)} %copy-done.23) | copy-start | bytes 52
  190.2 26.2 %copy-start.30 = (s32[8]{0:T(128)S(1)}, s32[8]{0:T(128)}, u32[]{:S(2)}) copy-start(s32[8]{0:T(128)} %copy-done.29) | copy-start | bytes 100
  190.2 14.5 %collective-permute-start.47 = (bf16[4,48,1024]{2,1,0:T(8,128)(2,1)S(1)}, bf16[4,48,1024]{2,1,0:T(8,128)(2,1)}, u32[]{:S(2)}, u32[]{:S(2)}) collective-permute-start(bf16[4,48,1024]{2,1,0:T(8,128)(2,1)S(1)} %constant_dynamic-update-slice_fusion.refs_4_), channel_id=1, source_target_pairs={{0,4},{4,0},{8,12},{12,8},{16,20},{20,16},{24,28},{28,24},{1,5},{5... | collective-permute-start | bytes 1179656 | tf_op jit(solution)/shard_map/ppermute | solution.py:618
  198.9 16.4 %collective-permute-start.40 = (bf16[4,112,512]{2,1,0:T(8,128)(2,1)S(1)}, bf16[4,112,512]{2,1,0:T(8,128)(2,1)S(1)}, u32[]{:S(2)}, u32[]{:S(2)}) collective-permute-start(bf16[4,112,512]{2,1,0:T(8,128)(2,1)S(1)} %pad_maximum_fusion.refs_0_), channel_id=1, source_target_pairs={{0,4},{4,0},{8,12},{12,8},{16,20},{20,16},{24,28},{28,24},{1,5},{5... | collective-permute-start | bytes 1376264 | tf_op jit(solution)/shard_map/ppermute | solution.py:618
  201.1 26.3 %all-to-all-start.2 = ((bf16[8,64,512]{2,1,0:T(8,128)(2,1)}), bf16[8,64,512]{2,1,0:T(8,128)(2,1)S(1)}, u32[]{:S(2)}, u32[]{:S(2)}) async-start(bf16[8,64,512]{2,1,0:T(8,128)(2,1)} %bitcast.14), calls=%async_computation.2 | async-start | bytes 1048576 | tf_op jit(solution)/shard_map/all_to_all | solution.py:836
  204.6 21.4 %copy-start.28 = (s32[8]{0:T(128)S(1)}, s32[8]{0:T(128)}, u32[]{:S(2)}) copy-start(s32[8]{0:T(128)} %slots.4) | copy-start | bytes 100
  204.6 11.7 %collective-permute-start.48 = (bf16[4,48,1024]{2,1,0:T(8,128)(2,1)S(1)}, bf16[4,48,1024]{2,1,0:T(8,128)(2,1)S(1)}, u32[]{:S(2)}, u32[]{:S(2)}) collective-permute-start(bf16[4,48,1024]{2,1,0:T(8,128)(2,1)S(1)} %constant_dynamic-update-slice_fusion.refs_4_), channel_id=1, source_target_pairs={{0,1},{1,0},{2,3},{3,2},{4,5},{5,4},{6,7},{7,6},{8,9},{9,8},{10,11... | collective-permute-start | bytes 1179656 | tf_op jit(solution)/shard_map/ppermute | solution.py:618
  204.7 11.7 %collective-permute-start.49 = (bf16[4,48,1024]{2,1,0:T(8,128)(2,1)}, bf16[4,48,1024]{2,1,0:T(8,128)(2,1)S(1)}, u32[]{:S(2)}, u32[]{:S(2)}) collective-permute-start(bf16[4,48,1024]{2,1,0:T(8,128)(2,1)} %collective-permute-done.47.refs_5_), channel_id=1, source_target_pairs={{0,1},{1,0},{2,3},{3,2},{4,5},{5,4},{6,7},{7,6},{8,9},{9,8},{10,11... | collective-permute-start | bytes 1179656 | tf_op jit(solution)/shard_map/ppermute | solution.py:618
  205.2 10.6 %collective-permute-start.43 = (bf16[4,64,512]{2,1,0:T(8,128)(2,1)S(1)}, bf16[4,64,512]{2,1,0:T(8,128)(2,1)S(1)}, u32[]{:S(2)}, u32[]{:S(2)}) collective-permute-start(bf16[4,64,512]{2,1,0:T(8,128)(2,1)S(1)} %slice.107.refs_2_), channel_id=1, source_target_pairs={{0,2},{1,3},{2,0},{3,1},{4,6},{5,7},{6,4},{7,5},{8,10},{9,11},{10,... | collective-permute-start | bytes 786440 | tf_op jit(solution)/shard_map/ppermute | solution.py:618
  215.3 10.3 %collective-permute-start.44 = (bf16[4,64,512]{2,1,0:T(8,128)(2,1)S(1)}, bf16[4,64,512]{2,1,0:T(8,128)(2,1)}, u32[]{:S(2)}, u32[]{:S(2)}) collective-permute-start(bf16[4,64,512]{2,1,0:T(8,128)(2,1)S(1)} %slice.108.refs_3_), channel_id=1, source_target_pairs={{0,2},{1,3},{2,0},{3,1},{4,6},{5,7},{6,4},{7,5},{8,10},{9,11},{10,... | collective-permute-start | bytes 786440 | tf_op jit(solution)/shard_map/ppermute | solution.py:618
  215.8 13.1 %collective-permute-start.41 = (bf16[4,64,512]{2,1,0:T(8,128)(2,1)S(1)}, bf16[4,64,512]{2,1,0:T(8,128)(2,1)}, u32[]{:S(2)}, u32[]{:S(2)}) collective-permute-start(bf16[4,64,512]{2,1,0:T(8,128)(2,1)S(1)} %slice.107.refs_2_), channel_id=1, source_target_pairs={{0,1},{1,0},{2,3},{3,2},{4,5},{5,4},{6,7},{7,6},{8,9},{9,8},{10,11... | collective-permute-start | bytes 786440 | tf_op jit(solution)/shard_map/ppermute | solution.py:618
  215.8 13.1 %collective-permute-start.45 = (bf16[4,64,512]{2,1,0:T(8,128)(2,1)S(1)}, bf16[4,64,512]{2,1,0:T(8,128)(2,1)}, u32[]{:S(2)}, u32[]{:S(2)}) collective-permute-start(bf16[4,64,512]{2,1,0:T(8,128)(2,1)S(1)} %collective-permute-done.43.refs_6_), channel_id=1, source_target_pairs={{0,1},{1,0},{2,3},{3,2},{4,5},{5,4},{6,7},{7,6},{8,9},{9,8},{10,11... | collective-permute-start | bytes 786440 | tf_op jit(solution)/shard_map/ppermute | solution.py:618
  216.3 12.6 %collective-permute-start.42 = (bf16[4,64,512]{2,1,0:T(8,128)(2,1)S(1)}, bf16[4,64,512]{2,1,0:T(8,128)(2,1)}, u32[]{:S(2)}, u32[]{:S(2)}) collective-permute-start(bf16[4,64,512]{2,1,0:T(8,128)(2,1)S(1)} %slice.108.refs_3_), channel_id=1, source_target_pairs={{0,1},{1,0},{2,3},{3,2},{4,5},{5,4},{6,7},{7,6},{8,9},{9,8},{10,11... | collective-permute-start | bytes 786440 | tf_op jit(solution)/shard_map/ppermute | solution.py:618
  225.6 3.3 %collective-permute-start.50 = (bf16[4,64,512]{2,1,0:T(8,128)(2,1)}, bf16[4,64,512]{2,1,0:T(8,128)(2,1)S(1)}, u32[]{:S(2)}, u32[]{:S(2)}) collective-permute-start(bf16[4,64,512]{2,1,0:T(8,128)(2,1)} %collective-permute-done.44.refs_7_), channel_id=1, source_target_pairs={{0,1},{1,0},{2,3},{3,2},{4,5},{5,4},{6,7},{7,6},{8,9},{9,8},{10,11... | collective-permute-start | bytes 786440 | tf_op jit(solution)/shard_map/ppermute | solution.py:618
  (35 other events, 207.1 us)

commit v4 on v3

--- a/solution.py
+++ b/solution.py
@@ -111,7 +111,7 @@
 
 
 def project_kernel(chunk, info, wq_h, wkv_h, x0, x1, x2, x3, gains, a1, qb, kvb, cos_t, sin_t,
-                   h_out, t1t_out, qt_out, kn_out, vn_out, kt_out, vt_out, wq, wkv, sems):
+                   t1t_out, qt_out, kn_out, vn_out, kt_out, vt_out, h_out, wq, wkv, sems):
     copies = copies_of(((wkv_h, wkv), (wq_h, wq)), sems)
     me = info[0]
     rows = h_out.shape[0]
@@ -189,11 +189,26 @@
         put_block(r, nn(o, wo[:, at]) + nn(to, ob[:, at]), z_keep, z_send)
 
 
-def front_kernel(chunk, last, info, wgu, wd, x0, x1, x2, x3, zo, zp, g0, g1, g2, g3, gains, a2, bd, fb, da,
+def front_kernel(chunk, last, info, wgu_in, wd_in, x0, x1, x2, x3, zo, zp, g0, g1, g2, g3, gains, a2, bd, fb, da,
                  *rest):
+    units = wd_in.shape[0]
+    if chunk:
+        wgu, wd = wgu_in, wd_in
+    else:
+        (wgu, wd, f_s, sems), rest = rest[-4:], rest[:-4]
+        rest = (*rest, f_s)
+
+    def copies(i):
+        c = pl.ds(pl.multiple_of(i * QUARTER, QUARTER), QUARTER)
+        return (pltpu.make_async_copy(wgu_in.at[:, :, c], wgu.at[:, :, c], sems.at[0, i]),
+                pltpu.make_async_copy(wd_in.at[c, :], wd.at[c, :], sems.at[1, i]))
+
+    if not chunk:
+        for i in range(units // QUARTER):
+            for copy in copies(i):
+                copy.start()
     f_s = rest[-1]
     xm_out, xq_out, h_out, g_out, act_out, dg_out, du_out, t2_s, dtd_s, b_out = rest[-11:-1]
-    units = wd.shape[0]
     me, length = info[0], info[1]
     rows = h_out.shape[0]
     xs, gs = ([chunk_of(v, chunk, rows) for v in vs] for vs in ((x0, x1, x2, x3), (g0, g1, g2, g3)))
@@ -225,6 +240,9 @@
 
     def block(i, carry):
         c = pl.ds(pl.multiple_of(i * QUARTER, QUARTER), QUARTER)
+        if not chunk:
+            for copy in copies(i):
+                copy.wait()
         h, g = h_out[...], g_out[...]
         gate = nn(h, wgu[0, :, c]) + nn(t2_s[:, :RANK], fb[0, :, c])
         up = nn(h, wgu[1, :, c]) + nn(t2_s[:, RANK:], fb[1, :, c])
@@ -278,9 +296,9 @@
 
 
 def attend_back_kernel(chunk, last, info, wq_h, wkv_h, wo_h, x0, x1, x2, x3, g0, g1, g2, g3, xm, do_, dp, gains, a1,
-                       qb, kvb, oa, ob, cos_t, sin_t, h_in, t1t, qt, ot, lse, tot, *rest):
-    scratch, rest = rest[-13:], rest[:-13]
-    z_s, f_s, dot_s, dqt_s, dkt_s, dvt_s, dq_s, value_s, low_s, wq, wkv, wo, sems = scratch
+                       qb, kvb, oa, ob, cos_t, sin_t, t1t, qt, ot, lse, tot, *rest):
+    scratch, rest = rest[-14:], rest[:-14]
+    h_in, z_s, f_s, dot_s, dqt_s, dkt_s, dvt_s, dq_s, value_s, low_s, wq, wkv, wo, sems = scratch
     copies = copies_of(((wo_h, wo), (wq_h, wq), (wkv_h, wkv)), sems)
     n_out = 7 if last else 8
     outs, rest = rest[-n_out:], rest[:-n_out]
@@ -307,7 +325,8 @@
             inner = inner + jnp.sum(v * w, axis=1, keepdims=True)
             u = xs[r][at, :].astype(F32)
             first = first + jnp.sum(u * u, axis=1, keepdims=True)
-        inv_out[at, :] = lax.rsqrt(first / WIDTH + EPS)
+        inv_one = lax.rsqrt(first / WIDTH + EPS)
+        inv_out[at, :] = inv_one
         inv = lax.rsqrt(square / WIDTH + EPS)
         back = inv * inv * inv * inner / WIDTH
         for r in range(PARTS):
@@ -317,6 +336,8 @@
             if r == 0:
                 dxq_out[at, :] = d
             z_s[at, quarter(me, r)] = d.astype(BF16)
+            u = xs[r][at, :].astype(F32)
+            h_in[at, quarter(me, r)] = (u * inv_one * gains[r, 0:1, :].astype(F32)).astype(BF16)
         return carry
 
     lax.fori_loop(0, rows // ROW_BLOCK, norm_back, 0)
@@ -507,14 +528,6 @@
         copy.wait()
 
 
-def load_kernel(count, *refs):
-    made = [pltpu.make_async_copy(refs[i], refs[count + i], refs[-1].at[i]) for i in range(count)]
-    for copy in made:
-        copy.start()
-    for copy in made:
-        copy.wait()
-
-
 def adapter_kernel(count, info, *refs):
     made = [pltpu.make_async_copy(refs[i].at[info[2]], refs[count + i], refs[-1].at[i]) for i in range(count)]
     for copy in made:
@@ -523,27 +536,18 @@
         copy.wait()
 
 
-def load(arrays, name, info=None, after=()):
+def load_adapters(arrays, info):
     count = len(arrays)
-    scalars = () if info is None else (info,)
-    kernel = load_kernel if info is None else adapter_kernel
-    shapes = [a.shape if info is None else a.shape[1:] for a in arrays]
-
-    def body(*refs):
-        at = len(scalars) + count
-        kernel(count, *refs[:at], *refs[at + len(after):])
-
     return pl.pallas_call(
-        body,
-        in_specs=[pl.BlockSpec(memory_space=pltpu.SMEM)] * len(scalars) + [pl.BlockSpec(memory_space=pltpu.HBM)] * count
-        + [pl.BlockSpec(memory_space=pl.ANY)] * len(after),
+        functools.partial(adapter_kernel, count),
+        in_specs=[pl.BlockSpec(memory_space=pltpu.SMEM)] + [pl.BlockSpec(memory_space=pltpu.HBM)] * count,
         out_specs=[pl.BlockSpec(memory_space=pltpu.VMEM)] * count,
-        out_shape=[pltpu.VMEM(tuple(s), a.dtype) for s, a in zip(shapes, arrays)],
+        out_shape=[pltpu.VMEM(a.shape[1:], a.dtype) for a in arrays],
         scratch_shapes=[pltpu.SemaphoreType.DMA((count,))],
         compiler_params=pltpu.CompilerParams(vmem_limit_bytes=MIB),
         cost_estimate=pl.CostEstimate(flops=1000, transcendentals=0, bytes_accessed=1000),
-        name=name,
-    )(*scalars, *(in_hbm(a) for a in arrays), *after)
+        name="adapters",
+    )(info, *(in_hbm(a) for a in arrays))
 
 
 def move_rows(kernel, value, slots, name, here):
@@ -594,6 +598,11 @@
     )(*scalars, *(in_hbm(a) for a in weights), *(in_vmem(a) for a in args), *after)
 
 
+def whole_spec(value):
+    zeros = (0,) * value.ndim
+    return pl.BlockSpec(value.shape, lambda i, *_: zeros)
+
+
 def sum_call(kernel, scalars, groups, outs, name):
     args = [v for group in groups for v in group]
     steps = 2
@@ -603,15 +612,15 @@
         functools.partial(kernel, [len(group) for group in groups]),
         grid_spec=pltpu.PrefetchScalarGridSpec(
             num_scalar_prefetch=len(scalars), grid=(steps,),
-            in_specs=[pl.BlockSpec(memory_space=pltpu.VMEM)] * len(args), out_specs=specs),
+            in_specs=[whole_spec(a) for a in args], out_specs=specs),
         out_shape=outs,
         compiler_params=pltpu.CompilerParams(
             dimension_semantics=("arbitrary",),
-            vmem_limit_bytes=4 * MIB + sum(a.size * a.dtype.itemsize for a in args)
+            vmem_limit_bytes=4 * MIB + 2 * sum(a.size * a.dtype.itemsize for a in args)
             + sum(o.size * o.dtype.itemsize for o in outs)),
         cost_estimate=pl.CostEstimate(flops=0, transcendentals=0, bytes_accessed=12000000),
         name=name,
-    )(*scalars, *(in_vmem(a) for a in args))
+    )(*scalars, *args)
 
 
 def swap(value, bit, axis, size):
@@ -700,10 +709,10 @@
     dealt = lax.all_to_all(
         move_rows(deal_kernel, residual, dealing_slots, "deal", True), "dp", split_axis=0, concat_axis=1, tiled=True
     )[0]
-    adapters_here = load(
+    adapters_here = load_adapters(
         (attention_adapter_input, query_adapter_output, key_value_adapter_output, output_adapter_input,
          output_adapter_output, feedfwd_adapter_input, feedfwd_adapter_output, down_adapter_input,
-         down_adapter_output), "adapters", info)
+         down_adapter_output), info)
     a1, qb, kvb, oa, ob, a2, fba, da, bd = adapters_here
     dealt = late(dealt, gs[2], a1, gains)
     beside = near(dealt)
@@ -712,44 +721,40 @@
     cos_np, sin_np = rope_tables(length)
     cos = [jnp.asarray(cos_np[:, c * rows:(c + 1) * rows]) for c in range(CHUNKS)]
     sin = [jnp.asarray(sin_np[:, c * rows:(c + 1) * rows]) for c in range(CHUNKS)]
-    wq, wkv, wo, wgu, wd = query_matrix, key_value_matrix, output_matrix, gate_up_matrix, down_matrix
+    wq, wkv, wo = query_matrix, key_value_matrix, output_matrix
 
     def like(*arrays):
         return [(a.shape, a.dtype) for a in arrays]
 
     wide, col, block, thin = (rows, WIDTH), (rows, half), (rows, QUARTER), (rows, 1)
-    saved = [None] * CHUNKS
+    saved, kept, z_own, z_far = ([None] * CHUNKS for _ in range(4))
     order = ()
     for c in range(CHUNKS):
-        xs[c] = (dealt, beside, there[c], near(late(there[c], *order)))
-        outs = [(wide, BF16), ((3 * RANK, rows), BF16), ((q_cols, rows), BF16), ((kv_heads, rows, HEAD), BF16),
+        xs[c] = (dealt, beside, there[c], near(late(there[c], saved[0][0]) if c else there[c]))
+        outs = [((3 * RANK, rows), BF16), ((q_cols, rows), BF16), ((kv_heads, rows, HEAD), BF16),
                 ((kv_heads, rows, HEAD), BF16), ((kv_cols, rows), BF16), ((kv_cols, rows), BF16)]
         saved[c] = call(
             functools.partial(project_kernel, c), info, (wq, wkv), (*xs[c], gains, a1, qb, kvb, cos[c], sin[c]), outs,
-            like(wq, wkv), "project_%d" % c, 12, order, (2,))
-        order = (saved[c][1],)
-
-    kept, z_own = [None] * CHUNKS, [None] * CHUNKS
-    for c in reversed(range(CHUNKS)):
+            [(wide, BF16)] + like(wq, wkv), "project_%d" % c, 12, order, (2,))
         outs = [(col, F32), (col, BF16), ((q_cols, rows), BF16), ((heads, rows), F32), ((RANK, rows), BF16)]
-        pairs = [v for p in saved[:c + 1] for v in (p[3], p[6])]
+        pairs = [v for p in saved[:c + 1] for v in (p[2], p[5])]
         z_keep, z_send, *kept[c] = call(
-            functools.partial(attend_kernel, c), info, (wo,), (saved[c][2], oa, ob, *pairs), outs, like(wo),
-            "attend_%d" % c, 10, order, (1,))
-        z_own[c] = pair_sum(z_keep, z_send)
-        order = (kept[c][1], z_own[1])
-    z_far = [far(v) for v in z_own]
-    wgu, wd = load((wgu, wd), "load", None, order)
-
+            functools.partial(attend_kernel, c), info, (wo,), (saved[c][1], oa, ob, *pairs), outs, like(wo),
+            "attend_%d" % c, 10, (saved[c][0], there[-1]), (1,))
+        z_own[c] = pair_sum(z_keep, late(z_send, z_far[0]) if c else z_send)
+        z_far[c] = far(z_own[c])
+        order = (kept[c][1], z_own[c])
     def front(c, total, partial, order):
         hidden = (rows, units)
         outs = [(wide, BF16), (block, F32), (wide, BF16), (wide, BF16), (hidden, BF16), (hidden, BF16), (hidden, BF16),
                 ((rows, 2 * RANK), BF16), ((rows, RANK), BF16),
-                ((3 * RANK * units // QUARTER, QUARTER), F32 if c else BF16)]
+                ((3 * RANK * units // QUARTER, QUARTER), BF16 if c else F32)]
+        args = (*xs[c], total, near(total), *gs, gains, a2, bd, fba, da, *partial)
+        weights = () if c else (gate_up_matrix, down_matrix)
+        outs += like(*weights)
         return call(
-            functools.partial(front_kernel, c, c == 0), info, (),
-            (wgu, wd, *xs[c], total, near(total), *gs, gains, a2, bd, fba, da, *partial), outs,
-            [((ROW_BLOCK, WIDTH), F32)], "front_%d" % c, 8, order)
+            functools.partial(front_kernel, c, c == CHUNKS - 1), info, weights, (wgu, wd, *args) if c else args, outs,
+            [((ROW_BLOCK, WIDTH), F32)], "front_%d" % c, 8, order, () if c else (2, units // QUARTER))
 
     def back(c, hidden, partial, order):
         first = col if c else (rows + 3 * RANK, half)
@@ -764,61 +769,52 @@
         outs = [(block, F32), (padded, F32), (padded, BF16), (thin, F32), ((3 * RANK, QUARTER), F32 if c else BF16)]
         outs += ([((4 * RANK, WIDTH), F32), ((kv_cols, rows), F32), ((kv_cols, rows), F32)] if c
                  else [((4 * RANK, half), F32), ((4 * RANK, half), BF16)])
-        scratch = [(wide, BF16), ((ROW_BLOCK, WIDTH), F32), ((q_cols, rows), BF16), ((q_cols, rows), F32),
+        scratch = [(wide, BF16), (wide, BF16), ((ROW_BLOCK, WIDTH), F32), ((q_cols, rows), BF16), ((q_cols, rows), F32),
                    ((c + 1, kv_cols, rows), F32), ((c + 1, kv_cols, rows), F32), ((rows, q_cols + 2 * kv_cols), BF16),
                    (block, F32), ((4 * RANK, QUARTER), F32)]
-        triples = [v for p in saved[:c + 1] for v in (p[3], p[4], p[5])]
+        triples = [v for p in saved[:c + 1] for v in (p[2], p[3], p[4])]
         return call(
             functools.partial(attend_back_kernel, c, c == 0), info, (wq, wkv, wo),
-            (*xs[c], *gs, hidden[c][0], total, near(total), gains, a1, qb, kvb, oa, ob, cos[c], sin[c], *saved[c][:3],
+            (*xs[c], *gs, hidden[c][0], total, near(total), gains, a1, qb, kvb, oa, ob, cos[c], sin[c], *saved[c][:2],
              *kept[c], *triples, *partial), outs, scratch + like(wq, wkv, wo), "attend_back_%d" % c, 18, order, (3,))
 
     bits = [1 << b for b in reversed(range(dp.bit_length() - 1))]
-    hidden, d_own, d_far = ([None] * CHUNKS for _ in range(3))
-    hidden[1] = front(1, far_sum(z_own[1], late(z_far[1], wd)), (), order)
-    step = hidden[1][8]
-    total = far_sum(z_own[0], late(z_far[0], step))
-    d_keep, d_send, y_keep_1, y_send_1, fa = back(1, hidden[1], (), (step, total))
-    d_own[1] = pair_sum(d_keep, d_send)
+    hidden, d_own, d_far, y_keep, y_send = ([None] * CHUNKS for _ in range(5))
+    *hidden[0], wgu, wd = front(0, far_sum(z_own[0], z_far[0]), (), order)
+    step = hidden[0][8]
+    hidden[1] = front(1, far_sum(z_own[1], late(z_far[1], step)), hidden[0][9:], (step,))
+    fb = hidden[1][9][None]
+    fb_first = swap(fb, bits[0], "dp", dp)
+    d_keep, d_send, y_keep[1], y_send[1], fa = back(1, hidden[1], (), (hidden[1][8],))
+    d_own[1] = pair_sum(d_keep, late(d_send, fb_first))
     d_far[1] = far(d_own[1])
-    hidden[0] = front(0, total, hidden[1][9:], (d_own[1],))
-    step = hidden[0][8]
-    total = far_sum(d_own[1], late(d_far[1], step))
-    fb = hidden[0][9][None]
-    fb_first = swap(fb, bits[0], "dp", dp)
-    y_keep, y_got = [None, y_keep_1], [None, near(y_send_1)]
-
-    def y_high(c, *others):
-        return (y_keep[c][:, QUARTER:] + late(y_got[c], *others)[:, QUARTER:].astype(F32)).astype(BF16)
-
-    high = y_high(1, step)
-    y_far = [None, far(high)]
-    d_keep, d_send, y_keep[0], y_send_0 = back(0, hidden[0], (fa,), (step, total, high))
-    d_own[0] = pair_sum(d_keep, late(d_send, fb_first, y_far[1]))
-    d_far[0] = far(d_own[0])
     fb = fb_more = jnp.concatenate([fb, fb_first], axis=0)
     for bit in bits[1:-1]:
         fb_more = doubled(fb_more, bit, dp)
     fb_more = fb_more[2:]
     fb_side = swap(fb, bits[-1], "dp", dp)
-    y_got[0] = near(y_send_0)
+    d_keep, d_send, y_keep[0], y_send[0] = back(0, hidden[0], (fa,), (d_own[1],))
+    total = far_sum(d_own[1], late(d_far[1], d_send))
+    d_own[0] = pair_sum(d_keep, late(d_send, fb_more, fb_side))
+    d_far[0] = far(d_own[0])
+    fb_more_side = swap(fb_more, bits[-1], "dp", dp)
     dxq, h_keep, h_send, inv, *sums = attend_back(1, total, (), (d_own[0],))
     total = far_sum(d_own[0], late(d_far[0], inv))
-    h_low, h_high = chip_sum(h_keep, late(h_send, fb_more, fb_side, d_far[0]))
+    h_low, h_high = chip_sum(h_keep, late(h_send, fb_more_side))
     h_far = far(h_high)
     final = [None, (dxq, h_low, h_high, h_far, inv)]
-    high = y_high(0, h_high)
-    y_far[0] = far(high)
+    y_got = [near(late(v, inv)) for v in y_send]
     fa = total[rows:][None]
     fa_first = swap(fa, bits[0], "dp", dp)
-    fb_more_side = swap(fb_more, bits[-1], "dp", dp)
-    dxq, h_keep, h_send, inv, att_b, aa_keep, aa_send = attend_back(0, total, sums, (h_high, high))
-    ready = (fa_first, fb_more_side, h_far, y_far[0])
+    dxq, h_keep, h_send, inv, att_b, aa_keep, aa_send = attend_back(0, total, sums, (h_high, *y_got))
+    ready = (fa_first, h_far)
     aa_low, aa_high = chip_sum(aa_keep, late(aa_send, *ready))
     aa_far = far(aa_high)
     h_low, h_high = chip_sum(h_keep, late(h_send, *ready))
     h_far = far(h_high)
     final[0] = (dxq, h_low, h_high, h_far, inv)
+    y_sums = [k + late(g, h_high).astype(F32) for k, g in zip(y_keep, y_got)]
+    y_far = far(jnp.concatenate([v[:, QUARTER:] for v in y_sums], axis=0).astype(BF16))
     att = jnp.concatenate([att_b, (aa_low + late(aa_far, h_high).astype(F32)).astype(BF16)], axis=0)[None]
     att = doubled(att, bits[0], dp)
 
@@ -829,20 +825,13 @@
     input_grad = move_rows(collect_kernel, back_grad, dealing_slots, "collect_grad", False)
 
     valid = (jnp.arange(length, dtype=jnp.int32) < my_length)[:, None]
-    result = jnp.concatenate(
-        [hidden[c][1] + y_keep[c][:, :QUARTER] + late(y_got[c], h_high)[:, :QUARTER].astype(F32) + y_far[c].astype(F32)
-         for c in range(CHUNKS)], axis=0)
-    result = late(jnp.where(valid, result, 0.0).astype(BF16), dinput)
+    result = jnp.concatenate([h[1] + v[:, :QUARTER] for h, v in zip(hidden, y_sums)], axis=0)
+    result = result + late(y_far, dinput).astype(F32)
+    result = jnp.where(valid, result, 0.0).astype(BF16)
     back_out = lax.all_to_all(
         result.reshape(dp, length // dp, QUARTER), "dp", split_axis=0, concat_axis=0, tiled=True)
     output = move_rows(collect_kernel, back_out, late(dealing_slots, input_grad), "collect_out", False)
 
-    n_b = att_b.shape[0]
-    for bit in bits[1:-1]:
-        att = doubled(att, bit, dp)
-    att_side = swap(att, bits[-1], "dp", dp)
-    a_parts = [att[:, n_b:], att_side[:, n_b:]]
-    a_far = [far(v) for v in a_parts]
     fa = late(jnp.concatenate([fa, fa_first], axis=0), h_high)
     for bit in bits[1:-1]:
         fa = doubled(fa, bit, dp)
@@ -853,12 +842,19 @@
         feedforward_sum_kernel, (info, owners),
         ((fb, fb_more, fb_side, fb_more_side), (fa, fa_side), (near(fa), near(fa_side))), outs, "feedforward_sum")
 
+    n_b = att_b.shape[0]
+    for bit in bits[1:-1]:
+        att = doubled(att, bit, dp)
+    att_side = swap(att, bits[-1], "dp", dp)
+    att_side = late(att_side, g_down_a, input_grad)
+    a_parts = [att[:, n_b:], att_side[:, n_b:]]
+    a_far = [far(v) for v in a_parts]
     outs = [sds((adapters, 3 * RANK, WIDTH), F32), sds((adapters, RANK, WIDTH), F32),
             sds((adapters, RANK, q_cols), F32), sds((adapters, 2, RANK, kv_cols), F32),
             sds((adapters, RANK, q_cols), F32)]
     ga_att, g_out_b, g_query_b, g_kv_b, g_out_a = sum_call(
         attention_sum_kernel, (info, owners),
-        ((att, att_side), a_parts, [near(v) for v in a_parts], a_far, (near(a_far[0]), near(late(a_far[1], g_down_a)))), outs, "attention_sum")
+        ((att, att_side), a_parts, [near(v) for v in a_parts], a_far, [near(v) for v in a_far]), outs, "attention_sum")
     return (output, input_grad, ga_att, g_query_b, g_kv_b, g_out_a, g_out_b, ga_ffn, g_ffn_b, g_down_a, g_down_b)
 
 

time: 235 us -> 228 us (0.970)
  Pallas kernels: 108 us -> 101 us
    pallas_call x2 -> x1, Pallas kernels: 9.97 us -> 1.8 us  [load_adapters(): pl.pallas_call(functools.partial(adapter_kernel, count), in_specs=[pl.Blo...]
    unnamed x91 -> x83, local copies, waits for them, and re-layouts: 9.8 us -> 7.97 us
    ppermute x51 -> x50, starting transfers between devices: 31.6 us -> 31.3 us  [swap(): return lax.ppermute(value, axis, [(i, i ^ bit) for i in range(size)])]
    ppermute x51 -> x50, waiting for transfers between devices: 58.8 us -> 58.7 us  [swap(): return lax.ppermute(value, axis, [(i, i ^ bit) for i in range(size)])]
  transfers between devices with their start and end apart: 54 -> 53, of which waited for: 19 -> 22; matrix products, arithmetic and copies ran while one was open for 5% -> 5% of each run, Pallas kernels for 35% -> 35%
where the time goes in v4:
time: 228 us; the launch traced here: 227 us
  Pallas kernels  101 us (44%)
  waiting for transfers between devices  58.7 us (26%)
  starting transfers between devices  47 us (21%)
  local copies, waits for them, and re-layouts  10.7 us (5%)
  other arithmetic  8.22 us (4%)
    pallas_call x19, Pallas kernels, call(): pl.pallas_call(body, in_specs=[pl.BlockSpec(memory_space=pltpu.SMEM)] * n...  84.7 us
    ppermute x50, waiting for transfers between devices, swap(): return lax.ppermute(value, axis, [(i, i ^ bit) for i in range(size)])  58.7 us
    ppermute x50, starting transfers between devices, swap(): return lax.ppermute(value, axis, [(i, i ^ bit) for i in range(size)])  31.3 us
    pallas_call x2, Pallas kernels, sum_call(): pl.pallas_call(functools.partial(kernel, [len(group) for group in groups]...  9.67 us
    unnamed x83, local copies, waits for them, and re-layouts  7.97 us
    all_to_all x1, starting transfers between devices, shards(): lax.all_to_all(move_rows(deal_kernel, residual, dealing_slots, 'deal', Tr...  7.26 us
    pallas_call x3, Pallas kernels, move_rows(): pl.pallas_call(kernel, in_specs=[pl.BlockSpec(memory_space=pltpu.SMEM), p...  5.25 us
  transfers between devices with their start and end apart: 53, of which 22 were waited for; matrix products, arithmetic and copies ran while one was open for 5% of the time, Pallas kernels for 35%

profile of v4, /device:TPU:0, one launch (start us, length us, event | category | flops | bytes accessed | tf_op | source)
XLA Modules:
  0.0 227.4 jit_solution(9556085394528276650)
XLA Ops:
  1.4 2.5 %deal.1 = bf16[8,64,512]{2,1,0:T(8,128)(2,1)} custom-call(s32[8]{0:T(128)S(1)} %copy-done.26, bf16[8,64,512]{2,1,0:T(8,128)(2,1)} %source.1), custom_call_target="tpu_custom_call" | custom-call | flops 1000 | bytes 1000 | tf_op jit(solution)/shard_map/deal/pallas_call | solution.py:555
  3.9 7.3 %all-to-all-start = ((bf16[8,64,512]{2,1,0:T(8,128)(2,1)}), bf16[8,64,512]{2,1,0:T(8,128)(2,1)S(1)}, u32[]{:S(2)}, u32[]{:S(2)}) async-start(bf16[8,64,512]{2,1,0:T(8,128)(2,1)} %deal.1), calls=%async_computation | async-start | bytes 1048576 | tf_op jit(solution)/shard_map/all_to_all | solution.py:709
  11.3 1.6 collective-permute-start.1
  15.5 1.4 pad_add_fusion.info.refs_0_
  16.9 1.8 adapters.1
  18.7 8.1 %collective-permute-done.3.refs_11_.refs_10_ = bf16[512,512]{1,0:T(8,128)(2,1)S(1)} collective-permute-done((bf16[512,512]{1,0:T(8,128)(2,1)S(1)}, bf16[512,512]{1,0:T(8,128)(2,1)S(1)}, u32[]{:S(2)}, u32[]{:S(2)}) %collective-permute-start.3) | collective-permute-done | bytes 524320 | tf_op jit(solution)/shard_map/ppermute | solution.py:627
  27.5 7.0 %collective-permute-done.5.refs_5_.refs_6_ = bf16[256,512]{1,0:T(8,128)(2,1)S(1)} collective-permute-done((bf16[256,512]{1,0:T(8,128)(2,1)S(1)}, bf16[256,512]{1,0:T(8,128)(2,1)S(1)}, u32[]{:S(2)}, u32[]{:S(2)}) %collective-permute-start.5) | collective-permute-done | bytes 262176 | tf_op jit(solution)/shard_map/ppermute | solution.py:627
  35.1 1.0 collective-permute-done.6.refs_6_.refs_7_
  36.1 4.1 %project_0.1 = (bf16[48,256]{1,0:T(8,128)(2,1)S(1)}, bf16[512,256]{1,0:T(8,128)(2,1)S(1)}, bf16[2,256,64]{2,1,0:T(8,128)(2,1)S(1)}, bf16[2,256,64]{2,1,0:T(8,128...) custom-call(s32[4]{0:T(128)S(1)} %pad_add_fusion.info.refs_0_, bf16[2048,512]{1,0:T(8,128)(2,1)} %refs_1_.15, ...), custom_call_target="tpu_custom_call" | custom-call | flops 1000 | bytes 1000 | tf_op jit(solution)/shard_map/project_0/pallas_call | solution.py:588
  40.1 3.1 %collective-permute-done.9.refs_8_.refs_5_.refs_10_.refs_6_ = bf16[256,512]{1,0:T(8,128)(2,1)S(1)} collective-permute-done((bf16[256,512]{1,0:T(8,128)(2,1)S(1)}, bf16[256,512]{1,0:T(8,128)(2,1)S(1)}, u32[]{:S(2)}, u32[]{:S(2)}) %collective-permute-start.9) | collective-permute-done | bytes 262176 | tf_op jit(solution)/shard_map/ppermute | solution.py:627
  43.2 3.1 %attend_0.1 = (f32[256,1024]{1,0:T(8,128)S(1)}, bf16[256,1024]{1,0:T(8,128)(2,1)S(1)}, bf16[512,256]{1,0:T(8,128)(2,1)S(1)}, f32[8,256]{1,0:T(8,128)S(1)}, bf16[16,256]{1,0:T(8,128)(2,1)S(1)}) custom-call(s32[4]{0:T(128)S(1)} %pad_add_fusion.info.refs_0_, bf16[512,2048]{1,0:T(8,128)(2,1)} %refs_3_.5, ...), custom_call_target="tpu_custom_call" | custom-call | flops 1000 | bytes 1000 | tf_op jit(solution)/shard_map/attend_0/pallas_call | solution.py:588
  46.4 1.9 collective-permute-done.10.refs_1_
  49.1 1.5 collective-permute-done.13.refs_6_.refs_7_
  50.6 4.1 %project_1.1 = (bf16[48,256]{1,0:T(8,128)(2,1)S(1)}, bf16[512,256]{1,0:T(8,128)(2,1)S(1)}, bf16[2,256,64]{2,1,0:T(8,128)(2,1)S(1)}, bf16[2,256,64]{2,1,0:T(8,128...) custom-call(s32[4]{0:T(128)S(1)} %pad_add_fusion.info.refs_0_, bf16[2048,512]{1,0:T(8,128)(2,1)} %refs_1_.15, ...), custom_call_target="tpu_custom_call" | custom-call | flops 1000 | bytes 1000 | tf_op jit(solution)/shard_map/project_1/pallas_call | solution.py:588
  54.7 3.7 %attend_1.1 = (f32[256,1024]{1,0:T(8,128)S(1)}, bf16[256,1024]{1,0:T(8,128)(2,1)S(1)}, bf16[512,256]{1,0:T(8,128)(2,1)S(1)}, f32[8,256]{1,0:T(8,128)S(1)}, bf16[16,256]{1,0:T(8,128)(2,1)S(1)}) custom-call(s32[4]{0:T(128)S(1)} %pad_add_fusion.info.refs_0_, bf16[512,2048]{1,0:T(8,128)(2,1)} %refs_3_.5, ...), custom_call_target="tpu_custom_call" | custom-call | flops 1000 | bytes 1000 | tf_op jit(solution)/shard_map/attend_1/pallas_call | solution.py:588
  58.5 4.0 %collective-permute-done.11.refs_1_ = bf16[256,1024]{1,0:T(8,128)(2,1)S(1)} collective-permute-done((bf16[256,1024]{1,0:T(8,128)(2,1)S(1)}, bf16[256,1024]{1,0:T(8,128)(2,1)S(1)}, u32[]{:S(2)}, u32[]{:S(2)}) %collective-permute-start.11) | collective-permute-done | bytes 524320 | tf_op jit(solution)/shard_map/ppermute | solution.py:627
  65.1 0.7 collective-permute-done.8.refs_12_.refs_11_
  65.9 0.7 collective-permute-done.12.refs_8_
  66.6 12.9 %front_0.1 = (bf16[256,2048]{1,0:T(8,128)(2,1)S(1)}, f32[256,512]{1,0:T(8,128)S(1)}, bf16[256,2048]{1,0:T(8,128)(2,1)S(1)}, bf16[256,2048]{1,0:T(8,128)(2,1)S(1)...) custom-call(s32[4]{0:T(128)S(1)} %pad_add_fusion.info.refs_0_, ...), custom_call_target="tpu_custom_call" | custom-call | flops 1000 | bytes 1000 | tf_op jit(solution)/shard_map/front_0/pallas_call | solution.py:588
  79.5 1.0 copy-done.1
  80.8 1.8 collective-permute-done.16.refs_8_
  82.6 12.2 %front_1.1 = (bf16[256,2048]{1,0:T(8,128)(2,1)S(1)}, f32[256,512]{1,0:T(8,128)S(1)}, bf16[256,2048]{1,0:T(8,128)(2,1)S(1)}, bf16[256,2048]{1,0:T(8,128)(2,1)S(1)...) custom-call(s32[4]{0:T(128)S(1)} %pad_add_fusion.info.refs_0_, ...), custom_call_target="tpu_custom_call" | custom-call | flops 1000 | bytes 1000 | tf_op jit(solution)/shard_map/front_1/pallas_call | solution.py:588
  94.8 1.0 copy-done.3
  95.8 2.9 %collective-permute-start.17 = (bf16[1,192,512]{2,1,0:T(8,128)(2,1)S(1)}, bf16[1,192,512]{2,1,0:T(8,128)(2,1)S(1)}, u32[]{:S(2)}, u32[]{:S(2)}) collective-permute-start(bf16[1,192,512]{2,1,0:T(8,128)(2,1)S(1)} %bitcast.33), channel_id=1, source_target_pairs={{0,16},{4,20},{8,24},{12,28},{16,0},{20,4},{24,8},{28,12},{1,17},{... | collective-permute-start | bytes 589832 | tf_op jit(solution)/shard_map/ppermute | solution.py:627
  98.7 11.0 %back_1.1 = (f32[256,1024]{1,0:T(8,128)S(1)}, bf16[256,1024]{1,0:T(8,128)(2,1)S(1)}, f32[256,1024]{1,0:T(8,128)S(1)}, bf16[256,1024]{1,0:T(8,128)(2,1)S(1)}, f32[48,2048]{1,0:T(8,128)S(1)}) custom-call(s32[4]{0:T(128)S(1)} %pad_add_fusion.info.refs_0_, bf16[2,2048,2048]{2,1,0:T(8,128)(2,1)S(1)} %get-tuple-element.142.refs_1_, ...), custom_call_target="tpu_custom_call" | custom-call | flops 1000 | bytes 1000 | tf_op jit(solution)/shard_map/back_1/pallas_call | solution.py:588
  109.8 1.5 collective-permute-start.20
  111.3 1.5 collective-permute-start.19
  113.5 11.0 %back_0.1 = (f32[304,1024]{1,0:T(8,128)S(1)}, bf16[304,1024]{1,0:T(8,128)(2,1)S(1)}, f32[256,1024]{1,0:T(8,128)S(1)}, bf16[256,1024]{1,0:T(8,128)(2,1)S(1)}) custom-call(s32[4]{0:T(128)S(1)} %copy-done.24, bf16[2,2048,2048]{2,1,0:T(8,128)(2,1)S(1)} %get-tuple-element.142.refs_1_, bf16[2048,2048]{1,0:T(8,128)(2,1)S(1)} %get-tuple-element.143.refs_2_, ...), custom_call_target="tpu_custom_call" | custom-call | flops 1000 | bytes 1000 | tf_op jit(solution)/shard_map/back_0/pallas_call | solution.py:588
  124.7 2.0 collective-permute-done.23.refs_1_
  128.8 10.7 %attend_back_1.1 = (f32[256,512]{1,0:T(8,128)S(1)}, f32[256,1152]{1,0:T(8,128)S(1)}, bf16[256,1152]{1,0:T(8,128)(2,1)S(1)}, f32[256,1]{1,0:T(8,128)S(1)}, f32[48...) custom-call(s32[4]{0:T(128)S(1)} %copy-done.24, ...), custom_call_target="tpu_custom_call" | custom-call | flops 1000 | bytes 1000 | tf_op jit(solution)/shard_map/attend_back_1/pallas_call | solution.py:588
  139.8 4.1 %collective-permute-done.22.refs_1_ = bf16[304,1024]{1,0:T(8,128)(2,1)S(1)} collective-permute-done((bf16[304,1024]{1,0:T(8,128)(2,1)S(1)}, bf16[304,1024]{1,0:T(8,128)(2,1)S(1)}, u32[]{:S(2)}, u32[]{:S(2)}) %collective-permute-start.22) | collective-permute-done | bytes 622624 | tf_op jit(solution)/shard_map/ppermute | solution.py:627
  145.4 1.0 collective-permute-start.30
  147.6 9.7 %attend_back_0.1 = (f32[256,512]{1,0:T(8,128)S(1)}, f32[256,1152]{1,0:T(8,128)S(1)}, bf16[256,1152]{1,0:T(8,128)(2,1)S(1)}, f32[256,1]{1,0:T(8,128)S(1)}, bf16[4...) custom-call(s32[4]{0:T(128)S(1)} %copy-done.24, bf16[2048,512]{1,0:T(8,128)(2,1)} %refs_1_.15, ...), custom_call_target="tpu_custom_call" | custom-call | flops 1000 | bytes 1000 | tf_op jit(solution)/shard_map/attend_back_0/pallas_call | solution.py:588
  158.7 0.9 collective-permute-done.34
  159.7 1.0 collective-permute-start.35
  160.7 1.2 collective-permute-start.33
  162.3 1.0 slice.116
  163.2 0.7 slice.115
  164.7 1.1 collective-permute-start.36
  165.9 1.3 collective-permute-start.40
  167.2 4.7 %collective-permute-done.36 = bf16[1,112,512]{2,1,0:T(8,128)(2,1)S(1)} collective-permute-done((bf16[1,112,512]{2,1,0:T(8,128)(2,1)S(1)}, bf16[1,112,512]{2,1,0:T(8,128)(2,1)S(1)}, u32[]{:S(2)}, u32[]{:S(2)}) %collective-permute-start.36) | collective-permute-done | bytes 114720 | tf_op jit(solution)/shard_map/ppermute | solution.py:627
  172.0 1.2 finish.1
  173.2 4.1 %all-to-all-start.1 = ((bf16[8,64,512]{2,1,0:T(8,128)(2,1)}), bf16[8,64,512]{2,1,0:T(8,128)(2,1)S(1)}, u32[]{:S(2)}, u32[]{:S(2)}) async-start(bf16[8,64,512]{2,1,0:T(8,128)(2,1)} %bitcast.13), calls=%async_computation.1 | async-start | bytes 1048576 | tf_op jit(solution)/shard_map/all_to_all | solution.py:823
  177.3 1.2 pad_maximum_fusion
  178.5 1.5 collective-permute-start.37
  180.0 0.9 constant_dynamic-update-slice_fusion.1
  180.9 2.1 collective-permute-start.38
  183.0 0.9 constant_dynamic-update-slice_fusion.refs_4_
  184.0 1.5 collective-permute-start.41
  185.5 1.2 slice_add_fusion
  186.9 6.1 %collective-permute-done.38 = bf16[2,112,512]{2,1,0:T(8,128)(2,1)S(1)} collective-permute-done((bf16[2,112,512]{2,1,0:T(8,128)(2,1)S(1)}, bf16[2,112,512]{2,1,0:T(8,128)(2,1)S(1)}, u32[]{:S(2)}, u32[]{:S(2)}) %collective-permute-start.38) | collective-permute-done | bytes 229408 | tf_op jit(solution)/shard_map/ppermute | solution.py:627
  193.1 1.6 collective-permute-start.39
  194.6 0.9 collective-permute-done.41.refs_5_
  195.5 0.9 fusion.1
  196.4 4.4 %all-to-all-start.2 = ((bf16[8,64,512]{2,1,0:T(8,128)(2,1)}), bf16[8,64,512]{2,1,0:T(8,128)(2,1)S(1)}, u32[]{:S(2)}, u32[]{:S(2)}) async-start(bf16[8,64,512]{2,1,0:T(8,128)(2,1)} %bitcast.35), calls=%async_computation.2 | async-start | bytes 1048576 | tf_op jit(solution)/shard_map/all_to_all | solution.py:831
  200.9 2.0 collective-permute-start.46
  202.9 1.0 copy-done.8
  203.9 1.0 copy-done.10
  204.9 5.2 %feedforward_sum.1 = (f32[8,32,2048]{2,1,0:T(8,128)}, f32[8,16,2048]{2,1,0:T(8,128)}, f32[8,2,16,2048]{3,2,1,0:T(8,128)}, f32[8,16,2048]{2,1,0:T(8,128)}) custom-call(s32[4]{0:T(128)S(1)} %copy-done.25, s32[8]{0:T(128)S(1)} %copy-done.30, bf16[2,192,512]{2,1,0:T(8,128)(2,1)S(1)} %pad_maximum_fusion.2.refs_0_, bf16[2,192,512]{2,1,0:T(8,128)(2,1)S(1)} %copy-done.8, ...), custom_call_target="tpu_custom_call" | custom-call | bytes 12000000 | tf_op jit(solution)/shard_map/feedforward_sum/pallas_call | solution.py:611
  210.1 1.4 collect_grad.1
  212.3 7.5 %collective-permute-done.47.refs_7_ = bf16[4,64,512]{2,1,0:T(8,128)(2,1)S(1)} collective-permute-done((bf16[4,64,512]{2,1,0:T(8,128)(2,1)S(1)}, bf16[4,64,512]{2,1,0:T(8,128)(2,1)S(1)}, u32[]{:S(2)}, u32[]{:S(2)}) %collective-permute-start.47) | collective-permute-done | bytes 262176 | tf_op jit(solution)/shard_map/ppermute | solution.py:627
  219.8 1.4 collect_out.1
  222.1 0.9 copy-done.14
  223.0 4.4 %attention_sum.1 = (f32[8,48,2048]{2,1,0:T(8,128)}, f32[8,16,2048]{2,1,0:T(8,128)}, f32[8,16,512]{2,1,0:T(8,128)}, f32[8,2,16,128]{3,2,1,0:T(8,128)}, f32[8,16,512]{2,1,0:T(8,128)}) custom-call(s32[4]{0:T(128)S(1)} %copy-done.25, s32[8]{0:T(128)S(1)} %copy-done.31, bf16[4,112,512]{2,1,0:T(8,128)(2,1)S(1)} %pad_maximum_fusion.1.refs_0_, ...), custom_call_target="tpu_custom_call" | custom-call | bytes 12000000 | tf_op jit(solution)/shard_map/attention_sum/pallas_call | solution.py:611
  (183 shorter events, 18.7 us)
Async XLA Ops:
  3.9 23.0 %all-to-all-start = ((bf16[8,64,512]{2,1,0:T(8,128)(2,1)}), bf16[8,64,512]{2,1,0:T(8,128)(2,1)S(1)}, u32[]{:S(2)}, u32[]{:S(2)}) async-start(bf16[8,64,512]{2,1,0:T(8,128)(2,1)} %deal.1), calls=%async_computation | async-start | bytes 1048576 | tf_op jit(solution)/shard_map/all_to_all | solution.py:709
  11.2 7.5 %collective-permute-start = (bf16[2,512]{1,0:T(2,128)(2,1)S(1)}, bf16[2,512]{1,0:T(2,128)(2,1)S(1)}, u32[]{:S(2)}, u32[]{:S(2)}) collective-permute-start(bf16[2,512]{1,0:T(2,128)(2,1)S(1)} %pad_maximum_fusion.6), channel_id=1, source_target_pairs={{0,1},{1,0},{2,3},{3,2},{4,5},{5,4},{6,7},{7,6},{8,9},{9,8},{10,11... | collective-permute-start | bytes 6152 | tf_op jit(solution)/shard_map/ppermute | solution.py:627
  11.3 4.1 %collective-permute-start.1 = (bf16[2,512]{1,0:T(2,128)(2,1)S(1)}, bf16[2,512]{1,0:T(2,128)(2,1)S(1)}, u32[]{:S(2)}, u32[]{:S(2)}) collective-permute-start(bf16[2,512]{1,0:T(2,128)(2,1)S(1)} %pad_maximum_fusion.6), channel_id=1, source_target_pairs={{0,2},{1,3},{2,0},{3,1},{4,6},{5,7},{6,4},{7,5},{8,10},{9,11},{10,... | collective-permute-start | bytes 6152 | tf_op jit(solution)/shard_map/ppermute | solution.py:627
  12.9 14.0 %collective-permute-start.3 = (bf16[512,512]{1,0:T(8,128)(2,1)S(1)}, bf16[512,512]{1,0:T(8,128)(2,1)S(1)}, u32[]{:S(2)}, u32[]{:S(2)}) collective-permute-start(bf16[512,512]{1,0:T(8,128)(2,1)S(1)} %bitcast.27), channel_id=1, source_target_pairs={{0,2},{1,3},{2,0},{3,1},{4,6},{5,7},{6,4},{7,5},{8,10},{9,11},{10,... | collective-permute-start | bytes 1572872 | tf_op jit(solution)/shard_map/ppermute | solution.py:627
  15.4 3.3 %collective-permute-start.2 = (bf16[2,512]{1,0:T(2,128)(2,1)S(1)}, bf16[2,512]{1,0:T(2,128)(2,1)S(1)}, u32[]{:S(2)}, u32[]{:S(2)}) collective-permute-start(bf16[2,512]{1,0:T(2,128)(2,1)S(1)} %collective-permute-done.1), channel_id=1, source_target_pairs={{0,1},{1,0},{2,3},{3,2},{4,5},{5,4},{6,7},{7,6},{8,9},{9,8},{10,11... | collective-permute-start | bytes 6152 | tf_op jit(solution)/shard_map/ppermute | solution.py:627
  16.8 81.8 %copy-start.23 = (s32[4]{0:T(128)}, s32[4]{0:T(128)S(1)}, u32[]{:S(2)}) copy-start(s32[4]{0:T(128)S(1)} %pad_add_fusion.info.refs_0_) | copy-start | bytes 52
  16.9 19.2 %copy-start.19 = (f32[32,256]{1,0:T(8,128)S(1)}, f32[32,256]{1,0:T(8,128)}, u32[]{:S(2)}) copy-start(f32[32,256]{1,0:T(8,128)} %constant.23.clone.refs_12_.refs_22_) | copy-start | bytes 98308
  16.9 19.2 %copy-start.21 = (f32[32,256]{1,0:T(8,128)S(1)}, f32[32,256]{1,0:T(8,128)}, u32[]{:S(2)}) copy-start(f32[32,256]{1,0:T(8,128)} %constant.21.clone.refs_11_.refs_21_) | copy-start | bytes 98308
  18.7 31.9 %copy-start.15 = (bf16[16,512]{1,0:T(8,128)(2,1)}, bf16[16,512]{1,0:T(8,128)(2,1)S(1)}, u32[]{:S(2)}) copy-start(bf16[16,512]{1,0:T(8,128)(2,1)S(1)} %get-tuple-element.117.refs_9_.refs_17_) | copy-start | bytes 49156
  18.7 36.0 %copy-start.11 = (bf16[16,512]{1,0:T(8,128)(2,1)}, bf16[16,512]{1,0:T(8,128)(2,1)S(1)}, u32[]{:S(2)}) copy-start(bf16[16,512]{1,0:T(8,128)(2,1)S(1)} %get-tuple-element.120.refs_3_.refs_19_) | copy-start | bytes 49156
  26.9 7.6 %collective-permute-start.5 = (bf16[256,512]{1,0:T(8,128)(2,1)S(1)}, bf16[256,512]{1,0:T(8,128)(2,1)S(1)}, u32[]{:S(2)}, u32[]{:S(2)}) collective-permute-start(bf16[256,512]{1,0:T(8,128)(2,1)S(1)} %get-tuple-element.222), channel_id=1, source_target_pairs={{0,2},{1,3},{2,0},{3,1},{4,6},{5,7},{6,4},{7,5},{8,10},{9,11},{10,... | collective-permute-start | bytes 786440 | tf_op jit(solution)/shard_map/ppermute | solution.py:627
  27.5 8.6 %collective-permute-start.4 = (bf16[512,512]{1,0:T(8,128)(2,1)S(1)}, bf16[512,512]{1,0:T(8,128)(2,1)S(1)}, u32[]{:S(2)}, u32[]{:S(2)}) collective-permute-start(bf16[512,512]{1,0:T(8,128)(2,1)S(1)} %bitcast.19), channel_id=1, source_target_pairs={{0,1},{1,0},{2,3},{3,2},{4,5},{5,4},{6,7},{7,6},{8,9},{9,8},{10,11... | collective-permute-start | bytes 1572872 | tf_op jit(solution)/shard_map/ppermute | solution.py:627
  34.5 1.5 collective-permute-start.6
  34.5 8.7 %collective-permute-start.9 = (bf16[256,512]{1,0:T(8,128)(2,1)S(1)}, bf16[256,512]{1,0:T(8,128)(2,1)S(1)}, u32[]{:S(2)}, u32[]{:S(2)}) collective-permute-start(bf16[256,512]{1,0:T(8,128)(2,1)S(1)} %get-tuple-element.221), channel_id=1, source_target_pairs={{0,2},{1,3},{2,0},{3,1},{4,6},{5,7},{6,4},{7,5},{8,10},{9,11},{10,... | collective-permute-start | bytes 786440 | tf_op jit(solution)/shard_map/ppermute | solution.py:627
  46.3 2.0 collective-permute-start.10
  48.5 14.0 %collective-permute-start.11 = (bf16[256,1024]{1,0:T(8,128)(2,1)S(1)}, bf16[256,1024]{1,0:T(8,128)(2,1)S(1)}, u32[]{:S(2)}, u32[]{:S(2)}) collective-permute-start(bf16[256,1024]{1,0:T(8,128)(2,1)S(1)} %pair_sum.4.refs_0_.refs_14_), channel_id=1, source_target_pairs={{0,2},{1,3},{2,0},{3,1},{4,6},{5,7},{6,4},{7,5},{8,10},{9,11},{10,... | collective-permute-start | bytes 1572872 | tf_op jit(solution)/shard_map/ppermute | solution.py:627
  49.1 1.5 collective-permute-start.13
  62.5 1.9 collective-permute-start.14
  62.5 2.7 %collective-permute-start.7 = (bf16[512,512]{1,0:T(8,128)(2,1)S(1)}, bf16[512,512]{1,0:T(8,128)(2,1)S(1)}, u32[]{:S(2)}, u32[]{:S(2)}) collective-permute-start(bf16[512,512]{1,0:T(8,128)(2,1)S(1)} %bitcast.28), channel_id=1, source_target_pairs={{0,1},{1,0},{2,3},{3,2},{4,5},{5,4},{6,7},{7,6},{8,9},{9,8},{10,11... | collective-permute-start | bytes 1572872 | tf_op jit(solution)/shard_map/ppermute | solution.py:627
  63.0 2.9 %collective-permute-start.8 = (bf16[512,512]{1,0:T(8,128)(2,1)S(1)}, bf16[512,512]{1,0:T(8,128)(2,1)S(1)}, u32[]{:S(2)}, u32[]{:S(2)}) collective-permute-start(bf16[512,512]{1,0:T(8,128)(2,1)S(1)} %collective-permute-done.3.refs_11_.refs_10_), channel_id=1, source_target_pairs={{0,1},{1,0},{2,3},{3,2},{4,5},{5,4},{6,7},{7,6},{8,9},{9,8},{10,11... | collective-permute-start | bytes 1572872 | tf_op jit(solution)/shard_map/ppermute | solution.py:627
  63.1 3.5 %collective-permute-start.12 = (bf16[256,1024]{1,0:T(8,128)(2,1)S(1)}, bf16[256,1024]{1,0:T(8,128)(2,1)S(1)}, u32[]{:S(2)}, u32[]{:S(2)}) collective-permute-start(bf16[256,1024]{1,0:T(8,128)(2,1)S(1)} %far_sum.4.refs_7_), channel_id=1, source_target_pairs={{0,1},{1,0},{2,3},{3,2},{4,5},{5,4},{6,7},{7,6},{8,9},{9,8},{10,11... | collective-permute-start | bytes 1572872 | tf_op jit(solution)/shard_map/ppermute | solution.py:627
  64.5 16.0 %collective-permute-start.15 = (bf16[256,1024]{1,0:T(8,128)(2,1)S(1)}, bf16[256,1024]{1,0:T(8,128)(2,1)S(1)}, u32[]{:S(2)}, u32[]{:S(2)}) collective-permute-start(bf16[256,1024]{1,0:T(8,128)(2,1)S(1)} %pair_sum.5.refs_19_.refs_0_), channel_id=1, source_target_pairs={{0,2},{1,3},{2,0},{3,1},{4,6},{5,7},{6,4},{7,5},{8,10},{9,11},{10,... | collective-permute-start | bytes 1572872 | tf_op jit(solution)/shard_map/ppermute | solution.py:627
  80.5 14.3 %copy-start.5 = (f32[256,512]{1,0:T(8,128)}, f32[256,512]{1,0:T(8,128)S(1)}, u32[]{:S(2)}) copy-start(f32[256,512]{1,0:T(8,128)S(1)} %get-tuple-element.201) | copy-start | bytes 1572868
  80.6 2.0 collective-permute-start.16
  95.8 14.0 %collective-permute-start.17 = (bf16[1,192,512]{2,1,0:T(8,128)(2,1)S(1)}, bf16[1,192,512]{2,1,0:T(8,128)(2,1)S(1)}, u32[]{:S(2)}, u32[]{:S(2)}) collective-permute-start(bf16[1,192,512]{2,1,0:T(8,128)(2,1)S(1)} %bitcast.33), channel_id=1, source_target_pairs={{0,16},{4,20},{8,24},{12,28},{16,0},{20,4},{24,8},{28,12},{1,17},{... | collective-permute-start | bytes 589832 | tf_op jit(solution)/shard_map/ppermute | solution.py:627
  109.7 3.1 %collective-permute-start.18 = (bf16[256,1024]{1,0:T(8,128)(2,1)S(1)}, bf16[256,1024]{1,0:T(8,128)(2,1)S(1)}, u32[]{:S(2)}, u32[]{:S(2)}) collective-permute-start(bf16[256,1024]{1,0:T(8,128)(2,1)S(1)} %get-tuple-element.162), channel_id=1, source_target_pairs={{0,1},{1,0},{2,3},{3,2},{4,5},{5,4},{6,7},{7,6},{8,9},{9,8},{10,11... | collective-permute-start | bytes 1572872 | tf_op jit(solution)/shard_map/ppermute | solution.py:627
  109.8 14.7 %collective-permute-start.20 = (bf16[2,192,512]{2,1,0:T(8,128)(2,1)S(1)}, bf16[2,192,512]{2,1,0:T(8,128)(2,1)S(1)}, u32[]{:S(2)}, u32[]{:S(2)}) collective-permute-start(bf16[2,192,512]{2,1,0:T(8,128)(2,1)S(1)} %pad_maximum_fusion.2.refs_0_), channel_id=1, source_target_pairs={{0,4},{4,0},{8,12},{12,8},{16,20},{20,16},{24,28},{28,24},{1,5},{5... | collective-permute-start | bytes 1179656 | tf_op jit(solution)/shard_map/ppermute | solution.py:627
  111.3 13.3 %collective-permute-start.19 = (bf16[2,192,512]{2,1,0:T(8,128)(2,1)S(1)}, bf16[2,192,512]{2,1,0:T(8,128)(2,1)S(1)}, u32[]{:S(2)}, u32[]{:S(2)}) collective-permute-start(bf16[2,192,512]{2,1,0:T(8,128)(2,1)S(1)} %pad_maximum_fusion.2.refs_0_), channel_id=1, source_target_pairs={{0,8},{4,12},{8,0},{12,4},{16,24},{20,28},{24,16},{28,20},{1,9},{5... | collective-permute-start | bytes 1179656 | tf_op jit(solution)/shard_map/ppermute | solution.py:627
  112.9 13.8 %collective-permute-start.23 = (bf16[256,1024]{1,0:T(8,128)(2,1)S(1)}, bf16[256,1024]{1,0:T(8,128)(2,1)S(1)}, u32[]{:S(2)}, u32[]{:S(2)}) collective-permute-start(bf16[256,1024]{1,0:T(8,128)(2,1)S(1)} %pair_sum.6.refs_13_.refs_0_), channel_id=1, source_target_pairs={{0,2},{1,3},{2,0},{3,1},{4,6},{5,7},{6,4},{7,5},{8,10},{9,11},{10,... | collective-permute-start | bytes 1572872 | tf_op jit(solution)/shard_map/ppermute | solution.py:627
  124.6 15.0 %copy-start.7 = (bf16[2,192,512]{2,1,0:T(8,128)(2,1)}, bf16[2,192,512]{2,1,0:T(8,128)(2,1)S(1)}, u32[]{:S(2)}) copy-start(bf16[2,192,512]{2,1,0:T(8,128)(2,1)S(1)} %collective-permute-done.19.refs_1_) | copy-start | bytes 1179652
  124.6 2.9 %collective-permute-start.21 = (bf16[304,1024]{1,0:T(8,128)(2,1)S(1)}, bf16[304,1024]{1,0:T(8,128)(2,1)S(1)}, u32[]{:S(2)}, u32[]{:S(2)}) collective-permute-start(bf16[304,1024]{1,0:T(8,128)(2,1)S(1)} %get-tuple-element.165), channel_id=1, source_target_pairs={{0,1},{1,0},{2,3},{3,2},{4,5},{5,4},{6,7},{7,6},{8,9},{9,8},{10,11... | collective-permute-start | bytes 1867784 | tf_op jit(solution)/shard_map/ppermute | solution.py:627
  126.8 2.0 collective-permute-start.24
  126.9 12.7 %collective-permute-start.26 = (bf16[2,192,512]{2,1,0:T(8,128)(2,1)S(1)}, bf16[2,192,512]{2,1,0:T(8,128)(2,1)S(1)}, u32[]{:S(2)}, u32[]{:S(2)}) collective-permute-start(bf16[2,192,512]{2,1,0:T(8,128)(2,1)S(1)} %collective-permute-done.19.refs_1_), channel_id=1, source_target_pairs={{0,4},{4,0},{8,12},{12,8},{16,20},{20,16},{24,28},{28,24},{1,5},{5... | collective-permute-start | bytes 1179656 | tf_op jit(solution)/shard_map/ppermute | solution.py:627
  127.7 16.2 %collective-permute-start.22 = (bf16[304,1024]{1,0:T(8,128)(2,1)S(1)}, bf16[304,1024]{1,0:T(8,128)(2,1)S(1)}, u32[]{:S(2)}, u32[]{:S(2)}) collective-permute-start(bf16[304,1024]{1,0:T(8,128)(2,1)S(1)} %pair_sum.7.refs_34_.refs_0_), channel_id=1, source_target_pairs={{0,2},{1,3},{2,0},{3,1},{4,6},{5,7},{6,4},{7,5},{8,10},{9,11},{10,... | collective-permute-start | bytes 1867784 | tf_op jit(solution)/shard_map/ppermute | solution.py:627
  139.6 17.8 %copy-start.9 = (bf16[2,192,512]{2,1,0:T(8,128)(2,1)}, bf16[2,192,512]{2,1,0:T(8,128)(2,1)S(1)}, u32[]{:S(2)}) copy-start(bf16[2,192,512]{2,1,0:T(8,128)(2,1)S(1)} %collective-permute-done.26.refs_3_) | copy-start | bytes 1179652
  139.6 5.0 %collective-permute-start.27 = (bf16[256,1152]{1,0:T(8,128)(2,1)S(1)}, bf16[256,1152]{1,0:T(8,128)(2,1)S(1)}, u32[]{:S(2)}, u32[]{:S(2)}) collective-permute-start(bf16[256,1152]{1,0:T(8,128)(2,1)S(1)} %get-tuple-element.184), channel_id=1, source_target_pairs={{0,1},{1,0},{2,3},{3,2},{4,5},{5,4},{6,7},{7,6},{8,9},{9,8},{10,11... | collective-permute-start | bytes 1769480 | tf_op jit(solution)/shard_map/ppermute | solution.py:627
  144.0 3.6 %collective-permute-start.25 = (bf16[304,1024]{1,0:T(8,128)(2,1)S(1)}, bf16[304,1024]{1,0:T(8,128)(2,1)S(1)}, u32[]{:S(2)}, u32[]{:S(2)}) collective-permute-start(bf16[304,1024]{1,0:T(8,128)(2,1)S(1)} %far_sum.7.refs_13_), channel_id=1, source_target_pairs={{0,1},{1,0},{2,3},{3,2},{4,5},{5,4},{6,7},{7,6},{8,9},{9,8},{10,11... | collective-permute-start | bytes 1867784 | tf_op jit(solution)/shard_map/ppermute | solution.py:627
  144.1 3.0 %collective-permute-start.28 = (bf16[256,1024]{1,0:T(8,128)(2,1)S(1)}, bf16[256,1024]{1,0:T(8,128)(2,1)S(1)}, u32[]{:S(2)}, u32[]{:S(2)}) collective-permute-start(bf16[256,1024]{1,0:T(8,128)(2,1)S(1)} %get-tuple-element.186), channel_id=1, source_target_pairs={{0,1},{1,0},{2,3},{3,2},{4,5},{5,4},{6,7},{7,6},{8,9},{9,8},{10,11... | collective-permute-start | bytes 1572872 | tf_op jit(solution)/shard_map/ppermute | solution.py:627
  144.6 3.0 %collective-permute-start.29 = (bf16[256,1024]{1,0:T(8,128)(2,1)S(1)}, bf16[256,1024]{1,0:T(8,128)(2,1)S(1)}, u32[]{:S(2)}, u32[]{:S(2)}) collective-permute-start(bf16[256,1024]{1,0:T(8,128)(2,1)S(1)} %get-tuple-element.188), channel_id=1, source_target_pairs={{0,1},{1,0},{2,3},{3,2},{4,5},{5,4},{6,7},{7,6},{8,9},{9,8},{10,11... | collective-permute-start | bytes 1572872 | tf_op jit(solution)/shard_map/ppermute | solution.py:627
  144.7 12.7 %collective-permute-start.31 = (bf16[256,640]{1,0:T(8,128)(2,1)S(1)}, bf16[256,640]{1,0:T(8,128)(2,1)S(1)}, u32[]{:S(2)}, u32[]{:S(2)}) collective-permute-start(bf16[256,640]{1,0:T(8,128)(2,1)S(1)} %add_convert_fusion.1.refs_35_.refs_9_), channel_id=1, source_target_pairs={{0,2},{1,3},{2,0},{3,1},{4,6},{5,7},{6,4},{7,5},{8,10},{9,11},{10,... | collective-permute-start | bytes 983048 | tf_op jit(solution)/shard_map/ppermute | solution.py:627
  145.4 12.0 %collective-permute-start.30 = (bf16[1,48,1024]{2,1,0:T(8,128)(2,1)S(1)}, bf16[1,48,1024]{2,1,0:T(8,128)(2,1)S(1)}, u32[]{:S(2)}, u32[]{:S(2)}) collective-permute-start(bf16[1,48,1024]{2,1,0:T(8,128)(2,1)S(1)} %slice_bitcast_fusion), channel_id=1, source_target_pairs={{0,16},{4,20},{8,24},{12,28},{16,0},{20,4},{24,8},{28,12},{1,17},{... | collective-permute-start | bytes 294920 | tf_op jit(solution)/shard_map/ppermute | solution.py:627
  157.4 3.3 %collective-permute-start.32 = (bf16[256,1152]{1,0:T(8,128)(2,1)S(1)}, bf16[256,1152]{1,0:T(8,128)(2,1)S(1)}, u32[]{:S(2)}, u32[]{:S(2)}) collective-permute-start(bf16[256,1152]{1,0:T(8,128)(2,1)S(1)} %get-tuple-element.192), channel_id=1, source_target_pairs={{0,1},{1,0},{2,3},{3,2},{4,5},{5,4},{6,7},{7,6},{8,9},{9,8},{10,11... | collective-permute-start | bytes 1769480 | tf_op jit(solution)/shard_map/ppermute | solution.py:627
  158.3 1.4 collective-permute-start.34
  159.7 5.0 %collective-permute-start.35 = (bf16[64,512]{1,0:T(8,128)(2,1)S(1)}, bf16[64,512]{1,0:T(8,128)(2,1)S(1)}, u32[]{:S(2)}, u32[]{:S(2)}) collective-permute-start(bf16[64,512]{1,0:T(8,128)(2,1)S(1)} %add_convert_fusion.3), channel_id=1, source_target_pairs={{0,2},{1,3},{2,0},{3,1},{4,6},{5,7},{6,4},{7,5},{8,10},{9,11},{10,... | collective-permute-start | bytes 196616 | tf_op jit(solution)/shard_map/ppermute | solution.py:627
  160.7 11.2 %collective-permute-start.33 = (bf16[256,640]{1,0:T(8,128)(2,1)S(1)}, bf16[256,640]{1,0:T(8,128)(2,1)S(1)}, u32[]{:S(2)}, u32[]{:S(2)}) collective-permute-start(bf16[256,640]{1,0:T(8,128)(2,1)S(1)} %add_convert_fusion.refs_4_), channel_id=1, source_target_pairs={{0,2},{1,3},{2,0},{3,1},{4,6},{5,7},{6,4},{7,5},{8,10},{9,11},{10,... | collective-permute-start | bytes 983048 | tf_op jit(solution)/shard_map/ppermute | solution.py:627
  164.7 7.2 %collective-permute-start.36 = (bf16[1,112,512]{2,1,0:T(8,128)(2,1)S(1)}, bf16[1,112,512]{2,1,0:T(8,128)(2,1)S(1)}, u32[]{:S(2)}, u32[]{:S(2)}) collective-permute-start(bf16[1,112,512]{2,1,0:T(8,128)(2,1)S(1)} %maximum_bitcast_fusion), channel_id=1, source_target_pairs={{0,16},{4,20},{8,24},{12,28},{16,0},{20,4},{24,8},{28,12},{1,17},{... | collective-permute-start | bytes 344072 | tf_op jit(solution)/shard_map/ppermute | solution.py:627
  165.9 17.2 %collective-permute-start.40 = (bf16[2,48,1024]{2,1,0:T(8,128)(2,1)}, bf16[2,48,1024]{2,1,0:T(8,128)(2,1)}, u32[]{:S(2)}, u32[]{:S(2)}) collective-permute-start(bf16[2,48,1024]{2,1,0:T(8,128)(2,1)} %pad_maximum_fusion.4), channel_id=1, source_target_pairs={{0,8},{4,12},{8,0},{12,4},{16,24},{20,28},{24,16},{28,20},{1,9},{5... | collective-permute-start | bytes 589832 | tf_op jit(solution)/shard_map/ppermute | solution.py:627
  173.2 23.2 %all-to-all-start.1 = ((bf16[8,64,512]{2,1,0:T(8,128)(2,1)}), bf16[8,64,512]{2,1,0:T(8,128)(2,1)S(1)}, u32[]{:S(2)}, u32[]{:S(2)}) async-start(bf16[8,64,512]{2,1,0:T(8,128)(2,1)} %bitcast.13), calls=%async_computation.1 | async-start | bytes 1048576 | tf_op jit(solution)/shard_map/all_to_all | solution.py:823
  178.4 14.6 %copy-start.36 = (bf16[1,112,512]{2,1,0:T(8,128)(2,1)S(1)}, bf16[1,112,512]{2,1,0:T(8,128)(2,1)}, u32[]{:S(2)}) copy-start(bf16[1,112,512]{2,1,0:T(8,128)(2,1)} %copy-done.35) | copy-start | bytes 344068
  178.5 16.2 %collective-permute-start.37 = (bf16[512,512]{1,0:T(8,128)(2,1)S(1)}, bf16[512,512]{1,0:T(8,128)(2,1)S(1)}, u32[]{:S(2)}, u32[]{:S(2)}) collective-permute-start(bf16[512,512]{1,0:T(8,128)(2,1)S(1)} %pad_maximum_fusion), channel_id=1, source_target_pairs={{0,2},{1,3},{2,0},{3,1},{4,6},{5,7},{6,4},{7,5},{8,10},{9,11},{10,... | collective-permute-start | bytes 1572872 | tf_op jit(solution)/shard_map/ppermute | solution.py:627
  180.9 12.1 %collective-permute-start.38 = (bf16[2,112,512]{2,1,0:T(8,128)(2,1)S(1)}, bf16[2,112,512]{2,1,0:T(8,128)(2,1)S(1)}, u32[]{:S(2)}, u32[]{:S(2)}) collective-permute-start(bf16[2,112,512]{2,1,0:T(8,128)(2,1)S(1)} %pad_maximum_fusion.3.refs_12_), channel_id=1, source_target_pairs={{0,8},{4,12},{8,0},{12,4},{16,24},{20,28},{24,16},{28,20},{1,9},{5... | collective-permute-start | bytes 688136 | tf_op jit(solution)/shard_map/ppermute | solution.py:627
  184.0 11.5 %collective-permute-start.41 = (bf16[4,48,1024]{2,1,0:T(8,128)(2,1)S(1)}, bf16[4,48,1024]{2,1,0:T(8,128)(2,1)}, u32[]{:S(2)}, u32[]{:S(2)}) collective-permute-start(bf16[4,48,1024]{2,1,0:T(8,128)(2,1)S(1)} %constant_dynamic-update-slice_fusion.refs_4_), channel_id=1, source_target_pairs={{0,4},{4,0},{8,12},{12,8},{16,20},{20,16},{24,28},{28,24},{1,5},{5... | collective-permute-start | bytes 1179656 | tf_op jit(solution)/shard_map/ppermute | solution.py:627
  186.8 16.1 %copy-start.25 = (s32[4]{0:T(128)S(1)}, s32[4]{0:T(128)}, u32[]{:S(2)}) copy-start(s32[4]{0:T(128)} %copy-done.23) | copy-start | bytes 52
  186.8 16.1 %copy-start.30 = (s32[8]{0:T(128)S(1)}, s32[8]{0:T(128)}, u32[]{:S(2)}) copy-start(s32[8]{0:T(128)} %copy-done.29) | copy-start | bytes 100
  186.8 16.1 %collective-permute-start.42 = (bf16[4,48,1024]{2,1,0:T(8,128)(2,1)S(1)}, bf16[4,48,1024]{2,1,0:T(8,128)(2,1)}, u32[]{:S(2)}, u32[]{:S(2)}) collective-permute-start(bf16[4,48,1024]{2,1,0:T(8,128)(2,1)S(1)} %constant_dynamic-update-slice_fusion.refs_4_), channel_id=1, source_target_pairs={{0,1},{1,0},{2,3},{3,2},{4,5},{5,4},{6,7},{7,6},{8,9},{9,8},{10,11... | collective-permute-start | bytes 1179656 | tf_op jit(solution)/shard_map/ppermute | solution.py:627
  193.1 18.5 %collective-permute-start.39 = (bf16[4,112,512]{2,1,0:T(8,128)(2,1)S(1)}, bf16[4,112,512]{2,1,0:T(8,128)(2,1)S(1)}, u32[]{:S(2)}, u32[]{:S(2)}) collective-permute-start(bf16[4,112,512]{2,1,0:T(8,128)(2,1)S(1)} %pad_maximum_fusion.1.refs_0_), channel_id=1, source_target_pairs={{0,4},{4,0},{8,12},{12,8},{16,20},{20,16},{24,28},{28,24},{1,5},{5... | collective-permute-start | bytes 1376264 | tf_op jit(solution)/shard_map/ppermute | solution.py:627
  195.5 7.4 %collective-permute-start.43 = (bf16[4,48,1024]{2,1,0:T(8,128)(2,1)}, bf16[4,48,1024]{2,1,0:T(8,128)(2,1)}, u32[]{:S(2)}, u32[]{:S(2)}) collective-permute-start(bf16[4,48,1024]{2,1,0:T(8,128)(2,1)} %collective-permute-done.41.refs_5_), channel_id=1, source_target_pairs={{0,1},{1,0},{2,3},{3,2},{4,5},{5,4},{6,7},{7,6},{8,9},{9,8},{10,11... | collective-permute-start | bytes 1179656 | tf_op jit(solution)/shard_map/ppermute | solution.py:627
  196.4 23.4 %all-to-all-start.2 = ((bf16[8,64,512]{2,1,0:T(8,128)(2,1)}), bf16[8,64,512]{2,1,0:T(8,128)(2,1)S(1)}, u32[]{:S(2)}, u32[]{:S(2)}) async-start(bf16[8,64,512]{2,1,0:T(8,128)(2,1)} %bitcast.35), calls=%async_computation.2 | async-start | bytes 1048576 | tf_op jit(solution)/shard_map/all_to_all | solution.py:831
  200.9 10.9 %collective-permute-start.46 = (bf16[4,64,512]{2,1,0:T(8,128)(2,1)S(1)}, bf16[4,64,512]{2,1,0:T(8,128)(2,1)}, u32[]{:S(2)}, u32[]{:S(2)}) collective-permute-start(bf16[4,64,512]{2,1,0:T(8,128)(2,1)S(1)} %slice.97.refs_2_), channel_id=1, source_target_pairs={{0,2},{1,3},{2,0},{3,1},{4,6},{5,7},{6,4},{7,5},{8,10},{9,11},{10,... | collective-permute-start | bytes 786440 | tf_op jit(solution)/shard_map/ppermute | solution.py:627
  211.6 8.2 %collective-permute-start.47 = (bf16[4,64,512]{2,1,0:T(8,128)(2,1)S(1)}, bf16[4,64,512]{2,1,0:T(8,128)(2,1)S(1)}, u32[]{:S(2)}, u32[]{:S(2)}) collective-permute-start(bf16[4,64,512]{2,1,0:T(8,128)(2,1)S(1)} %slice.85.refs_3_), channel_id=1, source_target_pairs={{0,2},{1,3},{2,0},{3,1},{4,6},{5,7},{6,4},{7,5},{8,10},{9,11},{10,... | collective-permute-start | bytes 786440 | tf_op jit(solution)/shard_map/ppermute | solution.py:627
  211.7 9.5 %collective-permute-start.44 = (bf16[4,64,512]{2,1,0:T(8,128)(2,1)S(1)}, bf16[4,64,512]{2,1,0:T(8,128)(2,1)S(1)}, u32[]{:S(2)}, u32[]{:S(2)}) collective-permute-start(bf16[4,64,512]{2,1,0:T(8,128)(2,1)S(1)} %slice.97.refs_2_), channel_id=1, source_target_pairs={{0,1},{1,0},{2,3},{3,2},{4,5},{5,4},{6,7},{7,6},{8,9},{9,8},{10,11... | collective-permute-start | bytes 786440 | tf_op jit(solution)/shard_map/ppermute | solution.py:627
  211.8 9.5 %collective-permute-start.48 = (bf16[4,64,512]{2,1,0:T(8,128)(2,1)}, bf16[4,64,512]{2,1,0:T(8,128)(2,1)S(1)}, u32[]{:S(2)}, u32[]{:S(2)}) collective-permute-start(bf16[4,64,512]{2,1,0:T(8,128)(2,1)} %collective-permute-done.46.refs_6_), channel_id=1, source_target_pairs={{0,1},{1,0},{2,3},{3,2},{4,5},{5,4},{6,7},{7,6},{8,9},{9,8},{10,11... | collective-permute-start | bytes 786440 | tf_op jit(solution)/shard_map/ppermute | solution.py:627
  212.2 9.0 %collective-permute-start.45 = (bf16[4,64,512]{2,1,0:T(8,128)(2,1)S(1)}, bf16[4,64,512]{2,1,0:T(8,128)(2,1)S(1)}, u32[]{:S(2)}, u32[]{:S(2)}) collective-permute-start(bf16[4,64,512]{2,1,0:T(8,128)(2,1)S(1)} %slice.85.refs_3_), channel_id=1, source_target_pairs={{0,1},{1,0},{2,3},{3,2},{4,5},{5,4},{6,7},{7,6},{8,9},{9,8},{10,11... | collective-permute-start | bytes 786440 | tf_op jit(solution)/shard_map/ppermute | solution.py:627
  219.8 1.5 collective-permute-start.49
  (30 other events, 186.7 us)

commit v5 on v4

--- a/solution.py
+++ b/solution.py
@@ -17,6 +17,7 @@
 NEG_FILL = -1e30
 PARTS = 4
 LANES = 128
+SPARE = 32
 ROW_BLOCK = 64
 QUARTER = WIDTH // PARTS
 CHUNKS = 2
@@ -300,7 +301,7 @@
     scratch, rest = rest[-14:], rest[:-14]
     h_in, z_s, f_s, dot_s, dqt_s, dkt_s, dvt_s, dq_s, value_s, low_s, wq, wkv, wo, sems = scratch
     copies = copies_of(((wo_h, wo), (wq_h, wq), (wkv_h, wkv)), sems)
-    n_out = 7 if last else 8
+    n_out = 7 if last else 9
     outs, rest = rest[-n_out:], rest[:-n_out]
     dxq_out, h_keep, h_send, inv_out, b_out = outs[:5]
     triples, rest = rest[:3 * (chunk + 1)], rest[3 * (chunk + 1):]
@@ -409,22 +410,49 @@
         return inner + jnp.sum(d * h_in[:, at].astype(F32), axis=1, keepdims=True)
 
     inner = lax.fori_loop(0, PARTS, block, jnp.zeros((rows, 1), F32))
-    for ref in (h_keep, h_send):
-        ref[:, 2 * QUARTER:] = jnp.broadcast_to(inner, (rows, LANES)).astype(ref.dtype)
-
-
-def finish_kernel(gains, x_all, *refs):
+    inner = jnp.broadcast_to(inner, (rows, LANES)).T[:SPARE // 2, :]
+    if last:
+        for ref in outs[5:7]:
+            for c, value in enumerate((inner, rest[4][...])):
+                at = slice(4 * RANK + c * SPARE // 2, 4 * RANK + (c + 1) * SPARE // 2)
+                ref[at, QUARTER:QUARTER + rows] = value.astype(ref.dtype)
+                ref[at, QUARTER + rows:] = jnp.zeros((SPARE // 2, QUARTER - rows), ref.dtype)
+                ref[at, :QUARTER] = jnp.zeros((SPARE // 2, QUARTER), ref.dtype)
+    else:
+        outs[8][...] = inner
+
+
+def finish_kernel(info, gains, x_all, aa_high, aa_far, y_far, *refs):
     out = refs[-1]
     gain = gains[0, 0:1, :].astype(F32)
     rows = out.shape[0] // CHUNKS
+    inner = aa_high[4 * RANK:, :].astype(F32) + aa_far[4 * RANK:, :].astype(F32)
     for c in range(CHUNKS):
-        dx, low, high, got, inv = refs[5 * c:5 * (c + 1)]
+        dx, keep, got, there, inv, xq, y_keep, y_got = refs[8 * c:8 * (c + 1)]
         x = chunk_of(x_all, c, rows)
+        at = slice(c * rows, (c + 1) * rows)
+        mine = inner[c * SPARE // 2:c * SPARE // 2 + 8, :rows].T[:, 0:1]
         inv = inv[...]
-        inner = high[:rows, QUARTER:QUARTER + 1].astype(F32) + got[:rows, QUARTER:QUARTER + 1].astype(F32)
-        scale = inv * inv * inner / WIDTH
-        grad = inv * (gain * (low[:rows, :] + got[:rows, :QUARTER].astype(F32))) - x[...].astype(F32) * scale
-        out[c * rows:(c + 1) * rows, :] = (dx[...] + grad).astype(BF16)
+        grad = keep[:, LO] + got[:, LO].astype(F32) + there[...].astype(F32)
+        grad = inv * (gain * grad) - x[...].astype(F32) * (inv * inv * mine / WIDTH)
+        out[at, LO] = (dx[...] + grad).astype(BF16)
+        valid = c * rows + lax.broadcasted_iota(jnp.int32, (rows, 1), 0) < info[1]
+        y = xq[...] + y_keep[:, LO] + y_got[:, LO].astype(F32) + y_far[at, :].astype(F32)
+        out[at, HI] = jnp.where(valid, y, 0.0).astype(BF16)
+
+
+def high_sum_kernel(*refs):
+    out = refs[-1]
+    rows = out.shape[0] // (len(refs) // 2)
+    for c in range(len(refs) // 2):
+        keep, got = refs[2 * c:2 * c + 2]
+        out[c * rows:(c + 1) * rows, :] = (keep[:, HI] + got[:, HI].astype(F32)).astype(BF16)
+
+
+def high_sum(*pairs):
+    args = [v for pair in pairs for v in pair]
+    rows = sum(keep.shape[0] for keep, _ in pairs)
+    return call(high_sum_kernel, None, (), args, [((rows, QUARTER), BF16)], [], "high_sum", 8)[0]
 
 
 def split_refs(refs, counts):
@@ -520,8 +548,10 @@
         copy.wait()
 
 
-def collect_kernel(slots, source, out, sems):
-    made = [pltpu.make_async_copy(source.at[slots[i]], out.at[i], sems.at[i]) for i in range(source.shape[0])]
+def collect_kernel(slots, source, *refs):
+    sems = refs[-1]
+    made = [pltpu.make_async_copy(source.at[slots[i], :, cols], ref.at[i], sems.at[k, i])
+            for i in range(source.shape[0]) for k, (ref, cols) in enumerate(zip(refs, (LO, HI)))]
     for copy in made:
         copy.start()
     for copy in made:
@@ -550,18 +580,17 @@
     )(info, *(in_hbm(a) for a in arrays))
 
 
-def move_rows(kernel, value, slots, name, here):
-    space = pltpu.VMEM if here else pl.ANY
+def move_rows(kernel, value, slots, name, outs, in_space, out_space, sems):
     return pl.pallas_call(
         kernel,
-        in_specs=[pl.BlockSpec(memory_space=pltpu.SMEM), pl.BlockSpec(memory_space=pl.ANY if here else pltpu.VMEM)],
-        out_specs=pl.BlockSpec(memory_space=space),
-        out_shape=(pltpu.VMEM if here else jax.ShapeDtypeStruct)(value.shape, value.dtype),
-        scratch_shapes=[pltpu.SemaphoreType.DMA((value.shape[0],))],
+        in_specs=[pl.BlockSpec(memory_space=pltpu.SMEM), pl.BlockSpec(memory_space=in_space)],
+        out_specs=[pl.BlockSpec(memory_space=out_space)] * len(outs),
+        out_shape=outs,
+        scratch_shapes=[pltpu.SemaphoreType.DMA(sems)],
         compiler_params=pltpu.CompilerParams(vmem_limit_bytes=MIB),
         cost_estimate=pl.CostEstimate(flops=1000, transcendentals=0, bytes_accessed=1000),
         name=name,
-    )(slots, in_hbm(value) if here else in_vmem(value))
+    )(slots, pltpu.with_memory_space_constraint(value, in_space))
 
 
 def sds(shape, dtype):
@@ -640,13 +669,6 @@
     return (value, near(value), there, near(there))
 
 
-def chip_sum(keep, send):
-    got = near(send)
-    lo = keep[:, :QUARTER].astype(F32) + got[:, :QUARTER].astype(F32)
-    hi = keep[:, QUARTER:].astype(F32) + got[:, QUARTER:].astype(F32)
-    return lo, hi.astype(BF16)
-
-
 def far_sum_kernel(own, got, out):
     for to, other in ((LO, HI), (HI, LO)):
         out[:, to] = (own[:, to].astype(F32) + got[:, other].astype(F32)).astype(BF16)
@@ -704,17 +726,18 @@
     my_adapter = jnp.sum(jnp.where(mine, owners, 0))
     info = jnp.stack([me.astype(jnp.int32), my_length, my_adapter, place.astype(jnp.int32)])
 
-    gs = spread(cotangent[0])
-    gains = jnp.stack(spread(jnp.stack([attention_gain, feedfwd_gain])))
-    dealt = lax.all_to_all(
-        move_rows(deal_kernel, residual, dealing_slots, "deal", True), "dp", split_axis=0, concat_axis=1, tiled=True
-    )[0]
+    both = jnp.stack([attention_gain, feedfwd_gain])
+    gs = spread(jnp.concatenate([cotangent[0], both, jnp.zeros((14, QUARTER), BF16)], axis=0))
+    gains = jnp.stack([v[length:length + 2] for v in gs])
+    ordered, = move_rows(deal_kernel, residual, dealing_slots, "deal", [pltpu.VMEM(residual.shape, BF16)], pltpu.HBM,
+                         pltpu.VMEM, (seqs,))
+    dealt = lax.all_to_all(ordered, "dp", split_axis=0, concat_axis=1, tiled=True)[0]
     adapters_here = load_adapters(
         (attention_adapter_input, query_adapter_output, key_value_adapter_output, output_adapter_input,
          output_adapter_output, feedfwd_adapter_input, feedfwd_adapter_output, down_adapter_input,
          down_adapter_output), info)
     a1, qb, kvb, oa, ob, a2, fba, da, bd = adapters_here
-    dealt = late(dealt, gs[2], a1, gains)
+    dealt = late(dealt, gs[2], a1)
     beside = near(dealt)
     there = [far(dealt[c * rows:(c + 1) * rows]) for c in range(CHUNKS)]
     xs = [None] * CHUNKS
@@ -740,8 +763,8 @@
         pairs = [v for p in saved[:c + 1] for v in (p[2], p[5])]
         z_keep, z_send, *kept[c] = call(
             functools.partial(attend_kernel, c), info, (wo,), (saved[c][1], oa, ob, *pairs), outs, like(wo),
-            "attend_%d" % c, 10, (saved[c][0], there[-1]), (1,))
-        z_own[c] = pair_sum(z_keep, late(z_send, z_far[0]) if c else z_send)
+            "attend_%d" % c, 10, (saved[c][0],), (1,))
+        z_own[c] = pair_sum(z_keep, late(z_send, z_far[0] if c else there[-1]))
         z_far[c] = far(z_own[c])
         order = (kept[c][1], z_own[c])
     def front(c, total, partial, order):
@@ -765,10 +788,10 @@
             [(block, F32), ((3 * RANK, QUARTER), F32)], "back_%d" % c, 8, order)
 
     def attend_back(c, total, partial, order):
-        padded = (rows, half + LANES)
-        outs = [(block, F32), (padded, F32), (padded, BF16), (thin, F32), ((3 * RANK, QUARTER), F32 if c else BF16)]
-        outs += ([((4 * RANK, WIDTH), F32), ((kv_cols, rows), F32), ((kv_cols, rows), F32)] if c
-                 else [((4 * RANK, half), F32), ((4 * RANK, half), BF16)])
+        outs = [(block, F32), (col, F32), (col, BF16), (thin, F32), ((3 * RANK, QUARTER), F32 if c else BF16)]
+        low = (4 * RANK + SPARE, half)
+        outs += ([((4 * RANK, WIDTH), F32), ((kv_cols, rows), F32), ((kv_cols, rows), F32), ((SPARE // 2, rows), F32)]
+                 if c else [(low, F32), (low, BF16)])
         scratch = [(wide, BF16), (wide, BF16), ((ROW_BLOCK, WIDTH), F32), ((q_cols, rows), BF16), ((q_cols, rows), F32),
                    ((c + 1, kv_cols, rows), F32), ((c + 1, kv_cols, rows), F32), ((rows, q_cols + 2 * kv_cols), BF16),
                    (block, F32), ((4 * RANK, QUARTER), F32)]
@@ -798,55 +821,55 @@
     d_own[0] = pair_sum(d_keep, late(d_send, fb_more, fb_side))
     d_far[0] = far(d_own[0])
     fb_more_side = swap(fb_more, bits[-1], "dp", dp)
+    y_got = [near(late(v, d_own[0])) for v in y_send]
     dxq, h_keep, h_send, inv, *sums = attend_back(1, total, (), (d_own[0],))
     total = far_sum(d_own[0], late(d_far[0], inv))
-    h_low, h_high = chip_sum(h_keep, late(h_send, fb_more_side))
+    y_high = high_sum(*((y_keep[c], late(y_got[c], inv)) for c in range(CHUNKS)))
+    y_far = far(y_high)
+    h_got = near(late(h_send, fb_more_side))
+    h_high = high_sum((h_keep, h_got))
     h_far = far(h_high)
-    final = [None, (dxq, h_low, h_high, h_far, inv)]
-    y_got = [near(late(v, inv)) for v in y_send]
+    final = [None, (dxq, h_keep, h_got, h_far, inv)]
     fa = total[rows:][None]
     fa_first = swap(fa, bits[0], "dp", dp)
-    dxq, h_keep, h_send, inv, att_b, aa_keep, aa_send = attend_back(0, total, sums, (h_high, *y_got))
-    ready = (fa_first, h_far)
-    aa_low, aa_high = chip_sum(aa_keep, late(aa_send, *ready))
+    dxq, h_keep, h_send, inv, att_b, aa_keep, aa_send = attend_back(0, total, sums, (h_high, y_high))
+    ready = (fa_first, h_far, y_far)
+    aa_got = near(late(aa_send, *ready))
+    aa_high = high_sum((aa_keep, aa_got))
     aa_far = far(aa_high)
-    h_low, h_high = chip_sum(h_keep, late(h_send, *ready))
+    h_got = near(late(h_send, *ready))
+    h_high = high_sum((h_keep, h_got))
     h_far = far(h_high)
-    final[0] = (dxq, h_low, h_high, h_far, inv)
-    y_sums = [k + late(g, h_high).astype(F32) for k, g in zip(y_keep, y_got)]
-    y_far = far(jnp.concatenate([v[:, QUARTER:] for v in y_sums], axis=0).astype(BF16))
-    att = jnp.concatenate([att_b, (aa_low + late(aa_far, h_high).astype(F32)).astype(BF16)], axis=0)[None]
+    final[0] = (dxq, h_keep, h_got, h_far, inv)
+    att_a = aa_keep[:4 * RANK, :QUARTER] + aa_got[:4 * RANK, :QUARTER].astype(F32)
+    att_a = (att_a + late(aa_far, h_high)[:4 * RANK].astype(F32)).astype(BF16)
+    n_b = att_b.shape[0]
+    att = jnp.concatenate([att_b, att_a], axis=0)[None]
     att = doubled(att, bits[0], dp)
-
-    dinput, = call(finish_kernel, None, (), (gains, dealt, *(v for f in final for v in f)), [((length, QUARTER), BF16)],
-                   [], "finish", 8, (att,))
-    back_grad = lax.all_to_all(
-        dinput.reshape(dp, length // dp, QUARTER), "dp", split_axis=0, concat_axis=0, tiled=True)
-    input_grad = move_rows(collect_kernel, back_grad, dealing_slots, "collect_grad", False)
-
-    valid = (jnp.arange(length, dtype=jnp.int32) < my_length)[:, None]
-    result = jnp.concatenate([h[1] + v[:, :QUARTER] for h, v in zip(hidden, y_sums)], axis=0)
-    result = result + late(y_far, dinput).astype(F32)
-    result = jnp.where(valid, result, 0.0).astype(BF16)
-    back_out = lax.all_to_all(
-        result.reshape(dp, length // dp, QUARTER), "dp", split_axis=0, concat_axis=0, tiled=True)
-    output = move_rows(collect_kernel, back_out, late(dealing_slots, input_grad), "collect_out", False)
-
-    fa = late(jnp.concatenate([fa, fa_first], axis=0), h_high)
+    att = late(att, h_far)
+    for bit in bits[1:-1]:
+        att = doubled(att, bit, dp)
+    fa = late(jnp.concatenate([fa, fa_first], axis=0), aa_high)
     for bit in bits[1:-1]:
         fa = doubled(fa, bit, dp)
     fa_side = swap(fa, bits[-1], "dp", dp)
+
+    parts = [v for c in range(CHUNKS) for v in (*final[c], hidden[c][1], y_keep[c], y_got[c])]
+    both, = call(finish_kernel, info, (), (gains, dealt, aa_high, aa_far, y_far, *parts), [((length, half), BF16)], [],
+                 "finish", 12, (att, fa_side))
+    both = lax.all_to_all(both.reshape(dp, length // dp, half), "dp", split_axis=0, concat_axis=0, tiled=True)
+    rows_out = sds((seqs, length // dp, QUARTER), BF16)
+    input_grad, output = move_rows(collect_kernel, both, dealing_slots, "collect", [rows_out, rows_out], pltpu.VMEM,
+                                   pl.ANY, (2, seqs))
+
     outs = [sds((adapters, 2 * RANK, WIDTH), F32), sds((adapters, RANK, WIDTH), F32),
             sds((adapters, 2, RANK, units), F32), sds((adapters, RANK, units), F32)]
     ga_ffn, g_down_b, g_ffn_b, g_down_a = sum_call(
         feedforward_sum_kernel, (info, owners),
         ((fb, fb_more, fb_side, fb_more_side), (fa, fa_side), (near(fa), near(fa_side))), outs, "feedforward_sum")
 
-    n_b = att_b.shape[0]
-    for bit in bits[1:-1]:
-        att = doubled(att, bit, dp)
     att_side = swap(att, bits[-1], "dp", dp)
-    att_side = late(att_side, g_down_a, input_grad)
+    att_side = late(att_side, g_down_a)
     a_parts = [att[:, n_b:], att_side[:, n_b:]]
     a_far = [far(v) for v in a_parts]
     outs = [sds((adapters, 3 * RANK, WIDTH), F32), sds((adapters, RANK, WIDTH), F32),

time: 228 us -> 227 us (level)
  waiting for transfers between devices: 58.7 us -> 72.8 us
  starting transfers between devices: 47 us -> 40 us
  other arithmetic: 8.22 us -> 2.46 us
    ppermute x50 -> x47, waiting for transfers between devices: 58.7 us -> 72.4 us  [swap(): return lax.ppermute(value, axis, [(i, i ^ bit) for i in range(size)])]
    all_to_all x3 -> x2, starting transfers between devices: 15.7 us -> 11 us  [the longest x1 7.26 us: shards(): lax.all_to_all(ordered, 'dp', split_axis=0, concat_axis=1, tiled=True)[0]]
    ppermute x50 -> x47, starting transfers between devices: 31.3 us -> 29 us  [swap(): return lax.ppermute(value, axis, [(i, i ^ bit) for i in range(size)])]
    pallas_call x19 -> x23, Pallas kernels: 84.7 us -> 86.9 us  [call(): pl.pallas_call(body, in_specs=[pl.BlockSpec(memory_space=pltpu.SMEM)] * n...]
    pallas_call x3 -> x2, Pallas kernels: 5.25 us -> 4.1 us  [move_rows(): pl.pallas_call(kernel, in_specs=[pl.BlockSpec(memory_space=pltpu.SMEM), p...]
    unnamed x83 -> x82, local copies, waits for them, and re-layouts: 7.97 us -> 8.87 us
  transfers between devices with their start and end apart: 53 -> 49, of which waited for: 22 -> 24; matrix products, arithmetic and copies ran while one was open for 5% -> 1% of each run, Pallas kernels for 35% -> 36%
where the time goes in v5:
time: 227 us
  Pallas kernels  101 us (44%)
  waiting for transfers between devices  72.8 us (32%)
  starting transfers between devices  40 us (18%)
  local copies, waits for them, and re-layouts  9.08 us (4%)
  other arithmetic  2.46 us (1%)
    pallas_call x23, Pallas kernels, call(): pl.pallas_call(body, in_specs=[pl.BlockSpec(memory_space=pltpu.SMEM)] * n...  86.9 us
    ppermute x47, waiting for transfers between devices, swap(): return lax.ppermute(value, axis, [(i, i ^ bit) for i in range(size)])  72.4 us
    ppermute x47, starting transfers between devices, swap(): return lax.ppermute(value, axis, [(i, i ^ bit) for i in range(size)])  29 us
    unnamed x82, local copies, waits for them, and re-layouts  8.87 us
    pallas_call x2, Pallas kernels, sum_call(): pl.pallas_call(functools.partial(kernel, [len(group) for group in groups]...  7.94 us
    all_to_all x1, starting transfers between devices, shards(): lax.all_to_all(ordered, 'dp', split_axis=0, concat_axis=1, tiled=True)[0]  7.26 us
  transfers between devices with their start and end apart: 49, of which 24 were waited for; matrix products, arithmetic and copies ran while one was open for 1% of the time, Pallas kernels for 36%

profile of v5, /device:TPU:0, one launch (start us, length us, event | category | flops | bytes accessed | tf_op | source)
XLA Modules:
  0.0 226.7 jit_solution(1399972390539502424)
XLA Ops:
  0.7 0.6 copy-done.32
  1.3 2.5 %deal.1 = bf16[8,64,512]{2,1,0:T(8,128)(2,1)} custom-call(s32[8]{0:T(128)S(1)} %copy-done.32, bf16[8,64,512]{2,1,0:T(8,128)(2,1)} %source.1), custom_call_target="tpu_custom_call" | custom-call | flops 1000 | bytes 1000 | tf_op jit(solution)/shard_map/deal/pallas_call | solution.py:584
  3.8 7.3 %all-to-all-start = ((bf16[8,64,512]{2,1,0:T(8,128)(2,1)}), bf16[8,64,512]{2,1,0:T(8,128)(2,1)S(1)}, u32[]{:S(2)}, u32[]{:S(2)}) async-start(bf16[8,64,512]{2,1,0:T(8,128)(2,1)} %deal.1), calls=%async_computation | async-start | bytes 1048576 | tf_op jit(solution)/shard_map/all_to_all | solution.py:734
  11.4 1.6 collective-permute-start.1
  13.8 1.4 pad_add_fusion.info.refs_0_
  15.1 1.8 adapters.1
  19.5 5.7 %collective-permute-done.1.refs_11_.refs_10_ = bf16[528,512]{1,0:T(8,128)(2,1)S(1)} collective-permute-done((bf16[528,512]{1,0:T(8,128)(2,1)S(1)}, bf16[528,512]{1,0:T(8,128)(2,1)S(1)}, u32[]{:S(2)}, u32[]{:S(2)}) %collective-permute-start.1) | collective-permute-done | bytes 540704 | tf_op jit(solution)/shard_map/ppermute | solution.py:656
  25.6 1.6 collective-permute-start.4
  27.8 7.0 %collective-permute-done.4.refs_5_.refs_6_ = bf16[256,512]{1,0:T(8,128)(2,1)S(1)} collective-permute-done((bf16[256,512]{1,0:T(8,128)(2,1)S(1)}, bf16[256,512]{1,0:T(8,128)(2,1)S(1)}, u32[]{:S(2)}, u32[]{:S(2)}) %collective-permute-start.4) | collective-permute-done | bytes 262176 | tf_op jit(solution)/shard_map/ppermute | solution.py:656
  34.9 1.5 collective-permute-done.5.refs_6_.refs_7_
  36.4 0.7 copy-done.17
  37.1 0.8 copy-done.20
  37.8 0.8 copy-done.22
  38.6 0.7 copy-done.25
  39.3 0.7 copy-done.27
  40.0 4.1 %project_0.1 = (bf16[48,256]{1,0:T(8,128)(2,1)S(1)}, bf16[512,256]{1,0:T(8,128)(2,1)S(1)}, bf16[2,256,64]{2,1,0:T(8,128)(2,1)S(1)}, bf16[2,256,64]{2,1,0:T(8,128...) custom-call(s32[4]{0:T(128)S(1)} %copy-done.27, bf16[2048,512]{1,0:T(8,128)(2,1)} %refs_1_.15, ...), custom_call_target="tpu_custom_call" | custom-call | flops 1000 | bytes 1000 | tf_op jit(solution)/shard_map/project_0/pallas_call | solution.py:617
  44.1 3.1 %attend_0.1 = (f32[256,1024]{1,0:T(8,128)S(1)}, bf16[256,1024]{1,0:T(8,128)(2,1)S(1)}, bf16[512,256]{1,0:T(8,128)(2,1)S(1)}, f32[8,256]{1,0:T(8,128)S(1)}, bf16[16,256]{1,0:T(8,128)(2,1)S(1)}) custom-call(s32[4]{0:T(128)S(1)} %copy-done.28, bf16[512,2048]{1,0:T(8,128)(2,1)} %refs_3_.5, bf16[512,256]{1,0:T(8,128)(2,1)S(1)} %get-tuple-element.122.refs_2_.refs_24_, ...), custom_call_target="tpu_custom_call" | custom-call | flops 1000 | bytes 1000 | tf_op jit(solution)/shard_map/attend_0/pallas_call | solution.py:617
  47.4 1.8 collective-permute-done.7.refs_1_
  49.3 1.6 collective-permute-start.8
  50.9 1.5 collective-permute-done.10.refs_6_.refs_7_
  52.4 4.1 %project_1.1 = (bf16[48,256]{1,0:T(8,128)(2,1)S(1)}, bf16[512,256]{1,0:T(8,128)(2,1)S(1)}, bf16[2,256,64]{2,1,0:T(8,128)(2,1)S(1)}, bf16[2,256,64]{2,1,0:T(8,128...) custom-call(s32[4]{0:T(128)S(1)} %copy-done.28, bf16[2048,512]{1,0:T(8,128)(2,1)} %refs_1_.15, ...), custom_call_target="tpu_custom_call" | custom-call | flops 1000 | bytes 1000 | tf_op jit(solution)/shard_map/project_1/pallas_call | solution.py:617
  56.5 3.7 %attend_1.1 = (f32[256,1024]{1,0:T(8,128)S(1)}, bf16[256,1024]{1,0:T(8,128)(2,1)S(1)}, bf16[512,256]{1,0:T(8,128)(2,1)S(1)}, f32[8,256]{1,0:T(8,128)S(1)}, bf16[16,256]{1,0:T(8,128)(2,1)S(1)}) custom-call(s32[4]{0:T(128)S(1)} %copy-done.28, bf16[512,2048]{1,0:T(8,128)(2,1)} %refs_3_.5, bf16[512,256]{1,0:T(8,128)(2,1)S(1)} %get-tuple-element.137.refs_2_.refs_24_, ...), custom_call_target="tpu_custom_call" | custom-call | flops 1000 | bytes 1000 | tf_op jit(solution)/shard_map/attend_1/pallas_call | solution.py:617
  60.3 3.0 %collective-permute-done.8.refs_1_ = bf16[256,1024]{1,0:T(8,128)(2,1)S(1)} collective-permute-done((bf16[256,1024]{1,0:T(8,128)(2,1)S(1)}, bf16[256,1024]{1,0:T(8,128)(2,1)S(1)}, u32[]{:S(2)}, u32[]{:S(2)}) %collective-permute-start.8) | collective-permute-done | bytes 524320 | tf_op jit(solution)/shard_map/ppermute | solution.py:656
  64.1 1.2 collective-permute-done.11.refs_1_
  65.4 1.6 collective-permute-start.12
  67.0 12.9 %front_0.1 = (bf16[256,2048]{1,0:T(8,128)(2,1)S(1)}, f32[256,512]{1,0:T(8,128)S(1)}, bf16[256,2048]{1,0:T(8,128)(2,1)S(1)}, bf16[256,2048]{1,0:T(8,128)(2,1)S(1)...) custom-call(s32[4]{0:T(128)S(1)} %copy-done.28, ...), custom_call_target="tpu_custom_call" | custom-call | flops 1000 | bytes 1000 | tf_op jit(solution)/shard_map/front_0/pallas_call | solution.py:617
  80.1 1.9 collective-permute-done.13.refs_8_
  82.0 12.2 %front_1.1 = (bf16[256,2048]{1,0:T(8,128)(2,1)S(1)}, f32[256,512]{1,0:T(8,128)S(1)}, bf16[256,2048]{1,0:T(8,128)(2,1)S(1)}, bf16[256,2048]{1,0:T(8,128)(2,1)S(1)...) custom-call(s32[4]{0:T(128)S(1)} %copy-done.28, ...), custom_call_target="tpu_custom_call" | custom-call | flops 1000 | bytes 1000 | tf_op jit(solution)/shard_map/front_1/pallas_call | solution.py:617
  94.2 2.2 collective-permute-start.14
  96.4 11.6 %back_1.1 = (f32[256,1024]{1,0:T(8,128)S(1)}, bf16[256,1024]{1,0:T(8,128)(2,1)S(1)}, f32[256,1024]{1,0:T(8,128)S(1)}, bf16[256,1024]{1,0:T(8,128)(2,1)}, f32[48,2048]{1,0:T(8,128)S(1)}) custom-call(s32[4]{0:T(128)S(1)} %copy-done.28, bf16[2,2048,2048]{2,1,0:T(8,128)(2,1)S(1)} %get-tuple-element.146.refs_1_, ...), custom_call_target="tpu_custom_call" | custom-call | flops 1000 | bytes 1000 | tf_op jit(solution)/shard_map/back_1/pallas_call | solution.py:617
  108.1 1.5 collective-permute-start.17
  109.6 1.5 collective-permute-start.16
  111.2 1.1 collective-permute-start.20
  112.3 11.0 %back_0.1 = (f32[304,1024]{1,0:T(8,128)S(1)}, bf16[304,1024]{1,0:T(8,128)(2,1)S(1)}, f32[256,1024]{1,0:T(8,128)S(1)}, bf16[256,1024]{1,0:T(8,128)(2,1)S(1)}) custom-call(s32[4]{0:T(128)S(1)} %copy-done.28, bf16[2,2048,2048]{2,1,0:T(8,128)(2,1)S(1)} %get-tuple-element.146.refs_1_, bf16[2048,2048]{1,0:T(8,128)(2,1)S(1)} %get-tuple-element.147.refs_2_, ...), custom_call_target="tpu_custom_call" | custom-call | flops 1000 | bytes 1000 | tf_op jit(solution)/shard_map/back_0/pallas_call | solution.py:617
  123.4 1.6 collective-permute-done.20.refs_1_
  125.6 1.1 collective-permute-start.19
  127.7 10.7 %attend_back_1.1 = (f32[256,512]{1,0:T(8,128)S(1)}, f32[256,1024]{1,0:T(8,128)S(1)}, bf16[256,1024]{1,0:T(8,128)(2,1)S(1)}, f32[256,1]{1,0:T(8,128)S(1)}, f32[48...) custom-call(s32[4]{0:T(128)S(1)} %copy-done.28, ...), custom_call_target="tpu_custom_call" | custom-call | flops 1000 | bytes 1000 | tf_op jit(solution)/shard_map/attend_back_1/pallas_call | solution.py:617
  138.5 3.4 %collective-permute-done.19.refs_1_ = bf16[304,1024]{1,0:T(8,128)(2,1)S(1)} collective-permute-done((bf16[304,1024]{1,0:T(8,128)(2,1)S(1)}, bf16[304,1024]{1,0:T(8,128)(2,1)S(1)}, u32[]{:S(2)}, u32[]{:S(2)}) %collective-permute-start.19) | collective-permute-done | bytes 622624 | tf_op jit(solution)/shard_map/ppermute | solution.py:656
  142.2 1.1 collective-permute-start.29
  143.4 1.1 collective-permute-start.28
  145.1 9.8 %attend_back_0.1 = (f32[256,512]{1,0:T(8,128)S(1)}, f32[256,1024]{1,0:T(8,128)S(1)}, bf16[256,1024]{1,0:T(8,128)(2,1)S(1)}, f32[256,1]{1,0:T(8,128)S(1)}, bf16[4...) custom-call(s32[4]{0:T(128)S(1)} %copy-done.28, bf16[2048,512]{1,0:T(8,128)(2,1)} %refs_1_.15, ...), custom_call_target="tpu_custom_call" | custom-call | flops 1000 | bytes 1000 | tf_op jit(solution)/shard_map/attend_back_0/pallas_call | solution.py:617
  154.9 2.1 collective-permute-done.29.refs_5_
  157.0 5.2 %collective-permute-done.28.refs_17_ = bf16[256,512]{1,0:T(8,128)(2,1)S(1)} collective-permute-done((bf16[256,512]{1,0:T(8,128)(2,1)S(1)}, bf16[256,512]{1,0:T(8,128)(2,1)S(1)}, u32[]{:S(2)}, u32[]{:S(2)}) %collective-permute-start.28) | collective-permute-done | bytes 262176 | tf_op jit(solution)/shard_map/ppermute | solution.py:656
  162.8 1.7 collective-permute-done.30.refs_1_
  164.4 1.1 collective-permute-start.31
  166.2 1.1 collective-permute-start.33
  167.3 2.9 %collective-permute-done.31.refs_4_ = bf16[96,512]{1,0:T(8,128)(2,1)S(1)} collective-permute-done((bf16[96,512]{1,0:T(8,128)(2,1)S(1)}, bf16[96,512]{1,0:T(8,128)(2,1)S(1)}, u32[]{:S(2)}, u32[]{:S(2)}) %collective-permute-start.31) | collective-permute-done | bytes 98336 | tf_op jit(solution)/shard_map/ppermute | solution.py:656
  170.8 1.4 collective-permute-done.36
  172.2 0.7 collective-permute-start.37
  172.9 4.3 %collective-permute-done.34 = bf16[1,112,512]{2,1,0:T(8,128)(2,1)S(1)} collective-permute-done((bf16[1,112,512]{2,1,0:T(8,128)(2,1)S(1)}, bf16[1,112,512]{2,1,0:T(8,128)(2,1)S(1)}, u32[]{:S(2)}, u32[]{:S(2)}) %collective-permute-start.34) | collective-permute-done | bytes 114720 | tf_op jit(solution)/shard_map/ppermute | solution.py:656
  177.3 7.1 %collective-permute-done.35 = bf16[2,112,512]{2,1,0:T(8,128)(2,1)S(1)} collective-permute-done((bf16[2,112,512]{2,1,0:T(8,128)(2,1)S(1)}, bf16[2,112,512]{2,1,0:T(8,128)(2,1)S(1)}, u32[]{:S(2)}, u32[]{:S(2)}) %collective-permute-start.35) | collective-permute-done | bytes 229408 | tf_op jit(solution)/shard_map/ppermute | solution.py:656
  184.4 2.5 %finish.1 = bf16[512,1024]{1,0:T(8,128)(2,1)} custom-call(s32[4]{0:T(128)S(1)} %copy-done.28, bf16[4,2,512]{2,1,0:T(2,128)(2,1)S(1)} %pad_maximum_fusion.3.refs_7_.refs_13_.refs_15_.refs_1_, bf16[512,512]{1,0:T(8,128)(2,1)S(1)} %bitcast.28, bf16[96,512]{1,0:T(8,128)(2,1)S(1)} %high_sum.6.refs_3_, bf16[96,512]{1,0:T(8,128)(2,1)S(1)} %collective-permute-done.31.refs_4_, ...), custom_call_target="tpu_custom_call" | custom-call | flops 1000 | bytes 1000 | tf_op jit(solution)/shard_map/finish/pallas_call | solution.py:617
  187.0 3.7 %all-to-all-start.1 = ((bf16[8,64,1024]{2,1,0:T(8,128)(2,1)}), bf16[8,64,1024]{2,1,0:T(8,128)(2,1)S(1)}, u32[]{:S(2)}, u32[]{:S(2)}) async-start(bf16[8,64,1024]{2,1,0:T(8,128)(2,1)} %bitcast.13), calls=%async_computation.1 | async-start | bytes 2097152 | tf_op jit(solution)/shard_map/all_to_all | solution.py:860
  190.7 1.9 collective-permute-start.38
  193.1 1.1 collective-permute-start.43
  194.9 1.0 copy-done.13
  195.9 1.0 copy-done.15
  196.9 4.2 %feedforward_sum.1 = (f32[8,32,2048]{2,1,0:T(8,128)}, f32[8,16,2048]{2,1,0:T(8,128)}, f32[8,2,16,2048]{3,2,1,0:T(8,128)}, f32[8,16,2048]{2,1,0:T(8,128)}) custom-call(s32[4]{0:T(128)S(1)} %copy-done.29, s32[8]{0:T(128)S(1)} %copy-done.31, bf16[2,192,512]{2,1,0:T(8,128)(2,1)S(1)} %copy-done.1, bf16[2,192,512]{2,1,0:T(8,128)(2,1)S(1)} %copy-done.13, ...), custom_call_target="tpu_custom_call" | custom-call | bytes 12000000 | tf_op jit(solution)/shard_map/feedforward_sum/pallas_call | solution.py:640
  201.2 12.0 %collective-permute-done.38.refs_1_ = bf16[4,112,512]{2,1,0:T(8,128)(2,1)S(1)} collective-permute-done((bf16[4,112,512]{2,1,0:T(8,128)(2,1)S(1)}, bf16[4,112,512]{2,1,0:T(8,128)(2,1)S(1)}, u32[]{:S(2)}, u32[]{:S(2)}) %collective-permute-start.38) | collective-permute-done | bytes 458784 | tf_op jit(solution)/shard_map/ppermute | solution.py:656
  213.2 1.1 collective-permute-start.44
  214.8 4.8 %collective-permute-done.44.refs_7_ = bf16[4,64,512]{2,1,0:T(8,128)(2,1)S(1)} collective-permute-done((bf16[4,64,512]{2,1,0:T(8,128)(2,1)S(1)}, bf16[4,64,512]{2,1,0:T(8,128)(2,1)S(1)}, u32[]{:S(2)}, u32[]{:S(2)}) %collective-permute-start.44) | collective-permute-done | bytes 262176 | tf_op jit(solution)/shard_map/ppermute | solution.py:656
  219.6 1.5 collective-permute-done.46.refs_9_
  221.1 3.7 %attention_sum.1 = (f32[8,48,2048]{2,1,0:T(8,128)}, f32[8,16,2048]{2,1,0:T(8,128)}, f32[8,16,512]{2,1,0:T(8,128)}, f32[8,2,16,128]{3,2,1,0:T(8,128)}, f32[8,16,512]{2,1,0:T(8,128)}) custom-call(s32[4]{0:T(128)S(1)} %copy-done.29, s32[8]{0:T(128)S(1)} %copy-done.31, bf16[4,112,512]{2,1,0:T(8,128)(2,1)S(1)} %constant_dynamic-update-slice_fusion.refs_22_.refs_0_, ...), custom_call_target="tpu_custom_call" | custom-call | bytes 12000000 | tf_op jit(solution)/shard_map/attention_sum/pallas_call | solution.py:640
  224.9 1.6 collect.1
  (168 shorter events, 12.8 us)
Async XLA Ops:
  1.3 9.8 %copy-start.36 = (bf16[512]{0:T(512)(128)(2,1)S(1)}, bf16[512]{0:T(512)(128)(2,1)}, u32[]{:S(2)}) copy-start(bf16[512]{0:T(512)(128)(2,1)} %param.26) | copy-start | bytes 3076
  1.3 9.8 %copy-start.37 = (bf16[512]{0:T(512)(128)(2,1)S(1)}, bf16[512]{0:T(512)(128)(2,1)}, u32[]{:S(2)}) copy-start(bf16[512]{0:T(512)(128)(2,1)} %param.30) | copy-start | bytes 3076
  1.3 9.9 %copy-start.35 = (bf16[1,512,512]{2,1,0:T(8,128)(2,1)S(1)}, bf16[1,512,512]{2,1,0:T(8,128)(2,1)}, u32[]{:S(2)}) copy-start(bf16[1,512,512]{2,1,0:T(8,128)(2,1)} %param.45) | copy-start | bytes 1572868
  1.3 11.7 %copy-start.33 = (s32[8]{0:T(128)S(1)}, s32[8]{0:T(128)}, u32[]{:S(2)}) copy-start(s32[8]{0:T(128)} %slots.3) | copy-start | bytes 100
  1.3 11.7 %copy-start.38 = (s32[8]{0:T(128)S(1)}, s32[8]{0:T(128)}, u32[]{:S(2)}) copy-start(s32[8]{0:T(128)} %param.42) | copy-start | bytes 100
  1.3 11.6 %copy-start.39 = (s32[8]{0:T(128)S(1)}, s32[8]{0:T(128)}, u32[]{:S(2)}) copy-start(s32[8]{0:T(128)} %param.43) | copy-start | bytes 100
  3.8 21.8 %all-to-all-start = ((bf16[8,64,512]{2,1,0:T(8,128)(2,1)}), bf16[8,64,512]{2,1,0:T(8,128)(2,1)S(1)}, u32[]{:S(2)}, u32[]{:S(2)}) async-start(bf16[8,64,512]{2,1,0:T(8,128)(2,1)} %deal.1), calls=%async_computation | async-start | bytes 1048576 | tf_op jit(solution)/shard_map/all_to_all | solution.py:734
  11.4 13.8 %collective-permute-start.1 = (bf16[528,512]{1,0:T(8,128)(2,1)S(1)}, bf16[528,512]{1,0:T(8,128)(2,1)S(1)}, u32[]{:S(2)}, u32[]{:S(2)}) collective-permute-start(bf16[528,512]{1,0:T(8,128)(2,1)S(1)} %maximum_maximum_fusion.refs_9_.refs_8_), channel_id=1, source_target_pairs={{0,2},{1,3},{2,0},{3,1},{4,6},{5,7},{6,4},{7,5},{8,10},{9,11},{10,... | collective-permute-start | bytes 1622024 | tf_op jit(solution)/shard_map/ppermute | solution.py:656
  13.0 14.2 %collective-permute-start = (bf16[528,512]{1,0:T(8,128)(2,1)S(1)}, bf16[528,512]{1,0:T(8,128)(2,1)S(1)}, u32[]{:S(2)}, u32[]{:S(2)}) collective-permute-start(bf16[528,512]{1,0:T(8,128)(2,1)S(1)} %maximum_maximum_fusion.refs_9_.refs_8_), channel_id=1, source_target_pairs={{0,1},{1,0},{2,3},{3,2},{4,5},{5,4},{6,7},{7,6},{8,9},{9,8},{10,11... | collective-permute-start | bytes 1622024 | tf_op jit(solution)/shard_map/ppermute | solution.py:656
  19.5 16.9 %copy-start.24 = (bf16[2,16,128]{2,1,0:T(8,128)(2,1)}, bf16[2,16,128]{2,1,0:T(8,128)(2,1)S(1)}, u32[]{:S(2)}) copy-start(bf16[2,16,128]{2,1,0:T(8,128)(2,1)S(1)} %get-tuple-element.121.refs_10_.refs_18_) | copy-start | bytes 24580
  25.2 9.7 %collective-permute-start.2 = (bf16[528,512]{1,0:T(8,128)(2,1)S(1)}, bf16[528,512]{1,0:T(8,128)(2,1)S(1)}, u32[]{:S(2)}, u32[]{:S(2)}) collective-permute-start(bf16[528,512]{1,0:T(8,128)(2,1)S(1)} %collective-permute-done.1.refs_11_.refs_10_), channel_id=1, source_target_pairs={{0,1},{1,0},{2,3},{3,2},{4,5},{5,4},{6,7},{7,6},{8,9},{9,8},{10,11... | collective-permute-start | bytes 1622024 | tf_op jit(solution)/shard_map/ppermute | solution.py:656
  25.6 9.2 %collective-permute-start.4 = (bf16[256,512]{1,0:T(8,128)(2,1)S(1)}, bf16[256,512]{1,0:T(8,128)(2,1)S(1)}, u32[]{:S(2)}, u32[]{:S(2)}) collective-permute-start(bf16[256,512]{1,0:T(8,128)(2,1)S(1)} %get-tuple-element.228), channel_id=1, source_target_pairs={{0,2},{1,3},{2,0},{3,1},{4,6},{5,7},{6,4},{7,5},{8,10},{9,11},{10,... | collective-permute-start | bytes 786440 | tf_op jit(solution)/shard_map/ppermute | solution.py:656
  27.2 9.2 %collective-permute-start.3 = (bf16[512,512]{1,0:T(8,128)(2,1)S(1)}, bf16[512,512]{1,0:T(8,128)(2,1)S(1)}, u32[]{:S(2)}, u32[]{:S(2)}) collective-permute-start(bf16[512,512]{1,0:T(8,128)(2,1)S(1)} %bitcast.21), channel_id=1, source_target_pairs={{0,1},{1,0},{2,3},{3,2},{4,5},{5,4},{6,7},{7,6},{8,9},{9,8},{10,11... | collective-permute-start | bytes 1572872 | tf_op jit(solution)/shard_map/ppermute | solution.py:656
  27.2 20.0 %collective-permute-start.6 = (bf16[256,512]{1,0:T(8,128)(2,1)S(1)}, bf16[256,512]{1,0:T(8,128)(2,1)S(1)}, u32[]{:S(2)}, u32[]{:S(2)}) collective-permute-start(bf16[256,512]{1,0:T(8,128)(2,1)S(1)} %get-tuple-element.227), channel_id=1, source_target_pairs={{0,2},{1,3},{2,0},{3,1},{4,6},{5,7},{6,4},{7,5},{8,10},{9,11},{10,... | collective-permute-start | bytes 786440 | tf_op jit(solution)/shard_map/ppermute | solution.py:656
  34.8 1.5 collective-permute-start.5
  44.1 8.3 %copy-start.18 = (f32[32,256]{1,0:T(8,128)S(1)}, f32[32,256]{1,0:T(8,128)}, u32[]{:S(2)}) copy-start(f32[32,256]{1,0:T(8,128)} %constant.24.clone.refs_12_.refs_22_) | copy-start | bytes 98308
  44.1 8.3 %copy-start.19 = (f32[32,256]{1,0:T(8,128)S(1)}, f32[32,256]{1,0:T(8,128)}, u32[]{:S(2)}) copy-start(f32[32,256]{1,0:T(8,128)} %constant.22.clone.refs_11_.refs_21_) | copy-start | bytes 98308
  47.2 2.0 collective-permute-start.7
  49.3 14.0 %collective-permute-start.8 = (bf16[256,1024]{1,0:T(8,128)(2,1)S(1)}, bf16[256,1024]{1,0:T(8,128)(2,1)S(1)}, u32[]{:S(2)}, u32[]{:S(2)}) collective-permute-start(bf16[256,1024]{1,0:T(8,128)(2,1)S(1)} %pair_sum.4.refs_0_.refs_14_), channel_id=1, source_target_pairs={{0,2},{1,3},{2,0},{3,1},{4,6},{5,7},{6,4},{7,5},{8,10},{9,11},{10,... | collective-permute-start | bytes 1572872 | tf_op jit(solution)/shard_map/ppermute | solution.py:656
  50.9 1.5 collective-permute-start.10
  63.3 1.9 collective-permute-start.11
  63.5 3.5 %collective-permute-start.9 = (bf16[256,1024]{1,0:T(8,128)(2,1)S(1)}, bf16[256,1024]{1,0:T(8,128)(2,1)S(1)}, u32[]{:S(2)}, u32[]{:S(2)}) collective-permute-start(bf16[256,1024]{1,0:T(8,128)(2,1)S(1)} %far_sum.4.refs_7_), channel_id=1, source_target_pairs={{0,1},{1,0},{2,3},{3,2},{4,5},{5,4},{6,7},{7,6},{8,9},{9,8},{10,11... | collective-permute-start | bytes 1572872 | tf_op jit(solution)/shard_map/ppermute | solution.py:656
  65.4 14.5 %collective-permute-start.12 = (bf16[256,1024]{1,0:T(8,128)(2,1)S(1)}, bf16[256,1024]{1,0:T(8,128)(2,1)S(1)}, u32[]{:S(2)}, u32[]{:S(2)}) collective-permute-start(bf16[256,1024]{1,0:T(8,128)(2,1)S(1)} %pair_sum.5.refs_19_.refs_0_), channel_id=1, source_target_pairs={{0,2},{1,3},{2,0},{3,1},{4,6},{5,7},{6,4},{7,5},{8,10},{9,11},{10,... | collective-permute-start | bytes 1572872 | tf_op jit(solution)/shard_map/ppermute | solution.py:656
  79.9 14.3 %copy-start.8 = (bf16[256,2048]{1,0:T(8,128)(2,1)}, bf16[256,2048]{1,0:T(8,128)(2,1)S(1)}, u32[]{:S(2)}) copy-start(bf16[256,2048]{1,0:T(8,128)(2,1)S(1)} %get-tuple-element.152.refs_7_) | copy-start | bytes 3145732
  80.0 2.0 collective-permute-start.13
  94.2 13.8 %collective-permute-start.14 = (bf16[1,192,512]{2,1,0:T(8,128)(2,1)S(1)}, bf16[1,192,512]{2,1,0:T(8,128)(2,1)S(1)}, u32[]{:S(2)}, u32[]{:S(2)}) collective-permute-start(bf16[1,192,512]{2,1,0:T(8,128)(2,1)S(1)} %bitcast.29), channel_id=1, source_target_pairs={{0,16},{4,20},{8,24},{12,28},{16,0},{20,4},{24,8},{28,12},{1,17},{... | collective-permute-start | bytes 589832 | tf_op jit(solution)/shard_map/ppermute | solution.py:656
  108.0 3.0 %collective-permute-start.15 = (bf16[256,1024]{1,0:T(8,128)(2,1)S(1)}, bf16[256,1024]{1,0:T(8,128)(2,1)S(1)}, u32[]{:S(2)}, u32[]{:S(2)}) collective-permute-start(bf16[256,1024]{1,0:T(8,128)(2,1)S(1)} %get-tuple-element.166), channel_id=1, source_target_pairs={{0,1},{1,0},{2,3},{3,2},{4,5},{5,4},{6,7},{7,6},{8,9},{9,8},{10,11... | collective-permute-start | bytes 1572872 | tf_op jit(solution)/shard_map/ppermute | solution.py:656
  108.1 15.2 %copy-start = (bf16[2,192,512]{2,1,0:T(8,128)(2,1)}, bf16[2,192,512]{2,1,0:T(8,128)(2,1)S(1)}, u32[]{:S(2)}) copy-start(bf16[2,192,512]{2,1,0:T(8,128)(2,1)S(1)} %pad_maximum_fusion.refs_0_) | copy-start | bytes 1179652
  108.1 15.2 %collective-permute-start.17 = (bf16[2,192,512]{2,1,0:T(8,128)(2,1)S(1)}, bf16[2,192,512]{2,1,0:T(8,128)(2,1)S(1)}, u32[]{:S(2)}, u32[]{:S(2)}) collective-permute-start(bf16[2,192,512]{2,1,0:T(8,128)(2,1)S(1)} %pad_maximum_fusion.refs_0_), channel_id=1, source_target_pairs={{0,4},{4,0},{8,12},{12,8},{16,20},{20,16},{24,28},{28,24},{1,5},{5... | collective-permute-start | bytes 1179656 | tf_op jit(solution)/shard_map/ppermute | solution.py:656
  109.6 13.7 %collective-permute-start.16 = (bf16[2,192,512]{2,1,0:T(8,128)(2,1)S(1)}, bf16[2,192,512]{2,1,0:T(8,128)(2,1)S(1)}, u32[]{:S(2)}, u32[]{:S(2)}) collective-permute-start(bf16[2,192,512]{2,1,0:T(8,128)(2,1)S(1)} %pad_maximum_fusion.refs_0_), channel_id=1, source_target_pairs={{0,8},{4,12},{8,0},{12,4},{16,24},{20,28},{24,16},{28,20},{1,9},{5... | collective-permute-start | bytes 1179656 | tf_op jit(solution)/shard_map/ppermute | solution.py:656
  111.2 13.8 %collective-permute-start.20 = (bf16[256,1024]{1,0:T(8,128)(2,1)S(1)}, bf16[256,1024]{1,0:T(8,128)(2,1)S(1)}, u32[]{:S(2)}, u32[]{:S(2)}) collective-permute-start(bf16[256,1024]{1,0:T(8,128)(2,1)S(1)} %pair_sum.6.refs_13_.refs_0_), channel_id=1, source_target_pairs={{0,2},{1,3},{2,0},{3,1},{4,6},{5,7},{6,4},{7,5},{8,10},{9,11},{10,... | collective-permute-start | bytes 1572872 | tf_op jit(solution)/shard_map/ppermute | solution.py:656
  123.3 15.1 %copy-start.10 = (bf16[2,192,512]{2,1,0:T(8,128)(2,1)}, bf16[2,192,512]{2,1,0:T(8,128)(2,1)S(1)}, u32[]{:S(2)}) copy-start(bf16[2,192,512]{2,1,0:T(8,128)(2,1)S(1)} %collective-permute-done.17.refs_2_) | copy-start | bytes 1179652
  123.3 15.0 %copy-start.12 = (bf16[2,192,512]{2,1,0:T(8,128)(2,1)}, bf16[2,192,512]{2,1,0:T(8,128)(2,1)S(1)}, u32[]{:S(2)}) copy-start(bf16[2,192,512]{2,1,0:T(8,128)(2,1)S(1)} %collective-permute-done.16.refs_1_) | copy-start | bytes 1179652
  123.4 2.1 collective-permute-start.18
  125.2 2.5 %collective-permute-start.21 = (bf16[256,1024]{1,0:T(8,128)(2,1)S(1)}, bf16[256,1024]{1,0:T(8,128)(2,1)S(1)}, u32[]{:S(2)}, u32[]{:S(2)}) collective-permute-start(bf16[256,1024]{1,0:T(8,128)(2,1)S(1)} %far_sum.6.refs_13_), channel_id=1, source_target_pairs={{0,1},{1,0},{2,3},{3,2},{4,5},{5,4},{6,7},{7,6},{8,9},{9,8},{10,11... | collective-permute-start | bytes 1572872 | tf_op jit(solution)/shard_map/ppermute | solution.py:656
  125.6 16.3 %collective-permute-start.19 = (bf16[304,1024]{1,0:T(8,128)(2,1)S(1)}, bf16[304,1024]{1,0:T(8,128)(2,1)S(1)}, u32[]{:S(2)}, u32[]{:S(2)}) collective-permute-start(bf16[304,1024]{1,0:T(8,128)(2,1)S(1)} %pair_sum.7.refs_34_.refs_0_), channel_id=1, source_target_pairs={{0,2},{1,3},{2,0},{3,1},{4,6},{5,7},{6,4},{7,5},{8,10},{9,11},{10,... | collective-permute-start | bytes 1867784 | tf_op jit(solution)/shard_map/ppermute | solution.py:656
  126.6 11.8 %collective-permute-start.23 = (bf16[2,192,512]{2,1,0:T(8,128)(2,1)S(1)}, bf16[2,192,512]{2,1,0:T(8,128)(2,1)S(1)}, u32[]{:S(2)}, u32[]{:S(2)}) collective-permute-start(bf16[2,192,512]{2,1,0:T(8,128)(2,1)S(1)} %collective-permute-done.16.refs_1_), channel_id=1, source_target_pairs={{0,4},{4,0},{8,12},{12,8},{16,20},{20,16},{24,28},{28,24},{1,5},{5... | collective-permute-start | bytes 1179656 | tf_op jit(solution)/shard_map/ppermute | solution.py:656
  127.2 14.9 %collective-permute-start.25 = (bf16[256,1024]{1,0:T(8,128)(2,1)S(1)}, bf16[256,1024]{1,0:T(8,128)(2,1)S(1)}, u32[]{:S(2)}, u32[]{:S(2)}) collective-permute-start(bf16[256,1024]{1,0:T(8,128)(2,1)S(1)} %get-tuple-element.192), channel_id=1, source_target_pairs={{0,1},{1,0},{2,3},{3,2},{4,5},{5,4},{6,7},{7,6},{8,9},{9,8},{10,11... | collective-permute-start | bytes 1572872 | tf_op jit(solution)/shard_map/ppermute | solution.py:656
  127.2 14.9 %collective-permute-start.26 = (bf16[256,1024]{1,0:T(8,128)(2,1)}, bf16[256,1024]{1,0:T(8,128)(2,1)S(1)}, u32[]{:S(2)}, u32[]{:S(2)}) collective-permute-start(bf16[256,1024]{1,0:T(8,128)(2,1)} %get-tuple-element.196), channel_id=1, source_target_pairs={{0,1},{1,0},{2,3},{3,2},{4,5},{5,4},{6,7},{7,6},{8,9},{9,8},{10,11... | collective-permute-start | bytes 1572872 | tf_op jit(solution)/shard_map/ppermute | solution.py:656
  138.4 4.9 %collective-permute-start.24 = (bf16[256,1024]{1,0:T(8,128)(2,1)S(1)}, bf16[256,1024]{1,0:T(8,128)(2,1)S(1)}, u32[]{:S(2)}, u32[]{:S(2)}) collective-permute-start(bf16[256,1024]{1,0:T(8,128)(2,1)S(1)} %get-tuple-element.189), channel_id=1, source_target_pairs={{0,1},{1,0},{2,3},{3,2},{4,5},{5,4},{6,7},{7,6},{8,9},{9,8},{10,11... | collective-permute-start | bytes 1572872 | tf_op jit(solution)/shard_map/ppermute | solution.py:656
  142.0 3.1 %collective-permute-start.22 = (bf16[304,1024]{1,0:T(8,128)(2,1)S(1)}, bf16[304,1024]{1,0:T(8,128)(2,1)S(1)}, u32[]{:S(2)}, u32[]{:S(2)}) collective-permute-start(bf16[304,1024]{1,0:T(8,128)(2,1)S(1)} %far_sum.7.refs_13_), channel_id=1, source_target_pairs={{0,1},{1,0},{2,3},{3,2},{4,5},{5,4},{6,7},{7,6},{8,9},{9,8},{10,11... | collective-permute-start | bytes 1867784 | tf_op jit(solution)/shard_map/ppermute | solution.py:656
  142.2 14.8 %collective-permute-start.29 = (bf16[512,512]{1,0:T(8,128)(2,1)S(1)}, bf16[512,512]{1,0:T(8,128)(2,1)S(1)}, u32[]{:S(2)}, u32[]{:S(2)}) collective-permute-start(bf16[512,512]{1,0:T(8,128)(2,1)S(1)} %high_sum.5.refs_37_), channel_id=1, source_target_pairs={{0,2},{1,3},{2,0},{3,1},{4,6},{5,7},{6,4},{7,5},{8,10},{9,11},{10,... | collective-permute-start | bytes 1572872 | tf_op jit(solution)/shard_map/ppermute | solution.py:656
  143.4 18.8 %collective-permute-start.28 = (bf16[256,512]{1,0:T(8,128)(2,1)S(1)}, bf16[256,512]{1,0:T(8,128)(2,1)S(1)}, u32[]{:S(2)}, u32[]{:S(2)}) collective-permute-start(bf16[256,512]{1,0:T(8,128)(2,1)S(1)} %high_sum.4.refs_36_), channel_id=1, source_target_pairs={{0,2},{1,3},{2,0},{3,1},{4,6},{5,7},{6,4},{7,5},{8,10},{9,11},{10,... | collective-permute-start | bytes 786440 | tf_op jit(solution)/shard_map/ppermute | solution.py:656
  144.5 10.4 %collective-permute-start.27 = (bf16[1,48,1024]{2,1,0:T(8,128)(2,1)S(1)}, bf16[1,48,1024]{2,1,0:T(8,128)(2,1)S(1)}, u32[]{:S(2)}, u32[]{:S(2)}) collective-permute-start(bf16[1,48,1024]{2,1,0:T(8,128)(2,1)S(1)} %slice_bitcast_fusion), channel_id=1, source_target_pairs={{0,16},{4,20},{8,24},{12,28},{16,0},{20,4},{24,8},{28,12},{1,17},{... | collective-permute-start | bytes 294920 | tf_op jit(solution)/shard_map/ppermute | solution.py:656
  162.2 3.9 %collective-permute-start.32 = (bf16[256,1024]{1,0:T(8,128)(2,1)S(1)}, bf16[256,1024]{1,0:T(8,128)(2,1)S(1)}, u32[]{:S(2)}, u32[]{:S(2)}) collective-permute-start(bf16[256,1024]{1,0:T(8,128)(2,1)S(1)} %get-tuple-element.204), channel_id=1, source_target_pairs={{0,1},{1,0},{2,3},{3,2},{4,5},{5,4},{6,7},{7,6},{8,9},{9,8},{10,11... | collective-permute-start | bytes 1572872 | tf_op jit(solution)/shard_map/ppermute | solution.py:656
  162.2 2.2 collective-permute-start.30
  164.4 5.7 %collective-permute-start.31 = (bf16[96,512]{1,0:T(8,128)(2,1)S(1)}, bf16[96,512]{1,0:T(8,128)(2,1)S(1)}, u32[]{:S(2)}, u32[]{:S(2)}) collective-permute-start(bf16[96,512]{1,0:T(8,128)(2,1)S(1)} %high_sum.6.refs_3_), channel_id=1, source_target_pairs={{0,2},{1,3},{2,0},{3,1},{4,6},{5,7},{6,4},{7,5},{8,10},{9,11},{10,... | collective-permute-start | bytes 294920 | tf_op jit(solution)/shard_map/ppermute | solution.py:656
  165.6 6.7 %collective-permute-start.36 = (bf16[2,48,1024]{2,1,0:T(8,128)(2,1)S(1)}, bf16[2,48,1024]{2,1,0:T(8,128)(2,1)S(1)}, u32[]{:S(2)}, u32[]{:S(2)}) collective-permute-start(bf16[2,48,1024]{2,1,0:T(8,128)(2,1)S(1)} %pad_maximum_fusion.2), channel_id=1, source_target_pairs={{0,8},{4,12},{8,0},{12,4},{16,24},{20,28},{24,16},{28,20},{1,9},{5... | collective-permute-start | bytes 589832 | tf_op jit(solution)/shard_map/ppermute | solution.py:656
  166.2 11.0 %collective-permute-start.33 = (bf16[256,512]{1,0:T(8,128)(2,1)S(1)}, bf16[256,512]{1,0:T(8,128)(2,1)S(1)}, u32[]{:S(2)}, u32[]{:S(2)}) collective-permute-start(bf16[256,512]{1,0:T(8,128)(2,1)S(1)} %high_sum.7), channel_id=1, source_target_pairs={{0,2},{1,3},{2,0},{3,1},{4,6},{5,7},{6,4},{7,5},{8,10},{9,11},{10,... | collective-permute-start | bytes 786440 | tf_op jit(solution)/shard_map/ppermute | solution.py:656
  170.2 7.0 %collective-permute-start.34 = (bf16[1,112,512]{2,1,0:T(8,128)(2,1)S(1)}, bf16[1,112,512]{2,1,0:T(8,128)(2,1)S(1)}, u32[]{:S(2)}, u32[]{:S(2)}) collective-permute-start(bf16[1,112,512]{2,1,0:T(8,128)(2,1)S(1)} %maximum_bitcast_fusion), channel_id=1, source_target_pairs={{0,16},{4,20},{8,24},{12,28},{16,0},{20,4},{24,8},{28,12},{1,17},{... | collective-permute-start | bytes 344072 | tf_op jit(solution)/shard_map/ppermute | solution.py:656
  172.2 12.2 %collective-permute-start.37 = (bf16[4,48,1024]{2,1,0:T(8,128)(2,1)S(1)}, bf16[4,48,1024]{2,1,0:T(8,128)(2,1)S(1)}, u32[]{:S(2)}, u32[]{:S(2)}) collective-permute-start(bf16[4,48,1024]{2,1,0:T(8,128)(2,1)S(1)} %constant_dynamic-update-slice_fusion.2.refs_4_), channel_id=1, source_target_pairs={{0,4},{4,0},{8,12},{12,8},{16,20},{20,16},{24,28},{28,24},{1,5},{5... | collective-permute-start | bytes 1179656 | tf_op jit(solution)/shard_map/ppermute | solution.py:656
  177.2 7.2 %collective-permute-start.35 = (bf16[2,112,512]{2,1,0:T(8,128)(2,1)S(1)}, bf16[2,112,512]{2,1,0:T(8,128)(2,1)S(1)}, u32[]{:S(2)}, u32[]{:S(2)}) collective-permute-start(bf16[2,112,512]{2,1,0:T(8,128)(2,1)S(1)} %pad_maximum_fusion.1), channel_id=1, source_target_pairs={{0,8},{4,12},{8,0},{12,4},{16,24},{20,28},{24,16},{28,20},{1,9},{5... | collective-permute-start | bytes 688136 | tf_op jit(solution)/shard_map/ppermute | solution.py:656
  187.0 7.9 %copy-start.31 = (s32[8]{0:T(128)S(1)}, s32[8]{0:T(128)}, u32[]{:S(2)}) copy-start(s32[8]{0:T(128)} %copy-done.30) | copy-start | bytes 100
  187.0 37.9 %all-to-all-start.1 = ((bf16[8,64,1024]{2,1,0:T(8,128)(2,1)}), bf16[8,64,1024]{2,1,0:T(8,128)(2,1)S(1)}, u32[]{:S(2)}, u32[]{:S(2)}) async-start(bf16[8,64,1024]{2,1,0:T(8,128)(2,1)} %bitcast.13), calls=%async_computation.1 | async-start | bytes 2097152 | tf_op jit(solution)/shard_map/all_to_all | solution.py:860
  190.7 22.5 %collective-permute-start.38 = (bf16[4,112,512]{2,1,0:T(8,128)(2,1)S(1)}, bf16[4,112,512]{2,1,0:T(8,128)(2,1)S(1)}, u32[]{:S(2)}, u32[]{:S(2)}) collective-permute-start(bf16[4,112,512]{2,1,0:T(8,128)(2,1)S(1)} %constant_dynamic-update-slice_fusion.refs_22_.refs_0_), channel_id=1, source_target_pairs={{0,4},{4,0},{8,12},{12,8},{16,20},{20,16},{24,28},{28,24},{1,5},{5... | collective-permute-start | bytes 1376264 | tf_op jit(solution)/shard_map/ppermute | solution.py:656
  192.6 1.7 collective-permute-start.39
  192.6 2.3 %collective-permute-start.40 = (bf16[4,48,1024]{2,1,0:T(8,128)(2,1)S(1)}, bf16[4,48,1024]{2,1,0:T(8,128)(2,1)S(1)}, u32[]{:S(2)}, u32[]{:S(2)}) collective-permute-start(bf16[4,48,1024]{2,1,0:T(8,128)(2,1)S(1)} %collective-permute-done.37.refs_23_.refs_5_), channel_id=1, source_target_pairs={{0,1},{1,0},{2,3},{3,2},{4,5},{5,4},{6,7},{7,6},{8,9},{9,8},{10,11... | collective-permute-start | bytes 1179656 | tf_op jit(solution)/shard_map/ppermute | solution.py:656
  193.1 21.1 %collective-permute-start.43 = (bf16[4,64,512]{2,1,0:T(8,128)(2,1)S(1)}, bf16[4,64,512]{2,1,0:T(8,128)(2,1)S(1)}, u32[]{:S(2)}, u32[]{:S(2)}) collective-permute-start(bf16[4,64,512]{2,1,0:T(8,128)(2,1)S(1)} %slice.49.refs_2_), channel_id=1, source_target_pairs={{0,2},{1,3},{2,0},{3,1},{4,6},{5,7},{6,4},{7,5},{8,10},{9,11},{10,... | collective-permute-start | bytes 786440 | tf_op jit(solution)/shard_map/ppermute | solution.py:656
  201.1 23.7 %copy-start.34 = (s32[8]{0:T(128)S(1)}, s32[8]{0:T(128)}, u32[]{:S(2)}) copy-start(s32[8]{0:T(128)} %slots.3) | copy-start | bytes 100
  213.2 6.4 %collective-permute-start.44 = (bf16[4,64,512]{2,1,0:T(8,128)(2,1)S(1)}, bf16[4,64,512]{2,1,0:T(8,128)(2,1)S(1)}, u32[]{:S(2)}, u32[]{:S(2)}) collective-permute-start(bf16[4,64,512]{2,1,0:T(8,128)(2,1)S(1)} %slice.43.refs_3_), channel_id=1, source_target_pairs={{0,2},{1,3},{2,0},{3,1},{4,6},{5,7},{6,4},{7,5},{8,10},{9,11},{10,... | collective-permute-start | bytes 786440 | tf_op jit(solution)/shard_map/ppermute | solution.py:656
  214.3 5.3 %collective-permute-start.41 = (bf16[4,64,512]{2,1,0:T(8,128)(2,1)S(1)}, bf16[4,64,512]{2,1,0:T(8,128)(2,1)S(1)}, u32[]{:S(2)}, u32[]{:S(2)}) collective-permute-start(bf16[4,64,512]{2,1,0:T(8,128)(2,1)S(1)} %slice.49.refs_2_), channel_id=1, source_target_pairs={{0,1},{1,0},{2,3},{3,2},{4,5},{5,4},{6,7},{7,6},{8,9},{9,8},{10,11... | collective-permute-start | bytes 786440 | tf_op jit(solution)/shard_map/ppermute | solution.py:656
  214.3 5.3 %collective-permute-start.45 = (bf16[4,64,512]{2,1,0:T(8,128)(2,1)S(1)}, bf16[4,64,512]{2,1,0:T(8,128)(2,1)S(1)}, u32[]{:S(2)}, u32[]{:S(2)}) collective-permute-start(bf16[4,64,512]{2,1,0:T(8,128)(2,1)S(1)} %collective-permute-done.43.refs_6_), channel_id=1, source_target_pairs={{0,1},{1,0},{2,3},{3,2},{4,5},{5,4},{6,7},{7,6},{8,9},{9,8},{10,11... | collective-permute-start | bytes 786440 | tf_op jit(solution)/shard_map/ppermute | solution.py:656
  214.8 4.8 %collective-permute-start.42 = (bf16[4,64,512]{2,1,0:T(8,128)(2,1)S(1)}, bf16[4,64,512]{2,1,0:T(8,128)(2,1)S(1)}, u32[]{:S(2)}, u32[]{:S(2)}) collective-permute-start(bf16[4,64,512]{2,1,0:T(8,128)(2,1)S(1)} %slice.43.refs_3_), channel_id=1, source_target_pairs={{0,1},{1,0},{2,3},{3,2},{4,5},{5,4},{6,7},{7,6},{8,9},{9,8},{10,11... | collective-permute-start | bytes 786440 | tf_op jit(solution)/shard_map/ppermute | solution.py:656
  219.6 1.5 collective-permute-start.46
  (25 other events, 73.8 us)

commit v6 on v5

--- a/solution.py
+++ b/solution.py
@@ -195,9 +195,10 @@
     units = wd_in.shape[0]
     if chunk:
         wgu, wd = wgu_in, wd_in
+        outs, (f_s, value_s) = rest[-15:-2], rest[-2:]
     else:
-        (wgu, wd, f_s, sems), rest = rest[-4:], rest[:-4]
-        rest = (*rest, f_s)
+        outs, (wgu, wd, f_s, value_s, sems) = rest[-18:-5], rest[-5:]
+    xm_out, xq_out, h_out, g_out, act_out, dg_out, du_out, t2_s, dtd_s, b_out, y_keep, y_send, td_out = outs
 
     def copies(i):
         c = pl.ds(pl.multiple_of(i * QUARTER, QUARTER), QUARTER)
@@ -208,8 +209,6 @@
         for i in range(units // QUARTER):
             for copy in copies(i):
                 copy.start()
-    f_s = rest[-1]
-    xm_out, xq_out, h_out, g_out, act_out, dg_out, du_out, t2_s, dtd_s, b_out = rest[-11:-1]
     me, length = info[0], info[1]
     rows = h_out.shape[0]
     xs, gs = ([chunk_of(v, chunk, rows) for v in vs] for vs in ((x0, x1, x2, x3), (g0, g1, g2, g3)))
@@ -262,35 +261,40 @@
         return carry
 
     lax.fori_loop(0, units // QUARTER, block, 0)
-
-
-def back_kernel(last, info, wgu, wd, h, g, act, dg, du, a2, bd, fb, da, *rest):
+    td = nt(act_out[...], da[...])
+    td_out[...] = td
+    tdb = td.astype(BF16)
+
+    def down(r, carry):
+        at = quarter(me, r)
+        value_s[...] = nn(act_out[...], wd[:, at]) + nn(tdb, bd[:, at])
+        store_block(r, value_s, slice(0, rows), y_keep, y_send)
+        return carry
+
+    lax.fori_loop(0, PARTS, down, 0)
+
+
+def back_kernel(last, info, wgu, h, g, td, dg, du, a2, fb, *rest):
     (value_s, low_s), rest = rest[-2:], rest[:-2]
-    outs, rest = (rest[-4:], rest[:-4]) if last else (rest[-5:], rest[:-5])
-    d_keep, d_send, y_keep, y_send = outs[:4]
+    outs, rest = (rest[-2:], rest[:-2]) if last else (rest[-3:], rest[:-3])
+    d_keep, d_send = outs[:2]
     me = info[0]
     rows = h.shape[0]
-    own = slice(0, rows)
-
     dt2 = jnp.concatenate([nt(dg[...], fb[0]), nt(du[...], fb[1])], axis=1)
     dt2b = dt2.astype(BF16)
-    td = nt(act[...], da[...])
-    tdb = td.astype(BF16)
-    dt2t, tdt = dt2.T.astype(BF16), td.T.astype(BF16)
+    dt2t, tdt = dt2.T.astype(BF16), td[...].T.astype(BF16)
 
     def block(r, carry):
         at = quarter(me, r)
         value_s[...] = nt(dg[...], wgu[0, at, :]) + nt(du[...], wgu[1, at, :]) + nn(dt2b, a2[:, at])
-        store_block(r, value_s, own, d_keep, d_send)
-        value_s[...] = nn(act[...], wd[:, at]) + nn(tdb, bd[:, at])
-        store_block(r, value_s, own, y_keep, y_send)
+        store_block(r, value_s, slice(0, rows), d_keep, d_send)
         low_s[:2 * RANK, :] = nn(dt2t, h[:, at])
         low_s[2 * RANK:, :] = nn(tdt, g[:, at])
         if last:
             low_s[...] += rest[0][:, at]
             store_block(r, low_s, slice(rows, rows + 3 * RANK), d_keep, d_send)
         else:
-            outs[4][:, at] = low_s[...]
+            outs[2][:, at] = low_s[...]
         return carry
 
     lax.fori_loop(0, PARTS, block, 0)
@@ -422,23 +426,30 @@
         outs[8][...] = inner
 
 
-def finish_kernel(info, gains, x_all, aa_high, aa_far, y_far, *refs):
+def output_kernel(info, y_far, *refs):
+    out = refs[-1]
+    rows = out.shape[0] // CHUNKS
+    for c in range(CHUNKS):
+        xq, y_keep, y_got = refs[3 * c:3 * (c + 1)]
+        at = slice(c * rows, (c + 1) * rows)
+        valid = c * rows + lax.broadcasted_iota(jnp.int32, (rows, 1), 0) < info[1]
+        y = xq[...] + y_keep[:, LO] + y_got[:, LO].astype(F32) + y_far[at, :].astype(F32)
+        out[at, :] = jnp.where(valid, y, 0.0).astype(BF16)
+
+
+def finish_kernel(gains, x_all, aa_high, aa_far, *refs):
     out = refs[-1]
     gain = gains[0, 0:1, :].astype(F32)
     rows = out.shape[0] // CHUNKS
     inner = aa_high[4 * RANK:, :].astype(F32) + aa_far[4 * RANK:, :].astype(F32)
     for c in range(CHUNKS):
-        dx, keep, got, there, inv, xq, y_keep, y_got = refs[8 * c:8 * (c + 1)]
+        dx, keep, got, there, inv = refs[5 * c:5 * (c + 1)]
         x = chunk_of(x_all, c, rows)
-        at = slice(c * rows, (c + 1) * rows)
         mine = inner[c * SPARE // 2:c * SPARE // 2 + 8, :rows].T[:, 0:1]
         inv = inv[...]
         grad = keep[:, LO] + got[:, LO].astype(F32) + there[...].astype(F32)
         grad = inv * (gain * grad) - x[...].astype(F32) * (inv * inv * mine / WIDTH)
-        out[at, LO] = (dx[...] + grad).astype(BF16)
-        valid = c * rows + lax.broadcasted_iota(jnp.int32, (rows, 1), 0) < info[1]
-        y = xq[...] + y_keep[:, LO] + y_got[:, LO].astype(F32) + y_far[at, :].astype(F32)
-        out[at, HI] = jnp.where(valid, y, 0.0).astype(BF16)
+        out[c * rows:(c + 1) * rows, :] = (dx[...] + grad).astype(BF16)
 
 
 def high_sum_kernel(*refs):
@@ -548,10 +559,8 @@
         copy.wait()
 
 
-def collect_kernel(slots, source, *refs):
-    sems = refs[-1]
-    made = [pltpu.make_async_copy(source.at[slots[i], :, cols], ref.at[i], sems.at[k, i])
-            for i in range(source.shape[0]) for k, (ref, cols) in enumerate(zip(refs, (LO, HI)))]
+def collect_kernel(slots, source, out, sems):
+    made = [pltpu.make_async_copy(source.at[slots[i]], out.at[i], sems.at[i]) for i in range(source.shape[0])]
     for copy in made:
         copy.start()
     for copy in made:
@@ -726,9 +735,8 @@
     my_adapter = jnp.sum(jnp.where(mine, owners, 0))
     info = jnp.stack([me.astype(jnp.int32), my_length, my_adapter, place.astype(jnp.int32)])
 
-    both = jnp.stack([attention_gain, feedfwd_gain])
-    gs = spread(jnp.concatenate([cotangent[0], both, jnp.zeros((14, QUARTER), BF16)], axis=0))
-    gains = jnp.stack([v[length:length + 2] for v in gs])
+    gs = spread(cotangent[0])
+    gains = jnp.stack(spread(jnp.stack([attention_gain, feedfwd_gain])))
     ordered, = move_rows(deal_kernel, residual, dealing_slots, "deal", [pltpu.VMEM(residual.shape, BF16)], pltpu.HBM,
                          pltpu.VMEM, (seqs,))
     dealt = lax.all_to_all(ordered, "dp", split_axis=0, concat_axis=1, tiled=True)[0]
@@ -737,7 +745,7 @@
          output_adapter_output, feedfwd_adapter_input, feedfwd_adapter_output, down_adapter_input,
          down_adapter_output), info)
     a1, qb, kvb, oa, ob, a2, fba, da, bd = adapters_here
-    dealt = late(dealt, gs[2], a1)
+    dealt = late(dealt, gs[2], a1, gains)
     beside = near(dealt)
     there = [far(dealt[c * rows:(c + 1) * rows]) for c in range(CHUNKS)]
     xs = [None] * CHUNKS
@@ -771,20 +779,22 @@
         hidden = (rows, units)
         outs = [(wide, BF16), (block, F32), (wide, BF16), (wide, BF16), (hidden, BF16), (hidden, BF16), (hidden, BF16),
                 ((rows, 2 * RANK), BF16), ((rows, RANK), BF16),
-                ((3 * RANK * units // QUARTER, QUARTER), BF16 if c else F32)]
+                ((3 * RANK * units // QUARTER, QUARTER), BF16 if c else F32),
+                (col, F32), (col, BF16), ((rows, RANK), F32)]
         args = (*xs[c], total, near(total), *gs, gains, a2, bd, fba, da, *partial)
         weights = () if c else (gate_up_matrix, down_matrix)
         outs += like(*weights)
         return call(
             functools.partial(front_kernel, c, c == CHUNKS - 1), info, weights, (wgu, wd, *args) if c else args, outs,
-            [((ROW_BLOCK, WIDTH), F32)], "front_%d" % c, 8, order, () if c else (2, units // QUARTER))
+            [((ROW_BLOCK, WIDTH), F32), (block, F32)], "front_%d" % c, 8, order, () if c else (2, units // QUARTER))
 
     def back(c, hidden, partial, order):
         first = col if c else (rows + 3 * RANK, half)
-        outs = [(first, F32), (first, BF16), (col, F32), (col, BF16)]
+        outs = [(first, F32), (first, BF16)]
         outs += [((3 * RANK, WIDTH), F32)] if c else []
+        _, _, h2, g2, _, dg, du = hidden[:7]
         return call(
-            functools.partial(back_kernel, c == 0), info, (), (wgu, wd, *hidden[2:7], a2, bd, fba, da, *partial), outs,
+            functools.partial(back_kernel, c == 0), info, (), (wgu, h2, g2, hidden[12], dg, du, a2, fba, *partial), outs,
             [(block, F32), ((3 * RANK, QUARTER), F32)], "back_%d" % c, 8, order)
 
     def attend_back(c, total, partial, order):
@@ -802,38 +812,49 @@
              *kept[c], *triples, *partial), outs, scratch + like(wq, wkv, wo), "attend_back_%d" % c, 18, order, (3,))
 
     bits = [1 << b for b in reversed(range(dp.bit_length() - 1))]
-    hidden, d_own, d_far, y_keep, y_send = ([None] * CHUNKS for _ in range(5))
+    def to_bands(value):
+        return lax.all_to_all(value.reshape(dp, length // dp, QUARTER), "dp", split_axis=0, concat_axis=0, tiled=True)
+
+    def collect(value, name, *before):
+        rows_out = sds((seqs, length // dp, QUARTER), BF16)
+        return move_rows(collect_kernel, value, late(dealing_slots, *before), name, [rows_out], pltpu.VMEM, pl.ANY,
+                         (seqs,))[0]
+
+    hidden, d_own, d_far = ([None] * CHUNKS for _ in range(3))
     *hidden[0], wgu, wd = front(0, far_sum(z_own[0], z_far[0]), (), order)
     step = hidden[0][8]
-    hidden[1] = front(1, far_sum(z_own[1], late(z_far[1], step)), hidden[0][9:], (step,))
+    hidden[1] = front(1, far_sum(z_own[1], late(z_far[1], step)), hidden[0][9:10], (step,))
+    y_keep, y_got = [h[10] for h in hidden], [near(h[11]) for h in hidden]
+    y_high = high_sum(*zip(y_keep, y_got))
+    y_far = far(y_high)
     fb = hidden[1][9][None]
     fb_first = swap(fb, bits[0], "dp", dp)
-    d_keep, d_send, y_keep[1], y_send[1], fa = back(1, hidden[1], (), (hidden[1][8],))
-    d_own[1] = pair_sum(d_keep, late(d_send, fb_first))
+    d_keep, d_send, fa = back(1, hidden[1], (), (y_high,))
+    ready = (fb_first, y_far)
+    d_own[1] = pair_sum(d_keep, late(d_send, *ready))
     d_far[1] = far(d_own[1])
     fb = fb_more = jnp.concatenate([fb, fb_first], axis=0)
     for bit in bits[1:-1]:
         fb_more = doubled(fb_more, bit, dp)
     fb_more = fb_more[2:]
     fb_side = swap(fb, bits[-1], "dp", dp)
-    d_keep, d_send, y_keep[0], y_send[0] = back(0, hidden[0], (fa,), (d_own[1],))
+    d_keep, d_send = back(0, hidden[0], (fa,), (d_own[1],))
     total = far_sum(d_own[1], late(d_far[1], d_send))
     d_own[0] = pair_sum(d_keep, late(d_send, fb_more, fb_side))
     d_far[0] = far(d_own[0])
     fb_more_side = swap(fb_more, bits[-1], "dp", dp)
-    y_got = [near(late(v, d_own[0])) for v in y_send]
+    parts = [v for c in range(CHUNKS) for v in (hidden[c][1], y_keep[c], y_got[c])]
+    result, = call(output_kernel, info, (), (y_far, *parts), [((length, QUARTER), BF16)], [], "output", 8, (d_own[0],))
     dxq, h_keep, h_send, inv, *sums = attend_back(1, total, (), (d_own[0],))
     total = far_sum(d_own[0], late(d_far[0], inv))
-    y_high = high_sum(*((y_keep[c], late(y_got[c], inv)) for c in range(CHUNKS)))
-    y_far = far(y_high)
     h_got = near(late(h_send, fb_more_side))
     h_high = high_sum((h_keep, h_got))
     h_far = far(h_high)
     final = [None, (dxq, h_keep, h_got, h_far, inv)]
     fa = total[rows:][None]
     fa_first = swap(fa, bits[0], "dp", dp)
-    dxq, h_keep, h_send, inv, att_b, aa_keep, aa_send = attend_back(0, total, sums, (h_high, y_high))
-    ready = (fa_first, h_far, y_far)
+    dxq, h_keep, h_send, inv, att_b, aa_keep, aa_send = attend_back(0, total, sums, (h_high,))
+    ready = (fa_first, h_far)
     aa_got = near(late(aa_send, *ready))
     aa_high = high_sum((aa_keep, aa_got))
     aa_far = far(aa_high)
@@ -854,13 +875,10 @@
         fa = doubled(fa, bit, dp)
     fa_side = swap(fa, bits[-1], "dp", dp)
 
-    parts = [v for c in range(CHUNKS) for v in (*final[c], hidden[c][1], y_keep[c], y_got[c])]
-    both, = call(finish_kernel, info, (), (gains, dealt, aa_high, aa_far, y_far, *parts), [((length, half), BF16)], [],
-                 "finish", 12, (att, fa_side))
-    both = lax.all_to_all(both.reshape(dp, length // dp, half), "dp", split_axis=0, concat_axis=0, tiled=True)
-    rows_out = sds((seqs, length // dp, QUARTER), BF16)
-    input_grad, output = move_rows(collect_kernel, both, dealing_slots, "collect", [rows_out, rows_out], pltpu.VMEM,
-                                   pl.ANY, (2, seqs))
+    dinput, = call(finish_kernel, None, (), (gains, dealt, aa_high, aa_far, *(v for f in final for v in f)),
+                   [((length, QUARTER), BF16)], [], "finish", 8, (att, fa_side))
+    input_grad = collect(to_bands(dinput), "collect_grad")
+    output = collect(to_bands(late(result, dinput)), "collect_out", input_grad)
 
     outs = [sds((adapters, 2 * RANK, WIDTH), F32), sds((adapters, RANK, WIDTH), F32),
             sds((adapters, 2, RANK, units), F32), sds((adapters, RANK, units), F32)]

time: 227 us -> 233 us (1.026)
  waiting for transfers between devices: 72.8 us -> 65.2 us
  starting transfers between devices: 40 us -> 44.7 us
  local copies, waits for them, and re-layouts: 9.08 us -> 13.4 us
  Pallas kernels: 101 us -> 105 us
    ppermute x47 -> x50, waiting for transfers between devices: 72.4 us -> 61.9 us  [swap(): return lax.ppermute(value, axis, [(i, i ^ bit) for i in range(size)])]
    all_to_all x1 -> x2, starting transfers between devices: 3.7 us -> 7.11 us  [to_bands(): lax.all_to_all(value.reshape(dp, length // dp, QUARTER), 'dp', split_axis...]
    all_to_all x1 -> x2, waiting for transfers between devices: 0.01 us -> 3.25 us  [to_bands(): lax.all_to_all(value.reshape(dp, length // dp, QUARTER), 'dp', split_axis...]
    unnamed x82, local copies, waits for them, and re-layouts: 8.87 us -> 11.6 us
    ppermute x47 -> x50, starting transfers between devices: 29 us -> 30.4 us  [swap(): return lax.ppermute(value, axis, [(i, i ^ bit) for i in range(size)])]
    pallas_call x23 -> x24, Pallas kernels: 86.9 us -> 88.2 us  [call(): pl.pallas_call(body, in_specs=[pl.BlockSpec(memory_space=pltpu.SMEM)] * n...]
    pallas_call x2 -> x3, Pallas kernels: 4.1 us -> 5.25 us  [move_rows(): pl.pallas_call(kernel, in_specs=[pl.BlockSpec(memory_space=pltpu.SMEM), p...]
  transfers between devices with their start and end apart: 49 -> 53, of which waited for: 24 -> 25; matrix products, arithmetic and copies ran while one was open for 1% -> 2% of each run, Pallas kernels for 36% -> 41%
where the time goes in v6:
time: 233 us; the launch traced here: 232 us
  Pallas kernels  105 us (45%)
  waiting for transfers between devices  65.2 us (28%)
  starting transfers between devices  44.7 us (19%)
  local copies, waits for them, and re-layouts  13.4 us (6%)
    pallas_call x24, Pallas kernels, call(): pl.pallas_call(body, in_specs=[pl.BlockSpec(memory_space=pltpu.SMEM)] * n...  88.2 us
    ppermute x50, waiting for transfers between devices, swap(): return lax.ppermute(value, axis, [(i, i ^ bit) for i in range(size)])  61.9 us
    ppermute x50, starting transfers between devices, swap(): return lax.ppermute(value, axis, [(i, i ^ bit) for i in range(size)])  30.4 us
    unnamed x82, local copies, waits for them, and re-layouts  11.6 us
    pallas_call x2, Pallas kernels, sum_call(): pl.pallas_call(functools.partial(kernel, [len(group) for group in groups]...  9.43 us
    all_to_all x1, starting transfers between devices, shards(): lax.all_to_all(ordered, 'dp', split_axis=0, concat_axis=1, tiled=True)[0]  7.26 us
    all_to_all x2, starting transfers between devices, to_bands(): lax.all_to_all(value.reshape(dp, length // dp, QUARTER), 'dp', split_axis...  7.11 us
    pallas_call x3, Pallas kernels, move_rows(): pl.pallas_call(kernel, in_specs=[pl.BlockSpec(memory_space=pltpu.SMEM), p...  5.25 us
  transfers between devices with their start and end apart: 53, of which 25 were waited for; matrix products, arithmetic and copies ran while one was open for 2% of the time, Pallas kernels for 41%

profile of v6, /device:TPU:0, one launch (start us, length us, event | category | flops | bytes accessed | tf_op | source)
XLA Modules:
  0.0 231.6 jit_solution(8710782472171618075)
XLA Ops:
  1.4 2.5 %deal.1 = bf16[8,64,512]{2,1,0:T(8,128)(2,1)} custom-call(s32[8]{0:T(128)S(1)} %copy-done.34, bf16[8,64,512]{2,1,0:T(8,128)(2,1)} %source.1), custom_call_target="tpu_custom_call" | custom-call | flops 1000 | bytes 1000 | tf_op jit(solution)/shard_map/deal/pallas_call | solution.py:593
  3.9 7.3 %all-to-all-start = ((bf16[8,64,512]{2,1,0:T(8,128)(2,1)}), bf16[8,64,512]{2,1,0:T(8,128)(2,1)S(1)}, u32[]{:S(2)}, u32[]{:S(2)}) async-start(bf16[8,64,512]{2,1,0:T(8,128)(2,1)} %deal.1), calls=%async_computation | async-start | bytes 1048576 | tf_op jit(solution)/shard_map/all_to_all | solution.py:742
  11.3 1.6 collective-permute-start.1
  14.2 0.7 collective-permute-done.1
  14.9 1.4 pad_add_fusion.info.refs_0_
  16.3 1.8 adapters.1
  18.8 8.1 %collective-permute-done.3.refs_11_.refs_10_ = bf16[512,512]{1,0:T(8,128)(2,1)S(1)} collective-permute-done((bf16[512,512]{1,0:T(8,128)(2,1)S(1)}, bf16[512,512]{1,0:T(8,128)(2,1)S(1)}, u32[]{:S(2)}, u32[]{:S(2)}) %collective-permute-start.3) | collective-permute-done | bytes 524320 | tf_op jit(solution)/shard_map/ppermute | solution.py:665
  27.5 7.0 %collective-permute-done.5.refs_5_.refs_6_ = bf16[256,512]{1,0:T(8,128)(2,1)S(1)} collective-permute-done((bf16[256,512]{1,0:T(8,128)(2,1)S(1)}, bf16[256,512]{1,0:T(8,128)(2,1)S(1)}, u32[]{:S(2)}, u32[]{:S(2)}) %collective-permute-start.5) | collective-permute-done | bytes 262176 | tf_op jit(solution)/shard_map/ppermute | solution.py:665
  35.1 1.0 collective-permute-done.6.refs_6_.refs_7_
  36.1 4.1 %project_0.1 = (bf16[48,256]{1,0:T(8,128)(2,1)S(1)}, bf16[512,256]{1,0:T(8,128)(2,1)S(1)}, bf16[2,256,64]{2,1,0:T(8,128)(2,1)S(1)}, bf16[2,256,64]{2,1,0:T(8,128...) custom-call(s32[4]{0:T(128)S(1)} %pad_add_fusion.info.refs_0_, bf16[2048,512]{1,0:T(8,128)(2,1)} %refs_1_.15, ...), custom_call_target="tpu_custom_call" | custom-call | flops 1000 | bytes 1000 | tf_op jit(solution)/shard_map/project_0/pallas_call | solution.py:626
  40.2 3.1 %attend_0.1 = (f32[256,1024]{1,0:T(8,128)S(1)}, bf16[256,1024]{1,0:T(8,128)(2,1)S(1)}, bf16[512,256]{1,0:T(8,128)(2,1)S(1)}, f32[8,256]{1,0:T(8,128)S(1)}, bf16[16,256]{1,0:T(8,128)(2,1)S(1)}) custom-call(s32[4]{0:T(128)S(1)} %pad_add_fusion.info.refs_0_, bf16[512,2048]{1,0:T(8,128)(2,1)} %refs_3_.5, ...), custom_call_target="tpu_custom_call" | custom-call | flops 1000 | bytes 1000 | tf_op jit(solution)/shard_map/attend_0/pallas_call | solution.py:626
  43.5 1.8 collective-permute-done.10.refs_1_
  46.0 1.5 collective-permute-done.13.refs_6_.refs_7_
  47.6 4.1 %project_1.1 = (bf16[48,256]{1,0:T(8,128)(2,1)S(1)}, bf16[512,256]{1,0:T(8,128)(2,1)S(1)}, bf16[2,256,64]{2,1,0:T(8,128)(2,1)S(1)}, bf16[2,256,64]{2,1,0:T(8,128...) custom-call(s32[4]{0:T(128)S(1)} %pad_add_fusion.info.refs_0_, bf16[2048,512]{1,0:T(8,128)(2,1)} %refs_1_.15, ...), custom_call_target="tpu_custom_call" | custom-call | flops 1000 | bytes 1000 | tf_op jit(solution)/shard_map/project_1/pallas_call | solution.py:626
  51.6 3.7 %attend_1.1 = (f32[256,1024]{1,0:T(8,128)S(1)}, bf16[256,1024]{1,0:T(8,128)(2,1)S(1)}, bf16[512,256]{1,0:T(8,128)(2,1)S(1)}, f32[8,256]{1,0:T(8,128)S(1)}, bf16[16,256]{1,0:T(8,128)(2,1)S(1)}) custom-call(s32[4]{0:T(128)S(1)} %pad_add_fusion.info.refs_0_, bf16[512,2048]{1,0:T(8,128)(2,1)} %refs_3_.5, ...), custom_call_target="tpu_custom_call" | custom-call | flops 1000 | bytes 1000 | tf_op jit(solution)/shard_map/attend_1/pallas_call | solution.py:626
  55.4 4.0 %collective-permute-done.11.refs_1_ = bf16[256,1024]{1,0:T(8,128)(2,1)S(1)} collective-permute-done((bf16[256,1024]{1,0:T(8,128)(2,1)S(1)}, bf16[256,1024]{1,0:T(8,128)(2,1)S(1)}, u32[]{:S(2)}, u32[]{:S(2)}) %collective-permute-start.11) | collective-permute-done | bytes 524320 | tf_op jit(solution)/shard_map/ppermute | solution.py:665
  62.8 0.7 collective-permute-done.12.refs_8_
  63.6 17.4 %front_0.1 = (bf16[256,2048]{1,0:T(8,128)(2,1)S(1)}, f32[256,512]{1,0:T(8,128)S(1)}, bf16[256,2048]{1,0:T(8,128)(2,1)S(1)}, bf16[256,2048]{1,0:T(8,128)(2,1)S(1)...) custom-call(s32[4]{0:T(128)S(1)} %pad_add_fusion.info.refs_0_, ...), custom_call_target="tpu_custom_call" | custom-call | flops 1000 | bytes 1000 | tf_op jit(solution)/shard_map/front_0/pallas_call | solution.py:626
  81.7 1.4 collective-permute-done.16.refs_8_
  83.2 16.0 %front_1.1 = (bf16[256,2048]{1,0:T(8,128)(2,1)S(1)}, f32[256,512]{1,0:T(8,128)S(1)}, bf16[256,2048]{1,0:T(8,128)(2,1)S(1)}, bf16[256,2048]{1,0:T(8,128)(2,1)S(1)...) custom-call(s32[4]{0:T(128)S(1)} %pad_add_fusion.info.refs_0_, ...), custom_call_target="tpu_custom_call" | custom-call | flops 1000 | bytes 1000 | tf_op jit(solution)/shard_map/front_1/pallas_call | solution.py:626
  99.3 1.8 collective-permute-done.18.refs_3_.refs_7_
  101.8 2.9 %collective-permute-start.19 = (bf16[1,192,512]{2,1,0:T(8,128)(2,1)S(1)}, bf16[1,192,512]{2,1,0:T(8,128)(2,1)S(1)}, u32[]{:S(2)}, u32[]{:S(2)}) collective-permute-start(bf16[1,192,512]{2,1,0:T(8,128)(2,1)S(1)} %bitcast.33), channel_id=1, source_target_pairs={{0,16},{4,20},{8,24},{12,28},{16,0},{20,4},{24,8},{28,12},{1,17},{... | collective-permute-start | bytes 589832 | tf_op jit(solution)/shard_map/ppermute | solution.py:665
  104.7 7.7 %back_1.1 = (f32[256,1024]{1,0:T(8,128)S(1)}, bf16[256,1024]{1,0:T(8,128)(2,1)S(1)}, f32[48,2048]{1,0:T(8,128)S(1)}) custom-call(s32[4]{0:T(128)S(1)} %pad_add_fusion.info.refs_0_, bf16[2,2048,2048]{2,1,0:T(8,128)(2,1)S(1)} %get-tuple-element.141.refs_1_, bf16[256,2048]{1,0:T(8,128)(2,1)S(1)} %get-tuple-element.151.refs_2_, ...), custom_call_target="tpu_custom_call" | custom-call | flops 1000 | bytes 1000 | tf_op jit(solution)/shard_map/back_1/pallas_call | solution.py:626
  112.4 1.4 collective-permute-done.19
  113.8 1.3 collective-permute-done.20.refs_1_
  115.2 2.1 collective-permute-start.23
  117.3 1.5 collective-permute-start.22
  119.5 7.7 %back_0.1 = (f32[304,1024]{1,0:T(8,128)S(1)}, bf16[304,1024]{1,0:T(8,128)(2,1)S(1)}) custom-call(s32[4]{0:T(128)S(1)} %pad_add_fusion.info.refs_0_, bf16[2,2048,2048]{2,1,0:T(8,128)(2,1)S(1)} %get-tuple-element.141.refs_1_, bf16[256,2048]{1,0:T(8,128)(2,1)S(1)} %get-tuple-element.142.refs_2_, bf16[256,2048]{1,0:T(8,128)(2,1)S(1)} %get-tuple-element.143.refs_3_, ...), custom_call_target="tpu_custom_call" | custom-call | flops 1000 | bytes 1000 | tf_op jit(solution)/shard_map/back_0/pallas_call | solution.py:626
  127.2 1.3 collective-permute-done.22.refs_1_
  128.5 4.2 %collective-permute-done.26.refs_1_ = bf16[256,1024]{1,0:T(8,128)(2,1)S(1)} collective-permute-done((bf16[256,1024]{1,0:T(8,128)(2,1)S(1)}, bf16[256,1024]{1,0:T(8,128)(2,1)S(1)}, u32[]{:S(2)}, u32[]{:S(2)}) %collective-permute-start.26) | collective-permute-done | bytes 524320 | tf_op jit(solution)/shard_map/ppermute | solution.py:665
  134.8 10.7 %attend_back_1.1 = (f32[256,512]{1,0:T(8,128)S(1)}, f32[256,1024]{1,0:T(8,128)S(1)}, bf16[256,1024]{1,0:T(8,128)(2,1)S(1)}, f32[256,1]{1,0:T(8,128)S(1)}, f32[48...) custom-call(s32[4]{0:T(128)S(1)} %pad_add_fusion.info.refs_0_, ...), custom_call_target="tpu_custom_call" | custom-call | flops 1000 | bytes 1000 | tf_op jit(solution)/shard_map/attend_back_1/pallas_call | solution.py:626
  145.7 3.8 %collective-permute-done.25.refs_1_ = bf16[304,1024]{1,0:T(8,128)(2,1)S(1)} collective-permute-done((bf16[304,1024]{1,0:T(8,128)(2,1)S(1)}, bf16[304,1024]{1,0:T(8,128)(2,1)S(1)}, u32[]{:S(2)}, u32[]{:S(2)}) %collective-permute-start.25) | collective-permute-done | bytes 622624 | tf_op jit(solution)/shard_map/ppermute | solution.py:665
  150.5 2.4 %collective-permute-start.31 = (bf16[1,48,1024]{2,1,0:T(8,128)(2,1)S(1)}, bf16[1,48,1024]{2,1,0:T(8,128)(2,1)S(1)}, u32[]{:S(2)}, u32[]{:S(2)}) collective-permute-start(bf16[1,48,1024]{2,1,0:T(8,128)(2,1)S(1)} %slice_bitcast_fusion), channel_id=1, source_target_pairs={{0,16},{4,20},{8,24},{12,28},{16,0},{20,4},{24,8},{28,12},{1,17},{... | collective-permute-start | bytes 294920 | tf_op jit(solution)/shard_map/ppermute | solution.py:665
  152.9 9.7 %attend_back_0.1 = (f32[256,512]{1,0:T(8,128)S(1)}, f32[256,1024]{1,0:T(8,128)S(1)}, bf16[256,1024]{1,0:T(8,128)(2,1)S(1)}, f32[256,1]{1,0:T(8,128)S(1)}, bf16[4...) custom-call(s32[4]{0:T(128)S(1)} %pad_add_fusion.info.refs_0_, ...), custom_call_target="tpu_custom_call" | custom-call | flops 1000 | bytes 1000 | tf_op jit(solution)/shard_map/attend_back_0/pallas_call | solution.py:626
  163.2 1.7 collective-permute-done.33.refs_1_
  164.9 1.5 collective-permute-start.34
  168.4 1.4 collective-permute-done.34.refs_3_
  169.9 1.9 collective-permute-start.37
  171.8 1.8 collective-permute-done.39
  174.2 1.1 collective-permute-start.40
  175.3 2.3 %collective-permute-done.37 = bf16[1,112,512]{2,1,0:T(8,128)(2,1)S(1)} collective-permute-done((bf16[1,112,512]{2,1,0:T(8,128)(2,1)S(1)}, bf16[1,112,512]{2,1,0:T(8,128)(2,1)S(1)}, u32[]{:S(2)}, u32[]{:S(2)}) %collective-permute-start.37) | collective-permute-done | bytes 114720 | tf_op jit(solution)/shard_map/ppermute | solution.py:665
  177.8 7.1 %collective-permute-done.38 = bf16[2,112,512]{2,1,0:T(8,128)(2,1)S(1)} collective-permute-done((bf16[2,112,512]{2,1,0:T(8,128)(2,1)S(1)}, bf16[2,112,512]{2,1,0:T(8,128)(2,1)S(1)}, u32[]{:S(2)}, u32[]{:S(2)}) %collective-permute-start.38) | collective-permute-done | bytes 229408 | tf_op jit(solution)/shard_map/ppermute | solution.py:665
  184.9 1.3 finish.1
  186.2 3.5 %all-to-all-start.1 = ((bf16[8,64,512]{2,1,0:T(8,128)(2,1)}), bf16[8,64,512]{2,1,0:T(8,128)(2,1)S(1)}, u32[]{:S(2)}, u32[]{:S(2)}) async-start(bf16[8,64,512]{2,1,0:T(8,128)(2,1)} %bitcast.13), calls=%async_computation.1 | async-start | bytes 1048576 | tf_op jit(solution)/shard_map/all_to_all | solution.py:816
  189.7 1.9 collective-permute-start.41
  191.6 1.2 copy-done.11
  192.8 1.0 copy-done.15
  193.9 1.0 copy-done.17
  194.9 1.0 copy-done.19
  196.0 1.0 copy-done.21
  197.0 1.0 copy-done.23
  198.0 1.6 output.1
  200.1 3.3 %all-to-all-done.1.source = bf16[8,64,512]{2,1,0:T(8,128)(2,1)S(1)} async-done(((bf16[8,64,512]{2,1,0:T(8,128)(2,1)}), bf16[8,64,512]{2,1,0:T(8,128)(2,1)S(1)}, u32[]{:S(2)}, u32[]{:S(2)}) %all-to-all-start.1) | async-done | bytes 524320 | tf_op jit(solution)/shard_map/all_to_all | solution.py:816
  203.4 3.6 %all-to-all-start.2 = ((bf16[8,64,512]{2,1,0:T(8,128)(2,1)}), bf16[8,64,512]{2,1,0:T(8,128)(2,1)S(1)}, u32[]{:S(2)}, u32[]{:S(2)}) async-start(bf16[8,64,512]{2,1,0:T(8,128)(2,1)} %bitcast.14), calls=%async_computation.2 | async-start | bytes 1048576 | tf_op jit(solution)/shard_map/all_to_all | solution.py:816
  207.0 1.5 collective-permute-start.46
  208.5 1.0 copy-done.25
  209.5 1.0 copy-done.27
  210.5 1.0 copy-done.29
  211.5 4.9 %feedforward_sum.1 = (f32[8,32,2048]{2,1,0:T(8,128)}, f32[8,16,2048]{2,1,0:T(8,128)}, f32[8,2,16,2048]{3,2,1,0:T(8,128)}, f32[8,16,2048]{2,1,0:T(8,128)}) custom-call(s32[4]{0:T(128)S(1)} %pad_add_fusion.info.refs_0_, s32[8]{0:T(128)S(1)} %get-tuple-element.216.owners, bf16[2,192,512]{2,1,0:T(8,128)(2,1)S(1)} %pad_maximum_fusion.refs_0_, ...), custom_call_target="tpu_custom_call" | custom-call | bytes 12000000 | tf_op jit(solution)/shard_map/feedforward_sum/pallas_call | solution.py:649
  216.4 1.0 slice.31.refs_3_
  218.6 5.6 %collective-permute-done.47.refs_7_ = bf16[4,64,512]{2,1,0:T(8,128)(2,1)S(1)} collective-permute-done((bf16[4,64,512]{2,1,0:T(8,128)(2,1)S(1)}, bf16[4,64,512]{2,1,0:T(8,128)(2,1)S(1)}, u32[]{:S(2)}, u32[]{:S(2)}) %collective-permute-start.47) | collective-permute-done | bytes 262176 | tf_op jit(solution)/shard_map/ppermute | solution.py:665
  224.2 1.4 collect_grad.1
  225.6 1.4 collect_out.1
  227.1 4.5 %attention_sum.1 = (f32[8,48,2048]{2,1,0:T(8,128)}, f32[8,16,2048]{2,1,0:T(8,128)}, f32[8,16,512]{2,1,0:T(8,128)}, f32[8,2,16,128]{3,2,1,0:T(8,128)}, f32[8,16,512]{2,1,0:T(8,128)}) custom-call(s32[4]{0:T(128)S(1)} %pad_add_fusion.info.refs_0_, s32[8]{0:T(128)S(1)} %get-tuple-element.216.owners, ...), custom_call_target="tpu_custom_call" | custom-call | bytes 12000000 | tf_op jit(solution)/shard_map/attention_sum/pallas_call | solution.py:649
  (173 shorter events, 19.2 us)
Async XLA Ops:
  3.9 23.0 %all-to-all-start = ((bf16[8,64,512]{2,1,0:T(8,128)(2,1)}), bf16[8,64,512]{2,1,0:T(8,128)(2,1)S(1)}, u32[]{:S(2)}, u32[]{:S(2)}) async-start(bf16[8,64,512]{2,1,0:T(8,128)(2,1)} %deal.1), calls=%async_computation | async-start | bytes 1048576 | tf_op jit(solution)/shard_map/all_to_all | solution.py:742
  11.2 7.6 %collective-permute-start = (bf16[2,512]{1,0:T(2,128)(2,1)S(1)}, bf16[2,512]{1,0:T(2,128)(2,1)S(1)}, u32[]{:S(2)}, u32[]{:S(2)}) collective-permute-start(bf16[2,512]{1,0:T(2,128)(2,1)S(1)} %pad_maximum_fusion.4), channel_id=1, source_target_pairs={{0,1},{1,0},{2,3},{3,2},{4,5},{5,4},{6,7},{7,6},{8,9},{9,8},{10,11... | collective-permute-start | bytes 6152 | tf_op jit(solution)/shard_map/ppermute | solution.py:665
  11.3 3.7 %collective-permute-start.1 = (bf16[2,512]{1,0:T(2,128)(2,1)S(1)}, bf16[2,512]{1,0:T(2,128)(2,1)S(1)}, u32[]{:S(2)}, u32[]{:S(2)}) collective-permute-start(bf16[2,512]{1,0:T(2,128)(2,1)S(1)} %pad_maximum_fusion.4), channel_id=1, source_target_pairs={{0,2},{1,3},{2,0},{3,1},{4,6},{5,7},{6,4},{7,5},{8,10},{9,11},{10,... | collective-permute-start | bytes 6152 | tf_op jit(solution)/shard_map/ppermute | solution.py:665
  12.9 14.0 %collective-permute-start.3 = (bf16[512,512]{1,0:T(8,128)(2,1)S(1)}, bf16[512,512]{1,0:T(8,128)(2,1)S(1)}, u32[]{:S(2)}, u32[]{:S(2)}) collective-permute-start(bf16[512,512]{1,0:T(8,128)(2,1)S(1)} %bitcast.27), channel_id=1, source_target_pairs={{0,2},{1,3},{2,0},{3,1},{4,6},{5,7},{6,4},{7,5},{8,10},{9,11},{10,... | collective-permute-start | bytes 1572872 | tf_op jit(solution)/shard_map/ppermute | solution.py:665
  14.9 3.8 %collective-permute-start.2 = (bf16[2,512]{1,0:T(2,128)(2,1)S(1)}, bf16[2,512]{1,0:T(2,128)(2,1)S(1)}, u32[]{:S(2)}, u32[]{:S(2)}) collective-permute-start(bf16[2,512]{1,0:T(2,128)(2,1)S(1)} %collective-permute-done.1), channel_id=1, source_target_pairs={{0,1},{1,0},{2,3},{3,2},{4,5},{5,4},{6,7},{7,6},{8,9},{9,8},{10,11... | collective-permute-start | bytes 6152 | tf_op jit(solution)/shard_map/ppermute | solution.py:665
  16.3 19.8 %copy-start.32 = (f32[32,256]{1,0:T(8,128)S(1)}, f32[32,256]{1,0:T(8,128)}, u32[]{:S(2)}) copy-start(f32[32,256]{1,0:T(8,128)} %constant.21.clone.refs_12_.refs_22_) | copy-start | bytes 98308
  16.3 19.8 %copy-start.33 = (f32[32,256]{1,0:T(8,128)S(1)}, f32[32,256]{1,0:T(8,128)}, u32[]{:S(2)}) copy-start(f32[32,256]{1,0:T(8,128)} %constant.19.clone.refs_11_.refs_21_) | copy-start | bytes 98308
  26.8 33.1 %copy-start.1 = (bf16[512,512]{1,0:T(8,128)(2,1)}, bf16[512,512]{1,0:T(8,128)(2,1)S(1)}, u32[]{:S(2)}) copy-start(bf16[512,512]{1,0:T(8,128)(2,1)S(1)} %collective-permute-done.3.refs_11_.refs_10_) | copy-start | bytes 1572868
  26.9 7.6 %collective-permute-start.5 = (bf16[256,512]{1,0:T(8,128)(2,1)S(1)}, bf16[256,512]{1,0:T(8,128)(2,1)S(1)}, u32[]{:S(2)}, u32[]{:S(2)}) collective-permute-start(bf16[256,512]{1,0:T(8,128)(2,1)S(1)} %get-tuple-element.218), channel_id=1, source_target_pairs={{0,2},{1,3},{2,0},{3,1},{4,6},{5,7},{6,4},{7,5},{8,10},{9,11},{10,... | collective-permute-start | bytes 786440 | tf_op jit(solution)/shard_map/ppermute | solution.py:665
  27.5 8.6 %collective-permute-start.4 = (bf16[512,512]{1,0:T(8,128)(2,1)S(1)}, bf16[512,512]{1,0:T(8,128)(2,1)S(1)}, u32[]{:S(2)}, u32[]{:S(2)}) collective-permute-start(bf16[512,512]{1,0:T(8,128)(2,1)S(1)} %bitcast.19), channel_id=1, source_target_pairs={{0,1},{1,0},{2,3},{3,2},{4,5},{5,4},{6,7},{7,6},{8,9},{9,8},{10,11... | collective-permute-start | bytes 1572872 | tf_op jit(solution)/shard_map/ppermute | solution.py:665
  34.5 1.5 collective-permute-start.6
  34.5 8.8 %collective-permute-start.9 = (bf16[256,512]{1,0:T(8,128)(2,1)S(1)}, bf16[256,512]{1,0:T(8,128)(2,1)S(1)}, u32[]{:S(2)}, u32[]{:S(2)}) collective-permute-start(bf16[256,512]{1,0:T(8,128)(2,1)S(1)} %get-tuple-element.217), channel_id=1, source_target_pairs={{0,2},{1,3},{2,0},{3,1},{4,6},{5,7},{6,4},{7,5},{8,10},{9,11},{10,... | collective-permute-start | bytes 786440 | tf_op jit(solution)/shard_map/ppermute | solution.py:665
  43.3 2.0 collective-permute-start.10
  45.4 14.0 %collective-permute-start.11 = (bf16[256,1024]{1,0:T(8,128)(2,1)S(1)}, bf16[256,1024]{1,0:T(8,128)(2,1)S(1)}, u32[]{:S(2)}, u32[]{:S(2)}) collective-permute-start(bf16[256,1024]{1,0:T(8,128)(2,1)S(1)} %pair_sum.4.refs_0_.refs_14_), channel_id=1, source_target_pairs={{0,2},{1,3},{2,0},{3,1},{4,6},{5,7},{6,4},{7,5},{8,10},{9,11},{10,... | collective-permute-start | bytes 1572872 | tf_op jit(solution)/shard_map/ppermute | solution.py:665
  46.0 1.5 collective-permute-start.13
  59.4 1.9 collective-permute-start.14
  59.4 2.7 %collective-permute-start.7 = (bf16[512,512]{1,0:T(8,128)(2,1)S(1)}, bf16[512,512]{1,0:T(8,128)(2,1)S(1)}, u32[]{:S(2)}, u32[]{:S(2)}) collective-permute-start(bf16[512,512]{1,0:T(8,128)(2,1)S(1)} %bitcast.28), channel_id=1, source_target_pairs={{0,1},{1,0},{2,3},{3,2},{4,5},{5,4},{6,7},{7,6},{8,9},{9,8},{10,11... | collective-permute-start | bytes 1572872 | tf_op jit(solution)/shard_map/ppermute | solution.py:665
  60.0 2.9 %collective-permute-start.8 = (bf16[512,512]{1,0:T(8,128)(2,1)S(1)}, bf16[512,512]{1,0:T(8,128)(2,1)S(1)}, u32[]{:S(2)}, u32[]{:S(2)}) collective-permute-start(bf16[512,512]{1,0:T(8,128)(2,1)S(1)} %collective-permute-done.3.refs_11_.refs_10_), channel_id=1, source_target_pairs={{0,1},{1,0},{2,3},{3,2},{4,5},{5,4},{6,7},{7,6},{8,9},{9,8},{10,11... | collective-permute-start | bytes 1572872 | tf_op jit(solution)/shard_map/ppermute | solution.py:665
  60.1 3.5 %collective-permute-start.12 = (bf16[256,1024]{1,0:T(8,128)(2,1)S(1)}, bf16[256,1024]{1,0:T(8,128)(2,1)S(1)}, u32[]{:S(2)}, u32[]{:S(2)}) collective-permute-start(bf16[256,1024]{1,0:T(8,128)(2,1)S(1)} %far_sum.4.refs_7_), channel_id=1, source_target_pairs={{0,1},{1,0},{2,3},{3,2},{4,5},{5,4},{6,7},{7,6},{8,9},{9,8},{10,11... | collective-permute-start | bytes 1572872 | tf_op jit(solution)/shard_map/ppermute | solution.py:665
  61.5 19.5 %collective-permute-start.15 = (bf16[256,1024]{1,0:T(8,128)(2,1)S(1)}, bf16[256,1024]{1,0:T(8,128)(2,1)S(1)}, u32[]{:S(2)}, u32[]{:S(2)}) collective-permute-start(bf16[256,1024]{1,0:T(8,128)(2,1)S(1)} %pair_sum.5.refs_19_.refs_0_), channel_id=1, source_target_pairs={{0,2},{1,3},{2,0},{3,1},{4,6},{5,7},{6,4},{7,5},{8,10},{9,11},{10,... | collective-permute-start | bytes 1572872 | tf_op jit(solution)/shard_map/ppermute | solution.py:665
  62.2 72.7 %copy-start.4 = (bf16[512,512]{1,0:T(8,128)(2,1)}, bf16[512,512]{1,0:T(8,128)(2,1)S(1)}, u32[]{:S(2)}) copy-start(bf16[512,512]{1,0:T(8,128)(2,1)S(1)} %collective-permute-done.7.refs_10_.refs_9_) | copy-start | bytes 1572868
  62.8 20.3 %copy-start.6 = (bf16[512,512]{1,0:T(8,128)(2,1)}, bf16[512,512]{1,0:T(8,128)(2,1)S(1)}, u32[]{:S(2)}) copy-start(bf16[512,512]{1,0:T(8,128)(2,1)S(1)} %collective-permute-done.8.refs_12_.refs_11_) | copy-start | bytes 1572868
  81.0 20.0 %copy-start.8 = (f32[256,1024]{1,0:T(8,128)}, f32[256,1024]{1,0:T(8,128)S(1)}, u32[]{:S(2)}) copy-start(f32[256,1024]{1,0:T(8,128)S(1)} %get-tuple-element.156.refs_0_.refs_3_) | copy-start | bytes 3145732
  81.2 2.0 collective-permute-start.16
  81.4 17.9 %collective-permute-start.17 = (bf16[256,1024]{1,0:T(8,128)(2,1)S(1)}, bf16[256,1024]{1,0:T(8,128)(2,1)S(1)}, u32[]{:S(2)}, u32[]{:S(2)}) collective-permute-start(bf16[256,1024]{1,0:T(8,128)(2,1)S(1)} %get-tuple-element.157), channel_id=1, source_target_pairs={{0,1},{1,0},{2,3},{3,2},{4,5},{5,4},{6,7},{7,6},{8,9},{9,8},{10,11... | collective-permute-start | bytes 1572872 | tf_op jit(solution)/shard_map/ppermute | solution.py:665
  99.1 13.3 %copy-start.10 = (f32[256,1024]{1,0:T(8,128)}, f32[256,1024]{1,0:T(8,128)S(1)}, u32[]{:S(2)}) copy-start(f32[256,1024]{1,0:T(8,128)S(1)} %get-tuple-element.158.refs_2_.refs_6_) | copy-start | bytes 3145732
  99.1 1.9 collective-permute-start.18
  99.3 13.2 %copy-start.14 = (bf16[256,1024]{1,0:T(8,128)(2,1)}, bf16[256,1024]{1,0:T(8,128)(2,1)S(1)}, u32[]{:S(2)}) copy-start(bf16[256,1024]{1,0:T(8,128)(2,1)S(1)} %collective-permute-done.17.refs_1_.refs_4_) | copy-start | bytes 1572868
  101.1 14.0 %collective-permute-start.20 = (bf16[512,512]{1,0:T(8,128)(2,1)S(1)}, bf16[512,512]{1,0:T(8,128)(2,1)S(1)}, u32[]{:S(2)}, u32[]{:S(2)}) collective-permute-start(bf16[512,512]{1,0:T(8,128)(2,1)S(1)} %high_sum.4.refs_9_), channel_id=1, source_target_pairs={{0,2},{1,3},{2,0},{3,1},{4,6},{5,7},{6,4},{7,5},{8,10},{9,11},{10,... | collective-permute-start | bytes 1572872 | tf_op jit(solution)/shard_map/ppermute | solution.py:665
  101.8 12.1 %collective-permute-start.19 = (bf16[1,192,512]{2,1,0:T(8,128)(2,1)S(1)}, bf16[1,192,512]{2,1,0:T(8,128)(2,1)S(1)}, u32[]{:S(2)}, u32[]{:S(2)}) collective-permute-start(bf16[1,192,512]{2,1,0:T(8,128)(2,1)S(1)} %bitcast.33), channel_id=1, source_target_pairs={{0,16},{4,20},{8,24},{12,28},{16,0},{20,4},{24,8},{28,12},{1,17},{... | collective-permute-start | bytes 589832 | tf_op jit(solution)/shard_map/ppermute | solution.py:665
  115.2 3.6 %collective-permute-start.21 = (bf16[256,1024]{1,0:T(8,128)(2,1)S(1)}, bf16[256,1024]{1,0:T(8,128)(2,1)S(1)}, u32[]{:S(2)}, u32[]{:S(2)}) collective-permute-start(bf16[256,1024]{1,0:T(8,128)(2,1)S(1)} %get-tuple-element.164), channel_id=1, source_target_pairs={{0,1},{1,0},{2,3},{3,2},{4,5},{5,4},{6,7},{7,6},{8,9},{9,8},{10,11... | collective-permute-start | bytes 1572872 | tf_op jit(solution)/shard_map/ppermute | solution.py:665
  115.2 12.0 %collective-permute-start.23 = (bf16[2,192,512]{2,1,0:T(8,128)(2,1)S(1)}, bf16[2,192,512]{2,1,0:T(8,128)(2,1)S(1)}, u32[]{:S(2)}, u32[]{:S(2)}) collective-permute-start(bf16[2,192,512]{2,1,0:T(8,128)(2,1)S(1)} %pad_maximum_fusion.refs_0_), channel_id=1, source_target_pairs={{0,4},{4,0},{8,12},{12,8},{16,20},{20,16},{24,28},{28,24},{1,5},{5... | collective-permute-start | bytes 1179656 | tf_op jit(solution)/shard_map/ppermute | solution.py:665
  117.3 11.2 %collective-permute-start.22 = (bf16[2,192,512]{2,1,0:T(8,128)(2,1)S(1)}, bf16[2,192,512]{2,1,0:T(8,128)(2,1)S(1)}, u32[]{:S(2)}, u32[]{:S(2)}) collective-permute-start(bf16[2,192,512]{2,1,0:T(8,128)(2,1)S(1)} %pad_maximum_fusion.refs_0_), channel_id=1, source_target_pairs={{0,8},{4,12},{8,0},{12,4},{16,24},{20,28},{24,16},{28,20},{1,9},{5... | collective-permute-start | bytes 1179656 | tf_op jit(solution)/shard_map/ppermute | solution.py:665
  118.9 13.8 %collective-permute-start.26 = (bf16[256,1024]{1,0:T(8,128)(2,1)S(1)}, bf16[256,1024]{1,0:T(8,128)(2,1)S(1)}, u32[]{:S(2)}, u32[]{:S(2)}) collective-permute-start(bf16[256,1024]{1,0:T(8,128)(2,1)S(1)} %pair_sum.6.refs_10_.refs_0_), channel_id=1, source_target_pairs={{0,2},{1,3},{2,0},{3,1},{4,6},{5,7},{6,4},{7,5},{8,10},{9,11},{10,... | collective-permute-start | bytes 1572872 | tf_op jit(solution)/shard_map/ppermute | solution.py:665
  127.2 18.3 %copy-start.24 = (bf16[2,192,512]{2,1,0:T(8,128)(2,1)}, bf16[2,192,512]{2,1,0:T(8,128)(2,1)S(1)}, u32[]{:S(2)}) copy-start(bf16[2,192,512]{2,1,0:T(8,128)(2,1)S(1)} %collective-permute-done.23.refs_2_) | copy-start | bytes 1179652
  128.5 17.0 %copy-start.26 = (bf16[2,192,512]{2,1,0:T(8,128)(2,1)}, bf16[2,192,512]{2,1,0:T(8,128)(2,1)S(1)}, u32[]{:S(2)}) copy-start(bf16[2,192,512]{2,1,0:T(8,128)(2,1)S(1)} %collective-permute-done.22.refs_1_) | copy-start | bytes 1179652
  128.5 4.4 %collective-permute-start.24 = (bf16[304,1024]{1,0:T(8,128)(2,1)S(1)}, bf16[304,1024]{1,0:T(8,128)(2,1)S(1)}, u32[]{:S(2)}, u32[]{:S(2)}) collective-permute-start(bf16[304,1024]{1,0:T(8,128)(2,1)S(1)} %get-tuple-element.167), channel_id=1, source_target_pairs={{0,1},{1,0},{2,3},{3,2},{4,5},{5,4},{6,7},{7,6},{8,9},{9,8},{10,11... | collective-permute-start | bytes 1867784 | tf_op jit(solution)/shard_map/ppermute | solution.py:665
  132.8 2.0 collective-permute-start.27
  133.0 16.5 %collective-permute-start.25 = (bf16[304,1024]{1,0:T(8,128)(2,1)S(1)}, bf16[304,1024]{1,0:T(8,128)(2,1)S(1)}, u32[]{:S(2)}, u32[]{:S(2)}) collective-permute-start(bf16[304,1024]{1,0:T(8,128)(2,1)S(1)} %pair_sum.7.refs_34_.refs_0_.refs_8_), channel_id=1, source_target_pairs={{0,2},{1,3},{2,0},{3,1},{4,6},{5,7},{6,4},{7,5},{8,10},{9,11},{10,... | collective-permute-start | bytes 1867784 | tf_op jit(solution)/shard_map/ppermute | solution.py:665
  133.7 11.9 %collective-permute-start.29 = (bf16[2,192,512]{2,1,0:T(8,128)(2,1)S(1)}, bf16[2,192,512]{2,1,0:T(8,128)(2,1)S(1)}, u32[]{:S(2)}, u32[]{:S(2)}) collective-permute-start(bf16[2,192,512]{2,1,0:T(8,128)(2,1)S(1)} %collective-permute-done.22.refs_1_), channel_id=1, source_target_pairs={{0,4},{4,0},{8,12},{12,8},{16,20},{20,16},{24,28},{28,24},{1,5},{5... | collective-permute-start | bytes 1179656 | tf_op jit(solution)/shard_map/ppermute | solution.py:665
  145.6 17.0 %copy-start.28 = (bf16[2,192,512]{2,1,0:T(8,128)(2,1)}, bf16[2,192,512]{2,1,0:T(8,128)(2,1)S(1)}, u32[]{:S(2)}) copy-start(bf16[2,192,512]{2,1,0:T(8,128)(2,1)S(1)} %collective-permute-done.29.refs_3_) | copy-start | bytes 1179652
  145.6 4.2 %collective-permute-start.30 = (bf16[256,1024]{1,0:T(8,128)(2,1)S(1)}, bf16[256,1024]{1,0:T(8,128)(2,1)S(1)}, u32[]{:S(2)}, u32[]{:S(2)}) collective-permute-start(bf16[256,1024]{1,0:T(8,128)(2,1)S(1)} %get-tuple-element.187), channel_id=1, source_target_pairs={{0,1},{1,0},{2,3},{3,2},{4,5},{5,4},{6,7},{7,6},{8,9},{9,8},{10,11... | collective-permute-start | bytes 1572872 | tf_op jit(solution)/shard_map/ppermute | solution.py:665
  149.7 3.2 %collective-permute-start.28 = (bf16[304,1024]{1,0:T(8,128)(2,1)S(1)}, bf16[304,1024]{1,0:T(8,128)(2,1)S(1)}, u32[]{:S(2)}, u32[]{:S(2)}) collective-permute-start(bf16[304,1024]{1,0:T(8,128)(2,1)S(1)} %far_sum.7.refs_13_), channel_id=1, source_target_pairs={{0,1},{1,0},{2,3},{3,2},{4,5},{5,4},{6,7},{7,6},{8,9},{9,8},{10,11... | collective-permute-start | bytes 1867784 | tf_op jit(solution)/shard_map/ppermute | solution.py:665
  149.8 12.8 %collective-permute-start.32 = (bf16[256,512]{1,0:T(8,128)(2,1)S(1)}, bf16[256,512]{1,0:T(8,128)(2,1)S(1)}, u32[]{:S(2)}, u32[]{:S(2)}) collective-permute-start(bf16[256,512]{1,0:T(8,128)(2,1)S(1)} %high_sum.5.refs_36_), channel_id=1, source_target_pairs={{0,2},{1,3},{2,0},{3,1},{4,6},{5,7},{6,4},{7,5},{8,10},{9,11},{10,... | collective-permute-start | bytes 786440 | tf_op jit(solution)/shard_map/ppermute | solution.py:665
  150.5 12.1 %collective-permute-start.31 = (bf16[1,48,1024]{2,1,0:T(8,128)(2,1)S(1)}, bf16[1,48,1024]{2,1,0:T(8,128)(2,1)S(1)}, u32[]{:S(2)}, u32[]{:S(2)}) collective-permute-start(bf16[1,48,1024]{2,1,0:T(8,128)(2,1)S(1)} %slice_bitcast_fusion), channel_id=1, source_target_pairs={{0,16},{4,20},{8,24},{12,28},{16,0},{20,4},{24,8},{28,12},{1,17},{... | collective-permute-start | bytes 294920 | tf_op jit(solution)/shard_map/ppermute | solution.py:665
  162.6 5.0 %collective-permute-start.35 = (bf16[256,1024]{1,0:T(8,128)(2,1)S(1)}, bf16[256,1024]{1,0:T(8,128)(2,1)S(1)}, u32[]{:S(2)}, u32[]{:S(2)}) collective-permute-start(bf16[256,1024]{1,0:T(8,128)(2,1)S(1)} %get-tuple-element.194), channel_id=1, source_target_pairs={{0,1},{1,0},{2,3},{3,2},{4,5},{5,4},{6,7},{7,6},{8,9},{9,8},{10,11... | collective-permute-start | bytes 1572872 | tf_op jit(solution)/shard_map/ppermute | solution.py:665
  162.7 2.2 collective-permute-start.33
  164.9 4.9 %collective-permute-start.34 = (bf16[96,512]{1,0:T(8,128)(2,1)S(1)}, bf16[96,512]{1,0:T(8,128)(2,1)S(1)}, u32[]{:S(2)}, u32[]{:S(2)}) collective-permute-start(bf16[96,512]{1,0:T(8,128)(2,1)S(1)} %high_sum.6.refs_2_), channel_id=1, source_target_pairs={{0,2},{1,3},{2,0},{3,1},{4,6},{5,7},{6,4},{7,5},{8,10},{9,11},{10,... | collective-permute-start | bytes 294920 | tf_op jit(solution)/shard_map/ppermute | solution.py:665
  166.4 7.1 %collective-permute-start.39 = (bf16[2,48,1024]{2,1,0:T(8,128)(2,1)S(1)}, bf16[2,48,1024]{2,1,0:T(8,128)(2,1)S(1)}, u32[]{:S(2)}, u32[]{:S(2)}) collective-permute-start(bf16[2,48,1024]{2,1,0:T(8,128)(2,1)S(1)} %pad_maximum_fusion.2), channel_id=1, source_target_pairs={{0,8},{4,12},{8,0},{12,4},{16,24},{20,28},{24,16},{28,20},{1,9},{5... | collective-permute-start | bytes 589832 | tf_op jit(solution)/shard_map/ppermute | solution.py:665
  167.7 10.0 %collective-permute-start.36 = (bf16[256,512]{1,0:T(8,128)(2,1)S(1)}, bf16[256,512]{1,0:T(8,128)(2,1)S(1)}, u32[]{:S(2)}, u32[]{:S(2)}) collective-permute-start(bf16[256,512]{1,0:T(8,128)(2,1)S(1)} %high_sum.7), channel_id=1, source_target_pairs={{0,2},{1,3},{2,0},{3,1},{4,6},{5,7},{6,4},{7,5},{8,10},{9,11},{10,... | collective-permute-start | bytes 786440 | tf_op jit(solution)/shard_map/ppermute | solution.py:665
  169.9 7.8 %collective-permute-start.37 = (bf16[1,112,512]{2,1,0:T(8,128)(2,1)S(1)}, bf16[1,112,512]{2,1,0:T(8,128)(2,1)S(1)}, u32[]{:S(2)}, u32[]{:S(2)}) collective-permute-start(bf16[1,112,512]{2,1,0:T(8,128)(2,1)S(1)} %maximum_bitcast_fusion), channel_id=1, source_target_pairs={{0,16},{4,20},{8,24},{12,28},{16,0},{20,4},{24,8},{28,12},{1,17},{... | collective-permute-start | bytes 344072 | tf_op jit(solution)/shard_map/ppermute | solution.py:665
  174.2 10.6 %collective-permute-start.40 = (bf16[4,48,1024]{2,1,0:T(8,128)(2,1)}, bf16[4,48,1024]{2,1,0:T(8,128)(2,1)}, u32[]{:S(2)}, u32[]{:S(2)}) collective-permute-start(bf16[4,48,1024]{2,1,0:T(8,128)(2,1)} %constant_dynamic-update-slice_fusion.2.refs_4_), channel_id=1, source_target_pairs={{0,4},{4,0},{8,12},{12,8},{16,20},{20,16},{24,28},{28,24},{1,5},{5... | collective-permute-start | bytes 1179656 | tf_op jit(solution)/shard_map/ppermute | solution.py:665
  177.7 7.2 %collective-permute-start.38 = (bf16[2,112,512]{2,1,0:T(8,128)(2,1)S(1)}, bf16[2,112,512]{2,1,0:T(8,128)(2,1)S(1)}, u32[]{:S(2)}, u32[]{:S(2)}) collective-permute-start(bf16[2,112,512]{2,1,0:T(8,128)(2,1)S(1)} %pad_maximum_fusion.1), channel_id=1, source_target_pairs={{0,8},{4,12},{8,0},{12,4},{16,24},{20,28},{24,16},{28,20},{1,9},{5... | collective-permute-start | bytes 688136 | tf_op jit(solution)/shard_map/ppermute | solution.py:665
  186.2 17.2 %all-to-all-start.1 = ((bf16[8,64,512]{2,1,0:T(8,128)(2,1)}), bf16[8,64,512]{2,1,0:T(8,128)(2,1)S(1)}, u32[]{:S(2)}, u32[]{:S(2)}) async-start(bf16[8,64,512]{2,1,0:T(8,128)(2,1)} %bitcast.13), calls=%async_computation.1 | async-start | bytes 1048576 | tf_op jit(solution)/shard_map/all_to_all | solution.py:816
  189.7 26.7 %collective-permute-start.41 = (bf16[4,112,512]{2,1,0:T(8,128)(2,1)S(1)}, bf16[4,112,512]{2,1,0:T(8,128)(2,1)}, u32[]{:S(2)}, u32[]{:S(2)}) collective-permute-start(bf16[4,112,512]{2,1,0:T(8,128)(2,1)S(1)} %constant_dynamic-update-slice_fusion.refs_14_.refs_0_), channel_id=1, source_target_pairs={{0,4},{4,0},{8,12},{12,8},{16,20},{20,16},{24,28},{28,24},{1,5},{5... | collective-permute-start | bytes 1376264 | tf_op jit(solution)/shard_map/ppermute | solution.py:665
  199.6 8.9 %collective-permute-start.42 = (bf16[4,48,1024]{2,1,0:T(8,128)(2,1)}, bf16[4,48,1024]{2,1,0:T(8,128)(2,1)S(1)}, u32[]{:S(2)}, u32[]{:S(2)}) collective-permute-start(bf16[4,48,1024]{2,1,0:T(8,128)(2,1)} %constant_dynamic-update-slice_fusion.2.refs_4_), channel_id=1, source_target_pairs={{0,1},{1,0},{2,3},{3,2},{4,5},{5,4},{6,7},{7,6},{8,9},{9,8},{10,11... | collective-permute-start | bytes 1179656 | tf_op jit(solution)/shard_map/ppermute | solution.py:665
  199.6 8.9 %collective-permute-start.43 = (bf16[4,48,1024]{2,1,0:T(8,128)(2,1)}, bf16[4,48,1024]{2,1,0:T(8,128)(2,1)S(1)}, u32[]{:S(2)}, u32[]{:S(2)}) collective-permute-start(bf16[4,48,1024]{2,1,0:T(8,128)(2,1)} %collective-permute-done.40.refs_15_.refs_5_), channel_id=1, source_target_pairs={{0,1},{1,0},{2,3},{3,2},{4,5},{5,4},{6,7},{7,6},{8,9},{9,8},{10,11... | collective-permute-start | bytes 1179656 | tf_op jit(solution)/shard_map/ppermute | solution.py:665
  203.4 22.2 %all-to-all-start.2 = ((bf16[8,64,512]{2,1,0:T(8,128)(2,1)}), bf16[8,64,512]{2,1,0:T(8,128)(2,1)S(1)}, u32[]{:S(2)}, u32[]{:S(2)}) async-start(bf16[8,64,512]{2,1,0:T(8,128)(2,1)} %bitcast.14), calls=%async_computation.2 | async-start | bytes 1048576 | tf_op jit(solution)/shard_map/all_to_all | solution.py:816
  207.0 11.0 %collective-permute-start.46 = (bf16[4,64,512]{2,1,0:T(8,128)(2,1)S(1)}, bf16[4,64,512]{2,1,0:T(8,128)(2,1)S(1)}, u32[]{:S(2)}, u32[]{:S(2)}) collective-permute-start(bf16[4,64,512]{2,1,0:T(8,128)(2,1)S(1)} %slice.34.refs_2_), channel_id=1, source_target_pairs={{0,2},{1,3},{2,0},{3,1},{4,6},{5,7},{6,4},{7,5},{8,10},{9,11},{10,... | collective-permute-start | bytes 786440 | tf_op jit(solution)/shard_map/ppermute | solution.py:665
  217.4 6.9 %collective-permute-start.47 = (bf16[4,64,512]{2,1,0:T(8,128)(2,1)S(1)}, bf16[4,64,512]{2,1,0:T(8,128)(2,1)S(1)}, u32[]{:S(2)}, u32[]{:S(2)}) collective-permute-start(bf16[4,64,512]{2,1,0:T(8,128)(2,1)S(1)} %slice.31.refs_3_), channel_id=1, source_target_pairs={{0,2},{1,3},{2,0},{3,1},{4,6},{5,7},{6,4},{7,5},{8,10},{9,11},{10,... | collective-permute-start | bytes 786440 | tf_op jit(solution)/shard_map/ppermute | solution.py:665
  218.1 9.0 %collective-permute-start.44 = (bf16[4,64,512]{2,1,0:T(8,128)(2,1)S(1)}, bf16[4,64,512]{2,1,0:T(8,128)(2,1)S(1)}, u32[]{:S(2)}, u32[]{:S(2)}) collective-permute-start(bf16[4,64,512]{2,1,0:T(8,128)(2,1)S(1)} %slice.34.refs_2_), channel_id=1, source_target_pairs={{0,1},{1,0},{2,3},{3,2},{4,5},{5,4},{6,7},{7,6},{8,9},{9,8},{10,11... | collective-permute-start | bytes 786440 | tf_op jit(solution)/shard_map/ppermute | solution.py:665
  218.1 9.0 %collective-permute-start.48 = (bf16[4,64,512]{2,1,0:T(8,128)(2,1)S(1)}, bf16[4,64,512]{2,1,0:T(8,128)(2,1)S(1)}, u32[]{:S(2)}, u32[]{:S(2)}) collective-permute-start(bf16[4,64,512]{2,1,0:T(8,128)(2,1)S(1)} %collective-permute-done.46.refs_6_), channel_id=1, source_target_pairs={{0,1},{1,0},{2,3},{3,2},{4,5},{5,4},{6,7},{7,6},{8,9},{9,8},{10,11... | collective-permute-start | bytes 786440 | tf_op jit(solution)/shard_map/ppermute | solution.py:665
  218.6 8.5 %collective-permute-start.45 = (bf16[4,64,512]{2,1,0:T(8,128)(2,1)S(1)}, bf16[4,64,512]{2,1,0:T(8,128)(2,1)S(1)}, u32[]{:S(2)}, u32[]{:S(2)}) collective-permute-start(bf16[4,64,512]{2,1,0:T(8,128)(2,1)S(1)} %slice.31.refs_3_), channel_id=1, source_target_pairs={{0,1},{1,0},{2,3},{3,2},{4,5},{5,4},{6,7},{7,6},{8,9},{9,8},{10,11... | collective-permute-start | bytes 786440 | tf_op jit(solution)/shard_map/ppermute | solution.py:665
  224.2 2.8 %collective-permute-start.49 = (bf16[4,64,512]{2,1,0:T(8,128)(2,1)S(1)}, bf16[4,64,512]{2,1,0:T(8,128)(2,1)}, u32[]{:S(2)}, u32[]{:S(2)}) collective-permute-start(bf16[4,64,512]{2,1,0:T(8,128)(2,1)S(1)} %collective-permute-done.47.refs_7_), channel_id=1, source_target_pairs={{0,1},{1,0},{2,3},{3,2},{4,5},{5,4},{6,7},{7,6},{8,9},{9,8},{10,11... | collective-permute-start | bytes 786440 | tf_op jit(solution)/shard_map/ppermute | solution.py:665
  (29 other events, 165.7 us)

commit v7 on v6

--- a/solution.py
+++ b/solution.py
@@ -195,10 +195,9 @@
     units = wd_in.shape[0]
     if chunk:
         wgu, wd = wgu_in, wd_in
-        outs, (f_s, value_s) = rest[-15:-2], rest[-2:]
     else:
-        outs, (wgu, wd, f_s, value_s, sems) = rest[-18:-5], rest[-5:]
-    xm_out, xq_out, h_out, g_out, act_out, dg_out, du_out, t2_s, dtd_s, b_out, y_keep, y_send, td_out = outs
+        (wgu, wd, f_s, sems), rest = rest[-4:], rest[:-4]
+        rest = (*rest, f_s)
 
     def copies(i):
         c = pl.ds(pl.multiple_of(i * QUARTER, QUARTER), QUARTER)
@@ -209,6 +208,8 @@
         for i in range(units // QUARTER):
             for copy in copies(i):
                 copy.start()
+    f_s = rest[-1]
+    xm_out, xq_out, h_out, g_out, act_out, dg_out, du_out, t2_s, dtd_s, b_out = rest[-11:-1]
     me, length = info[0], info[1]
     rows = h_out.shape[0]
     xs, gs = ([chunk_of(v, chunk, rows) for v in vs] for vs in ((x0, x1, x2, x3), (g0, g1, g2, g3)))
@@ -261,28 +262,19 @@
         return carry
 
     lax.fori_loop(0, units // QUARTER, block, 0)
-    td = nt(act_out[...], da[...])
-    td_out[...] = td
-    tdb = td.astype(BF16)
-
-    def down(r, carry):
-        at = quarter(me, r)
-        value_s[...] = nn(act_out[...], wd[:, at]) + nn(tdb, bd[:, at])
-        store_block(r, value_s, slice(0, rows), y_keep, y_send)
-        return carry
-
-    lax.fori_loop(0, PARTS, down, 0)
-
-
-def back_kernel(last, info, wgu, h, g, td, dg, du, a2, fb, *rest):
+
+
+def back_kernel(last, info, wgu, h, g, act, dg, du, a2, fb, da, *rest):
     (value_s, low_s), rest = rest[-2:], rest[:-2]
-    outs, rest = (rest[-2:], rest[:-2]) if last else (rest[-3:], rest[:-3])
-    d_keep, d_send = outs[:2]
+    outs, rest = (rest[-3:], rest[:-3]) if last else (rest[-4:], rest[:-4])
+    td_out, d_keep, d_send = outs[:3]
     me = info[0]
     rows = h.shape[0]
     dt2 = jnp.concatenate([nt(dg[...], fb[0]), nt(du[...], fb[1])], axis=1)
+    td = nt(act[...], da[...])
+    td_out[...] = td
     dt2b = dt2.astype(BF16)
-    dt2t, tdt = dt2.T.astype(BF16), td[...].T.astype(BF16)
+    dt2t, tdt = dt2.T.astype(BF16), td.T.astype(BF16)
 
     def block(r, carry):
         at = quarter(me, r)
@@ -294,10 +286,24 @@
             low_s[...] += rest[0][:, at]
             store_block(r, low_s, slice(rows, rows + 3 * RANK), d_keep, d_send)
         else:
-            outs[2][:, at] = low_s[...]
+            outs[3][:, at] = low_s[...]
         return carry
 
     lax.fori_loop(0, PARTS, block, 0)
+
+
+def down_kernel(info, wd, act, td, bd, xq, y_keep, y_send, value_s):
+    me = info[0]
+    tdb = td[...].astype(BF16)
+
+    def block(r, carry):
+        at = quarter(me, r)
+        value_s[...] = nn(act[...], wd[:, at]) + nn(tdb, bd[:, at])
+        store_block(r, value_s, slice(0, act.shape[0]), y_keep, y_send)
+        return carry
+
+    lax.fori_loop(0, PARTS, block, 0)
+    y_keep[:, LO] += xq[...]
 
 
 def attend_back_kernel(chunk, last, info, wq_h, wkv_h, wo_h, x0, x1, x2, x3, g0, g1, g2, g3, xm, do_, dp, gains, a1,
@@ -430,10 +436,10 @@
     out = refs[-1]
     rows = out.shape[0] // CHUNKS
     for c in range(CHUNKS):
-        xq, y_keep, y_got = refs[3 * c:3 * (c + 1)]
+        y_keep, y_got = refs[2 * c:2 * (c + 1)]
         at = slice(c * rows, (c + 1) * rows)
         valid = c * rows + lax.broadcasted_iota(jnp.int32, (rows, 1), 0) < info[1]
-        y = xq[...] + y_keep[:, LO] + y_got[:, LO].astype(F32) + y_far[at, :].astype(F32)
+        y = y_keep[:, LO] + y_got[:, LO].astype(F32) + y_far[at, :].astype(F32)
         out[at, :] = jnp.where(valid, y, 0.0).astype(BF16)
 
 
@@ -691,8 +697,10 @@
     out[...] = (keep[...] + got[...].astype(F32)).astype(BF16)
 
 
-def pair_sum(keep, send):
-    return call(pair_sum_kernel, None, (), (keep, near(send)), [(send.shape, BF16)], [], "pair_sum", 6)[0]
+def pair_sum(keep, send, *before):
+    got = near(send)
+    got = late(got, *before) if before else got
+    return call(pair_sum_kernel, None, (), (keep, got), [(send.shape, BF16)], [], "pair_sum", 6)[0]
 
 
 def late(value, *others):
@@ -779,23 +787,25 @@
         hidden = (rows, units)
         outs = [(wide, BF16), (block, F32), (wide, BF16), (wide, BF16), (hidden, BF16), (hidden, BF16), (hidden, BF16),
                 ((rows, 2 * RANK), BF16), ((rows, RANK), BF16),
-                ((3 * RANK * units // QUARTER, QUARTER), BF16 if c else F32),
-                (col, F32), (col, BF16), ((rows, RANK), F32)]
+                ((3 * RANK * units // QUARTER, QUARTER), BF16 if c else F32)]
         args = (*xs[c], total, near(total), *gs, gains, a2, bd, fba, da, *partial)
         weights = () if c else (gate_up_matrix, down_matrix)
         outs += like(*weights)
         return call(
             functools.partial(front_kernel, c, c == CHUNKS - 1), info, weights, (wgu, wd, *args) if c else args, outs,
-            [((ROW_BLOCK, WIDTH), F32), (block, F32)], "front_%d" % c, 8, order, () if c else (2, units // QUARTER))
+            [((ROW_BLOCK, WIDTH), F32)], "front_%d" % c, 8, order, () if c else (2, units // QUARTER))
 
     def back(c, hidden, partial, order):
         first = col if c else (rows + 3 * RANK, half)
-        outs = [(first, F32), (first, BF16)]
+        outs = [((rows, RANK), F32), (first, F32), (first, BF16)]
         outs += [((3 * RANK, WIDTH), F32)] if c else []
-        _, _, h2, g2, _, dg, du = hidden[:7]
         return call(
-            functools.partial(back_kernel, c == 0), info, (), (wgu, h2, g2, hidden[12], dg, du, a2, fba, *partial), outs,
+            functools.partial(back_kernel, c == 0), info, (), (wgu, *hidden[2:7], a2, fba, da, *partial), outs,
             [(block, F32), ((3 * RANK, QUARTER), F32)], "back_%d" % c, 8, order)
+
+    def down(c, td, order):
+        return call(down_kernel, info, (), (wd, hidden[c][4], td, bd, hidden[c][1]), [(col, F32), (col, BF16)],
+                    [(block, F32)], "down_%d" % c, 6, order)
 
     def attend_back(c, total, partial, order):
         outs = [(block, F32), (col, F32), (col, BF16), (thin, F32), ((3 * RANK, QUARTER), F32 if c else BF16)]
@@ -820,32 +830,28 @@
         return move_rows(collect_kernel, value, late(dealing_slots, *before), name, [rows_out], pltpu.VMEM, pl.ANY,
                          (seqs,))[0]
 
-    hidden, d_own, d_far = ([None] * CHUNKS for _ in range(3))
+    hidden, d_own, d_far, y_keep, y_got = ([None] * CHUNKS for _ in range(5))
     *hidden[0], wgu, wd = front(0, far_sum(z_own[0], z_far[0]), (), order)
     step = hidden[0][8]
-    hidden[1] = front(1, far_sum(z_own[1], late(z_far[1], step)), hidden[0][9:10], (step,))
-    y_keep, y_got = [h[10] for h in hidden], [near(h[11]) for h in hidden]
-    y_high = high_sum(*zip(y_keep, y_got))
-    y_far = far(y_high)
+    hidden[1] = front(1, far_sum(z_own[1], late(z_far[1], step)), hidden[0][9:], (step,))
     fb = hidden[1][9][None]
     fb_first = swap(fb, bits[0], "dp", dp)
-    d_keep, d_send, fa = back(1, hidden[1], (), (y_high,))
-    ready = (fb_first, y_far)
-    d_own[1] = pair_sum(d_keep, late(d_send, *ready))
+    td, d_keep, d_send, fa = back(1, hidden[1], (), (hidden[1][8],))
+    d_own[1] = pair_sum(d_keep, late(d_send, fb_first))
     d_far[1] = far(d_own[1])
     fb = fb_more = jnp.concatenate([fb, fb_first], axis=0)
     for bit in bits[1:-1]:
         fb_more = doubled(fb_more, bit, dp)
     fb_more = fb_more[2:]
     fb_side = swap(fb, bits[-1], "dp", dp)
-    d_keep, d_send = back(0, hidden[0], (fa,), (d_own[1],))
-    total = far_sum(d_own[1], late(d_far[1], d_send))
-    d_own[0] = pair_sum(d_keep, late(d_send, fb_more, fb_side))
+    td_0, d_keep, d_send = back(0, hidden[0], (fa,), (d_own[1],))
+    y_keep[1], y_send = down(1, td, (td_0,))
+    total = far_sum(d_own[1], late(d_far[1], y_send))
+    d_own[0] = pair_sum(d_keep, late(d_send, fb_more, fb_side), total)
     d_far[0] = far(d_own[0])
     fb_more_side = swap(fb_more, bits[-1], "dp", dp)
-    parts = [v for c in range(CHUNKS) for v in (hidden[c][1], y_keep[c], y_got[c])]
-    result, = call(output_kernel, info, (), (y_far, *parts), [((length, QUARTER), BF16)], [], "output", 8, (d_own[0],))
-    dxq, h_keep, h_send, inv, *sums = attend_back(1, total, (), (d_own[0],))
+    y_got[1] = near(late(y_send, d_own[0]))
+    dxq, h_keep, h_send, inv, *sums = attend_back(1, total, (), (d_own[0], y_send))
     total = far_sum(d_own[0], late(d_far[0], inv))
     h_got = near(late(h_send, fb_more_side))
     h_high = high_sum((h_keep, h_got))
@@ -866,19 +872,24 @@
     att_a = (att_a + late(aa_far, h_high)[:4 * RANK].astype(F32)).astype(BF16)
     n_b = att_b.shape[0]
     att = jnp.concatenate([att_b, att_a], axis=0)[None]
+    y_keep[0], y_send = down(0, td_0, (att,))
+    y_got[0] = near(y_send)
     att = doubled(att, bits[0], dp)
-    att = late(att, h_far)
+    att = late(att, h_far, y_send)
     for bit in bits[1:-1]:
         att = doubled(att, bit, dp)
     fa = late(jnp.concatenate([fa, fa_first], axis=0), aa_high)
     for bit in bits[1:-1]:
         fa = doubled(fa, bit, dp)
     fa_side = swap(fa, bits[-1], "dp", dp)
+    y_far = far(high_sum(*((k, late(g, h_far)) for k, g in zip(y_keep, y_got))))
 
     dinput, = call(finish_kernel, None, (), (gains, dealt, aa_high, aa_far, *(v for f in final for v in f)),
                    [((length, QUARTER), BF16)], [], "finish", 8, (att, fa_side))
     input_grad = collect(to_bands(dinput), "collect_grad")
-    output = collect(to_bands(late(result, dinput)), "collect_out", input_grad)
+    result, = call(output_kernel, info, (), (late(y_far, dinput), *(v for p in zip(y_keep, y_got) for v in p)),
+                   [((length, QUARTER), BF16)], [], "output", 8)
+    output = collect(to_bands(result), "collect_out", input_grad)
 
     outs = [sds((adapters, 2 * RANK, WIDTH), F32), sds((adapters, RANK, WIDTH), F32),
             sds((adapters, 2, RANK, units), F32), sds((adapters, RANK, units), F32)]
@@ -887,9 +898,9 @@
         ((fb, fb_more, fb_side, fb_more_side), (fa, fa_side), (near(fa), near(fa_side))), outs, "feedforward_sum")
 
     att_side = swap(att, bits[-1], "dp", dp)
-    att_side = late(att_side, g_down_a)
     a_parts = [att[:, n_b:], att_side[:, n_b:]]
     a_far = [far(v) for v in a_parts]
+    a_far[1] = late(a_far[1], g_down_a)
     outs = [sds((adapters, 3 * RANK, WIDTH), F32), sds((adapters, RANK, WIDTH), F32),
             sds((adapters, RANK, q_cols), F32), sds((adapters, 2, RANK, kv_cols), F32),
             sds((adapters, RANK, q_cols), F32)]

time: 233 us -> 223 us (0.957)
  waiting for transfers between devices: 65.2 us -> 55.2 us
  local copies, waits for them, and re-layouts: 13.4 us -> 8.27 us
  starting transfers between devices: 44.7 us -> 48.7 us
    ppermute x50, waiting for transfers between devices: 61.9 us -> 55.2 us  [swap(): return lax.ppermute(value, axis, [(i, i ^ bit) for i in range(size)])]
    unnamed x82 -> x150, local copies, waits for them, and re-layouts: 11.6 us -> 7.2 us
    all_to_all x2, waiting for transfers between devices: 3.25 us -> 0.01 us  [to_bands(): lax.all_to_all(value.reshape(dp, length // dp, QUARTER), 'dp', split_axis...]
    all_to_all x2, starting transfers between devices: 7.11 us -> 9.78 us  [to_bands(): lax.all_to_all(value.reshape(dp, length // dp, QUARTER), 'dp', split_axis...]
    pallas_call x24 -> x26, Pallas kernels: 88.2 us -> 90.5 us  [call(): pl.pallas_call(body, in_specs=[pl.BlockSpec(memory_space=pltpu.SMEM)] * n...]
  transfers between devices with their start and end apart: 53 -> 53, of which waited for: 25 -> 23; matrix products, arithmetic and copies ran while one was open for 2% -> 2% of each run, Pallas kernels for 41% -> 40%
where the time goes in v7:
time: 223 us; the launch traced here: 222 us
  Pallas kernels  106 us (48%)
  waiting for transfers between devices  55.2 us (25%)
  starting transfers between devices  48.7 us (22%)
  local copies, waits for them, and re-layouts  8.27 us (4%)
  other arithmetic  2.31 us (1%)
    pallas_call x26, Pallas kernels, call(): pl.pallas_call(body, in_specs=[pl.BlockSpec(memory_space=pltpu.SMEM)] * n...  90.5 us
    ppermute x50, waiting for transfers between devices, swap(): return lax.ppermute(value, axis, [(i, i ^ bit) for i in range(size)])  55.2 us
    ppermute x50, starting transfers between devices, swap(): return lax.ppermute(value, axis, [(i, i ^ bit) for i in range(size)])  31.7 us
    all_to_all x2, starting transfers between devices, to_bands(): lax.all_to_all(value.reshape(dp, length // dp, QUARTER), 'dp', split_axis...  9.78 us
    pallas_call x2, Pallas kernels, sum_call(): pl.pallas_call(functools.partial(kernel, [len(group) for group in groups]...  8.34 us
    all_to_all x1, starting transfers between devices, shards(): lax.all_to_all(ordered, 'dp', split_axis=0, concat_axis=1, tiled=True)[0]  7.26 us
    unnamed x150, local copies, waits for them, and re-layouts  7.2 us
    pallas_call x3, Pallas kernels, move_rows(): pl.pallas_call(kernel, in_specs=[pl.BlockSpec(memory_space=pltpu.SMEM), p...  5.25 us
  transfers between devices with their start and end apart: 53, of which 23 were waited for; matrix products, arithmetic and copies ran while one was open for 2% of the time, Pallas kernels for 40%

profile of v7, /device:TPU:0, one launch (start us, length us, event | category | flops | bytes accessed | tf_op | source)
XLA Modules:
  0.0 222.3 jit_solution(16939661139362481110)
XLA Ops:
  0.7 0.7 copy-done.64
  1.4 2.5 %deal.1 = bf16[8,64,512]{2,1,0:T(8,128)(2,1)} custom-call(s32[8]{0:T(128)S(1)} %copy-done.64, bf16[8,64,512]{2,1,0:T(8,128)(2,1)} %source.1), custom_call_target="tpu_custom_call" | custom-call | flops 1000 | bytes 1000 | tf_op jit(solution)/shard_map/deal/pallas_call | solution.py:599
  3.9 7.3 %all-to-all-start = ((bf16[8,64,512]{2,1,0:T(8,128)(2,1)}), bf16[8,64,512]{2,1,0:T(8,128)(2,1)S(1)}, u32[]{:S(2)}, u32[]{:S(2)}) async-start(bf16[8,64,512]{2,1,0:T(8,128)(2,1)} %deal.1), calls=%async_computation | async-start | bytes 1048576 | tf_op jit(solution)/shard_map/all_to_all | solution.py:750
  11.3 1.6 collective-permute-start.1
  14.2 0.7 collective-permute-done.1
  14.9 1.4 pad_add_fusion.info.refs_0_
  16.3 1.8 adapters.1
  19.4 7.4 %collective-permute-done.3.refs_11_.refs_10_ = bf16[512,512]{1,0:T(8,128)(2,1)S(1)} collective-permute-done((bf16[512,512]{1,0:T(8,128)(2,1)S(1)}, bf16[512,512]{1,0:T(8,128)(2,1)S(1)}, u32[]{:S(2)}, u32[]{:S(2)}) %collective-permute-start.3) | collective-permute-done | bytes 524320 | tf_op jit(solution)/shard_map/ppermute | solution.py:671
  27.5 7.0 %collective-permute-done.5.refs_5_.refs_6_ = bf16[256,512]{1,0:T(8,128)(2,1)S(1)} collective-permute-done((bf16[256,512]{1,0:T(8,128)(2,1)S(1)}, bf16[256,512]{1,0:T(8,128)(2,1)S(1)}, u32[]{:S(2)}, u32[]{:S(2)}) %collective-permute-start.5) | collective-permute-done | bytes 262176 | tf_op jit(solution)/shard_map/ppermute | solution.py:671
  35.1 1.0 collective-permute-done.6.refs_6_.refs_7_
  36.1 4.1 %project_0.1 = (bf16[48,256]{1,0:T(8,128)(2,1)S(1)}, bf16[512,256]{1,0:T(8,128)(2,1)S(1)}, bf16[2,256,64]{2,1,0:T(8,128)(2,1)S(1)}, bf16[2,256,64]{2,1,0:T(8,128...) custom-call(s32[4]{0:T(128)S(1)} %pad_add_fusion.info.refs_0_, bf16[2048,512]{1,0:T(8,128)(2,1)} %refs_1_.15, ...), custom_call_target="tpu_custom_call" | custom-call | flops 1000 | bytes 1000 | tf_op jit(solution)/shard_map/project_0/pallas_call | solution.py:632
  40.2 3.1 %attend_0.1 = (f32[256,1024]{1,0:T(8,128)S(1)}, bf16[256,1024]{1,0:T(8,128)(2,1)S(1)}, bf16[512,256]{1,0:T(8,128)(2,1)S(1)}, f32[8,256]{1,0:T(8,128)S(1)}, bf16[16,256]{1,0:T(8,128)(2,1)S(1)}) custom-call(s32[4]{0:T(128)S(1)} %pad_add_fusion.info.refs_0_, bf16[512,2048]{1,0:T(8,128)(2,1)} %refs_3_.5, ...), custom_call_target="tpu_custom_call" | custom-call | flops 1000 | bytes 1000 | tf_op jit(solution)/shard_map/attend_0/pallas_call | solution.py:632
  43.5 1.8 collective-permute-done.10.refs_1_
  46.0 1.5 collective-permute-done.13.refs_6_.refs_7_
  47.6 4.1 %project_1.1 = (bf16[48,256]{1,0:T(8,128)(2,1)S(1)}, bf16[512,256]{1,0:T(8,128)(2,1)S(1)}, bf16[2,256,64]{2,1,0:T(8,128)(2,1)S(1)}, bf16[2,256,64]{2,1,0:T(8,128...) custom-call(s32[4]{0:T(128)S(1)} %pad_add_fusion.info.refs_0_, bf16[2048,512]{1,0:T(8,128)(2,1)} %refs_1_.15, ...), custom_call_target="tpu_custom_call" | custom-call | flops 1000 | bytes 1000 | tf_op jit(solution)/shard_map/project_1/pallas_call | solution.py:632
  51.8 3.7 %attend_1.1 = (f32[256,1024]{1,0:T(8,128)S(1)}, bf16[256,1024]{1,0:T(8,128)(2,1)S(1)}, bf16[512,256]{1,0:T(8,128)(2,1)S(1)}, f32[8,256]{1,0:T(8,128)S(1)}, bf16[16,256]{1,0:T(8,128)(2,1)S(1)}) custom-call(s32[4]{0:T(128)S(1)} %pad_add_fusion.info.refs_0_, bf16[512,2048]{1,0:T(8,128)(2,1)} %refs_3_.5, ...), custom_call_target="tpu_custom_call" | custom-call | flops 1000 | bytes 1000 | tf_op jit(solution)/shard_map/attend_1/pallas_call | solution.py:632
  55.5 3.9 %collective-permute-done.11.refs_1_ = bf16[256,1024]{1,0:T(8,128)(2,1)S(1)} collective-permute-done((bf16[256,1024]{1,0:T(8,128)(2,1)S(1)}, bf16[256,1024]{1,0:T(8,128)(2,1)S(1)}, u32[]{:S(2)}, u32[]{:S(2)}) %collective-permute-start.11) | collective-permute-done | bytes 524320 | tf_op jit(solution)/shard_map/ppermute | solution.py:671
  62.2 0.7 collective-permute-done.8.refs_12_.refs_11_
  62.8 0.7 collective-permute-done.12.refs_8_
  63.6 13.0 %front_0.1 = (bf16[256,2048]{1,0:T(8,128)(2,1)S(1)}, f32[256,512]{1,0:T(8,128)S(1)}, bf16[256,2048]{1,0:T(8,128)(2,1)S(1)}, bf16[256,2048]{1,0:T(8,128)(2,1)S(1)...) custom-call(s32[4]{0:T(128)S(1)} %pad_add_fusion.info.refs_0_, ...), custom_call_target="tpu_custom_call" | custom-call | flops 1000 | bytes 1000 | tf_op jit(solution)/shard_map/front_0/pallas_call | solution.py:632
  76.6 1.0 copy-done.24
  77.9 1.8 collective-permute-done.16.refs_8_
  79.7 12.0 %front_1.1 = (bf16[256,2048]{1,0:T(8,128)(2,1)S(1)}, f32[256,512]{1,0:T(8,128)S(1)}, bf16[256,2048]{1,0:T(8,128)(2,1)S(1)}, bf16[256,2048]{1,0:T(8,128)(2,1)S(1)...) custom-call(s32[4]{0:T(128)S(1)} %pad_add_fusion.info.refs_0_, ...), custom_call_target="tpu_custom_call" | custom-call | flops 1000 | bytes 1000 | tf_op jit(solution)/shard_map/front_1/pallas_call | solution.py:632
  91.7 3.0 %collective-permute-start.17 = (bf16[1,192,512]{2,1,0:T(8,128)(2,1)S(1)}, bf16[1,192,512]{2,1,0:T(8,128)(2,1)S(1)}, u32[]{:S(2)}, u32[]{:S(2)}) collective-permute-start(bf16[1,192,512]{2,1,0:T(8,128)(2,1)S(1)} %bitcast.36), channel_id=1, source_target_pairs={{0,16},{4,20},{8,24},{12,28},{16,0},{20,4},{24,8},{28,12},{1,17},{... | collective-permute-start | bytes 589832 | tf_op jit(solution)/shard_map/ppermute | solution.py:671
  94.7 7.9 %back_1.1 = (f32[256,16]{1,0:T(8,128)S(1)}, f32[256,1024]{1,0:T(8,128)S(1)}, bf16[256,1024]{1,0:T(8,128)(2,1)S(1)}, f32[48,2048]{1,0:T(8,128)S(1)}) custom-call(s32[4]{0:T(128)S(1)} %pad_add_fusion.info.refs_0_, bf16[2,2048,2048]{2,1,0:T(8,128)(2,1)S(1)} %get-tuple-element.148.refs_1_, bf16[256,2048]{1,0:T(8,128)(2,1)S(1)} %get-tuple-element.158.refs_2_, ...), custom_call_target="tpu_custom_call" | custom-call | flops 1000 | bytes 1000 | tf_op jit(solution)/shard_map/back_1/pallas_call | solution.py:632
  102.6 1.5 collective-permute-done.17
  104.2 1.8 collective-permute-start.20
  106.5 0.7 collective-permute-start.22
  107.2 7.9 %back_0.1 = (f32[256,16]{1,0:T(8,128)S(1)}, f32[304,1024]{1,0:T(8,128)S(1)}, bf16[304,1024]{1,0:T(8,128)(2,1)S(1)}) custom-call(s32[4]{0:T(128)S(1)} %pad_add_fusion.info.refs_0_, bf16[2,2048,2048]{2,1,0:T(8,128)(2,1)S(1)} %get-tuple-element.148.refs_1_, bf16[256,2048]{1,0:T(8,128)(2,1)S(1)} %get-tuple-element.149.refs_2_, ...), custom_call_target="tpu_custom_call" | custom-call | flops 1000 | bytes 1000 | tf_op jit(solution)/shard_map/back_0/pallas_call | solution.py:632
  115.1 0.7 collective-permute-done.20.refs_2_
  115.8 1.4 collective-permute-done.19.refs_1_
  117.3 4.5 %down_1.1 = (f32[256,1024]{1,0:T(8,128)S(1)}, bf16[256,1024]{1,0:T(8,128)(2,1)}) custom-call(s32[4]{0:T(128)S(1)} %pad_add_fusion.info.refs_0_, bf16[2048,2048]{1,0:T(8,128)(2,1)S(1)} %bitcast.19, bf16[256,2048]{1,0:T(8,128)(2,1)S(1)} %get-tuple-element.160.refs_4_.refs_2_, f32[256,16]{1,0:T(8,128)S(1)} %get-tuple-element.172.refs_3_, ...), custom_call_target="tpu_custom_call" | custom-call | flops 1000 | bytes 1000 | tf_op jit(solution)/shard_map/down_1/pallas_call | solution.py:632
  124.2 10.7 %attend_back_1.1 = (f32[256,512]{1,0:T(8,128)S(1)}, f32[256,1024]{1,0:T(8,128)S(1)}, bf16[256,1024]{1,0:T(8,128)(2,1)S(1)}, f32[256,1]{1,0:T(8,128)S(1)}, f32[48...) custom-call(s32[4]{0:T(128)S(1)} %pad_add_fusion.info.refs_0_, ...), custom_call_target="tpu_custom_call" | custom-call | flops 1000 | bytes 1000 | tf_op jit(solution)/shard_map/attend_back_1/pallas_call | solution.py:632
  135.5 3.8 %collective-permute-done.23.refs_1_ = bf16[304,1024]{1,0:T(8,128)(2,1)S(1)} collective-permute-done((bf16[304,1024]{1,0:T(8,128)(2,1)S(1)}, bf16[304,1024]{1,0:T(8,128)(2,1)S(1)}, u32[]{:S(2)}, u32[]{:S(2)}) %collective-permute-start.23) | collective-permute-done | bytes 622624 | tf_op jit(solution)/shard_map/ppermute | solution.py:671
  140.3 2.3 %collective-permute-start.28 = (bf16[1,48,1024]{2,1,0:T(8,128)(2,1)S(1)}, bf16[1,48,1024]{2,1,0:T(8,128)(2,1)S(1)}, u32[]{:S(2)}, u32[]{:S(2)}) collective-permute-start(bf16[1,48,1024]{2,1,0:T(8,128)(2,1)S(1)} %slice_bitcast_fusion), channel_id=1, source_target_pairs={{0,16},{4,20},{8,24},{12,28},{16,0},{20,4},{24,8},{28,12},{1,17},{... | collective-permute-start | bytes 294920 | tf_op jit(solution)/shard_map/ppermute | solution.py:671
  142.6 9.8 %attend_back_0.1 = (f32[256,512]{1,0:T(8,128)S(1)}, f32[256,1024]{1,0:T(8,128)S(1)}, bf16[256,1024]{1,0:T(8,128)(2,1)S(1)}, f32[256,1]{1,0:T(8,128)S(1)}, bf16[4...) custom-call(s32[4]{0:T(128)S(1)} %pad_add_fusion.info.refs_0_, ...), custom_call_target="tpu_custom_call" | custom-call | flops 1000 | bytes 1000 | tf_op jit(solution)/shard_map/attend_back_0/pallas_call | solution.py:632
  153.1 1.7 collective-permute-done.30.refs_1_
  154.7 1.3 collective-permute-start.31
  156.1 1.7 collective-permute-start.36
  158.6 1.1 collective-permute-done.31.refs_3_
  159.7 1.3 collective-permute-start.34
  161.0 2.9 %collective-permute-done.36 = bf16[2,48,1024]{2,1,0:T(8,128)(2,1)S(1)} collective-permute-done((bf16[2,48,1024]{2,1,0:T(8,128)(2,1)S(1)}, bf16[2,48,1024]{2,1,0:T(8,128)(2,1)S(1)}, u32[]{:S(2)}, u32[]{:S(2)}) %collective-permute-start.36) | collective-permute-done | bytes 196640 | tf_op jit(solution)/shard_map/ppermute | solution.py:671
  164.5 4.5 %down_0.1 = (f32[256,1024]{1,0:T(8,128)S(1)}, bf16[256,1024]{1,0:T(8,128)(2,1)}) custom-call(s32[4]{0:T(128)S(1)} %pad_add_fusion.info.refs_0_, bf16[2048,2048]{1,0:T(8,128)(2,1)S(1)} %bitcast.19, bf16[256,2048]{1,0:T(8,128)(2,1)S(1)} %copy-done.3, f32[256,16]{1,0:T(8,128)S(1)} %get-tuple-element.174.refs_6_.refs_3_, ...), custom_call_target="tpu_custom_call" | custom-call | flops 1000 | bytes 1000 | tf_op jit(solution)/shard_map/down_0/pallas_call | solution.py:632
  169.1 1.8 collective-permute-start.35
  171.5 3.7 %collective-permute-done.35 = bf16[2,112,512]{2,1,0:T(8,128)(2,1)S(1)} collective-permute-done((bf16[2,112,512]{2,1,0:T(8,128)(2,1)S(1)}, bf16[2,112,512]{2,1,0:T(8,128)(2,1)S(1)}, u32[]{:S(2)}, u32[]{:S(2)}) %collective-permute-start.35) | collective-permute-done | bytes 229408 | tf_op jit(solution)/shard_map/ppermute | solution.py:671
  175.8 0.8 copy-done.16
  176.6 3.9 %all-to-all-start.1 = ((bf16[8,64,512]{2,1,0:T(8,128)(2,1)}), bf16[8,64,512]{2,1,0:T(8,128)(2,1)S(1)}, u32[]{:S(2)}, u32[]{:S(2)}) async-start(bf16[8,64,512]{2,1,0:T(8,128)(2,1)} %bitcast.35), calls=%async_computation.1 | async-start | bytes 1048576 | tf_op jit(solution)/shard_map/all_to_all | solution.py:826
  180.6 1.3 high_sum.7
  181.9 0.9 collective-permute-start.40
  182.7 2.0 collective-permute-start.41
  184.7 7.4 %collective-permute-done.40.refs_1_ = bf16[512,512]{1,0:T(8,128)(2,1)S(1)} collective-permute-done((bf16[512,512]{1,0:T(8,128)(2,1)S(1)}, bf16[512,512]{1,0:T(8,128)(2,1)S(1)}, u32[]{:S(2)}, u32[]{:S(2)}) %collective-permute-start.40) | collective-permute-done | bytes 524320 | tf_op jit(solution)/shard_map/ppermute | solution.py:671
  192.2 2.2 output.1
  194.4 5.9 %all-to-all-start.2 = ((bf16[8,64,512]{2,1,0:T(8,128)(2,1)}), bf16[8,64,512]{2,1,0:T(8,128)(2,1)S(1)}, u32[]{:S(2)}, u32[]{:S(2)}) async-start(bf16[8,64,512]{2,1,0:T(8,128)(2,1)} %bitcast.14), calls=%async_computation.2 | async-start | bytes 1048576 | tf_op jit(solution)/shard_map/all_to_all | solution.py:826
  200.8 1.3 collective-permute-start.44
  202.1 1.0 slice.35.refs_3_
  203.1 0.8 collective-permute-start.45
  204.0 1.0 copy-done.39
  205.0 1.0 copy-done.41
  206.0 1.0 copy-done.43
  207.0 3.9 %feedforward_sum.1 = (f32[8,32,2048]{2,1,0:T(8,128)}, f32[8,16,2048]{2,1,0:T(8,128)}, f32[8,2,16,2048]{3,2,1,0:T(8,128)}, f32[8,16,2048]{2,1,0:T(8,128)}) custom-call(s32[4]{0:T(128)S(1)} %pad_add_fusion.info.refs_0_, s32[8]{0:T(128)S(1)} %copy-done.67, bf16[2,192,512]{2,1,0:T(8,128)(2,1)S(1)} %copy-done.18, bf16[2,192,512]{2,1,0:T(8,128)(2,1)S(1)} %copy-done.41, ...), custom_call_target="tpu_custom_call" | custom-call | bytes 12000000 | tf_op jit(solution)/shard_map/feedforward_sum/pallas_call | solution.py:655
  211.5 3.3 %collective-permute-done.45.refs_7_ = bf16[4,64,512]{2,1,0:T(8,128)(2,1)S(1)} collective-permute-done((bf16[4,64,512]{2,1,0:T(8,128)(2,1)S(1)}, bf16[4,64,512]{2,1,0:T(8,128)(2,1)S(1)}, u32[]{:S(2)}, u32[]{:S(2)}) %collective-permute-start.45) | collective-permute-done | bytes 262176 | tf_op jit(solution)/shard_map/ppermute | solution.py:671
  214.8 1.4 collect_grad.1
  216.3 4.4 %attention_sum.1 = (f32[8,48,2048]{2,1,0:T(8,128)}, f32[8,16,2048]{2,1,0:T(8,128)}, f32[8,16,512]{2,1,0:T(8,128)}, f32[8,2,16,128]{3,2,1,0:T(8,128)}, f32[8,16,512]{2,1,0:T(8,128)}) custom-call(s32[4]{0:T(128)S(1)} %pad_add_fusion.info.refs_0_, s32[8]{0:T(128)S(1)} %copy-done.67, bf16[4,112,512]{2,1,0:T(8,128)(2,1)S(1)} %constant_dynamic-update-slice_fusion.refs_14_.refs_0_, ...), custom_call_target="tpu_custom_call" | custom-call | bytes 12000000 | tf_op jit(solution)/shard_map/attention_sum/pallas_call | solution.py:655
  220.8 1.4 collect_out.1
  (244 shorter events, 16.6 us)
Async XLA Ops:
  3.9 23.0 %all-to-all-start = ((bf16[8,64,512]{2,1,0:T(8,128)(2,1)}), bf16[8,64,512]{2,1,0:T(8,128)(2,1)S(1)}, u32[]{:S(2)}, u32[]{:S(2)}) async-start(bf16[8,64,512]{2,1,0:T(8,128)(2,1)} %deal.1), calls=%async_computation | async-start | bytes 1048576 | tf_op jit(solution)/shard_map/all_to_all | solution.py:750
  11.2 8.2 %collective-permute-start = (bf16[2,512]{1,0:T(2,128)(2,1)S(1)}, bf16[2,512]{1,0:T(2,128)(2,1)S(1)}, u32[]{:S(2)}, u32[]{:S(2)}) collective-permute-start(bf16[2,512]{1,0:T(2,128)(2,1)S(1)} %pad_maximum_fusion.4), channel_id=1, source_target_pairs={{0,1},{1,0},{2,3},{3,2},{4,5},{5,4},{6,7},{7,6},{8,9},{9,8},{10,11... | collective-permute-start | bytes 6152 | tf_op jit(solution)/shard_map/ppermute | solution.py:671
  11.3 3.7 %collective-permute-start.1 = (bf16[2,512]{1,0:T(2,128)(2,1)S(1)}, bf16[2,512]{1,0:T(2,128)(2,1)S(1)}, u32[]{:S(2)}, u32[]{:S(2)}) collective-permute-start(bf16[2,512]{1,0:T(2,128)(2,1)S(1)} %pad_maximum_fusion.4), channel_id=1, source_target_pairs={{0,2},{1,3},{2,0},{3,1},{4,6},{5,7},{6,4},{7,5},{8,10},{9,11},{10,... | collective-permute-start | bytes 6152 | tf_op jit(solution)/shard_map/ppermute | solution.py:671
  12.9 14.0 %collective-permute-start.3 = (bf16[512,512]{1,0:T(8,128)(2,1)S(1)}, bf16[512,512]{1,0:T(8,128)(2,1)S(1)}, u32[]{:S(2)}, u32[]{:S(2)}) collective-permute-start(bf16[512,512]{1,0:T(8,128)(2,1)S(1)} %bitcast.29), channel_id=1, source_target_pairs={{0,2},{1,3},{2,0},{3,1},{4,6},{5,7},{6,4},{7,5},{8,10},{9,11},{10,... | collective-permute-start | bytes 1572872 | tf_op jit(solution)/shard_map/ppermute | solution.py:671
  14.9 4.5 %collective-permute-start.2 = (bf16[2,512]{1,0:T(2,128)(2,1)S(1)}, bf16[2,512]{1,0:T(2,128)(2,1)S(1)}, u32[]{:S(2)}, u32[]{:S(2)}) collective-permute-start(bf16[2,512]{1,0:T(2,128)(2,1)S(1)} %collective-permute-done.1), channel_id=1, source_target_pairs={{0,1},{1,0},{2,3},{3,2},{4,5},{5,4},{6,7},{7,6},{8,9},{9,8},{10,11... | collective-permute-start | bytes 6152 | tf_op jit(solution)/shard_map/ppermute | solution.py:671
  16.3 19.8 %copy-start.54 = (f32[32,256]{1,0:T(8,128)S(1)}, f32[32,256]{1,0:T(8,128)}, u32[]{:S(2)}) copy-start(f32[32,256]{1,0:T(8,128)} %constant.21.clone.refs_12_.refs_22_) | copy-start | bytes 98308
  16.3 19.8 %copy-start.56 = (f32[32,256]{1,0:T(8,128)S(1)}, f32[32,256]{1,0:T(8,128)}, u32[]{:S(2)}) copy-start(f32[32,256]{1,0:T(8,128)} %constant.19.clone.refs_11_.refs_21_) | copy-start | bytes 98308
  19.4 28.2 %copy-start.50 = (bf16[16,512]{1,0:T(8,128)(2,1)}, bf16[16,512]{1,0:T(8,128)(2,1)S(1)}, u32[]{:S(2)}) copy-start(bf16[16,512]{1,0:T(8,128)(2,1)S(1)} %get-tuple-element.122.refs_9_.refs_17_) | copy-start | bytes 49156
  19.4 28.2 %copy-start.58 = (bf16[2,16,128]{2,1,0:T(8,128)(2,1)}, bf16[2,16,128]{2,1,0:T(8,128)(2,1)S(1)}, u32[]{:S(2)}) copy-start(bf16[2,16,128]{2,1,0:T(8,128)(2,1)S(1)} %get-tuple-element.123.refs_10_.refs_18_) | copy-start | bytes 24580
  19.4 32.3 %copy-start.22 = (bf16[16,2048]{1,0:T(8,128)(2,1)}, bf16[16,2048]{1,0:T(8,128)(2,1)S(1)}, u32[]{:S(2)}) copy-start(bf16[16,2048]{1,0:T(8,128)(2,1)S(1)} %get-tuple-element.126.refs_4_.refs_20_) | copy-start | bytes 196612
  19.4 32.3 %copy-start.44 = (bf16[16,512]{1,0:T(8,128)(2,1)}, bf16[16,512]{1,0:T(8,128)(2,1)S(1)}, u32[]{:S(2)}) copy-start(bf16[16,512]{1,0:T(8,128)(2,1)S(1)} %get-tuple-element.125.refs_3_.refs_19_) | copy-start | bytes 49156
  26.9 7.6 %collective-permute-start.5 = (bf16[256,512]{1,0:T(8,128)(2,1)S(1)}, bf16[256,512]{1,0:T(8,128)(2,1)S(1)}, u32[]{:S(2)}, u32[]{:S(2)}) collective-permute-start(bf16[256,512]{1,0:T(8,128)(2,1)S(1)} %get-tuple-element.232), channel_id=1, source_target_pairs={{0,2},{1,3},{2,0},{3,1},{4,6},{5,7},{6,4},{7,5},{8,10},{9,11},{10,... | collective-permute-start | bytes 786440 | tf_op jit(solution)/shard_map/ppermute | solution.py:671
  27.5 8.6 %collective-permute-start.4 = (bf16[512,512]{1,0:T(8,128)(2,1)S(1)}, bf16[512,512]{1,0:T(8,128)(2,1)S(1)}, u32[]{:S(2)}, u32[]{:S(2)}) collective-permute-start(bf16[512,512]{1,0:T(8,128)(2,1)S(1)} %bitcast.21), channel_id=1, source_target_pairs={{0,1},{1,0},{2,3},{3,2},{4,5},{5,4},{6,7},{7,6},{8,9},{9,8},{10,11... | collective-permute-start | bytes 1572872 | tf_op jit(solution)/shard_map/ppermute | solution.py:671
  34.5 29.1 %copy-start.8 = (bf16[256,512]{1,0:T(8,128)(2,1)}, bf16[256,512]{1,0:T(8,128)(2,1)S(1)}, u32[]{:S(2)}) copy-start(bf16[256,512]{1,0:T(8,128)(2,1)S(1)} %collective-permute-done.5.refs_5_.refs_6_) | copy-start | bytes 786436
  34.5 1.5 collective-permute-start.6
  34.5 8.8 %collective-permute-start.9 = (bf16[256,512]{1,0:T(8,128)(2,1)S(1)}, bf16[256,512]{1,0:T(8,128)(2,1)S(1)}, u32[]{:S(2)}, u32[]{:S(2)}) collective-permute-start(bf16[256,512]{1,0:T(8,128)(2,1)S(1)} %get-tuple-element.231), channel_id=1, source_target_pairs={{0,2},{1,3},{2,0},{3,1},{4,6},{5,7},{6,4},{7,5},{8,10},{9,11},{10,... | collective-permute-start | bytes 786440 | tf_op jit(solution)/shard_map/ppermute | solution.py:671
  36.0 27.6 %copy-start.10 = (bf16[256,512]{1,0:T(8,128)(2,1)}, bf16[256,512]{1,0:T(8,128)(2,1)S(1)}, u32[]{:S(2)}) copy-start(bf16[256,512]{1,0:T(8,128)(2,1)S(1)} %collective-permute-done.6.refs_6_.refs_7_) | copy-start | bytes 786436
  43.3 2.0 collective-permute-start.10
  45.4 14.0 %collective-permute-start.11 = (bf16[256,1024]{1,0:T(8,128)(2,1)S(1)}, bf16[256,1024]{1,0:T(8,128)(2,1)S(1)}, u32[]{:S(2)}, u32[]{:S(2)}) collective-permute-start(bf16[256,1024]{1,0:T(8,128)(2,1)S(1)} %pair_sum.4.refs_0_.refs_14_), channel_id=1, source_target_pairs={{0,2},{1,3},{2,0},{3,1},{4,6},{5,7},{6,4},{7,5},{8,10},{9,11},{10,... | collective-permute-start | bytes 1572872 | tf_op jit(solution)/shard_map/ppermute | solution.py:671
  46.0 1.5 collective-permute-start.13
  47.6 32.1 %copy-start.6 = (bf16[256,512]{1,0:T(8,128)(2,1)}, bf16[256,512]{1,0:T(8,128)(2,1)S(1)}, u32[]{:S(2)}) copy-start(bf16[256,512]{1,0:T(8,128)(2,1)S(1)} %collective-permute-done.13.refs_6_.refs_7_) | copy-start | bytes 786436
  55.5 21.1 %copy-start.48 = (bf16[512,256]{1,0:T(8,128)(2,1)}, bf16[512,256]{1,0:T(8,128)(2,1)S(1)}, u32[]{:S(2)}) copy-start(bf16[512,256]{1,0:T(8,128)(2,1)S(1)} %get-tuple-element.179.refs_25_) | copy-start | bytes 786436
  59.4 1.9 collective-permute-start.14
  59.4 2.7 %collective-permute-start.7 = (bf16[512,512]{1,0:T(8,128)(2,1)S(1)}, bf16[512,512]{1,0:T(8,128)(2,1)S(1)}, u32[]{:S(2)}, u32[]{:S(2)}) collective-permute-start(bf16[512,512]{1,0:T(8,128)(2,1)S(1)} %bitcast.30), channel_id=1, source_target_pairs={{0,1},{1,0},{2,3},{3,2},{4,5},{5,4},{6,7},{7,6},{8,9},{9,8},{10,11... | collective-permute-start | bytes 1572872 | tf_op jit(solution)/shard_map/ppermute | solution.py:671
  59.9 2.9 %collective-permute-start.8 = (bf16[512,512]{1,0:T(8,128)(2,1)S(1)}, bf16[512,512]{1,0:T(8,128)(2,1)S(1)}, u32[]{:S(2)}, u32[]{:S(2)}) collective-permute-start(bf16[512,512]{1,0:T(8,128)(2,1)S(1)} %collective-permute-done.3.refs_11_.refs_10_), channel_id=1, source_target_pairs={{0,1},{1,0},{2,3},{3,2},{4,5},{5,4},{6,7},{7,6},{8,9},{9,8},{10,11... | collective-permute-start | bytes 1572872 | tf_op jit(solution)/shard_map/ppermute | solution.py:671
  60.2 3.4 %collective-permute-start.12 = (bf16[256,1024]{1,0:T(8,128)(2,1)S(1)}, bf16[256,1024]{1,0:T(8,128)(2,1)S(1)}, u32[]{:S(2)}, u32[]{:S(2)}) collective-permute-start(bf16[256,1024]{1,0:T(8,128)(2,1)S(1)} %far_sum.4.refs_7_), channel_id=1, source_target_pairs={{0,1},{1,0},{2,3},{3,2},{4,5},{5,4},{6,7},{7,6},{8,9},{9,8},{10,11... | collective-permute-start | bytes 1572872 | tf_op jit(solution)/shard_map/ppermute | solution.py:671
  61.5 16.1 %collective-permute-start.15 = (bf16[256,1024]{1,0:T(8,128)(2,1)S(1)}, bf16[256,1024]{1,0:T(8,128)(2,1)S(1)}, u32[]{:S(2)}, u32[]{:S(2)}) collective-permute-start(bf16[256,1024]{1,0:T(8,128)(2,1)S(1)} %pair_sum.5.refs_19_.refs_0_), channel_id=1, source_target_pairs={{0,2},{1,3},{2,0},{3,1},{4,6},{5,7},{6,4},{7,5},{8,10},{9,11},{10,... | collective-permute-start | bytes 1572872 | tf_op jit(solution)/shard_map/ppermute | solution.py:671
  77.6 29.6 %copy-start.2 = (bf16[256,2048]{1,0:T(8,128)(2,1)}, bf16[256,2048]{1,0:T(8,128)(2,1)S(1)}, u32[]{:S(2)}) copy-start(bf16[256,2048]{1,0:T(8,128)(2,1)S(1)} %get-tuple-element.151.refs_4_.refs_2_) | copy-start | bytes 3145732
  77.7 2.0 collective-permute-start.16
  91.7 12.4 %collective-permute-start.17 = (bf16[1,192,512]{2,1,0:T(8,128)(2,1)S(1)}, bf16[1,192,512]{2,1,0:T(8,128)(2,1)S(1)}, u32[]{:S(2)}, u32[]{:S(2)}) collective-permute-start(bf16[1,192,512]{2,1,0:T(8,128)(2,1)S(1)} %bitcast.36), channel_id=1, source_target_pairs={{0,16},{4,20},{8,24},{12,28},{16,0},{20,4},{24,8},{28,12},{1,17},{... | collective-permute-start | bytes 589832 | tf_op jit(solution)/shard_map/ppermute | solution.py:671
  104.1 2.3 %collective-permute-start.18 = (bf16[256,1024]{1,0:T(8,128)(2,1)S(1)}, bf16[256,1024]{1,0:T(8,128)(2,1)S(1)}, u32[]{:S(2)}, u32[]{:S(2)}) collective-permute-start(bf16[256,1024]{1,0:T(8,128)(2,1)S(1)} %get-tuple-element.168), channel_id=1, source_target_pairs={{0,1},{1,0},{2,3},{3,2},{4,5},{5,4},{6,7},{7,6},{8,9},{9,8},{10,11... | collective-permute-start | bytes 1572872 | tf_op jit(solution)/shard_map/ppermute | solution.py:671
  104.2 11.6 %collective-permute-start.20 = (bf16[2,192,512]{2,1,0:T(8,128)(2,1)S(1)}, bf16[2,192,512]{2,1,0:T(8,128)(2,1)S(1)}, u32[]{:S(2)}, u32[]{:S(2)}) collective-permute-start(bf16[2,192,512]{2,1,0:T(8,128)(2,1)S(1)} %pad_maximum_fusion.refs_0_), channel_id=1, source_target_pairs={{0,4},{4,0},{8,12},{12,8},{16,20},{20,16},{24,28},{28,24},{1,5},{5... | collective-permute-start | bytes 1179656 | tf_op jit(solution)/shard_map/ppermute | solution.py:671
  106.0 11.2 %collective-permute-start.19 = (bf16[2,192,512]{2,1,0:T(8,128)(2,1)S(1)}, bf16[2,192,512]{2,1,0:T(8,128)(2,1)S(1)}, u32[]{:S(2)}, u32[]{:S(2)}) collective-permute-start(bf16[2,192,512]{2,1,0:T(8,128)(2,1)S(1)} %pad_maximum_fusion.refs_0_), channel_id=1, source_target_pairs={{0,8},{4,12},{8,0},{12,4},{16,24},{20,28},{24,16},{28,20},{1,9},{5... | collective-permute-start | bytes 1179656 | tf_op jit(solution)/shard_map/ppermute | solution.py:671
  106.5 15.4 %collective-permute-start.22 = (bf16[256,1024]{1,0:T(8,128)(2,1)S(1)}, bf16[256,1024]{1,0:T(8,128)(2,1)S(1)}, u32[]{:S(2)}, u32[]{:S(2)}) collective-permute-start(bf16[256,1024]{1,0:T(8,128)(2,1)S(1)} %pair_sum.6.refs_11_.refs_0_), channel_id=1, source_target_pairs={{0,2},{1,3},{2,0},{3,1},{4,6},{5,7},{6,4},{7,5},{8,10},{9,11},{10,... | collective-permute-start | bytes 1572872 | tf_op jit(solution)/shard_map/ppermute | solution.py:671
  117.2 5.4 %collective-permute-start.21 = (bf16[304,1024]{1,0:T(8,128)(2,1)S(1)}, bf16[304,1024]{1,0:T(8,128)(2,1)S(1)}, u32[]{:S(2)}, u32[]{:S(2)}) collective-permute-start(bf16[304,1024]{1,0:T(8,128)(2,1)S(1)} %get-tuple-element.171), channel_id=1, source_target_pairs={{0,1},{1,0},{2,3},{3,2},{4,5},{5,4},{6,7},{7,6},{8,9},{9,8},{10,11... | collective-permute-start | bytes 1867784 | tf_op jit(solution)/shard_map/ppermute | solution.py:671
  122.1 2.1 collective-permute-start.24
  122.9 16.5 %collective-permute-start.23 = (bf16[304,1024]{1,0:T(8,128)(2,1)S(1)}, bf16[304,1024]{1,0:T(8,128)(2,1)S(1)}, u32[]{:S(2)}, u32[]{:S(2)}) collective-permute-start(bf16[304,1024]{1,0:T(8,128)(2,1)S(1)} %pair_sum.7.refs_34_.refs_0_), channel_id=1, source_target_pairs={{0,2},{1,3},{2,0},{3,1},{4,6},{5,7},{6,4},{7,5},{8,10},{9,11},{10,... | collective-permute-start | bytes 1867784 | tf_op jit(solution)/shard_map/ppermute | solution.py:671
  123.5 11.5 %collective-permute-start.26 = (bf16[2,192,512]{2,1,0:T(8,128)(2,1)S(1)}, bf16[2,192,512]{2,1,0:T(8,128)(2,1)S(1)}, u32[]{:S(2)}, u32[]{:S(2)}) collective-permute-start(bf16[2,192,512]{2,1,0:T(8,128)(2,1)S(1)} %collective-permute-done.19.refs_1_), channel_id=1, source_target_pairs={{0,4},{4,0},{8,12},{12,8},{16,20},{20,16},{24,28},{28,24},{1,5},{5... | collective-permute-start | bytes 1179656 | tf_op jit(solution)/shard_map/ppermute | solution.py:671
  135.1 4.5 %collective-permute-start.27 = (bf16[256,1024]{1,0:T(8,128)(2,1)S(1)}, bf16[256,1024]{1,0:T(8,128)(2,1)S(1)}, u32[]{:S(2)}, u32[]{:S(2)}) collective-permute-start(bf16[256,1024]{1,0:T(8,128)(2,1)S(1)} %get-tuple-element.196), channel_id=1, source_target_pairs={{0,1},{1,0},{2,3},{3,2},{4,5},{5,4},{6,7},{7,6},{8,9},{9,8},{10,11... | collective-permute-start | bytes 1572872 | tf_op jit(solution)/shard_map/ppermute | solution.py:671
  139.5 3.1 %collective-permute-start.25 = (bf16[304,1024]{1,0:T(8,128)(2,1)S(1)}, bf16[304,1024]{1,0:T(8,128)(2,1)S(1)}, u32[]{:S(2)}, u32[]{:S(2)}) collective-permute-start(bf16[304,1024]{1,0:T(8,128)(2,1)S(1)} %far_sum.7.refs_13_), channel_id=1, source_target_pairs={{0,1},{1,0},{2,3},{3,2},{4,5},{5,4},{6,7},{7,6},{8,9},{9,8},{10,11... | collective-permute-start | bytes 1867784 | tf_op jit(solution)/shard_map/ppermute | solution.py:671
  139.7 12.8 %collective-permute-start.29 = (bf16[256,512]{1,0:T(8,128)(2,1)S(1)}, bf16[256,512]{1,0:T(8,128)(2,1)S(1)}, u32[]{:S(2)}, u32[]{:S(2)}) collective-permute-start(bf16[256,512]{1,0:T(8,128)(2,1)S(1)} %high_sum.4.refs_36_), channel_id=1, source_target_pairs={{0,2},{1,3},{2,0},{3,1},{4,6},{5,7},{6,4},{7,5},{8,10},{9,11},{10,... | collective-permute-start | bytes 786440 | tf_op jit(solution)/shard_map/ppermute | solution.py:671
  140.3 12.1 %collective-permute-start.28 = (bf16[1,48,1024]{2,1,0:T(8,128)(2,1)S(1)}, bf16[1,48,1024]{2,1,0:T(8,128)(2,1)S(1)}, u32[]{:S(2)}, u32[]{:S(2)}) collective-permute-start(bf16[1,48,1024]{2,1,0:T(8,128)(2,1)S(1)} %slice_bitcast_fusion), channel_id=1, source_target_pairs={{0,16},{4,20},{8,24},{12,28},{16,0},{20,4},{24,8},{28,12},{1,17},{... | collective-permute-start | bytes 294920 | tf_op jit(solution)/shard_map/ppermute | solution.py:671
  152.5 5.4 %collective-permute-start.32 = (bf16[256,1024]{1,0:T(8,128)(2,1)S(1)}, bf16[256,1024]{1,0:T(8,128)(2,1)S(1)}, u32[]{:S(2)}, u32[]{:S(2)}) collective-permute-start(bf16[256,1024]{1,0:T(8,128)(2,1)S(1)} %get-tuple-element.203), channel_id=1, source_target_pairs={{0,1},{1,0},{2,3},{3,2},{4,5},{5,4},{6,7},{7,6},{8,9},{9,8},{10,11... | collective-permute-start | bytes 1572872 | tf_op jit(solution)/shard_map/ppermute | solution.py:671
  152.6 2.2 collective-permute-start.30
  154.7 4.9 %collective-permute-start.31 = (bf16[96,512]{1,0:T(8,128)(2,1)S(1)}, bf16[96,512]{1,0:T(8,128)(2,1)S(1)}, u32[]{:S(2)}, u32[]{:S(2)}) collective-permute-start(bf16[96,512]{1,0:T(8,128)(2,1)S(1)} %high_sum.5.refs_2_), channel_id=1, source_target_pairs={{0,2},{1,3},{2,0},{3,1},{4,6},{5,7},{6,4},{7,5},{8,10},{9,11},{10,... | collective-permute-start | bytes 294920 | tf_op jit(solution)/shard_map/ppermute | solution.py:671
  156.1 7.8 %collective-permute-start.36 = (bf16[2,48,1024]{2,1,0:T(8,128)(2,1)S(1)}, bf16[2,48,1024]{2,1,0:T(8,128)(2,1)S(1)}, u32[]{:S(2)}, u32[]{:S(2)}) collective-permute-start(bf16[2,48,1024]{2,1,0:T(8,128)(2,1)S(1)} %pad_maximum_fusion.2), channel_id=1, source_target_pairs={{0,8},{4,12},{8,0},{12,4},{16,24},{20,28},{24,16},{28,20},{1,9},{5... | collective-permute-start | bytes 589832 | tf_op jit(solution)/shard_map/ppermute | solution.py:671
  157.9 11.2 %collective-permute-start.33 = (bf16[256,512]{1,0:T(8,128)(2,1)S(1)}, bf16[256,512]{1,0:T(8,128)(2,1)S(1)}, u32[]{:S(2)}, u32[]{:S(2)}) collective-permute-start(bf16[256,512]{1,0:T(8,128)(2,1)S(1)} %high_sum.6), channel_id=1, source_target_pairs={{0,2},{1,3},{2,0},{3,1},{4,6},{5,7},{6,4},{7,5},{8,10},{9,11},{10,... | collective-permute-start | bytes 786440 | tf_op jit(solution)/shard_map/ppermute | solution.py:671
  159.7 9.4 %collective-permute-start.34 = (bf16[1,112,512]{2,1,0:T(8,128)(2,1)S(1)}, bf16[1,112,512]{2,1,0:T(8,128)(2,1)S(1)}, u32[]{:S(2)}, u32[]{:S(2)}) collective-permute-start(bf16[1,112,512]{2,1,0:T(8,128)(2,1)S(1)} %maximum_bitcast_fusion.refs_6_), channel_id=1, source_target_pairs={{0,16},{4,20},{8,24},{12,28},{16,0},{20,4},{24,8},{28,12},{1,17},{... | collective-permute-start | bytes 344072 | tf_op jit(solution)/shard_map/ppermute | solution.py:671
  163.9 11.4 %collective-permute-start.37 = (bf16[4,48,1024]{2,1,0:T(8,128)(2,1)S(1)}, bf16[4,48,1024]{2,1,0:T(8,128)(2,1)S(1)}, u32[]{:S(2)}, u32[]{:S(2)}) collective-permute-start(bf16[4,48,1024]{2,1,0:T(8,128)(2,1)S(1)} %constant_dynamic-update-slice_fusion.2.refs_4_), channel_id=1, source_target_pairs={{0,4},{4,0},{8,12},{12,8},{16,20},{20,16},{24,28},{28,24},{1,5},{5... | collective-permute-start | bytes 1179656 | tf_op jit(solution)/shard_map/ppermute | solution.py:671
  169.1 6.1 %collective-permute-start.35 = (bf16[2,112,512]{2,1,0:T(8,128)(2,1)S(1)}, bf16[2,112,512]{2,1,0:T(8,128)(2,1)S(1)}, u32[]{:S(2)}, u32[]{:S(2)}) collective-permute-start(bf16[2,112,512]{2,1,0:T(8,128)(2,1)S(1)} %pad_maximum_fusion.1), channel_id=1, source_target_pairs={{0,8},{4,12},{8,0},{12,4},{16,24},{20,28},{24,16},{28,20},{1,9},{5... | collective-permute-start | bytes 688136 | tf_op jit(solution)/shard_map/ppermute | solution.py:671
  171.0 9.6 %collective-permute-start.39 = (bf16[256,1024]{1,0:T(8,128)(2,1)}, bf16[256,1024]{1,0:T(8,128)(2,1)}, u32[]{:S(2)}, u32[]{:S(2)}) collective-permute-start(bf16[256,1024]{1,0:T(8,128)(2,1)} %get-tuple-element.216.refs_35_), channel_id=1, source_target_pairs={{0,1},{1,0},{2,3},{3,2},{4,5},{5,4},{6,7},{7,6},{8,9},{9,8},{10,11... | collective-permute-start | bytes 1572872 | tf_op jit(solution)/shard_map/ppermute | solution.py:671
  171.0 9.6 %collective-permute-start.38 = (bf16[256,1024]{1,0:T(8,128)(2,1)}, bf16[256,1024]{1,0:T(8,128)(2,1)}, u32[]{:S(2)}, u32[]{:S(2)}) collective-permute-start(bf16[256,1024]{1,0:T(8,128)(2,1)} %get-tuple-element.209), channel_id=1, source_target_pairs={{0,1},{1,0},{2,3},{3,2},{4,5},{5,4},{6,7},{7,6},{8,9},{9,8},{10,11... | collective-permute-start | bytes 1572872 | tf_op jit(solution)/shard_map/ppermute | solution.py:671
  176.6 17.8 %all-to-all-start.1 = ((bf16[8,64,512]{2,1,0:T(8,128)(2,1)}), bf16[8,64,512]{2,1,0:T(8,128)(2,1)S(1)}, u32[]{:S(2)}, u32[]{:S(2)}) async-start(bf16[8,64,512]{2,1,0:T(8,128)(2,1)} %bitcast.35), calls=%async_computation.1 | async-start | bytes 1048576 | tf_op jit(solution)/shard_map/all_to_all | solution.py:826
  181.9 10.3 %collective-permute-start.40 = (bf16[512,512]{1,0:T(8,128)(2,1)S(1)}, bf16[512,512]{1,0:T(8,128)(2,1)S(1)}, u32[]{:S(2)}, u32[]{:S(2)}) collective-permute-start(bf16[512,512]{1,0:T(8,128)(2,1)S(1)} %high_sum.7), channel_id=1, source_target_pairs={{0,2},{1,3},{2,0},{3,1},{4,6},{5,7},{6,4},{7,5},{8,10},{9,11},{10,... | collective-permute-start | bytes 1572872 | tf_op jit(solution)/shard_map/ppermute | solution.py:671
  182.7 19.4 %collective-permute-start.41 = (bf16[4,112,512]{2,1,0:T(8,128)(2,1)S(1)}, bf16[4,112,512]{2,1,0:T(8,128)(2,1)}, u32[]{:S(2)}, u32[]{:S(2)}) collective-permute-start(bf16[4,112,512]{2,1,0:T(8,128)(2,1)S(1)} %constant_dynamic-update-slice_fusion.refs_14_.refs_0_), channel_id=1, source_target_pairs={{0,4},{4,0},{8,12},{12,8},{16,20},{20,16},{24,28},{28,24},{1,5},{5... | collective-permute-start | bytes 1376264 | tf_op jit(solution)/shard_map/ppermute | solution.py:671
  194.4 26.3 %all-to-all-start.2 = ((bf16[8,64,512]{2,1,0:T(8,128)(2,1)}), bf16[8,64,512]{2,1,0:T(8,128)(2,1)S(1)}, u32[]{:S(2)}, u32[]{:S(2)}) async-start(bf16[8,64,512]{2,1,0:T(8,128)(2,1)} %bitcast.14), calls=%async_computation.2 | async-start | bytes 1048576 | tf_op jit(solution)/shard_map/all_to_all | solution.py:826
  200.3 3.7 %collective-permute-start.46 = (bf16[4,48,1024]{2,1,0:T(8,128)(2,1)}, bf16[4,48,1024]{2,1,0:T(8,128)(2,1)S(1)}, u32[]{:S(2)}, u32[]{:S(2)}) collective-permute-start(bf16[4,48,1024]{2,1,0:T(8,128)(2,1)} %copy-done.32), channel_id=1, source_target_pairs={{0,1},{1,0},{2,3},{3,2},{4,5},{5,4},{6,7},{7,6},{8,9},{9,8},{10,11... | collective-permute-start | bytes 1179656 | tf_op jit(solution)/shard_map/ppermute | solution.py:671
  200.3 3.7 %collective-permute-start.47 = (bf16[4,48,1024]{2,1,0:T(8,128)(2,1)S(1)}, bf16[4,48,1024]{2,1,0:T(8,128)(2,1)S(1)}, u32[]{:S(2)}, u32[]{:S(2)}) collective-permute-start(bf16[4,48,1024]{2,1,0:T(8,128)(2,1)S(1)} %collective-permute-done.37.refs_15_.refs_5_), channel_id=1, source_target_pairs={{0,1},{1,0},{2,3},{3,2},{4,5},{5,4},{6,7},{7,6},{8,9},{9,8},{10,11... | collective-permute-start | bytes 1179656 | tf_op jit(solution)/shard_map/ppermute | solution.py:671
  200.8 10.1 %collective-permute-start.44 = (bf16[4,64,512]{2,1,0:T(8,128)(2,1)S(1)}, bf16[4,64,512]{2,1,0:T(8,128)(2,1)S(1)}, u32[]{:S(2)}, u32[]{:S(2)}) collective-permute-start(bf16[4,64,512]{2,1,0:T(8,128)(2,1)S(1)} %slice.34.refs_2_), channel_id=1, source_target_pairs={{0,2},{1,3},{2,0},{3,1},{4,6},{5,7},{6,4},{7,5},{8,10},{9,11},{10,... | collective-permute-start | bytes 786440 | tf_op jit(solution)/shard_map/ppermute | solution.py:671
  203.1 11.7 %collective-permute-start.45 = (bf16[4,64,512]{2,1,0:T(8,128)(2,1)S(1)}, bf16[4,64,512]{2,1,0:T(8,128)(2,1)S(1)}, u32[]{:S(2)}, u32[]{:S(2)}) collective-permute-start(bf16[4,64,512]{2,1,0:T(8,128)(2,1)S(1)} %slice.35.refs_3_), channel_id=1, source_target_pairs={{0,2},{1,3},{2,0},{3,1},{4,6},{5,7},{6,4},{7,5},{8,10},{9,11},{10,... | collective-permute-start | bytes 786440 | tf_op jit(solution)/shard_map/ppermute | solution.py:671
  203.9 12.2 %collective-permute-start.42 = (bf16[4,64,512]{2,1,0:T(8,128)(2,1)S(1)}, bf16[4,64,512]{2,1,0:T(8,128)(2,1)S(1)}, u32[]{:S(2)}, u32[]{:S(2)}) collective-permute-start(bf16[4,64,512]{2,1,0:T(8,128)(2,1)S(1)} %slice.34.refs_2_), channel_id=1, source_target_pairs={{0,1},{1,0},{2,3},{3,2},{4,5},{5,4},{6,7},{7,6},{8,9},{9,8},{10,11... | collective-permute-start | bytes 786440 | tf_op jit(solution)/shard_map/ppermute | solution.py:671
  210.9 5.3 %collective-permute-start.48 = (bf16[4,64,512]{2,1,0:T(8,128)(2,1)S(1)}, bf16[4,64,512]{2,1,0:T(8,128)(2,1)S(1)}, u32[]{:S(2)}, u32[]{:S(2)}) collective-permute-start(bf16[4,64,512]{2,1,0:T(8,128)(2,1)S(1)} %collective-permute-done.44.refs_6_), channel_id=1, source_target_pairs={{0,1},{1,0},{2,3},{3,2},{4,5},{5,4},{6,7},{7,6},{8,9},{9,8},{10,11... | collective-permute-start | bytes 786440 | tf_op jit(solution)/shard_map/ppermute | solution.py:671
  211.4 4.8 %collective-permute-start.43 = (bf16[4,64,512]{2,1,0:T(8,128)(2,1)S(1)}, bf16[4,64,512]{2,1,0:T(8,128)(2,1)S(1)}, u32[]{:S(2)}, u32[]{:S(2)}) collective-permute-start(bf16[4,64,512]{2,1,0:T(8,128)(2,1)S(1)} %slice.35.refs_3_), channel_id=1, source_target_pairs={{0,1},{1,0},{2,3},{3,2},{4,5},{5,4},{6,7},{7,6},{8,9},{9,8},{10,11... | collective-permute-start | bytes 786440 | tf_op jit(solution)/shard_map/ppermute | solution.py:671
  214.8 1.5 collective-permute-start.49
  (63 other events, 420.7 us)

commit v8 on v7

--- a/solution.py
+++ b/solution.py
@@ -845,13 +845,12 @@
     fb_more = fb_more[2:]
     fb_side = swap(fb, bits[-1], "dp", dp)
     td_0, d_keep, d_send = back(0, hidden[0], (fa,), (d_own[1],))
-    y_keep[1], y_send = down(1, td, (td_0,))
-    total = far_sum(d_own[1], late(d_far[1], y_send))
+    total = far_sum(d_own[1], late(d_far[1], td_0))
     d_own[0] = pair_sum(d_keep, late(d_send, fb_more, fb_side), total)
     d_far[0] = far(d_own[0])
     fb_more_side = swap(fb_more, bits[-1], "dp", dp)
-    y_got[1] = near(late(y_send, d_own[0]))
-    dxq, h_keep, h_send, inv, *sums = attend_back(1, total, (), (d_own[0], y_send))
+    dxq, h_keep, h_send, inv, *sums = attend_back(1, total, (), (d_own[0],))
+    y_keep[1], y_send = down(1, td, (inv,))
     total = far_sum(d_own[0], late(d_far[0], inv))
     h_got = near(late(h_send, fb_more_side))
     h_high = high_sum((h_keep, h_got))
@@ -859,7 +858,8 @@
     final = [None, (dxq, h_keep, h_got, h_far, inv)]
     fa = total[rows:][None]
     fa_first = swap(fa, bits[0], "dp", dp)
-    dxq, h_keep, h_send, inv, att_b, aa_keep, aa_send = attend_back(0, total, sums, (h_high,))
+    dxq, h_keep, h_send, inv, att_b, aa_keep, aa_send = attend_back(0, total, sums, (h_high, y_send))
+    y_got[1] = near(late(y_send, inv))
     ready = (fa_first, h_far)
     aa_got = near(late(aa_send, *ready))
     aa_high = high_sum((aa_keep, aa_got))
@@ -874,7 +874,7 @@
     att = jnp.concatenate([att_b, att_a], axis=0)[None]
     y_keep[0], y_send = down(0, td_0, (att,))
     y_got[0] = near(y_send)
-    att = doubled(att, bits[0], dp)
+    att = first = doubled(att, bits[0], dp)
     att = late(att, h_far, y_send)
     for bit in bits[1:-1]:
         att = doubled(att, bit, dp)
@@ -882,12 +882,12 @@
     for bit in bits[1:-1]:
         fa = doubled(fa, bit, dp)
     fa_side = swap(fa, bits[-1], "dp", dp)
-    y_far = far(high_sum(*((k, late(g, h_far)) for k, g in zip(y_keep, y_got))))
 
     dinput, = call(finish_kernel, None, (), (gains, dealt, aa_high, aa_far, *(v for f in final for v in f)),
-                   [((length, QUARTER), BF16)], [], "finish", 8, (att, fa_side))
+                   [((length, QUARTER), BF16)], [], "finish", 8, (y_send, first, fa))
+    y_far = far(high_sum(*((k, late(g, dinput)) for k, g in zip(y_keep, y_got))))
     input_grad = collect(to_bands(dinput), "collect_grad")
-    result, = call(output_kernel, info, (), (late(y_far, dinput), *(v for p in zip(y_keep, y_got) for v in p)),
+    result, = call(output_kernel, info, (), (y_far, *(v for p in zip(y_keep, y_got) for v in p)),
                    [((length, QUARTER), BF16)], [], "output", 8)
     output = collect(to_bands(result), "collect_out", input_grad)
 

time: 223 us -> 227 us (1.018)
  waiting for transfers between devices: 55.2 us -> 58.6 us
  starting transfers between devices: 48.7 us -> 46.2 us
  local copies, waits for them, and re-layouts: 8.27 us -> 10.6 us
    ppermute x50, waiting for transfers between devices: 55.2 us -> 58.6 us  [swap(): return lax.ppermute(value, axis, [(i, i ^ bit) for i in range(size)])]
    all_to_all x2, starting transfers between devices: 9.78 us -> 7.35 us  [to_bands(): lax.all_to_all(value.reshape(dp, length // dp, QUARTER), 'dp', split_axis...]
    unnamed x150 -> x130, local copies, waits for them, and re-layouts: 7.2 us -> 7.91 us
  transfers between devices with their start and end apart: 53 -> 53, of which waited for: 23 -> 21; matrix products, arithmetic and copies ran while one was open for 2% -> 3% of each run, Pallas kernels for 40% -> 40%
where the time goes in v8:
time: 227 us
  Pallas kernels  107 us (47%)
  waiting for transfers between devices  58.6 us (26%)
  starting transfers between devices  46.2 us (20%)
  local copies, waits for them, and re-layouts  10.6 us (5%)
  other arithmetic  2.31 us (1%)
    pallas_call x26, Pallas kernels, call(): pl.pallas_call(body, in_specs=[pl.BlockSpec(memory_space=pltpu.SMEM)] * n...  90.4 us
    ppermute x50, waiting for transfers between devices, swap(): return lax.ppermute(value, axis, [(i, i ^ bit) for i in range(size)])  58.6 us
    ppermute x50, starting transfers between devices, swap(): return lax.ppermute(value, axis, [(i, i ^ bit) for i in range(size)])  31.6 us
    pallas_call x2, Pallas kernels, sum_call(): pl.pallas_call(functools.partial(kernel, [len(group) for group in groups]...  9.86 us
    unnamed x130, local copies, waits for them, and re-layouts  7.91 us
    all_to_all x2, starting transfers between devices, to_bands(): lax.all_to_all(value.reshape(dp, length // dp, QUARTER), 'dp', split_axis...  7.35 us
    all_to_all x1, starting transfers between devices, shards(): lax.all_to_all(ordered, 'dp', split_axis=0, concat_axis=1, tiled=True)[0]  7.26 us
    pallas_call x3, Pallas kernels, move_rows(): pl.pallas_call(kernel, in_specs=[pl.BlockSpec(memory_space=pltpu.SMEM), p...  5.25 us
  transfers between devices with their start and end apart: 53, of which 21 were waited for; matrix products, arithmetic and copies ran while one was open for 3% of the time, Pallas kernels for 40%

profile of v8, /device:TPU:0, one launch (start us, length us, event | category | flops | bytes accessed | tf_op | source)
XLA Modules:
  0.0 226.9 jit_solution(5964256675879241680)
XLA Ops:
  0.7 0.7 copy-done.54
  1.4 2.5 %deal.1 = bf16[8,64,512]{2,1,0:T(8,128)(2,1)} custom-call(s32[8]{0:T(128)S(1)} %copy-done.54, bf16[8,64,512]{2,1,0:T(8,128)(2,1)} %source.1), custom_call_target="tpu_custom_call" | custom-call | flops 1000 | bytes 1000 | tf_op jit(solution)/shard_map/deal/pallas_call | solution.py:599
  3.9 7.3 %all-to-all-start = ((bf16[8,64,512]{2,1,0:T(8,128)(2,1)}), bf16[8,64,512]{2,1,0:T(8,128)(2,1)S(1)}, u32[]{:S(2)}, u32[]{:S(2)}) async-start(bf16[8,64,512]{2,1,0:T(8,128)(2,1)} %deal.1), calls=%async_computation | async-start | bytes 1048576 | tf_op jit(solution)/shard_map/all_to_all | solution.py:750
  11.3 1.6 collective-permute-start.1
  14.2 0.7 collective-permute-done.1
  14.9 1.4 pad_add_fusion.info.refs_0_
  16.3 1.8 adapters.1
  19.4 7.4 %collective-permute-done.3.refs_11_.refs_10_ = bf16[512,512]{1,0:T(8,128)(2,1)S(1)} collective-permute-done((bf16[512,512]{1,0:T(8,128)(2,1)S(1)}, bf16[512,512]{1,0:T(8,128)(2,1)S(1)}, u32[]{:S(2)}, u32[]{:S(2)}) %collective-permute-start.3) | collective-permute-done | bytes 524320 | tf_op jit(solution)/shard_map/ppermute | solution.py:671
  27.5 7.0 %collective-permute-done.5.refs_5_.refs_6_ = bf16[256,512]{1,0:T(8,128)(2,1)S(1)} collective-permute-done((bf16[256,512]{1,0:T(8,128)(2,1)S(1)}, bf16[256,512]{1,0:T(8,128)(2,1)S(1)}, u32[]{:S(2)}, u32[]{:S(2)}) %collective-permute-start.5) | collective-permute-done | bytes 262176 | tf_op jit(solution)/shard_map/ppermute | solution.py:671
  35.1 1.0 collective-permute-done.6.refs_6_.refs_7_
  36.1 4.1 %project_0.1 = (bf16[48,256]{1,0:T(8,128)(2,1)S(1)}, bf16[512,256]{1,0:T(8,128)(2,1)S(1)}, bf16[2,256,64]{2,1,0:T(8,128)(2,1)S(1)}, bf16[2,256,64]{2,1,0:T(8,128...) custom-call(s32[4]{0:T(128)S(1)} %pad_add_fusion.info.refs_0_, bf16[2048,512]{1,0:T(8,128)(2,1)} %refs_1_.15, ...), custom_call_target="tpu_custom_call" | custom-call | flops 1000 | bytes 1000 | tf_op jit(solution)/shard_map/project_0/pallas_call | solution.py:632
  40.8 3.1 %attend_0.1 = (f32[256,1024]{1,0:T(8,128)S(1)}, bf16[256,1024]{1,0:T(8,128)(2,1)S(1)}, bf16[512,256]{1,0:T(8,128)(2,1)S(1)}, f32[8,256]{1,0:T(8,128)S(1)}, bf16[16,256]{1,0:T(8,128)(2,1)S(1)}) custom-call(s32[4]{0:T(128)S(1)} %pad_add_fusion.info.refs_0_, bf16[512,2048]{1,0:T(8,128)(2,1)} %refs_3_.5, ...), custom_call_target="tpu_custom_call" | custom-call | flops 1000 | bytes 1000 | tf_op jit(solution)/shard_map/attend_0/pallas_call | solution.py:632
  44.1 1.8 collective-permute-done.10.refs_1_
  46.6 1.5 collective-permute-done.13.refs_6_.refs_7_
  48.2 4.1 %project_1.1 = (bf16[48,256]{1,0:T(8,128)(2,1)S(1)}, bf16[512,256]{1,0:T(8,128)(2,1)S(1)}, bf16[2,256,64]{2,1,0:T(8,128)(2,1)S(1)}, bf16[2,256,64]{2,1,0:T(8,128...) custom-call(s32[4]{0:T(128)S(1)} %pad_add_fusion.info.refs_0_, bf16[2048,512]{1,0:T(8,128)(2,1)} %refs_1_.15, ...), custom_call_target="tpu_custom_call" | custom-call | flops 1000 | bytes 1000 | tf_op jit(solution)/shard_map/project_1/pallas_call | solution.py:632
  53.0 3.7 %attend_1.1 = (f32[256,1024]{1,0:T(8,128)S(1)}, bf16[256,1024]{1,0:T(8,128)(2,1)S(1)}, bf16[512,256]{1,0:T(8,128)(2,1)S(1)}, f32[8,256]{1,0:T(8,128)S(1)}, bf16[16,256]{1,0:T(8,128)(2,1)S(1)}) custom-call(s32[4]{0:T(128)S(1)} %pad_add_fusion.info.refs_0_, bf16[512,2048]{1,0:T(8,128)(2,1)} %refs_3_.5, ...), custom_call_target="tpu_custom_call" | custom-call | flops 1000 | bytes 1000 | tf_op jit(solution)/shard_map/attend_1/pallas_call | solution.py:632
  56.8 3.3 %collective-permute-done.11.refs_1_ = bf16[256,1024]{1,0:T(8,128)(2,1)S(1)} collective-permute-done((bf16[256,1024]{1,0:T(8,128)(2,1)S(1)}, bf16[256,1024]{1,0:T(8,128)(2,1)S(1)}, u32[]{:S(2)}, u32[]{:S(2)}) %collective-permute-start.11) | collective-permute-done | bytes 524320 | tf_op jit(solution)/shard_map/ppermute | solution.py:671
  62.8 0.7 collective-permute-done.8.refs_12_.refs_11_
  63.5 0.7 collective-permute-done.12.refs_8_
  64.2 12.9 %front_0.1 = (bf16[256,2048]{1,0:T(8,128)(2,1)S(1)}, f32[256,512]{1,0:T(8,128)S(1)}, bf16[256,2048]{1,0:T(8,128)(2,1)S(1)}, bf16[256,2048]{1,0:T(8,128)(2,1)S(1)...) custom-call(s32[4]{0:T(128)S(1)} %pad_add_fusion.info.refs_0_, ...), custom_call_target="tpu_custom_call" | custom-call | flops 1000 | bytes 1000 | tf_op jit(solution)/shard_map/front_0/pallas_call | solution.py:632
  77.1 0.8 copy-done.21
  78.2 1.8 collective-permute-done.16.refs_8_
  80.0 12.2 %front_1.1 = (bf16[256,2048]{1,0:T(8,128)(2,1)S(1)}, f32[256,512]{1,0:T(8,128)S(1)}, bf16[256,2048]{1,0:T(8,128)(2,1)S(1)}, bf16[256,2048]{1,0:T(8,128)(2,1)S(1)...) custom-call(s32[4]{0:T(128)S(1)} %pad_add_fusion.info.refs_0_, ...), custom_call_target="tpu_custom_call" | custom-call | flops 1000 | bytes 1000 | tf_op jit(solution)/shard_map/front_1/pallas_call | solution.py:632
  92.2 2.9 %collective-permute-start.17 = (bf16[1,192,512]{2,1,0:T(8,128)(2,1)S(1)}, bf16[1,192,512]{2,1,0:T(8,128)(2,1)S(1)}, u32[]{:S(2)}, u32[]{:S(2)}) collective-permute-start(bf16[1,192,512]{2,1,0:T(8,128)(2,1)S(1)} %bitcast.36), channel_id=1, source_target_pairs={{0,16},{4,20},{8,24},{12,28},{16,0},{20,4},{24,8},{28,12},{1,17},{... | collective-permute-start | bytes 589832 | tf_op jit(solution)/shard_map/ppermute | solution.py:671
  95.1 7.9 %back_1.1 = (f32[256,16]{1,0:T(8,128)S(1)}, f32[256,1024]{1,0:T(8,128)S(1)}, bf16[256,1024]{1,0:T(8,128)(2,1)S(1)}, f32[48,2048]{1,0:T(8,128)S(1)}) custom-call(s32[4]{0:T(128)S(1)} %pad_add_fusion.info.refs_0_, bf16[2,2048,2048]{2,1,0:T(8,128)(2,1)S(1)} %get-tuple-element.147.refs_1_, bf16[256,2048]{1,0:T(8,128)(2,1)S(1)} %get-tuple-element.157.refs_2_, ...), custom_call_target="tpu_custom_call" | custom-call | flops 1000 | bytes 1000 | tf_op jit(solution)/shard_map/back_1/pallas_call | solution.py:632
  103.0 1.5 collective-permute-done.17
  104.6 1.8 collective-permute-start.20
  107.6 7.9 %back_0.1 = (f32[256,16]{1,0:T(8,128)S(1)}, f32[304,1024]{1,0:T(8,128)S(1)}, bf16[304,1024]{1,0:T(8,128)(2,1)S(1)}) custom-call(s32[4]{0:T(128)S(1)} %pad_add_fusion.info.refs_0_, bf16[2,2048,2048]{2,1,0:T(8,128)(2,1)S(1)} %get-tuple-element.147.refs_1_, bf16[256,2048]{1,0:T(8,128)(2,1)S(1)} %get-tuple-element.148.refs_2_, ...), custom_call_target="tpu_custom_call" | custom-call | flops 1000 | bytes 1000 | tf_op jit(solution)/shard_map/back_0/pallas_call | solution.py:632
  116.2 1.5 collective-permute-done.19.refs_1_
  117.6 3.2 %collective-permute-done.22.refs_1_ = bf16[256,1024]{1,0:T(8,128)(2,1)S(1)} collective-permute-done((bf16[256,1024]{1,0:T(8,128)(2,1)S(1)}, bf16[256,1024]{1,0:T(8,128)(2,1)S(1)}, u32[]{:S(2)}, u32[]{:S(2)}) %collective-permute-start.22) | collective-permute-done | bytes 524320 | tf_op jit(solution)/shard_map/ppermute | solution.py:671
  121.8 1.5 collective-permute-start.26
  123.4 10.5 %attend_back_1.1 = (f32[256,512]{1,0:T(8,128)S(1)}, f32[256,1024]{1,0:T(8,128)S(1)}, bf16[256,1024]{1,0:T(8,128)(2,1)S(1)}, f32[256,1]{1,0:T(8,128)S(1)}, f32[48...) custom-call(s32[4]{0:T(128)S(1)} %pad_add_fusion.info.refs_0_, ...), custom_call_target="tpu_custom_call" | custom-call | flops 1000 | bytes 1000 | tf_op jit(solution)/shard_map/attend_back_1/pallas_call | solution.py:632
  134.1 3.5 %collective-permute-done.23.refs_1_ = bf16[304,1024]{1,0:T(8,128)(2,1)S(1)} collective-permute-done((bf16[304,1024]{1,0:T(8,128)(2,1)S(1)}, bf16[304,1024]{1,0:T(8,128)(2,1)S(1)}, u32[]{:S(2)}, u32[]{:S(2)}) %collective-permute-start.23) | collective-permute-done | bytes 622624 | tf_op jit(solution)/shard_map/ppermute | solution.py:671
  138.6 3.4 %collective-permute-start.28 = (bf16[1,48,1024]{2,1,0:T(8,128)(2,1)S(1)}, bf16[1,48,1024]{2,1,0:T(8,128)(2,1)S(1)}, u32[]{:S(2)}, u32[]{:S(2)}) collective-permute-start(bf16[1,48,1024]{2,1,0:T(8,128)(2,1)S(1)} %slice_bitcast_fusion), channel_id=1, source_target_pairs={{0,16},{4,20},{8,24},{12,28},{16,0},{20,4},{24,8},{28,12},{1,17},{... | collective-permute-start | bytes 294920 | tf_op jit(solution)/shard_map/ppermute | solution.py:671
  142.1 4.8 %down_1.1 = (f32[256,1024]{1,0:T(8,128)S(1)}, bf16[256,1024]{1,0:T(8,128)(2,1)}) custom-call(s32[4]{0:T(128)S(1)} %pad_add_fusion.info.refs_0_, bf16[2048,2048]{1,0:T(8,128)(2,1)S(1)} %bitcast.19, bf16[256,2048]{1,0:T(8,128)(2,1)S(1)} %get-tuple-element.159.refs_4_.refs_2_, f32[256,16]{1,0:T(8,128)S(1)} %get-tuple-element.193.refs_3_, ...), custom_call_target="tpu_custom_call" | custom-call | flops 1000 | bytes 1000 | tf_op jit(solution)/shard_map/down_1/pallas_call | solution.py:632
  146.8 1.0 copy-done.4
  147.9 9.8 %attend_back_0.1 = (f32[256,512]{1,0:T(8,128)S(1)}, f32[256,1024]{1,0:T(8,128)S(1)}, bf16[256,1024]{1,0:T(8,128)(2,1)S(1)}, f32[256,1]{1,0:T(8,128)S(1)}, bf16[4...) custom-call(s32[4]{0:T(128)S(1)} %pad_add_fusion.info.refs_0_, ...), custom_call_target="tpu_custom_call" | custom-call | flops 1000 | bytes 1000 | tf_op jit(solution)/shard_map/attend_back_0/pallas_call | solution.py:632
  158.4 1.8 collective-permute-done.30.refs_1_
  160.2 1.5 collective-permute-start.31
  162.3 0.7 collective-permute-start.33
  163.0 2.8 %collective-permute-done.31.refs_3_ = bf16[96,512]{1,0:T(8,128)(2,1)S(1)} collective-permute-done((bf16[96,512]{1,0:T(8,128)(2,1)S(1)}, bf16[96,512]{1,0:T(8,128)(2,1)S(1)}, u32[]{:S(2)}, u32[]{:S(2)}) %collective-permute-start.31) | collective-permute-done | bytes 98336 | tf_op jit(solution)/shard_map/ppermute | solution.py:671
  165.9 4.5 %down_0.1 = (f32[256,1024]{1,0:T(8,128)S(1)}, bf16[256,1024]{1,0:T(8,128)(2,1)}) custom-call(s32[4]{0:T(128)S(1)} %pad_add_fusion.info.refs_0_, bf16[2048,2048]{1,0:T(8,128)(2,1)S(1)} %bitcast.19, bf16[256,2048]{1,0:T(8,128)(2,1)S(1)} %copy-done.3, f32[256,16]{1,0:T(8,128)S(1)} %get-tuple-element.171.refs_3_, bf16[16,2048]{1,0:T(8,128)(2,1)S(1)} %copy-done.14, ...), custom_call_target="tpu_custom_call" | custom-call | flops 1000 | bytes 1000 | tf_op jit(solution)/shard_map/down_0/pallas_call | solution.py:632
  170.5 2.4 %collective-permute-done.34 = bf16[1,112,512]{2,1,0:T(8,128)(2,1)S(1)} collective-permute-done((bf16[1,112,512]{2,1,0:T(8,128)(2,1)S(1)}, bf16[1,112,512]{2,1,0:T(8,128)(2,1)S(1)}, u32[]{:S(2)}, u32[]{:S(2)}) %collective-permute-start.34) | collective-permute-done | bytes 114720 | tf_op jit(solution)/shard_map/ppermute | solution.py:671
  173.6 0.8 copy-done.8
  174.4 3.5 %all-to-all-start.1 = ((bf16[8,64,512]{2,1,0:T(8,128)(2,1)}), bf16[8,64,512]{2,1,0:T(8,128)(2,1)S(1)}, u32[]{:S(2)}, u32[]{:S(2)}) async-start(bf16[8,64,512]{2,1,0:T(8,128)(2,1)} %bitcast.35), calls=%async_computation.1 | async-start | bytes 1048576 | tf_op jit(solution)/shard_map/all_to_all | solution.py:826
  178.0 1.2 high_sum.7
  179.2 1.5 collective-permute-start.38
  180.7 1.9 collective-permute-start.39
  182.6 1.5 collective-permute-start.45
  184.0 0.7 constant_dynamic-update-slice_fusion.3
  184.7 8.9 %collective-permute-done.39 = bf16[2,112,512]{2,1,0:T(8,128)(2,1)S(1)} collective-permute-done((bf16[2,112,512]{2,1,0:T(8,128)(2,1)S(1)}, bf16[2,112,512]{2,1,0:T(8,128)(2,1)S(1)}, u32[]{:S(2)}, u32[]{:S(2)}) %collective-permute-start.39) | collective-permute-done | bytes 229408 | tf_op jit(solution)/shard_map/ppermute | solution.py:671
  193.6 0.7 constant_dynamic-update-slice_fusion.2.refs_0_
  194.3 1.5 collective-permute-start.40
  195.8 2.1 output.1
  197.9 3.9 %all-to-all-start.2 = ((bf16[8,64,512]{2,1,0:T(8,128)(2,1)}), bf16[8,64,512]{2,1,0:T(8,128)(2,1)S(1)}, u32[]{:S(2)}, u32[]{:S(2)}) async-start(bf16[8,64,512]{2,1,0:T(8,128)(2,1)} %bitcast.14), calls=%async_computation.2 | async-start | bytes 1048576 | tf_op jit(solution)/shard_map/all_to_all | solution.py:826
  202.3 1.0 slice.34.refs_2_
  203.3 1.4 collective-permute-start.43
  204.7 5.9 %collective-permute-done.40.refs_1_ = bf16[4,112,512]{2,1,0:T(8,128)(2,1)} collective-permute-done((bf16[4,112,512]{2,1,0:T(8,128)(2,1)}, bf16[4,112,512]{2,1,0:T(8,128)(2,1)}, u32[]{:S(2)}, u32[]{:S(2)}) %collective-permute-start.40) | collective-permute-done | bytes 458784 | tf_op jit(solution)/shard_map/ppermute | solution.py:671
  210.5 1.0 slice.35.refs_3_
  212.0 1.0 copy-done.30
  213.0 5.1 %feedforward_sum.1 = (f32[8,32,2048]{2,1,0:T(8,128)}, f32[8,16,2048]{2,1,0:T(8,128)}, f32[8,2,16,2048]{3,2,1,0:T(8,128)}, f32[8,16,2048]{2,1,0:T(8,128)}) custom-call(s32[4]{0:T(128)S(1)} %pad_add_fusion.info.refs_0_, s32[8]{0:T(128)S(1)} %copy-done.57, bf16[2,192,512]{2,1,0:T(8,128)(2,1)S(1)} %copy-done.12, bf16[2,192,512]{2,1,0:T(8,128)(2,1)S(1)} %copy-done.28, ...), custom_call_target="tpu_custom_call" | custom-call | bytes 12000000 | tf_op jit(solution)/shard_map/feedforward_sum/pallas_call | solution.py:655
  219.1 1.4 collect_grad.1
  220.5 4.8 %attention_sum.1 = (f32[8,48,2048]{2,1,0:T(8,128)}, f32[8,16,2048]{2,1,0:T(8,128)}, f32[8,16,512]{2,1,0:T(8,128)}, f32[8,2,16,128]{3,2,1,0:T(8,128)}, f32[8,16,512]{2,1,0:T(8,128)}) custom-call(s32[4]{0:T(128)S(1)} %pad_add_fusion.info.refs_0_, s32[8]{0:T(128)S(1)} %copy-done.57, bf16[4,112,512]{2,1,0:T(8,128)(2,1)} %constant_dynamic-update-slice_fusion.2.refs_0_, ...), custom_call_target="tpu_custom_call" | custom-call | bytes 12000000 | tf_op jit(solution)/shard_map/attention_sum/pallas_call | solution.py:655
  225.3 1.4 collect_out.1
  (224 shorter events, 17.3 us)
Async XLA Ops:
  3.9 23.0 %all-to-all-start = ((bf16[8,64,512]{2,1,0:T(8,128)(2,1)}), bf16[8,64,512]{2,1,0:T(8,128)(2,1)S(1)}, u32[]{:S(2)}, u32[]{:S(2)}) async-start(bf16[8,64,512]{2,1,0:T(8,128)(2,1)} %deal.1), calls=%async_computation | async-start | bytes 1048576 | tf_op jit(solution)/shard_map/all_to_all | solution.py:750
  11.2 8.2 %collective-permute-start = (bf16[2,512]{1,0:T(2,128)(2,1)S(1)}, bf16[2,512]{1,0:T(2,128)(2,1)S(1)}, u32[]{:S(2)}, u32[]{:S(2)}) collective-permute-start(bf16[2,512]{1,0:T(2,128)(2,1)S(1)} %pad_maximum_fusion.4), channel_id=1, source_target_pairs={{0,1},{1,0},{2,3},{3,2},{4,5},{5,4},{6,7},{7,6},{8,9},{9,8},{10,11... | collective-permute-start | bytes 6152 | tf_op jit(solution)/shard_map/ppermute | solution.py:671
  11.3 3.7 %collective-permute-start.1 = (bf16[2,512]{1,0:T(2,128)(2,1)S(1)}, bf16[2,512]{1,0:T(2,128)(2,1)S(1)}, u32[]{:S(2)}, u32[]{:S(2)}) collective-permute-start(bf16[2,512]{1,0:T(2,128)(2,1)S(1)} %pad_maximum_fusion.4), channel_id=1, source_target_pairs={{0,2},{1,3},{2,0},{3,1},{4,6},{5,7},{6,4},{7,5},{8,10},{9,11},{10,... | collective-permute-start | bytes 6152 | tf_op jit(solution)/shard_map/ppermute | solution.py:671
  12.9 14.0 %collective-permute-start.3 = (bf16[512,512]{1,0:T(8,128)(2,1)S(1)}, bf16[512,512]{1,0:T(8,128)(2,1)S(1)}, u32[]{:S(2)}, u32[]{:S(2)}) collective-permute-start(bf16[512,512]{1,0:T(8,128)(2,1)S(1)} %bitcast.29), channel_id=1, source_target_pairs={{0,2},{1,3},{2,0},{3,1},{4,6},{5,7},{6,4},{7,5},{8,10},{9,11},{10,... | collective-permute-start | bytes 1572872 | tf_op jit(solution)/shard_map/ppermute | solution.py:671
  14.9 4.5 %collective-permute-start.2 = (bf16[2,512]{1,0:T(2,128)(2,1)S(1)}, bf16[2,512]{1,0:T(2,128)(2,1)S(1)}, u32[]{:S(2)}, u32[]{:S(2)}) collective-permute-start(bf16[2,512]{1,0:T(2,128)(2,1)S(1)} %collective-permute-done.1), channel_id=1, source_target_pairs={{0,1},{1,0},{2,3},{3,2},{4,5},{5,4},{6,7},{7,6},{8,9},{9,8},{10,11... | collective-permute-start | bytes 6152 | tf_op jit(solution)/shard_map/ppermute | solution.py:671
  16.3 19.8 %copy-start.44 = (f32[32,256]{1,0:T(8,128)S(1)}, f32[32,256]{1,0:T(8,128)}, u32[]{:S(2)}) copy-start(f32[32,256]{1,0:T(8,128)} %constant.21.clone.refs_12_.refs_22_) | copy-start | bytes 98308
  16.3 19.8 %copy-start.46 = (f32[32,256]{1,0:T(8,128)S(1)}, f32[32,256]{1,0:T(8,128)}, u32[]{:S(2)}) copy-start(f32[32,256]{1,0:T(8,128)} %constant.19.clone.refs_11_.refs_21_) | copy-start | bytes 98308
  19.4 28.8 %copy-start.37 = (bf16[16,512]{1,0:T(8,128)(2,1)}, bf16[16,512]{1,0:T(8,128)(2,1)S(1)}, u32[]{:S(2)}) copy-start(bf16[16,512]{1,0:T(8,128)(2,1)S(1)} %get-tuple-element.121.refs_9_.refs_17_) | copy-start | bytes 49156
  19.4 28.8 %copy-start.48 = (bf16[2,16,128]{2,1,0:T(8,128)(2,1)}, bf16[2,16,128]{2,1,0:T(8,128)(2,1)S(1)}, u32[]{:S(2)}) copy-start(bf16[2,16,128]{2,1,0:T(8,128)(2,1)S(1)} %get-tuple-element.122.refs_10_.refs_18_) | copy-start | bytes 24580
  19.4 33.6 %copy-start.17 = (bf16[16,2048]{1,0:T(8,128)(2,1)}, bf16[16,2048]{1,0:T(8,128)(2,1)S(1)}, u32[]{:S(2)}) copy-start(bf16[16,2048]{1,0:T(8,128)(2,1)S(1)} %get-tuple-element.125.refs_4_.refs_20_) | copy-start | bytes 196612
  19.4 33.6 %copy-start.35 = (bf16[16,512]{1,0:T(8,128)(2,1)}, bf16[16,512]{1,0:T(8,128)(2,1)S(1)}, u32[]{:S(2)}) copy-start(bf16[16,512]{1,0:T(8,128)(2,1)S(1)} %get-tuple-element.124.refs_3_.refs_19_) | copy-start | bytes 49156
  19.4 122.6 %copy-start.13 = (bf16[16,2048]{1,0:T(8,128)(2,1)}, bf16[16,2048]{1,0:T(8,128)(2,1)S(1)}, u32[]{:S(2)}) copy-start(bf16[16,2048]{1,0:T(8,128)(2,1)S(1)} %get-tuple-element.133.refs_15_.refs_4_) | copy-start | bytes 196612
  26.9 7.6 %collective-permute-start.5 = (bf16[256,512]{1,0:T(8,128)(2,1)S(1)}, bf16[256,512]{1,0:T(8,128)(2,1)S(1)}, u32[]{:S(2)}, u32[]{:S(2)}) collective-permute-start(bf16[256,512]{1,0:T(8,128)(2,1)S(1)} %get-tuple-element.230), channel_id=1, source_target_pairs={{0,2},{1,3},{2,0},{3,1},{4,6},{5,7},{6,4},{7,5},{8,10},{9,11},{10,... | collective-permute-start | bytes 786440 | tf_op jit(solution)/shard_map/ppermute | solution.py:671
  27.5 8.6 %collective-permute-start.4 = (bf16[512,512]{1,0:T(8,128)(2,1)S(1)}, bf16[512,512]{1,0:T(8,128)(2,1)S(1)}, u32[]{:S(2)}, u32[]{:S(2)}) collective-permute-start(bf16[512,512]{1,0:T(8,128)(2,1)S(1)} %bitcast.21), channel_id=1, source_target_pairs={{0,1},{1,0},{2,3},{3,2},{4,5},{5,4},{6,7},{7,6},{8,9},{9,8},{10,11... | collective-permute-start | bytes 1572872 | tf_op jit(solution)/shard_map/ppermute | solution.py:671
  34.5 1.5 collective-permute-start.6
  34.5 9.4 %collective-permute-start.9 = (bf16[256,512]{1,0:T(8,128)(2,1)S(1)}, bf16[256,512]{1,0:T(8,128)(2,1)S(1)}, u32[]{:S(2)}, u32[]{:S(2)}) collective-permute-start(bf16[256,512]{1,0:T(8,128)(2,1)S(1)} %get-tuple-element.229), channel_id=1, source_target_pairs={{0,2},{1,3},{2,0},{3,1},{4,6},{5,7},{6,4},{7,5},{8,10},{9,11},{10,... | collective-permute-start | bytes 786440 | tf_op jit(solution)/shard_map/ppermute | solution.py:671
  43.9 2.0 collective-permute-start.10
  46.0 14.0 %collective-permute-start.11 = (bf16[256,1024]{1,0:T(8,128)(2,1)S(1)}, bf16[256,1024]{1,0:T(8,128)(2,1)S(1)}, u32[]{:S(2)}, u32[]{:S(2)}) collective-permute-start(bf16[256,1024]{1,0:T(8,128)(2,1)S(1)} %pair_sum.4.refs_0_.refs_14_), channel_id=1, source_target_pairs={{0,2},{1,3},{2,0},{3,1},{4,6},{5,7},{6,4},{7,5},{8,10},{9,11},{10,... | collective-permute-start | bytes 1572872 | tf_op jit(solution)/shard_map/ppermute | solution.py:671
  46.6 1.5 collective-permute-start.13
  56.7 20.4 %copy-start.31 = (bf16[512,256]{1,0:T(8,128)(2,1)}, bf16[512,256]{1,0:T(8,128)(2,1)S(1)}, u32[]{:S(2)}) copy-start(bf16[512,256]{1,0:T(8,128)(2,1)S(1)} %get-tuple-element.175.refs_25_) | copy-start | bytes 786436
  60.1 1.9 collective-permute-start.14
  60.1 2.7 %collective-permute-start.7 = (bf16[512,512]{1,0:T(8,128)(2,1)S(1)}, bf16[512,512]{1,0:T(8,128)(2,1)S(1)}, u32[]{:S(2)}, u32[]{:S(2)}) collective-permute-start(bf16[512,512]{1,0:T(8,128)(2,1)S(1)} %bitcast.30), channel_id=1, source_target_pairs={{0,1},{1,0},{2,3},{3,2},{4,5},{5,4},{6,7},{7,6},{8,9},{9,8},{10,11... | collective-permute-start | bytes 1572872 | tf_op jit(solution)/shard_map/ppermute | solution.py:671
  60.6 2.9 %collective-permute-start.8 = (bf16[512,512]{1,0:T(8,128)(2,1)S(1)}, bf16[512,512]{1,0:T(8,128)(2,1)S(1)}, u32[]{:S(2)}, u32[]{:S(2)}) collective-permute-start(bf16[512,512]{1,0:T(8,128)(2,1)S(1)} %collective-permute-done.3.refs_11_.refs_10_), channel_id=1, source_target_pairs={{0,1},{1,0},{2,3},{3,2},{4,5},{5,4},{6,7},{7,6},{8,9},{9,8},{10,11... | collective-permute-start | bytes 1572872 | tf_op jit(solution)/shard_map/ppermute | solution.py:671
  60.7 3.5 %collective-permute-start.12 = (bf16[256,1024]{1,0:T(8,128)(2,1)S(1)}, bf16[256,1024]{1,0:T(8,128)(2,1)S(1)}, u32[]{:S(2)}, u32[]{:S(2)}) collective-permute-start(bf16[256,1024]{1,0:T(8,128)(2,1)S(1)} %far_sum.4.refs_7_), channel_id=1, source_target_pairs={{0,1},{1,0},{2,3},{3,2},{4,5},{5,4},{6,7},{7,6},{8,9},{9,8},{10,11... | collective-permute-start | bytes 1572872 | tf_op jit(solution)/shard_map/ppermute | solution.py:671
  62.1 15.8 %collective-permute-start.15 = (bf16[256,1024]{1,0:T(8,128)(2,1)S(1)}, bf16[256,1024]{1,0:T(8,128)(2,1)S(1)}, u32[]{:S(2)}, u32[]{:S(2)}) collective-permute-start(bf16[256,1024]{1,0:T(8,128)(2,1)S(1)} %pair_sum.5.refs_19_.refs_0_), channel_id=1, source_target_pairs={{0,2},{1,3},{2,0},{3,1},{4,6},{5,7},{6,4},{7,5},{8,10},{9,11},{10,... | collective-permute-start | bytes 1572872 | tf_op jit(solution)/shard_map/ppermute | solution.py:671
  77.9 29.7 %copy-start.2 = (bf16[256,2048]{1,0:T(8,128)(2,1)}, bf16[256,2048]{1,0:T(8,128)(2,1)S(1)}, u32[]{:S(2)}) copy-start(bf16[256,2048]{1,0:T(8,128)(2,1)S(1)} %get-tuple-element.150.refs_4_.refs_2_) | copy-start | bytes 3145732
  78.0 2.0 collective-permute-start.16
  92.2 12.3 %collective-permute-start.17 = (bf16[1,192,512]{2,1,0:T(8,128)(2,1)S(1)}, bf16[1,192,512]{2,1,0:T(8,128)(2,1)S(1)}, u32[]{:S(2)}, u32[]{:S(2)}) collective-permute-start(bf16[1,192,512]{2,1,0:T(8,128)(2,1)S(1)} %bitcast.36), channel_id=1, source_target_pairs={{0,16},{4,20},{8,24},{12,28},{16,0},{20,4},{24,8},{28,12},{1,17},{... | collective-permute-start | bytes 589832 | tf_op jit(solution)/shard_map/ppermute | solution.py:671
  104.5 2.4 %collective-permute-start.18 = (bf16[256,1024]{1,0:T(8,128)(2,1)S(1)}, bf16[256,1024]{1,0:T(8,128)(2,1)S(1)}, u32[]{:S(2)}, u32[]{:S(2)}) collective-permute-start(bf16[256,1024]{1,0:T(8,128)(2,1)S(1)} %get-tuple-element.167), channel_id=1, source_target_pairs={{0,1},{1,0},{2,3},{3,2},{4,5},{5,4},{6,7},{7,6},{8,9},{9,8},{10,11... | collective-permute-start | bytes 1572872 | tf_op jit(solution)/shard_map/ppermute | solution.py:671
  104.6 11.6 %collective-permute-start.20 = (bf16[2,192,512]{2,1,0:T(8,128)(2,1)S(1)}, bf16[2,192,512]{2,1,0:T(8,128)(2,1)S(1)}, u32[]{:S(2)}, u32[]{:S(2)}) collective-permute-start(bf16[2,192,512]{2,1,0:T(8,128)(2,1)S(1)} %pad_maximum_fusion.refs_0_), channel_id=1, source_target_pairs={{0,4},{4,0},{8,12},{12,8},{16,20},{20,16},{24,28},{28,24},{1,5},{5... | collective-permute-start | bytes 1179656 | tf_op jit(solution)/shard_map/ppermute | solution.py:671
  106.4 11.2 %collective-permute-start.19 = (bf16[2,192,512]{2,1,0:T(8,128)(2,1)S(1)}, bf16[2,192,512]{2,1,0:T(8,128)(2,1)S(1)}, u32[]{:S(2)}, u32[]{:S(2)}) collective-permute-start(bf16[2,192,512]{2,1,0:T(8,128)(2,1)S(1)} %pad_maximum_fusion.refs_0_), channel_id=1, source_target_pairs={{0,8},{4,12},{8,0},{12,4},{16,24},{20,28},{24,16},{28,20},{1,9},{5... | collective-permute-start | bytes 1179656 | tf_op jit(solution)/shard_map/ppermute | solution.py:671
  107.0 13.8 %collective-permute-start.22 = (bf16[256,1024]{1,0:T(8,128)(2,1)S(1)}, bf16[256,1024]{1,0:T(8,128)(2,1)S(1)}, u32[]{:S(2)}, u32[]{:S(2)}) collective-permute-start(bf16[256,1024]{1,0:T(8,128)(2,1)S(1)} %pair_sum.6.refs_11_.refs_0_), channel_id=1, source_target_pairs={{0,2},{1,3},{2,0},{3,1},{4,6},{5,7},{6,4},{7,5},{8,10},{9,11},{10,... | collective-permute-start | bytes 1572872 | tf_op jit(solution)/shard_map/ppermute | solution.py:671
  117.6 3.4 %collective-permute-start.21 = (bf16[304,1024]{1,0:T(8,128)(2,1)S(1)}, bf16[304,1024]{1,0:T(8,128)(2,1)S(1)}, u32[]{:S(2)}, u32[]{:S(2)}) collective-permute-start(bf16[304,1024]{1,0:T(8,128)(2,1)S(1)} %get-tuple-element.170), channel_id=1, source_target_pairs={{0,1},{1,0},{2,3},{3,2},{4,5},{5,4},{6,7},{7,6},{8,9},{9,8},{10,11... | collective-permute-start | bytes 1867784 | tf_op jit(solution)/shard_map/ppermute | solution.py:671
  120.9 2.4 %collective-permute-start.24 = (bf16[256,1024]{1,0:T(8,128)(2,1)S(1)}, bf16[256,1024]{1,0:T(8,128)(2,1)S(1)}, u32[]{:S(2)}, u32[]{:S(2)}) collective-permute-start(bf16[256,1024]{1,0:T(8,128)(2,1)S(1)} %far_sum.6.refs_13_), channel_id=1, source_target_pairs={{0,1},{1,0},{2,3},{3,2},{4,5},{5,4},{6,7},{7,6},{8,9},{9,8},{10,11... | collective-permute-start | bytes 1572872 | tf_op jit(solution)/shard_map/ppermute | solution.py:671
  121.1 16.5 %collective-permute-start.23 = (bf16[304,1024]{1,0:T(8,128)(2,1)S(1)}, bf16[304,1024]{1,0:T(8,128)(2,1)S(1)}, u32[]{:S(2)}, u32[]{:S(2)}) collective-permute-start(bf16[304,1024]{1,0:T(8,128)(2,1)S(1)} %pair_sum.7.refs_34_.refs_0_), channel_id=1, source_target_pairs={{0,2},{1,3},{2,0},{3,1},{4,6},{5,7},{6,4},{7,5},{8,10},{9,11},{10,... | collective-permute-start | bytes 1867784 | tf_op jit(solution)/shard_map/ppermute | solution.py:671
  121.8 12.2 %collective-permute-start.26 = (bf16[2,192,512]{2,1,0:T(8,128)(2,1)S(1)}, bf16[2,192,512]{2,1,0:T(8,128)(2,1)S(1)}, u32[]{:S(2)}, u32[]{:S(2)}) collective-permute-start(bf16[2,192,512]{2,1,0:T(8,128)(2,1)S(1)} %collective-permute-done.19.refs_1_), channel_id=1, source_target_pairs={{0,4},{4,0},{8,12},{12,8},{16,20},{20,16},{24,28},{28,24},{1,5},{5... | collective-permute-start | bytes 1179656 | tf_op jit(solution)/shard_map/ppermute | solution.py:671
  123.3 18.7 %slice-start = ((s8[8388608]{0:T(1024)(128)(4,1)}), s8[4194304]{0:T(1024)(128)(4,1)S(1)}, s32[]{:S(2)}) async-start(s8[8388608]{0:T(1024)(128)(4,1)} %bitcast.18), calls=%async_computation.3 | async-start | bytes 8388608
  123.4 18.6 %slice-start.1 = ((s8[8388608]{0:T(1024)(128)(4,1)}), s8[4194304]{0:T(1024)(128)(4,1)S(1)}, s32[]{:S(2)}) async-start(s8[8388608]{0:T(1024)(128)(4,1)} %bitcast.18), calls=%async_computation.4 | async-start | bytes 8388608
  134.0 3.9 %collective-permute-start.27 = (bf16[256,1024]{1,0:T(8,128)(2,1)S(1)}, bf16[256,1024]{1,0:T(8,128)(2,1)S(1)}, u32[]{:S(2)}, u32[]{:S(2)}) collective-permute-start(bf16[256,1024]{1,0:T(8,128)(2,1)S(1)} %get-tuple-element.192), channel_id=1, source_target_pairs={{0,1},{1,0},{2,3},{3,2},{4,5},{5,4},{6,7},{7,6},{8,9},{9,8},{10,11... | collective-permute-start | bytes 1572872 | tf_op jit(solution)/shard_map/ppermute | solution.py:671
  137.8 10.0 %collective-permute-start.25 = (bf16[304,1024]{1,0:T(8,128)(2,1)S(1)}, bf16[304,1024]{1,0:T(8,128)(2,1)S(1)}, u32[]{:S(2)}, u32[]{:S(2)}) collective-permute-start(bf16[304,1024]{1,0:T(8,128)(2,1)S(1)} %far_sum.7.refs_13_), channel_id=1, source_target_pairs={{0,1},{1,0},{2,3},{3,2},{4,5},{5,4},{6,7},{7,6},{8,9},{9,8},{10,11... | collective-permute-start | bytes 1867784 | tf_op jit(solution)/shard_map/ppermute | solution.py:671
  137.9 19.8 %collective-permute-start.29 = (bf16[256,512]{1,0:T(8,128)(2,1)S(1)}, bf16[256,512]{1,0:T(8,128)(2,1)S(1)}, u32[]{:S(2)}, u32[]{:S(2)}) collective-permute-start(bf16[256,512]{1,0:T(8,128)(2,1)S(1)} %high_sum.4.refs_36_), channel_id=1, source_target_pairs={{0,2},{1,3},{2,0},{3,1},{4,6},{5,7},{6,4},{7,5},{8,10},{9,11},{10,... | collective-permute-start | bytes 786440 | tf_op jit(solution)/shard_map/ppermute | solution.py:671
  138.6 19.1 %collective-permute-start.28 = (bf16[1,48,1024]{2,1,0:T(8,128)(2,1)S(1)}, bf16[1,48,1024]{2,1,0:T(8,128)(2,1)S(1)}, u32[]{:S(2)}, u32[]{:S(2)}) collective-permute-start(bf16[1,48,1024]{2,1,0:T(8,128)(2,1)S(1)} %slice_bitcast_fusion), channel_id=1, source_target_pairs={{0,16},{4,20},{8,24},{12,28},{16,0},{20,4},{24,8},{28,12},{1,17},{... | collective-permute-start | bytes 294920 | tf_op jit(solution)/shard_map/ppermute | solution.py:671
  157.7 4.6 %collective-permute-start.32 = (bf16[256,1024]{1,0:T(8,128)(2,1)S(1)}, bf16[256,1024]{1,0:T(8,128)(2,1)S(1)}, u32[]{:S(2)}, u32[]{:S(2)}) collective-permute-start(bf16[256,1024]{1,0:T(8,128)(2,1)S(1)} %get-tuple-element.202), channel_id=1, source_target_pairs={{0,1},{1,0},{2,3},{3,2},{4,5},{5,4},{6,7},{7,6},{8,9},{9,8},{10,11... | collective-permute-start | bytes 1572872 | tf_op jit(solution)/shard_map/ppermute | solution.py:671
  157.8 2.5 %collective-permute-start.30 = (bf16[96,1024]{1,0:T(8,128)(2,1)S(1)}, bf16[96,1024]{1,0:T(8,128)(2,1)S(1)}, u32[]{:S(2)}, u32[]{:S(2)}) collective-permute-start(bf16[96,1024]{1,0:T(8,128)(2,1)S(1)} %get-tuple-element.198), channel_id=1, source_target_pairs={{0,1},{1,0},{2,3},{3,2},{4,5},{5,4},{6,7},{7,6},{8,9},{9,8},{10,11... | collective-permute-start | bytes 589832 | tf_op jit(solution)/shard_map/ppermute | solution.py:671
  158.3 19.7 %collective-permute-start.37 = (bf16[256,1024]{1,0:T(8,128)(2,1)}, bf16[256,1024]{1,0:T(8,128)(2,1)S(1)}, u32[]{:S(2)}, u32[]{:S(2)}) collective-permute-start(bf16[256,1024]{1,0:T(8,128)(2,1)} %get-tuple-element.214.refs_37_), channel_id=1, source_target_pairs={{0,1},{1,0},{2,3},{3,2},{4,5},{5,4},{6,7},{7,6},{8,9},{9,8},{10,11... | collective-permute-start | bytes 1572872 | tf_op jit(solution)/shard_map/ppermute | solution.py:671
  160.2 5.5 %collective-permute-start.31 = (bf16[96,512]{1,0:T(8,128)(2,1)S(1)}, bf16[96,512]{1,0:T(8,128)(2,1)S(1)}, u32[]{:S(2)}, u32[]{:S(2)}) collective-permute-start(bf16[96,512]{1,0:T(8,128)(2,1)S(1)} %high_sum.5.refs_2_), channel_id=1, source_target_pairs={{0,2},{1,3},{2,0},{3,1},{4,6},{5,7},{6,4},{7,5},{8,10},{9,11},{10,... | collective-permute-start | bytes 294920 | tf_op jit(solution)/shard_map/ppermute | solution.py:671
  161.7 8.7 %collective-permute-start.35 = (bf16[2,48,1024]{2,1,0:T(8,128)(2,1)S(1)}, bf16[2,48,1024]{2,1,0:T(8,128)(2,1)S(1)}, u32[]{:S(2)}, u32[]{:S(2)}) collective-permute-start(bf16[2,48,1024]{2,1,0:T(8,128)(2,1)S(1)} %pad_maximum_fusion.2), channel_id=1, source_target_pairs={{0,8},{4,12},{8,0},{12,4},{16,24},{20,28},{24,16},{28,20},{1,9},{5... | collective-permute-start | bytes 589832 | tf_op jit(solution)/shard_map/ppermute | solution.py:671
  162.3 10.6 %collective-permute-start.33 = (bf16[256,512]{1,0:T(8,128)(2,1)S(1)}, bf16[256,512]{1,0:T(8,128)(2,1)S(1)}, u32[]{:S(2)}, u32[]{:S(2)}) collective-permute-start(bf16[256,512]{1,0:T(8,128)(2,1)S(1)} %high_sum.6), channel_id=1, source_target_pairs={{0,2},{1,3},{2,0},{3,1},{4,6},{5,7},{6,4},{7,5},{8,10},{9,11},{10,... | collective-permute-start | bytes 786440 | tf_op jit(solution)/shard_map/ppermute | solution.py:671
  165.8 7.1 %collective-permute-start.34 = (bf16[1,112,512]{2,1,0:T(8,128)(2,1)S(1)}, bf16[1,112,512]{2,1,0:T(8,128)(2,1)S(1)}, u32[]{:S(2)}, u32[]{:S(2)}) collective-permute-start(bf16[1,112,512]{2,1,0:T(8,128)(2,1)S(1)} %maximum_bitcast_fusion.refs_6_), channel_id=1, source_target_pairs={{0,16},{4,20},{8,24},{12,28},{16,0},{20,4},{24,8},{28,12},{1,17},{... | collective-permute-start | bytes 344072 | tf_op jit(solution)/shard_map/ppermute | solution.py:671
  170.5 7.5 %collective-permute-start.36 = (bf16[256,1024]{1,0:T(8,128)(2,1)}, bf16[256,1024]{1,0:T(8,128)(2,1)}, u32[]{:S(2)}, u32[]{:S(2)}) collective-permute-start(bf16[256,1024]{1,0:T(8,128)(2,1)} %get-tuple-element.208.refs_14_), channel_id=1, source_target_pairs={{0,1},{1,0},{2,3},{3,2},{4,5},{5,4},{6,7},{7,6},{8,9},{9,8},{10,11... | collective-permute-start | bytes 1572872 | tf_op jit(solution)/shard_map/ppermute | solution.py:671
  174.4 23.5 %all-to-all-start.1 = ((bf16[8,64,512]{2,1,0:T(8,128)(2,1)}), bf16[8,64,512]{2,1,0:T(8,128)(2,1)S(1)}, u32[]{:S(2)}, u32[]{:S(2)}) async-start(bf16[8,64,512]{2,1,0:T(8,128)(2,1)} %bitcast.35), calls=%async_computation.1 | async-start | bytes 1048576 | tf_op jit(solution)/shard_map/all_to_all | solution.py:826
  179.2 16.7 %collective-permute-start.38 = (bf16[512,512]{1,0:T(8,128)(2,1)S(1)}, bf16[512,512]{1,0:T(8,128)(2,1)S(1)}, u32[]{:S(2)}, u32[]{:S(2)}) collective-permute-start(bf16[512,512]{1,0:T(8,128)(2,1)S(1)} %high_sum.7), channel_id=1, source_target_pairs={{0,2},{1,3},{2,0},{3,1},{4,6},{5,7},{6,4},{7,5},{8,10},{9,11},{10,... | collective-permute-start | bytes 1572872 | tf_op jit(solution)/shard_map/ppermute | solution.py:671
  180.7 12.9 %collective-permute-start.39 = (bf16[2,112,512]{2,1,0:T(8,128)(2,1)S(1)}, bf16[2,112,512]{2,1,0:T(8,128)(2,1)S(1)}, u32[]{:S(2)}, u32[]{:S(2)}) collective-permute-start(bf16[2,112,512]{2,1,0:T(8,128)(2,1)S(1)} %copy-done.10), channel_id=1, source_target_pairs={{0,8},{4,12},{8,0},{12,4},{16,24},{20,28},{24,16},{28,20},{1,9},{5... | collective-permute-start | bytes 688136 | tf_op jit(solution)/shard_map/ppermute | solution.py:671
  182.6 19.2 %collective-permute-start.45 = (bf16[4,48,1024]{2,1,0:T(8,128)(2,1)S(1)}, bf16[4,48,1024]{2,1,0:T(8,128)(2,1)}, u32[]{:S(2)}, u32[]{:S(2)}) collective-permute-start(bf16[4,48,1024]{2,1,0:T(8,128)(2,1)S(1)} %constant_dynamic-update-slice_fusion.refs_16_.refs_4_), channel_id=1, source_target_pairs={{0,4},{4,0},{8,12},{12,8},{16,20},{20,16},{24,28},{28,24},{1,5},{5... | collective-permute-start | bytes 1179656 | tf_op jit(solution)/shard_map/ppermute | solution.py:671
  194.3 16.2 %collective-permute-start.40 = (bf16[4,112,512]{2,1,0:T(8,128)(2,1)}, bf16[4,112,512]{2,1,0:T(8,128)(2,1)}, u32[]{:S(2)}, u32[]{:S(2)}) collective-permute-start(bf16[4,112,512]{2,1,0:T(8,128)(2,1)} %constant_dynamic-update-slice_fusion.2.refs_0_), channel_id=1, source_target_pairs={{0,4},{4,0},{8,12},{12,8},{16,20},{20,16},{24,28},{28,24},{1,5},{5... | collective-permute-start | bytes 1376264 | tf_op jit(solution)/shard_map/ppermute | solution.py:671
  197.9 27.4 %all-to-all-start.2 = ((bf16[8,64,512]{2,1,0:T(8,128)(2,1)}), bf16[8,64,512]{2,1,0:T(8,128)(2,1)S(1)}, u32[]{:S(2)}, u32[]{:S(2)}) async-start(bf16[8,64,512]{2,1,0:T(8,128)(2,1)} %bitcast.14), calls=%async_computation.2 | async-start | bytes 1048576 | tf_op jit(solution)/shard_map/all_to_all | solution.py:826
  201.8 10.2 %collective-permute-start.46 = (bf16[4,48,1024]{2,1,0:T(8,128)(2,1)S(1)}, bf16[4,48,1024]{2,1,0:T(8,128)(2,1)S(1)}, u32[]{:S(2)}, u32[]{:S(2)}) collective-permute-start(bf16[4,48,1024]{2,1,0:T(8,128)(2,1)S(1)} %constant_dynamic-update-slice_fusion.refs_16_.refs_4_), channel_id=1, source_target_pairs={{0,1},{1,0},{2,3},{3,2},{4,5},{5,4},{6,7},{7,6},{8,9},{9,8},{10,11... | collective-permute-start | bytes 1179656 | tf_op jit(solution)/shard_map/ppermute | solution.py:671
  201.8 10.1 %collective-permute-start.47 = (bf16[4,48,1024]{2,1,0:T(8,128)(2,1)}, bf16[4,48,1024]{2,1,0:T(8,128)(2,1)S(1)}, u32[]{:S(2)}, u32[]{:S(2)}) collective-permute-start(bf16[4,48,1024]{2,1,0:T(8,128)(2,1)} %collective-permute-done.45.refs_5_), channel_id=1, source_target_pairs={{0,1},{1,0},{2,3},{3,2},{4,5},{5,4},{6,7},{7,6},{8,9},{9,8},{10,11... | collective-permute-start | bytes 1179656 | tf_op jit(solution)/shard_map/ppermute | solution.py:671
  203.3 14.8 %collective-permute-start.43 = (bf16[4,64,512]{2,1,0:T(8,128)(2,1)S(1)}, bf16[4,64,512]{2,1,0:T(8,128)(2,1)S(1)}, u32[]{:S(2)}, u32[]{:S(2)}) collective-permute-start(bf16[4,64,512]{2,1,0:T(8,128)(2,1)S(1)} %slice.34.refs_2_), channel_id=1, source_target_pairs={{0,2},{1,3},{2,0},{3,1},{4,6},{5,7},{6,4},{7,5},{8,10},{9,11},{10,... | collective-permute-start | bytes 786440 | tf_op jit(solution)/shard_map/ppermute | solution.py:671
  211.5 7.2 %collective-permute-start.44 = (bf16[4,64,512]{2,1,0:T(8,128)(2,1)S(1)}, bf16[4,64,512]{2,1,0:T(8,128)(2,1)S(1)}, u32[]{:S(2)}, u32[]{:S(2)}) collective-permute-start(bf16[4,64,512]{2,1,0:T(8,128)(2,1)S(1)} %slice.35.refs_3_), channel_id=1, source_target_pairs={{0,2},{1,3},{2,0},{3,1},{4,6},{5,7},{6,4},{7,5},{8,10},{9,11},{10,... | collective-permute-start | bytes 786440 | tf_op jit(solution)/shard_map/ppermute | solution.py:671
  211.9 8.6 %collective-permute-start.41 = (bf16[4,64,512]{2,1,0:T(8,128)(2,1)S(1)}, bf16[4,64,512]{2,1,0:T(8,128)(2,1)S(1)}, u32[]{:S(2)}, u32[]{:S(2)}) collective-permute-start(bf16[4,64,512]{2,1,0:T(8,128)(2,1)S(1)} %slice.34.refs_2_), channel_id=1, source_target_pairs={{0,1},{1,0},{2,3},{3,2},{4,5},{5,4},{6,7},{7,6},{8,9},{9,8},{10,11... | collective-permute-start | bytes 786440 | tf_op jit(solution)/shard_map/ppermute | solution.py:671
  218.1 2.4 %collective-permute-start.48 = (bf16[4,64,512]{2,1,0:T(8,128)(2,1)S(1)}, bf16[4,64,512]{2,1,0:T(8,128)(2,1)S(1)}, u32[]{:S(2)}, u32[]{:S(2)}) collective-permute-start(bf16[4,64,512]{2,1,0:T(8,128)(2,1)S(1)} %collective-permute-done.43.refs_6_), channel_id=1, source_target_pairs={{0,1},{1,0},{2,3},{3,2},{4,5},{5,4},{6,7},{7,6},{8,9},{9,8},{10,11... | collective-permute-start | bytes 786440 | tf_op jit(solution)/shard_map/ppermute | solution.py:671
  218.6 1.9 collective-permute-start.42
  218.7 1.9 collective-permute-start.49
  (53 other events, 382.0 us)

commit v9 on v7

--- a/solution.py
+++ b/solution.py
@@ -834,33 +834,33 @@
     *hidden[0], wgu, wd = front(0, far_sum(z_own[0], z_far[0]), (), order)
     step = hidden[0][8]
     hidden[1] = front(1, far_sum(z_own[1], late(z_far[1], step)), hidden[0][9:], (step,))
-    fb = hidden[1][9][None]
+    td, d_keep, d_send, fa = back(1, hidden[1], (), (hidden[1][8],))
+    d_own[1] = pair_sum(d_keep, d_send)
+    d_far[1] = far(d_own[1])
+    fb = late(hidden[1][9], d_own[1])[None]
     fb_first = swap(fb, bits[0], "dp", dp)
-    td, d_keep, d_send, fa = back(1, hidden[1], (), (hidden[1][8],))
-    d_own[1] = pair_sum(d_keep, late(d_send, fb_first))
-    d_far[1] = far(d_own[1])
-    fb = fb_more = jnp.concatenate([fb, fb_first], axis=0)
+    td_0, d_keep, d_send = back(0, hidden[0], (fa,), (d_own[1],))
+    total = far_sum(d_own[1], late(d_far[1], td_0))
+    d_own[0] = pair_sum(d_keep, late(d_send, fb_first, d_far[1]))
+    d_far[0] = far(d_own[0])
+    fb = fb_more = jnp.concatenate([fb, late(fb_first, d_own[0])], axis=0)
     for bit in bits[1:-1]:
         fb_more = doubled(fb_more, bit, dp)
     fb_more = fb_more[2:]
     fb_side = swap(fb, bits[-1], "dp", dp)
-    td_0, d_keep, d_send = back(0, hidden[0], (fa,), (d_own[1],))
-    y_keep[1], y_send = down(1, td, (td_0,))
-    total = far_sum(d_own[1], late(d_far[1], y_send))
-    d_own[0] = pair_sum(d_keep, late(d_send, fb_more, fb_side), total)
-    d_far[0] = far(d_own[0])
-    fb_more_side = swap(fb_more, bits[-1], "dp", dp)
+    y_keep[1], y_send = down(1, td, (d_own[0],))
     y_got[1] = near(late(y_send, d_own[0]))
     dxq, h_keep, h_send, inv, *sums = attend_back(1, total, (), (d_own[0], y_send))
     total = far_sum(d_own[0], late(d_far[0], inv))
-    h_got = near(late(h_send, fb_more_side))
+    h_got = near(late(h_send, fb_more, fb_side))
+    fb_more_side = swap(fb_more, bits[-1], "dp", dp)
     h_high = high_sum((h_keep, h_got))
     h_far = far(h_high)
     final = [None, (dxq, h_keep, h_got, h_far, inv)]
     fa = total[rows:][None]
     fa_first = swap(fa, bits[0], "dp", dp)
     dxq, h_keep, h_send, inv, att_b, aa_keep, aa_send = attend_back(0, total, sums, (h_high,))
-    ready = (fa_first, h_far)
+    ready = (fa_first, h_far, fb_more_side)
     aa_got = near(late(aa_send, *ready))
     aa_high = high_sum((aa_keep, aa_got))
     aa_far = far(aa_high)
@@ -874,7 +874,7 @@
     att = jnp.concatenate([att_b, att_a], axis=0)[None]
     y_keep[0], y_send = down(0, td_0, (att,))
     y_got[0] = near(y_send)
-    att = doubled(att, bits[0], dp)
+    att = first = doubled(att, bits[0], dp)
     att = late(att, h_far, y_send)
     for bit in bits[1:-1]:
         att = doubled(att, bit, dp)
@@ -882,12 +882,13 @@
     for bit in bits[1:-1]:
         fa = doubled(fa, bit, dp)
     fa_side = swap(fa, bits[-1], "dp", dp)
-    y_far = far(high_sum(*((k, late(g, h_far)) for k, g in zip(y_keep, y_got))))
 
     dinput, = call(finish_kernel, None, (), (gains, dealt, aa_high, aa_far, *(v for f in final for v in f)),
-                   [((length, QUARTER), BF16)], [], "finish", 8, (att, fa_side))
+                   [((length, QUARTER), BF16)], [], "finish", 8, (y_send, first, fa))
+    y_far = far(high_sum(*((k, late(g, att)) for k, g in zip(y_keep, y_got))))
+    att_side = swap(att, bits[-1], "dp", dp)
     input_grad = collect(to_bands(dinput), "collect_grad")
-    result, = call(output_kernel, info, (), (late(y_far, dinput), *(v for p in zip(y_keep, y_got) for v in p)),
+    result, = call(output_kernel, info, (), (late(y_far, att_side), *(v for p in zip(y_keep, y_got) for v in p)),
                    [((length, QUARTER), BF16)], [], "output", 8)
     output = collect(to_bands(result), "collect_out", input_grad)
 
@@ -897,7 +898,6 @@
         feedforward_sum_kernel, (info, owners),
         ((fb, fb_more, fb_side, fb_more_side), (fa, fa_side), (near(fa), near(fa_side))), outs, "feedforward_sum")
 
-    att_side = swap(att, bits[-1], "dp", dp)
     a_parts = [att[:, n_b:], att_side[:, n_b:]]
     a_far = [far(v) for v in a_parts]
     a_far[1] = late(a_far[1], g_down_a)

time: 223 us -> 237 us (1.063)
  waiting for transfers between devices: 55.2 us -> 68 us
  local copies, waits for them, and re-layouts: 8.27 us -> 11.3 us
    ppermute x50, waiting for transfers between devices: 55.2 us -> 68 us  [swap(): return lax.ppermute(value, axis, [(i, i ^ bit) for i in range(size)])]
    pallas_call x26, Pallas kernels: 90.5 us -> 87.9 us  [call(): pl.pallas_call(body, in_specs=[pl.BlockSpec(memory_space=pltpu.SMEM)] * n...]
    unnamed x150 -> x180, local copies, waits for them, and re-layouts: 7.2 us -> 9.33 us
  transfers between devices with their start and end apart: 53 -> 53, of which waited for: 23 -> 23; matrix products, arithmetic and copies ran while one was open for 2% -> 2% of each run, Pallas kernels for 40% -> 34%
where the time goes in v9:
time: 237 us; the launch traced here: 236 us
  Pallas kernels  104 us (44%)
  waiting for transfers between devices  68 us (29%)
  starting transfers between devices  48.4 us (20%)
  local copies, waits for them, and re-layouts  11.3 us (5%)
    pallas_call x26, Pallas kernels, call(): pl.pallas_call(body, in_specs=[pl.BlockSpec(memory_space=pltpu.SMEM)] * n...  87.9 us
    ppermute x50, waiting for transfers between devices, swap(): return lax.ppermute(value, axis, [(i, i ^ bit) for i in range(size)])  68 us
    ppermute x50, starting transfers between devices, swap(): return lax.ppermute(value, axis, [(i, i ^ bit) for i in range(size)])  32 us
    unnamed x180, local copies, waits for them, and re-layouts  9.33 us
    all_to_all x2, starting transfers between devices, to_bands(): lax.all_to_all(value.reshape(dp, length // dp, QUARTER), 'dp', split_axis...  9.09 us
    pallas_call x2, Pallas kernels, sum_call(): pl.pallas_call(functools.partial(kernel, [len(group) for group in groups]...  8.33 us
    all_to_all x1, starting transfers between devices, shards(): lax.all_to_all(ordered, 'dp', split_axis=0, concat_axis=1, tiled=True)[0]  7.26 us
    pallas_call x3, Pallas kernels, move_rows(): pl.pallas_call(kernel, in_specs=[pl.BlockSpec(memory_space=pltpu.SMEM), p...  5.76 us
  transfers between devices with their start and end apart: 53, of which 23 were waited for; matrix products, arithmetic and copies ran while one was open for 2% of the time, Pallas kernels for 34%

profile of v9, /device:TPU:0, one launch (start us, length us, event | category | flops | bytes accessed | tf_op | source)
XLA Modules:
  0.0 236.0 jit_solution(13629237430948785776)
XLA Ops:
  1.4 2.5 %deal.1 = bf16[8,64,512]{2,1,0:T(8,128)(2,1)} custom-call(s32[8]{0:T(128)S(1)} %copy-done.79, bf16[8,64,512]{2,1,0:T(8,128)(2,1)} %source.1), custom_call_target="tpu_custom_call" | custom-call | flops 1000 | bytes 1000 | tf_op jit(solution)/shard_map/deal/pallas_call | solution.py:599
  3.9 7.3 %all-to-all-start = ((bf16[8,64,512]{2,1,0:T(8,128)(2,1)}), bf16[8,64,512]{2,1,0:T(8,128)(2,1)S(1)}, u32[]{:S(2)}, u32[]{:S(2)}) async-start(bf16[8,64,512]{2,1,0:T(8,128)(2,1)} %deal.1), calls=%async_computation | async-start | bytes 1048576 | tf_op jit(solution)/shard_map/all_to_all | solution.py:750
  11.3 1.6 collective-permute-start.1
  14.2 0.7 collective-permute-done.1
  14.9 1.4 pad_add_fusion.info.refs_0_
  16.3 1.8 adapters.1
  19.4 7.4 %collective-permute-done.3.refs_11_.refs_10_ = bf16[512,512]{1,0:T(8,128)(2,1)S(1)} collective-permute-done((bf16[512,512]{1,0:T(8,128)(2,1)S(1)}, bf16[512,512]{1,0:T(8,128)(2,1)S(1)}, u32[]{:S(2)}, u32[]{:S(2)}) %collective-permute-start.3) | collective-permute-done | bytes 524320 | tf_op jit(solution)/shard_map/ppermute | solution.py:671
  27.5 7.0 %collective-permute-done.5.refs_5_.refs_6_ = bf16[256,512]{1,0:T(8,128)(2,1)S(1)} collective-permute-done((bf16[256,512]{1,0:T(8,128)(2,1)S(1)}, bf16[256,512]{1,0:T(8,128)(2,1)S(1)}, u32[]{:S(2)}, u32[]{:S(2)}) %collective-permute-start.5) | collective-permute-done | bytes 262176 | tf_op jit(solution)/shard_map/ppermute | solution.py:671
  35.1 1.0 collective-permute-done.6.refs_6_.refs_7_
  36.1 4.1 %project_0.1 = (bf16[48,256]{1,0:T(8,128)(2,1)S(1)}, bf16[512,256]{1,0:T(8,128)(2,1)S(1)}, bf16[2,256,64]{2,1,0:T(8,128)(2,1)S(1)}, bf16[2,256,64]{2,1,0:T(8,128...) custom-call(s32[4]{0:T(128)S(1)} %pad_add_fusion.info.refs_0_, bf16[2048,512]{1,0:T(8,128)(2,1)} %refs_1_.15, ...), custom_call_target="tpu_custom_call" | custom-call | flops 1000 | bytes 1000 | tf_op jit(solution)/shard_map/project_0/pallas_call | solution.py:632
  40.8 3.1 %attend_0.1 = (f32[256,1024]{1,0:T(8,128)S(1)}, bf16[256,1024]{1,0:T(8,128)(2,1)S(1)}, bf16[512,256]{1,0:T(8,128)(2,1)S(1)}, f32[8,256]{1,0:T(8,128)S(1)}, bf16[16,256]{1,0:T(8,128)(2,1)S(1)}) custom-call(s32[4]{0:T(128)S(1)} %pad_add_fusion.info.refs_0_, bf16[512,2048]{1,0:T(8,128)(2,1)} %refs_3_.5, ...), custom_call_target="tpu_custom_call" | custom-call | flops 1000 | bytes 1000 | tf_op jit(solution)/shard_map/attend_0/pallas_call | solution.py:632
  44.1 1.8 collective-permute-done.10.refs_1_
  46.6 1.5 collective-permute-done.13.refs_6_.refs_7_
  48.2 4.1 %project_1.1 = (bf16[48,256]{1,0:T(8,128)(2,1)S(1)}, bf16[512,256]{1,0:T(8,128)(2,1)S(1)}, bf16[2,256,64]{2,1,0:T(8,128)(2,1)S(1)}, bf16[2,256,64]{2,1,0:T(8,128...) custom-call(s32[4]{0:T(128)S(1)} %pad_add_fusion.info.refs_0_, bf16[2048,512]{1,0:T(8,128)(2,1)} %refs_1_.15, ...), custom_call_target="tpu_custom_call" | custom-call | flops 1000 | bytes 1000 | tf_op jit(solution)/shard_map/project_1/pallas_call | solution.py:632
  52.4 3.7 %attend_1.1 = (f32[256,1024]{1,0:T(8,128)S(1)}, bf16[256,1024]{1,0:T(8,128)(2,1)S(1)}, bf16[512,256]{1,0:T(8,128)(2,1)S(1)}, f32[8,256]{1,0:T(8,128)S(1)}, bf16[16,256]{1,0:T(8,128)(2,1)S(1)}) custom-call(s32[4]{0:T(128)S(1)} %pad_add_fusion.info.refs_0_, bf16[512,2048]{1,0:T(8,128)(2,1)} %refs_3_.5, ...), custom_call_target="tpu_custom_call" | custom-call | flops 1000 | bytes 1000 | tf_op jit(solution)/shard_map/attend_1/pallas_call | solution.py:632
  56.2 3.9 %collective-permute-done.11.refs_1_ = bf16[256,1024]{1,0:T(8,128)(2,1)S(1)} collective-permute-done((bf16[256,1024]{1,0:T(8,128)(2,1)S(1)}, bf16[256,1024]{1,0:T(8,128)(2,1)S(1)}, u32[]{:S(2)}, u32[]{:S(2)}) %collective-permute-start.11) | collective-permute-done | bytes 524320 | tf_op jit(solution)/shard_map/ppermute | solution.py:671
  62.7 0.7 collective-permute-done.8.refs_12_.refs_11_
  63.5 0.7 collective-permute-done.12.refs_8_
  64.2 13.0 %front_0.1 = (bf16[256,2048]{1,0:T(8,128)(2,1)S(1)}, f32[256,512]{1,0:T(8,128)S(1)}, bf16[256,2048]{1,0:T(8,128)(2,1)S(1)}, bf16[256,2048]{1,0:T(8,128)(2,1)S(1)...) custom-call(s32[4]{0:T(128)S(1)} %pad_add_fusion.info.refs_0_, ...), custom_call_target="tpu_custom_call" | custom-call | flops 1000 | bytes 1000 | tf_op jit(solution)/shard_map/front_0/pallas_call | solution.py:632
  77.3 1.0 copy-done.27
  78.5 1.8 collective-permute-done.16.refs_8_
  80.3 12.0 %front_1.1 = (bf16[256,2048]{1,0:T(8,128)(2,1)S(1)}, f32[256,512]{1,0:T(8,128)S(1)}, bf16[256,2048]{1,0:T(8,128)(2,1)S(1)}, bf16[256,2048]{1,0:T(8,128)(2,1)S(1)...) custom-call(s32[4]{0:T(128)S(1)} %pad_add_fusion.info.refs_0_, ...), custom_call_target="tpu_custom_call" | custom-call | flops 1000 | bytes 1000 | tf_op jit(solution)/shard_map/front_1/pallas_call | solution.py:632
  92.3 7.9 %back_1.1 = (f32[256,16]{1,0:T(8,128)S(1)}, f32[256,1024]{1,0:T(8,128)S(1)}, bf16[256,1024]{1,0:T(8,128)(2,1)S(1)}, f32[48,2048]{1,0:T(8,128)S(1)}) custom-call(s32[4]{0:T(128)S(1)} %pad_add_fusion.info.refs_0_, bf16[2,2048,2048]{2,1,0:T(8,128)(2,1)S(1)} %get-tuple-element.148.refs_1_, bf16[256,2048]{1,0:T(8,128)(2,1)S(1)} %get-tuple-element.158.refs_2_, ...), custom_call_target="tpu_custom_call" | custom-call | flops 1000 | bytes 1000 | tf_op jit(solution)/shard_map/back_1/pallas_call | solution.py:632
  100.4 1.8 collective-permute-done.17.refs_1_
  102.9 2.9 %collective-permute-start.18 = (bf16[1,192,512]{2,1,0:T(8,128)(2,1)S(1)}, bf16[1,192,512]{2,1,0:T(8,128)(2,1)S(1)}, u32[]{:S(2)}, u32[]{:S(2)}) collective-permute-start(bf16[1,192,512]{2,1,0:T(8,128)(2,1)S(1)} %bitcast.37), channel_id=1, source_target_pairs={{0,16},{4,20},{8,24},{12,28},{16,0},{20,4},{24,8},{28,12},{1,17},{... | collective-permute-start | bytes 589832 | tf_op jit(solution)/shard_map/ppermute | solution.py:671
  105.9 7.9 %back_0.1 = (f32[256,16]{1,0:T(8,128)S(1)}, f32[304,1024]{1,0:T(8,128)S(1)}, bf16[304,1024]{1,0:T(8,128)(2,1)S(1)}) custom-call(s32[4]{0:T(128)S(1)} %pad_add_fusion.info.refs_0_, bf16[2,2048,2048]{2,1,0:T(8,128)(2,1)S(1)} %get-tuple-element.148.refs_1_, bf16[256,2048]{1,0:T(8,128)(2,1)S(1)} %get-tuple-element.149.refs_2_, ...), custom_call_target="tpu_custom_call" | custom-call | flops 1000 | bytes 1000 | tf_op jit(solution)/shard_map/back_0/pallas_call | solution.py:632
  113.8 1.2 collective-permute-done.18
  115.0 1.3 collective-permute-done.19.refs_1_
  117.0 1.4 collective-permute-done.20.refs_1_
  119.2 2.1 collective-permute-start.25
  121.3 1.5 collective-permute-start.24
  122.9 4.5 %down_1.1 = (f32[256,1024]{1,0:T(8,128)S(1)}, bf16[256,1024]{1,0:T(8,128)(2,1)}) custom-call(s32[4]{0:T(128)S(1)} %pad_add_fusion.info.refs_0_, bf16[2048,2048]{1,0:T(8,128)(2,1)S(1)} %bitcast.19, bf16[256,2048]{1,0:T(8,128)(2,1)S(1)} %get-tuple-element.160.refs_4_.refs_2_, f32[256,16]{1,0:T(8,128)S(1)} %get-tuple-element.181.refs_3_, ...), custom_call_target="tpu_custom_call" | custom-call | flops 1000 | bytes 1000 | tf_op jit(solution)/shard_map/down_1/pallas_call | solution.py:632
  127.4 1.0 copy-done.4
  128.6 10.7 %attend_back_1.1 = (f32[256,512]{1,0:T(8,128)S(1)}, f32[256,1024]{1,0:T(8,128)S(1)}, bf16[256,1024]{1,0:T(8,128)(2,1)S(1)}, f32[256,1]{1,0:T(8,128)S(1)}, f32[48...) custom-call(s32[4]{0:T(128)S(1)} %pad_add_fusion.info.refs_0_, ...), custom_call_target="tpu_custom_call" | custom-call | flops 1000 | bytes 1000 | tf_op jit(solution)/shard_map/attend_back_1/pallas_call | solution.py:632
  141.5 1.5 collective-permute-start.28
  143.0 2.4 %collective-permute-start.27 = (bf16[1,48,1024]{2,1,0:T(8,128)(2,1)S(1)}, bf16[1,48,1024]{2,1,0:T(8,128)(2,1)S(1)}, u32[]{:S(2)}, u32[]{:S(2)}) collective-permute-start(bf16[1,48,1024]{2,1,0:T(8,128)(2,1)S(1)} %slice_bitcast_fusion), channel_id=1, source_target_pairs={{0,16},{4,20},{8,24},{12,28},{16,0},{20,4},{24,8},{28,12},{1,17},{... | collective-permute-start | bytes 294920 | tf_op jit(solution)/shard_map/ppermute | solution.py:671
  145.5 9.8 %attend_back_0.1 = (f32[256,512]{1,0:T(8,128)S(1)}, f32[256,1024]{1,0:T(8,128)S(1)}, bf16[256,1024]{1,0:T(8,128)(2,1)S(1)}, f32[256,1]{1,0:T(8,128)S(1)}, bf16[4...) custom-call(s32[4]{0:T(128)S(1)} %pad_add_fusion.info.refs_0_, ...), custom_call_target="tpu_custom_call" | custom-call | flops 1000 | bytes 1000 | tf_op jit(solution)/shard_map/attend_back_0/pallas_call | solution.py:632
  156.0 1.9 collective-permute-done.30.refs_1_
  159.2 1.5 collective-permute-start.33
  160.7 2.9 %collective-permute-done.31.refs_3_ = bf16[96,512]{1,0:T(8,128)(2,1)S(1)} collective-permute-done((bf16[96,512]{1,0:T(8,128)(2,1)S(1)}, bf16[96,512]{1,0:T(8,128)(2,1)S(1)}, u32[]{:S(2)}, u32[]{:S(2)}) %collective-permute-start.31) | collective-permute-done | bytes 98336 | tf_op jit(solution)/shard_map/ppermute | solution.py:671
  164.3 4.5 %down_0.1 = (f32[256,1024]{1,0:T(8,128)S(1)}, bf16[256,1024]{1,0:T(8,128)(2,1)}) custom-call(s32[4]{0:T(128)S(1)} %pad_add_fusion.info.refs_0_, bf16[2048,2048]{1,0:T(8,128)(2,1)S(1)} %bitcast.19, bf16[256,2048]{1,0:T(8,128)(2,1)S(1)} %copy-done.3, f32[256,16]{1,0:T(8,128)S(1)} %get-tuple-element.173.refs_3_, ...), custom_call_target="tpu_custom_call" | custom-call | flops 1000 | bytes 1000 | tf_op jit(solution)/shard_map/down_0/pallas_call | solution.py:632
  168.8 1.8 collective-permute-done.34
  171.4 0.8 copy-done.15
  172.2 4.3 %all-to-all-start.1 = ((bf16[8,64,512]{2,1,0:T(8,128)(2,1)}), bf16[8,64,512]{2,1,0:T(8,128)(2,1)}, u32[]{:S(2)}, u32[]{:S(2)}) async-start(bf16[8,64,512]{2,1,0:T(8,128)(2,1)} %bitcast.36), calls=%async_computation.1 | async-start | bytes 1048576 | tf_op jit(solution)/shard_map/all_to_all | solution.py:826
  176.4 1.9 collective-permute-start.37
  178.3 1.0 constant_dynamic-update-slice_fusion.3
  179.3 12.2 %collective-permute-done.37 = bf16[2,112,512]{2,1,0:T(8,128)(2,1)S(1)} collective-permute-done((bf16[2,112,512]{2,1,0:T(8,128)(2,1)}, bf16[2,112,512]{2,1,0:T(8,128)(2,1)S(1)}, u32[]{:S(2)}, u32[]{:S(2)}) %collective-permute-start.37) | collective-permute-done | bytes 229408 | tf_op jit(solution)/shard_map/ppermute | solution.py:671
  191.7 1.3 collective-permute-start.39
  192.9 1.5 collective-permute-start.40
  194.9 11.4 %collective-permute-done.40.refs_1_ = bf16[4,112,512]{2,1,0:T(8,128)(2,1)S(1)} collective-permute-done((bf16[4,112,512]{2,1,0:T(8,128)(2,1)S(1)}, bf16[4,112,512]{2,1,0:T(8,128)(2,1)S(1)}, u32[]{:S(2)}, u32[]{:S(2)}) %collective-permute-start.40) | collective-permute-done | bytes 458784 | tf_op jit(solution)/shard_map/ppermute | solution.py:671
  206.4 0.8 copy-done.21
  207.1 0.8 output.1
  207.9 0.8 copy-done.14
  208.7 4.8 %all-to-all-start.2 = ((bf16[8,64,512]{2,1,0:T(8,128)(2,1)}), bf16[8,64,512]{2,1,0:T(8,128)(2,1)S(1)}, u32[]{:S(2)}, u32[]{:S(2)}) async-start(bf16[8,64,512]{2,1,0:T(8,128)(2,1)} %bitcast.35), calls=%async_computation.2 | async-start | bytes 1048576 | tf_op jit(solution)/shard_map/all_to_all | solution.py:826
  214.0 1.0 slice.34.refs_2_
  215.0 0.8 collective-permute-start.43
  215.8 1.0 slice.35.refs_3_
  216.8 1.3 collective-permute-start.44
  218.2 1.0 copy-done.44
  219.2 4.9 %feedforward_sum.1 = (f32[8,32,2048]{2,1,0:T(8,128)}, f32[8,16,2048]{2,1,0:T(8,128)}, f32[8,2,16,2048]{3,2,1,0:T(8,128)}, f32[8,16,2048]{2,1,0:T(8,128)}) custom-call(s32[4]{0:T(128)S(1)} %pad_add_fusion.info.refs_0_, s32[8]{0:T(128)S(1)} %copy-done.82, bf16[2,192,512]{2,1,0:T(8,128)(2,1)S(1)} %copy-done.20, bf16[2,192,512]{2,1,0:T(8,128)(2,1)S(1)} %copy-done.42, ...), custom_call_target="tpu_custom_call" | custom-call | bytes 12000000 | tf_op jit(solution)/shard_map/feedforward_sum/pallas_call | solution.py:655
  224.8 4.2 %collective-permute-done.44.refs_7_ = bf16[4,64,512]{2,1,0:T(8,128)(2,1)S(1)} collective-permute-done((bf16[4,64,512]{2,1,0:T(8,128)(2,1)S(1)}, bf16[4,64,512]{2,1,0:T(8,128)(2,1)S(1)}, u32[]{:S(2)}, u32[]{:S(2)}) %collective-permute-start.44) | collective-permute-done | bytes 262176 | tf_op jit(solution)/shard_map/ppermute | solution.py:671
  229.0 1.9 collect_grad.1
  231.0 3.4 %attention_sum.1 = (f32[8,48,2048]{2,1,0:T(8,128)}, f32[8,16,2048]{2,1,0:T(8,128)}, f32[8,16,512]{2,1,0:T(8,128)}, f32[8,2,16,128]{3,2,1,0:T(8,128)}, f32[8,16,512]{2,1,0:T(8,128)}) custom-call(s32[4]{0:T(128)S(1)} %pad_add_fusion.info.refs_0_, s32[8]{0:T(128)S(1)} %copy-done.82, bf16[4,112,512]{2,1,0:T(8,128)(2,1)S(1)} %copy-done.18, ...), custom_call_target="tpu_custom_call" | custom-call | bytes 12000000 | tf_op jit(solution)/shard_map/attention_sum/pallas_call | solution.py:655
  234.4 1.4 collect_out.1
  (274 shorter events, 19.0 us)
Async XLA Ops:
  3.9 23.0 %all-to-all-start = ((bf16[8,64,512]{2,1,0:T(8,128)(2,1)}), bf16[8,64,512]{2,1,0:T(8,128)(2,1)S(1)}, u32[]{:S(2)}, u32[]{:S(2)}) async-start(bf16[8,64,512]{2,1,0:T(8,128)(2,1)} %deal.1), calls=%async_computation | async-start | bytes 1048576 | tf_op jit(solution)/shard_map/all_to_all | solution.py:750
  11.2 8.2 %collective-permute-start = (bf16[2,512]{1,0:T(2,128)(2,1)S(1)}, bf16[2,512]{1,0:T(2,128)(2,1)S(1)}, u32[]{:S(2)}, u32[]{:S(2)}) collective-permute-start(bf16[2,512]{1,0:T(2,128)(2,1)S(1)} %pad_maximum_fusion.4), channel_id=1, source_target_pairs={{0,1},{1,0},{2,3},{3,2},{4,5},{5,4},{6,7},{7,6},{8,9},{9,8},{10,11... | collective-permute-start | bytes 6152 | tf_op jit(solution)/shard_map/ppermute | solution.py:671
  11.3 3.7 %collective-permute-start.1 = (bf16[2,512]{1,0:T(2,128)(2,1)S(1)}, bf16[2,512]{1,0:T(2,128)(2,1)S(1)}, u32[]{:S(2)}, u32[]{:S(2)}) collective-permute-start(bf16[2,512]{1,0:T(2,128)(2,1)S(1)} %pad_maximum_fusion.4), channel_id=1, source_target_pairs={{0,2},{1,3},{2,0},{3,1},{4,6},{5,7},{6,4},{7,5},{8,10},{9,11},{10,... | collective-permute-start | bytes 6152 | tf_op jit(solution)/shard_map/ppermute | solution.py:671
  12.9 14.0 %collective-permute-start.3 = (bf16[512,512]{1,0:T(8,128)(2,1)S(1)}, bf16[512,512]{1,0:T(8,128)(2,1)S(1)}, u32[]{:S(2)}, u32[]{:S(2)}) collective-permute-start(bf16[512,512]{1,0:T(8,128)(2,1)S(1)} %bitcast.29), channel_id=1, source_target_pairs={{0,2},{1,3},{2,0},{3,1},{4,6},{5,7},{6,4},{7,5},{8,10},{9,11},{10,... | collective-permute-start | bytes 1572872 | tf_op jit(solution)/shard_map/ppermute | solution.py:671
  14.9 4.5 %collective-permute-start.2 = (bf16[2,512]{1,0:T(2,128)(2,1)S(1)}, bf16[2,512]{1,0:T(2,128)(2,1)S(1)}, u32[]{:S(2)}, u32[]{:S(2)}) collective-permute-start(bf16[2,512]{1,0:T(2,128)(2,1)S(1)} %collective-permute-done.1), channel_id=1, source_target_pairs={{0,1},{1,0},{2,3},{3,2},{4,5},{5,4},{6,7},{7,6},{8,9},{9,8},{10,11... | collective-permute-start | bytes 6152 | tf_op jit(solution)/shard_map/ppermute | solution.py:671
  16.3 19.8 %copy-start.63 = (f32[32,256]{1,0:T(8,128)S(1)}, f32[32,256]{1,0:T(8,128)}, u32[]{:S(2)}) copy-start(f32[32,256]{1,0:T(8,128)} %constant.19.clone.refs_11_.refs_21_) | copy-start | bytes 98308
  19.4 28.8 %copy-start.53 = (bf16[16,512]{1,0:T(8,128)(2,1)}, bf16[16,512]{1,0:T(8,128)(2,1)S(1)}, u32[]{:S(2)}) copy-start(bf16[16,512]{1,0:T(8,128)(2,1)S(1)} %get-tuple-element.122.refs_9_.refs_17_) | copy-start | bytes 49156
  19.4 28.8 %copy-start.65 = (bf16[2,16,128]{2,1,0:T(8,128)(2,1)}, bf16[2,16,128]{2,1,0:T(8,128)(2,1)S(1)}, u32[]{:S(2)}) copy-start(bf16[2,16,128]{2,1,0:T(8,128)(2,1)S(1)} %get-tuple-element.123.refs_10_.refs_18_) | copy-start | bytes 24580
  19.4 33.0 %copy-start.25 = (bf16[16,2048]{1,0:T(8,128)(2,1)}, bf16[16,2048]{1,0:T(8,128)(2,1)S(1)}, u32[]{:S(2)}) copy-start(bf16[16,2048]{1,0:T(8,128)(2,1)S(1)} %get-tuple-element.126.refs_4_.refs_20_) | copy-start | bytes 196612
  19.4 33.0 %copy-start.47 = (bf16[16,512]{1,0:T(8,128)(2,1)}, bf16[16,512]{1,0:T(8,128)(2,1)S(1)}, u32[]{:S(2)}) copy-start(bf16[16,512]{1,0:T(8,128)(2,1)S(1)} %get-tuple-element.125.refs_3_.refs_19_) | copy-start | bytes 49156
  26.9 7.6 %collective-permute-start.5 = (bf16[256,512]{1,0:T(8,128)(2,1)S(1)}, bf16[256,512]{1,0:T(8,128)(2,1)S(1)}, u32[]{:S(2)}, u32[]{:S(2)}) collective-permute-start(bf16[256,512]{1,0:T(8,128)(2,1)S(1)} %get-tuple-element.232), channel_id=1, source_target_pairs={{0,2},{1,3},{2,0},{3,1},{4,6},{5,7},{6,4},{7,5},{8,10},{9,11},{10,... | collective-permute-start | bytes 786440 | tf_op jit(solution)/shard_map/ppermute | solution.py:671
  27.5 8.6 %collective-permute-start.4 = (bf16[512,512]{1,0:T(8,128)(2,1)S(1)}, bf16[512,512]{1,0:T(8,128)(2,1)S(1)}, u32[]{:S(2)}, u32[]{:S(2)}) collective-permute-start(bf16[512,512]{1,0:T(8,128)(2,1)S(1)} %bitcast.21), channel_id=1, source_target_pairs={{0,1},{1,0},{2,3},{3,2},{4,5},{5,4},{6,7},{7,6},{8,9},{9,8},{10,11... | collective-permute-start | bytes 1572872 | tf_op jit(solution)/shard_map/ppermute | solution.py:671
  34.5 29.7 %copy-start.8 = (bf16[256,512]{1,0:T(8,128)(2,1)}, bf16[256,512]{1,0:T(8,128)(2,1)S(1)}, u32[]{:S(2)}) copy-start(bf16[256,512]{1,0:T(8,128)(2,1)S(1)} %collective-permute-done.5.refs_5_.refs_6_) | copy-start | bytes 786436
  34.5 1.5 collective-permute-start.6
  34.5 9.4 %collective-permute-start.9 = (bf16[256,512]{1,0:T(8,128)(2,1)S(1)}, bf16[256,512]{1,0:T(8,128)(2,1)S(1)}, u32[]{:S(2)}, u32[]{:S(2)}) collective-permute-start(bf16[256,512]{1,0:T(8,128)(2,1)S(1)} %get-tuple-element.231), channel_id=1, source_target_pairs={{0,2},{1,3},{2,0},{3,1},{4,6},{5,7},{6,4},{7,5},{8,10},{9,11},{10,... | collective-permute-start | bytes 786440 | tf_op jit(solution)/shard_map/ppermute | solution.py:671
  36.0 28.2 %copy-start.10 = (bf16[256,512]{1,0:T(8,128)(2,1)}, bf16[256,512]{1,0:T(8,128)(2,1)S(1)}, u32[]{:S(2)}) copy-start(bf16[256,512]{1,0:T(8,128)(2,1)S(1)} %collective-permute-done.6.refs_6_.refs_7_) | copy-start | bytes 786436
  43.9 2.0 collective-permute-start.10
  46.0 14.0 %collective-permute-start.11 = (bf16[256,1024]{1,0:T(8,128)(2,1)S(1)}, bf16[256,1024]{1,0:T(8,128)(2,1)S(1)}, u32[]{:S(2)}, u32[]{:S(2)}) collective-permute-start(bf16[256,1024]{1,0:T(8,128)(2,1)S(1)} %pair_sum.4.refs_0_.refs_14_), channel_id=1, source_target_pairs={{0,2},{1,3},{2,0},{3,1},{4,6},{5,7},{6,4},{7,5},{8,10},{9,11},{10,... | collective-permute-start | bytes 1572872 | tf_op jit(solution)/shard_map/ppermute | solution.py:671
  46.6 1.5 collective-permute-start.13
  48.2 32.2 %copy-start.6 = (bf16[256,512]{1,0:T(8,128)(2,1)}, bf16[256,512]{1,0:T(8,128)(2,1)S(1)}, u32[]{:S(2)}) copy-start(bf16[256,512]{1,0:T(8,128)(2,1)S(1)} %collective-permute-done.13.refs_6_.refs_7_) | copy-start | bytes 786436
  56.1 21.1 %copy-start.73 = (f32[8,256]{1,0:T(8,128)}, f32[8,256]{1,0:T(8,128)S(1)}, u32[]{:S(2)}) copy-start(f32[8,256]{1,0:T(8,128)S(1)} %get-tuple-element.143.refs_18_.refs_26_) | copy-start | bytes 24580
  56.1 21.1 %copy-start.77 = (bf16[16,256]{1,0:T(8,128)(2,1)}, bf16[16,256]{1,0:T(8,128)(2,1)S(1)}, u32[]{:S(2)}) copy-start(bf16[16,256]{1,0:T(8,128)(2,1)S(1)} %get-tuple-element.176.refs_27_) | copy-start | bytes 24580
  60.0 1.9 collective-permute-start.14
  60.0 2.7 %collective-permute-start.7 = (bf16[512,512]{1,0:T(8,128)(2,1)S(1)}, bf16[512,512]{1,0:T(8,128)(2,1)S(1)}, u32[]{:S(2)}, u32[]{:S(2)}) collective-permute-start(bf16[512,512]{1,0:T(8,128)(2,1)S(1)} %bitcast.30), channel_id=1, source_target_pairs={{0,1},{1,0},{2,3},{3,2},{4,5},{5,4},{6,7},{7,6},{8,9},{9,8},{10,11... | collective-permute-start | bytes 1572872 | tf_op jit(solution)/shard_map/ppermute | solution.py:671
  60.6 2.9 %collective-permute-start.8 = (bf16[512,512]{1,0:T(8,128)(2,1)S(1)}, bf16[512,512]{1,0:T(8,128)(2,1)S(1)}, u32[]{:S(2)}, u32[]{:S(2)}) collective-permute-start(bf16[512,512]{1,0:T(8,128)(2,1)S(1)} %collective-permute-done.3.refs_11_.refs_10_), channel_id=1, source_target_pairs={{0,1},{1,0},{2,3},{3,2},{4,5},{5,4},{6,7},{7,6},{8,9},{9,8},{10,11... | collective-permute-start | bytes 1572872 | tf_op jit(solution)/shard_map/ppermute | solution.py:671
  60.8 3.4 %collective-permute-start.12 = (bf16[256,1024]{1,0:T(8,128)(2,1)S(1)}, bf16[256,1024]{1,0:T(8,128)(2,1)S(1)}, u32[]{:S(2)}, u32[]{:S(2)}) collective-permute-start(bf16[256,1024]{1,0:T(8,128)(2,1)S(1)} %far_sum.4.refs_7_), channel_id=1, source_target_pairs={{0,1},{1,0},{2,3},{3,2},{4,5},{5,4},{6,7},{7,6},{8,9},{9,8},{10,11... | collective-permute-start | bytes 1572872 | tf_op jit(solution)/shard_map/ppermute | solution.py:671
  62.1 16.2 %collective-permute-start.15 = (bf16[256,1024]{1,0:T(8,128)(2,1)S(1)}, bf16[256,1024]{1,0:T(8,128)(2,1)S(1)}, u32[]{:S(2)}, u32[]{:S(2)}) collective-permute-start(bf16[256,1024]{1,0:T(8,128)(2,1)S(1)} %pair_sum.5.refs_19_.refs_0_), channel_id=1, source_target_pairs={{0,2},{1,3},{2,0},{3,1},{4,6},{5,7},{6,4},{7,5},{8,10},{9,11},{10,... | collective-permute-start | bytes 1572872 | tf_op jit(solution)/shard_map/ppermute | solution.py:671
  78.2 27.6 %copy-start.2 = (bf16[256,2048]{1,0:T(8,128)(2,1)}, bf16[256,2048]{1,0:T(8,128)(2,1)S(1)}, u32[]{:S(2)}) copy-start(bf16[256,2048]{1,0:T(8,128)(2,1)S(1)} %get-tuple-element.151.refs_4_.refs_2_) | copy-start | bytes 3145732
  78.4 2.0 collective-permute-start.16
  100.2 1.9 collective-permute-start.17
  102.3 14.0 %collective-permute-start.19 = (bf16[256,1024]{1,0:T(8,128)(2,1)S(1)}, bf16[256,1024]{1,0:T(8,128)(2,1)S(1)}, u32[]{:S(2)}, u32[]{:S(2)}) collective-permute-start(bf16[256,1024]{1,0:T(8,128)(2,1)S(1)} %pair_sum.6.refs_11_.refs_0_), channel_id=1, source_target_pairs={{0,2},{1,3},{2,0},{3,1},{4,6},{5,7},{6,4},{7,5},{8,10},{9,11},{10,... | collective-permute-start | bytes 1572872 | tf_op jit(solution)/shard_map/ppermute | solution.py:671
  102.9 12.0 %collective-permute-start.18 = (bf16[1,192,512]{2,1,0:T(8,128)(2,1)S(1)}, bf16[1,192,512]{2,1,0:T(8,128)(2,1)S(1)}, u32[]{:S(2)}, u32[]{:S(2)}) collective-permute-start(bf16[1,192,512]{2,1,0:T(8,128)(2,1)S(1)} %bitcast.37), channel_id=1, source_target_pairs={{0,16},{4,20},{8,24},{12,28},{16,0},{20,4},{24,8},{28,12},{1,17},{... | collective-permute-start | bytes 589832 | tf_op jit(solution)/shard_map/ppermute | solution.py:671
  116.3 2.1 collective-permute-start.20
  116.5 12.0 %collective-permute-start.22 = (bf16[256,1024]{1,0:T(8,128)(2,1)S(1)}, bf16[256,1024]{1,0:T(8,128)(2,1)S(1)}, u32[]{:S(2)}, u32[]{:S(2)}) collective-permute-start(bf16[256,1024]{1,0:T(8,128)(2,1)S(1)} %far_sum.6.refs_13_), channel_id=1, source_target_pairs={{0,1},{1,0},{2,3},{3,2},{4,5},{5,4},{6,7},{7,6},{8,9},{9,8},{10,11... | collective-permute-start | bytes 1572872 | tf_op jit(solution)/shard_map/ppermute | solution.py:671
  118.5 21.0 %collective-permute-start.21 = (bf16[304,1024]{1,0:T(8,128)(2,1)S(1)}, bf16[304,1024]{1,0:T(8,128)(2,1)S(1)}, u32[]{:S(2)}, u32[]{:S(2)}) collective-permute-start(bf16[304,1024]{1,0:T(8,128)(2,1)S(1)} %pair_sum.7.refs_6_.refs_34_.refs_0_), channel_id=1, source_target_pairs={{0,2},{1,3},{2,0},{3,1},{4,6},{5,7},{6,4},{7,5},{8,10},{9,11},{10,... | collective-permute-start | bytes 1867784 | tf_op jit(solution)/shard_map/ppermute | solution.py:671
  119.2 20.2 %collective-permute-start.25 = (bf16[2,192,512]{2,1,0:T(8,128)(2,1)S(1)}, bf16[2,192,512]{2,1,0:T(8,128)(2,1)S(1)}, u32[]{:S(2)}, u32[]{:S(2)}) collective-permute-start(bf16[2,192,512]{2,1,0:T(8,128)(2,1)S(1)} %pad_maximum_fusion.refs_0_), channel_id=1, source_target_pairs={{0,4},{4,0},{8,12},{12,8},{16,20},{20,16},{24,28},{28,24},{1,5},{5... | collective-permute-start | bytes 1179656 | tf_op jit(solution)/shard_map/ppermute | solution.py:671
  121.3 18.2 %collective-permute-start.24 = (bf16[2,192,512]{2,1,0:T(8,128)(2,1)S(1)}, bf16[2,192,512]{2,1,0:T(8,128)(2,1)S(1)}, u32[]{:S(2)}, u32[]{:S(2)}) collective-permute-start(bf16[2,192,512]{2,1,0:T(8,128)(2,1)S(1)} %pad_maximum_fusion.refs_0_), channel_id=1, source_target_pairs={{0,8},{4,12},{8,0},{12,4},{16,24},{20,28},{24,16},{28,20},{1,9},{5... | collective-permute-start | bytes 1179656 | tf_op jit(solution)/shard_map/ppermute | solution.py:671
  139.5 2.0 collective-permute-start.26
  139.7 5.7 %collective-permute-start.23 = (bf16[304,1024]{1,0:T(8,128)(2,1)S(1)}, bf16[304,1024]{1,0:T(8,128)(2,1)S(1)}, u32[]{:S(2)}, u32[]{:S(2)}) collective-permute-start(bf16[304,1024]{1,0:T(8,128)(2,1)S(1)} %far_sum.7.refs_13_), channel_id=1, source_target_pairs={{0,1},{1,0},{2,3},{3,2},{4,5},{5,4},{6,7},{7,6},{8,9},{9,8},{10,11... | collective-permute-start | bytes 1867784 | tf_op jit(solution)/shard_map/ppermute | solution.py:671
  140.2 15.1 %collective-permute-start.29 = (bf16[2,192,512]{2,1,0:T(8,128)(2,1)S(1)}, bf16[2,192,512]{2,1,0:T(8,128)(2,1)S(1)}, u32[]{:S(2)}, u32[]{:S(2)}) collective-permute-start(bf16[2,192,512]{2,1,0:T(8,128)(2,1)S(1)} %collective-permute-done.24.refs_1_), channel_id=1, source_target_pairs={{0,4},{4,0},{8,12},{12,8},{16,20},{20,16},{24,28},{28,24},{1,5},{5... | collective-permute-start | bytes 1179656 | tf_op jit(solution)/shard_map/ppermute | solution.py:671
  141.5 13.9 %collective-permute-start.28 = (bf16[256,512]{1,0:T(8,128)(2,1)S(1)}, bf16[256,512]{1,0:T(8,128)(2,1)S(1)}, u32[]{:S(2)}, u32[]{:S(2)}) collective-permute-start(bf16[256,512]{1,0:T(8,128)(2,1)S(1)} %high_sum.4.refs_36_), channel_id=1, source_target_pairs={{0,2},{1,3},{2,0},{3,1},{4,6},{5,7},{6,4},{7,5},{8,10},{9,11},{10,... | collective-permute-start | bytes 786440 | tf_op jit(solution)/shard_map/ppermute | solution.py:671
  143.0 12.3 %collective-permute-start.27 = (bf16[1,48,1024]{2,1,0:T(8,128)(2,1)S(1)}, bf16[1,48,1024]{2,1,0:T(8,128)(2,1)S(1)}, u32[]{:S(2)}, u32[]{:S(2)}) collective-permute-start(bf16[1,48,1024]{2,1,0:T(8,128)(2,1)S(1)} %slice_bitcast_fusion), channel_id=1, source_target_pairs={{0,16},{4,20},{8,24},{12,28},{16,0},{20,4},{24,8},{28,12},{1,17},{... | collective-permute-start | bytes 294920 | tf_op jit(solution)/shard_map/ppermute | solution.py:671
  155.3 3.8 %collective-permute-start.32 = (bf16[256,1024]{1,0:T(8,128)(2,1)S(1)}, bf16[256,1024]{1,0:T(8,128)(2,1)S(1)}, u32[]{:S(2)}, u32[]{:S(2)}) collective-permute-start(bf16[256,1024]{1,0:T(8,128)(2,1)S(1)} %get-tuple-element.203), channel_id=1, source_target_pairs={{0,1},{1,0},{2,3},{3,2},{4,5},{5,4},{6,7},{7,6},{8,9},{9,8},{10,11... | collective-permute-start | bytes 1572872 | tf_op jit(solution)/shard_map/ppermute | solution.py:671
  155.4 2.5 %collective-permute-start.30 = (bf16[96,1024]{1,0:T(8,128)(2,1)S(1)}, bf16[96,1024]{1,0:T(8,128)(2,1)S(1)}, u32[]{:S(2)}, u32[]{:S(2)}) collective-permute-start(bf16[96,1024]{1,0:T(8,128)(2,1)S(1)} %get-tuple-element.199), channel_id=1, source_target_pairs={{0,1},{1,0},{2,3},{3,2},{4,5},{5,4},{6,7},{7,6},{8,9},{9,8},{10,11... | collective-permute-start | bytes 589832 | tf_op jit(solution)/shard_map/ppermute | solution.py:671
  155.9 35.6 %collective-permute-start.38 = (bf16[256,1024]{1,0:T(8,128)(2,1)}, bf16[256,1024]{1,0:T(8,128)(2,1)S(1)}, u32[]{:S(2)}, u32[]{:S(2)}) collective-permute-start(bf16[256,1024]{1,0:T(8,128)(2,1)} %get-tuple-element.216.refs_35_), channel_id=1, source_target_pairs={{0,1},{1,0},{2,3},{3,2},{4,5},{5,4},{6,7},{7,6},{8,9},{9,8},{10,11... | collective-permute-start | bytes 1572872 | tf_op jit(solution)/shard_map/ppermute | solution.py:671
  157.9 5.7 %collective-permute-start.31 = (bf16[96,512]{1,0:T(8,128)(2,1)S(1)}, bf16[96,512]{1,0:T(8,128)(2,1)S(1)}, u32[]{:S(2)}, u32[]{:S(2)}) collective-permute-start(bf16[96,512]{1,0:T(8,128)(2,1)S(1)} %high_sum.5.refs_2_), channel_id=1, source_target_pairs={{0,2},{1,3},{2,0},{3,1},{4,6},{5,7},{6,4},{7,5},{8,10},{9,11},{10,... | collective-permute-start | bytes 294920 | tf_op jit(solution)/shard_map/ppermute | solution.py:671
  158.6 10.2 %collective-permute-start.35 = (bf16[2,48,1024]{2,1,0:T(8,128)(2,1)S(1)}, bf16[2,48,1024]{2,1,0:T(8,128)(2,1)S(1)}, u32[]{:S(2)}, u32[]{:S(2)}) collective-permute-start(bf16[2,48,1024]{2,1,0:T(8,128)(2,1)S(1)} %pad_maximum_fusion.2), channel_id=1, source_target_pairs={{0,8},{4,12},{8,0},{12,4},{16,24},{20,28},{24,16},{28,20},{1,9},{5... | collective-permute-start | bytes 589832 | tf_op jit(solution)/shard_map/ppermute | solution.py:671
  159.2 11.4 %collective-permute-start.33 = (bf16[256,512]{1,0:T(8,128)(2,1)S(1)}, bf16[256,512]{1,0:T(8,128)(2,1)S(1)}, u32[]{:S(2)}, u32[]{:S(2)}) collective-permute-start(bf16[256,512]{1,0:T(8,128)(2,1)S(1)} %high_sum.6), channel_id=1, source_target_pairs={{0,2},{1,3},{2,0},{3,1},{4,6},{5,7},{6,4},{7,5},{8,10},{9,11},{10,... | collective-permute-start | bytes 786440 | tf_op jit(solution)/shard_map/ppermute | solution.py:671
  163.7 7.0 %collective-permute-start.34 = (bf16[1,112,512]{2,1,0:T(8,128)(2,1)S(1)}, bf16[1,112,512]{2,1,0:T(8,128)(2,1)S(1)}, u32[]{:S(2)}, u32[]{:S(2)}) collective-permute-start(bf16[1,112,512]{2,1,0:T(8,128)(2,1)S(1)} %maximum_bitcast_fusion.refs_6_), channel_id=1, source_target_pairs={{0,16},{4,20},{8,24},{12,28},{16,0},{20,4},{24,8},{28,12},{1,17},{... | collective-permute-start | bytes 344072 | tf_op jit(solution)/shard_map/ppermute | solution.py:671
  168.8 22.7 %collective-permute-start.36 = (bf16[256,1024]{1,0:T(8,128)(2,1)}, bf16[256,1024]{1,0:T(8,128)(2,1)S(1)}, u32[]{:S(2)}, u32[]{:S(2)}) collective-permute-start(bf16[256,1024]{1,0:T(8,128)(2,1)} %get-tuple-element.209.refs_14_), channel_id=1, source_target_pairs={{0,1},{1,0},{2,3},{3,2},{4,5},{5,4},{6,7},{7,6},{8,9},{9,8},{10,11... | collective-permute-start | bytes 1572872 | tf_op jit(solution)/shard_map/ppermute | solution.py:671
  172.2 36.6 %all-to-all-start.1 = ((bf16[8,64,512]{2,1,0:T(8,128)(2,1)}), bf16[8,64,512]{2,1,0:T(8,128)(2,1)}, u32[]{:S(2)}, u32[]{:S(2)}) async-start(bf16[8,64,512]{2,1,0:T(8,128)(2,1)} %bitcast.36), calls=%async_computation.1 | async-start | bytes 1048576 | tf_op jit(solution)/shard_map/all_to_all | solution.py:826
  176.4 15.1 %collective-permute-start.37 = (bf16[2,112,512]{2,1,0:T(8,128)(2,1)}, bf16[2,112,512]{2,1,0:T(8,128)(2,1)S(1)}, u32[]{:S(2)}, u32[]{:S(2)}) collective-permute-start(bf16[2,112,512]{2,1,0:T(8,128)(2,1)} %copy-done.16), channel_id=1, source_target_pairs={{0,8},{4,12},{8,0},{12,4},{16,24},{20,28},{24,16},{28,20},{1,9},{5... | collective-permute-start | bytes 688136 | tf_op jit(solution)/shard_map/ppermute | solution.py:671
  191.7 15.5 %collective-permute-start.39 = (bf16[512,512]{1,0:T(8,128)(2,1)S(1)}, bf16[512,512]{1,0:T(8,128)(2,1)S(1)}, u32[]{:S(2)}, u32[]{:S(2)}) collective-permute-start(bf16[512,512]{1,0:T(8,128)(2,1)S(1)} %high_sum.7), channel_id=1, source_target_pairs={{0,2},{1,3},{2,0},{3,1},{4,6},{5,7},{6,4},{7,5},{8,10},{9,11},{10,... | collective-permute-start | bytes 1572872 | tf_op jit(solution)/shard_map/ppermute | solution.py:671
  192.9 13.5 %collective-permute-start.40 = (bf16[4,112,512]{2,1,0:T(8,128)(2,1)S(1)}, bf16[4,112,512]{2,1,0:T(8,128)(2,1)S(1)}, u32[]{:S(2)}, u32[]{:S(2)}) collective-permute-start(bf16[4,112,512]{2,1,0:T(8,128)(2,1)S(1)} %constant_dynamic-update-slice_fusion.2.refs_0_), channel_id=1, source_target_pairs={{0,4},{4,0},{8,12},{12,8},{16,20},{20,16},{24,28},{28,24},{1,5},{5... | collective-permute-start | bytes 1376264 | tf_op jit(solution)/shard_map/ppermute | solution.py:671
  194.4 19.1 %collective-permute-start.45 = (bf16[4,48,1024]{2,1,0:T(8,128)(2,1)S(1)}, bf16[4,48,1024]{2,1,0:T(8,128)(2,1)}, u32[]{:S(2)}, u32[]{:S(2)}) collective-permute-start(bf16[4,48,1024]{2,1,0:T(8,128)(2,1)S(1)} %constant_dynamic-update-slice_fusion.refs_16_.refs_4_), channel_id=1, source_target_pairs={{0,4},{4,0},{8,12},{12,8},{16,20},{20,16},{24,28},{28,24},{1,5},{5... | collective-permute-start | bytes 1179656 | tf_op jit(solution)/shard_map/ppermute | solution.py:671
  208.7 25.7 %all-to-all-start.2 = ((bf16[8,64,512]{2,1,0:T(8,128)(2,1)}), bf16[8,64,512]{2,1,0:T(8,128)(2,1)S(1)}, u32[]{:S(2)}, u32[]{:S(2)}) async-start(bf16[8,64,512]{2,1,0:T(8,128)(2,1)} %bitcast.35), calls=%async_computation.2 | async-start | bytes 1048576 | tf_op jit(solution)/shard_map/all_to_all | solution.py:826
  213.5 4.6 %collective-permute-start.46 = (bf16[4,48,1024]{2,1,0:T(8,128)(2,1)S(1)}, bf16[4,48,1024]{2,1,0:T(8,128)(2,1)S(1)}, u32[]{:S(2)}, u32[]{:S(2)}) collective-permute-start(bf16[4,48,1024]{2,1,0:T(8,128)(2,1)S(1)} %constant_dynamic-update-slice_fusion.refs_16_.refs_4_), channel_id=1, source_target_pairs={{0,1},{1,0},{2,3},{3,2},{4,5},{5,4},{6,7},{7,6},{8,9},{9,8},{10,11... | collective-permute-start | bytes 1179656 | tf_op jit(solution)/shard_map/ppermute | solution.py:671
  213.6 4.6 %collective-permute-start.47 = (bf16[4,48,1024]{2,1,0:T(8,128)(2,1)}, bf16[4,48,1024]{2,1,0:T(8,128)(2,1)S(1)}, u32[]{:S(2)}, u32[]{:S(2)}) collective-permute-start(bf16[4,48,1024]{2,1,0:T(8,128)(2,1)} %collective-permute-done.45.refs_5_), channel_id=1, source_target_pairs={{0,1},{1,0},{2,3},{3,2},{4,5},{5,4},{6,7},{7,6},{8,9},{9,8},{10,11... | collective-permute-start | bytes 1179656 | tf_op jit(solution)/shard_map/ppermute | solution.py:671
  215.0 9.2 %collective-permute-start.43 = (bf16[4,64,512]{2,1,0:T(8,128)(2,1)S(1)}, bf16[4,64,512]{2,1,0:T(8,128)(2,1)S(1)}, u32[]{:S(2)}, u32[]{:S(2)}) collective-permute-start(bf16[4,64,512]{2,1,0:T(8,128)(2,1)S(1)} %slice.34.refs_2_), channel_id=1, source_target_pairs={{0,2},{1,3},{2,0},{3,1},{4,6},{5,7},{6,4},{7,5},{8,10},{9,11},{10,... | collective-permute-start | bytes 786440 | tf_op jit(solution)/shard_map/ppermute | solution.py:671
  216.8 12.2 %collective-permute-start.44 = (bf16[4,64,512]{2,1,0:T(8,128)(2,1)S(1)}, bf16[4,64,512]{2,1,0:T(8,128)(2,1)S(1)}, u32[]{:S(2)}, u32[]{:S(2)}) collective-permute-start(bf16[4,64,512]{2,1,0:T(8,128)(2,1)S(1)} %slice.35.refs_3_), channel_id=1, source_target_pairs={{0,2},{1,3},{2,0},{3,1},{4,6},{5,7},{6,4},{7,5},{8,10},{9,11},{10,... | collective-permute-start | bytes 786440 | tf_op jit(solution)/shard_map/ppermute | solution.py:671
  218.2 12.7 %collective-permute-start.41 = (bf16[4,64,512]{2,1,0:T(8,128)(2,1)S(1)}, bf16[4,64,512]{2,1,0:T(8,128)(2,1)S(1)}, u32[]{:S(2)}, u32[]{:S(2)}) collective-permute-start(bf16[4,64,512]{2,1,0:T(8,128)(2,1)S(1)} %slice.34.refs_2_), channel_id=1, source_target_pairs={{0,1},{1,0},{2,3},{3,2},{4,5},{5,4},{6,7},{7,6},{8,9},{9,8},{10,11... | collective-permute-start | bytes 786440 | tf_op jit(solution)/shard_map/ppermute | solution.py:671
  224.2 6.7 %collective-permute-start.48 = (bf16[4,64,512]{2,1,0:T(8,128)(2,1)S(1)}, bf16[4,64,512]{2,1,0:T(8,128)(2,1)S(1)}, u32[]{:S(2)}, u32[]{:S(2)}) collective-permute-start(bf16[4,64,512]{2,1,0:T(8,128)(2,1)S(1)} %collective-permute-done.43.refs_6_), channel_id=1, source_target_pairs={{0,1},{1,0},{2,3},{3,2},{4,5},{5,4},{6,7},{7,6},{8,9},{9,8},{10,11... | collective-permute-start | bytes 786440 | tf_op jit(solution)/shard_map/ppermute | solution.py:671
  224.6 6.3 %collective-permute-start.42 = (bf16[4,64,512]{2,1,0:T(8,128)(2,1)S(1)}, bf16[4,64,512]{2,1,0:T(8,128)(2,1)S(1)}, u32[]{:S(2)}, u32[]{:S(2)}) collective-permute-start(bf16[4,64,512]{2,1,0:T(8,128)(2,1)S(1)} %slice.35.refs_3_), channel_id=1, source_target_pairs={{0,1},{1,0},{2,3},{3,2},{4,5},{5,4},{6,7},{7,6},{8,9},{9,8},{10,11... | collective-permute-start | bytes 786440 | tf_op jit(solution)/shard_map/ppermute | solution.py:671
  229.0 1.9 collective-permute-start.49
  (78 other events, 585.8 us)

commit v10 on v7

--- a/solution.py
+++ b/solution.py
@@ -887,20 +887,19 @@
     dinput, = call(finish_kernel, None, (), (gains, dealt, aa_high, aa_far, *(v for f in final for v in f)),
                    [((length, QUARTER), BF16)], [], "finish", 8, (att, fa_side))
     input_grad = collect(to_bands(dinput), "collect_grad")
-    result, = call(output_kernel, info, (), (late(y_far, dinput), *(v for p in zip(y_keep, y_got) for v in p)),
-                   [((length, QUARTER), BF16)], [], "output", 8)
-    output = collect(to_bands(result), "collect_out", input_grad)
-
     outs = [sds((adapters, 2 * RANK, WIDTH), F32), sds((adapters, RANK, WIDTH), F32),
             sds((adapters, 2, RANK, units), F32), sds((adapters, RANK, units), F32)]
     ga_ffn, g_down_b, g_ffn_b, g_down_a = sum_call(
         feedforward_sum_kernel, (info, owners),
         ((fb, fb_more, fb_side, fb_more_side), (fa, fa_side), (near(fa), near(fa_side))), outs, "feedforward_sum")
 
+    result, = call(output_kernel, info, (), (late(y_far, dinput, g_down_a), *(v for p in zip(y_keep, y_got) for v in p)),
+                   [((length, QUARTER), BF16)], [], "output", 8)
+    output = collect(to_bands(result), "collect_out", input_grad)
+
     att_side = swap(att, bits[-1], "dp", dp)
     a_parts = [att[:, n_b:], att_side[:, n_b:]]
     a_far = [far(v) for v in a_parts]
-    a_far[1] = late(a_far[1], g_down_a)
     outs = [sds((adapters, 3 * RANK, WIDTH), F32), sds((adapters, RANK, WIDTH), F32),
             sds((adapters, RANK, q_cols), F32), sds((adapters, 2, RANK, kv_cols), F32),
             sds((adapters, RANK, q_cols), F32)]

time: 223 us -> 220 us (0.987)
  local copies, waits for them, and re-layouts: 8.27 us -> 5.3 us
    unnamed x150, local copies, waits for them, and re-layouts: 7.2 us -> 4.24 us
  transfers between devices with their start and end apart: 53 -> 53, of which waited for: 23 -> 24; matrix products, arithmetic and copies ran while one was open for 2% -> 2% of each run, Pallas kernels for 40% -> 41%
where the time goes in v10:
time: 220 us; the launch traced here: 219 us
  Pallas kernels  106 us (48%)
  waiting for transfers between devices  54.5 us (25%)
  starting transfers between devices  48.5 us (22%)
  local copies, waits for them, and re-layouts  5.3 us (2%)
  other arithmetic  2.31 us (1%)
    pallas_call x26, Pallas kernels, call(): pl.pallas_call(body, in_specs=[pl.BlockSpec(memory_space=pltpu.SMEM)] * n...  90.7 us
    ppermute x50, waiting for transfers between devices, swap(): return lax.ppermute(value, axis, [(i, i ^ bit) for i in range(size)])  54.5 us
    ppermute x50, starting transfers between devices, swap(): return lax.ppermute(value, axis, [(i, i ^ bit) for i in range(size)])  31.6 us
    all_to_all x2, starting transfers between devices, to_bands(): lax.all_to_all(value.reshape(dp, length // dp, QUARTER), 'dp', split_axis...  9.63 us
    pallas_call x2, Pallas kernels, sum_call(): pl.pallas_call(functools.partial(kernel, [len(group) for group in groups]...  8.53 us
    all_to_all x1, starting transfers between devices, shards(): lax.all_to_all(ordered, 'dp', split_axis=0, concat_axis=1, tiled=True)[0]  7.26 us
    pallas_call x3, Pallas kernels, move_rows(): pl.pallas_call(kernel, in_specs=[pl.BlockSpec(memory_space=pltpu.SMEM), p...  5.25 us
  transfers between devices with their start and end apart: 53, of which 24 were waited for; matrix products, arithmetic and copies ran while one was open for 2% of the time, Pallas kernels for 41%

profile of v10, /device:TPU:0, one launch (start us, length us, event | category | flops | bytes accessed | tf_op | source)
XLA Modules:
  0.0 218.9 jit_solution(3400841736078052761)
XLA Ops:
  0.7 0.7 copy-done.64
  1.4 2.5 %deal.1 = bf16[8,64,512]{2,1,0:T(8,128)(2,1)} custom-call(s32[8]{0:T(128)S(1)} %copy-done.64, bf16[8,64,512]{2,1,0:T(8,128)(2,1)} %source.1), custom_call_target="tpu_custom_call" | custom-call | flops 1000 | bytes 1000 | tf_op jit(solution)/shard_map/deal/pallas_call | solution.py:599
  3.9 7.3 %all-to-all-start = ((bf16[8,64,512]{2,1,0:T(8,128)(2,1)}), bf16[8,64,512]{2,1,0:T(8,128)(2,1)S(1)}, u32[]{:S(2)}, u32[]{:S(2)}) async-start(bf16[8,64,512]{2,1,0:T(8,128)(2,1)} %deal.1), calls=%async_computation | async-start | bytes 1048576 | tf_op jit(solution)/shard_map/all_to_all | solution.py:750
  11.3 1.6 collective-permute-start.1
  14.2 0.7 collective-permute-done.1
  14.9 1.4 pad_add_fusion.info.refs_0_
  16.3 1.8 adapters.1
  19.4 7.4 %collective-permute-done.3.refs_11_.refs_10_ = bf16[512,512]{1,0:T(8,128)(2,1)S(1)} collective-permute-done((bf16[512,512]{1,0:T(8,128)(2,1)S(1)}, bf16[512,512]{1,0:T(8,128)(2,1)S(1)}, u32[]{:S(2)}, u32[]{:S(2)}) %collective-permute-start.3) | collective-permute-done | bytes 524320 | tf_op jit(solution)/shard_map/ppermute | solution.py:671
  27.5 7.0 %collective-permute-done.5.refs_5_.refs_6_ = bf16[256,512]{1,0:T(8,128)(2,1)S(1)} collective-permute-done((bf16[256,512]{1,0:T(8,128)(2,1)S(1)}, bf16[256,512]{1,0:T(8,128)(2,1)S(1)}, u32[]{:S(2)}, u32[]{:S(2)}) %collective-permute-start.5) | collective-permute-done | bytes 262176 | tf_op jit(solution)/shard_map/ppermute | solution.py:671
  35.1 1.0 collective-permute-done.6.refs_6_.refs_7_
  36.1 4.1 %project_0.1 = (bf16[48,256]{1,0:T(8,128)(2,1)S(1)}, bf16[512,256]{1,0:T(8,128)(2,1)S(1)}, bf16[2,256,64]{2,1,0:T(8,128)(2,1)S(1)}, bf16[2,256,64]{2,1,0:T(8,128...) custom-call(s32[4]{0:T(128)S(1)} %pad_add_fusion.info.refs_0_, bf16[2048,512]{1,0:T(8,128)(2,1)} %refs_1_.15, ...), custom_call_target="tpu_custom_call" | custom-call | flops 1000 | bytes 1000 | tf_op jit(solution)/shard_map/project_0/pallas_call | solution.py:632
  40.2 3.1 %attend_0.1 = (f32[256,1024]{1,0:T(8,128)S(1)}, bf16[256,1024]{1,0:T(8,128)(2,1)S(1)}, bf16[512,256]{1,0:T(8,128)(2,1)S(1)}, f32[8,256]{1,0:T(8,128)S(1)}, bf16[16,256]{1,0:T(8,128)(2,1)S(1)}) custom-call(s32[4]{0:T(128)S(1)} %pad_add_fusion.info.refs_0_, bf16[512,2048]{1,0:T(8,128)(2,1)} %refs_3_.5, ...), custom_call_target="tpu_custom_call" | custom-call | flops 1000 | bytes 1000 | tf_op jit(solution)/shard_map/attend_0/pallas_call | solution.py:632
  43.5 1.8 collective-permute-done.10.refs_1_
  46.0 1.5 collective-permute-done.13.refs_6_.refs_7_
  47.6 4.1 %project_1.1 = (bf16[48,256]{1,0:T(8,128)(2,1)S(1)}, bf16[512,256]{1,0:T(8,128)(2,1)S(1)}, bf16[2,256,64]{2,1,0:T(8,128)(2,1)S(1)}, bf16[2,256,64]{2,1,0:T(8,128...) custom-call(s32[4]{0:T(128)S(1)} %pad_add_fusion.info.refs_0_, bf16[2048,512]{1,0:T(8,128)(2,1)} %refs_1_.15, ...), custom_call_target="tpu_custom_call" | custom-call | flops 1000 | bytes 1000 | tf_op jit(solution)/shard_map/project_1/pallas_call | solution.py:632
  51.8 3.7 %attend_1.1 = (f32[256,1024]{1,0:T(8,128)S(1)}, bf16[256,1024]{1,0:T(8,128)(2,1)S(1)}, bf16[512,256]{1,0:T(8,128)(2,1)S(1)}, f32[8,256]{1,0:T(8,128)S(1)}, bf16[16,256]{1,0:T(8,128)(2,1)S(1)}) custom-call(s32[4]{0:T(128)S(1)} %pad_add_fusion.info.refs_0_, bf16[512,2048]{1,0:T(8,128)(2,1)} %refs_3_.5, ...), custom_call_target="tpu_custom_call" | custom-call | flops 1000 | bytes 1000 | tf_op jit(solution)/shard_map/attend_1/pallas_call | solution.py:632
  55.5 3.9 %collective-permute-done.11.refs_1_ = bf16[256,1024]{1,0:T(8,128)(2,1)S(1)} collective-permute-done((bf16[256,1024]{1,0:T(8,128)(2,1)S(1)}, bf16[256,1024]{1,0:T(8,128)(2,1)S(1)}, u32[]{:S(2)}, u32[]{:S(2)}) %collective-permute-start.11) | collective-permute-done | bytes 524320 | tf_op jit(solution)/shard_map/ppermute | solution.py:671
  61.5 0.7 collective-permute-start.15
  62.2 0.7 collective-permute-done.8.refs_12_.refs_11_
  62.8 0.7 collective-permute-done.12.refs_8_
  63.6 13.0 %front_0.1 = (bf16[256,2048]{1,0:T(8,128)(2,1)S(1)}, f32[256,512]{1,0:T(8,128)S(1)}, bf16[256,2048]{1,0:T(8,128)(2,1)S(1)}, bf16[256,2048]{1,0:T(8,128)(2,1)S(1)...) custom-call(s32[4]{0:T(128)S(1)} %pad_add_fusion.info.refs_0_, ...), custom_call_target="tpu_custom_call" | custom-call | flops 1000 | bytes 1000 | tf_op jit(solution)/shard_map/front_0/pallas_call | solution.py:632
  76.6 1.0 copy-done.24
  77.9 1.8 collective-permute-done.16.refs_8_
  79.7 12.0 %front_1.1 = (bf16[256,2048]{1,0:T(8,128)(2,1)S(1)}, f32[256,512]{1,0:T(8,128)S(1)}, bf16[256,2048]{1,0:T(8,128)(2,1)S(1)}, bf16[256,2048]{1,0:T(8,128)(2,1)S(1)...) custom-call(s32[4]{0:T(128)S(1)} %pad_add_fusion.info.refs_0_, ...), custom_call_target="tpu_custom_call" | custom-call | flops 1000 | bytes 1000 | tf_op jit(solution)/shard_map/front_1/pallas_call | solution.py:632
  91.7 3.0 %collective-permute-start.17 = (bf16[1,192,512]{2,1,0:T(8,128)(2,1)S(1)}, bf16[1,192,512]{2,1,0:T(8,128)(2,1)S(1)}, u32[]{:S(2)}, u32[]{:S(2)}) collective-permute-start(bf16[1,192,512]{2,1,0:T(8,128)(2,1)S(1)} %bitcast.36), channel_id=1, source_target_pairs={{0,16},{4,20},{8,24},{12,28},{16,0},{20,4},{24,8},{28,12},{1,17},{... | collective-permute-start | bytes 589832 | tf_op jit(solution)/shard_map/ppermute | solution.py:671
  94.7 7.9 %back_1.1 = (f32[256,16]{1,0:T(8,128)S(1)}, f32[256,1024]{1,0:T(8,128)S(1)}, bf16[256,1024]{1,0:T(8,128)(2,1)S(1)}, f32[48,2048]{1,0:T(8,128)S(1)}) custom-call(s32[4]{0:T(128)S(1)} %pad_add_fusion.info.refs_0_, bf16[2,2048,2048]{2,1,0:T(8,128)(2,1)S(1)} %get-tuple-element.147.refs_1_, bf16[256,2048]{1,0:T(8,128)(2,1)S(1)} %get-tuple-element.157.refs_2_, ...), custom_call_target="tpu_custom_call" | custom-call | flops 1000 | bytes 1000 | tf_op jit(solution)/shard_map/back_1/pallas_call | solution.py:632
  102.6 1.5 collective-permute-done.17
  104.2 1.8 collective-permute-start.20
  106.5 0.7 collective-permute-start.22
  107.2 7.9 %back_0.1 = (f32[256,16]{1,0:T(8,128)S(1)}, f32[304,1024]{1,0:T(8,128)S(1)}, bf16[304,1024]{1,0:T(8,128)(2,1)S(1)}) custom-call(s32[4]{0:T(128)S(1)} %pad_add_fusion.info.refs_0_, bf16[2,2048,2048]{2,1,0:T(8,128)(2,1)S(1)} %get-tuple-element.147.refs_1_, bf16[256,2048]{1,0:T(8,128)(2,1)S(1)} %get-tuple-element.148.refs_2_, ...), custom_call_target="tpu_custom_call" | custom-call | flops 1000 | bytes 1000 | tf_op jit(solution)/shard_map/back_0/pallas_call | solution.py:632
  115.1 0.7 collective-permute-done.20.refs_2_
  115.8 1.4 collective-permute-done.19.refs_1_
  117.3 4.5 %down_1.1 = (f32[256,1024]{1,0:T(8,128)S(1)}, bf16[256,1024]{1,0:T(8,128)(2,1)}) custom-call(s32[4]{0:T(128)S(1)} %pad_add_fusion.info.refs_0_, bf16[2048,2048]{1,0:T(8,128)(2,1)S(1)} %bitcast.19, bf16[256,2048]{1,0:T(8,128)(2,1)S(1)} %get-tuple-element.159.refs_4_.refs_2_, f32[256,16]{1,0:T(8,128)S(1)} %get-tuple-element.171.refs_3_, ...), custom_call_target="tpu_custom_call" | custom-call | flops 1000 | bytes 1000 | tf_op jit(solution)/shard_map/down_1/pallas_call | solution.py:632
  124.2 10.7 %attend_back_1.1 = (f32[256,512]{1,0:T(8,128)S(1)}, f32[256,1024]{1,0:T(8,128)S(1)}, bf16[256,1024]{1,0:T(8,128)(2,1)S(1)}, f32[256,1]{1,0:T(8,128)S(1)}, f32[48...) custom-call(s32[4]{0:T(128)S(1)} %pad_add_fusion.info.refs_0_, ...), custom_call_target="tpu_custom_call" | custom-call | flops 1000 | bytes 1000 | tf_op jit(solution)/shard_map/attend_back_1/pallas_call | solution.py:632
  135.5 3.8 %collective-permute-done.23.refs_1_ = bf16[304,1024]{1,0:T(8,128)(2,1)S(1)} collective-permute-done((bf16[304,1024]{1,0:T(8,128)(2,1)S(1)}, bf16[304,1024]{1,0:T(8,128)(2,1)S(1)}, u32[]{:S(2)}, u32[]{:S(2)}) %collective-permute-start.23) | collective-permute-done | bytes 622624 | tf_op jit(solution)/shard_map/ppermute | solution.py:671
  140.3 2.3 %collective-permute-start.28 = (bf16[1,48,1024]{2,1,0:T(8,128)(2,1)S(1)}, bf16[1,48,1024]{2,1,0:T(8,128)(2,1)S(1)}, u32[]{:S(2)}, u32[]{:S(2)}) collective-permute-start(bf16[1,48,1024]{2,1,0:T(8,128)(2,1)S(1)} %slice_bitcast_fusion), channel_id=1, source_target_pairs={{0,16},{4,20},{8,24},{12,28},{16,0},{20,4},{24,8},{28,12},{1,17},{... | collective-permute-start | bytes 294920 | tf_op jit(solution)/shard_map/ppermute | solution.py:671
  142.6 9.8 %attend_back_0.1 = (f32[256,512]{1,0:T(8,128)S(1)}, f32[256,1024]{1,0:T(8,128)S(1)}, bf16[256,1024]{1,0:T(8,128)(2,1)S(1)}, f32[256,1]{1,0:T(8,128)S(1)}, bf16[4...) custom-call(s32[4]{0:T(128)S(1)} %pad_add_fusion.info.refs_0_, ...), custom_call_target="tpu_custom_call" | custom-call | flops 1000 | bytes 1000 | tf_op jit(solution)/shard_map/attend_back_0/pallas_call | solution.py:632
  153.1 1.7 collective-permute-done.30.refs_1_
  154.7 1.3 collective-permute-start.31
  156.1 1.7 collective-permute-start.36
  157.9 0.7 collective-permute-start.33
  158.6 1.1 collective-permute-done.31.refs_3_
  159.7 1.3 collective-permute-start.34
  161.0 2.9 %collective-permute-done.36 = bf16[2,48,1024]{2,1,0:T(8,128)(2,1)S(1)} collective-permute-done((bf16[2,48,1024]{2,1,0:T(8,128)(2,1)S(1)}, bf16[2,48,1024]{2,1,0:T(8,128)(2,1)S(1)}, u32[]{:S(2)}, u32[]{:S(2)}) %collective-permute-start.36) | collective-permute-done | bytes 196640 | tf_op jit(solution)/shard_map/ppermute | solution.py:671
  164.5 4.5 %down_0.1 = (f32[256,1024]{1,0:T(8,128)S(1)}, bf16[256,1024]{1,0:T(8,128)(2,1)}) custom-call(s32[4]{0:T(128)S(1)} %pad_add_fusion.info.refs_0_, bf16[2048,2048]{1,0:T(8,128)(2,1)S(1)} %bitcast.19, bf16[256,2048]{1,0:T(8,128)(2,1)S(1)} %copy-done.5, f32[256,16]{1,0:T(8,128)S(1)} %get-tuple-element.173.refs_6_.refs_3_, ...), custom_call_target="tpu_custom_call" | custom-call | flops 1000 | bytes 1000 | tf_op jit(solution)/shard_map/down_0/pallas_call | solution.py:632
  169.1 1.8 collective-permute-start.35
  171.5 3.7 %collective-permute-done.35 = bf16[2,112,512]{2,1,0:T(8,128)(2,1)S(1)} collective-permute-done((bf16[2,112,512]{2,1,0:T(8,128)(2,1)S(1)}, bf16[2,112,512]{2,1,0:T(8,128)(2,1)S(1)}, u32[]{:S(2)}, u32[]{:S(2)}) %collective-permute-start.35) | collective-permute-done | bytes 229408 | tf_op jit(solution)/shard_map/ppermute | solution.py:671
  175.8 0.8 copy-done.16
  176.6 3.9 %all-to-all-start.1 = ((bf16[8,64,512]{2,1,0:T(8,128)(2,1)}), bf16[8,64,512]{2,1,0:T(8,128)(2,1)S(1)}, u32[]{:S(2)}, u32[]{:S(2)}) async-start(bf16[8,64,512]{2,1,0:T(8,128)(2,1)} %bitcast.35), calls=%async_computation.1 | async-start | bytes 1048576 | tf_op jit(solution)/shard_map/all_to_all | solution.py:826
  180.6 1.4 high_sum.7
  182.0 0.9 collective-permute-start.40
  183.4 2.0 collective-permute-start.43
  185.5 4.0 %feedforward_sum.1 = (f32[8,32,2048]{2,1,0:T(8,128)}, f32[8,16,2048]{2,1,0:T(8,128)}, f32[8,2,16,2048]{3,2,1,0:T(8,128)}, f32[8,16,2048]{2,1,0:T(8,128)}) custom-call(s32[4]{0:T(128)S(1)} %pad_add_fusion.info.refs_0_, s32[8]{0:T(128)S(1)} %copy-done.67, bf16[2,192,512]{2,1,0:T(8,128)(2,1)S(1)} %copy-done.18, bf16[2,192,512]{2,1,0:T(8,128)(2,1)S(1)} %copy-done.41, ...), custom_call_target="tpu_custom_call" | custom-call | bytes 12000000 | tf_op jit(solution)/shard_map/feedforward_sum/pallas_call | solution.py:655
  189.5 2.9 %collective-permute-done.40.refs_1_ = bf16[512,512]{1,0:T(8,128)(2,1)S(1)} collective-permute-done((bf16[512,512]{1,0:T(8,128)(2,1)S(1)}, bf16[512,512]{1,0:T(8,128)(2,1)S(1)}, u32[]{:S(2)}, u32[]{:S(2)}) %collective-permute-start.40) | collective-permute-done | bytes 524320 | tf_op jit(solution)/shard_map/ppermute | solution.py:671
  192.4 2.2 %output.1 = bf16[512,512]{1,0:T(8,128)(2,1)} custom-call(s32[4]{0:T(128)S(1)} %pad_add_fusion.info.refs_0_, bf16[512,512]{1,0:T(8,128)(2,1)S(1)} %collective-permute-done.40.refs_1_, f32[256,1024]{1,0:T(8,128)S(1)} %get-tuple-element.212.refs_0_.refs_2_, bf16[256,1024]{1,0:T(8,128)(2,1)} %collective-permute-done.38.refs_1_.refs_3_, ...), custom_call_target="tpu_custom_call" | custom-call | flops 1000 | bytes 1000 | tf_op jit(solution)/shard_map/output/pallas_call | solution.py:632
  194.6 5.7 %all-to-all-start.2 = ((bf16[8,64,512]{2,1,0:T(8,128)(2,1)}), bf16[8,64,512]{2,1,0:T(8,128)(2,1)S(1)}, u32[]{:S(2)}, u32[]{:S(2)}) async-start(bf16[8,64,512]{2,1,0:T(8,128)(2,1)} %bitcast.14), calls=%async_computation.2 | async-start | bytes 1048576 | tf_op jit(solution)/shard_map/all_to_all | solution.py:826
  200.3 1.3 collective-permute-start.46
  201.7 1.0 slice.35.refs_3_
  202.6 0.8 collective-permute-start.47
  203.5 5.0 %collective-permute-done.46.refs_6_ = bf16[4,64,512]{2,1,0:T(8,128)(2,1)S(1)} collective-permute-done((bf16[4,64,512]{2,1,0:T(8,128)(2,1)S(1)}, bf16[4,64,512]{2,1,0:T(8,128)(2,1)S(1)}, u32[]{:S(2)}, u32[]{:S(2)}) %collective-permute-start.46) | collective-permute-done | bytes 262176 | tf_op jit(solution)/shard_map/ppermute | solution.py:671
  209.0 2.3 %collective-permute-done.47.refs_7_ = bf16[4,64,512]{2,1,0:T(8,128)(2,1)S(1)} collective-permute-done((bf16[4,64,512]{2,1,0:T(8,128)(2,1)S(1)}, bf16[4,64,512]{2,1,0:T(8,128)(2,1)S(1)}, u32[]{:S(2)}, u32[]{:S(2)}) %collective-permute-start.47) | collective-permute-done | bytes 262176 | tf_op jit(solution)/shard_map/ppermute | solution.py:671
  211.3 1.4 collect_grad.1
  212.8 4.5 %attention_sum.1 = (f32[8,48,2048]{2,1,0:T(8,128)}, f32[8,16,2048]{2,1,0:T(8,128)}, f32[8,16,512]{2,1,0:T(8,128)}, f32[8,2,16,128]{3,2,1,0:T(8,128)}, f32[8,16,512]{2,1,0:T(8,128)}) custom-call(s32[4]{0:T(128)S(1)} %pad_add_fusion.info.refs_0_, s32[8]{0:T(128)S(1)} %copy-done.67, bf16[4,112,512]{2,1,0:T(8,128)(2,1)S(1)} %constant_dynamic-update-slice_fusion.refs_14_.refs_0_, ...), custom_call_target="tpu_custom_call" | custom-call | bytes 12000000 | tf_op jit(solution)/shard_map/attention_sum/pallas_call | solution.py:655
  217.3 1.4 collect_out.1
  (244 shorter events, 15.3 us)
Async XLA Ops:
  3.9 23.0 %all-to-all-start = ((bf16[8,64,512]{2,1,0:T(8,128)(2,1)}), bf16[8,64,512]{2,1,0:T(8,128)(2,1)S(1)}, u32[]{:S(2)}, u32[]{:S(2)}) async-start(bf16[8,64,512]{2,1,0:T(8,128)(2,1)} %deal.1), calls=%async_computation | async-start | bytes 1048576 | tf_op jit(solution)/shard_map/all_to_all | solution.py:750
  11.2 8.2 %collective-permute-start = (bf16[2,512]{1,0:T(2,128)(2,1)S(1)}, bf16[2,512]{1,0:T(2,128)(2,1)S(1)}, u32[]{:S(2)}, u32[]{:S(2)}) collective-permute-start(bf16[2,512]{1,0:T(2,128)(2,1)S(1)} %pad_maximum_fusion.4), channel_id=1, source_target_pairs={{0,1},{1,0},{2,3},{3,2},{4,5},{5,4},{6,7},{7,6},{8,9},{9,8},{10,11... | collective-permute-start | bytes 6152 | tf_op jit(solution)/shard_map/ppermute | solution.py:671
  11.3 3.7 %collective-permute-start.1 = (bf16[2,512]{1,0:T(2,128)(2,1)S(1)}, bf16[2,512]{1,0:T(2,128)(2,1)S(1)}, u32[]{:S(2)}, u32[]{:S(2)}) collective-permute-start(bf16[2,512]{1,0:T(2,128)(2,1)S(1)} %pad_maximum_fusion.4), channel_id=1, source_target_pairs={{0,2},{1,3},{2,0},{3,1},{4,6},{5,7},{6,4},{7,5},{8,10},{9,11},{10,... | collective-permute-start | bytes 6152 | tf_op jit(solution)/shard_map/ppermute | solution.py:671
  12.9 14.0 %collective-permute-start.3 = (bf16[512,512]{1,0:T(8,128)(2,1)S(1)}, bf16[512,512]{1,0:T(8,128)(2,1)S(1)}, u32[]{:S(2)}, u32[]{:S(2)}) collective-permute-start(bf16[512,512]{1,0:T(8,128)(2,1)S(1)} %bitcast.29), channel_id=1, source_target_pairs={{0,2},{1,3},{2,0},{3,1},{4,6},{5,7},{6,4},{7,5},{8,10},{9,11},{10,... | collective-permute-start | bytes 1572872 | tf_op jit(solution)/shard_map/ppermute | solution.py:671
  14.9 4.5 %collective-permute-start.2 = (bf16[2,512]{1,0:T(2,128)(2,1)S(1)}, bf16[2,512]{1,0:T(2,128)(2,1)S(1)}, u32[]{:S(2)}, u32[]{:S(2)}) collective-permute-start(bf16[2,512]{1,0:T(2,128)(2,1)S(1)} %collective-permute-done.1), channel_id=1, source_target_pairs={{0,1},{1,0},{2,3},{3,2},{4,5},{5,4},{6,7},{7,6},{8,9},{9,8},{10,11... | collective-permute-start | bytes 6152 | tf_op jit(solution)/shard_map/ppermute | solution.py:671
  16.3 19.8 %copy-start.54 = (f32[32,256]{1,0:T(8,128)S(1)}, f32[32,256]{1,0:T(8,128)}, u32[]{:S(2)}) copy-start(f32[32,256]{1,0:T(8,128)} %constant.21.clone.refs_12_.refs_22_) | copy-start | bytes 98308
  16.3 19.8 %copy-start.56 = (f32[32,256]{1,0:T(8,128)S(1)}, f32[32,256]{1,0:T(8,128)}, u32[]{:S(2)}) copy-start(f32[32,256]{1,0:T(8,128)} %constant.19.clone.refs_11_.refs_21_) | copy-start | bytes 98308
  19.4 28.2 %copy-start.50 = (bf16[16,512]{1,0:T(8,128)(2,1)}, bf16[16,512]{1,0:T(8,128)(2,1)S(1)}, u32[]{:S(2)}) copy-start(bf16[16,512]{1,0:T(8,128)(2,1)S(1)} %get-tuple-element.121.refs_9_.refs_17_) | copy-start | bytes 49156
  19.4 28.2 %copy-start.58 = (bf16[2,16,128]{2,1,0:T(8,128)(2,1)}, bf16[2,16,128]{2,1,0:T(8,128)(2,1)S(1)}, u32[]{:S(2)}) copy-start(bf16[2,16,128]{2,1,0:T(8,128)(2,1)S(1)} %get-tuple-element.122.refs_10_.refs_18_) | copy-start | bytes 24580
  19.4 32.3 %copy-start.22 = (bf16[16,2048]{1,0:T(8,128)(2,1)}, bf16[16,2048]{1,0:T(8,128)(2,1)S(1)}, u32[]{:S(2)}) copy-start(bf16[16,2048]{1,0:T(8,128)(2,1)S(1)} %get-tuple-element.125.refs_4_.refs_20_) | copy-start | bytes 196612
  19.4 32.3 %copy-start.44 = (bf16[16,512]{1,0:T(8,128)(2,1)}, bf16[16,512]{1,0:T(8,128)(2,1)S(1)}, u32[]{:S(2)}) copy-start(bf16[16,512]{1,0:T(8,128)(2,1)S(1)} %get-tuple-element.124.refs_3_.refs_19_) | copy-start | bytes 49156
  26.9 7.6 %collective-permute-start.5 = (bf16[256,512]{1,0:T(8,128)(2,1)S(1)}, bf16[256,512]{1,0:T(8,128)(2,1)S(1)}, u32[]{:S(2)}, u32[]{:S(2)}) collective-permute-start(bf16[256,512]{1,0:T(8,128)(2,1)S(1)} %get-tuple-element.230), channel_id=1, source_target_pairs={{0,2},{1,3},{2,0},{3,1},{4,6},{5,7},{6,4},{7,5},{8,10},{9,11},{10,... | collective-permute-start | bytes 786440 | tf_op jit(solution)/shard_map/ppermute | solution.py:671
  27.5 8.6 %collective-permute-start.4 = (bf16[512,512]{1,0:T(8,128)(2,1)S(1)}, bf16[512,512]{1,0:T(8,128)(2,1)S(1)}, u32[]{:S(2)}, u32[]{:S(2)}) collective-permute-start(bf16[512,512]{1,0:T(8,128)(2,1)S(1)} %bitcast.21), channel_id=1, source_target_pairs={{0,1},{1,0},{2,3},{3,2},{4,5},{5,4},{6,7},{7,6},{8,9},{9,8},{10,11... | collective-permute-start | bytes 1572872 | tf_op jit(solution)/shard_map/ppermute | solution.py:671
  34.5 29.1 %copy-start.8 = (bf16[256,512]{1,0:T(8,128)(2,1)}, bf16[256,512]{1,0:T(8,128)(2,1)S(1)}, u32[]{:S(2)}) copy-start(bf16[256,512]{1,0:T(8,128)(2,1)S(1)} %collective-permute-done.5.refs_5_.refs_6_) | copy-start | bytes 786436
  34.5 1.5 collective-permute-start.6
  34.5 8.8 %collective-permute-start.9 = (bf16[256,512]{1,0:T(8,128)(2,1)S(1)}, bf16[256,512]{1,0:T(8,128)(2,1)S(1)}, u32[]{:S(2)}, u32[]{:S(2)}) collective-permute-start(bf16[256,512]{1,0:T(8,128)(2,1)S(1)} %get-tuple-element.229), channel_id=1, source_target_pairs={{0,2},{1,3},{2,0},{3,1},{4,6},{5,7},{6,4},{7,5},{8,10},{9,11},{10,... | collective-permute-start | bytes 786440 | tf_op jit(solution)/shard_map/ppermute | solution.py:671
  36.0 27.6 %copy-start.10 = (bf16[256,512]{1,0:T(8,128)(2,1)}, bf16[256,512]{1,0:T(8,128)(2,1)S(1)}, u32[]{:S(2)}) copy-start(bf16[256,512]{1,0:T(8,128)(2,1)S(1)} %collective-permute-done.6.refs_6_.refs_7_) | copy-start | bytes 786436
  43.3 2.0 collective-permute-start.10
  45.4 14.0 %collective-permute-start.11 = (bf16[256,1024]{1,0:T(8,128)(2,1)S(1)}, bf16[256,1024]{1,0:T(8,128)(2,1)S(1)}, u32[]{:S(2)}, u32[]{:S(2)}) collective-permute-start(bf16[256,1024]{1,0:T(8,128)(2,1)S(1)} %pair_sum.4.refs_0_.refs_14_), channel_id=1, source_target_pairs={{0,2},{1,3},{2,0},{3,1},{4,6},{5,7},{6,4},{7,5},{8,10},{9,11},{10,... | collective-permute-start | bytes 1572872 | tf_op jit(solution)/shard_map/ppermute | solution.py:671
  46.0 1.5 collective-permute-start.13
  47.6 32.1 %copy-start.6 = (bf16[256,512]{1,0:T(8,128)(2,1)}, bf16[256,512]{1,0:T(8,128)(2,1)S(1)}, u32[]{:S(2)}) copy-start(bf16[256,512]{1,0:T(8,128)(2,1)S(1)} %collective-permute-done.13.refs_6_.refs_7_) | copy-start | bytes 786436
  55.5 21.1 %copy-start.48 = (bf16[512,256]{1,0:T(8,128)(2,1)}, bf16[512,256]{1,0:T(8,128)(2,1)S(1)}, u32[]{:S(2)}) copy-start(bf16[512,256]{1,0:T(8,128)(2,1)S(1)} %get-tuple-element.178.refs_25_) | copy-start | bytes 786436
  59.4 1.9 collective-permute-start.14
  59.4 2.7 %collective-permute-start.7 = (bf16[512,512]{1,0:T(8,128)(2,1)S(1)}, bf16[512,512]{1,0:T(8,128)(2,1)S(1)}, u32[]{:S(2)}, u32[]{:S(2)}) collective-permute-start(bf16[512,512]{1,0:T(8,128)(2,1)S(1)} %bitcast.30), channel_id=1, source_target_pairs={{0,1},{1,0},{2,3},{3,2},{4,5},{5,4},{6,7},{7,6},{8,9},{9,8},{10,11... | collective-permute-start | bytes 1572872 | tf_op jit(solution)/shard_map/ppermute | solution.py:671
  59.9 2.9 %collective-permute-start.8 = (bf16[512,512]{1,0:T(8,128)(2,1)S(1)}, bf16[512,512]{1,0:T(8,128)(2,1)S(1)}, u32[]{:S(2)}, u32[]{:S(2)}) collective-permute-start(bf16[512,512]{1,0:T(8,128)(2,1)S(1)} %collective-permute-done.3.refs_11_.refs_10_), channel_id=1, source_target_pairs={{0,1},{1,0},{2,3},{3,2},{4,5},{5,4},{6,7},{7,6},{8,9},{9,8},{10,11... | collective-permute-start | bytes 1572872 | tf_op jit(solution)/shard_map/ppermute | solution.py:671
  60.2 3.4 %collective-permute-start.12 = (bf16[256,1024]{1,0:T(8,128)(2,1)S(1)}, bf16[256,1024]{1,0:T(8,128)(2,1)S(1)}, u32[]{:S(2)}, u32[]{:S(2)}) collective-permute-start(bf16[256,1024]{1,0:T(8,128)(2,1)S(1)} %far_sum.4.refs_7_), channel_id=1, source_target_pairs={{0,1},{1,0},{2,3},{3,2},{4,5},{5,4},{6,7},{7,6},{8,9},{9,8},{10,11... | collective-permute-start | bytes 1572872 | tf_op jit(solution)/shard_map/ppermute | solution.py:671
  61.5 16.1 %collective-permute-start.15 = (bf16[256,1024]{1,0:T(8,128)(2,1)S(1)}, bf16[256,1024]{1,0:T(8,128)(2,1)S(1)}, u32[]{:S(2)}, u32[]{:S(2)}) collective-permute-start(bf16[256,1024]{1,0:T(8,128)(2,1)S(1)} %pair_sum.5.refs_19_.refs_0_), channel_id=1, source_target_pairs={{0,2},{1,3},{2,0},{3,1},{4,6},{5,7},{6,4},{7,5},{8,10},{9,11},{10,... | collective-permute-start | bytes 1572872 | tf_op jit(solution)/shard_map/ppermute | solution.py:671
  77.6 29.6 %copy-start.4 = (bf16[256,2048]{1,0:T(8,128)(2,1)}, bf16[256,2048]{1,0:T(8,128)(2,1)S(1)}, u32[]{:S(2)}) copy-start(bf16[256,2048]{1,0:T(8,128)(2,1)S(1)} %get-tuple-element.150.refs_4_.refs_2_) | copy-start | bytes 3145732
  77.7 2.0 collective-permute-start.16
  91.7 12.4 %collective-permute-start.17 = (bf16[1,192,512]{2,1,0:T(8,128)(2,1)S(1)}, bf16[1,192,512]{2,1,0:T(8,128)(2,1)S(1)}, u32[]{:S(2)}, u32[]{:S(2)}) collective-permute-start(bf16[1,192,512]{2,1,0:T(8,128)(2,1)S(1)} %bitcast.36), channel_id=1, source_target_pairs={{0,16},{4,20},{8,24},{12,28},{16,0},{20,4},{24,8},{28,12},{1,17},{... | collective-permute-start | bytes 589832 | tf_op jit(solution)/shard_map/ppermute | solution.py:671
  104.1 2.3 %collective-permute-start.18 = (bf16[256,1024]{1,0:T(8,128)(2,1)S(1)}, bf16[256,1024]{1,0:T(8,128)(2,1)S(1)}, u32[]{:S(2)}, u32[]{:S(2)}) collective-permute-start(bf16[256,1024]{1,0:T(8,128)(2,1)S(1)} %get-tuple-element.167), channel_id=1, source_target_pairs={{0,1},{1,0},{2,3},{3,2},{4,5},{5,4},{6,7},{7,6},{8,9},{9,8},{10,11... | collective-permute-start | bytes 1572872 | tf_op jit(solution)/shard_map/ppermute | solution.py:671
  104.2 11.6 %collective-permute-start.20 = (bf16[2,192,512]{2,1,0:T(8,128)(2,1)S(1)}, bf16[2,192,512]{2,1,0:T(8,128)(2,1)S(1)}, u32[]{:S(2)}, u32[]{:S(2)}) collective-permute-start(bf16[2,192,512]{2,1,0:T(8,128)(2,1)S(1)} %pad_maximum_fusion.refs_0_), channel_id=1, source_target_pairs={{0,4},{4,0},{8,12},{12,8},{16,20},{20,16},{24,28},{28,24},{1,5},{5... | collective-permute-start | bytes 1179656 | tf_op jit(solution)/shard_map/ppermute | solution.py:671
  106.0 11.2 %collective-permute-start.19 = (bf16[2,192,512]{2,1,0:T(8,128)(2,1)S(1)}, bf16[2,192,512]{2,1,0:T(8,128)(2,1)S(1)}, u32[]{:S(2)}, u32[]{:S(2)}) collective-permute-start(bf16[2,192,512]{2,1,0:T(8,128)(2,1)S(1)} %pad_maximum_fusion.refs_0_), channel_id=1, source_target_pairs={{0,8},{4,12},{8,0},{12,4},{16,24},{20,28},{24,16},{28,20},{1,9},{5... | collective-permute-start | bytes 1179656 | tf_op jit(solution)/shard_map/ppermute | solution.py:671
  106.5 15.4 %collective-permute-start.22 = (bf16[256,1024]{1,0:T(8,128)(2,1)S(1)}, bf16[256,1024]{1,0:T(8,128)(2,1)S(1)}, u32[]{:S(2)}, u32[]{:S(2)}) collective-permute-start(bf16[256,1024]{1,0:T(8,128)(2,1)S(1)} %pair_sum.6.refs_11_.refs_0_), channel_id=1, source_target_pairs={{0,2},{1,3},{2,0},{3,1},{4,6},{5,7},{6,4},{7,5},{8,10},{9,11},{10,... | collective-permute-start | bytes 1572872 | tf_op jit(solution)/shard_map/ppermute | solution.py:671
  117.2 5.4 %collective-permute-start.21 = (bf16[304,1024]{1,0:T(8,128)(2,1)S(1)}, bf16[304,1024]{1,0:T(8,128)(2,1)S(1)}, u32[]{:S(2)}, u32[]{:S(2)}) collective-permute-start(bf16[304,1024]{1,0:T(8,128)(2,1)S(1)} %get-tuple-element.170), channel_id=1, source_target_pairs={{0,1},{1,0},{2,3},{3,2},{4,5},{5,4},{6,7},{7,6},{8,9},{9,8},{10,11... | collective-permute-start | bytes 1867784 | tf_op jit(solution)/shard_map/ppermute | solution.py:671
  122.1 2.1 collective-permute-start.24
  122.9 16.5 %collective-permute-start.23 = (bf16[304,1024]{1,0:T(8,128)(2,1)S(1)}, bf16[304,1024]{1,0:T(8,128)(2,1)S(1)}, u32[]{:S(2)}, u32[]{:S(2)}) collective-permute-start(bf16[304,1024]{1,0:T(8,128)(2,1)S(1)} %pair_sum.7.refs_34_.refs_0_), channel_id=1, source_target_pairs={{0,2},{1,3},{2,0},{3,1},{4,6},{5,7},{6,4},{7,5},{8,10},{9,11},{10,... | collective-permute-start | bytes 1867784 | tf_op jit(solution)/shard_map/ppermute | solution.py:671
  123.5 11.5 %collective-permute-start.26 = (bf16[2,192,512]{2,1,0:T(8,128)(2,1)S(1)}, bf16[2,192,512]{2,1,0:T(8,128)(2,1)S(1)}, u32[]{:S(2)}, u32[]{:S(2)}) collective-permute-start(bf16[2,192,512]{2,1,0:T(8,128)(2,1)S(1)} %collective-permute-done.19.refs_1_), channel_id=1, source_target_pairs={{0,4},{4,0},{8,12},{12,8},{16,20},{20,16},{24,28},{28,24},{1,5},{5... | collective-permute-start | bytes 1179656 | tf_op jit(solution)/shard_map/ppermute | solution.py:671
  135.1 4.5 %collective-permute-start.27 = (bf16[256,1024]{1,0:T(8,128)(2,1)S(1)}, bf16[256,1024]{1,0:T(8,128)(2,1)S(1)}, u32[]{:S(2)}, u32[]{:S(2)}) collective-permute-start(bf16[256,1024]{1,0:T(8,128)(2,1)S(1)} %get-tuple-element.195), channel_id=1, source_target_pairs={{0,1},{1,0},{2,3},{3,2},{4,5},{5,4},{6,7},{7,6},{8,9},{9,8},{10,11... | collective-permute-start | bytes 1572872 | tf_op jit(solution)/shard_map/ppermute | solution.py:671
  139.5 3.1 %collective-permute-start.25 = (bf16[304,1024]{1,0:T(8,128)(2,1)S(1)}, bf16[304,1024]{1,0:T(8,128)(2,1)S(1)}, u32[]{:S(2)}, u32[]{:S(2)}) collective-permute-start(bf16[304,1024]{1,0:T(8,128)(2,1)S(1)} %far_sum.7.refs_13_), channel_id=1, source_target_pairs={{0,1},{1,0},{2,3},{3,2},{4,5},{5,4},{6,7},{7,6},{8,9},{9,8},{10,11... | collective-permute-start | bytes 1867784 | tf_op jit(solution)/shard_map/ppermute | solution.py:671
  139.7 12.8 %collective-permute-start.29 = (bf16[256,512]{1,0:T(8,128)(2,1)S(1)}, bf16[256,512]{1,0:T(8,128)(2,1)S(1)}, u32[]{:S(2)}, u32[]{:S(2)}) collective-permute-start(bf16[256,512]{1,0:T(8,128)(2,1)S(1)} %high_sum.4.refs_36_), channel_id=1, source_target_pairs={{0,2},{1,3},{2,0},{3,1},{4,6},{5,7},{6,4},{7,5},{8,10},{9,11},{10,... | collective-permute-start | bytes 786440 | tf_op jit(solution)/shard_map/ppermute | solution.py:671
  140.3 12.1 %collective-permute-start.28 = (bf16[1,48,1024]{2,1,0:T(8,128)(2,1)S(1)}, bf16[1,48,1024]{2,1,0:T(8,128)(2,1)S(1)}, u32[]{:S(2)}, u32[]{:S(2)}) collective-permute-start(bf16[1,48,1024]{2,1,0:T(8,128)(2,1)S(1)} %slice_bitcast_fusion), channel_id=1, source_target_pairs={{0,16},{4,20},{8,24},{12,28},{16,0},{20,4},{24,8},{28,12},{1,17},{... | collective-permute-start | bytes 294920 | tf_op jit(solution)/shard_map/ppermute | solution.py:671
  152.5 5.4 %collective-permute-start.32 = (bf16[256,1024]{1,0:T(8,128)(2,1)S(1)}, bf16[256,1024]{1,0:T(8,128)(2,1)S(1)}, u32[]{:S(2)}, u32[]{:S(2)}) collective-permute-start(bf16[256,1024]{1,0:T(8,128)(2,1)S(1)} %get-tuple-element.202), channel_id=1, source_target_pairs={{0,1},{1,0},{2,3},{3,2},{4,5},{5,4},{6,7},{7,6},{8,9},{9,8},{10,11... | collective-permute-start | bytes 1572872 | tf_op jit(solution)/shard_map/ppermute | solution.py:671
  152.6 2.2 collective-permute-start.30
  154.7 4.9 %collective-permute-start.31 = (bf16[96,512]{1,0:T(8,128)(2,1)S(1)}, bf16[96,512]{1,0:T(8,128)(2,1)S(1)}, u32[]{:S(2)}, u32[]{:S(2)}) collective-permute-start(bf16[96,512]{1,0:T(8,128)(2,1)S(1)} %high_sum.5.refs_2_), channel_id=1, source_target_pairs={{0,2},{1,3},{2,0},{3,1},{4,6},{5,7},{6,4},{7,5},{8,10},{9,11},{10,... | collective-permute-start | bytes 294920 | tf_op jit(solution)/shard_map/ppermute | solution.py:671
  156.1 7.8 %collective-permute-start.36 = (bf16[2,48,1024]{2,1,0:T(8,128)(2,1)S(1)}, bf16[2,48,1024]{2,1,0:T(8,128)(2,1)S(1)}, u32[]{:S(2)}, u32[]{:S(2)}) collective-permute-start(bf16[2,48,1024]{2,1,0:T(8,128)(2,1)S(1)} %pad_maximum_fusion.2), channel_id=1, source_target_pairs={{0,8},{4,12},{8,0},{12,4},{16,24},{20,28},{24,16},{28,20},{1,9},{5... | collective-permute-start | bytes 589832 | tf_op jit(solution)/shard_map/ppermute | solution.py:671
  157.9 11.2 %collective-permute-start.33 = (bf16[256,512]{1,0:T(8,128)(2,1)S(1)}, bf16[256,512]{1,0:T(8,128)(2,1)S(1)}, u32[]{:S(2)}, u32[]{:S(2)}) collective-permute-start(bf16[256,512]{1,0:T(8,128)(2,1)S(1)} %high_sum.6), channel_id=1, source_target_pairs={{0,2},{1,3},{2,0},{3,1},{4,6},{5,7},{6,4},{7,5},{8,10},{9,11},{10,... | collective-permute-start | bytes 786440 | tf_op jit(solution)/shard_map/ppermute | solution.py:671
  159.7 9.4 %collective-permute-start.34 = (bf16[1,112,512]{2,1,0:T(8,128)(2,1)S(1)}, bf16[1,112,512]{2,1,0:T(8,128)(2,1)S(1)}, u32[]{:S(2)}, u32[]{:S(2)}) collective-permute-start(bf16[1,112,512]{2,1,0:T(8,128)(2,1)S(1)} %maximum_bitcast_fusion.refs_6_), channel_id=1, source_target_pairs={{0,16},{4,20},{8,24},{12,28},{16,0},{20,4},{24,8},{28,12},{1,17},{... | collective-permute-start | bytes 344072 | tf_op jit(solution)/shard_map/ppermute | solution.py:671
  163.9 11.4 %collective-permute-start.37 = (bf16[4,48,1024]{2,1,0:T(8,128)(2,1)S(1)}, bf16[4,48,1024]{2,1,0:T(8,128)(2,1)S(1)}, u32[]{:S(2)}, u32[]{:S(2)}) collective-permute-start(bf16[4,48,1024]{2,1,0:T(8,128)(2,1)S(1)} %constant_dynamic-update-slice_fusion.2.refs_4_), channel_id=1, source_target_pairs={{0,4},{4,0},{8,12},{12,8},{16,20},{20,16},{24,28},{28,24},{1,5},{5... | collective-permute-start | bytes 1179656 | tf_op jit(solution)/shard_map/ppermute | solution.py:671
  169.1 6.1 %collective-permute-start.35 = (bf16[2,112,512]{2,1,0:T(8,128)(2,1)S(1)}, bf16[2,112,512]{2,1,0:T(8,128)(2,1)S(1)}, u32[]{:S(2)}, u32[]{:S(2)}) collective-permute-start(bf16[2,112,512]{2,1,0:T(8,128)(2,1)S(1)} %pad_maximum_fusion.1), channel_id=1, source_target_pairs={{0,8},{4,12},{8,0},{12,4},{16,24},{20,28},{24,16},{28,20},{1,9},{5... | collective-permute-start | bytes 688136 | tf_op jit(solution)/shard_map/ppermute | solution.py:671
  171.0 9.6 %collective-permute-start.39 = (bf16[256,1024]{1,0:T(8,128)(2,1)}, bf16[256,1024]{1,0:T(8,128)(2,1)}, u32[]{:S(2)}, u32[]{:S(2)}) collective-permute-start(bf16[256,1024]{1,0:T(8,128)(2,1)} %get-tuple-element.215.refs_35_), channel_id=1, source_target_pairs={{0,1},{1,0},{2,3},{3,2},{4,5},{5,4},{6,7},{7,6},{8,9},{9,8},{10,11... | collective-permute-start | bytes 1572872 | tf_op jit(solution)/shard_map/ppermute | solution.py:671
  171.0 9.6 %collective-permute-start.38 = (bf16[256,1024]{1,0:T(8,128)(2,1)}, bf16[256,1024]{1,0:T(8,128)(2,1)}, u32[]{:S(2)}, u32[]{:S(2)}) collective-permute-start(bf16[256,1024]{1,0:T(8,128)(2,1)} %get-tuple-element.208), channel_id=1, source_target_pairs={{0,1},{1,0},{2,3},{3,2},{4,5},{5,4},{6,7},{7,6},{8,9},{9,8},{10,11... | collective-permute-start | bytes 1572872 | tf_op jit(solution)/shard_map/ppermute | solution.py:671
  176.6 18.0 %all-to-all-start.1 = ((bf16[8,64,512]{2,1,0:T(8,128)(2,1)}), bf16[8,64,512]{2,1,0:T(8,128)(2,1)S(1)}, u32[]{:S(2)}, u32[]{:S(2)}) async-start(bf16[8,64,512]{2,1,0:T(8,128)(2,1)} %bitcast.35), calls=%async_computation.1 | async-start | bytes 1048576 | tf_op jit(solution)/shard_map/all_to_all | solution.py:826
  182.0 10.3 %collective-permute-start.40 = (bf16[512,512]{1,0:T(8,128)(2,1)S(1)}, bf16[512,512]{1,0:T(8,128)(2,1)S(1)}, u32[]{:S(2)}, u32[]{:S(2)}) collective-permute-start(bf16[512,512]{1,0:T(8,128)(2,1)S(1)} %high_sum.7), channel_id=1, source_target_pairs={{0,2},{1,3},{2,0},{3,1},{4,6},{5,7},{6,4},{7,5},{8,10},{9,11},{10,... | collective-permute-start | bytes 1572872 | tf_op jit(solution)/shard_map/ppermute | solution.py:671
  182.9 2.5 %collective-permute-start.41 = (bf16[4,48,1024]{2,1,0:T(8,128)(2,1)S(1)}, bf16[4,48,1024]{2,1,0:T(8,128)(2,1)S(1)}, u32[]{:S(2)}, u32[]{:S(2)}) collective-permute-start(bf16[4,48,1024]{2,1,0:T(8,128)(2,1)S(1)} %copy-done.33), channel_id=1, source_target_pairs={{0,1},{1,0},{2,3},{3,2},{4,5},{5,4},{6,7},{7,6},{8,9},{9,8},{10,11... | collective-permute-start | bytes 1179656 | tf_op jit(solution)/shard_map/ppermute | solution.py:671
  182.9 2.5 %collective-permute-start.42 = (bf16[4,48,1024]{2,1,0:T(8,128)(2,1)S(1)}, bf16[4,48,1024]{2,1,0:T(8,128)(2,1)S(1)}, u32[]{:S(2)}, u32[]{:S(2)}) collective-permute-start(bf16[4,48,1024]{2,1,0:T(8,128)(2,1)S(1)} %collective-permute-done.37.refs_15_.refs_5_), channel_id=1, source_target_pairs={{0,1},{1,0},{2,3},{3,2},{4,5},{5,4},{6,7},{7,6},{8,9},{9,8},{10,11... | collective-permute-start | bytes 1179656 | tf_op jit(solution)/shard_map/ppermute | solution.py:671
  183.4 18.2 %collective-permute-start.43 = (bf16[4,112,512]{2,1,0:T(8,128)(2,1)S(1)}, bf16[4,112,512]{2,1,0:T(8,128)(2,1)}, u32[]{:S(2)}, u32[]{:S(2)}) collective-permute-start(bf16[4,112,512]{2,1,0:T(8,128)(2,1)S(1)} %constant_dynamic-update-slice_fusion.refs_14_.refs_0_), channel_id=1, source_target_pairs={{0,4},{4,0},{8,12},{12,8},{16,20},{20,16},{24,28},{28,24},{1,5},{5... | collective-permute-start | bytes 1376264 | tf_op jit(solution)/shard_map/ppermute | solution.py:671
  194.6 22.7 %all-to-all-start.2 = ((bf16[8,64,512]{2,1,0:T(8,128)(2,1)}), bf16[8,64,512]{2,1,0:T(8,128)(2,1)S(1)}, u32[]{:S(2)}, u32[]{:S(2)}) async-start(bf16[8,64,512]{2,1,0:T(8,128)(2,1)} %bitcast.14), calls=%async_computation.2 | async-start | bytes 1048576 | tf_op jit(solution)/shard_map/all_to_all | solution.py:826
  200.3 8.1 %collective-permute-start.46 = (bf16[4,64,512]{2,1,0:T(8,128)(2,1)S(1)}, bf16[4,64,512]{2,1,0:T(8,128)(2,1)S(1)}, u32[]{:S(2)}, u32[]{:S(2)}) collective-permute-start(bf16[4,64,512]{2,1,0:T(8,128)(2,1)S(1)} %slice.34.refs_2_), channel_id=1, source_target_pairs={{0,2},{1,3},{2,0},{3,1},{4,6},{5,7},{6,4},{7,5},{8,10},{9,11},{10,... | collective-permute-start | bytes 786440 | tf_op jit(solution)/shard_map/ppermute | solution.py:671
  202.6 8.6 %collective-permute-start.47 = (bf16[4,64,512]{2,1,0:T(8,128)(2,1)S(1)}, bf16[4,64,512]{2,1,0:T(8,128)(2,1)S(1)}, u32[]{:S(2)}, u32[]{:S(2)}) collective-permute-start(bf16[4,64,512]{2,1,0:T(8,128)(2,1)S(1)} %slice.35.refs_3_), channel_id=1, source_target_pairs={{0,2},{1,3},{2,0},{3,1},{4,6},{5,7},{6,4},{7,5},{8,10},{9,11},{10,... | collective-permute-start | bytes 786440 | tf_op jit(solution)/shard_map/ppermute | solution.py:671
  203.5 9.2 %collective-permute-start.44 = (bf16[4,64,512]{2,1,0:T(8,128)(2,1)S(1)}, bf16[4,64,512]{2,1,0:T(8,128)(2,1)S(1)}, u32[]{:S(2)}, u32[]{:S(2)}) collective-permute-start(bf16[4,64,512]{2,1,0:T(8,128)(2,1)S(1)} %slice.34.refs_2_), channel_id=1, source_target_pairs={{0,1},{1,0},{2,3},{3,2},{4,5},{5,4},{6,7},{7,6},{8,9},{9,8},{10,11... | collective-permute-start | bytes 786440 | tf_op jit(solution)/shard_map/ppermute | solution.py:671
  208.4 4.2 %collective-permute-start.48 = (bf16[4,64,512]{2,1,0:T(8,128)(2,1)S(1)}, bf16[4,64,512]{2,1,0:T(8,128)(2,1)S(1)}, u32[]{:S(2)}, u32[]{:S(2)}) collective-permute-start(bf16[4,64,512]{2,1,0:T(8,128)(2,1)S(1)} %collective-permute-done.46.refs_6_), channel_id=1, source_target_pairs={{0,1},{1,0},{2,3},{3,2},{4,5},{5,4},{6,7},{7,6},{8,9},{9,8},{10,11... | collective-permute-start | bytes 786440 | tf_op jit(solution)/shard_map/ppermute | solution.py:671
  208.4 4.2 %collective-permute-start.45 = (bf16[4,64,512]{2,1,0:T(8,128)(2,1)S(1)}, bf16[4,64,512]{2,1,0:T(8,128)(2,1)S(1)}, u32[]{:S(2)}, u32[]{:S(2)}) collective-permute-start(bf16[4,64,512]{2,1,0:T(8,128)(2,1)S(1)} %slice.35.refs_3_), channel_id=1, source_target_pairs={{0,1},{1,0},{2,3},{3,2},{4,5},{5,4},{6,7},{7,6},{8,9},{9,8},{10,11... | collective-permute-start | bytes 786440 | tf_op jit(solution)/shard_map/ppermute | solution.py:671
  211.3 1.5 collective-permute-start.49
  (63 other events, 409.3 us)

commit v11 on v9

--- a/solution.py
+++ b/solution.py
@@ -834,7 +834,7 @@
     *hidden[0], wgu, wd = front(0, far_sum(z_own[0], z_far[0]), (), order)
     step = hidden[0][8]
     hidden[1] = front(1, far_sum(z_own[1], late(z_far[1], step)), hidden[0][9:], (step,))
-    td, d_keep, d_send, fa = back(1, hidden[1], (), (hidden[1][8],))
+    td_1, d_keep, d_send, fa = back(1, hidden[1], (), (hidden[1][8],))
     d_own[1] = pair_sum(d_keep, d_send)
     d_far[1] = far(d_own[1])
     fb = late(hidden[1][9], d_own[1])[None]
@@ -848,9 +848,7 @@
         fb_more = doubled(fb_more, bit, dp)
     fb_more = fb_more[2:]
     fb_side = swap(fb, bits[-1], "dp", dp)
-    y_keep[1], y_send = down(1, td, (d_own[0],))
-    y_got[1] = near(late(y_send, d_own[0]))
-    dxq, h_keep, h_send, inv, *sums = attend_back(1, total, (), (d_own[0], y_send))
+    dxq, h_keep, h_send, inv, *sums = attend_back(1, total, (), (d_own[0],))
     total = far_sum(d_own[0], late(d_far[0], inv))
     h_got = near(late(h_send, fb_more, fb_side))
     fb_more_side = swap(fb_more, bits[-1], "dp", dp)
@@ -882,25 +880,26 @@
     for bit in bits[1:-1]:
         fa = doubled(fa, bit, dp)
     fa_side = swap(fa, bits[-1], "dp", dp)
+    y_keep[1], y_send = down(1, td_1, (first, y_send))
+    y_got[1] = near(y_send)
+    y_far = far(high_sum(*((k, late(g, h_far)) for k, g in zip(y_keep, y_got))))
 
     dinput, = call(finish_kernel, None, (), (gains, dealt, aa_high, aa_far, *(v for f in final for v in f)),
-                   [((length, QUARTER), BF16)], [], "finish", 8, (y_send, first, fa))
-    y_far = far(high_sum(*((k, late(g, att)) for k, g in zip(y_keep, y_got))))
-    att_side = swap(att, bits[-1], "dp", dp)
+                   [((length, QUARTER), BF16)], [], "finish", 8, (att, fa_side, y_send))
     input_grad = collect(to_bands(dinput), "collect_grad")
-    result, = call(output_kernel, info, (), (late(y_far, att_side), *(v for p in zip(y_keep, y_got) for v in p)),
-                   [((length, QUARTER), BF16)], [], "output", 8)
-    output = collect(to_bands(result), "collect_out", input_grad)
-
     outs = [sds((adapters, 2 * RANK, WIDTH), F32), sds((adapters, RANK, WIDTH), F32),
             sds((adapters, 2, RANK, units), F32), sds((adapters, RANK, units), F32)]
     ga_ffn, g_down_b, g_ffn_b, g_down_a = sum_call(
         feedforward_sum_kernel, (info, owners),
         ((fb, fb_more, fb_side, fb_more_side), (fa, fa_side), (near(fa), near(fa_side))), outs, "feedforward_sum")
 
+    result, = call(output_kernel, info, (), (late(y_far, dinput, g_down_a), *(v for p in zip(y_keep, y_got) for v in p)),
+                   [((length, QUARTER), BF16)], [], "output", 8)
+    output = collect(to_bands(result), "collect_out", input_grad)
+
+    att_side = swap(att, bits[-1], "dp", dp)
     a_parts = [att[:, n_b:], att_side[:, n_b:]]
     a_far = [far(v) for v in a_parts]
-    a_far[1] = late(a_far[1], g_down_a)
     outs = [sds((adapters, 3 * RANK, WIDTH), F32), sds((adapters, RANK, WIDTH), F32),
             sds((adapters, RANK, q_cols), F32), sds((adapters, 2, RANK, kv_cols), F32),
             sds((adapters, RANK, q_cols), F32)]

time: 237 us -> 222 us (0.937)
  waiting for transfers between devices: 68 us -> 56.1 us
  local copies, waits for them, and re-layouts: 11.3 us -> 5.09 us
    ppermute x50, waiting for transfers between devices: 68 us -> 56.1 us  [swap(): return lax.ppermute(value, axis, [(i, i ^ bit) for i in range(size)])]
    unnamed x180 -> x116, local copies, waits for them, and re-layouts: 9.33 us -> 4.02 us
    pallas_call x26, Pallas kernels: 87.9 us -> 90.7 us  [call(): pl.pallas_call(body, in_specs=[pl.BlockSpec(memory_space=pltpu.SMEM)] * n...]
  transfers between devices with their start and end apart: 53 -> 53, of which waited for: 23 -> 23; matrix products, arithmetic and copies ran while one was open for 2% -> 2% of each run, Pallas kernels for 34% -> 37%
where the time goes in v11:
time: 222 us
  Pallas kernels  106 us (48%)
  waiting for transfers between devices  56.1 us (25%)
  starting transfers between devices  49.7 us (22%)
  local copies, waits for them, and re-layouts  5.09 us (2%)
  other arithmetic  2.31 us (1%)
    pallas_call x26, Pallas kernels, call(): pl.pallas_call(body, in_specs=[pl.BlockSpec(memory_space=pltpu.SMEM)] * n...  90.7 us
    ppermute x50, waiting for transfers between devices, swap(): return lax.ppermute(value, axis, [(i, i ^ bit) for i in range(size)])  56.1 us
    ppermute x50, starting transfers between devices, swap(): return lax.ppermute(value, axis, [(i, i ^ bit) for i in range(size)])  33.3 us
    all_to_all x2, starting transfers between devices, to_bands(): lax.all_to_all(value.reshape(dp, length // dp, QUARTER), 'dp', split_axis...  9.13 us
    pallas_call x2, Pallas kernels, sum_call(): pl.pallas_call(functools.partial(kernel, [len(group) for group in groups]...  8.75 us
    all_to_all x1, starting transfers between devices, shards(): lax.all_to_all(ordered, 'dp', split_axis=0, concat_axis=1, tiled=True)[0]  7.26 us
    pallas_call x3, Pallas kernels, move_rows(): pl.pallas_call(kernel, in_specs=[pl.BlockSpec(memory_space=pltpu.SMEM), p...  5.25 us
  transfers between devices with their start and end apart: 53, of which 23 were waited for; matrix products, arithmetic and copies ran while one was open for 2% of the time, Pallas kernels for 37%

profile of v11, /device:TPU:0, one launch (start us, length us, event | category | flops | bytes accessed | tf_op | source)
XLA Modules:
  0.0 221.5 jit_solution(818118180739514548)
XLA Ops:
  0.7 0.7 copy-done.47
  1.4 2.5 %deal.1 = bf16[8,64,512]{2,1,0:T(8,128)(2,1)} custom-call(s32[8]{0:T(128)S(1)} %copy-done.47, bf16[8,64,512]{2,1,0:T(8,128)(2,1)} %source.1), custom_call_target="tpu_custom_call" | custom-call | flops 1000 | bytes 1000 | tf_op jit(solution)/shard_map/deal/pallas_call | solution.py:599
  3.9 7.3 %all-to-all-start = ((bf16[8,64,512]{2,1,0:T(8,128)(2,1)}), bf16[8,64,512]{2,1,0:T(8,128)(2,1)S(1)}, u32[]{:S(2)}, u32[]{:S(2)}) async-start(bf16[8,64,512]{2,1,0:T(8,128)(2,1)} %deal.1), calls=%async_computation | async-start | bytes 1048576 | tf_op jit(solution)/shard_map/all_to_all | solution.py:750
  11.3 1.6 collective-permute-start.1
  14.2 0.7 collective-permute-done.1
  14.9 1.4 pad_add_fusion.info.refs_0_
  16.3 1.8 adapters.1
  19.4 7.4 %collective-permute-done.3.refs_11_.refs_10_ = bf16[512,512]{1,0:T(8,128)(2,1)S(1)} collective-permute-done((bf16[512,512]{1,0:T(8,128)(2,1)S(1)}, bf16[512,512]{1,0:T(8,128)(2,1)S(1)}, u32[]{:S(2)}, u32[]{:S(2)}) %collective-permute-start.3) | collective-permute-done | bytes 524320 | tf_op jit(solution)/shard_map/ppermute | solution.py:671
  27.5 7.0 %collective-permute-done.5.refs_5_.refs_6_ = bf16[256,512]{1,0:T(8,128)(2,1)S(1)} collective-permute-done((bf16[256,512]{1,0:T(8,128)(2,1)S(1)}, bf16[256,512]{1,0:T(8,128)(2,1)S(1)}, u32[]{:S(2)}, u32[]{:S(2)}) %collective-permute-start.5) | collective-permute-done | bytes 262176 | tf_op jit(solution)/shard_map/ppermute | solution.py:671
  35.1 1.0 collective-permute-done.6.refs_6_.refs_7_
  36.1 4.1 %project_0.1 = (bf16[48,256]{1,0:T(8,128)(2,1)S(1)}, bf16[512,256]{1,0:T(8,128)(2,1)S(1)}, bf16[2,256,64]{2,1,0:T(8,128)(2,1)S(1)}, bf16[2,256,64]{2,1,0:T(8,128...) custom-call(s32[4]{0:T(128)S(1)} %pad_add_fusion.info.refs_0_, bf16[2048,512]{1,0:T(8,128)(2,1)} %refs_1_.15, ...), custom_call_target="tpu_custom_call" | custom-call | flops 1000 | bytes 1000 | tf_op jit(solution)/shard_map/project_0/pallas_call | solution.py:632
  40.2 3.1 %attend_0.1 = (f32[256,1024]{1,0:T(8,128)S(1)}, bf16[256,1024]{1,0:T(8,128)(2,1)S(1)}, bf16[512,256]{1,0:T(8,128)(2,1)S(1)}, f32[8,256]{1,0:T(8,128)S(1)}, bf16[16,256]{1,0:T(8,128)(2,1)S(1)}) custom-call(s32[4]{0:T(128)S(1)} %pad_add_fusion.info.refs_0_, bf16[512,2048]{1,0:T(8,128)(2,1)} %refs_3_.5, ...), custom_call_target="tpu_custom_call" | custom-call | flops 1000 | bytes 1000 | tf_op jit(solution)/shard_map/attend_0/pallas_call | solution.py:632
  43.5 1.8 collective-permute-done.10.refs_1_
  46.0 1.5 collective-permute-done.13.refs_6_.refs_7_
  47.6 4.1 %project_1.1 = (bf16[48,256]{1,0:T(8,128)(2,1)S(1)}, bf16[512,256]{1,0:T(8,128)(2,1)S(1)}, bf16[2,256,64]{2,1,0:T(8,128)(2,1)S(1)}, bf16[2,256,64]{2,1,0:T(8,128...) custom-call(s32[4]{0:T(128)S(1)} %pad_add_fusion.info.refs_0_, bf16[2048,512]{1,0:T(8,128)(2,1)} %refs_1_.15, ...), custom_call_target="tpu_custom_call" | custom-call | flops 1000 | bytes 1000 | tf_op jit(solution)/shard_map/project_1/pallas_call | solution.py:632
  51.7 3.7 %attend_1.1 = (f32[256,1024]{1,0:T(8,128)S(1)}, bf16[256,1024]{1,0:T(8,128)(2,1)S(1)}, bf16[512,256]{1,0:T(8,128)(2,1)S(1)}, f32[8,256]{1,0:T(8,128)S(1)}, bf16[16,256]{1,0:T(8,128)(2,1)S(1)}) custom-call(s32[4]{0:T(128)S(1)} %pad_add_fusion.info.refs_0_, bf16[512,2048]{1,0:T(8,128)(2,1)} %refs_3_.5, ...), custom_call_target="tpu_custom_call" | custom-call | flops 1000 | bytes 1000 | tf_op jit(solution)/shard_map/attend_1/pallas_call | solution.py:632
  55.5 4.0 %collective-permute-done.11.refs_1_ = bf16[256,1024]{1,0:T(8,128)(2,1)S(1)} collective-permute-done((bf16[256,1024]{1,0:T(8,128)(2,1)S(1)}, bf16[256,1024]{1,0:T(8,128)(2,1)S(1)}, u32[]{:S(2)}, u32[]{:S(2)}) %collective-permute-start.11) | collective-permute-done | bytes 524320 | tf_op jit(solution)/shard_map/ppermute | solution.py:671
  60.7 0.7 collective-permute-done.14.refs_1_
  62.1 0.7 collective-permute-done.8.refs_12_.refs_11_
  62.9 0.7 collective-permute-done.12.refs_8_
  63.6 12.9 %front_0.1 = (bf16[256,2048]{1,0:T(8,128)(2,1)S(1)}, f32[256,512]{1,0:T(8,128)S(1)}, bf16[256,2048]{1,0:T(8,128)(2,1)S(1)}, bf16[256,2048]{1,0:T(8,128)(2,1)S(1)...) custom-call(s32[4]{0:T(128)S(1)} %pad_add_fusion.info.refs_0_, ...), custom_call_target="tpu_custom_call" | custom-call | flops 1000 | bytes 1000 | tf_op jit(solution)/shard_map/front_0/pallas_call | solution.py:632
  76.6 1.0 copy-done.17
  77.9 1.8 collective-permute-done.16.refs_8_
  79.6 12.2 %front_1.1 = (bf16[256,2048]{1,0:T(8,128)(2,1)S(1)}, f32[256,512]{1,0:T(8,128)S(1)}, bf16[256,2048]{1,0:T(8,128)(2,1)S(1)}, bf16[256,2048]{1,0:T(8,128)(2,1)S(1)...) custom-call(s32[4]{0:T(128)S(1)} %pad_add_fusion.info.refs_0_, ...), custom_call_target="tpu_custom_call" | custom-call | flops 1000 | bytes 1000 | tf_op jit(solution)/shard_map/front_1/pallas_call | solution.py:632
  91.8 7.9 %back_1.1 = (f32[256,16]{1,0:T(8,128)S(1)}, f32[256,1024]{1,0:T(8,128)S(1)}, bf16[256,1024]{1,0:T(8,128)(2,1)S(1)}, f32[48,2048]{1,0:T(8,128)S(1)}) custom-call(s32[4]{0:T(128)S(1)} %pad_add_fusion.info.refs_0_, bf16[2,2048,2048]{2,1,0:T(8,128)(2,1)S(1)} %get-tuple-element.146.refs_1_, bf16[256,2048]{1,0:T(8,128)(2,1)S(1)} %get-tuple-element.156.refs_2_, ...), custom_call_target="tpu_custom_call" | custom-call | flops 1000 | bytes 1000 | tf_op jit(solution)/shard_map/back_1/pallas_call | solution.py:632
  99.8 1.8 collective-permute-done.17.refs_1_
  102.4 2.9 %collective-permute-start.18 = (bf16[1,192,512]{2,1,0:T(8,128)(2,1)S(1)}, bf16[1,192,512]{2,1,0:T(8,128)(2,1)S(1)}, u32[]{:S(2)}, u32[]{:S(2)}) collective-permute-start(bf16[1,192,512]{2,1,0:T(8,128)(2,1)S(1)} %bitcast.36), channel_id=1, source_target_pairs={{0,16},{4,20},{8,24},{12,28},{16,0},{20,4},{24,8},{28,12},{1,17},{... | collective-permute-start | bytes 589832 | tf_op jit(solution)/shard_map/ppermute | solution.py:671
  105.3 7.9 %back_0.1 = (f32[256,16]{1,0:T(8,128)S(1)}, f32[304,1024]{1,0:T(8,128)S(1)}, bf16[304,1024]{1,0:T(8,128)(2,1)S(1)}) custom-call(s32[4]{0:T(128)S(1)} %pad_add_fusion.info.refs_0_, bf16[2,2048,2048]{2,1,0:T(8,128)(2,1)S(1)} %get-tuple-element.146.refs_1_, bf16[256,2048]{1,0:T(8,128)(2,1)S(1)} %get-tuple-element.147.refs_2_, ...), custom_call_target="tpu_custom_call" | custom-call | flops 1000 | bytes 1000 | tf_op jit(solution)/shard_map/back_0/pallas_call | solution.py:632
  113.2 1.2 collective-permute-done.18
  114.4 1.3 collective-permute-done.19.refs_1_
  116.5 1.3 collective-permute-done.20.refs_1_
  118.6 2.1 collective-permute-start.25
  120.7 1.5 collective-permute-start.24
  122.2 10.5 %attend_back_1.1 = (f32[256,512]{1,0:T(8,128)S(1)}, f32[256,1024]{1,0:T(8,128)S(1)}, bf16[256,1024]{1,0:T(8,128)(2,1)S(1)}, f32[256,1]{1,0:T(8,128)S(1)}, f32[48...) custom-call(s32[4]{0:T(128)S(1)} %pad_add_fusion.info.refs_0_, ...), custom_call_target="tpu_custom_call" | custom-call | flops 1000 | bytes 1000 | tf_op jit(solution)/shard_map/attend_back_1/pallas_call | solution.py:632
  133.0 1.0 collective-permute-done.21.refs_1_
  134.3 2.1 collective-permute-start.29
  137.1 2.4 %collective-permute-start.27 = (bf16[1,48,1024]{2,1,0:T(8,128)(2,1)S(1)}, bf16[1,48,1024]{2,1,0:T(8,128)(2,1)S(1)}, u32[]{:S(2)}, u32[]{:S(2)}) collective-permute-start(bf16[1,48,1024]{2,1,0:T(8,128)(2,1)S(1)} %slice_bitcast_fusion), channel_id=1, source_target_pairs={{0,16},{4,20},{8,24},{12,28},{16,0},{20,4},{24,8},{28,12},{1,17},{... | collective-permute-start | bytes 294920 | tf_op jit(solution)/shard_map/ppermute | solution.py:671
  139.6 10.0 %attend_back_0.1 = (f32[256,512]{1,0:T(8,128)S(1)}, f32[256,1024]{1,0:T(8,128)S(1)}, bf16[256,1024]{1,0:T(8,128)(2,1)S(1)}, f32[256,1]{1,0:T(8,128)S(1)}, bf16[4...) custom-call(s32[4]{0:T(128)S(1)} %pad_add_fusion.info.refs_0_, ...), custom_call_target="tpu_custom_call" | custom-call | flops 1000 | bytes 1000 | tf_op jit(solution)/shard_map/attend_back_0/pallas_call | solution.py:632
  150.3 1.7 collective-permute-done.30.refs_1_
  151.9 1.5 collective-permute-start.31
  153.4 1.5 collective-permute-start.36
  155.0 0.7 collective-permute-start.33
  155.7 1.2 collective-permute-done.31.refs_3_
  157.5 3.6 %collective-permute-done.36 = bf16[2,48,1024]{2,1,0:T(8,128)(2,1)S(1)} collective-permute-done((bf16[2,48,1024]{2,1,0:T(8,128)(2,1)S(1)}, bf16[2,48,1024]{2,1,0:T(8,128)(2,1)S(1)}, u32[]{:S(2)}, u32[]{:S(2)}) %collective-permute-start.36) | collective-permute-done | bytes 196640 | tf_op jit(solution)/shard_map/ppermute | solution.py:671
  161.8 4.5 %down_0.1 = (f32[256,1024]{1,0:T(8,128)S(1)}, bf16[256,1024]{1,0:T(8,128)(2,1)}) custom-call(s32[4]{0:T(128)S(1)} %pad_add_fusion.info.refs_0_, bf16[2048,2048]{1,0:T(8,128)(2,1)S(1)} %bitcast.19, bf16[256,2048]{1,0:T(8,128)(2,1)S(1)} %copy-done.3, f32[256,16]{1,0:T(8,128)S(1)} %get-tuple-element.171.refs_3_, ...), custom_call_target="tpu_custom_call" | custom-call | flops 1000 | bytes 1000 | tf_op jit(solution)/shard_map/down_0/pallas_call | solution.py:632
  166.4 1.6 collective-permute-start.35
  168.0 4.5 %down_1.1 = (f32[256,1024]{1,0:T(8,128)S(1)}, bf16[256,1024]{1,0:T(8,128)(2,1)}) custom-call(s32[4]{0:T(128)S(1)} %pad_add_fusion.info.refs_0_, bf16[2048,2048]{1,0:T(8,128)(2,1)S(1)} %bitcast.19, bf16[256,2048]{1,0:T(8,128)(2,1)S(1)} %get-tuple-element.158.refs_4_.refs_2_, f32[256,16]{1,0:T(8,128)S(1)} %get-tuple-element.207.refs_3_, ...), custom_call_target="tpu_custom_call" | custom-call | flops 1000 | bytes 1000 | tf_op jit(solution)/shard_map/down_1/pallas_call | solution.py:632
  173.7 0.8 copy-done.10
  174.5 3.5 %all-to-all-start.1 = ((bf16[8,64,512]{2,1,0:T(8,128)(2,1)}), bf16[8,64,512]{2,1,0:T(8,128)(2,1)S(1)}, u32[]{:S(2)}, u32[]{:S(2)}) async-start(bf16[8,64,512]{2,1,0:T(8,128)(2,1)} %bitcast.35), calls=%async_computation.1 | async-start | bytes 1048576 | tf_op jit(solution)/shard_map/all_to_all | solution.py:826
  178.1 1.4 high_sum.7
  179.5 0.7 collective-permute-start.40
  180.7 1.9 collective-permute-start.43
  182.6 4.1 %feedforward_sum.1 = (f32[8,32,2048]{2,1,0:T(8,128)}, f32[8,16,2048]{2,1,0:T(8,128)}, f32[8,2,16,2048]{3,2,1,0:T(8,128)}, f32[8,16,2048]{2,1,0:T(8,128)}) custom-call(s32[4]{0:T(128)S(1)} %pad_add_fusion.info.refs_0_, s32[8]{0:T(128)S(1)} %copy-done.50, bf16[2,192,512]{2,1,0:T(8,128)(2,1)S(1)} %copy-done.12, bf16[2,192,512]{2,1,0:T(8,128)(2,1)S(1)} %copy-done.28, ...), custom_call_target="tpu_custom_call" | custom-call | bytes 12000000 | tf_op jit(solution)/shard_map/feedforward_sum/pallas_call | solution.py:655
  186.8 6.6 %collective-permute-done.40.refs_1_ = bf16[512,512]{1,0:T(8,128)(2,1)S(1)} collective-permute-done((bf16[512,512]{1,0:T(8,128)(2,1)S(1)}, bf16[512,512]{1,0:T(8,128)(2,1)S(1)}, u32[]{:S(2)}, u32[]{:S(2)}) %collective-permute-start.40) | collective-permute-done | bytes 524320 | tf_op jit(solution)/shard_map/ppermute | solution.py:671
  193.4 2.2 %output.1 = bf16[512,512]{1,0:T(8,128)(2,1)} custom-call(s32[4]{0:T(128)S(1)} %pad_add_fusion.info.refs_0_, bf16[512,512]{1,0:T(8,128)(2,1)S(1)} %collective-permute-done.40.refs_1_, f32[256,1024]{1,0:T(8,128)S(1)} %get-tuple-element.211.refs_0_.refs_2_, bf16[256,1024]{1,0:T(8,128)(2,1)} %collective-permute-done.38.refs_1_.refs_3_, ...), custom_call_target="tpu_custom_call" | custom-call | flops 1000 | bytes 1000 | tf_op jit(solution)/shard_map/output/pallas_call | solution.py:632
  195.6 5.6 %all-to-all-start.2 = ((bf16[8,64,512]{2,1,0:T(8,128)(2,1)}), bf16[8,64,512]{2,1,0:T(8,128)(2,1)S(1)}, u32[]{:S(2)}, u32[]{:S(2)}) async-start(bf16[8,64,512]{2,1,0:T(8,128)(2,1)} %bitcast.14), calls=%async_computation.2 | async-start | bytes 1048576 | tf_op jit(solution)/shard_map/all_to_all | solution.py:826
  201.3 0.7 collective-permute-start.46
  202.0 1.0 slice.35.refs_3_
  202.9 1.5 collective-permute-start.47
  204.4 6.2 %collective-permute-done.46.refs_6_ = bf16[4,64,512]{2,1,0:T(8,128)(2,1)S(1)} collective-permute-done((bf16[4,64,512]{2,1,0:T(8,128)(2,1)S(1)}, bf16[4,64,512]{2,1,0:T(8,128)(2,1)S(1)}, u32[]{:S(2)}, u32[]{:S(2)}) %collective-permute-start.46) | collective-permute-done | bytes 262176 | tf_op jit(solution)/shard_map/ppermute | solution.py:671
  211.1 2.7 %collective-permute-done.47.refs_7_ = bf16[4,64,512]{2,1,0:T(8,128)(2,1)S(1)} collective-permute-done((bf16[4,64,512]{2,1,0:T(8,128)(2,1)S(1)}, bf16[4,64,512]{2,1,0:T(8,128)(2,1)S(1)}, u32[]{:S(2)}, u32[]{:S(2)}) %collective-permute-start.47) | collective-permute-done | bytes 262176 | tf_op jit(solution)/shard_map/ppermute | solution.py:671
  213.8 1.4 collect_grad.1
  215.4 4.6 %attention_sum.1 = (f32[8,48,2048]{2,1,0:T(8,128)}, f32[8,16,2048]{2,1,0:T(8,128)}, f32[8,16,512]{2,1,0:T(8,128)}, f32[8,2,16,128]{3,2,1,0:T(8,128)}, f32[8,16,512]{2,1,0:T(8,128)}) custom-call(s32[4]{0:T(128)S(1)} %pad_add_fusion.info.refs_0_, s32[8]{0:T(128)S(1)} %copy-done.50, bf16[4,112,512]{2,1,0:T(8,128)(2,1)S(1)} %constant_dynamic-update-slice_fusion.refs_14_.refs_0_, ...), custom_call_target="tpu_custom_call" | custom-call | bytes 12000000 | tf_op jit(solution)/shard_map/attention_sum/pallas_call | solution.py:655
  220.0 1.4 collect_out.1
  (210 shorter events, 15.1 us)
Async XLA Ops:
  3.9 23.0 %all-to-all-start = ((bf16[8,64,512]{2,1,0:T(8,128)(2,1)}), bf16[8,64,512]{2,1,0:T(8,128)(2,1)S(1)}, u32[]{:S(2)}, u32[]{:S(2)}) async-start(bf16[8,64,512]{2,1,0:T(8,128)(2,1)} %deal.1), calls=%async_computation | async-start | bytes 1048576 | tf_op jit(solution)/shard_map/all_to_all | solution.py:750
  11.2 8.2 %collective-permute-start = (bf16[2,512]{1,0:T(2,128)(2,1)S(1)}, bf16[2,512]{1,0:T(2,128)(2,1)S(1)}, u32[]{:S(2)}, u32[]{:S(2)}) collective-permute-start(bf16[2,512]{1,0:T(2,128)(2,1)S(1)} %pad_maximum_fusion.4), channel_id=1, source_target_pairs={{0,1},{1,0},{2,3},{3,2},{4,5},{5,4},{6,7},{7,6},{8,9},{9,8},{10,11... | collective-permute-start | bytes 6152 | tf_op jit(solution)/shard_map/ppermute | solution.py:671
  11.3 3.7 %collective-permute-start.1 = (bf16[2,512]{1,0:T(2,128)(2,1)S(1)}, bf16[2,512]{1,0:T(2,128)(2,1)S(1)}, u32[]{:S(2)}, u32[]{:S(2)}) collective-permute-start(bf16[2,512]{1,0:T(2,128)(2,1)S(1)} %pad_maximum_fusion.4), channel_id=1, source_target_pairs={{0,2},{1,3},{2,0},{3,1},{4,6},{5,7},{6,4},{7,5},{8,10},{9,11},{10,... | collective-permute-start | bytes 6152 | tf_op jit(solution)/shard_map/ppermute | solution.py:671
  12.9 14.0 %collective-permute-start.3 = (bf16[512,512]{1,0:T(8,128)(2,1)S(1)}, bf16[512,512]{1,0:T(8,128)(2,1)S(1)}, u32[]{:S(2)}, u32[]{:S(2)}) collective-permute-start(bf16[512,512]{1,0:T(8,128)(2,1)S(1)} %bitcast.29), channel_id=1, source_target_pairs={{0,2},{1,3},{2,0},{3,1},{4,6},{5,7},{6,4},{7,5},{8,10},{9,11},{10,... | collective-permute-start | bytes 1572872 | tf_op jit(solution)/shard_map/ppermute | solution.py:671
  14.9 4.5 %collective-permute-start.2 = (bf16[2,512]{1,0:T(2,128)(2,1)S(1)}, bf16[2,512]{1,0:T(2,128)(2,1)S(1)}, u32[]{:S(2)}, u32[]{:S(2)}) collective-permute-start(bf16[2,512]{1,0:T(2,128)(2,1)S(1)} %collective-permute-done.1), channel_id=1, source_target_pairs={{0,1},{1,0},{2,3},{3,2},{4,5},{5,4},{6,7},{7,6},{8,9},{9,8},{10,11... | collective-permute-start | bytes 6152 | tf_op jit(solution)/shard_map/ppermute | solution.py:671
  16.3 19.8 %copy-start.37 = (f32[32,256]{1,0:T(8,128)S(1)}, f32[32,256]{1,0:T(8,128)}, u32[]{:S(2)}) copy-start(f32[32,256]{1,0:T(8,128)} %constant.21.clone.refs_12_.refs_22_) | copy-start | bytes 98308
  16.3 19.8 %copy-start.39 = (f32[32,256]{1,0:T(8,128)S(1)}, f32[32,256]{1,0:T(8,128)}, u32[]{:S(2)}) copy-start(f32[32,256]{1,0:T(8,128)} %constant.19.clone.refs_11_.refs_21_) | copy-start | bytes 98308
  19.4 28.2 %copy-start.33 = (bf16[16,512]{1,0:T(8,128)(2,1)}, bf16[16,512]{1,0:T(8,128)(2,1)S(1)}, u32[]{:S(2)}) copy-start(bf16[16,512]{1,0:T(8,128)(2,1)S(1)} %get-tuple-element.120.refs_9_.refs_17_) | copy-start | bytes 49156
  19.4 28.2 %copy-start.41 = (bf16[2,16,128]{2,1,0:T(8,128)(2,1)}, bf16[2,16,128]{2,1,0:T(8,128)(2,1)S(1)}, u32[]{:S(2)}) copy-start(bf16[2,16,128]{2,1,0:T(8,128)(2,1)S(1)} %get-tuple-element.121.refs_10_.refs_18_) | copy-start | bytes 24580
  19.4 32.3 %copy-start.15 = (bf16[16,2048]{1,0:T(8,128)(2,1)}, bf16[16,2048]{1,0:T(8,128)(2,1)S(1)}, u32[]{:S(2)}) copy-start(bf16[16,2048]{1,0:T(8,128)(2,1)S(1)} %get-tuple-element.124.refs_4_.refs_20_) | copy-start | bytes 196612
  19.4 32.3 %copy-start.31 = (bf16[16,512]{1,0:T(8,128)(2,1)}, bf16[16,512]{1,0:T(8,128)(2,1)S(1)}, u32[]{:S(2)}) copy-start(bf16[16,512]{1,0:T(8,128)(2,1)S(1)} %get-tuple-element.123.refs_3_.refs_19_) | copy-start | bytes 49156
  26.9 7.6 %collective-permute-start.5 = (bf16[256,512]{1,0:T(8,128)(2,1)S(1)}, bf16[256,512]{1,0:T(8,128)(2,1)S(1)}, u32[]{:S(2)}, u32[]{:S(2)}) collective-permute-start(bf16[256,512]{1,0:T(8,128)(2,1)S(1)} %get-tuple-element.228), channel_id=1, source_target_pairs={{0,2},{1,3},{2,0},{3,1},{4,6},{5,7},{6,4},{7,5},{8,10},{9,11},{10,... | collective-permute-start | bytes 786440 | tf_op jit(solution)/shard_map/ppermute | solution.py:671
  27.5 8.6 %collective-permute-start.4 = (bf16[512,512]{1,0:T(8,128)(2,1)S(1)}, bf16[512,512]{1,0:T(8,128)(2,1)S(1)}, u32[]{:S(2)}, u32[]{:S(2)}) collective-permute-start(bf16[512,512]{1,0:T(8,128)(2,1)S(1)} %bitcast.21), channel_id=1, source_target_pairs={{0,1},{1,0},{2,3},{3,2},{4,5},{5,4},{6,7},{7,6},{8,9},{9,8},{10,11... | collective-permute-start | bytes 1572872 | tf_op jit(solution)/shard_map/ppermute | solution.py:671
  34.5 29.1 %copy-start.4 = (bf16[256,512]{1,0:T(8,128)(2,1)}, bf16[256,512]{1,0:T(8,128)(2,1)S(1)}, u32[]{:S(2)}) copy-start(bf16[256,512]{1,0:T(8,128)(2,1)S(1)} %collective-permute-done.5.refs_5_.refs_6_) | copy-start | bytes 786436
  34.5 1.5 collective-permute-start.6
  34.5 8.8 %collective-permute-start.9 = (bf16[256,512]{1,0:T(8,128)(2,1)S(1)}, bf16[256,512]{1,0:T(8,128)(2,1)S(1)}, u32[]{:S(2)}, u32[]{:S(2)}) collective-permute-start(bf16[256,512]{1,0:T(8,128)(2,1)S(1)} %get-tuple-element.227), channel_id=1, source_target_pairs={{0,2},{1,3},{2,0},{3,1},{4,6},{5,7},{6,4},{7,5},{8,10},{9,11},{10,... | collective-permute-start | bytes 786440 | tf_op jit(solution)/shard_map/ppermute | solution.py:671
  36.0 27.6 %copy-start.6 = (bf16[256,512]{1,0:T(8,128)(2,1)}, bf16[256,512]{1,0:T(8,128)(2,1)S(1)}, u32[]{:S(2)}) copy-start(bf16[256,512]{1,0:T(8,128)(2,1)S(1)} %collective-permute-done.6.refs_6_.refs_7_) | copy-start | bytes 786436
  43.3 2.0 collective-permute-start.10
  45.4 14.0 %collective-permute-start.11 = (bf16[256,1024]{1,0:T(8,128)(2,1)S(1)}, bf16[256,1024]{1,0:T(8,128)(2,1)S(1)}, u32[]{:S(2)}, u32[]{:S(2)}) collective-permute-start(bf16[256,1024]{1,0:T(8,128)(2,1)S(1)} %pair_sum.4.refs_0_.refs_14_), channel_id=1, source_target_pairs={{0,2},{1,3},{2,0},{3,1},{4,6},{5,7},{6,4},{7,5},{8,10},{9,11},{10,... | collective-permute-start | bytes 1572872 | tf_op jit(solution)/shard_map/ppermute | solution.py:671
  46.0 1.5 collective-permute-start.13
  59.4 1.9 collective-permute-start.14
  59.4 2.7 %collective-permute-start.7 = (bf16[512,512]{1,0:T(8,128)(2,1)S(1)}, bf16[512,512]{1,0:T(8,128)(2,1)S(1)}, u32[]{:S(2)}, u32[]{:S(2)}) collective-permute-start(bf16[512,512]{1,0:T(8,128)(2,1)S(1)} %bitcast.30), channel_id=1, source_target_pairs={{0,1},{1,0},{2,3},{3,2},{4,5},{5,4},{6,7},{7,6},{8,9},{9,8},{10,11... | collective-permute-start | bytes 1572872 | tf_op jit(solution)/shard_map/ppermute | solution.py:671
  60.0 2.9 %collective-permute-start.8 = (bf16[512,512]{1,0:T(8,128)(2,1)S(1)}, bf16[512,512]{1,0:T(8,128)(2,1)S(1)}, u32[]{:S(2)}, u32[]{:S(2)}) collective-permute-start(bf16[512,512]{1,0:T(8,128)(2,1)S(1)} %collective-permute-done.3.refs_11_.refs_10_), channel_id=1, source_target_pairs={{0,1},{1,0},{2,3},{3,2},{4,5},{5,4},{6,7},{7,6},{8,9},{9,8},{10,11... | collective-permute-start | bytes 1572872 | tf_op jit(solution)/shard_map/ppermute | solution.py:671
  60.1 3.5 %collective-permute-start.12 = (bf16[256,1024]{1,0:T(8,128)(2,1)S(1)}, bf16[256,1024]{1,0:T(8,128)(2,1)S(1)}, u32[]{:S(2)}, u32[]{:S(2)}) collective-permute-start(bf16[256,1024]{1,0:T(8,128)(2,1)S(1)} %far_sum.4.refs_7_), channel_id=1, source_target_pairs={{0,1},{1,0},{2,3},{3,2},{4,5},{5,4},{6,7},{7,6},{8,9},{9,8},{10,11... | collective-permute-start | bytes 1572872 | tf_op jit(solution)/shard_map/ppermute | solution.py:671
  61.5 16.1 %collective-permute-start.15 = (bf16[256,1024]{1,0:T(8,128)(2,1)S(1)}, bf16[256,1024]{1,0:T(8,128)(2,1)S(1)}, u32[]{:S(2)}, u32[]{:S(2)}) collective-permute-start(bf16[256,1024]{1,0:T(8,128)(2,1)S(1)} %pair_sum.5.refs_19_.refs_0_), channel_id=1, source_target_pairs={{0,2},{1,3},{2,0},{3,1},{4,6},{5,7},{6,4},{7,5},{8,10},{9,11},{10,... | collective-permute-start | bytes 1572872 | tf_op jit(solution)/shard_map/ppermute | solution.py:671
  77.5 27.8 %copy-start.2 = (bf16[256,2048]{1,0:T(8,128)(2,1)}, bf16[256,2048]{1,0:T(8,128)(2,1)S(1)}, u32[]{:S(2)}) copy-start(bf16[256,2048]{1,0:T(8,128)(2,1)S(1)} %get-tuple-element.149.refs_4_.refs_2_) | copy-start | bytes 3145732
  77.7 2.0 collective-permute-start.16
  99.7 1.9 collective-permute-start.17
  101.7 14.0 %collective-permute-start.19 = (bf16[256,1024]{1,0:T(8,128)(2,1)S(1)}, bf16[256,1024]{1,0:T(8,128)(2,1)S(1)}, u32[]{:S(2)}, u32[]{:S(2)}) collective-permute-start(bf16[256,1024]{1,0:T(8,128)(2,1)S(1)} %pair_sum.6.refs_11_.refs_0_), channel_id=1, source_target_pairs={{0,2},{1,3},{2,0},{3,1},{4,6},{5,7},{6,4},{7,5},{8,10},{9,11},{10,... | collective-permute-start | bytes 1572872 | tf_op jit(solution)/shard_map/ppermute | solution.py:671
  102.4 12.0 %collective-permute-start.18 = (bf16[1,192,512]{2,1,0:T(8,128)(2,1)S(1)}, bf16[1,192,512]{2,1,0:T(8,128)(2,1)S(1)}, u32[]{:S(2)}, u32[]{:S(2)}) collective-permute-start(bf16[1,192,512]{2,1,0:T(8,128)(2,1)S(1)} %bitcast.36), channel_id=1, source_target_pairs={{0,16},{4,20},{8,24},{12,28},{16,0},{20,4},{24,8},{28,12},{1,17},{... | collective-permute-start | bytes 589832 | tf_op jit(solution)/shard_map/ppermute | solution.py:671
  115.8 2.1 collective-permute-start.20
  115.9 6.3 %collective-permute-start.22 = (bf16[256,1024]{1,0:T(8,128)(2,1)S(1)}, bf16[256,1024]{1,0:T(8,128)(2,1)S(1)}, u32[]{:S(2)}, u32[]{:S(2)}) collective-permute-start(bf16[256,1024]{1,0:T(8,128)(2,1)S(1)} %far_sum.6.refs_13_), channel_id=1, source_target_pairs={{0,1},{1,0},{2,3},{3,2},{4,5},{5,4},{6,7},{7,6},{8,9},{9,8},{10,11... | collective-permute-start | bytes 1572872 | tf_op jit(solution)/shard_map/ppermute | solution.py:671
  117.9 16.1 %collective-permute-start.21 = (bf16[304,1024]{1,0:T(8,128)(2,1)S(1)}, bf16[304,1024]{1,0:T(8,128)(2,1)S(1)}, u32[]{:S(2)}, u32[]{:S(2)}) collective-permute-start(bf16[304,1024]{1,0:T(8,128)(2,1)S(1)} %pair_sum.7.refs_34_.refs_0_), channel_id=1, source_target_pairs={{0,2},{1,3},{2,0},{3,1},{4,6},{5,7},{6,4},{7,5},{8,10},{9,11},{10,... | collective-permute-start | bytes 1867784 | tf_op jit(solution)/shard_map/ppermute | solution.py:671
  118.6 14.2 %collective-permute-start.25 = (bf16[2,192,512]{2,1,0:T(8,128)(2,1)S(1)}, bf16[2,192,512]{2,1,0:T(8,128)(2,1)S(1)}, u32[]{:S(2)}, u32[]{:S(2)}) collective-permute-start(bf16[2,192,512]{2,1,0:T(8,128)(2,1)S(1)} %pad_maximum_fusion.refs_0_), channel_id=1, source_target_pairs={{0,4},{4,0},{8,12},{12,8},{16,20},{20,16},{24,28},{28,24},{1,5},{5... | collective-permute-start | bytes 1179656 | tf_op jit(solution)/shard_map/ppermute | solution.py:671
  120.7 12.2 %collective-permute-start.24 = (bf16[2,192,512]{2,1,0:T(8,128)(2,1)S(1)}, bf16[2,192,512]{2,1,0:T(8,128)(2,1)S(1)}, u32[]{:S(2)}, u32[]{:S(2)}) collective-permute-start(bf16[2,192,512]{2,1,0:T(8,128)(2,1)S(1)} %pad_maximum_fusion.refs_0_), channel_id=1, source_target_pairs={{0,8},{4,12},{8,0},{12,4},{16,24},{20,28},{24,16},{28,20},{1,9},{5... | collective-permute-start | bytes 1179656 | tf_op jit(solution)/shard_map/ppermute | solution.py:671
  132.9 3.4 %collective-permute-start.26 = (bf16[256,1024]{1,0:T(8,128)(2,1)S(1)}, bf16[256,1024]{1,0:T(8,128)(2,1)S(1)}, u32[]{:S(2)}, u32[]{:S(2)}) collective-permute-start(bf16[256,1024]{1,0:T(8,128)(2,1)S(1)} %get-tuple-element.191), channel_id=1, source_target_pairs={{0,1},{1,0},{2,3},{3,2},{4,5},{5,4},{6,7},{7,6},{8,9},{9,8},{10,11... | collective-permute-start | bytes 1572872 | tf_op jit(solution)/shard_map/ppermute | solution.py:671
  134.2 5.3 %collective-permute-start.23 = (bf16[304,1024]{1,0:T(8,128)(2,1)S(1)}, bf16[304,1024]{1,0:T(8,128)(2,1)S(1)}, u32[]{:S(2)}, u32[]{:S(2)}) collective-permute-start(bf16[304,1024]{1,0:T(8,128)(2,1)S(1)} %far_sum.7.refs_13_), channel_id=1, source_target_pairs={{0,1},{1,0},{2,3},{3,2},{4,5},{5,4},{6,7},{7,6},{8,9},{9,8},{10,11... | collective-permute-start | bytes 1867784 | tf_op jit(solution)/shard_map/ppermute | solution.py:671
  134.3 15.4 %collective-permute-start.29 = (bf16[2,192,512]{2,1,0:T(8,128)(2,1)S(1)}, bf16[2,192,512]{2,1,0:T(8,128)(2,1)S(1)}, u32[]{:S(2)}, u32[]{:S(2)}) collective-permute-start(bf16[2,192,512]{2,1,0:T(8,128)(2,1)S(1)} %collective-permute-done.24.refs_1_), channel_id=1, source_target_pairs={{0,4},{4,0},{8,12},{12,8},{16,20},{20,16},{24,28},{28,24},{1,5},{5... | collective-permute-start | bytes 1179656 | tf_op jit(solution)/shard_map/ppermute | solution.py:671
  136.4 13.2 %collective-permute-start.28 = (bf16[256,512]{1,0:T(8,128)(2,1)S(1)}, bf16[256,512]{1,0:T(8,128)(2,1)S(1)}, u32[]{:S(2)}, u32[]{:S(2)}) collective-permute-start(bf16[256,512]{1,0:T(8,128)(2,1)S(1)} %high_sum.4.refs_36_), channel_id=1, source_target_pairs={{0,2},{1,3},{2,0},{3,1},{4,6},{5,7},{6,4},{7,5},{8,10},{9,11},{10,... | collective-permute-start | bytes 786440 | tf_op jit(solution)/shard_map/ppermute | solution.py:671
  137.1 12.5 %collective-permute-start.27 = (bf16[1,48,1024]{2,1,0:T(8,128)(2,1)S(1)}, bf16[1,48,1024]{2,1,0:T(8,128)(2,1)S(1)}, u32[]{:S(2)}, u32[]{:S(2)}) collective-permute-start(bf16[1,48,1024]{2,1,0:T(8,128)(2,1)S(1)} %slice_bitcast_fusion), channel_id=1, source_target_pairs={{0,16},{4,20},{8,24},{12,28},{16,0},{20,4},{24,8},{28,12},{1,17},{... | collective-permute-start | bytes 294920 | tf_op jit(solution)/shard_map/ppermute | solution.py:671
  139.5 22.3 %slice-start = ((s8[8388608]{0:T(1024)(128)(4,1)}), s8[4194304]{0:T(1024)(128)(4,1)S(1)}, s32[]{:S(2)}) async-start(s8[8388608]{0:T(1024)(128)(4,1)} %bitcast.18), calls=%async_computation.3 | async-start | bytes 8388608
  139.6 22.2 %slice-start.1 = ((s8[8388608]{0:T(1024)(128)(4,1)}), s8[4194304]{0:T(1024)(128)(4,1)S(1)}, s32[]{:S(2)}) async-start(s8[8388608]{0:T(1024)(128)(4,1)} %bitcast.18), calls=%async_computation.4 | async-start | bytes 8388608
  149.7 5.2 %collective-permute-start.32 = (bf16[256,1024]{1,0:T(8,128)(2,1)S(1)}, bf16[256,1024]{1,0:T(8,128)(2,1)S(1)}, u32[]{:S(2)}, u32[]{:S(2)}) collective-permute-start(bf16[256,1024]{1,0:T(8,128)(2,1)S(1)} %get-tuple-element.198), channel_id=1, source_target_pairs={{0,1},{1,0},{2,3},{3,2},{4,5},{5,4},{6,7},{7,6},{8,9},{9,8},{10,11... | collective-permute-start | bytes 1572872 | tf_op jit(solution)/shard_map/ppermute | solution.py:671
  149.8 2.2 collective-permute-start.30
  151.9 4.9 %collective-permute-start.31 = (bf16[96,512]{1,0:T(8,128)(2,1)S(1)}, bf16[96,512]{1,0:T(8,128)(2,1)S(1)}, u32[]{:S(2)}, u32[]{:S(2)}) collective-permute-start(bf16[96,512]{1,0:T(8,128)(2,1)S(1)} %high_sum.5.refs_2_), channel_id=1, source_target_pairs={{0,2},{1,3},{2,0},{3,1},{4,6},{5,7},{6,4},{7,5},{8,10},{9,11},{10,... | collective-permute-start | bytes 294920 | tf_op jit(solution)/shard_map/ppermute | solution.py:671
  153.4 7.7 %collective-permute-start.36 = (bf16[2,48,1024]{2,1,0:T(8,128)(2,1)S(1)}, bf16[2,48,1024]{2,1,0:T(8,128)(2,1)S(1)}, u32[]{:S(2)}, u32[]{:S(2)}) collective-permute-start(bf16[2,48,1024]{2,1,0:T(8,128)(2,1)S(1)} %pad_maximum_fusion.2), channel_id=1, source_target_pairs={{0,8},{4,12},{8,0},{12,4},{16,24},{20,28},{24,16},{28,20},{1,9},{5... | collective-permute-start | bytes 589832 | tf_op jit(solution)/shard_map/ppermute | solution.py:671
  155.0 11.4 %collective-permute-start.33 = (bf16[256,512]{1,0:T(8,128)(2,1)S(1)}, bf16[256,512]{1,0:T(8,128)(2,1)S(1)}, u32[]{:S(2)}, u32[]{:S(2)}) collective-permute-start(bf16[256,512]{1,0:T(8,128)(2,1)S(1)} %high_sum.6), channel_id=1, source_target_pairs={{0,2},{1,3},{2,0},{3,1},{4,6},{5,7},{6,4},{7,5},{8,10},{9,11},{10,... | collective-permute-start | bytes 786440 | tf_op jit(solution)/shard_map/ppermute | solution.py:671
  156.9 9.5 %collective-permute-start.34 = (bf16[1,112,512]{2,1,0:T(8,128)(2,1)S(1)}, bf16[1,112,512]{2,1,0:T(8,128)(2,1)S(1)}, u32[]{:S(2)}, u32[]{:S(2)}) collective-permute-start(bf16[1,112,512]{2,1,0:T(8,128)(2,1)S(1)} %maximum_bitcast_fusion.refs_6_), channel_id=1, source_target_pairs={{0,16},{4,20},{8,24},{12,28},{16,0},{20,4},{24,8},{28,12},{1,17},{... | collective-permute-start | bytes 344072 | tf_op jit(solution)/shard_map/ppermute | solution.py:671
  161.1 12.0 %collective-permute-start.37 = (bf16[4,48,1024]{2,1,0:T(8,128)(2,1)S(1)}, bf16[4,48,1024]{2,1,0:T(8,128)(2,1)S(1)}, u32[]{:S(2)}, u32[]{:S(2)}) collective-permute-start(bf16[4,48,1024]{2,1,0:T(8,128)(2,1)S(1)} %constant_dynamic-update-slice_fusion.2.refs_4_), channel_id=1, source_target_pairs={{0,4},{4,0},{8,12},{12,8},{16,20},{20,16},{24,28},{28,24},{1,5},{5... | collective-permute-start | bytes 1179656 | tf_op jit(solution)/shard_map/ppermute | solution.py:671
  166.4 6.6 %collective-permute-start.35 = (bf16[2,112,512]{2,1,0:T(8,128)(2,1)S(1)}, bf16[2,112,512]{2,1,0:T(8,128)(2,1)S(1)}, u32[]{:S(2)}, u32[]{:S(2)}) collective-permute-start(bf16[2,112,512]{2,1,0:T(8,128)(2,1)S(1)} %pad_maximum_fusion.1.refs_6_), channel_id=1, source_target_pairs={{0,8},{4,12},{8,0},{12,4},{16,24},{20,28},{24,16},{28,20},{1,9},{5... | collective-permute-start | bytes 688136 | tf_op jit(solution)/shard_map/ppermute | solution.py:671
  168.0 10.0 %collective-permute-start.38 = (bf16[256,1024]{1,0:T(8,128)(2,1)}, bf16[256,1024]{1,0:T(8,128)(2,1)}, u32[]{:S(2)}, u32[]{:S(2)}) collective-permute-start(bf16[256,1024]{1,0:T(8,128)(2,1)} %get-tuple-element.204.refs_7_), channel_id=1, source_target_pairs={{0,1},{1,0},{2,3},{3,2},{4,5},{5,4},{6,7},{7,6},{8,9},{9,8},{10,11... | collective-permute-start | bytes 1572872 | tf_op jit(solution)/shard_map/ppermute | solution.py:671
  172.5 5.5 %collective-permute-start.39 = (bf16[256,1024]{1,0:T(8,128)(2,1)}, bf16[256,1024]{1,0:T(8,128)(2,1)}, u32[]{:S(2)}, u32[]{:S(2)}) collective-permute-start(bf16[256,1024]{1,0:T(8,128)(2,1)} %get-tuple-element.209.refs_16_), channel_id=1, source_target_pairs={{0,1},{1,0},{2,3},{3,2},{4,5},{5,4},{6,7},{7,6},{8,9},{9,8},{10,11... | collective-permute-start | bytes 1572872 | tf_op jit(solution)/shard_map/ppermute | solution.py:671
  174.5 21.1 %all-to-all-start.1 = ((bf16[8,64,512]{2,1,0:T(8,128)(2,1)}), bf16[8,64,512]{2,1,0:T(8,128)(2,1)S(1)}, u32[]{:S(2)}, u32[]{:S(2)}) async-start(bf16[8,64,512]{2,1,0:T(8,128)(2,1)} %bitcast.35), calls=%async_computation.1 | async-start | bytes 1048576 | tf_op jit(solution)/shard_map/all_to_all | solution.py:826
  179.5 13.9 %collective-permute-start.40 = (bf16[512,512]{1,0:T(8,128)(2,1)S(1)}, bf16[512,512]{1,0:T(8,128)(2,1)S(1)}, u32[]{:S(2)}, u32[]{:S(2)}) collective-permute-start(bf16[512,512]{1,0:T(8,128)(2,1)S(1)} %high_sum.7), channel_id=1, source_target_pairs={{0,2},{1,3},{2,0},{3,1},{4,6},{5,7},{6,4},{7,5},{8,10},{9,11},{10,... | collective-permute-start | bytes 1572872 | tf_op jit(solution)/shard_map/ppermute | solution.py:671
  180.2 2.4 %collective-permute-start.41 = (bf16[4,48,1024]{2,1,0:T(8,128)(2,1)S(1)}, bf16[4,48,1024]{2,1,0:T(8,128)(2,1)S(1)}, u32[]{:S(2)}, u32[]{:S(2)}) collective-permute-start(bf16[4,48,1024]{2,1,0:T(8,128)(2,1)S(1)} %copy-done.22), channel_id=1, source_target_pairs={{0,1},{1,0},{2,3},{3,2},{4,5},{5,4},{6,7},{7,6},{8,9},{9,8},{10,11... | collective-permute-start | bytes 1179656 | tf_op jit(solution)/shard_map/ppermute | solution.py:671
  180.2 2.4 %collective-permute-start.42 = (bf16[4,48,1024]{2,1,0:T(8,128)(2,1)S(1)}, bf16[4,48,1024]{2,1,0:T(8,128)(2,1)S(1)}, u32[]{:S(2)}, u32[]{:S(2)}) collective-permute-start(bf16[4,48,1024]{2,1,0:T(8,128)(2,1)S(1)} %collective-permute-done.37.refs_15_.refs_5_), channel_id=1, source_target_pairs={{0,1},{1,0},{2,3},{3,2},{4,5},{5,4},{6,7},{7,6},{8,9},{9,8},{10,11... | collective-permute-start | bytes 1179656 | tf_op jit(solution)/shard_map/ppermute | solution.py:671
  180.7 21.3 %collective-permute-start.43 = (bf16[4,112,512]{2,1,0:T(8,128)(2,1)S(1)}, bf16[4,112,512]{2,1,0:T(8,128)(2,1)}, u32[]{:S(2)}, u32[]{:S(2)}) collective-permute-start(bf16[4,112,512]{2,1,0:T(8,128)(2,1)S(1)} %constant_dynamic-update-slice_fusion.refs_14_.refs_0_), channel_id=1, source_target_pairs={{0,4},{4,0},{8,12},{12,8},{16,20},{20,16},{24,28},{28,24},{1,5},{5... | collective-permute-start | bytes 1376264 | tf_op jit(solution)/shard_map/ppermute | solution.py:671
  195.6 24.4 %all-to-all-start.2 = ((bf16[8,64,512]{2,1,0:T(8,128)(2,1)}), bf16[8,64,512]{2,1,0:T(8,128)(2,1)S(1)}, u32[]{:S(2)}, u32[]{:S(2)}) async-start(bf16[8,64,512]{2,1,0:T(8,128)(2,1)} %bitcast.14), calls=%async_computation.2 | async-start | bytes 1048576 | tf_op jit(solution)/shard_map/all_to_all | solution.py:826
  201.3 9.3 %collective-permute-start.46 = (bf16[4,64,512]{2,1,0:T(8,128)(2,1)S(1)}, bf16[4,64,512]{2,1,0:T(8,128)(2,1)S(1)}, u32[]{:S(2)}, u32[]{:S(2)}) collective-permute-start(bf16[4,64,512]{2,1,0:T(8,128)(2,1)S(1)} %slice.34.refs_2_), channel_id=1, source_target_pairs={{0,2},{1,3},{2,0},{3,1},{4,6},{5,7},{6,4},{7,5},{8,10},{9,11},{10,... | collective-permute-start | bytes 786440 | tf_op jit(solution)/shard_map/ppermute | solution.py:671
  202.9 10.9 %collective-permute-start.47 = (bf16[4,64,512]{2,1,0:T(8,128)(2,1)S(1)}, bf16[4,64,512]{2,1,0:T(8,128)(2,1)S(1)}, u32[]{:S(2)}, u32[]{:S(2)}) collective-permute-start(bf16[4,64,512]{2,1,0:T(8,128)(2,1)S(1)} %slice.35.refs_3_), channel_id=1, source_target_pairs={{0,2},{1,3},{2,0},{3,1},{4,6},{5,7},{6,4},{7,5},{8,10},{9,11},{10,... | collective-permute-start | bytes 786440 | tf_op jit(solution)/shard_map/ppermute | solution.py:671
  204.4 10.8 %collective-permute-start.44 = (bf16[4,64,512]{2,1,0:T(8,128)(2,1)S(1)}, bf16[4,64,512]{2,1,0:T(8,128)(2,1)S(1)}, u32[]{:S(2)}, u32[]{:S(2)}) collective-permute-start(bf16[4,64,512]{2,1,0:T(8,128)(2,1)S(1)} %slice.34.refs_2_), channel_id=1, source_target_pairs={{0,1},{1,0},{2,3},{3,2},{4,5},{5,4},{6,7},{7,6},{8,9},{9,8},{10,11... | collective-permute-start | bytes 786440 | tf_op jit(solution)/shard_map/ppermute | solution.py:671
  210.6 4.7 %collective-permute-start.48 = (bf16[4,64,512]{2,1,0:T(8,128)(2,1)S(1)}, bf16[4,64,512]{2,1,0:T(8,128)(2,1)S(1)}, u32[]{:S(2)}, u32[]{:S(2)}) collective-permute-start(bf16[4,64,512]{2,1,0:T(8,128)(2,1)S(1)} %collective-permute-done.46.refs_6_), channel_id=1, source_target_pairs={{0,1},{1,0},{2,3},{3,2},{4,5},{5,4},{6,7},{7,6},{8,9},{9,8},{10,11... | collective-permute-start | bytes 786440 | tf_op jit(solution)/shard_map/ppermute | solution.py:671
  210.6 4.7 %collective-permute-start.45 = (bf16[4,64,512]{2,1,0:T(8,128)(2,1)S(1)}, bf16[4,64,512]{2,1,0:T(8,128)(2,1)S(1)}, u32[]{:S(2)}, u32[]{:S(2)}) collective-permute-start(bf16[4,64,512]{2,1,0:T(8,128)(2,1)S(1)} %slice.35.refs_3_), channel_id=1, source_target_pairs={{0,1},{1,0},{2,3},{3,2},{4,5},{5,4},{6,7},{7,6},{8,9},{9,8},{10,11... | collective-permute-start | bytes 786440 | tf_op jit(solution)/shard_map/ppermute | solution.py:671
  213.8 1.5 collective-permute-start.49
  (46 other events, 333.7 us)

commit v12 on v10

--- a/solution.py
+++ b/solution.py
@@ -874,18 +874,18 @@
     att = jnp.concatenate([att_b, att_a], axis=0)[None]
     y_keep[0], y_send = down(0, td_0, (att,))
     y_got[0] = near(y_send)
-    att = doubled(att, bits[0], dp)
+    att = first = doubled(att, bits[0], dp)
     att = late(att, h_far, y_send)
     for bit in bits[1:-1]:
         att = doubled(att, bit, dp)
-    fa = late(jnp.concatenate([fa, fa_first], axis=0), aa_high)
+    fa = late(jnp.concatenate([fa, fa_first], axis=0), aa_high, y_send)
     for bit in bits[1:-1]:
         fa = doubled(fa, bit, dp)
     fa_side = swap(fa, bits[-1], "dp", dp)
-    y_far = far(high_sum(*((k, late(g, h_far)) for k, g in zip(y_keep, y_got))))
 
     dinput, = call(finish_kernel, None, (), (gains, dealt, aa_high, aa_far, *(v for f in final for v in f)),
-                   [((length, QUARTER), BF16)], [], "finish", 8, (att, fa_side))
+                   [((length, QUARTER), BF16)], [], "finish", 8, (first, y_send))
+    y_far = far(high_sum(*((k, late(g, dinput)) for k, g in zip(y_keep, y_got))))
     input_grad = collect(to_bands(dinput), "collect_grad")
     outs = [sds((adapters, 2 * RANK, WIDTH), F32), sds((adapters, RANK, WIDTH), F32),
             sds((adapters, 2, RANK, units), F32), sds((adapters, RANK, units), F32)]

time: 220 us -> 228 us (1.036)
  waiting for transfers between devices: 54.5 us -> 61.5 us
  local copies, waits for them, and re-layouts: 5.3 us -> 10.2 us
    ppermute x50, waiting for transfers between devices: 54.5 us -> 61.5 us  [swap(): return lax.ppermute(value, axis, [(i, i ^ bit) for i in range(size)])]
    pallas_call x26, Pallas kernels: 90.7 us -> 87.9 us  [call(): pl.pallas_call(body, in_specs=[pl.BlockSpec(memory_space=pltpu.SMEM)] * n...]
    unnamed x150 -> x148, local copies, waits for them, and re-layouts: 4.24 us -> 6.62 us
  transfers between devices with their start and end apart: 53 -> 53, of which waited for: 24 -> 22; matrix products, arithmetic and copies ran while one was open for 2% -> 4% of each run, Pallas kernels for 41% -> 39%
where the time goes in v12:
time: 228 us
  Pallas kernels  104 us (46%)
  waiting for transfers between devices  61.5 us (27%)
  starting transfers between devices  46.8 us (21%)
  local copies, waits for them, and re-layouts  10.2 us (4%)
  other arithmetic  2.98 us (1%)
    pallas_call x26, Pallas kernels, call(): pl.pallas_call(body, in_specs=[pl.BlockSpec(memory_space=pltpu.SMEM)] * n...  87.9 us
    ppermute x50, waiting for transfers between devices, swap(): return lax.ppermute(value, axis, [(i, i ^ bit) for i in range(size)])  61.5 us
    ppermute x50, starting transfers between devices, swap(): return lax.ppermute(value, axis, [(i, i ^ bit) for i in range(size)])  29.7 us
    all_to_all x2, starting transfers between devices, to_bands(): lax.all_to_all(value.reshape(dp, length // dp, QUARTER), 'dp', split_axis...  9.85 us
    pallas_call x2, Pallas kernels, sum_call(): pl.pallas_call(functools.partial(kernel, [len(group) for group in groups]...  8.89 us
    all_to_all x1, starting transfers between devices, shards(): lax.all_to_all(ordered, 'dp', split_axis=0, concat_axis=1, tiled=True)[0]  7.26 us
    unnamed x148, local copies, waits for them, and re-layouts  6.62 us
    pallas_call x3, Pallas kernels, move_rows(): pl.pallas_call(kernel, in_specs=[pl.BlockSpec(memory_space=pltpu.SMEM), p...  5.76 us
  transfers between devices with their start and end apart: 53, of which 22 were waited for; matrix products, arithmetic and copies ran while one was open for 4% of the time, Pallas kernels for 39%

profile of v12, /device:TPU:0, one launch (start us, length us, event | category | flops | bytes accessed | tf_op | source)
XLA Modules:
  0.0 227.8 jit_solution(2442789062592606080)
XLA Ops:
  0.7 0.7 copy-done.63
  1.4 2.5 %deal.1 = bf16[8,64,512]{2,1,0:T(8,128)(2,1)} custom-call(s32[8]{0:T(128)S(1)} %copy-done.63, bf16[8,64,512]{2,1,0:T(8,128)(2,1)} %source.1), custom_call_target="tpu_custom_call" | custom-call | flops 1000 | bytes 1000 | tf_op jit(solution)/shard_map/deal/pallas_call | solution.py:599
  3.9 7.3 %all-to-all-start = ((bf16[8,64,512]{2,1,0:T(8,128)(2,1)}), bf16[8,64,512]{2,1,0:T(8,128)(2,1)S(1)}, u32[]{:S(2)}, u32[]{:S(2)}) async-start(bf16[8,64,512]{2,1,0:T(8,128)(2,1)} %deal.1), calls=%async_computation | async-start | bytes 1048576 | tf_op jit(solution)/shard_map/all_to_all | solution.py:750
  11.3 1.6 collective-permute-start.1
  14.2 0.7 collective-permute-done.1
  14.9 1.4 pad_add_fusion.info.refs_0_
  16.3 1.8 adapters.1
  19.4 7.4 %collective-permute-done.3.refs_11_.refs_10_ = bf16[512,512]{1,0:T(8,128)(2,1)S(1)} collective-permute-done((bf16[512,512]{1,0:T(8,128)(2,1)S(1)}, bf16[512,512]{1,0:T(8,128)(2,1)S(1)}, u32[]{:S(2)}, u32[]{:S(2)}) %collective-permute-start.3) | collective-permute-done | bytes 524320 | tf_op jit(solution)/shard_map/ppermute | solution.py:671
  27.5 7.0 %collective-permute-done.5.refs_5_.refs_6_ = bf16[256,512]{1,0:T(8,128)(2,1)S(1)} collective-permute-done((bf16[256,512]{1,0:T(8,128)(2,1)S(1)}, bf16[256,512]{1,0:T(8,128)(2,1)S(1)}, u32[]{:S(2)}, u32[]{:S(2)}) %collective-permute-start.5) | collective-permute-done | bytes 262176 | tf_op jit(solution)/shard_map/ppermute | solution.py:671
  35.1 1.0 collective-permute-done.6.refs_6_.refs_7_
  36.1 4.1 %project_0.1 = (bf16[48,256]{1,0:T(8,128)(2,1)S(1)}, bf16[512,256]{1,0:T(8,128)(2,1)S(1)}, bf16[2,256,64]{2,1,0:T(8,128)(2,1)S(1)}, bf16[2,256,64]{2,1,0:T(8,128...) custom-call(s32[4]{0:T(128)S(1)} %pad_add_fusion.info.refs_0_, bf16[2048,512]{1,0:T(8,128)(2,1)} %refs_1_.15, ...), custom_call_target="tpu_custom_call" | custom-call | flops 1000 | bytes 1000 | tf_op jit(solution)/shard_map/project_0/pallas_call | solution.py:632
  40.2 3.1 %attend_0.1 = (f32[256,1024]{1,0:T(8,128)S(1)}, bf16[256,1024]{1,0:T(8,128)(2,1)S(1)}, bf16[512,256]{1,0:T(8,128)(2,1)S(1)}, f32[8,256]{1,0:T(8,128)S(1)}, bf16[16,256]{1,0:T(8,128)(2,1)S(1)}) custom-call(s32[4]{0:T(128)S(1)} %pad_add_fusion.info.refs_0_, bf16[512,2048]{1,0:T(8,128)(2,1)} %refs_3_.5, ...), custom_call_target="tpu_custom_call" | custom-call | flops 1000 | bytes 1000 | tf_op jit(solution)/shard_map/attend_0/pallas_call | solution.py:632
  43.5 1.8 collective-permute-done.10.refs_1_
  46.0 1.5 collective-permute-done.13.refs_6_.refs_7_
  47.6 4.1 %project_1.1 = (bf16[48,256]{1,0:T(8,128)(2,1)S(1)}, bf16[512,256]{1,0:T(8,128)(2,1)S(1)}, bf16[2,256,64]{2,1,0:T(8,128)(2,1)S(1)}, bf16[2,256,64]{2,1,0:T(8,128...) custom-call(s32[4]{0:T(128)S(1)} %pad_add_fusion.info.refs_0_, bf16[2048,512]{1,0:T(8,128)(2,1)} %refs_1_.15, ...), custom_call_target="tpu_custom_call" | custom-call | flops 1000 | bytes 1000 | tf_op jit(solution)/shard_map/project_1/pallas_call | solution.py:632
  51.8 3.7 %attend_1.1 = (f32[256,1024]{1,0:T(8,128)S(1)}, bf16[256,1024]{1,0:T(8,128)(2,1)S(1)}, bf16[512,256]{1,0:T(8,128)(2,1)S(1)}, f32[8,256]{1,0:T(8,128)S(1)}, bf16[16,256]{1,0:T(8,128)(2,1)S(1)}) custom-call(s32[4]{0:T(128)S(1)} %pad_add_fusion.info.refs_0_, bf16[512,2048]{1,0:T(8,128)(2,1)} %refs_3_.5, ...), custom_call_target="tpu_custom_call" | custom-call | flops 1000 | bytes 1000 | tf_op jit(solution)/shard_map/attend_1/pallas_call | solution.py:632
  55.5 3.9 %collective-permute-done.11.refs_1_ = bf16[256,1024]{1,0:T(8,128)(2,1)S(1)} collective-permute-done((bf16[256,1024]{1,0:T(8,128)(2,1)S(1)}, bf16[256,1024]{1,0:T(8,128)(2,1)S(1)}, u32[]{:S(2)}, u32[]{:S(2)}) %collective-permute-start.11) | collective-permute-done | bytes 524320 | tf_op jit(solution)/shard_map/ppermute | solution.py:671
  62.2 0.7 collective-permute-done.8.refs_12_.refs_11_
  62.8 0.7 collective-permute-done.12.refs_8_
  63.6 13.0 %front_0.1 = (bf16[256,2048]{1,0:T(8,128)(2,1)S(1)}, f32[256,512]{1,0:T(8,128)S(1)}, bf16[256,2048]{1,0:T(8,128)(2,1)S(1)}, bf16[256,2048]{1,0:T(8,128)(2,1)S(1)...) custom-call(s32[4]{0:T(128)S(1)} %pad_add_fusion.info.refs_0_, ...), custom_call_target="tpu_custom_call" | custom-call | flops 1000 | bytes 1000 | tf_op jit(solution)/shard_map/front_0/pallas_call | solution.py:632
  76.6 1.0 copy-done.25
  77.9 1.8 collective-permute-done.16.refs_8_
  79.7 12.0 %front_1.1 = (bf16[256,2048]{1,0:T(8,128)(2,1)S(1)}, f32[256,512]{1,0:T(8,128)S(1)}, bf16[256,2048]{1,0:T(8,128)(2,1)S(1)}, bf16[256,2048]{1,0:T(8,128)(2,1)S(1)...) custom-call(s32[4]{0:T(128)S(1)} %pad_add_fusion.info.refs_0_, ...), custom_call_target="tpu_custom_call" | custom-call | flops 1000 | bytes 1000 | tf_op jit(solution)/shard_map/front_1/pallas_call | solution.py:632
  91.7 3.0 %collective-permute-start.17 = (bf16[1,192,512]{2,1,0:T(8,128)(2,1)S(1)}, bf16[1,192,512]{2,1,0:T(8,128)(2,1)S(1)}, u32[]{:S(2)}, u32[]{:S(2)}) collective-permute-start(bf16[1,192,512]{2,1,0:T(8,128)(2,1)S(1)} %bitcast.37), channel_id=1, source_target_pairs={{0,16},{4,20},{8,24},{12,28},{16,0},{20,4},{24,8},{28,12},{1,17},{... | collective-permute-start | bytes 589832 | tf_op jit(solution)/shard_map/ppermute | solution.py:671
  94.7 7.9 %back_1.1 = (f32[256,16]{1,0:T(8,128)S(1)}, f32[256,1024]{1,0:T(8,128)S(1)}, bf16[256,1024]{1,0:T(8,128)(2,1)S(1)}, f32[48,2048]{1,0:T(8,128)S(1)}) custom-call(s32[4]{0:T(128)S(1)} %pad_add_fusion.info.refs_0_, bf16[2,2048,2048]{2,1,0:T(8,128)(2,1)S(1)} %get-tuple-element.147.refs_1_, bf16[256,2048]{1,0:T(8,128)(2,1)S(1)} %get-tuple-element.157.refs_2_, ...), custom_call_target="tpu_custom_call" | custom-call | flops 1000 | bytes 1000 | tf_op jit(solution)/shard_map/back_1/pallas_call | solution.py:632
  102.6 1.5 collective-permute-done.17
  104.2 1.8 collective-permute-start.20
  107.2 7.9 %back_0.1 = (f32[256,16]{1,0:T(8,128)S(1)}, f32[304,1024]{1,0:T(8,128)S(1)}, bf16[304,1024]{1,0:T(8,128)(2,1)S(1)}) custom-call(s32[4]{0:T(128)S(1)} %pad_add_fusion.info.refs_0_, bf16[2,2048,2048]{2,1,0:T(8,128)(2,1)S(1)} %get-tuple-element.147.refs_1_, bf16[256,2048]{1,0:T(8,128)(2,1)S(1)} %get-tuple-element.148.refs_2_, ...), custom_call_target="tpu_custom_call" | custom-call | flops 1000 | bytes 1000 | tf_op jit(solution)/shard_map/back_0/pallas_call | solution.py:632
  115.1 0.7 collective-permute-done.20.refs_2_
  115.8 1.4 collective-permute-done.19.refs_1_
  117.3 4.5 %down_1.1 = (f32[256,1024]{1,0:T(8,128)S(1)}, bf16[256,1024]{1,0:T(8,128)(2,1)}) custom-call(s32[4]{0:T(128)S(1)} %pad_add_fusion.info.refs_0_, bf16[2048,2048]{1,0:T(8,128)(2,1)S(1)} %bitcast.19, bf16[256,2048]{1,0:T(8,128)(2,1)S(1)} %get-tuple-element.159.refs_4_.refs_2_, f32[256,16]{1,0:T(8,128)S(1)} %get-tuple-element.171.refs_3_, ...), custom_call_target="tpu_custom_call" | custom-call | flops 1000 | bytes 1000 | tf_op jit(solution)/shard_map/down_1/pallas_call | solution.py:632
  124.2 10.7 %attend_back_1.1 = (f32[256,512]{1,0:T(8,128)S(1)}, f32[256,1024]{1,0:T(8,128)S(1)}, bf16[256,1024]{1,0:T(8,128)(2,1)S(1)}, f32[256,1]{1,0:T(8,128)S(1)}, f32[48...) custom-call(s32[4]{0:T(128)S(1)} %pad_add_fusion.info.refs_0_, ...), custom_call_target="tpu_custom_call" | custom-call | flops 1000 | bytes 1000 | tf_op jit(solution)/shard_map/attend_back_1/pallas_call | solution.py:632
  135.5 3.8 %collective-permute-done.23.refs_1_ = bf16[304,1024]{1,0:T(8,128)(2,1)S(1)} collective-permute-done((bf16[304,1024]{1,0:T(8,128)(2,1)S(1)}, bf16[304,1024]{1,0:T(8,128)(2,1)S(1)}, u32[]{:S(2)}, u32[]{:S(2)}) %collective-permute-start.23) | collective-permute-done | bytes 622624 | tf_op jit(solution)/shard_map/ppermute | solution.py:671
  140.3 2.3 collective-permute-start.28
  142.6 9.8 %attend_back_0.1 = (f32[256,512]{1,0:T(8,128)S(1)}, f32[256,1024]{1,0:T(8,128)S(1)}, bf16[256,1024]{1,0:T(8,128)(2,1)S(1)}, f32[256,1]{1,0:T(8,128)S(1)}, bf16[4...) custom-call(s32[4]{0:T(128)S(1)} %pad_add_fusion.info.refs_0_, ...), custom_call_target="tpu_custom_call" | custom-call | flops 1000 | bytes 1000 | tf_op jit(solution)/shard_map/attend_back_0/pallas_call | solution.py:632
  153.1 1.7 collective-permute-done.30.refs_1_
  154.8 1.3 collective-permute-start.31
  156.2 0.8 collective-permute-start.33
  157.0 3.0 %collective-permute-done.31.refs_3_ = bf16[96,512]{1,0:T(8,128)(2,1)S(1)} collective-permute-done((bf16[96,512]{1,0:T(8,128)(2,1)S(1)}, bf16[96,512]{1,0:T(8,128)(2,1)S(1)}, u32[]{:S(2)}, u32[]{:S(2)}) %collective-permute-start.31) | collective-permute-done | bytes 98336 | tf_op jit(solution)/shard_map/ppermute | solution.py:671
  160.0 1.3 collective-permute-start.34
  161.4 0.7 pad_maximum_fusion.2
  162.1 4.5 %down_0.1 = (f32[256,1024]{1,0:T(8,128)S(1)}, bf16[256,1024]{1,0:T(8,128)(2,1)}) custom-call(s32[4]{0:T(128)S(1)} %pad_add_fusion.info.refs_0_, bf16[2048,2048]{1,0:T(8,128)(2,1)S(1)} %bitcast.19, bf16[256,2048]{1,0:T(8,128)(2,1)S(1)} %copy-done.5, f32[256,16]{1,0:T(8,128)S(1)} %get-tuple-element.173.refs_6_.refs_3_, ...), custom_call_target="tpu_custom_call" | custom-call | flops 1000 | bytes 1000 | tf_op jit(solution)/shard_map/down_0/pallas_call | solution.py:632
  166.6 2.0 collective-permute-start.38
  169.2 0.8 copy-done.17
  170.0 4.3 %all-to-all-start.1 = ((bf16[8,64,512]{2,1,0:T(8,128)(2,1)}), bf16[8,64,512]{2,1,0:T(8,128)(2,1)}, u32[]{:S(2)}, u32[]{:S(2)}) async-start(bf16[8,64,512]{2,1,0:T(8,128)(2,1)} %bitcast.36), calls=%async_computation.1 | async-start | bytes 1048576 | tf_op jit(solution)/shard_map/all_to_all | solution.py:826
  174.3 0.9 constant_dynamic-update-slice_fusion.1
  175.3 0.9 constant_dynamic-update-slice_fusion.refs_4_
  176.2 2.0 collective-permute-start.39
  178.8 1.5 collective-permute-start.42
  180.3 11.3 %collective-permute-done.39.refs_5_ = bf16[4,48,1024]{2,1,0:T(8,128)(2,1)S(1)} collective-permute-done((bf16[4,48,1024]{2,1,0:T(8,128)(2,1)S(1)}, bf16[4,48,1024]{2,1,0:T(8,128)(2,1)S(1)}, u32[]{:S(2)}, u32[]{:S(2)}) %collective-permute-start.39) | collective-permute-done | bytes 393248 | tf_op jit(solution)/shard_map/ppermute | solution.py:671
  191.6 0.7 constant_dynamic-update-slice_fusion.3
  192.3 0.7 constant_dynamic-update-slice_fusion.2.refs_0_
  193.4 4.1 %feedforward_sum.1 = (f32[8,32,2048]{2,1,0:T(8,128)}, f32[8,16,2048]{2,1,0:T(8,128)}, f32[8,2,16,2048]{3,2,1,0:T(8,128)}, f32[8,16,2048]{2,1,0:T(8,128)}) custom-call(s32[4]{0:T(128)S(1)} %pad_add_fusion.info.refs_0_, s32[8]{0:T(128)S(1)} %copy-done.66, bf16[2,192,512]{2,1,0:T(8,128)(2,1)S(1)} %copy-done.19, bf16[2,192,512]{2,1,0:T(8,128)(2,1)S(1)} %copy-done.40, ...), custom_call_target="tpu_custom_call" | custom-call | bytes 12000000 | tf_op jit(solution)/shard_map/feedforward_sum/pallas_call | solution.py:655
  197.6 0.8 output.1
  198.4 0.8 copy-done.16
  199.2 5.6 %all-to-all-start.2 = ((bf16[8,64,512]{2,1,0:T(8,128)(2,1)}), bf16[8,64,512]{2,1,0:T(8,128)(2,1)S(1)}, u32[]{:S(2)}, u32[]{:S(2)}) async-start(bf16[8,64,512]{2,1,0:T(8,128)(2,1)} %bitcast.35), calls=%async_computation.2 | async-start | bytes 1048576 | tf_op jit(solution)/shard_map/all_to_all | solution.py:826
  204.7 1.0 slice.34.refs_2_
  206.2 1.0 slice.35.refs_3_
  207.2 1.6 collective-permute-start.47
  208.8 6.1 %collective-permute-done.46.refs_6_ = bf16[4,64,512]{2,1,0:T(8,128)(2,1)S(1)} collective-permute-done((bf16[4,64,512]{2,1,0:T(8,128)(2,1)S(1)}, bf16[4,64,512]{2,1,0:T(8,128)(2,1)S(1)}, u32[]{:S(2)}, u32[]{:S(2)}) %collective-permute-start.46) | collective-permute-done | bytes 262176 | tf_op jit(solution)/shard_map/ppermute | solution.py:671
  215.5 4.1 %collective-permute-done.47.refs_7_ = bf16[4,64,512]{2,1,0:T(8,128)(2,1)S(1)} collective-permute-done((bf16[4,64,512]{2,1,0:T(8,128)(2,1)S(1)}, bf16[4,64,512]{2,1,0:T(8,128)(2,1)S(1)}, u32[]{:S(2)}, u32[]{:S(2)}) %collective-permute-start.47) | collective-permute-done | bytes 262176 | tf_op jit(solution)/shard_map/ppermute | solution.py:671
  219.5 1.9 collect_grad.1
  221.5 4.7 %attention_sum.1 = (f32[8,48,2048]{2,1,0:T(8,128)}, f32[8,16,2048]{2,1,0:T(8,128)}, f32[8,16,512]{2,1,0:T(8,128)}, f32[8,2,16,128]{3,2,1,0:T(8,128)}, f32[8,16,512]{2,1,0:T(8,128)}) custom-call(s32[4]{0:T(128)S(1)} %pad_add_fusion.info.refs_0_, s32[8]{0:T(128)S(1)} %copy-done.66, bf16[4,112,512]{2,1,0:T(8,128)(2,1)} %constant_dynamic-update-slice_fusion.2.refs_0_, ...), custom_call_target="tpu_custom_call" | custom-call | bytes 12000000 | tf_op jit(solution)/shard_map/attention_sum/pallas_call | solution.py:655
  226.2 1.4 collect_out.1
  (242 shorter events, 16.2 us)
Async XLA Ops:
  3.9 23.0 %all-to-all-start = ((bf16[8,64,512]{2,1,0:T(8,128)(2,1)}), bf16[8,64,512]{2,1,0:T(8,128)(2,1)S(1)}, u32[]{:S(2)}, u32[]{:S(2)}) async-start(bf16[8,64,512]{2,1,0:T(8,128)(2,1)} %deal.1), calls=%async_computation | async-start | bytes 1048576 | tf_op jit(solution)/shard_map/all_to_all | solution.py:750
  11.2 8.2 %collective-permute-start = (bf16[2,512]{1,0:T(2,128)(2,1)S(1)}, bf16[2,512]{1,0:T(2,128)(2,1)S(1)}, u32[]{:S(2)}, u32[]{:S(2)}) collective-permute-start(bf16[2,512]{1,0:T(2,128)(2,1)S(1)} %pad_maximum_fusion.4), channel_id=1, source_target_pairs={{0,1},{1,0},{2,3},{3,2},{4,5},{5,4},{6,7},{7,6},{8,9},{9,8},{10,11... | collective-permute-start | bytes 6152 | tf_op jit(solution)/shard_map/ppermute | solution.py:671
  11.3 3.7 %collective-permute-start.1 = (bf16[2,512]{1,0:T(2,128)(2,1)S(1)}, bf16[2,512]{1,0:T(2,128)(2,1)S(1)}, u32[]{:S(2)}, u32[]{:S(2)}) collective-permute-start(bf16[2,512]{1,0:T(2,128)(2,1)S(1)} %pad_maximum_fusion.4), channel_id=1, source_target_pairs={{0,2},{1,3},{2,0},{3,1},{4,6},{5,7},{6,4},{7,5},{8,10},{9,11},{10,... | collective-permute-start | bytes 6152 | tf_op jit(solution)/shard_map/ppermute | solution.py:671
  12.9 14.0 %collective-permute-start.3 = (bf16[512,512]{1,0:T(8,128)(2,1)S(1)}, bf16[512,512]{1,0:T(8,128)(2,1)S(1)}, u32[]{:S(2)}, u32[]{:S(2)}) collective-permute-start(bf16[512,512]{1,0:T(8,128)(2,1)S(1)} %bitcast.29), channel_id=1, source_target_pairs={{0,2},{1,3},{2,0},{3,1},{4,6},{5,7},{6,4},{7,5},{8,10},{9,11},{10,... | collective-permute-start | bytes 1572872 | tf_op jit(solution)/shard_map/ppermute | solution.py:671
  14.9 4.5 %collective-permute-start.2 = (bf16[2,512]{1,0:T(2,128)(2,1)S(1)}, bf16[2,512]{1,0:T(2,128)(2,1)S(1)}, u32[]{:S(2)}, u32[]{:S(2)}) collective-permute-start(bf16[2,512]{1,0:T(2,128)(2,1)S(1)} %collective-permute-done.1), channel_id=1, source_target_pairs={{0,1},{1,0},{2,3},{3,2},{4,5},{5,4},{6,7},{7,6},{8,9},{9,8},{10,11... | collective-permute-start | bytes 6152 | tf_op jit(solution)/shard_map/ppermute | solution.py:671
  16.3 19.8 %copy-start.53 = (f32[32,256]{1,0:T(8,128)S(1)}, f32[32,256]{1,0:T(8,128)}, u32[]{:S(2)}) copy-start(f32[32,256]{1,0:T(8,128)} %constant.21.clone.refs_12_.refs_22_) | copy-start | bytes 98308
  16.3 19.8 %copy-start.55 = (f32[32,256]{1,0:T(8,128)S(1)}, f32[32,256]{1,0:T(8,128)}, u32[]{:S(2)}) copy-start(f32[32,256]{1,0:T(8,128)} %constant.19.clone.refs_11_.refs_21_) | copy-start | bytes 98308
  19.4 28.2 %copy-start.49 = (bf16[16,512]{1,0:T(8,128)(2,1)}, bf16[16,512]{1,0:T(8,128)(2,1)S(1)}, u32[]{:S(2)}) copy-start(bf16[16,512]{1,0:T(8,128)(2,1)S(1)} %get-tuple-element.121.refs_9_.refs_17_) | copy-start | bytes 49156
  19.4 28.2 %copy-start.57 = (bf16[2,16,128]{2,1,0:T(8,128)(2,1)}, bf16[2,16,128]{2,1,0:T(8,128)(2,1)S(1)}, u32[]{:S(2)}) copy-start(bf16[2,16,128]{2,1,0:T(8,128)(2,1)S(1)} %get-tuple-element.122.refs_10_.refs_18_) | copy-start | bytes 24580
  19.4 32.3 %copy-start.23 = (bf16[16,2048]{1,0:T(8,128)(2,1)}, bf16[16,2048]{1,0:T(8,128)(2,1)S(1)}, u32[]{:S(2)}) copy-start(bf16[16,2048]{1,0:T(8,128)(2,1)S(1)} %get-tuple-element.125.refs_4_.refs_20_) | copy-start | bytes 196612
  19.4 32.3 %copy-start.43 = (bf16[16,512]{1,0:T(8,128)(2,1)}, bf16[16,512]{1,0:T(8,128)(2,1)S(1)}, u32[]{:S(2)}) copy-start(bf16[16,512]{1,0:T(8,128)(2,1)S(1)} %get-tuple-element.124.refs_3_.refs_19_) | copy-start | bytes 49156
  26.9 7.6 %collective-permute-start.5 = (bf16[256,512]{1,0:T(8,128)(2,1)S(1)}, bf16[256,512]{1,0:T(8,128)(2,1)S(1)}, u32[]{:S(2)}, u32[]{:S(2)}) collective-permute-start(bf16[256,512]{1,0:T(8,128)(2,1)S(1)} %get-tuple-element.230), channel_id=1, source_target_pairs={{0,2},{1,3},{2,0},{3,1},{4,6},{5,7},{6,4},{7,5},{8,10},{9,11},{10,... | collective-permute-start | bytes 786440 | tf_op jit(solution)/shard_map/ppermute | solution.py:671
  27.5 8.6 %collective-permute-start.4 = (bf16[512,512]{1,0:T(8,128)(2,1)S(1)}, bf16[512,512]{1,0:T(8,128)(2,1)S(1)}, u32[]{:S(2)}, u32[]{:S(2)}) collective-permute-start(bf16[512,512]{1,0:T(8,128)(2,1)S(1)} %bitcast.21), channel_id=1, source_target_pairs={{0,1},{1,0},{2,3},{3,2},{4,5},{5,4},{6,7},{7,6},{8,9},{9,8},{10,11... | collective-permute-start | bytes 1572872 | tf_op jit(solution)/shard_map/ppermute | solution.py:671
  34.5 29.1 %copy-start.8 = (bf16[256,512]{1,0:T(8,128)(2,1)}, bf16[256,512]{1,0:T(8,128)(2,1)S(1)}, u32[]{:S(2)}) copy-start(bf16[256,512]{1,0:T(8,128)(2,1)S(1)} %collective-permute-done.5.refs_5_.refs_6_) | copy-start | bytes 786436
  34.5 1.5 collective-permute-start.6
  34.5 8.8 %collective-permute-start.9 = (bf16[256,512]{1,0:T(8,128)(2,1)S(1)}, bf16[256,512]{1,0:T(8,128)(2,1)S(1)}, u32[]{:S(2)}, u32[]{:S(2)}) collective-permute-start(bf16[256,512]{1,0:T(8,128)(2,1)S(1)} %get-tuple-element.229), channel_id=1, source_target_pairs={{0,2},{1,3},{2,0},{3,1},{4,6},{5,7},{6,4},{7,5},{8,10},{9,11},{10,... | collective-permute-start | bytes 786440 | tf_op jit(solution)/shard_map/ppermute | solution.py:671
  36.0 27.6 %copy-start.10 = (bf16[256,512]{1,0:T(8,128)(2,1)}, bf16[256,512]{1,0:T(8,128)(2,1)S(1)}, u32[]{:S(2)}) copy-start(bf16[256,512]{1,0:T(8,128)(2,1)S(1)} %collective-permute-done.6.refs_6_.refs_7_) | copy-start | bytes 786436
  43.3 2.0 collective-permute-start.10
  45.4 14.0 %collective-permute-start.11 = (bf16[256,1024]{1,0:T(8,128)(2,1)S(1)}, bf16[256,1024]{1,0:T(8,128)(2,1)S(1)}, u32[]{:S(2)}, u32[]{:S(2)}) collective-permute-start(bf16[256,1024]{1,0:T(8,128)(2,1)S(1)} %pair_sum.4.refs_0_.refs_14_), channel_id=1, source_target_pairs={{0,2},{1,3},{2,0},{3,1},{4,6},{5,7},{6,4},{7,5},{8,10},{9,11},{10,... | collective-permute-start | bytes 1572872 | tf_op jit(solution)/shard_map/ppermute | solution.py:671
  46.0 1.5 collective-permute-start.13
  47.6 32.1 %copy-start.6 = (bf16[256,512]{1,0:T(8,128)(2,1)}, bf16[256,512]{1,0:T(8,128)(2,1)S(1)}, u32[]{:S(2)}) copy-start(bf16[256,512]{1,0:T(8,128)(2,1)S(1)} %collective-permute-done.13.refs_6_.refs_7_) | copy-start | bytes 786436
  55.5 21.1 %copy-start.47 = (bf16[512,256]{1,0:T(8,128)(2,1)}, bf16[512,256]{1,0:T(8,128)(2,1)S(1)}, u32[]{:S(2)}) copy-start(bf16[512,256]{1,0:T(8,128)(2,1)S(1)} %get-tuple-element.178.refs_25_) | copy-start | bytes 786436
  59.4 1.9 collective-permute-start.14
  59.4 2.7 %collective-permute-start.7 = (bf16[512,512]{1,0:T(8,128)(2,1)S(1)}, bf16[512,512]{1,0:T(8,128)(2,1)S(1)}, u32[]{:S(2)}, u32[]{:S(2)}) collective-permute-start(bf16[512,512]{1,0:T(8,128)(2,1)S(1)} %bitcast.30), channel_id=1, source_target_pairs={{0,1},{1,0},{2,3},{3,2},{4,5},{5,4},{6,7},{7,6},{8,9},{9,8},{10,11... | collective-permute-start | bytes 1572872 | tf_op jit(solution)/shard_map/ppermute | solution.py:671
  59.9 2.9 %collective-permute-start.8 = (bf16[512,512]{1,0:T(8,128)(2,1)S(1)}, bf16[512,512]{1,0:T(8,128)(2,1)S(1)}, u32[]{:S(2)}, u32[]{:S(2)}) collective-permute-start(bf16[512,512]{1,0:T(8,128)(2,1)S(1)} %collective-permute-done.3.refs_11_.refs_10_), channel_id=1, source_target_pairs={{0,1},{1,0},{2,3},{3,2},{4,5},{5,4},{6,7},{7,6},{8,9},{9,8},{10,11... | collective-permute-start | bytes 1572872 | tf_op jit(solution)/shard_map/ppermute | solution.py:671
  60.2 3.4 %collective-permute-start.12 = (bf16[256,1024]{1,0:T(8,128)(2,1)S(1)}, bf16[256,1024]{1,0:T(8,128)(2,1)S(1)}, u32[]{:S(2)}, u32[]{:S(2)}) collective-permute-start(bf16[256,1024]{1,0:T(8,128)(2,1)S(1)} %far_sum.4.refs_7_), channel_id=1, source_target_pairs={{0,1},{1,0},{2,3},{3,2},{4,5},{5,4},{6,7},{7,6},{8,9},{9,8},{10,11... | collective-permute-start | bytes 1572872 | tf_op jit(solution)/shard_map/ppermute | solution.py:671
  61.5 16.1 %collective-permute-start.15 = (bf16[256,1024]{1,0:T(8,128)(2,1)S(1)}, bf16[256,1024]{1,0:T(8,128)(2,1)S(1)}, u32[]{:S(2)}, u32[]{:S(2)}) collective-permute-start(bf16[256,1024]{1,0:T(8,128)(2,1)S(1)} %pair_sum.5.refs_19_.refs_0_), channel_id=1, source_target_pairs={{0,2},{1,3},{2,0},{3,1},{4,6},{5,7},{6,4},{7,5},{8,10},{9,11},{10,... | collective-permute-start | bytes 1572872 | tf_op jit(solution)/shard_map/ppermute | solution.py:671
  77.6 29.6 %copy-start.4 = (bf16[256,2048]{1,0:T(8,128)(2,1)}, bf16[256,2048]{1,0:T(8,128)(2,1)S(1)}, u32[]{:S(2)}) copy-start(bf16[256,2048]{1,0:T(8,128)(2,1)S(1)} %get-tuple-element.150.refs_4_.refs_2_) | copy-start | bytes 3145732
  77.7 2.0 collective-permute-start.16
  91.7 12.4 %collective-permute-start.17 = (bf16[1,192,512]{2,1,0:T(8,128)(2,1)S(1)}, bf16[1,192,512]{2,1,0:T(8,128)(2,1)S(1)}, u32[]{:S(2)}, u32[]{:S(2)}) collective-permute-start(bf16[1,192,512]{2,1,0:T(8,128)(2,1)S(1)} %bitcast.37), channel_id=1, source_target_pairs={{0,16},{4,20},{8,24},{12,28},{16,0},{20,4},{24,8},{28,12},{1,17},{... | collective-permute-start | bytes 589832 | tf_op jit(solution)/shard_map/ppermute | solution.py:671
  104.1 2.3 collective-permute-start.18
  104.2 11.6 %collective-permute-start.20 = (bf16[2,192,512]{2,1,0:T(8,128)(2,1)S(1)}, bf16[2,192,512]{2,1,0:T(8,128)(2,1)S(1)}, u32[]{:S(2)}, u32[]{:S(2)}) collective-permute-start(bf16[2,192,512]{2,1,0:T(8,128)(2,1)S(1)} %pad_maximum_fusion.refs_0_), channel_id=1, source_target_pairs={{0,4},{4,0},{8,12},{12,8},{16,20},{20,16},{24,28},{28,24},{1,5},{5... | collective-permute-start | bytes 1179656 | tf_op jit(solution)/shard_map/ppermute | solution.py:671
  106.0 11.2 %collective-permute-start.19 = (bf16[2,192,512]{2,1,0:T(8,128)(2,1)S(1)}, bf16[2,192,512]{2,1,0:T(8,128)(2,1)S(1)}, u32[]{:S(2)}, u32[]{:S(2)}) collective-permute-start(bf16[2,192,512]{2,1,0:T(8,128)(2,1)S(1)} %pad_maximum_fusion.refs_0_), channel_id=1, source_target_pairs={{0,8},{4,12},{8,0},{12,4},{16,24},{20,28},{24,16},{28,20},{1,9},{5... | collective-permute-start | bytes 1179656 | tf_op jit(solution)/shard_map/ppermute | solution.py:671
  106.5 15.4 %collective-permute-start.22 = (bf16[256,1024]{1,0:T(8,128)(2,1)S(1)}, bf16[256,1024]{1,0:T(8,128)(2,1)S(1)}, u32[]{:S(2)}, u32[]{:S(2)}) collective-permute-start(bf16[256,1024]{1,0:T(8,128)(2,1)S(1)} %pair_sum.6.refs_11_.refs_0_), channel_id=1, source_target_pairs={{0,2},{1,3},{2,0},{3,1},{4,6},{5,7},{6,4},{7,5},{8,10},{9,11},{10,... | collective-permute-start | bytes 1572872 | tf_op jit(solution)/shard_map/ppermute | solution.py:671
  117.2 5.4 %collective-permute-start.21 = (bf16[304,1024]{1,0:T(8,128)(2,1)S(1)}, bf16[304,1024]{1,0:T(8,128)(2,1)S(1)}, u32[]{:S(2)}, u32[]{:S(2)}) collective-permute-start(bf16[304,1024]{1,0:T(8,128)(2,1)S(1)} %get-tuple-element.170), channel_id=1, source_target_pairs={{0,1},{1,0},{2,3},{3,2},{4,5},{5,4},{6,7},{7,6},{8,9},{9,8},{10,11... | collective-permute-start | bytes 1867784 | tf_op jit(solution)/shard_map/ppermute | solution.py:671
  122.1 2.1 collective-permute-start.24
  122.9 16.5 %collective-permute-start.23 = (bf16[304,1024]{1,0:T(8,128)(2,1)S(1)}, bf16[304,1024]{1,0:T(8,128)(2,1)S(1)}, u32[]{:S(2)}, u32[]{:S(2)}) collective-permute-start(bf16[304,1024]{1,0:T(8,128)(2,1)S(1)} %pair_sum.7.refs_34_.refs_0_), channel_id=1, source_target_pairs={{0,2},{1,3},{2,0},{3,1},{4,6},{5,7},{6,4},{7,5},{8,10},{9,11},{10,... | collective-permute-start | bytes 1867784 | tf_op jit(solution)/shard_map/ppermute | solution.py:671
  123.5 11.5 %collective-permute-start.26 = (bf16[2,192,512]{2,1,0:T(8,128)(2,1)S(1)}, bf16[2,192,512]{2,1,0:T(8,128)(2,1)S(1)}, u32[]{:S(2)}, u32[]{:S(2)}) collective-permute-start(bf16[2,192,512]{2,1,0:T(8,128)(2,1)S(1)} %collective-permute-done.19.refs_1_), channel_id=1, source_target_pairs={{0,4},{4,0},{8,12},{12,8},{16,20},{20,16},{24,28},{28,24},{1,5},{5... | collective-permute-start | bytes 1179656 | tf_op jit(solution)/shard_map/ppermute | solution.py:671
  135.1 4.5 %collective-permute-start.27 = (bf16[256,1024]{1,0:T(8,128)(2,1)S(1)}, bf16[256,1024]{1,0:T(8,128)(2,1)S(1)}, u32[]{:S(2)}, u32[]{:S(2)}) collective-permute-start(bf16[256,1024]{1,0:T(8,128)(2,1)S(1)} %get-tuple-element.195), channel_id=1, source_target_pairs={{0,1},{1,0},{2,3},{3,2},{4,5},{5,4},{6,7},{7,6},{8,9},{9,8},{10,11... | collective-permute-start | bytes 1572872 | tf_op jit(solution)/shard_map/ppermute | solution.py:671
  139.5 3.1 %collective-permute-start.25 = (bf16[304,1024]{1,0:T(8,128)(2,1)S(1)}, bf16[304,1024]{1,0:T(8,128)(2,1)S(1)}, u32[]{:S(2)}, u32[]{:S(2)}) collective-permute-start(bf16[304,1024]{1,0:T(8,128)(2,1)S(1)} %far_sum.7.refs_13_), channel_id=1, source_target_pairs={{0,1},{1,0},{2,3},{3,2},{4,5},{5,4},{6,7},{7,6},{8,9},{9,8},{10,11... | collective-permute-start | bytes 1867784 | tf_op jit(solution)/shard_map/ppermute | solution.py:671
  139.7 12.8 %collective-permute-start.29 = (bf16[256,512]{1,0:T(8,128)(2,1)S(1)}, bf16[256,512]{1,0:T(8,128)(2,1)S(1)}, u32[]{:S(2)}, u32[]{:S(2)}) collective-permute-start(bf16[256,512]{1,0:T(8,128)(2,1)S(1)} %high_sum.4.refs_36_), channel_id=1, source_target_pairs={{0,2},{1,3},{2,0},{3,1},{4,6},{5,7},{6,4},{7,5},{8,10},{9,11},{10,... | collective-permute-start | bytes 786440 | tf_op jit(solution)/shard_map/ppermute | solution.py:671
  140.3 12.1 %collective-permute-start.28 = (bf16[1,48,1024]{2,1,0:T(8,128)(2,1)S(1)}, bf16[1,48,1024]{2,1,0:T(8,128)(2,1)S(1)}, u32[]{:S(2)}, u32[]{:S(2)}) collective-permute-start(bf16[1,48,1024]{2,1,0:T(8,128)(2,1)S(1)} %slice_bitcast_fusion), channel_id=1, source_target_pairs={{0,16},{4,20},{8,24},{12,28},{16,0},{20,4},{24,8},{28,12},{1,17},{... | collective-permute-start | bytes 294920 | tf_op jit(solution)/shard_map/ppermute | solution.py:671
  152.5 3.6 %collective-permute-start.32 = (bf16[256,1024]{1,0:T(8,128)(2,1)S(1)}, bf16[256,1024]{1,0:T(8,128)(2,1)S(1)}, u32[]{:S(2)}, u32[]{:S(2)}) collective-permute-start(bf16[256,1024]{1,0:T(8,128)(2,1)S(1)} %get-tuple-element.202), channel_id=1, source_target_pairs={{0,1},{1,0},{2,3},{3,2},{4,5},{5,4},{6,7},{7,6},{8,9},{9,8},{10,11... | collective-permute-start | bytes 1572872 | tf_op jit(solution)/shard_map/ppermute | solution.py:671
  152.6 2.2 collective-permute-start.30
  154.8 5.2 %collective-permute-start.31 = (bf16[96,512]{1,0:T(8,128)(2,1)S(1)}, bf16[96,512]{1,0:T(8,128)(2,1)S(1)}, u32[]{:S(2)}, u32[]{:S(2)}) collective-permute-start(bf16[96,512]{1,0:T(8,128)(2,1)S(1)} %high_sum.5.refs_2_), channel_id=1, source_target_pairs={{0,2},{1,3},{2,0},{3,1},{4,6},{5,7},{6,4},{7,5},{8,10},{9,11},{10,... | collective-permute-start | bytes 294920 | tf_op jit(solution)/shard_map/ppermute | solution.py:671
  156.1 22.1 %collective-permute-start.36 = (bf16[256,1024]{1,0:T(8,128)(2,1)}, bf16[256,1024]{1,0:T(8,128)(2,1)S(1)}, u32[]{:S(2)}, u32[]{:S(2)}) collective-permute-start(bf16[256,1024]{1,0:T(8,128)(2,1)} %get-tuple-element.213.refs_35_), channel_id=1, source_target_pairs={{0,1},{1,0},{2,3},{3,2},{4,5},{5,4},{6,7},{7,6},{8,9},{9,8},{10,11... | collective-permute-start | bytes 1572872 | tf_op jit(solution)/shard_map/ppermute | solution.py:671
  156.2 12.5 %collective-permute-start.33 = (bf16[256,512]{1,0:T(8,128)(2,1)S(1)}, bf16[256,512]{1,0:T(8,128)(2,1)S(1)}, u32[]{:S(2)}, u32[]{:S(2)}) collective-permute-start(bf16[256,512]{1,0:T(8,128)(2,1)S(1)} %high_sum.6), channel_id=1, source_target_pairs={{0,2},{1,3},{2,0},{3,1},{4,6},{5,7},{6,4},{7,5},{8,10},{9,11},{10,... | collective-permute-start | bytes 786440 | tf_op jit(solution)/shard_map/ppermute | solution.py:671
  160.0 8.6 %collective-permute-start.34 = (bf16[1,112,512]{2,1,0:T(8,128)(2,1)S(1)}, bf16[1,112,512]{2,1,0:T(8,128)(2,1)S(1)}, u32[]{:S(2)}, u32[]{:S(2)}) collective-permute-start(bf16[1,112,512]{2,1,0:T(8,128)(2,1)S(1)} %maximum_bitcast_fusion.refs_6_), channel_id=1, source_target_pairs={{0,16},{4,20},{8,24},{12,28},{16,0},{20,4},{24,8},{28,12},{1,17},{... | collective-permute-start | bytes 344072 | tf_op jit(solution)/shard_map/ppermute | solution.py:671
  166.6 11.6 %collective-permute-start.35 = (bf16[256,1024]{1,0:T(8,128)(2,1)}, bf16[256,1024]{1,0:T(8,128)(2,1)S(1)}, u32[]{:S(2)}, u32[]{:S(2)}) collective-permute-start(bf16[256,1024]{1,0:T(8,128)(2,1)} %get-tuple-element.208.refs_15_), channel_id=1, source_target_pairs={{0,1},{1,0},{2,3},{3,2},{4,5},{5,4},{6,7},{7,6},{8,9},{9,8},{10,11... | collective-permute-start | bytes 1572872 | tf_op jit(solution)/shard_map/ppermute | solution.py:671
  166.6 8.7 %collective-permute-start.38 = (bf16[2,48,1024]{2,1,0:T(8,128)(2,1)}, bf16[2,48,1024]{2,1,0:T(8,128)(2,1)}, u32[]{:S(2)}, u32[]{:S(2)}) collective-permute-start(bf16[2,48,1024]{2,1,0:T(8,128)(2,1)} %pad_maximum_fusion.2), channel_id=1, source_target_pairs={{0,8},{4,12},{8,0},{12,4},{16,24},{20,28},{24,16},{28,20},{1,9},{5... | collective-permute-start | bytes 589832 | tf_op jit(solution)/shard_map/ppermute | solution.py:671
  170.0 29.1 %all-to-all-start.1 = ((bf16[8,64,512]{2,1,0:T(8,128)(2,1)}), bf16[8,64,512]{2,1,0:T(8,128)(2,1)}, u32[]{:S(2)}, u32[]{:S(2)}) async-start(bf16[8,64,512]{2,1,0:T(8,128)(2,1)} %bitcast.36), calls=%async_computation.1 | async-start | bytes 1048576 | tf_op jit(solution)/shard_map/all_to_all | solution.py:826
  176.2 15.4 %collective-permute-start.39 = (bf16[4,48,1024]{2,1,0:T(8,128)(2,1)S(1)}, bf16[4,48,1024]{2,1,0:T(8,128)(2,1)S(1)}, u32[]{:S(2)}, u32[]{:S(2)}) collective-permute-start(bf16[4,48,1024]{2,1,0:T(8,128)(2,1)S(1)} %constant_dynamic-update-slice_fusion.refs_4_), channel_id=1, source_target_pairs={{0,4},{4,0},{8,12},{12,8},{16,20},{20,16},{24,28},{28,24},{1,5},{5... | collective-permute-start | bytes 1179656 | tf_op jit(solution)/shard_map/ppermute | solution.py:671
  178.3 19.3 %collective-permute-start.37 = (bf16[512,512]{1,0:T(8,128)(2,1)S(1)}, bf16[512,512]{1,0:T(8,128)(2,1)S(1)}, u32[]{:S(2)}, u32[]{:S(2)}) collective-permute-start(bf16[512,512]{1,0:T(8,128)(2,1)S(1)} %high_sum.7), channel_id=1, source_target_pairs={{0,2},{1,3},{2,0},{3,1},{4,6},{5,7},{6,4},{7,5},{8,10},{9,11},{10,... | collective-permute-start | bytes 1572872 | tf_op jit(solution)/shard_map/ppermute | solution.py:671
  178.8 13.5 %collective-permute-start.42 = (bf16[2,112,512]{2,1,0:T(8,128)(2,1)S(1)}, bf16[2,112,512]{2,1,0:T(8,128)(2,1)S(1)}, u32[]{:S(2)}, u32[]{:S(2)}) collective-permute-start(bf16[2,112,512]{2,1,0:T(8,128)(2,1)S(1)} %pad_maximum_fusion.1.refs_14_), channel_id=1, source_target_pairs={{0,8},{4,12},{8,0},{12,4},{16,24},{20,28},{24,16},{28,20},{1,9},{5... | collective-permute-start | bytes 688136 | tf_op jit(solution)/shard_map/ppermute | solution.py:671
  180.3 13.1 %collective-permute-start.40 = (bf16[4,48,1024]{2,1,0:T(8,128)(2,1)S(1)}, bf16[4,48,1024]{2,1,0:T(8,128)(2,1)S(1)}, u32[]{:S(2)}, u32[]{:S(2)}) collective-permute-start(bf16[4,48,1024]{2,1,0:T(8,128)(2,1)S(1)} %constant_dynamic-update-slice_fusion.refs_4_), channel_id=1, source_target_pairs={{0,1},{1,0},{2,3},{3,2},{4,5},{5,4},{6,7},{7,6},{8,9},{9,8},{10,11... | collective-permute-start | bytes 1179656 | tf_op jit(solution)/shard_map/ppermute | solution.py:671
  191.6 1.8 collective-permute-start.41
  193.0 13.2 %collective-permute-start.43 = (bf16[4,112,512]{2,1,0:T(8,128)(2,1)}, bf16[4,112,512]{2,1,0:T(8,128)(2,1)}, u32[]{:S(2)}, u32[]{:S(2)}) collective-permute-start(bf16[4,112,512]{2,1,0:T(8,128)(2,1)} %constant_dynamic-update-slice_fusion.2.refs_0_), channel_id=1, source_target_pairs={{0,4},{4,0},{8,12},{12,8},{16,20},{20,16},{24,28},{28,24},{1,5},{5... | collective-permute-start | bytes 1376264 | tf_op jit(solution)/shard_map/ppermute | solution.py:671
  199.2 27.1 %all-to-all-start.2 = ((bf16[8,64,512]{2,1,0:T(8,128)(2,1)}), bf16[8,64,512]{2,1,0:T(8,128)(2,1)S(1)}, u32[]{:S(2)}, u32[]{:S(2)}) async-start(bf16[8,64,512]{2,1,0:T(8,128)(2,1)} %bitcast.35), calls=%async_computation.2 | async-start | bytes 1048576 | tf_op jit(solution)/shard_map/all_to_all | solution.py:826
  205.7 9.2 %collective-permute-start.46 = (bf16[4,64,512]{2,1,0:T(8,128)(2,1)S(1)}, bf16[4,64,512]{2,1,0:T(8,128)(2,1)S(1)}, u32[]{:S(2)}, u32[]{:S(2)}) collective-permute-start(bf16[4,64,512]{2,1,0:T(8,128)(2,1)S(1)} %slice.34.refs_2_), channel_id=1, source_target_pairs={{0,2},{1,3},{2,0},{3,1},{4,6},{5,7},{6,4},{7,5},{8,10},{9,11},{10,... | collective-permute-start | bytes 786440 | tf_op jit(solution)/shard_map/ppermute | solution.py:671
  207.2 12.3 %collective-permute-start.47 = (bf16[4,64,512]{2,1,0:T(8,128)(2,1)S(1)}, bf16[4,64,512]{2,1,0:T(8,128)(2,1)S(1)}, u32[]{:S(2)}, u32[]{:S(2)}) collective-permute-start(bf16[4,64,512]{2,1,0:T(8,128)(2,1)S(1)} %slice.35.refs_3_), channel_id=1, source_target_pairs={{0,2},{1,3},{2,0},{3,1},{4,6},{5,7},{6,4},{7,5},{8,10},{9,11},{10,... | collective-permute-start | bytes 786440 | tf_op jit(solution)/shard_map/ppermute | solution.py:671
  208.8 12.6 %collective-permute-start.44 = (bf16[4,64,512]{2,1,0:T(8,128)(2,1)S(1)}, bf16[4,64,512]{2,1,0:T(8,128)(2,1)S(1)}, u32[]{:S(2)}, u32[]{:S(2)}) collective-permute-start(bf16[4,64,512]{2,1,0:T(8,128)(2,1)S(1)} %slice.34.refs_2_), channel_id=1, source_target_pairs={{0,1},{1,0},{2,3},{3,2},{4,5},{5,4},{6,7},{7,6},{8,9},{9,8},{10,11... | collective-permute-start | bytes 786440 | tf_op jit(solution)/shard_map/ppermute | solution.py:671
  214.9 6.5 %collective-permute-start.48 = (bf16[4,64,512]{2,1,0:T(8,128)(2,1)S(1)}, bf16[4,64,512]{2,1,0:T(8,128)(2,1)S(1)}, u32[]{:S(2)}, u32[]{:S(2)}) collective-permute-start(bf16[4,64,512]{2,1,0:T(8,128)(2,1)S(1)} %collective-permute-done.46.refs_6_), channel_id=1, source_target_pairs={{0,1},{1,0},{2,3},{3,2},{4,5},{5,4},{6,7},{7,6},{8,9},{9,8},{10,11... | collective-permute-start | bytes 786440 | tf_op jit(solution)/shard_map/ppermute | solution.py:671
  214.9 6.5 %collective-permute-start.45 = (bf16[4,64,512]{2,1,0:T(8,128)(2,1)S(1)}, bf16[4,64,512]{2,1,0:T(8,128)(2,1)S(1)}, u32[]{:S(2)}, u32[]{:S(2)}) collective-permute-start(bf16[4,64,512]{2,1,0:T(8,128)(2,1)S(1)} %slice.35.refs_3_), channel_id=1, source_target_pairs={{0,1},{1,0},{2,3},{3,2},{4,5},{5,4},{6,7},{7,6},{8,9},{9,8},{10,11... | collective-permute-start | bytes 786440 | tf_op jit(solution)/shard_map/ppermute | solution.py:671
  219.5 1.9 collective-permute-start.49
  (62 other events, 452.1 us)

commit v13 on v12

--- a/solution.py
+++ b/solution.py
@@ -878,13 +878,13 @@
     att = late(att, h_far, y_send)
     for bit in bits[1:-1]:
         att = doubled(att, bit, dp)
-    fa = late(jnp.concatenate([fa, fa_first], axis=0), aa_high, y_send)
+    fa = late(jnp.concatenate([fa, fa_first], axis=0), aa_high)
     for bit in bits[1:-1]:
         fa = doubled(fa, bit, dp)
     fa_side = swap(fa, bits[-1], "dp", dp)
 
     dinput, = call(finish_kernel, None, (), (gains, dealt, aa_high, aa_far, *(v for f in final for v in f)),
-                   [((length, QUARTER), BF16)], [], "finish", 8, (first, y_send))
+                   [((length, QUARTER), BF16)], [], "finish", 8, (first, y_send, fa_side))
     y_far = far(high_sum(*((k, late(g, dinput)) for k, g in zip(y_keep, y_got))))
     input_grad = collect(to_bands(dinput), "collect_grad")
     outs = [sds((adapters, 2 * RANK, WIDTH), F32), sds((adapters, RANK, WIDTH), F32),

time: 228 us -> 227 us (level)
    all_to_all x2, starting transfers between devices: 9.85 us -> 7.27 us  [to_bands(): lax.all_to_all(value.reshape(dp, length // dp, QUARTER), 'dp', split_axis...]
    pallas_call x26, Pallas kernels: 87.9 us -> 90.4 us  [call(): pl.pallas_call(body, in_specs=[pl.BlockSpec(memory_space=pltpu.SMEM)] * n...]
    unnamed x148 -> x158, local copies, waits for them, and re-layouts: 6.62 us -> 5.72 us
  transfers between devices with their start and end apart: 53 -> 53, of which waited for: 22 -> 24; matrix products, arithmetic and copies ran while one was open for 4% -> 3% of each run, Pallas kernels for 39% -> 40%
where the time goes in v13:
time: 227 us
  Pallas kernels  106 us (47%)
  waiting for transfers between devices  61.8 us (27%)
  starting transfers between devices  46.1 us (20%)
  local copies, waits for them, and re-layouts  8.43 us (4%)
  other arithmetic  2.31 us (1%)
    pallas_call x26, Pallas kernels, call(): pl.pallas_call(body, in_specs=[pl.BlockSpec(memory_space=pltpu.SMEM)] * n...  90.4 us
    ppermute x50, waiting for transfers between devices, swap(): return lax.ppermute(value, axis, [(i, i ^ bit) for i in range(size)])  61.8 us
    ppermute x50, starting transfers between devices, swap(): return lax.ppermute(value, axis, [(i, i ^ bit) for i in range(size)])  31.5 us
    pallas_call x2, Pallas kernels, sum_call(): pl.pallas_call(functools.partial(kernel, [len(group) for group in groups]...  8.88 us
    all_to_all x2, starting transfers between devices, to_bands(): lax.all_to_all(value.reshape(dp, length // dp, QUARTER), 'dp', split_axis...  7.27 us
    all_to_all x1, starting transfers between devices, shards(): lax.all_to_all(ordered, 'dp', split_axis=0, concat_axis=1, tiled=True)[0]  7.26 us
    unnamed x158, local copies, waits for them, and re-layouts  5.72 us
    pallas_call x3, Pallas kernels, move_rows(): pl.pallas_call(kernel, in_specs=[pl.BlockSpec(memory_space=pltpu.SMEM), p...  5.25 us
  transfers between devices with their start and end apart: 53, of which 24 were waited for; matrix products, arithmetic and copies ran while one was open for 3% of the time, Pallas kernels for 40%

profile of v13, /device:TPU:0, one launch (start us, length us, event | category | flops | bytes accessed | tf_op | source)
XLA Modules:
  0.0 226.8 jit_solution(9964671279453844839)
XLA Ops:
  0.7 0.7 copy-done.68
  1.4 2.5 %deal.1 = bf16[8,64,512]{2,1,0:T(8,128)(2,1)} custom-call(s32[8]{0:T(128)S(1)} %copy-done.68, bf16[8,64,512]{2,1,0:T(8,128)(2,1)} %source.1), custom_call_target="tpu_custom_call" | custom-call | flops 1000 | bytes 1000 | tf_op jit(solution)/shard_map/deal/pallas_call | solution.py:599
  3.9 7.3 %all-to-all-start = ((bf16[8,64,512]{2,1,0:T(8,128)(2,1)}), bf16[8,64,512]{2,1,0:T(8,128)(2,1)S(1)}, u32[]{:S(2)}, u32[]{:S(2)}) async-start(bf16[8,64,512]{2,1,0:T(8,128)(2,1)} %deal.1), calls=%async_computation | async-start | bytes 1048576 | tf_op jit(solution)/shard_map/all_to_all | solution.py:750
  11.3 1.6 collective-permute-start.1
  14.2 0.7 collective-permute-done.1
  14.9 1.4 pad_add_fusion.info.refs_0_
  16.3 1.8 adapters.1
  19.4 7.4 %collective-permute-done.3.refs_11_.refs_10_ = bf16[512,512]{1,0:T(8,128)(2,1)S(1)} collective-permute-done((bf16[512,512]{1,0:T(8,128)(2,1)S(1)}, bf16[512,512]{1,0:T(8,128)(2,1)S(1)}, u32[]{:S(2)}, u32[]{:S(2)}) %collective-permute-start.3) | collective-permute-done | bytes 524320 | tf_op jit(solution)/shard_map/ppermute | solution.py:671
  27.5 7.0 %collective-permute-done.5.refs_5_.refs_6_ = bf16[256,512]{1,0:T(8,128)(2,1)S(1)} collective-permute-done((bf16[256,512]{1,0:T(8,128)(2,1)S(1)}, bf16[256,512]{1,0:T(8,128)(2,1)S(1)}, u32[]{:S(2)}, u32[]{:S(2)}) %collective-permute-start.5) | collective-permute-done | bytes 262176 | tf_op jit(solution)/shard_map/ppermute | solution.py:671
  35.1 1.0 collective-permute-done.6.refs_6_.refs_7_
  36.1 4.1 %project_0.1 = (bf16[48,256]{1,0:T(8,128)(2,1)S(1)}, bf16[512,256]{1,0:T(8,128)(2,1)S(1)}, bf16[2,256,64]{2,1,0:T(8,128)(2,1)S(1)}, bf16[2,256,64]{2,1,0:T(8,128...) custom-call(s32[4]{0:T(128)S(1)} %pad_add_fusion.info.refs_0_, bf16[2048,512]{1,0:T(8,128)(2,1)} %refs_1_.15, ...), custom_call_target="tpu_custom_call" | custom-call | flops 1000 | bytes 1000 | tf_op jit(solution)/shard_map/project_0/pallas_call | solution.py:632
  40.8 3.1 %attend_0.1 = (f32[256,1024]{1,0:T(8,128)S(1)}, bf16[256,1024]{1,0:T(8,128)(2,1)S(1)}, bf16[512,256]{1,0:T(8,128)(2,1)S(1)}, f32[8,256]{1,0:T(8,128)S(1)}, bf16[16,256]{1,0:T(8,128)(2,1)S(1)}) custom-call(s32[4]{0:T(128)S(1)} %pad_add_fusion.info.refs_0_, bf16[512,2048]{1,0:T(8,128)(2,1)} %refs_3_.5, ...), custom_call_target="tpu_custom_call" | custom-call | flops 1000 | bytes 1000 | tf_op jit(solution)/shard_map/attend_0/pallas_call | solution.py:632
  44.1 1.8 collective-permute-done.10.refs_1_
  46.6 1.5 collective-permute-done.13.refs_6_.refs_7_
  48.2 4.1 %project_1.1 = (bf16[48,256]{1,0:T(8,128)(2,1)S(1)}, bf16[512,256]{1,0:T(8,128)(2,1)S(1)}, bf16[2,256,64]{2,1,0:T(8,128)(2,1)S(1)}, bf16[2,256,64]{2,1,0:T(8,128...) custom-call(s32[4]{0:T(128)S(1)} %pad_add_fusion.info.refs_0_, bf16[2048,512]{1,0:T(8,128)(2,1)} %refs_1_.15, ...), custom_call_target="tpu_custom_call" | custom-call | flops 1000 | bytes 1000 | tf_op jit(solution)/shard_map/project_1/pallas_call | solution.py:632
  52.3 3.7 %attend_1.1 = (f32[256,1024]{1,0:T(8,128)S(1)}, bf16[256,1024]{1,0:T(8,128)(2,1)S(1)}, bf16[512,256]{1,0:T(8,128)(2,1)S(1)}, f32[8,256]{1,0:T(8,128)S(1)}, bf16[16,256]{1,0:T(8,128)(2,1)S(1)}) custom-call(s32[4]{0:T(128)S(1)} %pad_add_fusion.info.refs_0_, bf16[512,2048]{1,0:T(8,128)(2,1)} %refs_3_.5, ...), custom_call_target="tpu_custom_call" | custom-call | flops 1000 | bytes 1000 | tf_op jit(solution)/shard_map/attend_1/pallas_call | solution.py:632
  56.1 3.9 %collective-permute-done.11.refs_1_ = bf16[256,1024]{1,0:T(8,128)(2,1)S(1)} collective-permute-done((bf16[256,1024]{1,0:T(8,128)(2,1)S(1)}, bf16[256,1024]{1,0:T(8,128)(2,1)S(1)}, u32[]{:S(2)}, u32[]{:S(2)}) %collective-permute-start.11) | collective-permute-done | bytes 524320 | tf_op jit(solution)/shard_map/ppermute | solution.py:671
  62.7 0.7 collective-permute-done.8.refs_12_.refs_11_
  63.4 0.7 collective-permute-done.12.refs_8_
  64.2 13.0 %front_0.1 = (bf16[256,2048]{1,0:T(8,128)(2,1)S(1)}, f32[256,512]{1,0:T(8,128)S(1)}, bf16[256,2048]{1,0:T(8,128)(2,1)S(1)}, bf16[256,2048]{1,0:T(8,128)(2,1)S(1)...) custom-call(s32[4]{0:T(128)S(1)} %pad_add_fusion.info.refs_0_, ...), custom_call_target="tpu_custom_call" | custom-call | flops 1000 | bytes 1000 | tf_op jit(solution)/shard_map/front_0/pallas_call | solution.py:632
  77.2 1.0 copy-done.26
  78.5 1.8 collective-permute-done.16.refs_8_
  80.3 12.0 %front_1.1 = (bf16[256,2048]{1,0:T(8,128)(2,1)S(1)}, f32[256,512]{1,0:T(8,128)S(1)}, bf16[256,2048]{1,0:T(8,128)(2,1)S(1)}, bf16[256,2048]{1,0:T(8,128)(2,1)S(1)...) custom-call(s32[4]{0:T(128)S(1)} %pad_add_fusion.info.refs_0_, ...), custom_call_target="tpu_custom_call" | custom-call | flops 1000 | bytes 1000 | tf_op jit(solution)/shard_map/front_1/pallas_call | solution.py:632
  92.3 3.0 %collective-permute-start.17 = (bf16[1,192,512]{2,1,0:T(8,128)(2,1)S(1)}, bf16[1,192,512]{2,1,0:T(8,128)(2,1)S(1)}, u32[]{:S(2)}, u32[]{:S(2)}) collective-permute-start(bf16[1,192,512]{2,1,0:T(8,128)(2,1)S(1)} %bitcast.36), channel_id=1, source_target_pairs={{0,16},{4,20},{8,24},{12,28},{16,0},{20,4},{24,8},{28,12},{1,17},{... | collective-permute-start | bytes 589832 | tf_op jit(solution)/shard_map/ppermute | solution.py:671
  95.3 7.9 %back_1.1 = (f32[256,16]{1,0:T(8,128)S(1)}, f32[256,1024]{1,0:T(8,128)S(1)}, bf16[256,1024]{1,0:T(8,128)(2,1)S(1)}, f32[48,2048]{1,0:T(8,128)S(1)}) custom-call(s32[4]{0:T(128)S(1)} %pad_add_fusion.info.refs_0_, bf16[2,2048,2048]{2,1,0:T(8,128)(2,1)S(1)} %get-tuple-element.147.refs_1_, bf16[256,2048]{1,0:T(8,128)(2,1)S(1)} %get-tuple-element.157.refs_2_, ...), custom_call_target="tpu_custom_call" | custom-call | flops 1000 | bytes 1000 | tf_op jit(solution)/shard_map/back_1/pallas_call | solution.py:632
  103.2 1.5 collective-permute-done.17
  104.8 1.8 collective-permute-start.20
  107.8 7.9 %back_0.1 = (f32[256,16]{1,0:T(8,128)S(1)}, f32[304,1024]{1,0:T(8,128)S(1)}, bf16[304,1024]{1,0:T(8,128)(2,1)S(1)}) custom-call(s32[4]{0:T(128)S(1)} %pad_add_fusion.info.refs_0_, bf16[2,2048,2048]{2,1,0:T(8,128)(2,1)S(1)} %get-tuple-element.147.refs_1_, bf16[256,2048]{1,0:T(8,128)(2,1)S(1)} %get-tuple-element.148.refs_2_, ...), custom_call_target="tpu_custom_call" | custom-call | flops 1000 | bytes 1000 | tf_op jit(solution)/shard_map/back_0/pallas_call | solution.py:632
  116.4 1.4 collective-permute-done.19.refs_1_
  117.8 4.5 %down_1.1 = (f32[256,1024]{1,0:T(8,128)S(1)}, bf16[256,1024]{1,0:T(8,128)(2,1)}) custom-call(s32[4]{0:T(128)S(1)} %pad_add_fusion.info.refs_0_, bf16[2048,2048]{1,0:T(8,128)(2,1)S(1)} %bitcast.19, bf16[256,2048]{1,0:T(8,128)(2,1)S(1)} %get-tuple-element.159.refs_4_.refs_2_, f32[256,16]{1,0:T(8,128)S(1)} %get-tuple-element.171.refs_3_, ...), custom_call_target="tpu_custom_call" | custom-call | flops 1000 | bytes 1000 | tf_op jit(solution)/shard_map/down_1/pallas_call | solution.py:632
  123.4 0.7 collective-permute-start.23
  124.8 10.7 %attend_back_1.1 = (f32[256,512]{1,0:T(8,128)S(1)}, f32[256,1024]{1,0:T(8,128)S(1)}, bf16[256,1024]{1,0:T(8,128)(2,1)S(1)}, f32[256,1]{1,0:T(8,128)S(1)}, f32[48...) custom-call(s32[4]{0:T(128)S(1)} %pad_add_fusion.info.refs_0_, ...), custom_call_target="tpu_custom_call" | custom-call | flops 1000 | bytes 1000 | tf_op jit(solution)/shard_map/attend_back_1/pallas_call | solution.py:632
  136.1 3.8 %collective-permute-done.23.refs_1_ = bf16[304,1024]{1,0:T(8,128)(2,1)S(1)} collective-permute-done((bf16[304,1024]{1,0:T(8,128)(2,1)S(1)}, bf16[304,1024]{1,0:T(8,128)(2,1)S(1)}, u32[]{:S(2)}, u32[]{:S(2)}) %collective-permute-start.23) | collective-permute-done | bytes 622624 | tf_op jit(solution)/shard_map/ppermute | solution.py:671
  140.2 0.7 collective-permute-start.29
  140.9 2.3 %collective-permute-start.28 = (bf16[1,48,1024]{2,1,0:T(8,128)(2,1)S(1)}, bf16[1,48,1024]{2,1,0:T(8,128)(2,1)S(1)}, u32[]{:S(2)}, u32[]{:S(2)}) collective-permute-start(bf16[1,48,1024]{2,1,0:T(8,128)(2,1)S(1)} %slice_bitcast_fusion), channel_id=1, source_target_pairs={{0,16},{4,20},{8,24},{12,28},{16,0},{20,4},{24,8},{28,12},{1,17},{... | collective-permute-start | bytes 294920 | tf_op jit(solution)/shard_map/ppermute | solution.py:671
  143.3 9.8 %attend_back_0.1 = (f32[256,512]{1,0:T(8,128)S(1)}, f32[256,1024]{1,0:T(8,128)S(1)}, bf16[256,1024]{1,0:T(8,128)(2,1)S(1)}, f32[256,1]{1,0:T(8,128)S(1)}, bf16[4...) custom-call(s32[4]{0:T(128)S(1)} %pad_add_fusion.info.refs_0_, ...), custom_call_target="tpu_custom_call" | custom-call | flops 1000 | bytes 1000 | tf_op jit(solution)/shard_map/attend_back_0/pallas_call | solution.py:632
  153.7 1.7 collective-permute-done.30.refs_1_
  155.3 1.7 collective-permute-start.35
  157.0 1.4 collective-permute-start.31
  158.4 3.9 %collective-permute-done.35 = bf16[2,48,1024]{2,1,0:T(8,128)(2,1)S(1)} collective-permute-done((bf16[2,48,1024]{2,1,0:T(8,128)(2,1)S(1)}, bf16[2,48,1024]{2,1,0:T(8,128)(2,1)S(1)}, u32[]{:S(2)}, u32[]{:S(2)}) %collective-permute-start.35) | collective-permute-done | bytes 196640 | tf_op jit(solution)/shard_map/ppermute | solution.py:671
  163.1 1.3 collective-permute-start.33
  165.2 4.5 %down_0.1 = (f32[256,1024]{1,0:T(8,128)S(1)}, bf16[256,1024]{1,0:T(8,128)(2,1)}) custom-call(s32[4]{0:T(128)S(1)} %pad_add_fusion.info.refs_0_, bf16[2048,2048]{1,0:T(8,128)(2,1)S(1)} %bitcast.19, bf16[256,2048]{1,0:T(8,128)(2,1)S(1)} %copy-done.5, f32[256,16]{1,0:T(8,128)S(1)} %get-tuple-element.173.refs_6_.refs_3_, ...), custom_call_target="tpu_custom_call" | custom-call | flops 1000 | bytes 1000 | tf_op jit(solution)/shard_map/down_0/pallas_call | solution.py:632
  170.2 1.5 collective-permute-done.34
  171.7 1.0 collective-permute-done.36.refs_16_.refs_5_
  173.5 0.8 copy-done.16
  174.3 3.5 %all-to-all-start.1 = ((bf16[8,64,512]{2,1,0:T(8,128)(2,1)}), bf16[8,64,512]{2,1,0:T(8,128)(2,1)S(1)}, u32[]{:S(2)}, u32[]{:S(2)}) async-start(bf16[8,64,512]{2,1,0:T(8,128)(2,1)} %bitcast.35), calls=%async_computation.1 | async-start | bytes 1048576 | tf_op jit(solution)/shard_map/all_to_all | solution.py:826
  178.0 1.3 high_sum.7
  179.2 1.3 collective-permute-start.39
  180.5 1.9 collective-permute-start.42
  183.0 0.7 constant_dynamic-update-slice_fusion.3
  183.7 9.8 %collective-permute-done.42 = bf16[2,112,512]{2,1,0:T(8,128)(2,1)S(1)} collective-permute-done((bf16[2,112,512]{2,1,0:T(8,128)(2,1)S(1)}, bf16[2,112,512]{2,1,0:T(8,128)(2,1)S(1)}, u32[]{:S(2)}, u32[]{:S(2)}) %collective-permute-start.42) | collective-permute-done | bytes 229408 | tf_op jit(solution)/shard_map/ppermute | solution.py:671
  193.5 0.7 constant_dynamic-update-slice_fusion.2.refs_0_
  194.2 1.3 collective-permute-start.43
  195.5 4.1 %feedforward_sum.1 = (f32[8,32,2048]{2,1,0:T(8,128)}, f32[8,16,2048]{2,1,0:T(8,128)}, f32[8,2,16,2048]{3,2,1,0:T(8,128)}, f32[8,16,2048]{2,1,0:T(8,128)}) custom-call(s32[4]{0:T(128)S(1)} %pad_add_fusion.info.refs_0_, s32[8]{0:T(128)S(1)} %copy-done.71, bf16[2,192,512]{2,1,0:T(8,128)(2,1)S(1)} %copy-done.20, bf16[2,192,512]{2,1,0:T(8,128)(2,1)S(1)} %copy-done.43, ...), custom_call_target="tpu_custom_call" | custom-call | bytes 12000000 | tf_op jit(solution)/shard_map/feedforward_sum/pallas_call | solution.py:655
  199.7 2.1 output.1
  201.8 3.7 %all-to-all-start.2 = ((bf16[8,64,512]{2,1,0:T(8,128)(2,1)}), bf16[8,64,512]{2,1,0:T(8,128)(2,1)S(1)}, u32[]{:S(2)}, u32[]{:S(2)}) async-start(bf16[8,64,512]{2,1,0:T(8,128)(2,1)} %bitcast.14), calls=%async_computation.2 | async-start | bytes 1048576 | tf_op jit(solution)/shard_map/all_to_all | solution.py:826
  205.5 1.0 slice.34.refs_2_
  207.1 1.0 slice.35.refs_3_
  208.0 1.6 collective-permute-start.47
  209.6 6.2 %collective-permute-done.46.refs_6_ = bf16[4,64,512]{2,1,0:T(8,128)(2,1)S(1)} collective-permute-done((bf16[4,64,512]{2,1,0:T(8,128)(2,1)S(1)}, bf16[4,64,512]{2,1,0:T(8,128)(2,1)S(1)}, u32[]{:S(2)}, u32[]{:S(2)}) %collective-permute-start.46) | collective-permute-done | bytes 262176 | tf_op jit(solution)/shard_map/ppermute | solution.py:671
  216.3 2.7 %collective-permute-done.47.refs_7_ = bf16[4,64,512]{2,1,0:T(8,128)(2,1)S(1)} collective-permute-done((bf16[4,64,512]{2,1,0:T(8,128)(2,1)S(1)}, bf16[4,64,512]{2,1,0:T(8,128)(2,1)S(1)}, u32[]{:S(2)}, u32[]{:S(2)}) %collective-permute-start.47) | collective-permute-done | bytes 262176 | tf_op jit(solution)/shard_map/ppermute | solution.py:671
  219.0 1.4 collect_grad.1
  220.5 4.7 %attention_sum.1 = (f32[8,48,2048]{2,1,0:T(8,128)}, f32[8,16,2048]{2,1,0:T(8,128)}, f32[8,16,512]{2,1,0:T(8,128)}, f32[8,2,16,128]{3,2,1,0:T(8,128)}, f32[8,16,512]{2,1,0:T(8,128)}) custom-call(s32[4]{0:T(128)S(1)} %pad_add_fusion.info.refs_0_, s32[8]{0:T(128)S(1)} %copy-done.71, bf16[4,112,512]{2,1,0:T(8,128)(2,1)} %constant_dynamic-update-slice_fusion.2.refs_0_, ...), custom_call_target="tpu_custom_call" | custom-call | bytes 12000000 | tf_op jit(solution)/shard_map/attention_sum/pallas_call | solution.py:655
  225.2 1.4 collect_out.1
  (252 shorter events, 17.9 us)
Async XLA Ops:
  3.9 23.0 %all-to-all-start = ((bf16[8,64,512]{2,1,0:T(8,128)(2,1)}), bf16[8,64,512]{2,1,0:T(8,128)(2,1)S(1)}, u32[]{:S(2)}, u32[]{:S(2)}) async-start(bf16[8,64,512]{2,1,0:T(8,128)(2,1)} %deal.1), calls=%async_computation | async-start | bytes 1048576 | tf_op jit(solution)/shard_map/all_to_all | solution.py:750
  11.2 8.2 %collective-permute-start = (bf16[2,512]{1,0:T(2,128)(2,1)S(1)}, bf16[2,512]{1,0:T(2,128)(2,1)S(1)}, u32[]{:S(2)}, u32[]{:S(2)}) collective-permute-start(bf16[2,512]{1,0:T(2,128)(2,1)S(1)} %pad_maximum_fusion.4), channel_id=1, source_target_pairs={{0,1},{1,0},{2,3},{3,2},{4,5},{5,4},{6,7},{7,6},{8,9},{9,8},{10,11... | collective-permute-start | bytes 6152 | tf_op jit(solution)/shard_map/ppermute | solution.py:671
  11.3 3.7 %collective-permute-start.1 = (bf16[2,512]{1,0:T(2,128)(2,1)S(1)}, bf16[2,512]{1,0:T(2,128)(2,1)S(1)}, u32[]{:S(2)}, u32[]{:S(2)}) collective-permute-start(bf16[2,512]{1,0:T(2,128)(2,1)S(1)} %pad_maximum_fusion.4), channel_id=1, source_target_pairs={{0,2},{1,3},{2,0},{3,1},{4,6},{5,7},{6,4},{7,5},{8,10},{9,11},{10,... | collective-permute-start | bytes 6152 | tf_op jit(solution)/shard_map/ppermute | solution.py:671
  12.9 14.0 %collective-permute-start.3 = (bf16[512,512]{1,0:T(8,128)(2,1)S(1)}, bf16[512,512]{1,0:T(8,128)(2,1)S(1)}, u32[]{:S(2)}, u32[]{:S(2)}) collective-permute-start(bf16[512,512]{1,0:T(8,128)(2,1)S(1)} %bitcast.29), channel_id=1, source_target_pairs={{0,2},{1,3},{2,0},{3,1},{4,6},{5,7},{6,4},{7,5},{8,10},{9,11},{10,... | collective-permute-start | bytes 1572872 | tf_op jit(solution)/shard_map/ppermute | solution.py:671
  14.9 4.5 %collective-permute-start.2 = (bf16[2,512]{1,0:T(2,128)(2,1)S(1)}, bf16[2,512]{1,0:T(2,128)(2,1)S(1)}, u32[]{:S(2)}, u32[]{:S(2)}) collective-permute-start(bf16[2,512]{1,0:T(2,128)(2,1)S(1)} %collective-permute-done.1), channel_id=1, source_target_pairs={{0,1},{1,0},{2,3},{3,2},{4,5},{5,4},{6,7},{7,6},{8,9},{9,8},{10,11... | collective-permute-start | bytes 6152 | tf_op jit(solution)/shard_map/ppermute | solution.py:671
  16.3 19.8 %copy-start.58 = (f32[32,256]{1,0:T(8,128)S(1)}, f32[32,256]{1,0:T(8,128)}, u32[]{:S(2)}) copy-start(f32[32,256]{1,0:T(8,128)} %constant.21.clone.refs_12_.refs_22_) | copy-start | bytes 98308
  16.3 19.8 %copy-start.60 = (f32[32,256]{1,0:T(8,128)S(1)}, f32[32,256]{1,0:T(8,128)}, u32[]{:S(2)}) copy-start(f32[32,256]{1,0:T(8,128)} %constant.19.clone.refs_11_.refs_21_) | copy-start | bytes 98308
  19.4 28.8 %copy-start.54 = (bf16[16,512]{1,0:T(8,128)(2,1)}, bf16[16,512]{1,0:T(8,128)(2,1)S(1)}, u32[]{:S(2)}) copy-start(bf16[16,512]{1,0:T(8,128)(2,1)S(1)} %get-tuple-element.121.refs_9_.refs_17_) | copy-start | bytes 49156
  19.4 28.8 %copy-start.62 = (bf16[2,16,128]{2,1,0:T(8,128)(2,1)}, bf16[2,16,128]{2,1,0:T(8,128)(2,1)S(1)}, u32[]{:S(2)}) copy-start(bf16[2,16,128]{2,1,0:T(8,128)(2,1)S(1)} %get-tuple-element.122.refs_10_.refs_18_) | copy-start | bytes 24580
  19.4 32.9 %copy-start.24 = (bf16[16,2048]{1,0:T(8,128)(2,1)}, bf16[16,2048]{1,0:T(8,128)(2,1)S(1)}, u32[]{:S(2)}) copy-start(bf16[16,2048]{1,0:T(8,128)(2,1)S(1)} %get-tuple-element.125.refs_4_.refs_20_) | copy-start | bytes 196612
  19.4 32.9 %copy-start.48 = (bf16[16,512]{1,0:T(8,128)(2,1)}, bf16[16,512]{1,0:T(8,128)(2,1)S(1)}, u32[]{:S(2)}) copy-start(bf16[16,512]{1,0:T(8,128)(2,1)S(1)} %get-tuple-element.124.refs_3_.refs_19_) | copy-start | bytes 49156
  26.9 7.6 %collective-permute-start.5 = (bf16[256,512]{1,0:T(8,128)(2,1)S(1)}, bf16[256,512]{1,0:T(8,128)(2,1)S(1)}, u32[]{:S(2)}, u32[]{:S(2)}) collective-permute-start(bf16[256,512]{1,0:T(8,128)(2,1)S(1)} %get-tuple-element.230), channel_id=1, source_target_pairs={{0,2},{1,3},{2,0},{3,1},{4,6},{5,7},{6,4},{7,5},{8,10},{9,11},{10,... | collective-permute-start | bytes 786440 | tf_op jit(solution)/shard_map/ppermute | solution.py:671
  27.5 8.6 %collective-permute-start.4 = (bf16[512,512]{1,0:T(8,128)(2,1)S(1)}, bf16[512,512]{1,0:T(8,128)(2,1)S(1)}, u32[]{:S(2)}, u32[]{:S(2)}) collective-permute-start(bf16[512,512]{1,0:T(8,128)(2,1)S(1)} %bitcast.21), channel_id=1, source_target_pairs={{0,1},{1,0},{2,3},{3,2},{4,5},{5,4},{6,7},{7,6},{8,9},{9,8},{10,11... | collective-permute-start | bytes 1572872 | tf_op jit(solution)/shard_map/ppermute | solution.py:671
  34.5 29.7 %copy-start.8 = (bf16[256,512]{1,0:T(8,128)(2,1)}, bf16[256,512]{1,0:T(8,128)(2,1)S(1)}, u32[]{:S(2)}) copy-start(bf16[256,512]{1,0:T(8,128)(2,1)S(1)} %collective-permute-done.5.refs_5_.refs_6_) | copy-start | bytes 786436
  34.5 1.5 collective-permute-start.6
  34.5 9.4 %collective-permute-start.9 = (bf16[256,512]{1,0:T(8,128)(2,1)S(1)}, bf16[256,512]{1,0:T(8,128)(2,1)S(1)}, u32[]{:S(2)}, u32[]{:S(2)}) collective-permute-start(bf16[256,512]{1,0:T(8,128)(2,1)S(1)} %get-tuple-element.229), channel_id=1, source_target_pairs={{0,2},{1,3},{2,0},{3,1},{4,6},{5,7},{6,4},{7,5},{8,10},{9,11},{10,... | collective-permute-start | bytes 786440 | tf_op jit(solution)/shard_map/ppermute | solution.py:671
  36.0 28.1 %copy-start.10 = (bf16[256,512]{1,0:T(8,128)(2,1)}, bf16[256,512]{1,0:T(8,128)(2,1)S(1)}, u32[]{:S(2)}) copy-start(bf16[256,512]{1,0:T(8,128)(2,1)S(1)} %collective-permute-done.6.refs_6_.refs_7_) | copy-start | bytes 786436
  43.9 2.0 collective-permute-start.10
  46.0 14.0 %collective-permute-start.11 = (bf16[256,1024]{1,0:T(8,128)(2,1)S(1)}, bf16[256,1024]{1,0:T(8,128)(2,1)S(1)}, u32[]{:S(2)}, u32[]{:S(2)}) collective-permute-start(bf16[256,1024]{1,0:T(8,128)(2,1)S(1)} %pair_sum.4.refs_0_.refs_14_), channel_id=1, source_target_pairs={{0,2},{1,3},{2,0},{3,1},{4,6},{5,7},{6,4},{7,5},{8,10},{9,11},{10,... | collective-permute-start | bytes 1572872 | tf_op jit(solution)/shard_map/ppermute | solution.py:671
  46.6 1.5 collective-permute-start.13
  48.1 32.2 %copy-start.6 = (bf16[256,512]{1,0:T(8,128)(2,1)}, bf16[256,512]{1,0:T(8,128)(2,1)S(1)}, u32[]{:S(2)}) copy-start(bf16[256,512]{1,0:T(8,128)(2,1)S(1)} %collective-permute-done.13.refs_6_.refs_7_) | copy-start | bytes 786436
  56.1 21.1 %copy-start.52 = (bf16[512,256]{1,0:T(8,128)(2,1)}, bf16[512,256]{1,0:T(8,128)(2,1)S(1)}, u32[]{:S(2)}) copy-start(bf16[512,256]{1,0:T(8,128)(2,1)S(1)} %get-tuple-element.178.refs_25_) | copy-start | bytes 786436
  60.0 1.9 collective-permute-start.14
  60.0 2.7 %collective-permute-start.7 = (bf16[512,512]{1,0:T(8,128)(2,1)S(1)}, bf16[512,512]{1,0:T(8,128)(2,1)S(1)}, u32[]{:S(2)}, u32[]{:S(2)}) collective-permute-start(bf16[512,512]{1,0:T(8,128)(2,1)S(1)} %bitcast.30), channel_id=1, source_target_pairs={{0,1},{1,0},{2,3},{3,2},{4,5},{5,4},{6,7},{7,6},{8,9},{9,8},{10,11... | collective-permute-start | bytes 1572872 | tf_op jit(solution)/shard_map/ppermute | solution.py:671
  60.5 2.9 %collective-permute-start.8 = (bf16[512,512]{1,0:T(8,128)(2,1)S(1)}, bf16[512,512]{1,0:T(8,128)(2,1)S(1)}, u32[]{:S(2)}, u32[]{:S(2)}) collective-permute-start(bf16[512,512]{1,0:T(8,128)(2,1)S(1)} %collective-permute-done.3.refs_11_.refs_10_), channel_id=1, source_target_pairs={{0,1},{1,0},{2,3},{3,2},{4,5},{5,4},{6,7},{7,6},{8,9},{9,8},{10,11... | collective-permute-start | bytes 1572872 | tf_op jit(solution)/shard_map/ppermute | solution.py:671
  60.7 3.4 %collective-permute-start.12 = (bf16[256,1024]{1,0:T(8,128)(2,1)S(1)}, bf16[256,1024]{1,0:T(8,128)(2,1)S(1)}, u32[]{:S(2)}, u32[]{:S(2)}) collective-permute-start(bf16[256,1024]{1,0:T(8,128)(2,1)S(1)} %far_sum.4.refs_7_), channel_id=1, source_target_pairs={{0,1},{1,0},{2,3},{3,2},{4,5},{5,4},{6,7},{7,6},{8,9},{9,8},{10,11... | collective-permute-start | bytes 1572872 | tf_op jit(solution)/shard_map/ppermute | solution.py:671
  62.1 16.1 %collective-permute-start.15 = (bf16[256,1024]{1,0:T(8,128)(2,1)S(1)}, bf16[256,1024]{1,0:T(8,128)(2,1)S(1)}, u32[]{:S(2)}, u32[]{:S(2)}) collective-permute-start(bf16[256,1024]{1,0:T(8,128)(2,1)S(1)} %pair_sum.5.refs_19_.refs_0_), channel_id=1, source_target_pairs={{0,2},{1,3},{2,0},{3,1},{4,6},{5,7},{6,4},{7,5},{8,10},{9,11},{10,... | collective-permute-start | bytes 1572872 | tf_op jit(solution)/shard_map/ppermute | solution.py:671
  78.2 29.6 %copy-start.4 = (bf16[256,2048]{1,0:T(8,128)(2,1)}, bf16[256,2048]{1,0:T(8,128)(2,1)S(1)}, u32[]{:S(2)}) copy-start(bf16[256,2048]{1,0:T(8,128)(2,1)S(1)} %get-tuple-element.150.refs_4_.refs_2_) | copy-start | bytes 3145732
  78.3 2.0 collective-permute-start.16
  92.3 12.4 %collective-permute-start.17 = (bf16[1,192,512]{2,1,0:T(8,128)(2,1)S(1)}, bf16[1,192,512]{2,1,0:T(8,128)(2,1)S(1)}, u32[]{:S(2)}, u32[]{:S(2)}) collective-permute-start(bf16[1,192,512]{2,1,0:T(8,128)(2,1)S(1)} %bitcast.36), channel_id=1, source_target_pairs={{0,16},{4,20},{8,24},{12,28},{16,0},{20,4},{24,8},{28,12},{1,17},{... | collective-permute-start | bytes 589832 | tf_op jit(solution)/shard_map/ppermute | solution.py:671
  104.7 2.3 %collective-permute-start.18 = (bf16[256,1024]{1,0:T(8,128)(2,1)S(1)}, bf16[256,1024]{1,0:T(8,128)(2,1)S(1)}, u32[]{:S(2)}, u32[]{:S(2)}) collective-permute-start(bf16[256,1024]{1,0:T(8,128)(2,1)S(1)} %get-tuple-element.167), channel_id=1, source_target_pairs={{0,1},{1,0},{2,3},{3,2},{4,5},{5,4},{6,7},{7,6},{8,9},{9,8},{10,11... | collective-permute-start | bytes 1572872 | tf_op jit(solution)/shard_map/ppermute | solution.py:671
  104.8 11.6 %collective-permute-start.20 = (bf16[2,192,512]{2,1,0:T(8,128)(2,1)S(1)}, bf16[2,192,512]{2,1,0:T(8,128)(2,1)S(1)}, u32[]{:S(2)}, u32[]{:S(2)}) collective-permute-start(bf16[2,192,512]{2,1,0:T(8,128)(2,1)S(1)} %pad_maximum_fusion.refs_0_), channel_id=1, source_target_pairs={{0,4},{4,0},{8,12},{12,8},{16,20},{20,16},{24,28},{28,24},{1,5},{5... | collective-permute-start | bytes 1179656 | tf_op jit(solution)/shard_map/ppermute | solution.py:671
  106.5 11.2 %collective-permute-start.19 = (bf16[2,192,512]{2,1,0:T(8,128)(2,1)S(1)}, bf16[2,192,512]{2,1,0:T(8,128)(2,1)S(1)}, u32[]{:S(2)}, u32[]{:S(2)}) collective-permute-start(bf16[2,192,512]{2,1,0:T(8,128)(2,1)S(1)} %pad_maximum_fusion.refs_0_), channel_id=1, source_target_pairs={{0,8},{4,12},{8,0},{12,4},{16,24},{20,28},{24,16},{28,20},{1,9},{5... | collective-permute-start | bytes 1179656 | tf_op jit(solution)/shard_map/ppermute | solution.py:671
  107.1 15.3 %collective-permute-start.22 = (bf16[256,1024]{1,0:T(8,128)(2,1)S(1)}, bf16[256,1024]{1,0:T(8,128)(2,1)S(1)}, u32[]{:S(2)}, u32[]{:S(2)}) collective-permute-start(bf16[256,1024]{1,0:T(8,128)(2,1)S(1)} %pair_sum.6.refs_11_.refs_0_), channel_id=1, source_target_pairs={{0,2},{1,3},{2,0},{3,1},{4,6},{5,7},{6,4},{7,5},{8,10},{9,11},{10,... | collective-permute-start | bytes 1572872 | tf_op jit(solution)/shard_map/ppermute | solution.py:671
  117.8 5.4 %collective-permute-start.21 = (bf16[304,1024]{1,0:T(8,128)(2,1)S(1)}, bf16[304,1024]{1,0:T(8,128)(2,1)S(1)}, u32[]{:S(2)}, u32[]{:S(2)}) collective-permute-start(bf16[304,1024]{1,0:T(8,128)(2,1)S(1)} %get-tuple-element.170), channel_id=1, source_target_pairs={{0,1},{1,0},{2,3},{3,2},{4,5},{5,4},{6,7},{7,6},{8,9},{9,8},{10,11... | collective-permute-start | bytes 1867784 | tf_op jit(solution)/shard_map/ppermute | solution.py:671
  122.6 2.1 collective-permute-start.24
  123.4 16.5 %collective-permute-start.23 = (bf16[304,1024]{1,0:T(8,128)(2,1)S(1)}, bf16[304,1024]{1,0:T(8,128)(2,1)S(1)}, u32[]{:S(2)}, u32[]{:S(2)}) collective-permute-start(bf16[304,1024]{1,0:T(8,128)(2,1)S(1)} %pair_sum.7.refs_34_.refs_0_), channel_id=1, source_target_pairs={{0,2},{1,3},{2,0},{3,1},{4,6},{5,7},{6,4},{7,5},{8,10},{9,11},{10,... | collective-permute-start | bytes 1867784 | tf_op jit(solution)/shard_map/ppermute | solution.py:671
  124.1 11.5 %collective-permute-start.26 = (bf16[2,192,512]{2,1,0:T(8,128)(2,1)S(1)}, bf16[2,192,512]{2,1,0:T(8,128)(2,1)S(1)}, u32[]{:S(2)}, u32[]{:S(2)}) collective-permute-start(bf16[2,192,512]{2,1,0:T(8,128)(2,1)S(1)} %collective-permute-done.19.refs_1_), channel_id=1, source_target_pairs={{0,4},{4,0},{8,12},{12,8},{16,20},{20,16},{24,28},{28,24},{1,5},{5... | collective-permute-start | bytes 1179656 | tf_op jit(solution)/shard_map/ppermute | solution.py:671
  135.6 4.5 %collective-permute-start.27 = (bf16[256,1024]{1,0:T(8,128)(2,1)S(1)}, bf16[256,1024]{1,0:T(8,128)(2,1)S(1)}, u32[]{:S(2)}, u32[]{:S(2)}) collective-permute-start(bf16[256,1024]{1,0:T(8,128)(2,1)S(1)} %get-tuple-element.195), channel_id=1, source_target_pairs={{0,1},{1,0},{2,3},{3,2},{4,5},{5,4},{6,7},{7,6},{8,9},{9,8},{10,11... | collective-permute-start | bytes 1572872 | tf_op jit(solution)/shard_map/ppermute | solution.py:671
  140.1 3.1 %collective-permute-start.25 = (bf16[304,1024]{1,0:T(8,128)(2,1)S(1)}, bf16[304,1024]{1,0:T(8,128)(2,1)S(1)}, u32[]{:S(2)}, u32[]{:S(2)}) collective-permute-start(bf16[304,1024]{1,0:T(8,128)(2,1)S(1)} %far_sum.7.refs_13_), channel_id=1, source_target_pairs={{0,1},{1,0},{2,3},{3,2},{4,5},{5,4},{6,7},{7,6},{8,9},{9,8},{10,11... | collective-permute-start | bytes 1867784 | tf_op jit(solution)/shard_map/ppermute | solution.py:671
  140.2 12.9 %collective-permute-start.29 = (bf16[256,512]{1,0:T(8,128)(2,1)S(1)}, bf16[256,512]{1,0:T(8,128)(2,1)S(1)}, u32[]{:S(2)}, u32[]{:S(2)}) collective-permute-start(bf16[256,512]{1,0:T(8,128)(2,1)S(1)} %high_sum.4.refs_36_), channel_id=1, source_target_pairs={{0,2},{1,3},{2,0},{3,1},{4,6},{5,7},{6,4},{7,5},{8,10},{9,11},{10,... | collective-permute-start | bytes 786440 | tf_op jit(solution)/shard_map/ppermute | solution.py:671
  140.9 12.1 %collective-permute-start.28 = (bf16[1,48,1024]{2,1,0:T(8,128)(2,1)S(1)}, bf16[1,48,1024]{2,1,0:T(8,128)(2,1)S(1)}, u32[]{:S(2)}, u32[]{:S(2)}) collective-permute-start(bf16[1,48,1024]{2,1,0:T(8,128)(2,1)S(1)} %slice_bitcast_fusion), channel_id=1, source_target_pairs={{0,16},{4,20},{8,24},{12,28},{16,0},{20,4},{24,8},{28,12},{1,17},{... | collective-permute-start | bytes 294920 | tf_op jit(solution)/shard_map/ppermute | solution.py:671
  153.1 10.0 %collective-permute-start.32 = (bf16[256,1024]{1,0:T(8,128)(2,1)S(1)}, bf16[256,1024]{1,0:T(8,128)(2,1)S(1)}, u32[]{:S(2)}, u32[]{:S(2)}) collective-permute-start(bf16[256,1024]{1,0:T(8,128)(2,1)S(1)} %get-tuple-element.202), channel_id=1, source_target_pairs={{0,1},{1,0},{2,3},{3,2},{4,5},{5,4},{6,7},{7,6},{8,9},{9,8},{10,11... | collective-permute-start | bytes 1572872 | tf_op jit(solution)/shard_map/ppermute | solution.py:671
  153.2 2.2 collective-permute-start.30
  155.3 7.0 %collective-permute-start.35 = (bf16[2,48,1024]{2,1,0:T(8,128)(2,1)S(1)}, bf16[2,48,1024]{2,1,0:T(8,128)(2,1)S(1)}, u32[]{:S(2)}, u32[]{:S(2)}) collective-permute-start(bf16[2,48,1024]{2,1,0:T(8,128)(2,1)S(1)} %pad_maximum_fusion.2), channel_id=1, source_target_pairs={{0,8},{4,12},{8,0},{12,4},{16,24},{20,28},{24,16},{28,20},{1,9},{5... | collective-permute-start | bytes 589832 | tf_op jit(solution)/shard_map/ppermute | solution.py:671
  157.0 7.4 %collective-permute-start.31 = (bf16[96,512]{1,0:T(8,128)(2,1)S(1)}, bf16[96,512]{1,0:T(8,128)(2,1)S(1)}, u32[]{:S(2)}, u32[]{:S(2)}) collective-permute-start(bf16[96,512]{1,0:T(8,128)(2,1)S(1)} %high_sum.5.refs_2_), channel_id=1, source_target_pairs={{0,2},{1,3},{2,0},{3,1},{4,6},{5,7},{6,4},{7,5},{8,10},{9,11},{10,... | collective-permute-start | bytes 294920 | tf_op jit(solution)/shard_map/ppermute | solution.py:671
  162.4 10.4 %collective-permute-start.36 = (bf16[4,48,1024]{2,1,0:T(8,128)(2,1)S(1)}, bf16[4,48,1024]{2,1,0:T(8,128)(2,1)S(1)}, u32[]{:S(2)}, u32[]{:S(2)}) collective-permute-start(bf16[4,48,1024]{2,1,0:T(8,128)(2,1)S(1)} %constant_dynamic-update-slice_fusion.refs_4_), channel_id=1, source_target_pairs={{0,4},{4,0},{8,12},{12,8},{16,20},{20,16},{24,28},{28,24},{1,5},{5... | collective-permute-start | bytes 1179656 | tf_op jit(solution)/shard_map/ppermute | solution.py:671
  163.1 9.7 %collective-permute-start.33 = (bf16[256,512]{1,0:T(8,128)(2,1)S(1)}, bf16[256,512]{1,0:T(8,128)(2,1)S(1)}, u32[]{:S(2)}, u32[]{:S(2)}) collective-permute-start(bf16[256,512]{1,0:T(8,128)(2,1)S(1)} %high_sum.6), channel_id=1, source_target_pairs={{0,2},{1,3},{2,0},{3,1},{4,6},{5,7},{6,4},{7,5},{8,10},{9,11},{10,... | collective-permute-start | bytes 786440 | tf_op jit(solution)/shard_map/ppermute | solution.py:671
  164.5 7.2 %collective-permute-start.34 = (bf16[1,112,512]{2,1,0:T(8,128)(2,1)S(1)}, bf16[1,112,512]{2,1,0:T(8,128)(2,1)S(1)}, u32[]{:S(2)}, u32[]{:S(2)}) collective-permute-start(bf16[1,112,512]{2,1,0:T(8,128)(2,1)S(1)} %maximum_bitcast_fusion.refs_6_), channel_id=1, source_target_pairs={{0,16},{4,20},{8,24},{12,28},{16,0},{20,4},{24,8},{28,12},{1,17},{... | collective-permute-start | bytes 344072 | tf_op jit(solution)/shard_map/ppermute | solution.py:671
  165.2 12.7 %collective-permute-start.38 = (bf16[256,1024]{1,0:T(8,128)(2,1)}, bf16[256,1024]{1,0:T(8,128)(2,1)S(1)}, u32[]{:S(2)}, u32[]{:S(2)}) collective-permute-start(bf16[256,1024]{1,0:T(8,128)(2,1)} %get-tuple-element.214.refs_35_), channel_id=1, source_target_pairs={{0,1},{1,0},{2,3},{3,2},{4,5},{5,4},{6,7},{7,6},{8,9},{9,8},{10,11... | collective-permute-start | bytes 1572872 | tf_op jit(solution)/shard_map/ppermute | solution.py:671
  169.7 8.2 %collective-permute-start.37 = (bf16[256,1024]{1,0:T(8,128)(2,1)}, bf16[256,1024]{1,0:T(8,128)(2,1)}, u32[]{:S(2)}, u32[]{:S(2)}) collective-permute-start(bf16[256,1024]{1,0:T(8,128)(2,1)} %get-tuple-element.208.refs_15_), channel_id=1, source_target_pairs={{0,1},{1,0},{2,3},{3,2},{4,5},{5,4},{6,7},{7,6},{8,9},{9,8},{10,11... | collective-permute-start | bytes 1572872 | tf_op jit(solution)/shard_map/ppermute | solution.py:671
  174.3 27.4 %all-to-all-start.1 = ((bf16[8,64,512]{2,1,0:T(8,128)(2,1)}), bf16[8,64,512]{2,1,0:T(8,128)(2,1)S(1)}, u32[]{:S(2)}, u32[]{:S(2)}) async-start(bf16[8,64,512]{2,1,0:T(8,128)(2,1)} %bitcast.35), calls=%async_computation.1 | async-start | bytes 1048576 | tf_op jit(solution)/shard_map/all_to_all | solution.py:826
  179.2 20.5 %collective-permute-start.39 = (bf16[512,512]{1,0:T(8,128)(2,1)S(1)}, bf16[512,512]{1,0:T(8,128)(2,1)S(1)}, u32[]{:S(2)}, u32[]{:S(2)}) collective-permute-start(bf16[512,512]{1,0:T(8,128)(2,1)S(1)} %high_sum.7), channel_id=1, source_target_pairs={{0,2},{1,3},{2,0},{3,1},{4,6},{5,7},{6,4},{7,5},{8,10},{9,11},{10,... | collective-permute-start | bytes 1572872 | tf_op jit(solution)/shard_map/ppermute | solution.py:671
  180.5 13.0 %collective-permute-start.42 = (bf16[2,112,512]{2,1,0:T(8,128)(2,1)S(1)}, bf16[2,112,512]{2,1,0:T(8,128)(2,1)S(1)}, u32[]{:S(2)}, u32[]{:S(2)}) collective-permute-start(bf16[2,112,512]{2,1,0:T(8,128)(2,1)S(1)} %pad_maximum_fusion.1.refs_14_), channel_id=1, source_target_pairs={{0,8},{4,12},{8,0},{12,4},{16,24},{20,28},{24,16},{28,20},{1,9},{5... | collective-permute-start | bytes 688136 | tf_op jit(solution)/shard_map/ppermute | solution.py:671
  182.4 13.0 %collective-permute-start.40 = (bf16[4,48,1024]{2,1,0:T(8,128)(2,1)S(1)}, bf16[4,48,1024]{2,1,0:T(8,128)(2,1)S(1)}, u32[]{:S(2)}, u32[]{:S(2)}) collective-permute-start(bf16[4,48,1024]{2,1,0:T(8,128)(2,1)S(1)} %copy-done.35), channel_id=1, source_target_pairs={{0,1},{1,0},{2,3},{3,2},{4,5},{5,4},{6,7},{7,6},{8,9},{9,8},{10,11... | collective-permute-start | bytes 1179656 | tf_op jit(solution)/shard_map/ppermute | solution.py:671
  182.5 13.0 %collective-permute-start.41 = (bf16[4,48,1024]{2,1,0:T(8,128)(2,1)S(1)}, bf16[4,48,1024]{2,1,0:T(8,128)(2,1)S(1)}, u32[]{:S(2)}, u32[]{:S(2)}) collective-permute-start(bf16[4,48,1024]{2,1,0:T(8,128)(2,1)S(1)} %copy-done.18), channel_id=1, source_target_pairs={{0,1},{1,0},{2,3},{3,2},{4,5},{5,4},{6,7},{7,6},{8,9},{9,8},{10,11... | collective-permute-start | bytes 1179656 | tf_op jit(solution)/shard_map/ppermute | solution.py:671
  194.2 12.9 %collective-permute-start.43 = (bf16[4,112,512]{2,1,0:T(8,128)(2,1)}, bf16[4,112,512]{2,1,0:T(8,128)(2,1)}, u32[]{:S(2)}, u32[]{:S(2)}) collective-permute-start(bf16[4,112,512]{2,1,0:T(8,128)(2,1)} %constant_dynamic-update-slice_fusion.2.refs_0_), channel_id=1, source_target_pairs={{0,4},{4,0},{8,12},{12,8},{16,20},{20,16},{24,28},{28,24},{1,5},{5... | collective-permute-start | bytes 1376264 | tf_op jit(solution)/shard_map/ppermute | solution.py:671
  201.8 23.5 %all-to-all-start.2 = ((bf16[8,64,512]{2,1,0:T(8,128)(2,1)}), bf16[8,64,512]{2,1,0:T(8,128)(2,1)S(1)}, u32[]{:S(2)}, u32[]{:S(2)}) async-start(bf16[8,64,512]{2,1,0:T(8,128)(2,1)} %bitcast.14), calls=%async_computation.2 | async-start | bytes 1048576 | tf_op jit(solution)/shard_map/all_to_all | solution.py:826
  206.5 9.3 %collective-permute-start.46 = (bf16[4,64,512]{2,1,0:T(8,128)(2,1)S(1)}, bf16[4,64,512]{2,1,0:T(8,128)(2,1)S(1)}, u32[]{:S(2)}, u32[]{:S(2)}) collective-permute-start(bf16[4,64,512]{2,1,0:T(8,128)(2,1)S(1)} %slice.34.refs_2_), channel_id=1, source_target_pairs={{0,2},{1,3},{2,0},{3,1},{4,6},{5,7},{6,4},{7,5},{8,10},{9,11},{10,... | collective-permute-start | bytes 786440 | tf_op jit(solution)/shard_map/ppermute | solution.py:671
  208.0 10.9 %collective-permute-start.47 = (bf16[4,64,512]{2,1,0:T(8,128)(2,1)S(1)}, bf16[4,64,512]{2,1,0:T(8,128)(2,1)S(1)}, u32[]{:S(2)}, u32[]{:S(2)}) collective-permute-start(bf16[4,64,512]{2,1,0:T(8,128)(2,1)S(1)} %slice.35.refs_3_), channel_id=1, source_target_pairs={{0,2},{1,3},{2,0},{3,1},{4,6},{5,7},{6,4},{7,5},{8,10},{9,11},{10,... | collective-permute-start | bytes 786440 | tf_op jit(solution)/shard_map/ppermute | solution.py:671
  209.6 10.8 %collective-permute-start.44 = (bf16[4,64,512]{2,1,0:T(8,128)(2,1)S(1)}, bf16[4,64,512]{2,1,0:T(8,128)(2,1)S(1)}, u32[]{:S(2)}, u32[]{:S(2)}) collective-permute-start(bf16[4,64,512]{2,1,0:T(8,128)(2,1)S(1)} %slice.34.refs_2_), channel_id=1, source_target_pairs={{0,1},{1,0},{2,3},{3,2},{4,5},{5,4},{6,7},{7,6},{8,9},{9,8},{10,11... | collective-permute-start | bytes 786440 | tf_op jit(solution)/shard_map/ppermute | solution.py:671
  215.8 4.6 %collective-permute-start.48 = (bf16[4,64,512]{2,1,0:T(8,128)(2,1)S(1)}, bf16[4,64,512]{2,1,0:T(8,128)(2,1)S(1)}, u32[]{:S(2)}, u32[]{:S(2)}) collective-permute-start(bf16[4,64,512]{2,1,0:T(8,128)(2,1)S(1)} %collective-permute-done.46.refs_6_), channel_id=1, source_target_pairs={{0,1},{1,0},{2,3},{3,2},{4,5},{5,4},{6,7},{7,6},{8,9},{9,8},{10,11... | collective-permute-start | bytes 786440 | tf_op jit(solution)/shard_map/ppermute | solution.py:671
  215.8 4.6 %collective-permute-start.45 = (bf16[4,64,512]{2,1,0:T(8,128)(2,1)S(1)}, bf16[4,64,512]{2,1,0:T(8,128)(2,1)S(1)}, u32[]{:S(2)}, u32[]{:S(2)}) collective-permute-start(bf16[4,64,512]{2,1,0:T(8,128)(2,1)S(1)} %slice.35.refs_3_), channel_id=1, source_target_pairs={{0,1},{1,0},{2,3},{3,2},{4,5},{5,4},{6,7},{7,6},{8,9},{9,8},{10,11... | collective-permute-start | bytes 786440 | tf_op jit(solution)/shard_map/ppermute | solution.py:671
  219.0 1.5 collective-permute-start.49
  (67 other events, 475.7 us)

commit v14 on v10

--- a/solution.py
+++ b/solution.py
@@ -753,7 +753,7 @@
          output_adapter_output, feedfwd_adapter_input, feedfwd_adapter_output, down_adapter_input,
          down_adapter_output), info)
     a1, qb, kvb, oa, ob, a2, fba, da, bd = adapters_here
-    dealt = late(dealt, gs[2], a1, gains)
+    dealt = late(dealt, a1, gains)
     beside = near(dealt)
     there = [far(dealt[c * rows:(c + 1) * rows]) for c in range(CHUNKS)]
     xs = [None] * CHUNKS
@@ -769,7 +769,7 @@
     saved, kept, z_own, z_far = ([None] * CHUNKS for _ in range(4))
     order = ()
     for c in range(CHUNKS):
-        xs[c] = (dealt, beside, there[c], near(late(there[c], saved[0][0]) if c else there[c]))
+        xs[c] = (dealt, beside, there[c], near(late(there[c], saved[0][0]) if c else late(there[c], gs[2])))
         outs = [((3 * RANK, rows), BF16), ((q_cols, rows), BF16), ((kv_heads, rows, HEAD), BF16),
                 ((kv_heads, rows, HEAD), BF16), ((kv_cols, rows), BF16), ((kv_cols, rows), BF16)]
         saved[c] = call(

time: 220 us -> 217 us (0.986)
  waiting for transfers between devices: 54.5 us -> 46.9 us
  starting transfers between devices: 48.5 us -> 54.2 us
    ppermute x50, waiting for transfers between devices: 54.5 us -> 40.7 us  [swap(): return lax.ppermute(value, axis, [(i, i ^ bit) for i in range(size)])]
    all_to_all x1, waiting for transfers between devices: 0.01 us -> 6.18 us  [shards(): lax.all_to_all(ordered, 'dp', split_axis=0, concat_axis=1, tiled=True)[0]]
    ppermute x50, starting transfers between devices: 31.6 us -> 37.2 us  [swap(): return lax.ppermute(value, axis, [(i, i ^ bit) for i in range(size)])]
  transfers between devices with their start and end apart: 53 -> 53, of which waited for: 24 -> 21; matrix products, arithmetic and copies ran while one was open for 2% -> 2% of each run, Pallas kernels for 41% -> 42%
where the time goes in v14:
time: 217 us
  Pallas kernels  106 us (49%)
  starting transfers between devices  54.2 us (25%)
  waiting for transfers between devices  46.9 us (22%)
  local copies, waits for them, and re-layouts  5.3 us (2%)
  other arithmetic  2.31 us (1%)
    pallas_call x26, Pallas kernels, call(): pl.pallas_call(body, in_specs=[pl.BlockSpec(memory_space=pltpu.SMEM)] * n...  90.7 us
    ppermute x50, waiting for transfers between devices, swap(): return lax.ppermute(value, axis, [(i, i ^ bit) for i in range(size)])  40.7 us
    ppermute x50, starting transfers between devices, swap(): return lax.ppermute(value, axis, [(i, i ^ bit) for i in range(size)])  37.2 us
    all_to_all x2, starting transfers between devices, to_bands(): lax.all_to_all(value.reshape(dp, length // dp, QUARTER), 'dp', split_axis...  9.69 us
    pallas_call x2, Pallas kernels, sum_call(): pl.pallas_call(functools.partial(kernel, [len(group) for group in groups]...  8.36 us
    all_to_all x1, starting transfers between devices, shards(): lax.all_to_all(ordered, 'dp', split_axis=0, concat_axis=1, tiled=True)[0]  7.26 us
    all_to_all x1, waiting for transfers between devices, shards(): lax.all_to_all(ordered, 'dp', split_axis=0, concat_axis=1, tiled=True)[0]  6.18 us
    pallas_call x3, Pallas kernels, move_rows(): pl.pallas_call(kernel, in_specs=[pl.BlockSpec(memory_space=pltpu.SMEM), p...  5.25 us
  transfers between devices with their start and end apart: 53, of which 21 were waited for; matrix products, arithmetic and copies ran while one was open for 2% of the time, Pallas kernels for 42%

profile of v14, /device:TPU:0, one launch (start us, length us, event | category | flops | bytes accessed | tf_op | source)
XLA Modules:
  0.0 216.7 jit_solution(10623631265059392966)
XLA Ops:
  0.7 0.7 copy-done.64
  1.4 2.5 %deal.1 = bf16[8,64,512]{2,1,0:T(8,128)(2,1)} custom-call(s32[8]{0:T(128)S(1)} %copy-done.64, bf16[8,64,512]{2,1,0:T(8,128)(2,1)} %source.1), custom_call_target="tpu_custom_call" | custom-call | flops 1000 | bytes 1000 | tf_op jit(solution)/shard_map/deal/pallas_call | solution.py:599
  3.9 7.3 %all-to-all-start = ((bf16[8,64,512]{2,1,0:T(8,128)(2,1)}), bf16[8,64,512]{2,1,0:T(8,128)(2,1)S(1)}, u32[]{:S(2)}, u32[]{:S(2)}) async-start(bf16[8,64,512]{2,1,0:T(8,128)(2,1)} %deal.1), calls=%async_computation | async-start | bytes 1048576 | tf_op jit(solution)/shard_map/all_to_all | solution.py:750
  11.3 1.6 collective-permute-start.1
  14.2 0.7 collective-permute-done.1
  14.9 1.4 pad_add_fusion.info.refs_0_
  16.3 1.8 adapters.1
  19.4 6.2 %all-to-all-done = bf16[8,64,512]{2,1,0:T(8,128)(2,1)S(1)} async-done(((bf16[8,64,512]{2,1,0:T(8,128)(2,1)}), bf16[8,64,512]{2,1,0:T(8,128)(2,1)S(1)}, u32[]{:S(2)}, u32[]{:S(2)}) %all-to-all-start) | async-done | bytes 524320 | tf_op jit(solution)/shard_map/all_to_all | solution.py:750
  25.7 1.6 collective-permute-start.4
  27.2 5.2 %collective-permute-done.4.refs_5_.refs_6_ = bf16[256,512]{1,0:T(8,128)(2,1)S(1)} collective-permute-done((bf16[256,512]{1,0:T(8,128)(2,1)S(1)}, bf16[256,512]{1,0:T(8,128)(2,1)S(1)}, u32[]{:S(2)}, u32[]{:S(2)}) %collective-permute-start.4) | collective-permute-done | bytes 262176 | tf_op jit(solution)/shard_map/ppermute | solution.py:671
  32.5 1.5 collective-permute-start.9
  34.0 4.1 %project_0.1 = (bf16[48,256]{1,0:T(8,128)(2,1)S(1)}, bf16[512,256]{1,0:T(8,128)(2,1)S(1)}, bf16[2,256,64]{2,1,0:T(8,128)(2,1)S(1)}, bf16[2,256,64]{2,1,0:T(8,128...) custom-call(s32[4]{0:T(128)S(1)} %pad_add_fusion.info.refs_0_, bf16[2048,512]{1,0:T(8,128)(2,1)} %refs_1_.15, ...), custom_call_target="tpu_custom_call" | custom-call | flops 1000 | bytes 1000 | tf_op jit(solution)/shard_map/project_0/pallas_call | solution.py:632
  38.2 3.1 %attend_0.1 = (f32[256,1024]{1,0:T(8,128)S(1)}, bf16[256,1024]{1,0:T(8,128)(2,1)S(1)}, bf16[512,256]{1,0:T(8,128)(2,1)S(1)}, f32[8,256]{1,0:T(8,128)S(1)}, bf16[16,256]{1,0:T(8,128)(2,1)S(1)}) custom-call(s32[4]{0:T(128)S(1)} %pad_add_fusion.info.refs_0_, bf16[512,2048]{1,0:T(8,128)(2,1)} %refs_3_.5, ...), custom_call_target="tpu_custom_call" | custom-call | flops 1000 | bytes 1000 | tf_op jit(solution)/shard_map/attend_0/pallas_call | solution.py:632
  41.5 1.7 collective-permute-done.10.refs_1_
  43.4 1.5 collective-permute-start.11
  44.9 1.5 collective-permute-done.13.refs_6_.refs_7_
  46.5 4.1 %project_1.1 = (bf16[48,256]{1,0:T(8,128)(2,1)S(1)}, bf16[512,256]{1,0:T(8,128)(2,1)S(1)}, bf16[2,256,64]{2,1,0:T(8,128)(2,1)S(1)}, bf16[2,256,64]{2,1,0:T(8,128...) custom-call(s32[4]{0:T(128)S(1)} %pad_add_fusion.info.refs_0_, bf16[2048,512]{1,0:T(8,128)(2,1)} %refs_1_.15, ...), custom_call_target="tpu_custom_call" | custom-call | flops 1000 | bytes 1000 | tf_op jit(solution)/shard_map/project_1/pallas_call | solution.py:632
  50.7 3.7 %attend_1.1 = (f32[256,1024]{1,0:T(8,128)S(1)}, bf16[256,1024]{1,0:T(8,128)(2,1)S(1)}, bf16[512,256]{1,0:T(8,128)(2,1)S(1)}, f32[8,256]{1,0:T(8,128)S(1)}, bf16[16,256]{1,0:T(8,128)(2,1)S(1)}) custom-call(s32[4]{0:T(128)S(1)} %pad_add_fusion.info.refs_0_, bf16[512,2048]{1,0:T(8,128)(2,1)} %refs_3_.5, ...), custom_call_target="tpu_custom_call" | custom-call | flops 1000 | bytes 1000 | tf_op jit(solution)/shard_map/attend_1/pallas_call | solution.py:632
  54.4 3.0 %collective-permute-done.11.refs_1_ = bf16[256,1024]{1,0:T(8,128)(2,1)S(1)} collective-permute-done((bf16[256,1024]{1,0:T(8,128)(2,1)S(1)}, bf16[256,1024]{1,0:T(8,128)(2,1)S(1)}, u32[]{:S(2)}, u32[]{:S(2)}) %collective-permute-start.11) | collective-permute-done | bytes 524320 | tf_op jit(solution)/shard_map/ppermute | solution.py:671
  59.5 1.5 collective-permute-start.15
  61.6 13.0 %front_0.1 = (bf16[256,2048]{1,0:T(8,128)(2,1)S(1)}, f32[256,512]{1,0:T(8,128)S(1)}, bf16[256,2048]{1,0:T(8,128)(2,1)S(1)}, bf16[256,2048]{1,0:T(8,128)(2,1)S(1)...) custom-call(s32[4]{0:T(128)S(1)} %pad_add_fusion.info.refs_0_, ...), custom_call_target="tpu_custom_call" | custom-call | flops 1000 | bytes 1000 | tf_op jit(solution)/shard_map/front_0/pallas_call | solution.py:632
  74.6 1.0 copy-done.24
  75.9 1.8 collective-permute-done.16.refs_8_
  77.7 12.0 %front_1.1 = (bf16[256,2048]{1,0:T(8,128)(2,1)S(1)}, f32[256,512]{1,0:T(8,128)S(1)}, bf16[256,2048]{1,0:T(8,128)(2,1)S(1)}, bf16[256,2048]{1,0:T(8,128)(2,1)S(1)...) custom-call(s32[4]{0:T(128)S(1)} %pad_add_fusion.info.refs_0_, ...), custom_call_target="tpu_custom_call" | custom-call | flops 1000 | bytes 1000 | tf_op jit(solution)/shard_map/front_1/pallas_call | solution.py:632
  89.7 2.9 %collective-permute-start.17 = (bf16[1,192,512]{2,1,0:T(8,128)(2,1)S(1)}, bf16[1,192,512]{2,1,0:T(8,128)(2,1)S(1)}, u32[]{:S(2)}, u32[]{:S(2)}) collective-permute-start(bf16[1,192,512]{2,1,0:T(8,128)(2,1)S(1)} %bitcast.36), channel_id=1, source_target_pairs={{0,16},{4,20},{8,24},{12,28},{16,0},{20,4},{24,8},{28,12},{1,17},{... | collective-permute-start | bytes 589832 | tf_op jit(solution)/shard_map/ppermute | solution.py:671
  92.7 7.9 %back_1.1 = (f32[256,16]{1,0:T(8,128)S(1)}, f32[256,1024]{1,0:T(8,128)S(1)}, bf16[256,1024]{1,0:T(8,128)(2,1)S(1)}, f32[48,2048]{1,0:T(8,128)S(1)}) custom-call(s32[4]{0:T(128)S(1)} %pad_add_fusion.info.refs_0_, bf16[2,2048,2048]{2,1,0:T(8,128)(2,1)S(1)} %get-tuple-element.149.refs_1_, bf16[256,2048]{1,0:T(8,128)(2,1)S(1)} %get-tuple-element.159.refs_2_, ...), custom_call_target="tpu_custom_call" | custom-call | flops 1000 | bytes 1000 | tf_op jit(solution)/shard_map/back_1/pallas_call | solution.py:632
  100.5 1.5 collective-permute-done.17
  102.2 1.9 collective-permute-start.20
  104.5 1.1 collective-permute-start.22
  105.6 7.9 %back_0.1 = (f32[256,16]{1,0:T(8,128)S(1)}, f32[304,1024]{1,0:T(8,128)S(1)}, bf16[304,1024]{1,0:T(8,128)(2,1)S(1)}) custom-call(s32[4]{0:T(128)S(1)} %pad_add_fusion.info.refs_0_, bf16[2,2048,2048]{2,1,0:T(8,128)(2,1)S(1)} %get-tuple-element.149.refs_1_, bf16[256,2048]{1,0:T(8,128)(2,1)S(1)} %get-tuple-element.150.refs_2_, ...), custom_call_target="tpu_custom_call" | custom-call | flops 1000 | bytes 1000 | tf_op jit(solution)/shard_map/back_0/pallas_call | solution.py:632
  113.8 1.5 collective-permute-done.19.refs_1_
  115.3 4.5 %down_1.1 = (f32[256,1024]{1,0:T(8,128)S(1)}, bf16[256,1024]{1,0:T(8,128)(2,1)}) custom-call(s32[4]{0:T(128)S(1)} %pad_add_fusion.info.refs_0_, bf16[2048,2048]{1,0:T(8,128)(2,1)S(1)} %bitcast.19, bf16[256,2048]{1,0:T(8,128)(2,1)S(1)} %get-tuple-element.161.refs_4_.refs_2_, f32[256,16]{1,0:T(8,128)S(1)} %get-tuple-element.173.refs_3_, ...), custom_call_target="tpu_custom_call" | custom-call | flops 1000 | bytes 1000 | tf_op jit(solution)/shard_map/down_1/pallas_call | solution.py:632
  120.9 1.5 collective-permute-start.23
  122.8 10.7 %attend_back_1.1 = (f32[256,512]{1,0:T(8,128)S(1)}, f32[256,1024]{1,0:T(8,128)S(1)}, bf16[256,1024]{1,0:T(8,128)(2,1)S(1)}, f32[256,1]{1,0:T(8,128)S(1)}, f32[48...) custom-call(s32[4]{0:T(128)S(1)} %pad_add_fusion.info.refs_0_, ...), custom_call_target="tpu_custom_call" | custom-call | flops 1000 | bytes 1000 | tf_op jit(solution)/shard_map/attend_back_1/pallas_call | solution.py:632
  133.8 3.6 %collective-permute-done.23.refs_1_ = bf16[304,1024]{1,0:T(8,128)(2,1)S(1)} collective-permute-done((bf16[304,1024]{1,0:T(8,128)(2,1)S(1)}, bf16[304,1024]{1,0:T(8,128)(2,1)S(1)}, u32[]{:S(2)}, u32[]{:S(2)}) %collective-permute-start.23) | collective-permute-done | bytes 622624 | tf_op jit(solution)/shard_map/ppermute | solution.py:671
  137.7 1.5 collective-permute-start.29
  139.2 1.5 collective-permute-start.28
  140.7 9.8 %attend_back_0.1 = (f32[256,512]{1,0:T(8,128)S(1)}, f32[256,1024]{1,0:T(8,128)S(1)}, bf16[256,1024]{1,0:T(8,128)(2,1)S(1)}, f32[256,1]{1,0:T(8,128)S(1)}, bf16[4...) custom-call(s32[4]{0:T(128)S(1)} %pad_add_fusion.info.refs_0_, ...), custom_call_target="tpu_custom_call" | custom-call | flops 1000 | bytes 1000 | tf_op jit(solution)/shard_map/attend_back_0/pallas_call | solution.py:632
  151.1 1.7 collective-permute-done.30.refs_1_
  152.8 1.3 collective-permute-start.31
  154.1 1.7 collective-permute-start.36
  156.6 1.1 collective-permute-done.31.refs_3_
  157.7 2.3 %collective-permute-start.34 = (bf16[1,112,512]{2,1,0:T(8,128)(2,1)S(1)}, bf16[1,112,512]{2,1,0:T(8,128)(2,1)S(1)}, u32[]{:S(2)}, u32[]{:S(2)}) collective-permute-start(bf16[1,112,512]{2,1,0:T(8,128)(2,1)S(1)} %maximum_bitcast_fusion.refs_6_), channel_id=1, source_target_pairs={{0,16},{4,20},{8,24},{12,28},{16,0},{20,4},{24,8},{28,12},{1,17},{... | collective-permute-start | bytes 344072 | tf_op jit(solution)/shard_map/ppermute | solution.py:671
  160.0 1.8 collective-permute-done.36
  162.5 4.5 %down_0.1 = (f32[256,1024]{1,0:T(8,128)S(1)}, bf16[256,1024]{1,0:T(8,128)(2,1)}) custom-call(s32[4]{0:T(128)S(1)} %pad_add_fusion.info.refs_0_, bf16[2048,2048]{1,0:T(8,128)(2,1)S(1)} %bitcast.19, bf16[256,2048]{1,0:T(8,128)(2,1)S(1)} %copy-done.5, f32[256,16]{1,0:T(8,128)S(1)} %get-tuple-element.175.refs_6_.refs_3_, ...), custom_call_target="tpu_custom_call" | custom-call | flops 1000 | bytes 1000 | tf_op jit(solution)/shard_map/down_0/pallas_call | solution.py:632
  167.0 1.8 collective-permute-start.35
  169.4 3.7 %collective-permute-done.35 = bf16[2,112,512]{2,1,0:T(8,128)(2,1)S(1)} collective-permute-done((bf16[2,112,512]{2,1,0:T(8,128)(2,1)S(1)}, bf16[2,112,512]{2,1,0:T(8,128)(2,1)S(1)}, u32[]{:S(2)}, u32[]{:S(2)}) %collective-permute-start.35) | collective-permute-done | bytes 229408 | tf_op jit(solution)/shard_map/ppermute | solution.py:671
  173.7 0.8 copy-done.16
  174.5 4.0 %all-to-all-start.1 = ((bf16[8,64,512]{2,1,0:T(8,128)(2,1)}), bf16[8,64,512]{2,1,0:T(8,128)(2,1)S(1)}, u32[]{:S(2)}, u32[]{:S(2)}) async-start(bf16[8,64,512]{2,1,0:T(8,128)(2,1)} %bitcast.35), calls=%async_computation.1 | async-start | bytes 1048576 | tf_op jit(solution)/shard_map/all_to_all | solution.py:826
  178.6 1.4 high_sum.7
  180.0 0.9 collective-permute-start.40
  181.4 2.0 collective-permute-start.43
  183.5 3.9 %feedforward_sum.1 = (f32[8,32,2048]{2,1,0:T(8,128)}, f32[8,16,2048]{2,1,0:T(8,128)}, f32[8,2,16,2048]{3,2,1,0:T(8,128)}, f32[8,16,2048]{2,1,0:T(8,128)}) custom-call(s32[4]{0:T(128)S(1)} %pad_add_fusion.info.refs_0_, s32[8]{0:T(128)S(1)} %copy-done.67, bf16[2,192,512]{2,1,0:T(8,128)(2,1)S(1)} %copy-done.18, bf16[2,192,512]{2,1,0:T(8,128)(2,1)S(1)} %copy-done.41, ...), custom_call_target="tpu_custom_call" | custom-call | bytes 12000000 | tf_op jit(solution)/shard_map/feedforward_sum/pallas_call | solution.py:655
  187.4 3.0 %collective-permute-done.40.refs_1_ = bf16[512,512]{1,0:T(8,128)(2,1)S(1)} collective-permute-done((bf16[512,512]{1,0:T(8,128)(2,1)S(1)}, bf16[512,512]{1,0:T(8,128)(2,1)S(1)}, u32[]{:S(2)}, u32[]{:S(2)}) %collective-permute-start.40) | collective-permute-done | bytes 524320 | tf_op jit(solution)/shard_map/ppermute | solution.py:671
  190.4 2.2 %output.1 = bf16[512,512]{1,0:T(8,128)(2,1)} custom-call(s32[4]{0:T(128)S(1)} %pad_add_fusion.info.refs_0_, bf16[512,512]{1,0:T(8,128)(2,1)S(1)} %collective-permute-done.40.refs_1_, f32[256,1024]{1,0:T(8,128)S(1)} %get-tuple-element.214.refs_0_.refs_2_, bf16[256,1024]{1,0:T(8,128)(2,1)} %collective-permute-done.38.refs_1_.refs_3_, ...), custom_call_target="tpu_custom_call" | custom-call | flops 1000 | bytes 1000 | tf_op jit(solution)/shard_map/output/pallas_call | solution.py:632
  192.6 5.7 %all-to-all-start.2 = ((bf16[8,64,512]{2,1,0:T(8,128)(2,1)}), bf16[8,64,512]{2,1,0:T(8,128)(2,1)S(1)}, u32[]{:S(2)}, u32[]{:S(2)}) async-start(bf16[8,64,512]{2,1,0:T(8,128)(2,1)} %bitcast.14), calls=%async_computation.2 | async-start | bytes 1048576 | tf_op jit(solution)/shard_map/all_to_all | solution.py:826
  198.3 1.3 collective-permute-start.46
  199.7 1.0 slice.35.refs_3_
  200.6 0.8 collective-permute-start.47
  201.5 4.9 %collective-permute-done.46.refs_6_ = bf16[4,64,512]{2,1,0:T(8,128)(2,1)S(1)} collective-permute-done((bf16[4,64,512]{2,1,0:T(8,128)(2,1)S(1)}, bf16[4,64,512]{2,1,0:T(8,128)(2,1)S(1)}, u32[]{:S(2)}, u32[]{:S(2)}) %collective-permute-start.46) | collective-permute-done | bytes 262176 | tf_op jit(solution)/shard_map/ppermute | solution.py:671
  206.8 2.3 %collective-permute-done.47.refs_7_ = bf16[4,64,512]{2,1,0:T(8,128)(2,1)S(1)} collective-permute-done((bf16[4,64,512]{2,1,0:T(8,128)(2,1)S(1)}, bf16[4,64,512]{2,1,0:T(8,128)(2,1)S(1)}, u32[]{:S(2)}, u32[]{:S(2)}) %collective-permute-start.47) | collective-permute-done | bytes 262176 | tf_op jit(solution)/shard_map/ppermute | solution.py:671
  209.1 1.4 collect_grad.1
  210.7 4.4 %attention_sum.1 = (f32[8,48,2048]{2,1,0:T(8,128)}, f32[8,16,2048]{2,1,0:T(8,128)}, f32[8,16,512]{2,1,0:T(8,128)}, f32[8,2,16,128]{3,2,1,0:T(8,128)}, f32[8,16,512]{2,1,0:T(8,128)}) custom-call(s32[4]{0:T(128)S(1)} %pad_add_fusion.info.refs_0_, s32[8]{0:T(128)S(1)} %copy-done.67, bf16[4,112,512]{2,1,0:T(8,128)(2,1)S(1)} %constant_dynamic-update-slice_fusion.refs_14_.refs_0_, ...), custom_call_target="tpu_custom_call" | custom-call | bytes 12000000 | tf_op jit(solution)/shard_map/attention_sum/pallas_call | solution.py:655
  215.1 1.4 collect_out.1
  (244 shorter events, 13.2 us)
Async XLA Ops:
  3.9 21.8 %all-to-all-start = ((bf16[8,64,512]{2,1,0:T(8,128)(2,1)}), bf16[8,64,512]{2,1,0:T(8,128)(2,1)S(1)}, u32[]{:S(2)}, u32[]{:S(2)}) async-start(bf16[8,64,512]{2,1,0:T(8,128)(2,1)} %deal.1), calls=%async_computation | async-start | bytes 1048576 | tf_op jit(solution)/shard_map/all_to_all | solution.py:750
  11.2 8.2 %collective-permute-start = (bf16[2,512]{1,0:T(2,128)(2,1)S(1)}, bf16[2,512]{1,0:T(2,128)(2,1)S(1)}, u32[]{:S(2)}, u32[]{:S(2)}) collective-permute-start(bf16[2,512]{1,0:T(2,128)(2,1)S(1)} %pad_maximum_fusion.4), channel_id=1, source_target_pairs={{0,1},{1,0},{2,3},{3,2},{4,5},{5,4},{6,7},{7,6},{8,9},{9,8},{10,11... | collective-permute-start | bytes 6152 | tf_op jit(solution)/shard_map/ppermute | solution.py:671
  11.3 3.7 %collective-permute-start.1 = (bf16[2,512]{1,0:T(2,128)(2,1)S(1)}, bf16[2,512]{1,0:T(2,128)(2,1)S(1)}, u32[]{:S(2)}, u32[]{:S(2)}) collective-permute-start(bf16[2,512]{1,0:T(2,128)(2,1)S(1)} %pad_maximum_fusion.4), channel_id=1, source_target_pairs={{0,2},{1,3},{2,0},{3,1},{4,6},{5,7},{6,4},{7,5},{8,10},{9,11},{10,... | collective-permute-start | bytes 6152 | tf_op jit(solution)/shard_map/ppermute | solution.py:671
  12.9 14.4 %collective-permute-start.5 = (bf16[512,512]{1,0:T(8,128)(2,1)S(1)}, bf16[512,512]{1,0:T(8,128)(2,1)S(1)}, u32[]{:S(2)}, u32[]{:S(2)}) collective-permute-start(bf16[512,512]{1,0:T(8,128)(2,1)S(1)} %bitcast.29), channel_id=1, source_target_pairs={{0,2},{1,3},{2,0},{3,1},{4,6},{5,7},{6,4},{7,5},{8,10},{9,11},{10,... | collective-permute-start | bytes 1572872 | tf_op jit(solution)/shard_map/ppermute | solution.py:671
  14.9 4.5 %collective-permute-start.2 = (bf16[2,512]{1,0:T(2,128)(2,1)S(1)}, bf16[2,512]{1,0:T(2,128)(2,1)S(1)}, u32[]{:S(2)}, u32[]{:S(2)}) collective-permute-start(bf16[2,512]{1,0:T(2,128)(2,1)S(1)} %collective-permute-done.1), channel_id=1, source_target_pairs={{0,1},{1,0},{2,3},{3,2},{4,5},{5,4},{6,7},{7,6},{8,9},{9,8},{10,11... | collective-permute-start | bytes 6152 | tf_op jit(solution)/shard_map/ppermute | solution.py:671
  16.3 17.7 %copy-start.54 = (f32[32,256]{1,0:T(8,128)S(1)}, f32[32,256]{1,0:T(8,128)}, u32[]{:S(2)}) copy-start(f32[32,256]{1,0:T(8,128)} %constant.21.clone.refs_12_.refs_22_) | copy-start | bytes 98308
  16.3 17.7 %copy-start.56 = (f32[32,256]{1,0:T(8,128)S(1)}, f32[32,256]{1,0:T(8,128)}, u32[]{:S(2)}) copy-start(f32[32,256]{1,0:T(8,128)} %constant.19.clone.refs_11_.refs_21_) | copy-start | bytes 98308
  19.4 27.1 %copy-start.50 = (bf16[16,512]{1,0:T(8,128)(2,1)}, bf16[16,512]{1,0:T(8,128)(2,1)S(1)}, u32[]{:S(2)}) copy-start(bf16[16,512]{1,0:T(8,128)(2,1)S(1)} %get-tuple-element.123.refs_9_.refs_17_) | copy-start | bytes 49156
  19.4 27.1 %copy-start.58 = (bf16[2,16,128]{2,1,0:T(8,128)(2,1)}, bf16[2,16,128]{2,1,0:T(8,128)(2,1)S(1)}, u32[]{:S(2)}) copy-start(bf16[2,16,128]{2,1,0:T(8,128)(2,1)S(1)} %get-tuple-element.124.refs_10_.refs_18_) | copy-start | bytes 24580
  19.4 31.2 %copy-start.22 = (bf16[16,2048]{1,0:T(8,128)(2,1)}, bf16[16,2048]{1,0:T(8,128)(2,1)S(1)}, u32[]{:S(2)}) copy-start(bf16[16,2048]{1,0:T(8,128)(2,1)S(1)} %get-tuple-element.127.refs_4_.refs_20_) | copy-start | bytes 196612
  19.4 31.2 %copy-start.44 = (bf16[16,512]{1,0:T(8,128)(2,1)}, bf16[16,512]{1,0:T(8,128)(2,1)S(1)}, u32[]{:S(2)}) copy-start(bf16[16,512]{1,0:T(8,128)(2,1)S(1)} %get-tuple-element.126.refs_3_.refs_19_) | copy-start | bytes 49156
  25.7 6.8 %collective-permute-start.4 = (bf16[256,512]{1,0:T(8,128)(2,1)S(1)}, bf16[256,512]{1,0:T(8,128)(2,1)S(1)}, u32[]{:S(2)}, u32[]{:S(2)}) collective-permute-start(bf16[256,512]{1,0:T(8,128)(2,1)S(1)} %get-tuple-element.232), channel_id=1, source_target_pairs={{0,2},{1,3},{2,0},{3,1},{4,6},{5,7},{6,4},{7,5},{8,10},{9,11},{10,... | collective-permute-start | bytes 786440 | tf_op jit(solution)/shard_map/ppermute | solution.py:671
  27.2 6.8 %collective-permute-start.3 = (bf16[512,512]{1,0:T(8,128)(2,1)S(1)}, bf16[512,512]{1,0:T(8,128)(2,1)S(1)}, u32[]{:S(2)}, u32[]{:S(2)}) collective-permute-start(bf16[512,512]{1,0:T(8,128)(2,1)S(1)} %bitcast.21), channel_id=1, source_target_pairs={{0,1},{1,0},{2,3},{3,2},{4,5},{5,4},{6,7},{7,6},{8,9},{9,8},{10,11... | collective-permute-start | bytes 1572872 | tf_op jit(solution)/shard_map/ppermute | solution.py:671
  32.5 29.1 %copy-start.8 = (bf16[256,512]{1,0:T(8,128)(2,1)}, bf16[256,512]{1,0:T(8,128)(2,1)S(1)}, u32[]{:S(2)}) copy-start(bf16[256,512]{1,0:T(8,128)(2,1)S(1)} %collective-permute-done.4.refs_5_.refs_6_) | copy-start | bytes 786436
  32.5 1.5 collective-permute-start.6
  32.5 8.8 %collective-permute-start.9 = (bf16[256,512]{1,0:T(8,128)(2,1)S(1)}, bf16[256,512]{1,0:T(8,128)(2,1)S(1)}, u32[]{:S(2)}, u32[]{:S(2)}) collective-permute-start(bf16[256,512]{1,0:T(8,128)(2,1)S(1)} %get-tuple-element.231), channel_id=1, source_target_pairs={{0,2},{1,3},{2,0},{3,1},{4,6},{5,7},{6,4},{7,5},{8,10},{9,11},{10,... | collective-permute-start | bytes 786440 | tf_op jit(solution)/shard_map/ppermute | solution.py:671
  34.0 27.6 %copy-start.10 = (bf16[256,512]{1,0:T(8,128)(2,1)}, bf16[256,512]{1,0:T(8,128)(2,1)S(1)}, u32[]{:S(2)}) copy-start(bf16[256,512]{1,0:T(8,128)(2,1)S(1)} %collective-permute-done.6.refs_6_.refs_7_) | copy-start | bytes 786436
  41.3 2.0 collective-permute-start.10
  43.4 14.1 %collective-permute-start.11 = (bf16[256,1024]{1,0:T(8,128)(2,1)S(1)}, bf16[256,1024]{1,0:T(8,128)(2,1)S(1)}, u32[]{:S(2)}, u32[]{:S(2)}) collective-permute-start(bf16[256,1024]{1,0:T(8,128)(2,1)S(1)} %pair_sum.4.refs_0_.refs_14_), channel_id=1, source_target_pairs={{0,2},{1,3},{2,0},{3,1},{4,6},{5,7},{6,4},{7,5},{8,10},{9,11},{10,... | collective-permute-start | bytes 1572872 | tf_op jit(solution)/shard_map/ppermute | solution.py:671
  44.9 1.5 collective-permute-start.13
  46.5 31.3 %copy-start.6 = (bf16[256,512]{1,0:T(8,128)(2,1)}, bf16[256,512]{1,0:T(8,128)(2,1)S(1)}, u32[]{:S(2)}) copy-start(bf16[256,512]{1,0:T(8,128)(2,1)S(1)} %collective-permute-done.13.refs_6_.refs_7_) | copy-start | bytes 786436
  54.4 20.2 %copy-start.48 = (bf16[512,256]{1,0:T(8,128)(2,1)}, bf16[512,256]{1,0:T(8,128)(2,1)S(1)}, u32[]{:S(2)}) copy-start(bf16[512,256]{1,0:T(8,128)(2,1)S(1)} %get-tuple-element.180.refs_25_) | copy-start | bytes 786436
  57.5 1.9 collective-permute-start.14
  57.5 3.6 %collective-permute-start.7 = (bf16[512,512]{1,0:T(8,128)(2,1)S(1)}, bf16[512,512]{1,0:T(8,128)(2,1)S(1)}, u32[]{:S(2)}, u32[]{:S(2)}) collective-permute-start(bf16[512,512]{1,0:T(8,128)(2,1)S(1)} %bitcast.30), channel_id=1, source_target_pairs={{0,1},{1,0},{2,3},{3,2},{4,5},{5,4},{6,7},{7,6},{8,9},{9,8},{10,11... | collective-permute-start | bytes 1572872 | tf_op jit(solution)/shard_map/ppermute | solution.py:671
  58.0 3.0 %collective-permute-start.8 = (bf16[512,512]{1,0:T(8,128)(2,1)S(1)}, bf16[512,512]{1,0:T(8,128)(2,1)S(1)}, u32[]{:S(2)}, u32[]{:S(2)}) collective-permute-start(bf16[512,512]{1,0:T(8,128)(2,1)S(1)} %collective-permute-done.5.refs_11_.refs_10_), channel_id=1, source_target_pairs={{0,1},{1,0},{2,3},{3,2},{4,5},{5,4},{6,7},{7,6},{8,9},{9,8},{10,11... | collective-permute-start | bytes 1572872 | tf_op jit(solution)/shard_map/ppermute | solution.py:671
  58.2 3.4 %collective-permute-start.12 = (bf16[256,1024]{1,0:T(8,128)(2,1)S(1)}, bf16[256,1024]{1,0:T(8,128)(2,1)S(1)}, u32[]{:S(2)}, u32[]{:S(2)}) collective-permute-start(bf16[256,1024]{1,0:T(8,128)(2,1)S(1)} %far_sum.4.refs_7_), channel_id=1, source_target_pairs={{0,1},{1,0},{2,3},{3,2},{4,5},{5,4},{6,7},{7,6},{8,9},{9,8},{10,11... | collective-permute-start | bytes 1572872 | tf_op jit(solution)/shard_map/ppermute | solution.py:671
  59.5 16.1 %collective-permute-start.15 = (bf16[256,1024]{1,0:T(8,128)(2,1)S(1)}, bf16[256,1024]{1,0:T(8,128)(2,1)S(1)}, u32[]{:S(2)}, u32[]{:S(2)}) collective-permute-start(bf16[256,1024]{1,0:T(8,128)(2,1)S(1)} %pair_sum.5.refs_19_.refs_0_), channel_id=1, source_target_pairs={{0,2},{1,3},{2,0},{3,1},{4,6},{5,7},{6,4},{7,5},{8,10},{9,11},{10,... | collective-permute-start | bytes 1572872 | tf_op jit(solution)/shard_map/ppermute | solution.py:671
  75.6 30.0 %copy-start.4 = (bf16[256,2048]{1,0:T(8,128)(2,1)}, bf16[256,2048]{1,0:T(8,128)(2,1)S(1)}, u32[]{:S(2)}) copy-start(bf16[256,2048]{1,0:T(8,128)(2,1)S(1)} %get-tuple-element.152.refs_4_.refs_2_) | copy-start | bytes 3145732
  75.7 2.0 collective-permute-start.16
  89.7 12.4 %collective-permute-start.17 = (bf16[1,192,512]{2,1,0:T(8,128)(2,1)S(1)}, bf16[1,192,512]{2,1,0:T(8,128)(2,1)S(1)}, u32[]{:S(2)}, u32[]{:S(2)}) collective-permute-start(bf16[1,192,512]{2,1,0:T(8,128)(2,1)S(1)} %bitcast.36), channel_id=1, source_target_pairs={{0,16},{4,20},{8,24},{12,28},{16,0},{20,4},{24,8},{28,12},{1,17},{... | collective-permute-start | bytes 589832 | tf_op jit(solution)/shard_map/ppermute | solution.py:671
  102.1 2.3 %collective-permute-start.18 = (bf16[256,1024]{1,0:T(8,128)(2,1)S(1)}, bf16[256,1024]{1,0:T(8,128)(2,1)S(1)}, u32[]{:S(2)}, u32[]{:S(2)}) collective-permute-start(bf16[256,1024]{1,0:T(8,128)(2,1)S(1)} %get-tuple-element.169), channel_id=1, source_target_pairs={{0,1},{1,0},{2,3},{3,2},{4,5},{5,4},{6,7},{7,6},{8,9},{9,8},{10,11... | collective-permute-start | bytes 1572872 | tf_op jit(solution)/shard_map/ppermute | solution.py:671
  102.2 11.6 %collective-permute-start.20 = (bf16[2,192,512]{2,1,0:T(8,128)(2,1)S(1)}, bf16[2,192,512]{2,1,0:T(8,128)(2,1)S(1)}, u32[]{:S(2)}, u32[]{:S(2)}) collective-permute-start(bf16[2,192,512]{2,1,0:T(8,128)(2,1)S(1)} %pad_maximum_fusion.refs_0_), channel_id=1, source_target_pairs={{0,4},{4,0},{8,12},{12,8},{16,20},{20,16},{24,28},{28,24},{1,5},{5... | collective-permute-start | bytes 1179656 | tf_op jit(solution)/shard_map/ppermute | solution.py:671
  104.0 11.2 %collective-permute-start.19 = (bf16[2,192,512]{2,1,0:T(8,128)(2,1)S(1)}, bf16[2,192,512]{2,1,0:T(8,128)(2,1)S(1)}, u32[]{:S(2)}, u32[]{:S(2)}) collective-permute-start(bf16[2,192,512]{2,1,0:T(8,128)(2,1)S(1)} %pad_maximum_fusion.refs_0_), channel_id=1, source_target_pairs={{0,8},{4,12},{8,0},{12,4},{16,24},{20,28},{24,16},{28,20},{1,9},{5... | collective-permute-start | bytes 1179656 | tf_op jit(solution)/shard_map/ppermute | solution.py:671
  104.5 15.4 %collective-permute-start.22 = (bf16[256,1024]{1,0:T(8,128)(2,1)S(1)}, bf16[256,1024]{1,0:T(8,128)(2,1)S(1)}, u32[]{:S(2)}, u32[]{:S(2)}) collective-permute-start(bf16[256,1024]{1,0:T(8,128)(2,1)S(1)} %pair_sum.6.refs_11_.refs_0_), channel_id=1, source_target_pairs={{0,2},{1,3},{2,0},{3,1},{4,6},{5,7},{6,4},{7,5},{8,10},{9,11},{10,... | collective-permute-start | bytes 1572872 | tf_op jit(solution)/shard_map/ppermute | solution.py:671
  115.3 5.4 %collective-permute-start.21 = (bf16[304,1024]{1,0:T(8,128)(2,1)S(1)}, bf16[304,1024]{1,0:T(8,128)(2,1)S(1)}, u32[]{:S(2)}, u32[]{:S(2)}) collective-permute-start(bf16[304,1024]{1,0:T(8,128)(2,1)S(1)} %get-tuple-element.172), channel_id=1, source_target_pairs={{0,1},{1,0},{2,3},{3,2},{4,5},{5,4},{6,7},{7,6},{8,9},{9,8},{10,11... | collective-permute-start | bytes 1867784 | tf_op jit(solution)/shard_map/ppermute | solution.py:671
  120.1 2.7 %collective-permute-start.24 = (bf16[256,1024]{1,0:T(8,128)(2,1)S(1)}, bf16[256,1024]{1,0:T(8,128)(2,1)S(1)}, u32[]{:S(2)}, u32[]{:S(2)}) collective-permute-start(bf16[256,1024]{1,0:T(8,128)(2,1)S(1)} %far_sum.6.refs_13_), channel_id=1, source_target_pairs={{0,1},{1,0},{2,3},{3,2},{4,5},{5,4},{6,7},{7,6},{8,9},{9,8},{10,11... | collective-permute-start | bytes 1572872 | tf_op jit(solution)/shard_map/ppermute | solution.py:671
  120.9 16.5 %collective-permute-start.23 = (bf16[304,1024]{1,0:T(8,128)(2,1)S(1)}, bf16[304,1024]{1,0:T(8,128)(2,1)S(1)}, u32[]{:S(2)}, u32[]{:S(2)}) collective-permute-start(bf16[304,1024]{1,0:T(8,128)(2,1)S(1)} %pair_sum.7.refs_34_.refs_0_), channel_id=1, source_target_pairs={{0,2},{1,3},{2,0},{3,1},{4,6},{5,7},{6,4},{7,5},{8,10},{9,11},{10,... | collective-permute-start | bytes 1867784 | tf_op jit(solution)/shard_map/ppermute | solution.py:671
  122.4 11.3 %collective-permute-start.26 = (bf16[2,192,512]{2,1,0:T(8,128)(2,1)S(1)}, bf16[2,192,512]{2,1,0:T(8,128)(2,1)S(1)}, u32[]{:S(2)}, u32[]{:S(2)}) collective-permute-start(bf16[2,192,512]{2,1,0:T(8,128)(2,1)S(1)} %collective-permute-done.19.refs_1_), channel_id=1, source_target_pairs={{0,4},{4,0},{8,12},{12,8},{16,20},{20,16},{24,28},{28,24},{1,5},{5... | collective-permute-start | bytes 1179656 | tf_op jit(solution)/shard_map/ppermute | solution.py:671
  133.7 3.9 %collective-permute-start.27 = (bf16[256,1024]{1,0:T(8,128)(2,1)S(1)}, bf16[256,1024]{1,0:T(8,128)(2,1)S(1)}, u32[]{:S(2)}, u32[]{:S(2)}) collective-permute-start(bf16[256,1024]{1,0:T(8,128)(2,1)S(1)} %get-tuple-element.197), channel_id=1, source_target_pairs={{0,1},{1,0},{2,3},{3,2},{4,5},{5,4},{6,7},{7,6},{8,9},{9,8},{10,11... | collective-permute-start | bytes 1572872 | tf_op jit(solution)/shard_map/ppermute | solution.py:671
  137.5 3.1 %collective-permute-start.25 = (bf16[304,1024]{1,0:T(8,128)(2,1)S(1)}, bf16[304,1024]{1,0:T(8,128)(2,1)S(1)}, u32[]{:S(2)}, u32[]{:S(2)}) collective-permute-start(bf16[304,1024]{1,0:T(8,128)(2,1)S(1)} %far_sum.7.refs_13_), channel_id=1, source_target_pairs={{0,1},{1,0},{2,3},{3,2},{4,5},{5,4},{6,7},{7,6},{8,9},{9,8},{10,11... | collective-permute-start | bytes 1867784 | tf_op jit(solution)/shard_map/ppermute | solution.py:671
  137.7 12.8 %collective-permute-start.29 = (bf16[256,512]{1,0:T(8,128)(2,1)S(1)}, bf16[256,512]{1,0:T(8,128)(2,1)S(1)}, u32[]{:S(2)}, u32[]{:S(2)}) collective-permute-start(bf16[256,512]{1,0:T(8,128)(2,1)S(1)} %high_sum.4.refs_36_), channel_id=1, source_target_pairs={{0,2},{1,3},{2,0},{3,1},{4,6},{5,7},{6,4},{7,5},{8,10},{9,11},{10,... | collective-permute-start | bytes 786440 | tf_op jit(solution)/shard_map/ppermute | solution.py:671
  139.2 11.3 %collective-permute-start.28 = (bf16[1,48,1024]{2,1,0:T(8,128)(2,1)S(1)}, bf16[1,48,1024]{2,1,0:T(8,128)(2,1)S(1)}, u32[]{:S(2)}, u32[]{:S(2)}) collective-permute-start(bf16[1,48,1024]{2,1,0:T(8,128)(2,1)S(1)} %slice_bitcast_fusion), channel_id=1, source_target_pairs={{0,16},{4,20},{8,24},{12,28},{16,0},{20,4},{24,8},{28,12},{1,17},{... | collective-permute-start | bytes 294920 | tf_op jit(solution)/shard_map/ppermute | solution.py:671
  150.5 5.4 %collective-permute-start.32 = (bf16[256,1024]{1,0:T(8,128)(2,1)S(1)}, bf16[256,1024]{1,0:T(8,128)(2,1)S(1)}, u32[]{:S(2)}, u32[]{:S(2)}) collective-permute-start(bf16[256,1024]{1,0:T(8,128)(2,1)S(1)} %get-tuple-element.204), channel_id=1, source_target_pairs={{0,1},{1,0},{2,3},{3,2},{4,5},{5,4},{6,7},{7,6},{8,9},{9,8},{10,11... | collective-permute-start | bytes 1572872 | tf_op jit(solution)/shard_map/ppermute | solution.py:671
  150.6 2.2 collective-permute-start.30
  152.8 4.9 %collective-permute-start.31 = (bf16[96,512]{1,0:T(8,128)(2,1)S(1)}, bf16[96,512]{1,0:T(8,128)(2,1)S(1)}, u32[]{:S(2)}, u32[]{:S(2)}) collective-permute-start(bf16[96,512]{1,0:T(8,128)(2,1)S(1)} %high_sum.5.refs_2_), channel_id=1, source_target_pairs={{0,2},{1,3},{2,0},{3,1},{4,6},{5,7},{6,4},{7,5},{8,10},{9,11},{10,... | collective-permute-start | bytes 294920 | tf_op jit(solution)/shard_map/ppermute | solution.py:671
  154.1 7.7 %collective-permute-start.36 = (bf16[2,48,1024]{2,1,0:T(8,128)(2,1)S(1)}, bf16[2,48,1024]{2,1,0:T(8,128)(2,1)S(1)}, u32[]{:S(2)}, u32[]{:S(2)}) collective-permute-start(bf16[2,48,1024]{2,1,0:T(8,128)(2,1)S(1)} %pad_maximum_fusion.2), channel_id=1, source_target_pairs={{0,8},{4,12},{8,0},{12,4},{16,24},{20,28},{24,16},{28,20},{1,9},{5... | collective-permute-start | bytes 589832 | tf_op jit(solution)/shard_map/ppermute | solution.py:671
  155.9 11.1 %collective-permute-start.33 = (bf16[256,512]{1,0:T(8,128)(2,1)S(1)}, bf16[256,512]{1,0:T(8,128)(2,1)S(1)}, u32[]{:S(2)}, u32[]{:S(2)}) collective-permute-start(bf16[256,512]{1,0:T(8,128)(2,1)S(1)} %high_sum.6), channel_id=1, source_target_pairs={{0,2},{1,3},{2,0},{3,1},{4,6},{5,7},{6,4},{7,5},{8,10},{9,11},{10,... | collective-permute-start | bytes 786440 | tf_op jit(solution)/shard_map/ppermute | solution.py:671
  157.7 9.3 %collective-permute-start.34 = (bf16[1,112,512]{2,1,0:T(8,128)(2,1)S(1)}, bf16[1,112,512]{2,1,0:T(8,128)(2,1)S(1)}, u32[]{:S(2)}, u32[]{:S(2)}) collective-permute-start(bf16[1,112,512]{2,1,0:T(8,128)(2,1)S(1)} %maximum_bitcast_fusion.refs_6_), channel_id=1, source_target_pairs={{0,16},{4,20},{8,24},{12,28},{16,0},{20,4},{24,8},{28,12},{1,17},{... | collective-permute-start | bytes 344072 | tf_op jit(solution)/shard_map/ppermute | solution.py:671
  161.8 11.3 %collective-permute-start.37 = (bf16[4,48,1024]{2,1,0:T(8,128)(2,1)S(1)}, bf16[4,48,1024]{2,1,0:T(8,128)(2,1)S(1)}, u32[]{:S(2)}, u32[]{:S(2)}) collective-permute-start(bf16[4,48,1024]{2,1,0:T(8,128)(2,1)S(1)} %constant_dynamic-update-slice_fusion.2.refs_4_), channel_id=1, source_target_pairs={{0,4},{4,0},{8,12},{12,8},{16,20},{20,16},{24,28},{28,24},{1,5},{5... | collective-permute-start | bytes 1179656 | tf_op jit(solution)/shard_map/ppermute | solution.py:671
  167.0 6.1 %collective-permute-start.35 = (bf16[2,112,512]{2,1,0:T(8,128)(2,1)S(1)}, bf16[2,112,512]{2,1,0:T(8,128)(2,1)S(1)}, u32[]{:S(2)}, u32[]{:S(2)}) collective-permute-start(bf16[2,112,512]{2,1,0:T(8,128)(2,1)S(1)} %pad_maximum_fusion.1), channel_id=1, source_target_pairs={{0,8},{4,12},{8,0},{12,4},{16,24},{20,28},{24,16},{28,20},{1,9},{5... | collective-permute-start | bytes 688136 | tf_op jit(solution)/shard_map/ppermute | solution.py:671
  168.9 9.7 %collective-permute-start.39 = (bf16[256,1024]{1,0:T(8,128)(2,1)}, bf16[256,1024]{1,0:T(8,128)(2,1)}, u32[]{:S(2)}, u32[]{:S(2)}) collective-permute-start(bf16[256,1024]{1,0:T(8,128)(2,1)} %get-tuple-element.217.refs_35_), channel_id=1, source_target_pairs={{0,1},{1,0},{2,3},{3,2},{4,5},{5,4},{6,7},{7,6},{8,9},{9,8},{10,11... | collective-permute-start | bytes 1572872 | tf_op jit(solution)/shard_map/ppermute | solution.py:671
  168.9 9.7 %collective-permute-start.38 = (bf16[256,1024]{1,0:T(8,128)(2,1)}, bf16[256,1024]{1,0:T(8,128)(2,1)}, u32[]{:S(2)}, u32[]{:S(2)}) collective-permute-start(bf16[256,1024]{1,0:T(8,128)(2,1)} %get-tuple-element.210), channel_id=1, source_target_pairs={{0,1},{1,0},{2,3},{3,2},{4,5},{5,4},{6,7},{7,6},{8,9},{9,8},{10,11... | collective-permute-start | bytes 1572872 | tf_op jit(solution)/shard_map/ppermute | solution.py:671
  174.5 18.1 %all-to-all-start.1 = ((bf16[8,64,512]{2,1,0:T(8,128)(2,1)}), bf16[8,64,512]{2,1,0:T(8,128)(2,1)S(1)}, u32[]{:S(2)}, u32[]{:S(2)}) async-start(bf16[8,64,512]{2,1,0:T(8,128)(2,1)} %bitcast.35), calls=%async_computation.1 | async-start | bytes 1048576 | tf_op jit(solution)/shard_map/all_to_all | solution.py:826
  180.0 10.3 %collective-permute-start.40 = (bf16[512,512]{1,0:T(8,128)(2,1)S(1)}, bf16[512,512]{1,0:T(8,128)(2,1)S(1)}, u32[]{:S(2)}, u32[]{:S(2)}) collective-permute-start(bf16[512,512]{1,0:T(8,128)(2,1)S(1)} %high_sum.7), channel_id=1, source_target_pairs={{0,2},{1,3},{2,0},{3,1},{4,6},{5,7},{6,4},{7,5},{8,10},{9,11},{10,... | collective-permute-start | bytes 1572872 | tf_op jit(solution)/shard_map/ppermute | solution.py:671
  180.9 2.5 %collective-permute-start.41 = (bf16[4,48,1024]{2,1,0:T(8,128)(2,1)S(1)}, bf16[4,48,1024]{2,1,0:T(8,128)(2,1)S(1)}, u32[]{:S(2)}, u32[]{:S(2)}) collective-permute-start(bf16[4,48,1024]{2,1,0:T(8,128)(2,1)S(1)} %copy-done.33), channel_id=1, source_target_pairs={{0,1},{1,0},{2,3},{3,2},{4,5},{5,4},{6,7},{7,6},{8,9},{9,8},{10,11... | collective-permute-start | bytes 1179656 | tf_op jit(solution)/shard_map/ppermute | solution.py:671
  180.9 2.5 %collective-permute-start.42 = (bf16[4,48,1024]{2,1,0:T(8,128)(2,1)S(1)}, bf16[4,48,1024]{2,1,0:T(8,128)(2,1)S(1)}, u32[]{:S(2)}, u32[]{:S(2)}) collective-permute-start(bf16[4,48,1024]{2,1,0:T(8,128)(2,1)S(1)} %collective-permute-done.37.refs_15_.refs_5_), channel_id=1, source_target_pairs={{0,1},{1,0},{2,3},{3,2},{4,5},{5,4},{6,7},{7,6},{8,9},{9,8},{10,11... | collective-permute-start | bytes 1179656 | tf_op jit(solution)/shard_map/ppermute | solution.py:671
  181.4 18.2 %collective-permute-start.43 = (bf16[4,112,512]{2,1,0:T(8,128)(2,1)S(1)}, bf16[4,112,512]{2,1,0:T(8,128)(2,1)}, u32[]{:S(2)}, u32[]{:S(2)}) collective-permute-start(bf16[4,112,512]{2,1,0:T(8,128)(2,1)S(1)} %constant_dynamic-update-slice_fusion.refs_14_.refs_0_), channel_id=1, source_target_pairs={{0,4},{4,0},{8,12},{12,8},{16,20},{20,16},{24,28},{28,24},{1,5},{5... | collective-permute-start | bytes 1376264 | tf_op jit(solution)/shard_map/ppermute | solution.py:671
  192.6 22.5 %all-to-all-start.2 = ((bf16[8,64,512]{2,1,0:T(8,128)(2,1)}), bf16[8,64,512]{2,1,0:T(8,128)(2,1)S(1)}, u32[]{:S(2)}, u32[]{:S(2)}) async-start(bf16[8,64,512]{2,1,0:T(8,128)(2,1)} %bitcast.14), calls=%async_computation.2 | async-start | bytes 1048576 | tf_op jit(solution)/shard_map/all_to_all | solution.py:826
  198.3 8.0 %collective-permute-start.46 = (bf16[4,64,512]{2,1,0:T(8,128)(2,1)S(1)}, bf16[4,64,512]{2,1,0:T(8,128)(2,1)S(1)}, u32[]{:S(2)}, u32[]{:S(2)}) collective-permute-start(bf16[4,64,512]{2,1,0:T(8,128)(2,1)S(1)} %slice.34.refs_2_), channel_id=1, source_target_pairs={{0,2},{1,3},{2,0},{3,1},{4,6},{5,7},{6,4},{7,5},{8,10},{9,11},{10,... | collective-permute-start | bytes 786440 | tf_op jit(solution)/shard_map/ppermute | solution.py:671
  200.6 8.5 %collective-permute-start.47 = (bf16[4,64,512]{2,1,0:T(8,128)(2,1)S(1)}, bf16[4,64,512]{2,1,0:T(8,128)(2,1)S(1)}, u32[]{:S(2)}, u32[]{:S(2)}) collective-permute-start(bf16[4,64,512]{2,1,0:T(8,128)(2,1)S(1)} %slice.35.refs_3_), channel_id=1, source_target_pairs={{0,2},{1,3},{2,0},{3,1},{4,6},{5,7},{6,4},{7,5},{8,10},{9,11},{10,... | collective-permute-start | bytes 786440 | tf_op jit(solution)/shard_map/ppermute | solution.py:671
  201.5 9.1 %collective-permute-start.44 = (bf16[4,64,512]{2,1,0:T(8,128)(2,1)S(1)}, bf16[4,64,512]{2,1,0:T(8,128)(2,1)S(1)}, u32[]{:S(2)}, u32[]{:S(2)}) collective-permute-start(bf16[4,64,512]{2,1,0:T(8,128)(2,1)S(1)} %slice.34.refs_2_), channel_id=1, source_target_pairs={{0,1},{1,0},{2,3},{3,2},{4,5},{5,4},{6,7},{7,6},{8,9},{9,8},{10,11... | collective-permute-start | bytes 786440 | tf_op jit(solution)/shard_map/ppermute | solution.py:671
  206.3 4.2 %collective-permute-start.48 = (bf16[4,64,512]{2,1,0:T(8,128)(2,1)S(1)}, bf16[4,64,512]{2,1,0:T(8,128)(2,1)S(1)}, u32[]{:S(2)}, u32[]{:S(2)}) collective-permute-start(bf16[4,64,512]{2,1,0:T(8,128)(2,1)S(1)} %collective-permute-done.46.refs_6_), channel_id=1, source_target_pairs={{0,1},{1,0},{2,3},{3,2},{4,5},{5,4},{6,7},{7,6},{8,9},{9,8},{10,11... | collective-permute-start | bytes 786440 | tf_op jit(solution)/shard_map/ppermute | solution.py:671
  206.3 4.2 %collective-permute-start.45 = (bf16[4,64,512]{2,1,0:T(8,128)(2,1)S(1)}, bf16[4,64,512]{2,1,0:T(8,128)(2,1)S(1)}, u32[]{:S(2)}, u32[]{:S(2)}) collective-permute-start(bf16[4,64,512]{2,1,0:T(8,128)(2,1)S(1)} %slice.35.refs_3_), channel_id=1, source_target_pairs={{0,1},{1,0},{2,3},{3,2},{4,5},{5,4},{6,7},{7,6},{8,9},{9,8},{10,11... | collective-permute-start | bytes 786440 | tf_op jit(solution)/shard_map/ppermute | solution.py:671
  209.1 1.5 collective-permute-start.49
  (63 other events, 410.8 us)

commit v15 on v14

--- a/solution.py
+++ b/solution.py
@@ -779,7 +779,7 @@
         pairs = [v for p in saved[:c + 1] for v in (p[2], p[5])]
         z_keep, z_send, *kept[c] = call(
             functools.partial(attend_kernel, c), info, (wo,), (saved[c][1], oa, ob, *pairs), outs, like(wo),
-            "attend_%d" % c, 10, (saved[c][0],), (1,))
+            "attend_%d" % c, 10, (saved[c][0], gs[1], gs[3]) if c else (saved[c][0],), (1,))
         z_own[c] = pair_sum(z_keep, late(z_send, z_far[0] if c else there[-1]))
         z_far[c] = far(z_own[c])
         order = (kept[c][1], z_own[c])

time: 217 us -> 217 us (level)
    unnamed x150 -> x158, local copies, waits for them, and re-layouts: 4.24 us -> 4.97 us
where the time goes in v15:
time: 217 us
  Pallas kernels  106 us (49%)
  starting transfers between devices  52.5 us (24%)
  waiting for transfers between devices  47.6 us (22%)
  local copies, waits for them, and re-layouts  6.04 us (3%)
  other arithmetic  2.31 us (1%)
    pallas_call x26, Pallas kernels, call(): pl.pallas_call(body, in_specs=[pl.BlockSpec(memory_space=pltpu.SMEM)] * n...  90.7 us
    ppermute x50, waiting for transfers between devices, swap(): return lax.ppermute(value, axis, [(i, i ^ bit) for i in range(size)])  41.4 us
    ppermute x50, starting transfers between devices, swap(): return lax.ppermute(value, axis, [(i, i ^ bit) for i in range(size)])  35.1 us
    all_to_all x2, starting transfers between devices, to_bands(): lax.all_to_all(value.reshape(dp, length // dp, QUARTER), 'dp', split_axis...  10.1 us
    pallas_call x2, Pallas kernels, sum_call(): pl.pallas_call(functools.partial(kernel, [len(group) for group in groups]...  8.53 us
    all_to_all x1, starting transfers between devices, shards(): lax.all_to_all(ordered, 'dp', split_axis=0, concat_axis=1, tiled=True)[0]  7.26 us
    all_to_all x1, waiting for transfers between devices, shards(): lax.all_to_all(ordered, 'dp', split_axis=0, concat_axis=1, tiled=True)[0]  6.18 us
    pallas_call x3, Pallas kernels, move_rows(): pl.pallas_call(kernel, in_specs=[pl.BlockSpec(memory_space=pltpu.SMEM), p...  5.25 us
  transfers between devices with their start and end apart: 53, of which 21 were waited for; matrix products, arithmetic and copies ran while one was open for 2% of the time, Pallas kernels for 42%

profile of v15, /device:TPU:0, one launch (start us, length us, event | category | flops | bytes accessed | tf_op | source)
XLA Modules:
  0.0 216.7 jit_solution(1949688358024846277)
XLA Ops:
  0.7 0.7 copy-done.68
  1.4 2.5 %deal.1 = bf16[8,64,512]{2,1,0:T(8,128)(2,1)} custom-call(s32[8]{0:T(128)S(1)} %copy-done.68, bf16[8,64,512]{2,1,0:T(8,128)(2,1)} %source.1), custom_call_target="tpu_custom_call" | custom-call | flops 1000 | bytes 1000 | tf_op jit(solution)/shard_map/deal/pallas_call | solution.py:599
  3.9 7.3 %all-to-all-start = ((bf16[8,64,512]{2,1,0:T(8,128)(2,1)}), bf16[8,64,512]{2,1,0:T(8,128)(2,1)S(1)}, u32[]{:S(2)}, u32[]{:S(2)}) async-start(bf16[8,64,512]{2,1,0:T(8,128)(2,1)} %deal.1), calls=%async_computation | async-start | bytes 1048576 | tf_op jit(solution)/shard_map/all_to_all | solution.py:750
  11.3 1.6 collective-permute-start.1
  14.2 0.7 collective-permute-done.1
  14.9 1.4 pad_add_fusion.info.refs_0_
  16.3 1.8 adapters.1
  19.4 6.2 %all-to-all-done = bf16[8,64,512]{2,1,0:T(8,128)(2,1)S(1)} async-done(((bf16[8,64,512]{2,1,0:T(8,128)(2,1)}), bf16[8,64,512]{2,1,0:T(8,128)(2,1)S(1)}, u32[]{:S(2)}, u32[]{:S(2)}) %all-to-all-start) | async-done | bytes 524320 | tf_op jit(solution)/shard_map/all_to_all | solution.py:750
  25.7 1.6 collective-permute-start.4
  27.2 5.2 %collective-permute-done.4.refs_5_.refs_6_ = bf16[256,512]{1,0:T(8,128)(2,1)S(1)} collective-permute-done((bf16[256,512]{1,0:T(8,128)(2,1)S(1)}, bf16[256,512]{1,0:T(8,128)(2,1)S(1)}, u32[]{:S(2)}, u32[]{:S(2)}) %collective-permute-start.4) | collective-permute-done | bytes 262176 | tf_op jit(solution)/shard_map/ppermute | solution.py:671
  32.5 1.5 collective-permute-start.9
  34.0 4.1 %project_0.1 = (bf16[48,256]{1,0:T(8,128)(2,1)S(1)}, bf16[512,256]{1,0:T(8,128)(2,1)S(1)}, bf16[2,256,64]{2,1,0:T(8,128)(2,1)S(1)}, bf16[2,256,64]{2,1,0:T(8,128...) custom-call(s32[4]{0:T(128)S(1)} %pad_add_fusion.info.refs_0_, bf16[2048,512]{1,0:T(8,128)(2,1)} %refs_1_.15, ...), custom_call_target="tpu_custom_call" | custom-call | flops 1000 | bytes 1000 | tf_op jit(solution)/shard_map/project_0/pallas_call | solution.py:632
  38.2 3.1 %attend_0.1 = (f32[256,1024]{1,0:T(8,128)S(1)}, bf16[256,1024]{1,0:T(8,128)(2,1)S(1)}, bf16[512,256]{1,0:T(8,128)(2,1)S(1)}, f32[8,256]{1,0:T(8,128)S(1)}, bf16[16,256]{1,0:T(8,128)(2,1)S(1)}) custom-call(s32[4]{0:T(128)S(1)} %pad_add_fusion.info.refs_0_, bf16[512,2048]{1,0:T(8,128)(2,1)} %refs_3_.5, ...), custom_call_target="tpu_custom_call" | custom-call | flops 1000 | bytes 1000 | tf_op jit(solution)/shard_map/attend_0/pallas_call | solution.py:632
  42.7 1.2 collective-permute-done.10.refs_1_
  44.1 1.5 collective-permute-start.11
  45.6 1.5 collective-permute-done.13.refs_6_.refs_7_
  47.2 4.1 %project_1.1 = (bf16[48,256]{1,0:T(8,128)(2,1)S(1)}, bf16[512,256]{1,0:T(8,128)(2,1)S(1)}, bf16[2,256,64]{2,1,0:T(8,128)(2,1)S(1)}, bf16[2,256,64]{2,1,0:T(8,128...) custom-call(s32[4]{0:T(128)S(1)} %pad_add_fusion.info.refs_0_, bf16[2048,512]{1,0:T(8,128)(2,1)} %refs_1_.15, ...), custom_call_target="tpu_custom_call" | custom-call | flops 1000 | bytes 1000 | tf_op jit(solution)/shard_map/project_1/pallas_call | solution.py:632
  51.4 3.7 %attend_1.1 = (f32[256,1024]{1,0:T(8,128)S(1)}, bf16[256,1024]{1,0:T(8,128)(2,1)S(1)}, bf16[512,256]{1,0:T(8,128)(2,1)S(1)}, f32[8,256]{1,0:T(8,128)S(1)}, bf16[16,256]{1,0:T(8,128)(2,1)S(1)}) custom-call(s32[4]{0:T(128)S(1)} %pad_add_fusion.info.refs_0_, bf16[512,2048]{1,0:T(8,128)(2,1)} %refs_3_.5, ...), custom_call_target="tpu_custom_call" | custom-call | flops 1000 | bytes 1000 | tf_op jit(solution)/shard_map/attend_1/pallas_call | solution.py:632
  55.2 3.0 %collective-permute-done.11.refs_1_ = bf16[256,1024]{1,0:T(8,128)(2,1)S(1)} collective-permute-done((bf16[256,1024]{1,0:T(8,128)(2,1)S(1)}, bf16[256,1024]{1,0:T(8,128)(2,1)S(1)}, u32[]{:S(2)}, u32[]{:S(2)}) %collective-permute-start.11) | collective-permute-done | bytes 524320 | tf_op jit(solution)/shard_map/ppermute | solution.py:671
  58.9 1.1 collective-permute-done.14.refs_1_
  60.2 1.5 collective-permute-start.15
  61.7 13.0 %front_0.1 = (bf16[256,2048]{1,0:T(8,128)(2,1)S(1)}, f32[256,512]{1,0:T(8,128)S(1)}, bf16[256,2048]{1,0:T(8,128)(2,1)S(1)}, bf16[256,2048]{1,0:T(8,128)(2,1)S(1)...) custom-call(s32[4]{0:T(128)S(1)} %pad_add_fusion.info.refs_0_, ...), custom_call_target="tpu_custom_call" | custom-call | flops 1000 | bytes 1000 | tf_op jit(solution)/shard_map/front_0/pallas_call | solution.py:632
  74.7 1.0 copy-done.25
  75.9 1.9 collective-permute-done.16.refs_8_
  77.8 12.0 %front_1.1 = (bf16[256,2048]{1,0:T(8,128)(2,1)S(1)}, f32[256,512]{1,0:T(8,128)S(1)}, bf16[256,2048]{1,0:T(8,128)(2,1)S(1)}, bf16[256,2048]{1,0:T(8,128)(2,1)S(1)...) custom-call(s32[4]{0:T(128)S(1)} %pad_add_fusion.info.refs_0_, ...), custom_call_target="tpu_custom_call" | custom-call | flops 1000 | bytes 1000 | tf_op jit(solution)/shard_map/front_1/pallas_call | solution.py:632
  89.8 2.1 collective-permute-start.17
  91.9 7.9 %back_1.1 = (f32[256,16]{1,0:T(8,128)S(1)}, f32[256,1024]{1,0:T(8,128)S(1)}, bf16[256,1024]{1,0:T(8,128)(2,1)S(1)}, f32[48,2048]{1,0:T(8,128)S(1)}) custom-call(s32[4]{0:T(128)S(1)} %pad_add_fusion.info.refs_0_, bf16[2,2048,2048]{2,1,0:T(8,128)(2,1)S(1)} %get-tuple-element.149.refs_1_, bf16[256,2048]{1,0:T(8,128)(2,1)S(1)} %get-tuple-element.159.refs_2_, ...), custom_call_target="tpu_custom_call" | custom-call | flops 1000 | bytes 1000 | tf_op jit(solution)/shard_map/back_1/pallas_call | solution.py:632
  99.8 2.1 collective-permute-done.17
  102.0 2.1 collective-permute-start.20
  104.2 1.0 collective-permute-start.22
  105.2 7.9 %back_0.1 = (f32[256,16]{1,0:T(8,128)S(1)}, f32[304,1024]{1,0:T(8,128)S(1)}, bf16[304,1024]{1,0:T(8,128)(2,1)S(1)}) custom-call(s32[4]{0:T(128)S(1)} %pad_add_fusion.info.refs_0_, bf16[2,2048,2048]{2,1,0:T(8,128)(2,1)S(1)} %get-tuple-element.149.refs_1_, bf16[256,2048]{1,0:T(8,128)(2,1)S(1)} %get-tuple-element.150.refs_2_, ...), custom_call_target="tpu_custom_call" | custom-call | flops 1000 | bytes 1000 | tf_op jit(solution)/shard_map/back_0/pallas_call | solution.py:632
  113.9 1.5 collective-permute-done.19.refs_1_
  115.4 4.5 %down_1.1 = (f32[256,1024]{1,0:T(8,128)S(1)}, bf16[256,1024]{1,0:T(8,128)(2,1)}) custom-call(s32[4]{0:T(128)S(1)} %pad_add_fusion.info.refs_0_, bf16[2048,2048]{1,0:T(8,128)(2,1)S(1)} %bitcast.19, bf16[256,2048]{1,0:T(8,128)(2,1)S(1)} %get-tuple-element.161.refs_4_.refs_2_, f32[256,16]{1,0:T(8,128)S(1)} %get-tuple-element.173.refs_3_, ...), custom_call_target="tpu_custom_call" | custom-call | flops 1000 | bytes 1000 | tf_op jit(solution)/shard_map/down_1/pallas_call | solution.py:632
  122.3 10.7 %attend_back_1.1 = (f32[256,512]{1,0:T(8,128)S(1)}, f32[256,1024]{1,0:T(8,128)S(1)}, bf16[256,1024]{1,0:T(8,128)(2,1)S(1)}, f32[256,1]{1,0:T(8,128)S(1)}, f32[48...) custom-call(s32[4]{0:T(128)S(1)} %pad_add_fusion.info.refs_0_, ...), custom_call_target="tpu_custom_call" | custom-call | flops 1000 | bytes 1000 | tf_op jit(solution)/shard_map/attend_back_1/pallas_call | solution.py:632
  133.6 3.9 %collective-permute-done.23.refs_1_ = bf16[304,1024]{1,0:T(8,128)(2,1)S(1)} collective-permute-done((bf16[304,1024]{1,0:T(8,128)(2,1)S(1)}, bf16[304,1024]{1,0:T(8,128)(2,1)S(1)}, u32[]{:S(2)}, u32[]{:S(2)}) %collective-permute-start.23) | collective-permute-done | bytes 622624 | tf_op jit(solution)/shard_map/ppermute | solution.py:671
  138.4 2.1 collective-permute-start.28
  140.6 9.8 %attend_back_0.1 = (f32[256,512]{1,0:T(8,128)S(1)}, f32[256,1024]{1,0:T(8,128)S(1)}, bf16[256,1024]{1,0:T(8,128)(2,1)S(1)}, f32[256,1]{1,0:T(8,128)S(1)}, bf16[4...) custom-call(s32[4]{0:T(128)S(1)} %pad_add_fusion.info.refs_0_, ...), custom_call_target="tpu_custom_call" | custom-call | flops 1000 | bytes 1000 | tf_op jit(solution)/shard_map/attend_back_0/pallas_call | solution.py:632
  151.0 1.7 collective-permute-done.30.refs_1_
  152.7 0.8 collective-permute-start.31
  153.5 1.6 collective-permute-start.36
  155.2 1.5 collective-permute-start.33
  156.7 1.0 collective-permute-done.31.refs_3_
  157.8 0.8 collective-permute-start.34
  158.6 1.8 collective-permute-done.36
  161.1 4.5 %down_0.1 = (f32[256,1024]{1,0:T(8,128)S(1)}, bf16[256,1024]{1,0:T(8,128)(2,1)}) custom-call(s32[4]{0:T(128)S(1)} %pad_add_fusion.info.refs_0_, bf16[2048,2048]{1,0:T(8,128)(2,1)S(1)} %bitcast.19, bf16[256,2048]{1,0:T(8,128)(2,1)S(1)} %copy-done.5, f32[256,16]{1,0:T(8,128)S(1)} %get-tuple-element.175.refs_6_.refs_3_, ...), custom_call_target="tpu_custom_call" | custom-call | flops 1000 | bytes 1000 | tf_op jit(solution)/shard_map/down_0/pallas_call | solution.py:632
  165.6 2.5 %collective-permute-start.35 = (bf16[2,112,512]{2,1,0:T(8,128)(2,1)S(1)}, bf16[2,112,512]{2,1,0:T(8,128)(2,1)S(1)}, u32[]{:S(2)}, u32[]{:S(2)}) collective-permute-start(bf16[2,112,512]{2,1,0:T(8,128)(2,1)S(1)} %pad_maximum_fusion.1), channel_id=1, source_target_pairs={{0,8},{4,12},{8,0},{12,4},{16,24},{20,28},{24,16},{28,20},{1,9},{5... | collective-permute-start | bytes 688136 | tf_op jit(solution)/shard_map/ppermute | solution.py:671
  168.7 3.5 %collective-permute-done.35 = bf16[2,112,512]{2,1,0:T(8,128)(2,1)S(1)} collective-permute-done((bf16[2,112,512]{2,1,0:T(8,128)(2,1)S(1)}, bf16[2,112,512]{2,1,0:T(8,128)(2,1)S(1)}, u32[]{:S(2)}, u32[]{:S(2)}) %collective-permute-start.35) | collective-permute-done | bytes 229408 | tf_op jit(solution)/shard_map/ppermute | solution.py:671
  172.8 0.8 copy-done.16
  173.6 4.4 %all-to-all-start.1 = ((bf16[8,64,512]{2,1,0:T(8,128)(2,1)}), bf16[8,64,512]{2,1,0:T(8,128)(2,1)S(1)}, u32[]{:S(2)}, u32[]{:S(2)}) async-start(bf16[8,64,512]{2,1,0:T(8,128)(2,1)} %bitcast.35), calls=%async_computation.1 | async-start | bytes 1048576 | tf_op jit(solution)/shard_map/all_to_all | solution.py:826
  178.1 1.4 high_sum.7
  179.5 1.3 collective-permute-start.40
  181.3 2.0 collective-permute-start.43
  183.4 4.0 %feedforward_sum.1 = (f32[8,32,2048]{2,1,0:T(8,128)}, f32[8,16,2048]{2,1,0:T(8,128)}, f32[8,2,16,2048]{3,2,1,0:T(8,128)}, f32[8,16,2048]{2,1,0:T(8,128)}) custom-call(s32[4]{0:T(128)S(1)} %pad_add_fusion.info.refs_0_, s32[8]{0:T(128)S(1)} %copy-done.71, bf16[2,192,512]{2,1,0:T(8,128)(2,1)S(1)} %copy-done.18, bf16[2,192,512]{2,1,0:T(8,128)(2,1)S(1)} %copy-done.42, ...), custom_call_target="tpu_custom_call" | custom-call | bytes 12000000 | tf_op jit(solution)/shard_map/feedforward_sum/pallas_call | solution.py:655
  187.4 2.9 %collective-permute-done.40.refs_1_ = bf16[512,512]{1,0:T(8,128)(2,1)S(1)} collective-permute-done((bf16[512,512]{1,0:T(8,128)(2,1)S(1)}, bf16[512,512]{1,0:T(8,128)(2,1)S(1)}, u32[]{:S(2)}, u32[]{:S(2)}) %collective-permute-start.40) | collective-permute-done | bytes 524320 | tf_op jit(solution)/shard_map/ppermute | solution.py:671
  190.3 2.2 %output.1 = bf16[512,512]{1,0:T(8,128)(2,1)} custom-call(s32[4]{0:T(128)S(1)} %pad_add_fusion.info.refs_0_, bf16[512,512]{1,0:T(8,128)(2,1)S(1)} %collective-permute-done.40.refs_1_, f32[256,1024]{1,0:T(8,128)S(1)} %get-tuple-element.214.refs_0_.refs_2_, bf16[256,1024]{1,0:T(8,128)(2,1)} %collective-permute-done.38.refs_1_.refs_3_, ...), custom_call_target="tpu_custom_call" | custom-call | flops 1000 | bytes 1000 | tf_op jit(solution)/shard_map/output/pallas_call | solution.py:632
  192.5 5.7 %all-to-all-start.2 = ((bf16[8,64,512]{2,1,0:T(8,128)(2,1)}), bf16[8,64,512]{2,1,0:T(8,128)(2,1)S(1)}, u32[]{:S(2)}, u32[]{:S(2)}) async-start(bf16[8,64,512]{2,1,0:T(8,128)(2,1)} %bitcast.14), calls=%async_computation.2 | async-start | bytes 1048576 | tf_op jit(solution)/shard_map/all_to_all | solution.py:826
  198.3 0.8 collective-permute-start.46
  199.1 1.0 slice.35.refs_3_
  200.1 1.3 collective-permute-start.47
  201.4 4.9 %collective-permute-done.46.refs_6_ = bf16[4,64,512]{2,1,0:T(8,128)(2,1)S(1)} collective-permute-done((bf16[4,64,512]{2,1,0:T(8,128)(2,1)S(1)}, bf16[4,64,512]{2,1,0:T(8,128)(2,1)S(1)}, u32[]{:S(2)}, u32[]{:S(2)}) %collective-permute-start.46) | collective-permute-done | bytes 262176 | tf_op jit(solution)/shard_map/ppermute | solution.py:671
  206.8 2.3 %collective-permute-done.47.refs_7_ = bf16[4,64,512]{2,1,0:T(8,128)(2,1)S(1)} collective-permute-done((bf16[4,64,512]{2,1,0:T(8,128)(2,1)S(1)}, bf16[4,64,512]{2,1,0:T(8,128)(2,1)S(1)}, u32[]{:S(2)}, u32[]{:S(2)}) %collective-permute-start.47) | collective-permute-done | bytes 262176 | tf_op jit(solution)/shard_map/ppermute | solution.py:671
  209.1 1.4 collect_grad.1
  210.7 4.5 %attention_sum.1 = (f32[8,48,2048]{2,1,0:T(8,128)}, f32[8,16,2048]{2,1,0:T(8,128)}, f32[8,16,512]{2,1,0:T(8,128)}, f32[8,2,16,128]{3,2,1,0:T(8,128)}, f32[8,16,512]{2,1,0:T(8,128)}) custom-call(s32[4]{0:T(128)S(1)} %pad_add_fusion.info.refs_0_, s32[8]{0:T(128)S(1)} %copy-done.71, bf16[4,112,512]{2,1,0:T(8,128)(2,1)S(1)} %constant_dynamic-update-slice_fusion.refs_14_.refs_0_, ...), custom_call_target="tpu_custom_call" | custom-call | bytes 12000000 | tf_op jit(solution)/shard_map/attention_sum/pallas_call | solution.py:655
  215.2 1.4 collect_out.1
  (252 shorter events, 13.8 us)
Async XLA Ops:
  3.9 21.8 %all-to-all-start = ((bf16[8,64,512]{2,1,0:T(8,128)(2,1)}), bf16[8,64,512]{2,1,0:T(8,128)(2,1)S(1)}, u32[]{:S(2)}, u32[]{:S(2)}) async-start(bf16[8,64,512]{2,1,0:T(8,128)(2,1)} %deal.1), calls=%async_computation | async-start | bytes 1048576 | tf_op jit(solution)/shard_map/all_to_all | solution.py:750
  11.2 8.2 %collective-permute-start = (bf16[2,512]{1,0:T(2,128)(2,1)S(1)}, bf16[2,512]{1,0:T(2,128)(2,1)S(1)}, u32[]{:S(2)}, u32[]{:S(2)}) collective-permute-start(bf16[2,512]{1,0:T(2,128)(2,1)S(1)} %pad_maximum_fusion.4), channel_id=1, source_target_pairs={{0,1},{1,0},{2,3},{3,2},{4,5},{5,4},{6,7},{7,6},{8,9},{9,8},{10,11... | collective-permute-start | bytes 6152 | tf_op jit(solution)/shard_map/ppermute | solution.py:671
  11.3 3.7 %collective-permute-start.1 = (bf16[2,512]{1,0:T(2,128)(2,1)S(1)}, bf16[2,512]{1,0:T(2,128)(2,1)S(1)}, u32[]{:S(2)}, u32[]{:S(2)}) collective-permute-start(bf16[2,512]{1,0:T(2,128)(2,1)S(1)} %pad_maximum_fusion.4), channel_id=1, source_target_pairs={{0,2},{1,3},{2,0},{3,1},{4,6},{5,7},{6,4},{7,5},{8,10},{9,11},{10,... | collective-permute-start | bytes 6152 | tf_op jit(solution)/shard_map/ppermute | solution.py:671
  12.9 14.4 %collective-permute-start.5 = (bf16[512,512]{1,0:T(8,128)(2,1)S(1)}, bf16[512,512]{1,0:T(8,128)(2,1)S(1)}, u32[]{:S(2)}, u32[]{:S(2)}) collective-permute-start(bf16[512,512]{1,0:T(8,128)(2,1)S(1)} %bitcast.29), channel_id=1, source_target_pairs={{0,2},{1,3},{2,0},{3,1},{4,6},{5,7},{6,4},{7,5},{8,10},{9,11},{10,... | collective-permute-start | bytes 1572872 | tf_op jit(solution)/shard_map/ppermute | solution.py:671
  14.9 4.5 %collective-permute-start.2 = (bf16[2,512]{1,0:T(2,128)(2,1)S(1)}, bf16[2,512]{1,0:T(2,128)(2,1)S(1)}, u32[]{:S(2)}, u32[]{:S(2)}) collective-permute-start(bf16[2,512]{1,0:T(2,128)(2,1)S(1)} %collective-permute-done.1), channel_id=1, source_target_pairs={{0,1},{1,0},{2,3},{3,2},{4,5},{5,4},{6,7},{7,6},{8,9},{9,8},{10,11... | collective-permute-start | bytes 6152 | tf_op jit(solution)/shard_map/ppermute | solution.py:671
  16.3 17.7 %copy-start.56 = (f32[32,256]{1,0:T(8,128)S(1)}, f32[32,256]{1,0:T(8,128)}, u32[]{:S(2)}) copy-start(f32[32,256]{1,0:T(8,128)} %constant.21.clone.refs_12_.refs_22_) | copy-start | bytes 98308
  16.3 17.7 %copy-start.58 = (f32[32,256]{1,0:T(8,128)S(1)}, f32[32,256]{1,0:T(8,128)}, u32[]{:S(2)}) copy-start(f32[32,256]{1,0:T(8,128)} %constant.19.clone.refs_11_.refs_21_) | copy-start | bytes 98308
  19.4 18.7 %copy-start.51 = (bf16[16,512]{1,0:T(8,128)(2,1)}, bf16[16,512]{1,0:T(8,128)(2,1)S(1)}, u32[]{:S(2)}) copy-start(bf16[16,512]{1,0:T(8,128)(2,1)S(1)} %get-tuple-element.123.refs_9_.refs_17_) | copy-start | bytes 49156
  19.4 18.8 %copy-start.60 = (bf16[2,16,128]{2,1,0:T(8,128)(2,1)}, bf16[2,16,128]{2,1,0:T(8,128)(2,1)S(1)}, u32[]{:S(2)}) copy-start(bf16[2,16,128]{2,1,0:T(8,128)(2,1)S(1)} %get-tuple-element.124.refs_10_.refs_18_) | copy-start | bytes 24580
  19.4 18.8 %copy-start.22 = (bf16[16,2048]{1,0:T(8,128)(2,1)}, bf16[16,2048]{1,0:T(8,128)(2,1)S(1)}, u32[]{:S(2)}) copy-start(bf16[16,2048]{1,0:T(8,128)(2,1)S(1)} %get-tuple-element.127.refs_4_.refs_20_) | copy-start | bytes 196612
  19.4 18.8 %copy-start.45 = (bf16[16,512]{1,0:T(8,128)(2,1)}, bf16[16,512]{1,0:T(8,128)(2,1)S(1)}, u32[]{:S(2)}) copy-start(bf16[16,512]{1,0:T(8,128)(2,1)S(1)} %get-tuple-element.126.refs_3_.refs_19_) | copy-start | bytes 49156
  25.7 6.8 %collective-permute-start.4 = (bf16[256,512]{1,0:T(8,128)(2,1)S(1)}, bf16[256,512]{1,0:T(8,128)(2,1)S(1)}, u32[]{:S(2)}, u32[]{:S(2)}) collective-permute-start(bf16[256,512]{1,0:T(8,128)(2,1)S(1)} %get-tuple-element.232), channel_id=1, source_target_pairs={{0,2},{1,3},{2,0},{3,1},{4,6},{5,7},{6,4},{7,5},{8,10},{9,11},{10,... | collective-permute-start | bytes 786440 | tf_op jit(solution)/shard_map/ppermute | solution.py:671
  27.2 6.8 %collective-permute-start.3 = (bf16[512,512]{1,0:T(8,128)(2,1)S(1)}, bf16[512,512]{1,0:T(8,128)(2,1)S(1)}, u32[]{:S(2)}, u32[]{:S(2)}) collective-permute-start(bf16[512,512]{1,0:T(8,128)(2,1)S(1)} %bitcast.21), channel_id=1, source_target_pairs={{0,1},{1,0},{2,3},{3,2},{4,5},{5,4},{6,7},{7,6},{8,9},{9,8},{10,11... | collective-permute-start | bytes 1572872 | tf_op jit(solution)/shard_map/ppermute | solution.py:671
  32.5 29.2 %copy-start.8 = (bf16[256,512]{1,0:T(8,128)(2,1)}, bf16[256,512]{1,0:T(8,128)(2,1)S(1)}, u32[]{:S(2)}) copy-start(bf16[256,512]{1,0:T(8,128)(2,1)S(1)} %collective-permute-done.4.refs_5_.refs_6_) | copy-start | bytes 786436
  32.5 1.5 collective-permute-start.6
  32.5 9.6 %collective-permute-start.9 = (bf16[256,512]{1,0:T(8,128)(2,1)S(1)}, bf16[256,512]{1,0:T(8,128)(2,1)S(1)}, u32[]{:S(2)}, u32[]{:S(2)}) collective-permute-start(bf16[256,512]{1,0:T(8,128)(2,1)S(1)} %get-tuple-element.231), channel_id=1, source_target_pairs={{0,2},{1,3},{2,0},{3,1},{4,6},{5,7},{6,4},{7,5},{8,10},{9,11},{10,... | collective-permute-start | bytes 786440 | tf_op jit(solution)/shard_map/ppermute | solution.py:671
  34.0 27.7 %copy-start.10 = (bf16[256,512]{1,0:T(8,128)(2,1)}, bf16[256,512]{1,0:T(8,128)(2,1)S(1)}, u32[]{:S(2)}) copy-start(bf16[256,512]{1,0:T(8,128)(2,1)S(1)} %collective-permute-done.6.refs_6_.refs_7_) | copy-start | bytes 786436
  42.0 1.9 collective-permute-start.10
  42.2 9.1 %collective-permute-start.7 = (bf16[512,512]{1,0:T(8,128)(2,1)S(1)}, bf16[512,512]{1,0:T(8,128)(2,1)S(1)}, u32[]{:S(2)}, u32[]{:S(2)}) collective-permute-start(bf16[512,512]{1,0:T(8,128)(2,1)S(1)} %bitcast.30), channel_id=1, source_target_pairs={{0,1},{1,0},{2,3},{3,2},{4,5},{5,4},{6,7},{7,6},{8,9},{9,8},{10,11... | collective-permute-start | bytes 1572872 | tf_op jit(solution)/shard_map/ppermute | solution.py:671
  42.6 8.8 %collective-permute-start.8 = (bf16[512,512]{1,0:T(8,128)(2,1)S(1)}, bf16[512,512]{1,0:T(8,128)(2,1)S(1)}, u32[]{:S(2)}, u32[]{:S(2)}) collective-permute-start(bf16[512,512]{1,0:T(8,128)(2,1)S(1)} %collective-permute-done.5.refs_11_.refs_10_), channel_id=1, source_target_pairs={{0,1},{1,0},{2,3},{3,2},{4,5},{5,4},{6,7},{7,6},{8,9},{9,8},{10,11... | collective-permute-start | bytes 1572872 | tf_op jit(solution)/shard_map/ppermute | solution.py:671
  44.1 14.1 %collective-permute-start.11 = (bf16[256,1024]{1,0:T(8,128)(2,1)S(1)}, bf16[256,1024]{1,0:T(8,128)(2,1)S(1)}, u32[]{:S(2)}, u32[]{:S(2)}) collective-permute-start(bf16[256,1024]{1,0:T(8,128)(2,1)S(1)} %pair_sum.4.refs_0_.refs_14_), channel_id=1, source_target_pairs={{0,2},{1,3},{2,0},{3,1},{4,6},{5,7},{6,4},{7,5},{8,10},{9,11},{10,... | collective-permute-start | bytes 1572872 | tf_op jit(solution)/shard_map/ppermute | solution.py:671
  45.6 1.5 collective-permute-start.13
  47.1 30.7 %copy-start.6 = (bf16[256,512]{1,0:T(8,128)(2,1)}, bf16[256,512]{1,0:T(8,128)(2,1)S(1)}, u32[]{:S(2)}) copy-start(bf16[256,512]{1,0:T(8,128)(2,1)S(1)} %collective-permute-done.13.refs_6_.refs_7_) | copy-start | bytes 786436
  55.1 19.5 %copy-start.49 = (bf16[512,256]{1,0:T(8,128)(2,1)}, bf16[512,256]{1,0:T(8,128)(2,1)S(1)}, u32[]{:S(2)}) copy-start(bf16[512,256]{1,0:T(8,128)(2,1)S(1)} %get-tuple-element.180.refs_25_) | copy-start | bytes 786436
  58.1 1.9 collective-permute-start.14
  58.4 3.3 %collective-permute-start.12 = (bf16[256,1024]{1,0:T(8,128)(2,1)S(1)}, bf16[256,1024]{1,0:T(8,128)(2,1)S(1)}, u32[]{:S(2)}, u32[]{:S(2)}) collective-permute-start(bf16[256,1024]{1,0:T(8,128)(2,1)S(1)} %far_sum.4.refs_7_), channel_id=1, source_target_pairs={{0,1},{1,0},{2,3},{3,2},{4,5},{5,4},{6,7},{7,6},{8,9},{9,8},{10,11... | collective-permute-start | bytes 1572872 | tf_op jit(solution)/shard_map/ppermute | solution.py:671
  60.2 15.5 %collective-permute-start.15 = (bf16[256,1024]{1,0:T(8,128)(2,1)S(1)}, bf16[256,1024]{1,0:T(8,128)(2,1)S(1)}, u32[]{:S(2)}, u32[]{:S(2)}) collective-permute-start(bf16[256,1024]{1,0:T(8,128)(2,1)S(1)} %pair_sum.5.refs_19_.refs_0_), channel_id=1, source_target_pairs={{0,2},{1,3},{2,0},{3,1},{4,6},{5,7},{6,4},{7,5},{8,10},{9,11},{10,... | collective-permute-start | bytes 1572872 | tf_op jit(solution)/shard_map/ppermute | solution.py:671
  75.7 29.6 %copy-start.4 = (bf16[256,2048]{1,0:T(8,128)(2,1)}, bf16[256,2048]{1,0:T(8,128)(2,1)S(1)}, u32[]{:S(2)}) copy-start(bf16[256,2048]{1,0:T(8,128)(2,1)S(1)} %get-tuple-element.152.refs_4_.refs_2_) | copy-start | bytes 3145732
  75.8 2.0 collective-permute-start.16
  89.8 12.1 %collective-permute-start.17 = (bf16[1,192,512]{2,1,0:T(8,128)(2,1)S(1)}, bf16[1,192,512]{2,1,0:T(8,128)(2,1)S(1)}, u32[]{:S(2)}, u32[]{:S(2)}) collective-permute-start(bf16[1,192,512]{2,1,0:T(8,128)(2,1)S(1)} %bitcast.36), channel_id=1, source_target_pairs={{0,16},{4,20},{8,24},{12,28},{16,0},{20,4},{24,8},{28,12},{1,17},{... | collective-permute-start | bytes 589832 | tf_op jit(solution)/shard_map/ppermute | solution.py:671
  102.0 2.2 collective-permute-start.18
  102.0 11.9 %collective-permute-start.20 = (bf16[2,192,512]{2,1,0:T(8,128)(2,1)S(1)}, bf16[2,192,512]{2,1,0:T(8,128)(2,1)S(1)}, u32[]{:S(2)}, u32[]{:S(2)}) collective-permute-start(bf16[2,192,512]{2,1,0:T(8,128)(2,1)S(1)} %pad_maximum_fusion.refs_0_), channel_id=1, source_target_pairs={{0,4},{4,0},{8,12},{12,8},{16,20},{20,16},{24,28},{28,24},{1,5},{5... | collective-permute-start | bytes 1179656 | tf_op jit(solution)/shard_map/ppermute | solution.py:671
  104.1 11.2 %collective-permute-start.19 = (bf16[2,192,512]{2,1,0:T(8,128)(2,1)S(1)}, bf16[2,192,512]{2,1,0:T(8,128)(2,1)S(1)}, u32[]{:S(2)}, u32[]{:S(2)}) collective-permute-start(bf16[2,192,512]{2,1,0:T(8,128)(2,1)S(1)} %pad_maximum_fusion.refs_0_), channel_id=1, source_target_pairs={{0,8},{4,12},{8,0},{12,4},{16,24},{20,28},{24,16},{28,20},{1,9},{5... | collective-permute-start | bytes 1179656 | tf_op jit(solution)/shard_map/ppermute | solution.py:671
  104.2 15.8 %collective-permute-start.22 = (bf16[256,1024]{1,0:T(8,128)(2,1)S(1)}, bf16[256,1024]{1,0:T(8,128)(2,1)S(1)}, u32[]{:S(2)}, u32[]{:S(2)}) collective-permute-start(bf16[256,1024]{1,0:T(8,128)(2,1)S(1)} %pair_sum.6.refs_11_.refs_0_), channel_id=1, source_target_pairs={{0,2},{1,3},{2,0},{3,1},{4,6},{5,7},{6,4},{7,5},{8,10},{9,11},{10,... | collective-permute-start | bytes 1572872 | tf_op jit(solution)/shard_map/ppermute | solution.py:671
  115.4 5.3 %collective-permute-start.21 = (bf16[304,1024]{1,0:T(8,128)(2,1)S(1)}, bf16[304,1024]{1,0:T(8,128)(2,1)S(1)}, u32[]{:S(2)}, u32[]{:S(2)}) collective-permute-start(bf16[304,1024]{1,0:T(8,128)(2,1)S(1)} %get-tuple-element.172), channel_id=1, source_target_pairs={{0,1},{1,0},{2,3},{3,2},{4,5},{5,4},{6,7},{7,6},{8,9},{9,8},{10,11... | collective-permute-start | bytes 1867784 | tf_op jit(solution)/shard_map/ppermute | solution.py:671
  120.1 2.1 collective-permute-start.24
  121.0 16.5 %collective-permute-start.23 = (bf16[304,1024]{1,0:T(8,128)(2,1)S(1)}, bf16[304,1024]{1,0:T(8,128)(2,1)S(1)}, u32[]{:S(2)}, u32[]{:S(2)}) collective-permute-start(bf16[304,1024]{1,0:T(8,128)(2,1)S(1)} %pair_sum.7.refs_34_.refs_0_), channel_id=1, source_target_pairs={{0,2},{1,3},{2,0},{3,1},{4,6},{5,7},{6,4},{7,5},{8,10},{9,11},{10,... | collective-permute-start | bytes 1867784 | tf_op jit(solution)/shard_map/ppermute | solution.py:671
  121.6 11.5 %collective-permute-start.26 = (bf16[2,192,512]{2,1,0:T(8,128)(2,1)S(1)}, bf16[2,192,512]{2,1,0:T(8,128)(2,1)S(1)}, u32[]{:S(2)}, u32[]{:S(2)}) collective-permute-start(bf16[2,192,512]{2,1,0:T(8,128)(2,1)S(1)} %collective-permute-done.19.refs_1_), channel_id=1, source_target_pairs={{0,4},{4,0},{8,12},{12,8},{16,20},{20,16},{24,28},{28,24},{1,5},{5... | collective-permute-start | bytes 1179656 | tf_op jit(solution)/shard_map/ppermute | solution.py:671
  133.1 4.6 %collective-permute-start.27 = (bf16[256,1024]{1,0:T(8,128)(2,1)S(1)}, bf16[256,1024]{1,0:T(8,128)(2,1)S(1)}, u32[]{:S(2)}, u32[]{:S(2)}) collective-permute-start(bf16[256,1024]{1,0:T(8,128)(2,1)S(1)} %get-tuple-element.197), channel_id=1, source_target_pairs={{0,1},{1,0},{2,3},{3,2},{4,5},{5,4},{6,7},{7,6},{8,9},{9,8},{10,11... | collective-permute-start | bytes 1572872 | tf_op jit(solution)/shard_map/ppermute | solution.py:671
  137.6 2.9 %collective-permute-start.25 = (bf16[304,1024]{1,0:T(8,128)(2,1)S(1)}, bf16[304,1024]{1,0:T(8,128)(2,1)S(1)}, u32[]{:S(2)}, u32[]{:S(2)}) collective-permute-start(bf16[304,1024]{1,0:T(8,128)(2,1)S(1)} %far_sum.7.refs_13_), channel_id=1, source_target_pairs={{0,1},{1,0},{2,3},{3,2},{4,5},{5,4},{6,7},{7,6},{8,9},{9,8},{10,11... | collective-permute-start | bytes 1867784 | tf_op jit(solution)/shard_map/ppermute | solution.py:671
  137.8 12.6 %collective-permute-start.29 = (bf16[256,512]{1,0:T(8,128)(2,1)S(1)}, bf16[256,512]{1,0:T(8,128)(2,1)S(1)}, u32[]{:S(2)}, u32[]{:S(2)}) collective-permute-start(bf16[256,512]{1,0:T(8,128)(2,1)S(1)} %high_sum.4.refs_36_), channel_id=1, source_target_pairs={{0,2},{1,3},{2,0},{3,1},{4,6},{5,7},{6,4},{7,5},{8,10},{9,11},{10,... | collective-permute-start | bytes 786440 | tf_op jit(solution)/shard_map/ppermute | solution.py:671
  138.4 11.9 %collective-permute-start.28 = (bf16[1,48,1024]{2,1,0:T(8,128)(2,1)S(1)}, bf16[1,48,1024]{2,1,0:T(8,128)(2,1)S(1)}, u32[]{:S(2)}, u32[]{:S(2)}) collective-permute-start(bf16[1,48,1024]{2,1,0:T(8,128)(2,1)S(1)} %slice_bitcast_fusion), channel_id=1, source_target_pairs={{0,16},{4,20},{8,24},{12,28},{16,0},{20,4},{24,8},{28,12},{1,17},{... | collective-permute-start | bytes 294920 | tf_op jit(solution)/shard_map/ppermute | solution.py:671
  150.4 4.7 %collective-permute-start.32 = (bf16[256,1024]{1,0:T(8,128)(2,1)S(1)}, bf16[256,1024]{1,0:T(8,128)(2,1)S(1)}, u32[]{:S(2)}, u32[]{:S(2)}) collective-permute-start(bf16[256,1024]{1,0:T(8,128)(2,1)S(1)} %get-tuple-element.204), channel_id=1, source_target_pairs={{0,1},{1,0},{2,3},{3,2},{4,5},{5,4},{6,7},{7,6},{8,9},{9,8},{10,11... | collective-permute-start | bytes 1572872 | tf_op jit(solution)/shard_map/ppermute | solution.py:671
  150.5 2.2 collective-permute-start.30
  152.7 5.0 %collective-permute-start.31 = (bf16[96,512]{1,0:T(8,128)(2,1)S(1)}, bf16[96,512]{1,0:T(8,128)(2,1)S(1)}, u32[]{:S(2)}, u32[]{:S(2)}) collective-permute-start(bf16[96,512]{1,0:T(8,128)(2,1)S(1)} %high_sum.5.refs_2_), channel_id=1, source_target_pairs={{0,2},{1,3},{2,0},{3,1},{4,6},{5,7},{6,4},{7,5},{8,10},{9,11},{10,... | collective-permute-start | bytes 294920 | tf_op jit(solution)/shard_map/ppermute | solution.py:671
  153.5 6.9 %collective-permute-start.36 = (bf16[2,48,1024]{2,1,0:T(8,128)(2,1)S(1)}, bf16[2,48,1024]{2,1,0:T(8,128)(2,1)S(1)}, u32[]{:S(2)}, u32[]{:S(2)}) collective-permute-start(bf16[2,48,1024]{2,1,0:T(8,128)(2,1)S(1)} %pad_maximum_fusion.2), channel_id=1, source_target_pairs={{0,8},{4,12},{8,0},{12,4},{16,24},{20,28},{24,16},{28,20},{1,9},{5... | collective-permute-start | bytes 589832 | tf_op jit(solution)/shard_map/ppermute | solution.py:671
  155.2 10.5 %collective-permute-start.33 = (bf16[256,512]{1,0:T(8,128)(2,1)S(1)}, bf16[256,512]{1,0:T(8,128)(2,1)S(1)}, u32[]{:S(2)}, u32[]{:S(2)}) collective-permute-start(bf16[256,512]{1,0:T(8,128)(2,1)S(1)} %high_sum.6), channel_id=1, source_target_pairs={{0,2},{1,3},{2,0},{3,1},{4,6},{5,7},{6,4},{7,5},{8,10},{9,11},{10,... | collective-permute-start | bytes 786440 | tf_op jit(solution)/shard_map/ppermute | solution.py:671
  157.8 7.9 %collective-permute-start.34 = (bf16[1,112,512]{2,1,0:T(8,128)(2,1)S(1)}, bf16[1,112,512]{2,1,0:T(8,128)(2,1)S(1)}, u32[]{:S(2)}, u32[]{:S(2)}) collective-permute-start(bf16[1,112,512]{2,1,0:T(8,128)(2,1)S(1)} %maximum_bitcast_fusion.refs_6_), channel_id=1, source_target_pairs={{0,16},{4,20},{8,24},{12,28},{16,0},{20,4},{24,8},{28,12},{1,17},{... | collective-permute-start | bytes 344072 | tf_op jit(solution)/shard_map/ppermute | solution.py:671
  160.4 11.8 %collective-permute-start.37 = (bf16[4,48,1024]{2,1,0:T(8,128)(2,1)S(1)}, bf16[4,48,1024]{2,1,0:T(8,128)(2,1)S(1)}, u32[]{:S(2)}, u32[]{:S(2)}) collective-permute-start(bf16[4,48,1024]{2,1,0:T(8,128)(2,1)S(1)} %constant_dynamic-update-slice_fusion.2.refs_4_), channel_id=1, source_target_pairs={{0,4},{4,0},{8,12},{12,8},{16,20},{20,16},{24,28},{28,24},{1,5},{5... | collective-permute-start | bytes 1179656 | tf_op jit(solution)/shard_map/ppermute | solution.py:671
  165.6 6.5 %collective-permute-start.35 = (bf16[2,112,512]{2,1,0:T(8,128)(2,1)S(1)}, bf16[2,112,512]{2,1,0:T(8,128)(2,1)S(1)}, u32[]{:S(2)}, u32[]{:S(2)}) collective-permute-start(bf16[2,112,512]{2,1,0:T(8,128)(2,1)S(1)} %pad_maximum_fusion.1), channel_id=1, source_target_pairs={{0,8},{4,12},{8,0},{12,4},{16,24},{20,28},{24,16},{28,20},{1,9},{5... | collective-permute-start | bytes 688136 | tf_op jit(solution)/shard_map/ppermute | solution.py:671
  168.2 9.9 %collective-permute-start.39 = (bf16[256,1024]{1,0:T(8,128)(2,1)}, bf16[256,1024]{1,0:T(8,128)(2,1)}, u32[]{:S(2)}, u32[]{:S(2)}) collective-permute-start(bf16[256,1024]{1,0:T(8,128)(2,1)} %get-tuple-element.217.refs_35_), channel_id=1, source_target_pairs={{0,1},{1,0},{2,3},{3,2},{4,5},{5,4},{6,7},{7,6},{8,9},{9,8},{10,11... | collective-permute-start | bytes 1572872 | tf_op jit(solution)/shard_map/ppermute | solution.py:671
  168.2 9.9 %collective-permute-start.38 = (bf16[256,1024]{1,0:T(8,128)(2,1)}, bf16[256,1024]{1,0:T(8,128)(2,1)}, u32[]{:S(2)}, u32[]{:S(2)}) collective-permute-start(bf16[256,1024]{1,0:T(8,128)(2,1)} %get-tuple-element.210), channel_id=1, source_target_pairs={{0,1},{1,0},{2,3},{3,2},{4,5},{5,4},{6,7},{7,6},{8,9},{9,8},{10,11... | collective-permute-start | bytes 1572872 | tf_op jit(solution)/shard_map/ppermute | solution.py:671
  173.6 18.9 %all-to-all-start.1 = ((bf16[8,64,512]{2,1,0:T(8,128)(2,1)}), bf16[8,64,512]{2,1,0:T(8,128)(2,1)S(1)}, u32[]{:S(2)}, u32[]{:S(2)}) async-start(bf16[8,64,512]{2,1,0:T(8,128)(2,1)} %bitcast.35), calls=%async_computation.1 | async-start | bytes 1048576 | tf_op jit(solution)/shard_map/all_to_all | solution.py:826
  179.5 10.8 %collective-permute-start.40 = (bf16[512,512]{1,0:T(8,128)(2,1)S(1)}, bf16[512,512]{1,0:T(8,128)(2,1)S(1)}, u32[]{:S(2)}, u32[]{:S(2)}) collective-permute-start(bf16[512,512]{1,0:T(8,128)(2,1)S(1)} %high_sum.7), channel_id=1, source_target_pairs={{0,2},{1,3},{2,0},{3,1},{4,6},{5,7},{6,4},{7,5},{8,10},{9,11},{10,... | collective-permute-start | bytes 1572872 | tf_op jit(solution)/shard_map/ppermute | solution.py:671
  180.8 2.5 %collective-permute-start.41 = (bf16[4,48,1024]{2,1,0:T(8,128)(2,1)S(1)}, bf16[4,48,1024]{2,1,0:T(8,128)(2,1)S(1)}, u32[]{:S(2)}, u32[]{:S(2)}) collective-permute-start(bf16[4,48,1024]{2,1,0:T(8,128)(2,1)S(1)} %copy-done.34), channel_id=1, source_target_pairs={{0,1},{1,0},{2,3},{3,2},{4,5},{5,4},{6,7},{7,6},{8,9},{9,8},{10,11... | collective-permute-start | bytes 1179656 | tf_op jit(solution)/shard_map/ppermute | solution.py:671
  180.8 2.5 %collective-permute-start.42 = (bf16[4,48,1024]{2,1,0:T(8,128)(2,1)S(1)}, bf16[4,48,1024]{2,1,0:T(8,128)(2,1)S(1)}, u32[]{:S(2)}, u32[]{:S(2)}) collective-permute-start(bf16[4,48,1024]{2,1,0:T(8,128)(2,1)S(1)} %collective-permute-done.37.refs_15_.refs_5_), channel_id=1, source_target_pairs={{0,1},{1,0},{2,3},{3,2},{4,5},{5,4},{6,7},{7,6},{8,9},{9,8},{10,11... | collective-permute-start | bytes 1179656 | tf_op jit(solution)/shard_map/ppermute | solution.py:671
  181.3 17.8 %collective-permute-start.43 = (bf16[4,112,512]{2,1,0:T(8,128)(2,1)S(1)}, bf16[4,112,512]{2,1,0:T(8,128)(2,1)}, u32[]{:S(2)}, u32[]{:S(2)}) collective-permute-start(bf16[4,112,512]{2,1,0:T(8,128)(2,1)S(1)} %constant_dynamic-update-slice_fusion.refs_14_.refs_0_), channel_id=1, source_target_pairs={{0,4},{4,0},{8,12},{12,8},{16,20},{20,16},{24,28},{28,24},{1,5},{5... | collective-permute-start | bytes 1376264 | tf_op jit(solution)/shard_map/ppermute | solution.py:671
  192.5 22.6 %all-to-all-start.2 = ((bf16[8,64,512]{2,1,0:T(8,128)(2,1)}), bf16[8,64,512]{2,1,0:T(8,128)(2,1)S(1)}, u32[]{:S(2)}, u32[]{:S(2)}) async-start(bf16[8,64,512]{2,1,0:T(8,128)(2,1)} %bitcast.14), calls=%async_computation.2 | async-start | bytes 1048576 | tf_op jit(solution)/shard_map/all_to_all | solution.py:826
  198.3 8.1 %collective-permute-start.46 = (bf16[4,64,512]{2,1,0:T(8,128)(2,1)S(1)}, bf16[4,64,512]{2,1,0:T(8,128)(2,1)S(1)}, u32[]{:S(2)}, u32[]{:S(2)}) collective-permute-start(bf16[4,64,512]{2,1,0:T(8,128)(2,1)S(1)} %slice.34.refs_2_), channel_id=1, source_target_pairs={{0,2},{1,3},{2,0},{3,1},{4,6},{5,7},{6,4},{7,5},{8,10},{9,11},{10,... | collective-permute-start | bytes 786440 | tf_op jit(solution)/shard_map/ppermute | solution.py:671
  200.1 9.1 %collective-permute-start.47 = (bf16[4,64,512]{2,1,0:T(8,128)(2,1)S(1)}, bf16[4,64,512]{2,1,0:T(8,128)(2,1)S(1)}, u32[]{:S(2)}, u32[]{:S(2)}) collective-permute-start(bf16[4,64,512]{2,1,0:T(8,128)(2,1)S(1)} %slice.35.refs_3_), channel_id=1, source_target_pairs={{0,2},{1,3},{2,0},{3,1},{4,6},{5,7},{6,4},{7,5},{8,10},{9,11},{10,... | collective-permute-start | bytes 786440 | tf_op jit(solution)/shard_map/ppermute | solution.py:671
  201.4 9.1 %collective-permute-start.44 = (bf16[4,64,512]{2,1,0:T(8,128)(2,1)S(1)}, bf16[4,64,512]{2,1,0:T(8,128)(2,1)S(1)}, u32[]{:S(2)}, u32[]{:S(2)}) collective-permute-start(bf16[4,64,512]{2,1,0:T(8,128)(2,1)S(1)} %slice.34.refs_2_), channel_id=1, source_target_pairs={{0,1},{1,0},{2,3},{3,2},{4,5},{5,4},{6,7},{7,6},{8,9},{9,8},{10,11... | collective-permute-start | bytes 786440 | tf_op jit(solution)/shard_map/ppermute | solution.py:671
  206.3 4.2 %collective-permute-start.48 = (bf16[4,64,512]{2,1,0:T(8,128)(2,1)S(1)}, bf16[4,64,512]{2,1,0:T(8,128)(2,1)S(1)}, u32[]{:S(2)}, u32[]{:S(2)}) collective-permute-start(bf16[4,64,512]{2,1,0:T(8,128)(2,1)S(1)} %collective-permute-done.46.refs_6_), channel_id=1, source_target_pairs={{0,1},{1,0},{2,3},{3,2},{4,5},{5,4},{6,7},{7,6},{8,9},{9,8},{10,11... | collective-permute-start | bytes 786440 | tf_op jit(solution)/shard_map/ppermute | solution.py:671
  206.3 4.2 %collective-permute-start.45 = (bf16[4,64,512]{2,1,0:T(8,128)(2,1)S(1)}, bf16[4,64,512]{2,1,0:T(8,128)(2,1)S(1)}, u32[]{:S(2)}, u32[]{:S(2)}) collective-permute-start(bf16[4,64,512]{2,1,0:T(8,128)(2,1)S(1)} %slice.35.refs_3_), channel_id=1, source_target_pairs={{0,1},{1,0},{2,3},{3,2},{4,5},{5,4},{6,7},{7,6},{8,9},{9,8},{10,11... | collective-permute-start | bytes 786440 | tf_op jit(solution)/shard_map/ppermute | solution.py:671
  209.1 1.5 collective-permute-start.49
  (67 other events, 434.1 us)

commit v16 on v15

--- a/solution.py
+++ b/solution.py
@@ -900,6 +900,7 @@
     att_side = swap(att, bits[-1], "dp", dp)
     a_parts = [att[:, n_b:], att_side[:, n_b:]]
     a_far = [far(v) for v in a_parts]
+    a_far[0] = late(a_far[0], input_grad)
     outs = [sds((adapters, 3 * RANK, WIDTH), F32), sds((adapters, RANK, WIDTH), F32),
             sds((adapters, RANK, q_cols), F32), sds((adapters, 2, RANK, kv_cols), F32),
             sds((adapters, RANK, q_cols), F32)]

time: 217 us -> 219 us (level)
  transfers between devices with their start and end apart: 53 -> 53, of which waited for: 21 -> 21; matrix products, arithmetic and copies ran while one was open for 2% -> 2% of each run, Pallas kernels for 42% -> 41%
where the time goes in v16:
time: 219 us; the launch traced here: 218 us
  Pallas kernels  106 us (48%)
  starting transfers between devices  52.5 us (24%)
  waiting for transfers between devices  49.5 us (23%)
  local copies, waits for them, and re-layouts  6.04 us (3%)
  other arithmetic  2.31 us (1%)
    pallas_call x26, Pallas kernels, call(): pl.pallas_call(body, in_specs=[pl.BlockSpec(memory_space=pltpu.SMEM)] * n...  90.7 us
    ppermute x50, waiting for transfers between devices, swap(): return lax.ppermute(value, axis, [(i, i ^ bit) for i in range(size)])  43.3 us
    ppermute x50, starting transfers between devices, swap(): return lax.ppermute(value, axis, [(i, i ^ bit) for i in range(size)])  35.1 us
    all_to_all x2, starting transfers between devices, to_bands(): lax.all_to_all(value.reshape(dp, length // dp, QUARTER), 'dp', split_axis...  10.1 us
    pallas_call x2, Pallas kernels, sum_call(): pl.pallas_call(functools.partial(kernel, [len(group) for group in groups]...  8.36 us
    all_to_all x1, starting transfers between devices, shards(): lax.all_to_all(ordered, 'dp', split_axis=0, concat_axis=1, tiled=True)[0]  7.26 us
    all_to_all x1, waiting for transfers between devices, shards(): lax.all_to_all(ordered, 'dp', split_axis=0, concat_axis=1, tiled=True)[0]  6.18 us
    pallas_call x3, Pallas kernels, move_rows(): pl.pallas_call(kernel, in_specs=[pl.BlockSpec(memory_space=pltpu.SMEM), p...  5.25 us
  transfers between devices with their start and end apart: 53, of which 21 were waited for; matrix products, arithmetic and copies ran while one was open for 2% of the time, Pallas kernels for 41%

profile of v16, /device:TPU:0, one launch (start us, length us, event | category | flops | bytes accessed | tf_op | source)
XLA Modules:
  0.0 218.4 jit_solution(3771356872650057344)
XLA Ops:
  1.4 2.5 %deal.1 = bf16[8,64,512]{2,1,0:T(8,128)(2,1)} custom-call(s32[8]{0:T(128)S(1)} %copy-done.68, bf16[8,64,512]{2,1,0:T(8,128)(2,1)} %source.1), custom_call_target="tpu_custom_call" | custom-call | flops 1000 | bytes 1000 | tf_op jit(solution)/shard_map/deal/pallas_call | solution.py:599
  3.9 7.3 %all-to-all-start = ((bf16[8,64,512]{2,1,0:T(8,128)(2,1)}), bf16[8,64,512]{2,1,0:T(8,128)(2,1)S(1)}, u32[]{:S(2)}, u32[]{:S(2)}) async-start(bf16[8,64,512]{2,1,0:T(8,128)(2,1)} %deal.1), calls=%async_computation | async-start | bytes 1048576 | tf_op jit(solution)/shard_map/all_to_all | solution.py:750
  11.3 1.6 collective-permute-start.1
  14.2 0.7 collective-permute-done.1
  14.9 1.4 pad_add_fusion.info.refs_0_
  16.3 1.8 adapters.1
  19.4 6.2 %all-to-all-done = bf16[8,64,512]{2,1,0:T(8,128)(2,1)S(1)} async-done(((bf16[8,64,512]{2,1,0:T(8,128)(2,1)}), bf16[8,64,512]{2,1,0:T(8,128)(2,1)S(1)}, u32[]{:S(2)}, u32[]{:S(2)}) %all-to-all-start) | async-done | bytes 524320 | tf_op jit(solution)/shard_map/all_to_all | solution.py:750
  25.7 1.6 collective-permute-start.4
  27.2 5.2 %collective-permute-done.4.refs_5_.refs_6_ = bf16[256,512]{1,0:T(8,128)(2,1)S(1)} collective-permute-done((bf16[256,512]{1,0:T(8,128)(2,1)S(1)}, bf16[256,512]{1,0:T(8,128)(2,1)S(1)}, u32[]{:S(2)}, u32[]{:S(2)}) %collective-permute-start.4) | collective-permute-done | bytes 262176 | tf_op jit(solution)/shard_map/ppermute | solution.py:671
  32.5 1.5 collective-permute-start.9
  34.0 4.1 %project_0.1 = (bf16[48,256]{1,0:T(8,128)(2,1)S(1)}, bf16[512,256]{1,0:T(8,128)(2,1)S(1)}, bf16[2,256,64]{2,1,0:T(8,128)(2,1)S(1)}, bf16[2,256,64]{2,1,0:T(8,128...) custom-call(s32[4]{0:T(128)S(1)} %pad_add_fusion.info.refs_0_, bf16[2048,512]{1,0:T(8,128)(2,1)} %refs_1_.15, ...), custom_call_target="tpu_custom_call" | custom-call | flops 1000 | bytes 1000 | tf_op jit(solution)/shard_map/project_0/pallas_call | solution.py:632
  38.2 3.1 %attend_0.1 = (f32[256,1024]{1,0:T(8,128)S(1)}, bf16[256,1024]{1,0:T(8,128)(2,1)S(1)}, bf16[512,256]{1,0:T(8,128)(2,1)S(1)}, f32[8,256]{1,0:T(8,128)S(1)}, bf16[16,256]{1,0:T(8,128)(2,1)S(1)}) custom-call(s32[4]{0:T(128)S(1)} %pad_add_fusion.info.refs_0_, bf16[512,2048]{1,0:T(8,128)(2,1)} %refs_3_.5, ...), custom_call_target="tpu_custom_call" | custom-call | flops 1000 | bytes 1000 | tf_op jit(solution)/shard_map/attend_0/pallas_call | solution.py:632
  42.7 1.2 collective-permute-done.10.refs_1_
  44.1 1.5 collective-permute-start.11
  45.6 1.5 collective-permute-done.13.refs_6_.refs_7_
  47.2 4.1 %project_1.1 = (bf16[48,256]{1,0:T(8,128)(2,1)S(1)}, bf16[512,256]{1,0:T(8,128)(2,1)S(1)}, bf16[2,256,64]{2,1,0:T(8,128)(2,1)S(1)}, bf16[2,256,64]{2,1,0:T(8,128...) custom-call(s32[4]{0:T(128)S(1)} %pad_add_fusion.info.refs_0_, bf16[2048,512]{1,0:T(8,128)(2,1)} %refs_1_.15, ...), custom_call_target="tpu_custom_call" | custom-call | flops 1000 | bytes 1000 | tf_op jit(solution)/shard_map/project_1/pallas_call | solution.py:632
  51.4 3.7 %attend_1.1 = (f32[256,1024]{1,0:T(8,128)S(1)}, bf16[256,1024]{1,0:T(8,128)(2,1)S(1)}, bf16[512,256]{1,0:T(8,128)(2,1)S(1)}, f32[8,256]{1,0:T(8,128)S(1)}, bf16[16,256]{1,0:T(8,128)(2,1)S(1)}) custom-call(s32[4]{0:T(128)S(1)} %pad_add_fusion.info.refs_0_, bf16[512,2048]{1,0:T(8,128)(2,1)} %refs_3_.5, ...), custom_call_target="tpu_custom_call" | custom-call | flops 1000 | bytes 1000 | tf_op jit(solution)/shard_map/attend_1/pallas_call | solution.py:632
  55.2 3.0 %collective-permute-done.11.refs_1_ = bf16[256,1024]{1,0:T(8,128)(2,1)S(1)} collective-permute-done((bf16[256,1024]{1,0:T(8,128)(2,1)S(1)}, bf16[256,1024]{1,0:T(8,128)(2,1)S(1)}, u32[]{:S(2)}, u32[]{:S(2)}) %collective-permute-start.11) | collective-permute-done | bytes 524320 | tf_op jit(solution)/shard_map/ppermute | solution.py:671
  58.9 1.1 collective-permute-done.14.refs_1_
  60.2 1.5 collective-permute-start.15
  61.7 13.0 %front_0.1 = (bf16[256,2048]{1,0:T(8,128)(2,1)S(1)}, f32[256,512]{1,0:T(8,128)S(1)}, bf16[256,2048]{1,0:T(8,128)(2,1)S(1)}, bf16[256,2048]{1,0:T(8,128)(2,1)S(1)...) custom-call(s32[4]{0:T(128)S(1)} %pad_add_fusion.info.refs_0_, ...), custom_call_target="tpu_custom_call" | custom-call | flops 1000 | bytes 1000 | tf_op jit(solution)/shard_map/front_0/pallas_call | solution.py:632
  74.7 1.0 copy-done.25
  75.9 1.9 collective-permute-done.16.refs_8_
  77.8 12.0 %front_1.1 = (bf16[256,2048]{1,0:T(8,128)(2,1)S(1)}, f32[256,512]{1,0:T(8,128)S(1)}, bf16[256,2048]{1,0:T(8,128)(2,1)S(1)}, bf16[256,2048]{1,0:T(8,128)(2,1)S(1)...) custom-call(s32[4]{0:T(128)S(1)} %pad_add_fusion.info.refs_0_, ...), custom_call_target="tpu_custom_call" | custom-call | flops 1000 | bytes 1000 | tf_op jit(solution)/shard_map/front_1/pallas_call | solution.py:632
  89.8 2.1 collective-permute-start.17
  91.9 7.9 %back_1.1 = (f32[256,16]{1,0:T(8,128)S(1)}, f32[256,1024]{1,0:T(8,128)S(1)}, bf16[256,1024]{1,0:T(8,128)(2,1)S(1)}, f32[48,2048]{1,0:T(8,128)S(1)}) custom-call(s32[4]{0:T(128)S(1)} %pad_add_fusion.info.refs_0_, bf16[2,2048,2048]{2,1,0:T(8,128)(2,1)S(1)} %get-tuple-element.150.refs_1_, bf16[256,2048]{1,0:T(8,128)(2,1)S(1)} %get-tuple-element.160.refs_2_, ...), custom_call_target="tpu_custom_call" | custom-call | flops 1000 | bytes 1000 | tf_op jit(solution)/shard_map/back_1/pallas_call | solution.py:632
  99.8 2.1 collective-permute-done.17
  102.0 2.1 collective-permute-start.20
  104.2 1.0 collective-permute-start.22
  105.2 7.9 %back_0.1 = (f32[256,16]{1,0:T(8,128)S(1)}, f32[304,1024]{1,0:T(8,128)S(1)}, bf16[304,1024]{1,0:T(8,128)(2,1)S(1)}) custom-call(s32[4]{0:T(128)S(1)} %pad_add_fusion.info.refs_0_, bf16[2,2048,2048]{2,1,0:T(8,128)(2,1)S(1)} %get-tuple-element.150.refs_1_, bf16[256,2048]{1,0:T(8,128)(2,1)S(1)} %get-tuple-element.151.refs_2_, ...), custom_call_target="tpu_custom_call" | custom-call | flops 1000 | bytes 1000 | tf_op jit(solution)/shard_map/back_0/pallas_call | solution.py:632
  113.9 1.5 collective-permute-done.19.refs_1_
  115.4 4.5 %down_1.1 = (f32[256,1024]{1,0:T(8,128)S(1)}, bf16[256,1024]{1,0:T(8,128)(2,1)}) custom-call(s32[4]{0:T(128)S(1)} %pad_add_fusion.info.refs_0_, bf16[2048,2048]{1,0:T(8,128)(2,1)S(1)} %bitcast.19, bf16[256,2048]{1,0:T(8,128)(2,1)S(1)} %get-tuple-element.162.refs_4_.refs_2_, f32[256,16]{1,0:T(8,128)S(1)} %get-tuple-element.174.refs_3_, ...), custom_call_target="tpu_custom_call" | custom-call | flops 1000 | bytes 1000 | tf_op jit(solution)/shard_map/down_1/pallas_call | solution.py:632
  122.3 10.7 %attend_back_1.1 = (f32[256,512]{1,0:T(8,128)S(1)}, f32[256,1024]{1,0:T(8,128)S(1)}, bf16[256,1024]{1,0:T(8,128)(2,1)S(1)}, f32[256,1]{1,0:T(8,128)S(1)}, f32[48...) custom-call(s32[4]{0:T(128)S(1)} %pad_add_fusion.info.refs_0_, ...), custom_call_target="tpu_custom_call" | custom-call | flops 1000 | bytes 1000 | tf_op jit(solution)/shard_map/attend_back_1/pallas_call | solution.py:632
  133.6 3.9 %collective-permute-done.23.refs_1_ = bf16[304,1024]{1,0:T(8,128)(2,1)S(1)} collective-permute-done((bf16[304,1024]{1,0:T(8,128)(2,1)S(1)}, bf16[304,1024]{1,0:T(8,128)(2,1)S(1)}, u32[]{:S(2)}, u32[]{:S(2)}) %collective-permute-start.23) | collective-permute-done | bytes 622624 | tf_op jit(solution)/shard_map/ppermute | solution.py:671
  138.4 2.1 collective-permute-start.28
  140.6 9.8 %attend_back_0.1 = (f32[256,512]{1,0:T(8,128)S(1)}, f32[256,1024]{1,0:T(8,128)S(1)}, bf16[256,1024]{1,0:T(8,128)(2,1)S(1)}, f32[256,1]{1,0:T(8,128)S(1)}, bf16[4...) custom-call(s32[4]{0:T(128)S(1)} %pad_add_fusion.info.refs_0_, ...), custom_call_target="tpu_custom_call" | custom-call | flops 1000 | bytes 1000 | tf_op jit(solution)/shard_map/attend_back_0/pallas_call | solution.py:632
  151.0 1.7 collective-permute-done.30.refs_1_
  152.7 0.8 collective-permute-start.31
  153.5 1.6 collective-permute-start.36
  155.2 1.5 collective-permute-start.33
  156.7 1.0 collective-permute-done.31.refs_3_
  157.8 0.8 collective-permute-start.34
  158.6 1.8 collective-permute-done.36
  161.1 4.5 %down_0.1 = (f32[256,1024]{1,0:T(8,128)S(1)}, bf16[256,1024]{1,0:T(8,128)(2,1)}) custom-call(s32[4]{0:T(128)S(1)} %pad_add_fusion.info.refs_0_, bf16[2048,2048]{1,0:T(8,128)(2,1)S(1)} %bitcast.19, bf16[256,2048]{1,0:T(8,128)(2,1)S(1)} %copy-done.5, f32[256,16]{1,0:T(8,128)S(1)} %get-tuple-element.176.refs_6_.refs_3_, ...), custom_call_target="tpu_custom_call" | custom-call | flops 1000 | bytes 1000 | tf_op jit(solution)/shard_map/down_0/pallas_call | solution.py:632
  165.6 2.5 %collective-permute-start.35 = (bf16[2,112,512]{2,1,0:T(8,128)(2,1)S(1)}, bf16[2,112,512]{2,1,0:T(8,128)(2,1)S(1)}, u32[]{:S(2)}, u32[]{:S(2)}) collective-permute-start(bf16[2,112,512]{2,1,0:T(8,128)(2,1)S(1)} %pad_maximum_fusion.1), channel_id=1, source_target_pairs={{0,8},{4,12},{8,0},{12,4},{16,24},{20,28},{24,16},{28,20},{1,9},{5... | collective-permute-start | bytes 688136 | tf_op jit(solution)/shard_map/ppermute | solution.py:671
  168.7 3.5 %collective-permute-done.35 = bf16[2,112,512]{2,1,0:T(8,128)(2,1)S(1)} collective-permute-done((bf16[2,112,512]{2,1,0:T(8,128)(2,1)S(1)}, bf16[2,112,512]{2,1,0:T(8,128)(2,1)S(1)}, u32[]{:S(2)}, u32[]{:S(2)}) %collective-permute-start.35) | collective-permute-done | bytes 229408 | tf_op jit(solution)/shard_map/ppermute | solution.py:671
  172.8 0.8 copy-done.16
  173.6 4.4 %all-to-all-start.1 = ((bf16[8,64,512]{2,1,0:T(8,128)(2,1)}), bf16[8,64,512]{2,1,0:T(8,128)(2,1)S(1)}, u32[]{:S(2)}, u32[]{:S(2)}) async-start(bf16[8,64,512]{2,1,0:T(8,128)(2,1)} %bitcast.35), calls=%async_computation.1 | async-start | bytes 1048576 | tf_op jit(solution)/shard_map/all_to_all | solution.py:826
  178.1 1.4 high_sum.7
  179.5 1.3 collective-permute-start.40
  181.3 2.0 collective-permute-start.43
  183.4 3.9 %feedforward_sum.1 = (f32[8,32,2048]{2,1,0:T(8,128)}, f32[8,16,2048]{2,1,0:T(8,128)}, f32[8,2,16,2048]{3,2,1,0:T(8,128)}, f32[8,16,2048]{2,1,0:T(8,128)}) custom-call(s32[4]{0:T(128)S(1)} %pad_add_fusion.info.refs_0_, s32[8]{0:T(128)S(1)} %copy-done.71, bf16[2,192,512]{2,1,0:T(8,128)(2,1)S(1)} %copy-done.18, bf16[2,192,512]{2,1,0:T(8,128)(2,1)S(1)} %copy-done.42, ...), custom_call_target="tpu_custom_call" | custom-call | bytes 12000000 | tf_op jit(solution)/shard_map/feedforward_sum/pallas_call | solution.py:655
  187.3 3.0 %collective-permute-done.40.refs_1_ = bf16[512,512]{1,0:T(8,128)(2,1)S(1)} collective-permute-done((bf16[512,512]{1,0:T(8,128)(2,1)S(1)}, bf16[512,512]{1,0:T(8,128)(2,1)S(1)}, u32[]{:S(2)}, u32[]{:S(2)}) %collective-permute-start.40) | collective-permute-done | bytes 524320 | tf_op jit(solution)/shard_map/ppermute | solution.py:671
  190.3 2.2 %output.1 = bf16[512,512]{1,0:T(8,128)(2,1)} custom-call(s32[4]{0:T(128)S(1)} %pad_add_fusion.info.refs_0_, bf16[512,512]{1,0:T(8,128)(2,1)S(1)} %collective-permute-done.40.refs_1_, f32[256,1024]{1,0:T(8,128)S(1)} %get-tuple-element.215.refs_0_.refs_2_, bf16[256,1024]{1,0:T(8,128)(2,1)} %collective-permute-done.38.refs_1_.refs_3_, ...), custom_call_target="tpu_custom_call" | custom-call | flops 1000 | bytes 1000 | tf_op jit(solution)/shard_map/output/pallas_call | solution.py:632
  192.5 5.7 %all-to-all-start.2 = ((bf16[8,64,512]{2,1,0:T(8,128)(2,1)}), bf16[8,64,512]{2,1,0:T(8,128)(2,1)S(1)}, u32[]{:S(2)}, u32[]{:S(2)}) async-start(bf16[8,64,512]{2,1,0:T(8,128)(2,1)} %bitcast.14), calls=%async_computation.2 | async-start | bytes 1048576 | tf_op jit(solution)/shard_map/all_to_all | solution.py:826
  198.2 1.0 slice.35.refs_3_
  199.2 0.8 collective-permute-start.47
  200.1 1.3 collective-permute-start.46
  201.9 6.2 %collective-permute-done.47.refs_7_ = bf16[4,64,512]{2,1,0:T(8,128)(2,1)S(1)} collective-permute-done((bf16[4,64,512]{2,1,0:T(8,128)(2,1)S(1)}, bf16[4,64,512]{2,1,0:T(8,128)(2,1)S(1)}, u32[]{:S(2)}, u32[]{:S(2)}) %collective-permute-start.47) | collective-permute-done | bytes 262176 | tf_op jit(solution)/shard_map/ppermute | solution.py:671
  208.1 1.4 collect_grad.1
  209.5 1.4 collective-permute-done.46.refs_6_
  210.9 1.5 collective-permute-done.48.refs_8_
  212.4 4.4 %attention_sum.1 = (f32[8,48,2048]{2,1,0:T(8,128)}, f32[8,16,2048]{2,1,0:T(8,128)}, f32[8,16,512]{2,1,0:T(8,128)}, f32[8,2,16,128]{3,2,1,0:T(8,128)}, f32[8,16,512]{2,1,0:T(8,128)}) custom-call(s32[4]{0:T(128)S(1)} %pad_add_fusion.info.refs_0_, s32[8]{0:T(128)S(1)} %copy-done.71, bf16[4,112,512]{2,1,0:T(8,128)(2,1)S(1)} %constant_dynamic-update-slice_fusion.refs_14_.refs_0_, ...), custom_call_target="tpu_custom_call" | custom-call | bytes 12000000 | tf_op jit(solution)/shard_map/attention_sum/pallas_call | solution.py:655
  216.9 1.4 collect_out.1
  (252 shorter events, 14.4 us)
Async XLA Ops:
  3.9 21.8 %all-to-all-start = ((bf16[8,64,512]{2,1,0:T(8,128)(2,1)}), bf16[8,64,512]{2,1,0:T(8,128)(2,1)S(1)}, u32[]{:S(2)}, u32[]{:S(2)}) async-start(bf16[8,64,512]{2,1,0:T(8,128)(2,1)} %deal.1), calls=%async_computation | async-start | bytes 1048576 | tf_op jit(solution)/shard_map/all_to_all | solution.py:750
  11.2 8.2 %collective-permute-start = (bf16[2,512]{1,0:T(2,128)(2,1)S(1)}, bf16[2,512]{1,0:T(2,128)(2,1)S(1)}, u32[]{:S(2)}, u32[]{:S(2)}) collective-permute-start(bf16[2,512]{1,0:T(2,128)(2,1)S(1)} %pad_maximum_fusion.4), channel_id=1, source_target_pairs={{0,1},{1,0},{2,3},{3,2},{4,5},{5,4},{6,7},{7,6},{8,9},{9,8},{10,11... | collective-permute-start | bytes 6152 | tf_op jit(solution)/shard_map/ppermute | solution.py:671
  11.3 3.7 %collective-permute-start.1 = (bf16[2,512]{1,0:T(2,128)(2,1)S(1)}, bf16[2,512]{1,0:T(2,128)(2,1)S(1)}, u32[]{:S(2)}, u32[]{:S(2)}) collective-permute-start(bf16[2,512]{1,0:T(2,128)(2,1)S(1)} %pad_maximum_fusion.4), channel_id=1, source_target_pairs={{0,2},{1,3},{2,0},{3,1},{4,6},{5,7},{6,4},{7,5},{8,10},{9,11},{10,... | collective-permute-start | bytes 6152 | tf_op jit(solution)/shard_map/ppermute | solution.py:671
  12.9 14.4 %collective-permute-start.5 = (bf16[512,512]{1,0:T(8,128)(2,1)S(1)}, bf16[512,512]{1,0:T(8,128)(2,1)S(1)}, u32[]{:S(2)}, u32[]{:S(2)}) collective-permute-start(bf16[512,512]{1,0:T(8,128)(2,1)S(1)} %bitcast.29), channel_id=1, source_target_pairs={{0,2},{1,3},{2,0},{3,1},{4,6},{5,7},{6,4},{7,5},{8,10},{9,11},{10,... | collective-permute-start | bytes 1572872 | tf_op jit(solution)/shard_map/ppermute | solution.py:671
  14.9 4.5 %collective-permute-start.2 = (bf16[2,512]{1,0:T(2,128)(2,1)S(1)}, bf16[2,512]{1,0:T(2,128)(2,1)S(1)}, u32[]{:S(2)}, u32[]{:S(2)}) collective-permute-start(bf16[2,512]{1,0:T(2,128)(2,1)S(1)} %collective-permute-done.1), channel_id=1, source_target_pairs={{0,1},{1,0},{2,3},{3,2},{4,5},{5,4},{6,7},{7,6},{8,9},{9,8},{10,11... | collective-permute-start | bytes 6152 | tf_op jit(solution)/shard_map/ppermute | solution.py:671
  16.3 17.7 %copy-start.56 = (f32[32,256]{1,0:T(8,128)S(1)}, f32[32,256]{1,0:T(8,128)}, u32[]{:S(2)}) copy-start(f32[32,256]{1,0:T(8,128)} %constant.21.clone.refs_12_.refs_22_) | copy-start | bytes 98308
  16.3 17.7 %copy-start.58 = (f32[32,256]{1,0:T(8,128)S(1)}, f32[32,256]{1,0:T(8,128)}, u32[]{:S(2)}) copy-start(f32[32,256]{1,0:T(8,128)} %constant.19.clone.refs_11_.refs_21_) | copy-start | bytes 98308
  19.4 18.7 %copy-start.51 = (bf16[16,512]{1,0:T(8,128)(2,1)}, bf16[16,512]{1,0:T(8,128)(2,1)S(1)}, u32[]{:S(2)}) copy-start(bf16[16,512]{1,0:T(8,128)(2,1)S(1)} %get-tuple-element.124.refs_9_.refs_17_) | copy-start | bytes 49156
  19.4 18.8 %copy-start.60 = (bf16[2,16,128]{2,1,0:T(8,128)(2,1)}, bf16[2,16,128]{2,1,0:T(8,128)(2,1)S(1)}, u32[]{:S(2)}) copy-start(bf16[2,16,128]{2,1,0:T(8,128)(2,1)S(1)} %get-tuple-element.125.refs_10_.refs_18_) | copy-start | bytes 24580
  19.4 18.8 %copy-start.22 = (bf16[16,2048]{1,0:T(8,128)(2,1)}, bf16[16,2048]{1,0:T(8,128)(2,1)S(1)}, u32[]{:S(2)}) copy-start(bf16[16,2048]{1,0:T(8,128)(2,1)S(1)} %get-tuple-element.128.refs_4_.refs_20_) | copy-start | bytes 196612
  19.4 18.8 %copy-start.45 = (bf16[16,512]{1,0:T(8,128)(2,1)}, bf16[16,512]{1,0:T(8,128)(2,1)S(1)}, u32[]{:S(2)}) copy-start(bf16[16,512]{1,0:T(8,128)(2,1)S(1)} %get-tuple-element.127.refs_3_.refs_19_) | copy-start | bytes 49156
  25.7 6.8 %collective-permute-start.4 = (bf16[256,512]{1,0:T(8,128)(2,1)S(1)}, bf16[256,512]{1,0:T(8,128)(2,1)S(1)}, u32[]{:S(2)}, u32[]{:S(2)}) collective-permute-start(bf16[256,512]{1,0:T(8,128)(2,1)S(1)} %get-tuple-element.234), channel_id=1, source_target_pairs={{0,2},{1,3},{2,0},{3,1},{4,6},{5,7},{6,4},{7,5},{8,10},{9,11},{10,... | collective-permute-start | bytes 786440 | tf_op jit(solution)/shard_map/ppermute | solution.py:671
  27.2 6.8 %collective-permute-start.3 = (bf16[512,512]{1,0:T(8,128)(2,1)S(1)}, bf16[512,512]{1,0:T(8,128)(2,1)S(1)}, u32[]{:S(2)}, u32[]{:S(2)}) collective-permute-start(bf16[512,512]{1,0:T(8,128)(2,1)S(1)} %bitcast.21), channel_id=1, source_target_pairs={{0,1},{1,0},{2,3},{3,2},{4,5},{5,4},{6,7},{7,6},{8,9},{9,8},{10,11... | collective-permute-start | bytes 1572872 | tf_op jit(solution)/shard_map/ppermute | solution.py:671
  32.5 29.2 %copy-start.8 = (bf16[256,512]{1,0:T(8,128)(2,1)}, bf16[256,512]{1,0:T(8,128)(2,1)S(1)}, u32[]{:S(2)}) copy-start(bf16[256,512]{1,0:T(8,128)(2,1)S(1)} %collective-permute-done.4.refs_5_.refs_6_) | copy-start | bytes 786436
  32.5 1.5 collective-permute-start.6
  32.5 9.6 %collective-permute-start.9 = (bf16[256,512]{1,0:T(8,128)(2,1)S(1)}, bf16[256,512]{1,0:T(8,128)(2,1)S(1)}, u32[]{:S(2)}, u32[]{:S(2)}) collective-permute-start(bf16[256,512]{1,0:T(8,128)(2,1)S(1)} %get-tuple-element.233), channel_id=1, source_target_pairs={{0,2},{1,3},{2,0},{3,1},{4,6},{5,7},{6,4},{7,5},{8,10},{9,11},{10,... | collective-permute-start | bytes 786440 | tf_op jit(solution)/shard_map/ppermute | solution.py:671
  34.0 27.7 %copy-start.10 = (bf16[256,512]{1,0:T(8,128)(2,1)}, bf16[256,512]{1,0:T(8,128)(2,1)S(1)}, u32[]{:S(2)}) copy-start(bf16[256,512]{1,0:T(8,128)(2,1)S(1)} %collective-permute-done.6.refs_6_.refs_7_) | copy-start | bytes 786436
  42.0 1.9 collective-permute-start.10
  42.2 9.1 %collective-permute-start.7 = (bf16[512,512]{1,0:T(8,128)(2,1)S(1)}, bf16[512,512]{1,0:T(8,128)(2,1)S(1)}, u32[]{:S(2)}, u32[]{:S(2)}) collective-permute-start(bf16[512,512]{1,0:T(8,128)(2,1)S(1)} %bitcast.30), channel_id=1, source_target_pairs={{0,1},{1,0},{2,3},{3,2},{4,5},{5,4},{6,7},{7,6},{8,9},{9,8},{10,11... | collective-permute-start | bytes 1572872 | tf_op jit(solution)/shard_map/ppermute | solution.py:671
  42.6 8.8 %collective-permute-start.8 = (bf16[512,512]{1,0:T(8,128)(2,1)S(1)}, bf16[512,512]{1,0:T(8,128)(2,1)S(1)}, u32[]{:S(2)}, u32[]{:S(2)}) collective-permute-start(bf16[512,512]{1,0:T(8,128)(2,1)S(1)} %collective-permute-done.5.refs_11_.refs_10_), channel_id=1, source_target_pairs={{0,1},{1,0},{2,3},{3,2},{4,5},{5,4},{6,7},{7,6},{8,9},{9,8},{10,11... | collective-permute-start | bytes 1572872 | tf_op jit(solution)/shard_map/ppermute | solution.py:671
  44.1 14.1 %collective-permute-start.11 = (bf16[256,1024]{1,0:T(8,128)(2,1)S(1)}, bf16[256,1024]{1,0:T(8,128)(2,1)S(1)}, u32[]{:S(2)}, u32[]{:S(2)}) collective-permute-start(bf16[256,1024]{1,0:T(8,128)(2,1)S(1)} %pair_sum.4.refs_0_.refs_14_), channel_id=1, source_target_pairs={{0,2},{1,3},{2,0},{3,1},{4,6},{5,7},{6,4},{7,5},{8,10},{9,11},{10,... | collective-permute-start | bytes 1572872 | tf_op jit(solution)/shard_map/ppermute | solution.py:671
  45.6 1.5 collective-permute-start.13
  47.1 30.7 %copy-start.6 = (bf16[256,512]{1,0:T(8,128)(2,1)}, bf16[256,512]{1,0:T(8,128)(2,1)S(1)}, u32[]{:S(2)}) copy-start(bf16[256,512]{1,0:T(8,128)(2,1)S(1)} %collective-permute-done.13.refs_6_.refs_7_) | copy-start | bytes 786436
  55.1 19.5 %copy-start.49 = (bf16[512,256]{1,0:T(8,128)(2,1)}, bf16[512,256]{1,0:T(8,128)(2,1)S(1)}, u32[]{:S(2)}) copy-start(bf16[512,256]{1,0:T(8,128)(2,1)S(1)} %get-tuple-element.181.refs_25_) | copy-start | bytes 786436
  58.1 1.9 collective-permute-start.14
  58.4 3.3 %collective-permute-start.12 = (bf16[256,1024]{1,0:T(8,128)(2,1)S(1)}, bf16[256,1024]{1,0:T(8,128)(2,1)S(1)}, u32[]{:S(2)}, u32[]{:S(2)}) collective-permute-start(bf16[256,1024]{1,0:T(8,128)(2,1)S(1)} %far_sum.4.refs_7_), channel_id=1, source_target_pairs={{0,1},{1,0},{2,3},{3,2},{4,5},{5,4},{6,7},{7,6},{8,9},{9,8},{10,11... | collective-permute-start | bytes 1572872 | tf_op jit(solution)/shard_map/ppermute | solution.py:671
  60.2 15.5 %collective-permute-start.15 = (bf16[256,1024]{1,0:T(8,128)(2,1)S(1)}, bf16[256,1024]{1,0:T(8,128)(2,1)S(1)}, u32[]{:S(2)}, u32[]{:S(2)}) collective-permute-start(bf16[256,1024]{1,0:T(8,128)(2,1)S(1)} %pair_sum.5.refs_19_.refs_0_), channel_id=1, source_target_pairs={{0,2},{1,3},{2,0},{3,1},{4,6},{5,7},{6,4},{7,5},{8,10},{9,11},{10,... | collective-permute-start | bytes 1572872 | tf_op jit(solution)/shard_map/ppermute | solution.py:671
  75.7 29.6 %copy-start.4 = (bf16[256,2048]{1,0:T(8,128)(2,1)}, bf16[256,2048]{1,0:T(8,128)(2,1)S(1)}, u32[]{:S(2)}) copy-start(bf16[256,2048]{1,0:T(8,128)(2,1)S(1)} %get-tuple-element.153.refs_4_.refs_2_) | copy-start | bytes 3145732
  75.8 2.0 collective-permute-start.16
  89.8 12.1 %collective-permute-start.17 = (bf16[1,192,512]{2,1,0:T(8,128)(2,1)S(1)}, bf16[1,192,512]{2,1,0:T(8,128)(2,1)S(1)}, u32[]{:S(2)}, u32[]{:S(2)}) collective-permute-start(bf16[1,192,512]{2,1,0:T(8,128)(2,1)S(1)} %bitcast.36), channel_id=1, source_target_pairs={{0,16},{4,20},{8,24},{12,28},{16,0},{20,4},{24,8},{28,12},{1,17},{... | collective-permute-start | bytes 589832 | tf_op jit(solution)/shard_map/ppermute | solution.py:671
  102.0 2.2 collective-permute-start.18
  102.0 11.9 %collective-permute-start.20 = (bf16[2,192,512]{2,1,0:T(8,128)(2,1)S(1)}, bf16[2,192,512]{2,1,0:T(8,128)(2,1)S(1)}, u32[]{:S(2)}, u32[]{:S(2)}) collective-permute-start(bf16[2,192,512]{2,1,0:T(8,128)(2,1)S(1)} %pad_maximum_fusion.refs_0_), channel_id=1, source_target_pairs={{0,4},{4,0},{8,12},{12,8},{16,20},{20,16},{24,28},{28,24},{1,5},{5... | collective-permute-start | bytes 1179656 | tf_op jit(solution)/shard_map/ppermute | solution.py:671
  104.1 11.2 %collective-permute-start.19 = (bf16[2,192,512]{2,1,0:T(8,128)(2,1)S(1)}, bf16[2,192,512]{2,1,0:T(8,128)(2,1)S(1)}, u32[]{:S(2)}, u32[]{:S(2)}) collective-permute-start(bf16[2,192,512]{2,1,0:T(8,128)(2,1)S(1)} %pad_maximum_fusion.refs_0_), channel_id=1, source_target_pairs={{0,8},{4,12},{8,0},{12,4},{16,24},{20,28},{24,16},{28,20},{1,9},{5... | collective-permute-start | bytes 1179656 | tf_op jit(solution)/shard_map/ppermute | solution.py:671
  104.2 15.8 %collective-permute-start.22 = (bf16[256,1024]{1,0:T(8,128)(2,1)S(1)}, bf16[256,1024]{1,0:T(8,128)(2,1)S(1)}, u32[]{:S(2)}, u32[]{:S(2)}) collective-permute-start(bf16[256,1024]{1,0:T(8,128)(2,1)S(1)} %pair_sum.6.refs_11_.refs_0_), channel_id=1, source_target_pairs={{0,2},{1,3},{2,0},{3,1},{4,6},{5,7},{6,4},{7,5},{8,10},{9,11},{10,... | collective-permute-start | bytes 1572872 | tf_op jit(solution)/shard_map/ppermute | solution.py:671
  115.4 5.3 %collective-permute-start.21 = (bf16[304,1024]{1,0:T(8,128)(2,1)S(1)}, bf16[304,1024]{1,0:T(8,128)(2,1)S(1)}, u32[]{:S(2)}, u32[]{:S(2)}) collective-permute-start(bf16[304,1024]{1,0:T(8,128)(2,1)S(1)} %get-tuple-element.173), channel_id=1, source_target_pairs={{0,1},{1,0},{2,3},{3,2},{4,5},{5,4},{6,7},{7,6},{8,9},{9,8},{10,11... | collective-permute-start | bytes 1867784 | tf_op jit(solution)/shard_map/ppermute | solution.py:671
  120.1 2.1 collective-permute-start.24
  121.0 16.5 %collective-permute-start.23 = (bf16[304,1024]{1,0:T(8,128)(2,1)S(1)}, bf16[304,1024]{1,0:T(8,128)(2,1)S(1)}, u32[]{:S(2)}, u32[]{:S(2)}) collective-permute-start(bf16[304,1024]{1,0:T(8,128)(2,1)S(1)} %pair_sum.7.refs_34_.refs_0_), channel_id=1, source_target_pairs={{0,2},{1,3},{2,0},{3,1},{4,6},{5,7},{6,4},{7,5},{8,10},{9,11},{10,... | collective-permute-start | bytes 1867784 | tf_op jit(solution)/shard_map/ppermute | solution.py:671
  121.6 11.5 %collective-permute-start.26 = (bf16[2,192,512]{2,1,0:T(8,128)(2,1)S(1)}, bf16[2,192,512]{2,1,0:T(8,128)(2,1)S(1)}, u32[]{:S(2)}, u32[]{:S(2)}) collective-permute-start(bf16[2,192,512]{2,1,0:T(8,128)(2,1)S(1)} %collective-permute-done.19.refs_1_), channel_id=1, source_target_pairs={{0,4},{4,0},{8,12},{12,8},{16,20},{20,16},{24,28},{28,24},{1,5},{5... | collective-permute-start | bytes 1179656 | tf_op jit(solution)/shard_map/ppermute | solution.py:671
  133.1 4.6 %collective-permute-start.27 = (bf16[256,1024]{1,0:T(8,128)(2,1)S(1)}, bf16[256,1024]{1,0:T(8,128)(2,1)S(1)}, u32[]{:S(2)}, u32[]{:S(2)}) collective-permute-start(bf16[256,1024]{1,0:T(8,128)(2,1)S(1)} %get-tuple-element.198), channel_id=1, source_target_pairs={{0,1},{1,0},{2,3},{3,2},{4,5},{5,4},{6,7},{7,6},{8,9},{9,8},{10,11... | collective-permute-start | bytes 1572872 | tf_op jit(solution)/shard_map/ppermute | solution.py:671
  137.6 2.9 %collective-permute-start.25 = (bf16[304,1024]{1,0:T(8,128)(2,1)S(1)}, bf16[304,1024]{1,0:T(8,128)(2,1)S(1)}, u32[]{:S(2)}, u32[]{:S(2)}) collective-permute-start(bf16[304,1024]{1,0:T(8,128)(2,1)S(1)} %far_sum.7.refs_13_), channel_id=1, source_target_pairs={{0,1},{1,0},{2,3},{3,2},{4,5},{5,4},{6,7},{7,6},{8,9},{9,8},{10,11... | collective-permute-start | bytes 1867784 | tf_op jit(solution)/shard_map/ppermute | solution.py:671
  137.8 12.6 %collective-permute-start.29 = (bf16[256,512]{1,0:T(8,128)(2,1)S(1)}, bf16[256,512]{1,0:T(8,128)(2,1)S(1)}, u32[]{:S(2)}, u32[]{:S(2)}) collective-permute-start(bf16[256,512]{1,0:T(8,128)(2,1)S(1)} %high_sum.4.refs_36_), channel_id=1, source_target_pairs={{0,2},{1,3},{2,0},{3,1},{4,6},{5,7},{6,4},{7,5},{8,10},{9,11},{10,... | collective-permute-start | bytes 786440 | tf_op jit(solution)/shard_map/ppermute | solution.py:671
  138.4 11.9 %collective-permute-start.28 = (bf16[1,48,1024]{2,1,0:T(8,128)(2,1)S(1)}, bf16[1,48,1024]{2,1,0:T(8,128)(2,1)S(1)}, u32[]{:S(2)}, u32[]{:S(2)}) collective-permute-start(bf16[1,48,1024]{2,1,0:T(8,128)(2,1)S(1)} %slice_bitcast_fusion), channel_id=1, source_target_pairs={{0,16},{4,20},{8,24},{12,28},{16,0},{20,4},{24,8},{28,12},{1,17},{... | collective-permute-start | bytes 294920 | tf_op jit(solution)/shard_map/ppermute | solution.py:671
  150.4 4.7 %collective-permute-start.32 = (bf16[256,1024]{1,0:T(8,128)(2,1)S(1)}, bf16[256,1024]{1,0:T(8,128)(2,1)S(1)}, u32[]{:S(2)}, u32[]{:S(2)}) collective-permute-start(bf16[256,1024]{1,0:T(8,128)(2,1)S(1)} %get-tuple-element.205), channel_id=1, source_target_pairs={{0,1},{1,0},{2,3},{3,2},{4,5},{5,4},{6,7},{7,6},{8,9},{9,8},{10,11... | collective-permute-start | bytes 1572872 | tf_op jit(solution)/shard_map/ppermute | solution.py:671
  150.5 2.2 collective-permute-start.30
  152.7 5.0 %collective-permute-start.31 = (bf16[96,512]{1,0:T(8,128)(2,1)S(1)}, bf16[96,512]{1,0:T(8,128)(2,1)S(1)}, u32[]{:S(2)}, u32[]{:S(2)}) collective-permute-start(bf16[96,512]{1,0:T(8,128)(2,1)S(1)} %high_sum.5.refs_2_), channel_id=1, source_target_pairs={{0,2},{1,3},{2,0},{3,1},{4,6},{5,7},{6,4},{7,5},{8,10},{9,11},{10,... | collective-permute-start | bytes 294920 | tf_op jit(solution)/shard_map/ppermute | solution.py:671
  153.5 6.9 %collective-permute-start.36 = (bf16[2,48,1024]{2,1,0:T(8,128)(2,1)S(1)}, bf16[2,48,1024]{2,1,0:T(8,128)(2,1)S(1)}, u32[]{:S(2)}, u32[]{:S(2)}) collective-permute-start(bf16[2,48,1024]{2,1,0:T(8,128)(2,1)S(1)} %pad_maximum_fusion.2), channel_id=1, source_target_pairs={{0,8},{4,12},{8,0},{12,4},{16,24},{20,28},{24,16},{28,20},{1,9},{5... | collective-permute-start | bytes 589832 | tf_op jit(solution)/shard_map/ppermute | solution.py:671
  155.2 10.5 %collective-permute-start.33 = (bf16[256,512]{1,0:T(8,128)(2,1)S(1)}, bf16[256,512]{1,0:T(8,128)(2,1)S(1)}, u32[]{:S(2)}, u32[]{:S(2)}) collective-permute-start(bf16[256,512]{1,0:T(8,128)(2,1)S(1)} %high_sum.6), channel_id=1, source_target_pairs={{0,2},{1,3},{2,0},{3,1},{4,6},{5,7},{6,4},{7,5},{8,10},{9,11},{10,... | collective-permute-start | bytes 786440 | tf_op jit(solution)/shard_map/ppermute | solution.py:671
  157.8 7.9 %collective-permute-start.34 = (bf16[1,112,512]{2,1,0:T(8,128)(2,1)S(1)}, bf16[1,112,512]{2,1,0:T(8,128)(2,1)S(1)}, u32[]{:S(2)}, u32[]{:S(2)}) collective-permute-start(bf16[1,112,512]{2,1,0:T(8,128)(2,1)S(1)} %maximum_bitcast_fusion.refs_6_), channel_id=1, source_target_pairs={{0,16},{4,20},{8,24},{12,28},{16,0},{20,4},{24,8},{28,12},{1,17},{... | collective-permute-start | bytes 344072 | tf_op jit(solution)/shard_map/ppermute | solution.py:671
  160.4 11.8 %collective-permute-start.37 = (bf16[4,48,1024]{2,1,0:T(8,128)(2,1)S(1)}, bf16[4,48,1024]{2,1,0:T(8,128)(2,1)S(1)}, u32[]{:S(2)}, u32[]{:S(2)}) collective-permute-start(bf16[4,48,1024]{2,1,0:T(8,128)(2,1)S(1)} %constant_dynamic-update-slice_fusion.2.refs_4_), channel_id=1, source_target_pairs={{0,4},{4,0},{8,12},{12,8},{16,20},{20,16},{24,28},{28,24},{1,5},{5... | collective-permute-start | bytes 1179656 | tf_op jit(solution)/shard_map/ppermute | solution.py:671
  165.6 6.5 %collective-permute-start.35 = (bf16[2,112,512]{2,1,0:T(8,128)(2,1)S(1)}, bf16[2,112,512]{2,1,0:T(8,128)(2,1)S(1)}, u32[]{:S(2)}, u32[]{:S(2)}) collective-permute-start(bf16[2,112,512]{2,1,0:T(8,128)(2,1)S(1)} %pad_maximum_fusion.1), channel_id=1, source_target_pairs={{0,8},{4,12},{8,0},{12,4},{16,24},{20,28},{24,16},{28,20},{1,9},{5... | collective-permute-start | bytes 688136 | tf_op jit(solution)/shard_map/ppermute | solution.py:671
  168.2 9.9 %collective-permute-start.39 = (bf16[256,1024]{1,0:T(8,128)(2,1)}, bf16[256,1024]{1,0:T(8,128)(2,1)}, u32[]{:S(2)}, u32[]{:S(2)}) collective-permute-start(bf16[256,1024]{1,0:T(8,128)(2,1)} %get-tuple-element.218.refs_35_), channel_id=1, source_target_pairs={{0,1},{1,0},{2,3},{3,2},{4,5},{5,4},{6,7},{7,6},{8,9},{9,8},{10,11... | collective-permute-start | bytes 1572872 | tf_op jit(solution)/shard_map/ppermute | solution.py:671
  168.2 9.9 %collective-permute-start.38 = (bf16[256,1024]{1,0:T(8,128)(2,1)}, bf16[256,1024]{1,0:T(8,128)(2,1)}, u32[]{:S(2)}, u32[]{:S(2)}) collective-permute-start(bf16[256,1024]{1,0:T(8,128)(2,1)} %get-tuple-element.211), channel_id=1, source_target_pairs={{0,1},{1,0},{2,3},{3,2},{4,5},{5,4},{6,7},{7,6},{8,9},{9,8},{10,11... | collective-permute-start | bytes 1572872 | tf_op jit(solution)/shard_map/ppermute | solution.py:671
  173.6 18.9 %all-to-all-start.1 = ((bf16[8,64,512]{2,1,0:T(8,128)(2,1)}), bf16[8,64,512]{2,1,0:T(8,128)(2,1)S(1)}, u32[]{:S(2)}, u32[]{:S(2)}) async-start(bf16[8,64,512]{2,1,0:T(8,128)(2,1)} %bitcast.35), calls=%async_computation.1 | async-start | bytes 1048576 | tf_op jit(solution)/shard_map/all_to_all | solution.py:826
  179.5 10.8 %collective-permute-start.40 = (bf16[512,512]{1,0:T(8,128)(2,1)S(1)}, bf16[512,512]{1,0:T(8,128)(2,1)S(1)}, u32[]{:S(2)}, u32[]{:S(2)}) collective-permute-start(bf16[512,512]{1,0:T(8,128)(2,1)S(1)} %high_sum.7), channel_id=1, source_target_pairs={{0,2},{1,3},{2,0},{3,1},{4,6},{5,7},{6,4},{7,5},{8,10},{9,11},{10,... | collective-permute-start | bytes 1572872 | tf_op jit(solution)/shard_map/ppermute | solution.py:671
  180.8 2.5 %collective-permute-start.41 = (bf16[4,48,1024]{2,1,0:T(8,128)(2,1)S(1)}, bf16[4,48,1024]{2,1,0:T(8,128)(2,1)S(1)}, u32[]{:S(2)}, u32[]{:S(2)}) collective-permute-start(bf16[4,48,1024]{2,1,0:T(8,128)(2,1)S(1)} %copy-done.34), channel_id=1, source_target_pairs={{0,1},{1,0},{2,3},{3,2},{4,5},{5,4},{6,7},{7,6},{8,9},{9,8},{10,11... | collective-permute-start | bytes 1179656 | tf_op jit(solution)/shard_map/ppermute | solution.py:671
  180.8 2.5 %collective-permute-start.42 = (bf16[4,48,1024]{2,1,0:T(8,128)(2,1)S(1)}, bf16[4,48,1024]{2,1,0:T(8,128)(2,1)S(1)}, u32[]{:S(2)}, u32[]{:S(2)}) collective-permute-start(bf16[4,48,1024]{2,1,0:T(8,128)(2,1)S(1)} %collective-permute-done.37.refs_15_.refs_5_), channel_id=1, source_target_pairs={{0,1},{1,0},{2,3},{3,2},{4,5},{5,4},{6,7},{7,6},{8,9},{9,8},{10,11... | collective-permute-start | bytes 1179656 | tf_op jit(solution)/shard_map/ppermute | solution.py:671
  181.3 16.9 %collective-permute-start.43 = (bf16[4,112,512]{2,1,0:T(8,128)(2,1)S(1)}, bf16[4,112,512]{2,1,0:T(8,128)(2,1)}, u32[]{:S(2)}, u32[]{:S(2)}) collective-permute-start(bf16[4,112,512]{2,1,0:T(8,128)(2,1)S(1)} %constant_dynamic-update-slice_fusion.refs_14_.refs_0_), channel_id=1, source_target_pairs={{0,4},{4,0},{8,12},{12,8},{16,20},{20,16},{24,28},{28,24},{1,5},{5... | collective-permute-start | bytes 1376264 | tf_op jit(solution)/shard_map/ppermute | solution.py:671
  192.5 24.3 %all-to-all-start.2 = ((bf16[8,64,512]{2,1,0:T(8,128)(2,1)}), bf16[8,64,512]{2,1,0:T(8,128)(2,1)S(1)}, u32[]{:S(2)}, u32[]{:S(2)}) async-start(bf16[8,64,512]{2,1,0:T(8,128)(2,1)} %bitcast.14), calls=%async_computation.2 | async-start | bytes 1048576 | tf_op jit(solution)/shard_map/all_to_all | solution.py:826
  199.2 8.8 %collective-permute-start.47 = (bf16[4,64,512]{2,1,0:T(8,128)(2,1)S(1)}, bf16[4,64,512]{2,1,0:T(8,128)(2,1)S(1)}, u32[]{:S(2)}, u32[]{:S(2)}) collective-permute-start(bf16[4,64,512]{2,1,0:T(8,128)(2,1)S(1)} %slice.35.refs_3_), channel_id=1, source_target_pairs={{0,2},{1,3},{2,0},{3,1},{4,6},{5,7},{6,4},{7,5},{8,10},{9,11},{10,... | collective-permute-start | bytes 786440 | tf_op jit(solution)/shard_map/ppermute | solution.py:671
  200.1 10.8 %collective-permute-start.46 = (bf16[4,64,512]{2,1,0:T(8,128)(2,1)S(1)}, bf16[4,64,512]{2,1,0:T(8,128)(2,1)S(1)}, u32[]{:S(2)}, u32[]{:S(2)}) collective-permute-start(bf16[4,64,512]{2,1,0:T(8,128)(2,1)S(1)} %slice.34.refs_2_), channel_id=1, source_target_pairs={{0,2},{1,3},{2,0},{3,1},{4,6},{5,7},{6,4},{7,5},{8,10},{9,11},{10,... | collective-permute-start | bytes 786440 | tf_op jit(solution)/shard_map/ppermute | solution.py:671
  201.4 9.5 %collective-permute-start.44 = (bf16[4,64,512]{2,1,0:T(8,128)(2,1)S(1)}, bf16[4,64,512]{2,1,0:T(8,128)(2,1)S(1)}, u32[]{:S(2)}, u32[]{:S(2)}) collective-permute-start(bf16[4,64,512]{2,1,0:T(8,128)(2,1)S(1)} %slice.34.refs_2_), channel_id=1, source_target_pairs={{0,1},{1,0},{2,3},{3,2},{4,5},{5,4},{6,7},{7,6},{8,9},{9,8},{10,11... | collective-permute-start | bytes 786440 | tf_op jit(solution)/shard_map/ppermute | solution.py:671
  201.4 9.5 %collective-permute-start.45 = (bf16[4,64,512]{2,1,0:T(8,128)(2,1)S(1)}, bf16[4,64,512]{2,1,0:T(8,128)(2,1)S(1)}, u32[]{:S(2)}, u32[]{:S(2)}) collective-permute-start(bf16[4,64,512]{2,1,0:T(8,128)(2,1)S(1)} %slice.35.refs_3_), channel_id=1, source_target_pairs={{0,1},{1,0},{2,3},{3,2},{4,5},{5,4},{6,7},{7,6},{8,9},{9,8},{10,11... | collective-permute-start | bytes 786440 | tf_op jit(solution)/shard_map/ppermute | solution.py:671
  208.1 2.8 %collective-permute-start.49 = (bf16[4,64,512]{2,1,0:T(8,128)(2,1)S(1)}, bf16[4,64,512]{2,1,0:T(8,128)(2,1)S(1)}, u32[]{:S(2)}, u32[]{:S(2)}) collective-permute-start(bf16[4,64,512]{2,1,0:T(8,128)(2,1)S(1)} %collective-permute-done.47.refs_7_), channel_id=1, source_target_pairs={{0,1},{1,0},{2,3},{3,2},{4,5},{5,4},{6,7},{7,6},{8,9},{9,8},{10,11... | collective-permute-start | bytes 786440 | tf_op jit(solution)/shard_map/ppermute | solution.py:671
  210.9 1.5 collective-permute-start.48
  (67 other events, 434.1 us)
